TPU v7x, 128 devices: a whole 4x4x4 slice. The times are simulated.
128 devices in a mesh: row: 32 (over z, y, x_lo), col: 2 (over core), layer: 2 (over x_hi).
Axes of the slice: x: 4 (x_hi: 2, x_lo: 2; x = x_hi * 2 + x_lo), y: 4, z: 4, core: 2. Of those that a mesh axis runs over, the one named last changes fastest.
Arguments:
- dens_resp: bfloat16 [5120, 5120], P('row', ('col', 'layer')), may hold values from -0.078125 to 0.078125
- density: bfloat16 [5120, 5120], P('row', ('col', 'layer')), may hold values from -0.078125 to 0.078125
- fock: bfloat16 [5120, 5120], P('row', ('col', 'layer')), may hold values from -6 to 6
- fock_resp: bfloat16 [5120, 5120], P('row', ('col', 'layer')), may hold values from -6 to 6
- pattern: int32 [40, 40], replicated, may hold values 0 or 1
Outputs:
- sym_resp: float32 [5120, 5120], P(('row', 'col', 'layer'))
All inputs are finite; a program needn't handle non-finite values.
Results may differ from a plain program's by a relative error of at most 0.0029.
Values may be sent and summed in bfloat16 or wider, within the bound.
No kernel may reach another device: no remote copies, remote signals or barrier semaphores. Data moves between devices by JAX's collectives and lax.ppermute only.
A program may use at most 128 MiB of HBM per device.

v0:
```python
import jax
import jax.numpy as jnp
from jax import lax
from jax.sharding import Mesh
from jax.sharding import PartitionSpec as P

BLK = 128
AXES = ("z", "y", "xl", "core", "xh")
SIZES = (4, 4, 2, 2, 2)
f32 = jnp.float32
bf16 = jnp.bfloat16


def flip(value, z=0, y=0, xl=0, core=0, xh=0):
    masks = (z, y, xl, core, xh)
    pairs = []
    for source in range(128):
        rest, digits = source, []
        for size in reversed(SIZES):
            digits.append(rest % size)
            rest //= size
        target = 0
        for digit, size, mask in zip(reversed(digits), SIZES, masks):
            target = target * size + (digit ^ mask)
        pairs.append((source, target))
    return lax.ppermute(value, AXES, pairs)


def remap(value, rule):
    pairs = []
    for source in range(128):
        rest, digits = source, []
        for size in reversed(SIZES):
            digits.append(rest % size)
            rest //= size
        target = 0
        for digit, size in zip(rule(*reversed(digits)), SIZES):
            target = target * size + digit
        pairs.append((source, target))
    return lax.ppermute(value, AXES, pairs)


def pick(stack, index):
    return lax.dynamic_index_in_dim(stack, index, 0, keepdims=False)


def dot(a, b):
    return jnp.dot(a, b, preferred_element_type=f32)


def shards(dens_resp, density, fock, fock_resp, pattern):
    z, y, xl, core, xh = (lax.axis_index(name) for name in AXES)

    with jax.named_scope("left_columns"):
        keep = jnp.where(core == 0, dens_resp, density)
        send = jnp.where(core == 0, density, dens_resp)
        came = flip(send, core=1)
    with jax.named_scope("right_pair"):
        rounds = []
        for turn in range(2):
            chosen = jnp.where((xl ^ turn) == 0, fock, fock_resp)
            chosen, _ = lax.optimization_barrier((chosen, send))
            rounds.append(
                remap(chosen, lambda a, b, c, d, e: (a, b, d, c ^ turn, e))
            )
    with jax.named_scope("left_columns"):
        low = jnp.where(core == 0, keep, came).reshape(160, 4, 320)
        high = jnp.where(core == 0, came, keep).reshape(160, 4, 320)
        pieces = jnp.stack(
            [jnp.concatenate((low[:, j], high[:, j]), axis=1) for j in range(4)]
        )
        slots = [pick(pieces, y)] + [
            flip(pick(pieces, y ^ q), y=q) for q in (1, 2, 3)
        ]
        left = jnp.concatenate(slots)
    with jax.named_scope("right_gather"):
        rounds[0], rounds[1], left = lax.optimization_barrier((rounds[0], rounds[1], left))
        right = jnp.where(
            core == 0,
            jnp.concatenate((rounds[0], rounds[1])),
            jnp.concatenate((rounds[1], rounds[0])),
        )
        right, left = lax.optimization_barrier((right, left))
        rights = jnp.stack([right] + [flip(right, z=q) for q in (1, 2, 3)])
    with jax.named_scope("left_gather"):
        lefts = {
            (0, 0): left,
            (1, 0): flip(left, xl=1),
            (0, 1): flip(left, xh=1),
            (1, 1): flip(left, xl=1, xh=1),
        }

    with jax.named_scope("density_columns"):
        cols, _ = lax.optimization_barrier((density, left))
        cols = cols.reshape(160, 4, 320).transpose(1, 0, 2)
        dslots = jnp.stack(
            [pick(cols, y)] + [flip(pick(cols, y ^ q), y=q) for q in (1, 2, 3)]
        )

    with jax.named_scope("first_product"):
        rights, dslots = lax.optimization_barrier((rights, dslots))
        rsel = [
            jnp.concatenate([pick(rights, z ^ (nzh * 2 + (xh ^ r))) for nzh in range(2)])
            for r in range(2)
        ]
        theirs = [jnp.where(core == 0, lefts[1, r], lefts[0, r]) for r in range(2)]
        mine = [jnp.where(core == 0, lefts[0, r], lefts[1, r]) for r in range(2)]
        theirs = (dot(theirs[0], rsel[0]) + dot(theirs[1], rsel[1])).reshape(4, 160, 1280)
        mine = (dot(mine[0], rsel[0]) + dot(mine[1], rsel[1])).reshape(4, 160, 1280)
    with jax.named_scope("mixed_sum"):
        both = [None] * 4
        for q in (2, 1, 3, 0):
            both[q] = mine[q] + flip(theirs[q], core=1)
        sums = [flip(both[q], y=q) for q in (1, 2, 3)]

    with jax.named_scope("density_gather"):
        dslots, _ = lax.optimization_barrier((dslots, (both[0], both[1], both[2], both[3])))
        turned = remap(
            dslots,
            lambda a, b, c, d, e: (c * 2 + e, b, a // 2, d, a % 2),
        )
        dparts = jnp.stack([turned] + [flip(turned, z=q) for q in (1, 2, 3)])
    with jax.named_scope("mixed_sum"):
        sums, dparts = lax.optimization_barrier((sums, dparts))
        total = both[0] + sums[0] + sums[1] + sums[2]
        mixed = total.astype(bf16)

    with jax.named_scope("density_rows"):
        dfull = jnp.concatenate(
            [
                jnp.concatenate(
                    [
                        pick(pick(dparts, z ^ (nxl * 2 + nzl)), y ^ ny)
                        for nzl in range(2)
                    ],
                    axis=1,
                )
                for ny in range(4)
                for nxl in range(2)
            ]
        )

    with jax.named_scope("mixed_gather"):
        mslots = jnp.concatenate([mixed] + [flip(mixed, y=q) for q in (1, 2, 3)])
        mother = flip(mslots, core=1)

    with jax.named_scope("second_product"):
        near = dot(mslots, dfull).reshape(4, 160, 640)
        far = dot(mother, dfull).reshape(4, 160, 640)
        place = xl * 2 + xh
        straight = (xl ^ core) == 0

        def piece(r):
            q = place ^ r ^ y
            a, b = pick(near, q), pick(far, q)
            return jnp.where(straight, jnp.stack((a, b)), jnp.stack((b, a)))

        total = piece(0)
        for r in (1, 2, 3):
            came = flip(piece(r).astype(bf16), xl=r // 2, xh=r % 2)
            total = total + came.astype(f32)
        stay = pick(total, core)
        away = flip(pick(total, 1 - core), core=1)
        rows = jnp.where(
            core == 0,
            jnp.concatenate((stay, away), axis=1),
            jnp.concatenate((away, stay), axis=1),
        )

    with jax.named_scope("transposed"):
        turned = rows.astype(bf16).T.reshape(32, 40, 160)
        turned = lax.all_to_all(
            turned, ("z", "xl", "core", "xh"), split_axis=0, concat_axis=0, tiled=True
        )
        turned = turned.reshape(4, 2, 2, 2, 40, 160)
        flipped = turned.transpose(4, 0, 1, 3, 2, 5).reshape(40, 5120)
    with jax.named_scope("direct"):
        quarters = rows.reshape(4, 40, 1280)
        direct = jnp.stack(
            [
                remap(
                    pick(quarters, y ^ t),
                    lambda a, b, c, d, e: (a, c * 2 + e, d, (b ^ t) // 2, (b ^ t) % 2),
                )
                for t in range(4)
            ]
        ).reshape(4, 40, 4, 320)
        mark = core * 2 + xh
        long_rows = jnp.stack([pick(direct, mark ^ ny) for ny in range(4)], axis=2)
        long_rows = long_rows.reshape(40, 5120)

    symmetric = 0.5 * (long_rows + flipped.astype(f32))
    first_row = ((((z * 4 + y) * 2 + xl) * 2 + core) * 2 + xh) * 40
    block_rows = (first_row + jnp.arange(40, dtype=jnp.int32)) // BLK
    block_count = pattern.shape[0]
    onehot = (
        block_rows[:, None] == jnp.arange(block_count, dtype=jnp.int32)[None, :]
    ).astype(f32)
    kept_blocks = jnp.dot(onehot, pattern.astype(f32), preferred_element_type=f32)
    kept_full = jnp.repeat(kept_blocks, BLK, axis=1)
    return symmetric * kept_full


def solution(mesh):
    fine = Mesh(mesh.devices.reshape(SIZES), AXES)
    split = P(("z", "y", "xl"), ("core", "xh"))
    return jax.shard_map(
        shards,
        mesh=fine,
        in_specs=(split, split, split, split, P()),
        out_specs=P(AXES, None),
        check_vma=False,
    )
```

profile of v0, /device:TPU:2, one launch (start us, length us, event | category | flops | bytes accessed | tf_op | source)
XLA Modules:
  0.0 253.0 jit_solution(18091403729881522011)
XLA Ops:
  3.2 2.4 collective-permute-start
  11.9 2.9 %collective-permute-start.4 = (bf16[160,640]{1,0:T(8,128)(2,1)S(1)}, bf16[160,640]{1,0:T(8,128)(2,1)S(1)}, u32[]{:S(2)}, u32[]{:S(2)}) collective-permute-start(bf16[160,640]{1,0:T(8,128)(2,1)S(1)} %get-tuple-element.83), channel_id=1, source_target_pairs={{0,16},{1,17},{2,18},{3,19},{4,20},{5,21},{6,22},{7,23},{8,24},{9,... | collective-permute-start | bytes 614408 | tf_op jit(solution)/shard_map/left_columns/ppermute | solution.py:26
  15.0 3.2 %collective-permute-done.3 = bf16[160,640]{1,0:T(8,128)(2,1)S(1)} collective-permute-done((bf16[160,640]{1,0:T(8,128)(2,1)S(1)}, bf16[160,640]{1,0:T(8,128)(2,1)S(1)}, u32[]{:S(2)}, u32[]{:S(2)}) %collective-permute-start.3) | collective-permute-done | bytes 204832 | tf_op jit(solution)/shard_map/left_columns/ppermute | solution.py:26
  18.2 6.6 %collective-permute-done.4 = bf16[160,640]{1,0:T(8,128)(2,1)S(1)} collective-permute-done((bf16[160,640]{1,0:T(8,128)(2,1)S(1)}, bf16[160,640]{1,0:T(8,128)(2,1)S(1)}, u32[]{:S(2)}, u32[]{:S(2)}) %collective-permute-start.4) | collective-permute-done | bytes 204832 | tf_op jit(solution)/shard_map/left_columns/ppermute | solution.py:26
  24.8 2.6 %collective-permute-done.5 = bf16[160,640]{1,0:T(8,128)(2,1)S(1)} collective-permute-done((bf16[160,640]{1,0:T(8,128)(2,1)S(1)}, bf16[160,640]{1,0:T(8,128)(2,1)S(1)}, u32[]{:S(2)}, u32[]{:S(2)}) %collective-permute-start.5) | collective-permute-done | bytes 204832 | tf_op jit(solution)/shard_map/left_columns/ppermute | solution.py:26
  30.8 3.6 %collective-permute-start.8 = (bf16[320,1280]{1,0:T(8,128)(2,1)S(1)}, bf16[320,1280]{1,0:T(8,128)(2,1)}, u32[]{:S(2)}, u32[]{:S(2)}) collective-permute-start(bf16[320,1280]{1,0:T(8,128)(2,1)S(1)} %maximum_select_fusion), channel_id=1, source_target_pairs={{0,64},{1,65},{2,66},{3,67},{4,68},{5,69},{6,70},{7,71},{8,72},{9,... | collective-permute-start | bytes 2457608 | tf_op jit(solution)/shard_map/right_gather/ppermute | solution.py:26
  37.9 3.1 %collective-permute-done.10 = bf16[160,320]{1,0:T(8,128)(2,1)S(1)} collective-permute-done((bf16[160,320]{1,0:T(8,128)(2,1)S(1)}, bf16[160,320]{1,0:T(8,128)(2,1)S(1)}, u32[]{:S(2)}, u32[]{:S(2)}) %collective-permute-start.10) | collective-permute-done | bytes 102432 | tf_op jit(solution)/shard_map/density_columns/ppermute | solution.py:26
  42.8 2.4 collective-permute-start.13
  52.2 17.1 %collective-permute-done.8 = bf16[320,1280]{1,0:T(8,128)(2,1)} collective-permute-done((bf16[320,1280]{1,0:T(8,128)(2,1)S(1)}, bf16[320,1280]{1,0:T(8,128)(2,1)}, u32[]{:S(2)}, u32[]{:S(2)}) %collective-permute-start.8) | collective-permute-done | bytes 819232 | tf_op jit(solution)/shard_map/right_gather/ppermute | solution.py:26
  69.3 2.6 %collective-permute-done.9 = bf16[320,1280]{1,0:T(8,128)(2,1)} collective-permute-done((bf16[320,1280]{1,0:T(8,128)(2,1)S(1)}, bf16[320,1280]{1,0:T(8,128)(2,1)}, u32[]{:S(2)}, u32[]{:S(2)}) %collective-permute-start.9) | collective-permute-done | bytes 819232 | tf_op jit(solution)/shard_map/right_gather/ppermute | solution.py:26
  73.7 6.3 %collective-permute-done.14 = bf16[640,640]{1,0:T(8,128)(2,1)S(1)} collective-permute-done((bf16[640,640]{1,0:T(8,128)(2,1)S(1)}, bf16[640,640]{1,0:T(8,128)(2,1)S(1)}, u32[]{:S(2)}, u32[]{:S(2)}) %collective-permute-start.14) | collective-permute-done | bytes 819232 | tf_op jit(solution)/shard_map/left_gather/ppermute | solution.py:26
  89.6 3.4 %collective-permute-start.22 = (bf16[4,160,320]{2,1,0:T(8,128)(2,1)S(1)}, bf16[4,160,320]{2,1,0:T(8,128)(2,1)S(1)}, u32[]{:S(2)}, u32[]{:S(2)}) collective-permute-start(bf16[4,160,320]{2,1,0:T(8,128)(2,1)S(1)} %pad_maximum_fusion.12), channel_id=1, source_target_pairs={{0,0},{1,32},{2,2},{3,34},{4,64},{5,96},{6,66},{7,98},{8,8},{9,40}... | collective-permute-start | bytes 1228808 | tf_op jit(solution)/shard_map/density_gather/ppermute | solution.py:40
  93.0 24.4 %collective-permute-done.22 = bf16[4,160,320]{2,1,0:T(8,128)(2,1)S(1)} collective-permute-done((bf16[4,160,320]{2,1,0:T(8,128)(2,1)S(1)}, bf16[4,160,320]{2,1,0:T(8,128)(2,1)S(1)}, u32[]{:S(2)}, u32[]{:S(2)}) %collective-permute-start.22) | collective-permute-done | bytes 409632 | tf_op jit(solution)/shard_map/density_gather/ppermute | solution.py:40
  122.0 2.4 collective-permute-start.24
  124.4 7.1 %collective-permute-done.23 = bf16[4,160,320]{2,1,0:T(8,128)(2,1)S(1)} collective-permute-done((bf16[4,160,320]{2,1,0:T(8,128)(2,1)S(1)}, bf16[4,160,320]{2,1,0:T(8,128)(2,1)S(1)}, u32[]{:S(2)}, u32[]{:S(2)}) %collective-permute-start.23) | collective-permute-done | bytes 409632 | tf_op jit(solution)/shard_map/density_gather/ppermute | solution.py:26
  132.4 7.7 %collective-permute-done.24 = bf16[4,160,320]{2,1,0:T(8,128)(2,1)S(1)} collective-permute-done((bf16[4,160,320]{2,1,0:T(8,128)(2,1)S(1)}, bf16[4,160,320]{2,1,0:T(8,128)(2,1)S(1)}, u32[]{:S(2)}, u32[]{:S(2)}) %collective-permute-start.24) | collective-permute-done | bytes 409632 | tf_op jit(solution)/shard_map/density_gather/ppermute | solution.py:26
  140.0 9.2 %collective-permute-done.25 = bf16[4,160,320]{2,1,0:T(8,128)(2,1)S(1)} collective-permute-done((bf16[4,160,320]{2,1,0:T(8,128)(2,1)S(1)}, bf16[4,160,320]{2,1,0:T(8,128)(2,1)S(1)}, u32[]{:S(2)}, u32[]{:S(2)}) %collective-permute-start.25) | collective-permute-done | bytes 409632 | tf_op jit(solution)/shard_map/density_gather/ppermute | solution.py:26
  149.7 4.2 %collective-permute-done.19 = f32[160,1280]{1,0:T(8,128)S(1)} collective-permute-done((f32[160,1280]{1,0:T(8,128)S(1)}, f32[160,1280]{1,0:T(8,128)S(1)}, u32[]{:S(2)}, u32[]{:S(2)}) %collective-permute-start.19) | collective-permute-done | bytes 819232 | tf_op jit(solution)/shard_map/mixed_sum/ppermute | solution.py:26
  153.9 2.6 %collective-permute-done.21 = f32[160,1280]{1,0:T(8,128)S(1)} collective-permute-done((f32[160,1280]{1,0:T(8,128)S(1)}, f32[160,1280]{1,0:T(8,128)S(1)}, u32[]{:S(2)}, u32[]{:S(2)}) %collective-permute-start.21) | collective-permute-done | bytes 819232 | tf_op jit(solution)/shard_map/mixed_sum/ppermute | solution.py:26
  156.8 3.3 %collective-permute-start.27 = (bf16[160,1280]{1,0:T(8,128)(2,1)S(1)}, bf16[160,1280]{1,0:T(8,128)(2,1)S(1)}, u32[]{:S(2)}, u32[]{:S(2)}) collective-permute-start(bf16[160,1280]{1,0:T(8,128)(2,1)S(1)} %add_convert_fusion), channel_id=1, source_target_pairs={{0,16},{1,17},{2,18},{3,19},{4,20},{5,21},{6,22},{7,23},{8,24},{9,... | collective-permute-start | bytes 1228808 | tf_op jit(solution)/shard_map/mixed_gather/ppermute | solution.py:26
  161.5 5.6 %collective-permute-done.26 = bf16[160,1280]{1,0:T(8,128)(2,1)S(1)} collective-permute-done((bf16[160,1280]{1,0:T(8,128)(2,1)S(1)}, bf16[160,1280]{1,0:T(8,128)(2,1)S(1)}, u32[]{:S(2)}, u32[]{:S(2)}) %collective-permute-start.26) | collective-permute-done | bytes 409632 | tf_op jit(solution)/shard_map/mixed_gather/ppermute | solution.py:26
  167.1 5.8 %collective-permute-done.27 = bf16[160,1280]{1,0:T(8,128)(2,1)S(1)} collective-permute-done((bf16[160,1280]{1,0:T(8,128)(2,1)S(1)}, bf16[160,1280]{1,0:T(8,128)(2,1)S(1)}, u32[]{:S(2)}, u32[]{:S(2)}) %collective-permute-start.27) | collective-permute-done | bytes 409632 | tf_op jit(solution)/shard_map/mixed_gather/ppermute | solution.py:26
  172.9 2.6 %collective-permute-done.28 = bf16[160,1280]{1,0:T(8,128)(2,1)} collective-permute-done((bf16[160,1280]{1,0:T(8,128)(2,1)S(1)}, bf16[160,1280]{1,0:T(8,128)(2,1)}, u32[]{:S(2)}, u32[]{:S(2)}) %collective-permute-start.28) | collective-permute-done | bytes 409632 | tf_op jit(solution)/shard_map/mixed_gather/ppermute | solution.py:26
  179.1 2.4 fusion.25
  181.7 2.9 %fusion.29 = f32[640,640]{1,0:T(8,128)S(1)} fusion(bf16[640,1280]{1,0:T(8,128)(2,1)} %collective-permute-done.29, bf16[1280,640]{1,0:T(8,128)(2,1)S(1)} %maximum_dynamic-update-slice_fusion), kind=kOutput, calls=%fused_computation.139 | convolution fusion | flops 1048576000 | bytes 4915200 | tf_op jit(solution)/shard_map/second_product/dot_general | solution.py:48
  185.5 8.4 %collective-permute-start.30 = (bf16[2,160,640]{2,1,0:T(8,128)(2,1)}, bf16[2,160,640]{2,1,0:T(8,128)(2,1)}, u32[]{:S(2)}, u32[]{:S(2)}) collective-permute-start(bf16[2,160,640]{2,1,0:T(8,128)(2,1)} %fusion.5), channel_id=1, source_target_pairs={{0,1},{1,0},{2,3},{3,2},{4,5},{5,4},{6,7},{7,6},{8,9},{9,8},{10,11... | collective-permute-start | bytes 1228808 | tf_op jit(solution)/shard_map/second_product/ppermute | solution.py:26
  196.2 8.4 %collective-permute-done.30 = bf16[2,160,640]{2,1,0:T(8,128)(2,1)} collective-permute-done((bf16[2,160,640]{2,1,0:T(8,128)(2,1)}, bf16[2,160,640]{2,1,0:T(8,128)(2,1)}, u32[]{:S(2)}, u32[]{:S(2)}) %collective-permute-start.30) | collective-permute-done | bytes 409632 | tf_op jit(solution)/shard_map/second_product/ppermute | solution.py:26
  204.5 7.8 %collective-permute-done.31 = bf16[2,160,640]{2,1,0:T(8,128)(2,1)} collective-permute-done((bf16[2,160,640]{2,1,0:T(8,128)(2,1)}, bf16[2,160,640]{2,1,0:T(8,128)(2,1)}, u32[]{:S(2)}, u32[]{:S(2)}) %collective-permute-start.31) | collective-permute-done | bytes 409632 | tf_op jit(solution)/shard_map/second_product/ppermute | solution.py:26
  216.6 3.3 %collective-permute-start.34 = (f32[40,1280]{1,0:T(8,128)S(1)}, f32[40,1280]{1,0:T(8,128)}, u32[]{:S(2)}, u32[]{:S(2)}) collective-permute-start(f32[40,1280]{1,0:T(8,128)S(1)} %get-tuple-element.78), channel_id=1, source_target_pairs={{0,0},{1,8},{2,4},{3,12},{4,16},{5,24},{6,20},{7,28},{8,1},{9,9},{... | collective-permute-start | bytes 614408 | tf_op jit(solution)/shard_map/direct/ppermute | solution.py:40
  221.1 5.6 %collective-permute-start.36 = (f32[40,1280]{1,0:T(8,128)S(1)}, f32[40,1280]{1,0:T(8,128)S(1)}, u32[]{:S(2)}, u32[]{:S(2)}) collective-permute-start(f32[40,1280]{1,0:T(8,128)S(1)} %get-tuple-element.76), channel_id=1, source_target_pairs={{0,2},{1,10},{2,6},{3,14},{4,18},{5,26},{6,22},{7,30},{8,3},{9,11}... | collective-permute-start | bytes 614408 | tf_op jit(solution)/shard_map/direct/ppermute | solution.py:40
  227.8 4.9 %all-to-all-start = ((bf16[32,40,160]{2,1,0:T(8,128)(2,1)}), bf16[32,40,160]{2,1,0:T(8,128)(2,1)S(1)}, u32[]{:S(2)}, u32[]{:S(2)}) async-start(bf16[32,40,160]{2,1,0:T(8,128)(2,1)} %bitcast.53), calls=%async_computation | async-start | bytes 1310720 | tf_op jit(solution)/shard_map/transposed/all_to_all | solution.py:172
  235.7 10.0 %collective-permute-done.37 = f32[40,1280]{1,0:T(8,128)S(1)} collective-permute-done((f32[40,1280]{1,0:T(8,128)S(1)}, f32[40,1280]{1,0:T(8,128)S(1)}, u32[]{:S(2)}, u32[]{:S(2)}) %collective-permute-start.37) | collective-permute-done | bytes 204832 | tf_op jit(solution)/shard_map/direct/ppermute | solution.py:40
  (135 shorter events, 67.6 us)
Async XLA Ops:
  3.2 24.2 %collective-permute-start = (bf16[160,1280]{1,0:T(8,128)(2,1)}, bf16[160,1280]{1,0:T(8,128)(2,1)S(1)}, u32[]{:S(2)}, u32[]{:S(2)}) collective-permute-start(bf16[160,1280]{1,0:T(8,128)(2,1)} %get-tuple-element.20), channel_id=1, source_target_pairs={{0,0},{1,1},{2,4},{3,5},{4,2},{5,3},{6,6},{7,7},{8,8},{9,9},{10,12... | collective-permute-start | bytes 1228808 | tf_op jit(solution)/shard_map/right_pair/ppermute | solution.py:40
  5.6 21.8 %collective-permute-start.1 = (bf16[160,1280]{1,0:T(8,128)(2,1)S(1)}, bf16[160,1280]{1,0:T(8,128)(2,1)}, u32[]{:S(2)}, u32[]{:S(2)}) collective-permute-start(bf16[160,1280]{1,0:T(8,128)(2,1)S(1)} %get-tuple-element.21), channel_id=1, source_target_pairs={{0,2},{1,3},{2,6},{3,7},{4,0},{5,1},{6,4},{7,5},{8,10},{9,11},{10,... | collective-permute-start | bytes 1228808 | tf_op jit(solution)/shard_map/right_pair/ppermute | solution.py:40
  10.2 8.0 %collective-permute-start.3 = (bf16[160,640]{1,0:T(8,128)(2,1)S(1)}, bf16[160,640]{1,0:T(8,128)(2,1)S(1)}, u32[]{:S(2)}, u32[]{:S(2)}) collective-permute-start(bf16[160,640]{1,0:T(8,128)(2,1)S(1)} %get-tuple-element.84), channel_id=1, source_target_pairs={{0,8},{1,9},{2,10},{3,11},{4,12},{5,13},{6,14},{7,15},{8,0},{9,1},... | collective-permute-start | bytes 614408 | tf_op jit(solution)/shard_map/left_columns/ppermute | solution.py:26
  11.9 12.8 %collective-permute-start.4 = (bf16[160,640]{1,0:T(8,128)(2,1)S(1)}, bf16[160,640]{1,0:T(8,128)(2,1)S(1)}, u32[]{:S(2)}, u32[]{:S(2)}) collective-permute-start(bf16[160,640]{1,0:T(8,128)(2,1)S(1)} %get-tuple-element.83), channel_id=1, source_target_pairs={{0,16},{1,17},{2,18},{3,19},{4,20},{5,21},{6,22},{7,23},{8,24},{9,... | collective-permute-start | bytes 614408 | tf_op jit(solution)/shard_map/left_columns/ppermute | solution.py:26
  14.9 12.5 %collective-permute-start.5 = (bf16[160,640]{1,0:T(8,128)(2,1)S(1)}, bf16[160,640]{1,0:T(8,128)(2,1)S(1)}, u32[]{:S(2)}, u32[]{:S(2)}) collective-permute-start(bf16[160,640]{1,0:T(8,128)(2,1)S(1)} %get-tuple-element.82), channel_id=1, source_target_pairs={{0,24},{1,25},{2,26},{3,27},{4,28},{5,29},{6,30},{7,31},{8,16},{9,... | collective-permute-start | bytes 614408 | tf_op jit(solution)/shard_map/left_columns/ppermute | solution.py:26
  28.8 21.3 %collective-permute-start.7 = (bf16[320,1280]{1,0:T(8,128)(2,1)S(1)}, bf16[320,1280]{1,0:T(8,128)(2,1)S(1)}, u32[]{:S(2)}, u32[]{:S(2)}) collective-permute-start(bf16[320,1280]{1,0:T(8,128)(2,1)S(1)} %maximum_select_fusion), channel_id=1, source_target_pairs={{0,32},{1,33},{2,34},{3,35},{4,36},{5,37},{6,38},{7,39},{8,40},{9,... | collective-permute-start | bytes 2457608 | tf_op jit(solution)/shard_map/right_gather/ppermute | solution.py:26
  30.8 38.5 %collective-permute-start.8 = (bf16[320,1280]{1,0:T(8,128)(2,1)S(1)}, bf16[320,1280]{1,0:T(8,128)(2,1)}, u32[]{:S(2)}, u32[]{:S(2)}) collective-permute-start(bf16[320,1280]{1,0:T(8,128)(2,1)S(1)} %maximum_select_fusion), channel_id=1, source_target_pairs={{0,64},{1,65},{2,66},{3,67},{4,68},{5,69},{6,70},{7,71},{8,72},{9,... | collective-permute-start | bytes 2457608 | tf_op jit(solution)/shard_map/right_gather/ppermute | solution.py:26
  34.4 37.5 %collective-permute-start.9 = (bf16[320,1280]{1,0:T(8,128)(2,1)S(1)}, bf16[320,1280]{1,0:T(8,128)(2,1)}, u32[]{:S(2)}, u32[]{:S(2)}) collective-permute-start(bf16[320,1280]{1,0:T(8,128)(2,1)S(1)} %maximum_select_fusion), channel_id=1, source_target_pairs={{0,96},{1,97},{2,98},{3,99},{4,100},{5,101},{6,102},{7,103},{8,104... | collective-permute-start | bytes 2457608 | tf_op jit(solution)/shard_map/right_gather/ppermute | solution.py:26
  36.1 6.7 %collective-permute-start.11 = (bf16[160,320]{1,0:T(8,128)(2,1)S(1)}, bf16[160,320]{1,0:T(8,128)(2,1)}, u32[]{:S(2)}, u32[]{:S(2)}) collective-permute-start(bf16[160,320]{1,0:T(8,128)(2,1)S(1)} %bitcast.141), channel_id=1, source_target_pairs={{0,16},{1,17},{2,18},{3,19},{4,20},{5,21},{6,22},{7,23},{8,24},{9,... | collective-permute-start | bytes 307208 | tf_op jit(solution)/shard_map/density_columns/ppermute | solution.py:26
  41.1 6.2 %collective-permute-start.12 = (bf16[160,320]{1,0:T(8,128)(2,1)S(1)}, bf16[160,320]{1,0:T(8,128)(2,1)}, u32[]{:S(2)}, u32[]{:S(2)}) collective-permute-start(bf16[160,320]{1,0:T(8,128)(2,1)S(1)} %bitcast.140), channel_id=1, source_target_pairs={{0,24},{1,25},{2,26},{3,27},{4,28},{5,29},{6,30},{7,31},{8,16},{9,... | collective-permute-start | bytes 307208 | tf_op jit(solution)/shard_map/density_columns/ppermute | solution.py:26
  42.8 30.9 %collective-permute-start.13 = (bf16[640,640]{1,0:T(8,128)(2,1)S(1)}, bf16[640,640]{1,0:T(8,128)(2,1)S(1)}, u32[]{:S(2)}, u32[]{:S(2)}) collective-permute-start(bf16[640,640]{1,0:T(8,128)(2,1)S(1)} %pad_maximum_fusion.11), channel_id=1, source_target_pairs={{0,1},{1,0},{2,3},{3,2},{4,5},{5,4},{6,7},{7,6},{8,9},{9,8},{10,11... | collective-permute-start | bytes 2457608 | tf_op jit(solution)/shard_map/left_gather/ppermute | solution.py:26
  47.3 32.7 %collective-permute-start.14 = (bf16[640,640]{1,0:T(8,128)(2,1)S(1)}, bf16[640,640]{1,0:T(8,128)(2,1)S(1)}, u32[]{:S(2)}, u32[]{:S(2)}) collective-permute-start(bf16[640,640]{1,0:T(8,128)(2,1)S(1)} %pad_maximum_fusion.11), channel_id=1, source_target_pairs={{0,5},{1,4},{2,7},{3,6},{4,1},{5,0},{6,3},{7,2},{8,13},{9,12},{10,... | collective-permute-start | bytes 2457608 | tf_op jit(solution)/shard_map/left_gather/ppermute | solution.py:26
  50.0 31.4 %collective-permute-start.6 = (bf16[640,640]{1,0:T(8,128)(2,1)S(1)}, bf16[640,640]{1,0:T(8,128)(2,1)S(1)}, u32[]{:S(2)}, u32[]{:S(2)}) collective-permute-start(bf16[640,640]{1,0:T(8,128)(2,1)S(1)} %pad_maximum_fusion.11), channel_id=1, source_target_pairs={{0,4},{1,5},{2,6},{3,7},{4,0},{5,1},{6,2},{7,3},{8,12},{9,13},{10,... | collective-permute-start | bytes 2457608 | tf_op jit(solution)/shard_map/left_gather/ppermute | solution.py:26
  83.9 5.2 %collective-permute-start.20 = (f32[160,1280]{1,0:T(8,128)S(1)}, f32[160,1280]{1,0:T(8,128)S(1)}, u32[]{:S(2)}, u32[]{:S(2)}) collective-permute-start(f32[160,1280]{1,0:T(8,128)S(1)} %get-tuple-element.40), channel_id=1, source_target_pairs={{0,2},{1,3},{2,0},{3,1},{4,6},{5,7},{6,4},{7,5},{8,10},{9,11},{10,... | collective-permute-start | bytes 2457608 | tf_op jit(solution)/shard_map/mixed_sum/ppermute | solution.py:26
  89.6 27.8 %collective-permute-start.22 = (bf16[4,160,320]{2,1,0:T(8,128)(2,1)S(1)}, bf16[4,160,320]{2,1,0:T(8,128)(2,1)S(1)}, u32[]{:S(2)}, u32[]{:S(2)}) collective-permute-start(bf16[4,160,320]{2,1,0:T(8,128)(2,1)S(1)} %pad_maximum_fusion.12), channel_id=1, source_target_pairs={{0,0},{1,32},{2,2},{3,34},{4,64},{5,96},{6,66},{7,98},{8,8},{9,40}... | collective-permute-start | bytes 1228808 | tf_op jit(solution)/shard_map/density_gather/ppermute | solution.py:40
  117.3 14.2 %collective-permute-start.23 = (bf16[4,160,320]{2,1,0:T(8,128)(2,1)S(1)}, bf16[4,160,320]{2,1,0:T(8,128)(2,1)S(1)}, u32[]{:S(2)}, u32[]{:S(2)}) collective-permute-start(bf16[4,160,320]{2,1,0:T(8,128)(2,1)S(1)} %collective-permute-done.22), channel_id=1, source_target_pairs={{0,32},{1,33},{2,34},{3,35},{4,36},{5,37},{6,38},{7,39},{8,40},{9,... | collective-permute-start | bytes 1228808 | tf_op jit(solution)/shard_map/density_gather/ppermute | solution.py:26
  117.3 32.4 %collective-permute-start.17 = (f32[160,1280]{1,0:T(8,128)S(1)}, f32[160,1280]{1,0:T(8,128)S(1)}, u32[]{:S(2)}, u32[]{:S(2)}) collective-permute-start(f32[160,1280]{1,0:T(8,128)S(1)} %get-tuple-element.38), channel_id=1, source_target_pairs={{0,8},{1,9},{2,10},{3,11},{4,12},{5,13},{6,14},{7,15},{8,0},{9,1},... | collective-permute-start | bytes 2457608 | tf_op jit(solution)/shard_map/mixed_sum/ppermute | solution.py:26
  118.2 35.8 %collective-permute-start.19 = (f32[160,1280]{1,0:T(8,128)S(1)}, f32[160,1280]{1,0:T(8,128)S(1)}, u32[]{:S(2)}, u32[]{:S(2)}) collective-permute-start(f32[160,1280]{1,0:T(8,128)S(1)} %get-tuple-element.37), channel_id=1, source_target_pairs={{0,16},{1,17},{2,18},{3,19},{4,20},{5,21},{6,22},{7,23},{8,24},{9,... | collective-permute-start | bytes 2457608 | tf_op jit(solution)/shard_map/mixed_sum/ppermute | solution.py:26
  120.1 36.4 %collective-permute-start.21 = (f32[160,1280]{1,0:T(8,128)S(1)}, f32[160,1280]{1,0:T(8,128)S(1)}, u32[]{:S(2)}, u32[]{:S(2)}) collective-permute-start(f32[160,1280]{1,0:T(8,128)S(1)} %get-tuple-element.36), channel_id=1, source_target_pairs={{0,24},{1,25},{2,26},{3,27},{4,28},{5,29},{6,30},{7,31},{8,16},{9,... | collective-permute-start | bytes 2457608 | tf_op jit(solution)/shard_map/mixed_sum/ppermute | solution.py:26
  122.0 18.0 %collective-permute-start.24 = (bf16[4,160,320]{2,1,0:T(8,128)(2,1)S(1)}, bf16[4,160,320]{2,1,0:T(8,128)(2,1)S(1)}, u32[]{:S(2)}, u32[]{:S(2)}) collective-permute-start(bf16[4,160,320]{2,1,0:T(8,128)(2,1)S(1)} %collective-permute-done.22), channel_id=1, source_target_pairs={{0,64},{1,65},{2,66},{3,67},{4,68},{5,69},{6,70},{7,71},{8,72},{9,... | collective-permute-start | bytes 1228808 | tf_op jit(solution)/shard_map/density_gather/ppermute | solution.py:26
  131.5 17.8 %collective-permute-start.25 = (bf16[4,160,320]{2,1,0:T(8,128)(2,1)S(1)}, bf16[4,160,320]{2,1,0:T(8,128)(2,1)S(1)}, u32[]{:S(2)}, u32[]{:S(2)}) collective-permute-start(bf16[4,160,320]{2,1,0:T(8,128)(2,1)S(1)} %collective-permute-done.22), channel_id=1, source_target_pairs={{0,96},{1,97},{2,98},{3,99},{4,100},{5,101},{6,102},{7,103},{8,104... | collective-permute-start | bytes 1228808 | tf_op jit(solution)/shard_map/density_gather/ppermute | solution.py:26
  156.7 10.3 %collective-permute-start.26 = (bf16[160,1280]{1,0:T(8,128)(2,1)S(1)}, bf16[160,1280]{1,0:T(8,128)(2,1)S(1)}, u32[]{:S(2)}, u32[]{:S(2)}) collective-permute-start(bf16[160,1280]{1,0:T(8,128)(2,1)S(1)} %add_convert_fusion), channel_id=1, source_target_pairs={{0,8},{1,9},{2,10},{3,11},{4,12},{5,13},{6,14},{7,15},{8,0},{9,1},... | collective-permute-start | bytes 1228808 | tf_op jit(solution)/shard_map/mixed_gather/ppermute | solution.py:26
  156.8 16.1 %collective-permute-start.27 = (bf16[160,1280]{1,0:T(8,128)(2,1)S(1)}, bf16[160,1280]{1,0:T(8,128)(2,1)S(1)}, u32[]{:S(2)}, u32[]{:S(2)}) collective-permute-start(bf16[160,1280]{1,0:T(8,128)(2,1)S(1)} %add_convert_fusion), channel_id=1, source_target_pairs={{0,16},{1,17},{2,18},{3,19},{4,20},{5,21},{6,22},{7,23},{8,24},{9,... | collective-permute-start | bytes 1228808 | tf_op jit(solution)/shard_map/mixed_gather/ppermute | solution.py:26
  160.1 15.4 %collective-permute-start.28 = (bf16[160,1280]{1,0:T(8,128)(2,1)S(1)}, bf16[160,1280]{1,0:T(8,128)(2,1)}, u32[]{:S(2)}, u32[]{:S(2)}) collective-permute-start(bf16[160,1280]{1,0:T(8,128)(2,1)S(1)} %add_convert_fusion), channel_id=1, source_target_pairs={{0,24},{1,25},{2,26},{3,27},{4,28},{5,29},{6,30},{7,31},{8,16},{9,... | collective-permute-start | bytes 1228808 | tf_op jit(solution)/shard_map/mixed_gather/ppermute | solution.py:26
  185.5 19.1 %collective-permute-start.30 = (bf16[2,160,640]{2,1,0:T(8,128)(2,1)}, bf16[2,160,640]{2,1,0:T(8,128)(2,1)}, u32[]{:S(2)}, u32[]{:S(2)}) collective-permute-start(bf16[2,160,640]{2,1,0:T(8,128)(2,1)} %fusion.5), channel_id=1, source_target_pairs={{0,1},{1,0},{2,3},{3,2},{4,5},{5,4},{6,7},{7,6},{8,9},{9,8},{10,11... | collective-permute-start | bytes 1228808 | tf_op jit(solution)/shard_map/second_product/ppermute | solution.py:26
  194.7 17.7 %collective-permute-start.31 = (bf16[2,160,640]{2,1,0:T(8,128)(2,1)}, bf16[2,160,640]{2,1,0:T(8,128)(2,1)}, u32[]{:S(2)}, u32[]{:S(2)}) collective-permute-start(bf16[2,160,640]{2,1,0:T(8,128)(2,1)} %fusion.6), channel_id=1, source_target_pairs={{0,4},{1,5},{2,6},{3,7},{4,0},{5,1},{6,2},{7,3},{8,12},{9,13},{10,... | collective-permute-start | bytes 1228808 | tf_op jit(solution)/shard_map/second_product/ppermute | solution.py:26
  195.5 17.6 %collective-permute-start.32 = (bf16[2,160,640]{2,1,0:T(8,128)(2,1)}, bf16[2,160,640]{2,1,0:T(8,128)(2,1)}, u32[]{:S(2)}, u32[]{:S(2)}) collective-permute-start(bf16[2,160,640]{2,1,0:T(8,128)(2,1)} %fusion.7), channel_id=1, source_target_pairs={{0,5},{1,4},{2,7},{3,6},{4,1},{5,0},{6,3},{7,2},{8,13},{9,12},{10,... | collective-permute-start | bytes 1228808 | tf_op jit(solution)/shard_map/second_product/ppermute | solution.py:26
  216.6 17.4 %collective-permute-start.34 = (f32[40,1280]{1,0:T(8,128)S(1)}, f32[40,1280]{1,0:T(8,128)}, u32[]{:S(2)}, u32[]{:S(2)}) collective-permute-start(f32[40,1280]{1,0:T(8,128)S(1)} %get-tuple-element.78), channel_id=1, source_target_pairs={{0,0},{1,8},{2,4},{3,12},{4,16},{5,24},{6,20},{7,28},{8,1},{9,9},{... | collective-permute-start | bytes 614408 | tf_op jit(solution)/shard_map/direct/ppermute | solution.py:40
  219.9 15.3 %collective-permute-start.35 = (f32[40,1280]{1,0:T(8,128)S(1)}, f32[40,1280]{1,0:T(8,128)S(1)}, u32[]{:S(2)}, u32[]{:S(2)}) collective-permute-start(f32[40,1280]{1,0:T(8,128)S(1)} %get-tuple-element.77), channel_id=1, source_target_pairs={{0,1},{1,9},{2,5},{3,13},{4,17},{5,25},{6,21},{7,29},{8,0},{9,8},{... | collective-permute-start | bytes 614408 | tf_op jit(solution)/shard_map/direct/ppermute | solution.py:40
  221.1 14.3 %collective-permute-start.36 = (f32[40,1280]{1,0:T(8,128)S(1)}, f32[40,1280]{1,0:T(8,128)S(1)}, u32[]{:S(2)}, u32[]{:S(2)}) collective-permute-start(f32[40,1280]{1,0:T(8,128)S(1)} %get-tuple-element.76), channel_id=1, source_target_pairs={{0,2},{1,10},{2,6},{3,14},{4,18},{5,26},{6,22},{7,30},{8,3},{9,11}... | collective-permute-start | bytes 614408 | tf_op jit(solution)/shard_map/direct/ppermute | solution.py:40
  227.8 20.8 %all-to-all-start = ((bf16[32,40,160]{2,1,0:T(8,128)(2,1)}), bf16[32,40,160]{2,1,0:T(8,128)(2,1)S(1)}, u32[]{:S(2)}, u32[]{:S(2)}) async-start(bf16[32,40,160]{2,1,0:T(8,128)(2,1)} %bitcast.53), calls=%async_computation | async-start | bytes 1310720 | tf_op jit(solution)/shard_map/transposed/all_to_all | solution.py:172
  232.8 13.0 %collective-permute-start.37 = (f32[40,1280]{1,0:T(8,128)S(1)}, f32[40,1280]{1,0:T(8,128)S(1)}, u32[]{:S(2)}, u32[]{:S(2)}) collective-permute-start(f32[40,1280]{1,0:T(8,128)S(1)} %get-tuple-element.75), channel_id=1, source_target_pairs={{0,3},{1,11},{2,7},{3,15},{4,19},{5,27},{6,23},{7,31},{8,2},{9,10}... | collective-permute-start | bytes 614408 | tf_op jit(solution)/shard_map/direct/ppermute | solution.py:40
  (10 other events, 57.8 us)
where the time goes:
time: 256 us; the launch traced here: 253 us
  waiting for transfers between devices  144 us (56%)
  starting transfers between devices  64.5 us (25%)
  other arithmetic  19.4 us (8%)
  local copies, waits for them, and re-layouts  13.2 us (5%)
  matrix products  11.5 us (4%)
    ppermute x31, waiting for transfers between devices, flip(): return lax.ppermute(value, AXES, pairs)  109 us
    ppermute x31, starting transfers between devices, flip(): return lax.ppermute(value, AXES, pairs)  42.3 us
    ppermute x7, waiting for transfers between devices, remap(): return lax.ppermute(value, AXES, pairs)  34.4 us
    ppermute x7, starting transfers between devices, remap(): return lax.ppermute(value, AXES, pairs)  17.3 us
    dot_general x6, matrix products, dot(): return jnp.dot(a, b, preferred_element_type=f32)  11.3 us
  transfers between devices with their start and end apart: 39, of which 26 were waited for; matrix products, arithmetic and copies ran while one was open for 11% of the time, Pallas kernels for 0%

commit v1 on v0

--- a/solution.py
+++ b/solution.py
@@ -42,6 +42,16 @@
 
 def pick(stack, index):
     return lax.dynamic_index_in_dim(stack, index, 0, keepdims=False)
+
+
+def ring_gather(block, axes):
+    near, far = axes
+    half = block.shape[0] // 2
+    one = flip(block, **near)
+    three = flip(block, **far)
+    upper = flip(three[:half], **near)
+    lower = flip(one[half:], **far)
+    return one, three, jnp.concatenate((upper, lower))
 
 
 def dot(a, b):
@@ -69,36 +79,41 @@
         pieces = jnp.stack(
             [jnp.concatenate((low[:, j], high[:, j]), axis=1) for j in range(4)]
         )
-        slots = [pick(pieces, y)] + [
-            flip(pick(pieces, y ^ q), y=q) for q in (1, 2, 3)
-        ]
-        left = jnp.concatenate(slots)
+        left = lax.all_to_all(pieces, "y", split_axis=0, concat_axis=0, tiled=True)
+        left = left.reshape(640, 640)
+    with jax.named_scope("density_turn"):
+        turned, _ = lax.optimization_barrier((density, send))
+        turned = remap(
+            turned,
+            lambda a, b, c, d, e: (c * 2 + e, b, a // 2, d, a % 2),
+        )
     with jax.named_scope("right_gather"):
-        rounds[0], rounds[1], left = lax.optimization_barrier((rounds[0], rounds[1], left))
+        rounds, left = lax.optimization_barrier((rounds, left))
         right = jnp.where(
             core == 0,
             jnp.concatenate((rounds[0], rounds[1])),
             jnp.concatenate((rounds[1], rounds[0])),
         )
-        right, left = lax.optimization_barrier((right, left))
-        rights = jnp.stack([right] + [flip(right, z=q) for q in (1, 2, 3)])
+        right, left, turned = lax.optimization_barrier((right, left, turned))
+        one, three, two = ring_gather(right, ({"z": 1}, {"z": 3}))
+        rights = [right, one, two, three]
     with jax.named_scope("left_gather"):
-        lefts = {
-            (0, 0): left,
-            (1, 0): flip(left, xl=1),
-            (0, 1): flip(left, xh=1),
-            (1, 1): flip(left, xl=1, xh=1),
-        }
+        one, three, two = ring_gather(left, ({"xl": 1}, {"xl": 1, "xh": 1}))
+        lefts = {(0, 0): left, (1, 0): one, (0, 1): two, (1, 1): three}
 
     with jax.named_scope("density_columns"):
-        cols, _ = lax.optimization_barrier((density, left))
-        cols = cols.reshape(160, 4, 320).transpose(1, 0, 2)
-        dslots = jnp.stack(
-            [pick(cols, y)] + [flip(pick(cols, y ^ q), y=q) for q in (1, 2, 3)]
-        )
+        turned, rights[1], rights[3] = lax.optimization_barrier((turned, rights[1], rights[3]))
+        cols = turned.reshape(160, 4, 320).transpose(1, 0, 2)
+        dslots = lax.all_to_all(cols, "y", split_axis=0, concat_axis=0, tiled=True)
+
+    with jax.named_scope("swap_matrix"):
+        at = jnp.arange(1280, dtype=jnp.int32)
+        to = at // 40 % 4 * 320 + at // 160 * 40 + at % 40
+        swap = (to[:, None] == at[None, :]).astype(bf16)
 
     with jax.named_scope("first_product"):
-        rights, dslots = lax.optimization_barrier((rights, dslots))
+        rights, dslots, swap = lax.optimization_barrier((rights, dslots, swap))
+        rights = jnp.stack(rights)
         rsel = [
             jnp.concatenate([pick(rights, z ^ (nzh * 2 + (xh ^ r))) for nzh in range(2)])
             for r in range(2)
@@ -110,29 +125,28 @@
     with jax.named_scope("mixed_sum"):
         both = [None] * 4
         for q in (2, 1, 3, 0):
-            both[q] = mine[q] + flip(theirs[q], core=1)
-        sums = [flip(both[q], y=q) for q in (1, 2, 3)]
+            both[q] = pick(mine, y ^ q) + flip(pick(theirs, y ^ q), core=1)
+        upper = flip(both[2][:80], y=1)
+        lower = flip(both[2][80:], y=3)
+        third = jnp.concatenate((both[3][:80] + upper, both[3][80:]))
+        first = jnp.concatenate((both[1][:80], both[1][80:] + lower))
+        sums = [flip(first, y=1), flip(third, y=3)]
 
     with jax.named_scope("density_gather"):
-        dslots, _ = lax.optimization_barrier((dslots, (both[0], both[1], both[2], both[3])))
-        turned = remap(
-            dslots,
-            lambda a, b, c, d, e: (c * 2 + e, b, a // 2, d, a % 2),
-        )
-        dparts = jnp.stack([turned] + [flip(turned, z=q) for q in (1, 2, 3)])
+        dslots, _ = lax.optimization_barrier((dslots, both))
+        dparts = [dslots] + [flip(dslots, z=q) for q in (1, 2, 3)]
+
     with jax.named_scope("mixed_sum"):
         sums, dparts = lax.optimization_barrier((sums, dparts))
-        total = both[0] + sums[0] + sums[1] + sums[2]
+        total = both[0] + sums[0] + sums[1]
         mixed = total.astype(bf16)
 
     with jax.named_scope("density_rows"):
+        dparts = jnp.stack(dparts)
         dfull = jnp.concatenate(
             [
                 jnp.concatenate(
-                    [
-                        pick(pick(dparts, z ^ (nxl * 2 + nzl)), y ^ ny)
-                        for nzl in range(2)
-                    ],
+                    [pick(dparts, z ^ (nxl * 2 + nzl))[ny] for nzl in range(2)],
                     axis=1,
                 )
                 for ny in range(4)
@@ -147,49 +161,40 @@
     with jax.named_scope("second_product"):
         near = dot(mslots, dfull).reshape(4, 160, 640)
         far = dot(mother, dfull).reshape(4, 160, 640)
-        place = xl * 2 + xh
-        straight = (xl ^ core) == 0
-
-        def piece(r):
-            q = place ^ r ^ y
-            a, b = pick(near, q), pick(far, q)
-            return jnp.where(straight, jnp.stack((a, b)), jnp.stack((b, a)))
-
-        total = piece(0)
-        for r in (1, 2, 3):
-            came = flip(piece(r).astype(bf16), xl=r // 2, xh=r % 2)
+
+        def piece(h, r):
+            rows = jnp.where(core == h, near, far).reshape(8, 2, 40, 640)
+            return lax.dynamic_index_in_dim(rows, xh ^ r, 1, keepdims=False).reshape(320, 640)
+
+        total = piece(0, 0)
+        for h, r in ((0, 1), (1, 0), (1, 1)):
+            came = flip(piece(h, r).astype(bf16), xl=h, xh=r)
             total = total + came.astype(f32)
-        stay = pick(total, core)
-        away = flip(pick(total, 1 - core), core=1)
+        total = total.reshape(4, 2, 40, 640)
+        stay = lax.dynamic_index_in_dim(total, core, 1, keepdims=False)
+        away = flip(lax.dynamic_index_in_dim(total, 1 - core, 1, keepdims=False), core=1)
         rows = jnp.where(
             core == 0,
-            jnp.concatenate((stay, away), axis=1),
-            jnp.concatenate((away, stay), axis=1),
+            jnp.concatenate((stay, away), axis=2),
+            jnp.concatenate((away, stay), axis=2),
         )
 
     with jax.named_scope("transposed"):
-        turned = rows.astype(bf16).T.reshape(32, 40, 160)
+        sorted_rows = jnp.concatenate([pick(rows, y ^ ny) for ny in range(4)])
+        turned = sorted_rows.astype(bf16).T.reshape(32, 40, 160)
         turned = lax.all_to_all(
             turned, ("z", "xl", "core", "xh"), split_axis=0, concat_axis=0, tiled=True
         )
-        turned = turned.reshape(4, 2, 2, 2, 40, 160)
-        flipped = turned.transpose(4, 0, 1, 3, 2, 5).reshape(40, 5120)
+        turned = turned.reshape(4, 8, 40, 160).transpose(0, 2, 1, 3).reshape(160, 1280)
+        flipped = dot(turned, swap).reshape(4, 40, 1280)
+        flipped = flipped.transpose(1, 0, 2).reshape(40, 5120)
     with jax.named_scope("direct"):
-        quarters = rows.reshape(4, 40, 1280)
-        direct = jnp.stack(
-            [
-                remap(
-                    pick(quarters, y ^ t),
-                    lambda a, b, c, d, e: (a, c * 2 + e, d, (b ^ t) // 2, (b ^ t) % 2),
-                )
-                for t in range(4)
-            ]
-        ).reshape(4, 40, 4, 320)
-        mark = core * 2 + xh
-        long_rows = jnp.stack([pick(direct, mark ^ ny) for ny in range(4)], axis=2)
+        direct = jnp.stack([rows[0]] + [flip(rows[q], y=q) for q in (1, 2, 3)])
+        direct = direct.reshape(4, 40, 4, 320)
+        long_rows = jnp.stack([pick(direct, y ^ ny) for ny in range(4)], axis=2)
         long_rows = long_rows.reshape(40, 5120)
 
-    symmetric = 0.5 * (long_rows + flipped.astype(f32))
+    symmetric = 0.5 * (long_rows + flipped)
     first_row = ((((z * 4 + y) * 2 + xl) * 2 + core) * 2 + xh) * 40
     block_rows = (first_row + jnp.arange(40, dtype=jnp.int32)) // BLK
     block_count = pattern.shape[0]

time: 256 us -> 248 us (0.969)
  waiting for transfers between devices: 144 us -> 105 us
  local copies, waits for them, and re-layouts: 13.2 us -> 41.1 us
  matrix products: 11.5 us -> 15.6 us
    ppermute x31, waiting for transfers between devices: 109 us -> 87.6 us  [flip(): return lax.ppermute(value, AXES, pairs)]
    ppermute x7 -> x3, waiting for transfers between devices: 34.4 us -> 17.6 us  [remap(): return lax.ppermute(value, AXES, pairs)]
    all_to_all x0 -> x2, starting transfers between devices: none -> 9.69 us  [the longest x1 5.09 us: shards(): dslots = lax.all_to_all(cols, 'y', split_axis=0, concat_axis=0, tiled=True)]
    ppermute x7 -> x3, starting transfers between devices: 17.3 us -> 9.32 us  [remap(): return lax.ppermute(value, AXES, pairs)]
    unnamed x15 -> x44, local copies, waits for them, and re-layouts: 0.29 us -> 5.82 us
    slice x1 -> x5, local copies, waits for them, and re-layouts: 0.22 us -> 5.42 us  [the longest x2 2.7 us: ring_gather(): lower = flip(one[half:], **far)]
    dot_general x6 -> x7, matrix products: 11.3 us -> 15.4 us  [dot(): return jnp.dot(a, b, preferred_element_type=f32)]
    transpose x1 -> x3, local copies, waits for them, and re-layouts: 1.08 us -> 5.01 us  [the longest x1 2.08 us: shards(): turned = sorted_rows.astype(bf16).T.reshape(32, 40, 160)]
  transfers between devices with their start and end apart: 39 -> 37, of which waited for: 26 -> 20; matrix products, arithmetic and copies ran while one was open for 11% -> 16% of each run, Pallas kernels for 0% -> 0%
where the time goes in v1:
time: 248 us; the launch traced here: 246 us
  waiting for transfers between devices  105 us (42%)
  starting transfers between devices  64.8 us (26%)
  local copies, waits for them, and re-layouts  41.1 us (17%)
  other arithmetic  18.7 us (8%)
  matrix products  15.6 us (6%)
    ppermute x31, waiting for transfers between devices, flip(): return lax.ppermute(value, AXES, pairs)  87.6 us
    ppermute x31, starting transfers between devices, flip(): return lax.ppermute(value, AXES, pairs)  39.5 us
    ppermute x3, waiting for transfers between devices, remap(): return lax.ppermute(value, AXES, pairs)  17.6 us
    dot_general x7, matrix products, dot(): return jnp.dot(a, b, preferred_element_type=f32)  15.4 us
    ppermute x3, starting transfers between devices, remap(): return lax.ppermute(value, AXES, pairs)  9.32 us
    all_to_all x1, starting transfers between devices, shards(): lax.all_to_all(turned, ('z', 'xl', 'core', 'xh'), split_axis=0, concat_ax...  6.31 us
    another operation x5, local copies, waits for them, and re-layouts, shards(): direct = jnp.stack([rows[0]] + [flip(rows[q], y=q) for q in (1, 2, 3)])  5.88 us
    unnamed x44, local copies, waits for them, and re-layouts  5.82 us
  transfers between devices with their start and end apart: 37, of which 20 were waited for; matrix products, arithmetic and copies ran while one was open for 16% of the time, Pallas kernels for 0%

profile of v1, /device:TPU:2, one launch (start us, length us, event | category | flops | bytes accessed | tf_op | source)
XLA Modules:
  0.0 246.2 jit_solution(6010755237729828501)
XLA Ops:
  8.2 4.6 %all-to-all-start = ((bf16[4,160,640]{2,1,0:T(8,128)(2,1)}), bf16[4,160,640]{2,1,0:T(8,128)(2,1)}, u32[]{:S(2)}, u32[]{:S(2)}) async-start(bf16[4,160,640]{2,1,0:T(8,128)(2,1)} %pad_maximum_fusion.10), calls=%async_computation | async-start | bytes 1638400 | tf_op jit(solution)/shard_map/left_columns/all_to_all | solution.py:82
  14.8 7.3 %collective-permute-start.3 = (bf16[160,1280]{1,0:T(8,128)(2,1)S(1)}, bf16[160,1280]{1,0:T(8,128)(2,1)S(1)}, u32[]{:S(2)}, u32[]{:S(2)}) collective-permute-start(bf16[160,1280]{1,0:T(8,128)(2,1)S(1)} %copy-done.6), channel_id=1, source_target_pairs={{0,0},{1,32},{2,2},{3,34},{4,64},{5,96},{6,66},{7,98},{8,8},{9,40}... | collective-permute-start | bytes 1228808 | tf_op jit(solution)/shard_map/density_turn/ppermute | solution.py:40
  22.2 4.6 %collective-permute-done.1 = bf16[160,1280]{1,0:T(8,128)(2,1)S(1)} collective-permute-done((bf16[160,1280]{1,0:T(8,128)(2,1)S(1)}, bf16[160,1280]{1,0:T(8,128)(2,1)S(1)}, u32[]{:S(2)}, u32[]{:S(2)}) %collective-permute-start.1) | collective-permute-done | bytes 409632 | tf_op jit(solution)/shard_map/right_pair/ppermute | solution.py:40
  27.0 13.0 %collective-permute-done.3 = bf16[160,1280]{1,0:T(8,128)(2,1)S(1)} collective-permute-done((bf16[160,1280]{1,0:T(8,128)(2,1)S(1)}, bf16[160,1280]{1,0:T(8,128)(2,1)S(1)}, u32[]{:S(2)}, u32[]{:S(2)}) %collective-permute-start.3) | collective-permute-done | bytes 409632 | tf_op jit(solution)/shard_map/density_turn/ppermute | solution.py:40
  40.0 3.7 %collective-permute-start.6 = (bf16[320,1280]{1,0:T(8,128)(2,1)S(1)}, bf16[320,1280]{1,0:T(8,128)(2,1)S(1)}, u32[]{:S(2)}, u32[]{:S(2)}) collective-permute-start(bf16[320,1280]{1,0:T(8,128)(2,1)S(1)} %maximum_select_fusion), channel_id=1, source_target_pairs={{0,96},{1,97},{2,98},{3,99},{4,100},{5,101},{6,102},{7,103},{8,104... | collective-permute-start | bytes 2457608 | tf_op jit(solution)/shard_map/right_gather/ppermute | solution.py:26
  43.8 2.3 collective-permute-start.9
  46.6 15.0 %collective-permute-done.6 = bf16[320,1280]{1,0:T(8,128)(2,1)S(1)} collective-permute-done((bf16[320,1280]{1,0:T(8,128)(2,1)S(1)}, bf16[320,1280]{1,0:T(8,128)(2,1)S(1)}, u32[]{:S(2)}, u32[]{:S(2)}) %collective-permute-start.6) | collective-permute-done | bytes 819232 | tf_op jit(solution)/shard_map/right_gather/ppermute | solution.py:26
  63.7 2.4 collective-permute-start.8
  67.4 5.1 %all-to-all-start.1 = ((bf16[4,160,320]{2,1,0:T(8,128)(2,1)}), bf16[4,160,320]{2,1,0:T(8,128)(2,1)}, u32[]{:S(2)}, u32[]{:S(2)}) async-start(bf16[4,160,320]{2,1,0:T(8,128)(2,1)} %copy.330), calls=%async_computation.1 | async-start | bytes 983040 | tf_op jit(solution)/shard_map/density_columns/all_to_all | solution.py:107
  75.0 2.4 collective-permute-start.10
  79.8 2.1 pad_maximum_fusion.11
  81.9 2.1 pad_maximum_fusion
  90.0 2.6 %fusion.6 = f32[640,1280]{1,0:T(8,128)S(1)} fusion(bf16[320,1280]{1,0:T(8,128)(2,1)S(1)} %get-tuple-element.64, bf16[320,1280]{1,0:T(8,128)(2,1)S(1)} %get-tuple-element.65, bf16[640,640]{1,0:T(8,128)(2,1)} %collective-permute-done.9, bf16[640,640]{1,0:T(8,128)(2,1)S(1)} %constant_dynamic-update-slice_fusion, pred[]{:T(512)S(6)} %eq.23), kind=kOutput, calls=%fused_computation.12 | convolution fusion | flops 1052262400 | bytes 6553601 | tf_op jit(solution)/shard_map/first_product/dot_general | solution.py:58
  92.6 2.6 %convolution_add_fusion = f32[640,1280]{1,0:T(8,128)S(1)} fusion(f32[640,1280]{1,0:T(8,128)S(1)} %fusion.6, bf16[320,1280]{1,0:T(8,128)(2,1)S(1)} %get-tuple-element.66, bf16[320,1280]{1,0:T(8,128)(2,1)S(1)} %get-tuple-element.63, bf16[640,640]{1,0:T(8,128)(2,1)} %collective-permute-done.4, bf16[640,640]{1,0:T(8,128)(2,1)} %bitcast.12, pred[]{:T(512)S(6)} %eq.23), kind=kOutput, calls=%fused_computation.2 | convolution fusion | flops 1053081600 | bytes 9830401 | tf_op jit(solution)/shard_map/first_product/dot_general | solution.py:58
  98.3 2.7 %convolution_add_fusion.1 = f32[640,1280]{1,0:T(8,128)S(1)} fusion(f32[640,1280]{1,0:T(8,128)S(1)} %fusion.7, bf16[320,1280]{1,0:T(8,128)(2,1)S(1)} %get-tuple-element.66, bf16[320,1280]{1,0:T(8,128)(2,1)S(1)} %get-tuple-element.63, bf16[640,640]{1,0:T(8,128)(2,1)} %bitcast.12, bf16[640,640]{1,0:T(8,128)(2,1)} %collective-permute-done.4, pred[]{:T(512)S(6)} %eq.23), kind=kOutput, calls=%fused_computation.3 | convolution fusion | flops 1053081600 | bytes 9830401 | tf_op jit(solution)/shard_map/first_product/dot_general | solution.py:58
  106.0 8.2 %collective-permute-done.18 = f32[80,1280]{1,0:T(8,128)S(1)} collective-permute-done((f32[80,1280]{1,0:T(8,128)S(1)}, f32[80,1280]{1,0:T(8,128)S(1)}, u32[]{:S(2)}, u32[]{:S(2)}) %collective-permute-start.18) | collective-permute-done | bytes 409632 | tf_op jit(solution)/shard_map/mixed_sum/ppermute | solution.py:26
  114.4 3.0 %collective-permute-start.19 = (f32[160,1280]{1,0:T(8,128)S(1)}, f32[160,1280]{1,0:T(8,128)S(1)}, u32[]{:S(2)}, u32[]{:S(2)}) collective-permute-start(f32[160,1280]{1,0:T(8,128)S(1)} %pad_maximum_fusion.13), channel_id=1, source_target_pairs={{0,24},{1,25},{2,26},{3,27},{4,28},{5,29},{6,30},{7,31},{8,16},{9,... | collective-permute-start | bytes 2457608 | tf_op jit(solution)/shard_map/mixed_sum/ppermute | solution.py:26
  120.0 2.6 %collective-permute-start.22 = (bf16[4,160,320]{2,1,0:T(8,128)(2,1)}, bf16[4,160,320]{2,1,0:T(8,128)(2,1)S(1)}, u32[]{:S(2)}, u32[]{:S(2)}) collective-permute-start(bf16[4,160,320]{2,1,0:T(8,128)(2,1)} %all-to-all-done.1), channel_id=1, source_target_pairs={{0,96},{1,97},{2,98},{3,99},{4,100},{5,101},{6,102},{7,103},{8,104... | collective-permute-start | bytes 1228808 | tf_op jit(solution)/shard_map/density_gather/ppermute | solution.py:26
  122.6 9.7 %collective-permute-done.20 = bf16[4,160,320]{2,1,0:T(8,128)(2,1)S(1)} collective-permute-done((bf16[4,160,320]{2,1,0:T(8,128)(2,1)}, bf16[4,160,320]{2,1,0:T(8,128)(2,1)S(1)}, u32[]{:S(2)}, u32[]{:S(2)}) %collective-permute-start.20) | collective-permute-done | bytes 409632 | tf_op jit(solution)/shard_map/density_gather/ppermute | solution.py:26
  132.3 9.0 %collective-permute-done.21 = bf16[4,160,320]{2,1,0:T(8,128)(2,1)S(1)} collective-permute-done((bf16[4,160,320]{2,1,0:T(8,128)(2,1)}, bf16[4,160,320]{2,1,0:T(8,128)(2,1)S(1)}, u32[]{:S(2)}, u32[]{:S(2)}) %collective-permute-start.21) | collective-permute-done | bytes 409632 | tf_op jit(solution)/shard_map/density_gather/ppermute | solution.py:26
  141.3 2.6 %collective-permute-done.22 = bf16[4,160,320]{2,1,0:T(8,128)(2,1)S(1)} collective-permute-done((bf16[4,160,320]{2,1,0:T(8,128)(2,1)}, bf16[4,160,320]{2,1,0:T(8,128)(2,1)S(1)}, u32[]{:S(2)}, u32[]{:S(2)}) %collective-permute-start.22) | collective-permute-done | bytes 409632 | tf_op jit(solution)/shard_map/density_gather/ppermute | solution.py:26
  149.6 7.7 %collective-permute-done.23 = bf16[160,1280]{1,0:T(8,128)(2,1)S(1)} collective-permute-done((bf16[160,1280]{1,0:T(8,128)(2,1)S(1)}, bf16[160,1280]{1,0:T(8,128)(2,1)S(1)}, u32[]{:S(2)}, u32[]{:S(2)}) %collective-permute-start.23) | collective-permute-done | bytes 409632 | tf_op jit(solution)/shard_map/mixed_gather/ppermute | solution.py:26
  157.3 6.8 %collective-permute-done.24 = bf16[160,1280]{1,0:T(8,128)(2,1)S(1)} collective-permute-done((bf16[160,1280]{1,0:T(8,128)(2,1)S(1)}, bf16[160,1280]{1,0:T(8,128)(2,1)S(1)}, u32[]{:S(2)}, u32[]{:S(2)}) %collective-permute-start.24) | collective-permute-done | bytes 409632 | tf_op jit(solution)/shard_map/mixed_gather/ppermute | solution.py:26
  164.1 2.6 %collective-permute-done.25 = bf16[160,1280]{1,0:T(8,128)(2,1)S(1)} collective-permute-done((bf16[160,1280]{1,0:T(8,128)(2,1)S(1)}, bf16[160,1280]{1,0:T(8,128)(2,1)S(1)}, u32[]{:S(2)}, u32[]{:S(2)}) %collective-permute-start.25) | collective-permute-done | bytes 409632 | tf_op jit(solution)/shard_map/mixed_gather/ppermute | solution.py:26
  172.0 2.9 %fusion.48 = f32[640,640]{1,0:T(8,128)S(1)} fusion(bf16[640,1280]{1,0:T(8,128)(2,1)} %collective-permute-done.26, bf16[1280,640]{1,0:T(8,128)(2,1)S(1)} %maximum_dynamic-update-slice_fusion), kind=kOutput, calls=%fused_computation.165 | convolution fusion | flops 1048576000 | bytes 4915200 | tf_op jit(solution)/shard_map/second_product/dot_general | solution.py:58
  177.8 2.6 %collective-permute-start.28 = (bf16[320,640]{1,0:T(8,128)(2,1)}, bf16[320,640]{1,0:T(8,128)(2,1)}, u32[]{:S(2)}, u32[]{:S(2)}) collective-permute-start(bf16[320,640]{1,0:T(8,128)(2,1)} %bitcast.56), channel_id=1, source_target_pairs={{0,4},{1,5},{2,6},{3,7},{4,0},{5,1},{6,2},{7,3},{8,12},{9,13},{10,... | collective-permute-start | bytes 1228808 | tf_op jit(solution)/shard_map/second_product/ppermute | solution.py:26
  184.5 6.5 %collective-permute-done.28 = bf16[320,640]{1,0:T(8,128)(2,1)} collective-permute-done((bf16[320,640]{1,0:T(8,128)(2,1)}, bf16[320,640]{1,0:T(8,128)(2,1)}, u32[]{:S(2)}, u32[]{:S(2)}) %collective-permute-start.28) | collective-permute-done | bytes 409632 | tf_op jit(solution)/shard_map/second_product/ppermute | solution.py:26
  191.0 9.9 %collective-permute-done.29 = bf16[320,640]{1,0:T(8,128)(2,1)} collective-permute-done((bf16[320,640]{1,0:T(8,128)(2,1)}, bf16[320,640]{1,0:T(8,128)(2,1)}, u32[]{:S(2)}, u32[]{:S(2)}) %collective-permute-start.29) | collective-permute-done | bytes 409632 | tf_op jit(solution)/shard_map/second_product/ppermute | solution.py:26
  207.8 3.1 %collective-permute-start.32 = (f32[40,1280]{1,0:T(8,128)}, f32[40,1280]{1,0:T(8,128)}, u32[]{:S(2)}, u32[]{:S(2)}) collective-permute-start(f32[40,1280]{1,0:T(8,128)} %get-tuple-element.94), channel_id=1, source_target_pairs={{0,16},{1,17},{2,18},{3,19},{4,20},{5,21},{6,22},{7,23},{8,24},{9,... | collective-permute-start | bytes 614408 | tf_op jit(solution)/shard_map/direct/ppermute | solution.py:26
  213.8 6.3 %all-to-all-start.2 = ((bf16[32,40,160]{2,1,0:T(8,128)(2,1)}), bf16[32,40,160]{2,1,0:T(8,128)(2,1)}, u32[]{:S(2)}, u32[]{:S(2)}) async-start(bf16[32,40,160]{2,1,0:T(8,128)(2,1)} %bitcast.166), calls=%async_computation.2 | async-start | bytes 1310720 | tf_op jit(solution)/shard_map/transposed/all_to_all | solution.py:185
  234.7 2.9 %reshape.178 = f32[40,5120]{1,0:T(8,128)} reshape(f32[40,4,4,320]{3,2,1,0:T(4,128)} %copy.335) | data formatting | bytes 1638400 | tf_op jit(solution)/shard_map/direct/reshape | solution.py:195
  239.7 2.6 %dot_general.32 = bf16[4,40,1280]{2,1,0:T(8,128)(2,1)} reshape(bf16[4,40,8,160]{3,2,1,0:T(8,128)(2,1)} %copy.337) | data formatting | bytes 819200 | tf_op jit(solution)/shard_map/transposed/dot_general | solution.py:58
  (172 shorter events, 84.0 us)
Async XLA Ops:
  8.2 18.7 %all-to-all-start = ((bf16[4,160,640]{2,1,0:T(8,128)(2,1)}), bf16[4,160,640]{2,1,0:T(8,128)(2,1)}, u32[]{:S(2)}, u32[]{:S(2)}) async-start(bf16[4,160,640]{2,1,0:T(8,128)(2,1)} %pad_maximum_fusion.10), calls=%async_computation | async-start | bytes 1638400 | tf_op jit(solution)/shard_map/left_columns/all_to_all | solution.py:82
  12.8 9.4 %collective-permute-start = (bf16[160,1280]{1,0:T(8,128)(2,1)S(1)}, bf16[160,1280]{1,0:T(8,128)(2,1)S(1)}, u32[]{:S(2)}, u32[]{:S(2)}) collective-permute-start(bf16[160,1280]{1,0:T(8,128)(2,1)S(1)} %get-tuple-element.30), channel_id=1, source_target_pairs={{0,0},{1,1},{2,4},{3,5},{4,2},{5,3},{6,6},{7,7},{8,8},{9,9},{10,12... | collective-permute-start | bytes 1228808 | tf_op jit(solution)/shard_map/right_pair/ppermute | solution.py:40
  14.7 12.1 %collective-permute-start.1 = (bf16[160,1280]{1,0:T(8,128)(2,1)S(1)}, bf16[160,1280]{1,0:T(8,128)(2,1)S(1)}, u32[]{:S(2)}, u32[]{:S(2)}) collective-permute-start(bf16[160,1280]{1,0:T(8,128)(2,1)S(1)} %get-tuple-element.31), channel_id=1, source_target_pairs={{0,2},{1,3},{2,6},{3,7},{4,0},{5,1},{6,4},{7,5},{8,10},{9,11},{10,... | collective-permute-start | bytes 1228808 | tf_op jit(solution)/shard_map/right_pair/ppermute | solution.py:40
  14.8 25.1 %collective-permute-start.3 = (bf16[160,1280]{1,0:T(8,128)(2,1)S(1)}, bf16[160,1280]{1,0:T(8,128)(2,1)S(1)}, u32[]{:S(2)}, u32[]{:S(2)}) collective-permute-start(bf16[160,1280]{1,0:T(8,128)(2,1)S(1)} %copy-done.6), channel_id=1, source_target_pairs={{0,0},{1,32},{2,2},{3,34},{4,64},{5,96},{6,66},{7,98},{8,8},{9,40}... | collective-permute-start | bytes 1228808 | tf_op jit(solution)/shard_map/density_turn/ppermute | solution.py:40
  40.0 21.6 %collective-permute-start.6 = (bf16[320,1280]{1,0:T(8,128)(2,1)S(1)}, bf16[320,1280]{1,0:T(8,128)(2,1)S(1)}, u32[]{:S(2)}, u32[]{:S(2)}) collective-permute-start(bf16[320,1280]{1,0:T(8,128)(2,1)S(1)} %maximum_select_fusion), channel_id=1, source_target_pairs={{0,96},{1,97},{2,98},{3,99},{4,100},{5,101},{6,102},{7,103},{8,104... | collective-permute-start | bytes 2457608 | tf_op jit(solution)/shard_map/right_gather/ppermute | solution.py:26
  43.7 19.1 %collective-permute-start.5 = (bf16[320,1280]{1,0:T(8,128)(2,1)S(1)}, bf16[320,1280]{1,0:T(8,128)(2,1)S(1)}, u32[]{:S(2)}, u32[]{:S(2)}) collective-permute-start(bf16[320,1280]{1,0:T(8,128)(2,1)S(1)} %maximum_select_fusion), channel_id=1, source_target_pairs={{0,32},{1,33},{2,34},{3,35},{4,36},{5,37},{6,38},{7,39},{8,40},{9,... | collective-permute-start | bytes 2457608 | tf_op jit(solution)/shard_map/right_gather/ppermute | solution.py:26
  43.8 29.4 %collective-permute-start.9 = (bf16[640,640]{1,0:T(8,128)(2,1)}, bf16[640,640]{1,0:T(8,128)(2,1)}, u32[]{:S(2)}, u32[]{:S(2)}) collective-permute-start(bf16[640,640]{1,0:T(8,128)(2,1)} %bitcast.12), channel_id=1, source_target_pairs={{0,5},{1,4},{2,7},{3,6},{4,1},{5,0},{6,3},{7,2},{8,13},{9,12},{10,... | collective-permute-start | bytes 2457608 | tf_op jit(solution)/shard_map/left_gather/ppermute | solution.py:26
  46.1 31.3 %collective-permute-start.4 = (bf16[640,640]{1,0:T(8,128)(2,1)}, bf16[640,640]{1,0:T(8,128)(2,1)}, u32[]{:S(2)}, u32[]{:S(2)}) collective-permute-start(bf16[640,640]{1,0:T(8,128)(2,1)} %bitcast.12), channel_id=1, source_target_pairs={{0,4},{1,5},{2,6},{3,7},{4,0},{5,1},{6,2},{7,3},{8,12},{9,13},{10,... | collective-permute-start | bytes 2457608 | tf_op jit(solution)/shard_map/left_gather/ppermute | solution.py:26
  62.5 17.3 %collective-permute-start.7 = (bf16[160,1280]{1,0:T(8,128)(2,1)}, bf16[160,1280]{1,0:T(8,128)(2,1)}, u32[]{:S(2)}, u32[]{:S(2)}) collective-permute-start(bf16[160,1280]{1,0:T(8,128)(2,1)} %slice.176), channel_id=1, source_target_pairs={{0,32},{1,33},{2,34},{3,35},{4,36},{5,37},{6,38},{7,39},{8,40},{9,... | collective-permute-start | bytes 1228808 | tf_op jit(solution)/shard_map/right_gather/ppermute | solution.py:26
  63.7 16.1 %collective-permute-start.8 = (bf16[160,1280]{1,0:T(8,128)(2,1)}, bf16[160,1280]{1,0:T(8,128)(2,1)}, u32[]{:S(2)}, u32[]{:S(2)}) collective-permute-start(bf16[160,1280]{1,0:T(8,128)(2,1)} %slice.177), channel_id=1, source_target_pairs={{0,96},{1,97},{2,98},{3,99},{4,100},{5,101},{6,102},{7,103},{8,104... | collective-permute-start | bytes 1228808 | tf_op jit(solution)/shard_map/right_gather/ppermute | solution.py:26
  67.4 14.5 %all-to-all-start.1 = ((bf16[4,160,320]{2,1,0:T(8,128)(2,1)}), bf16[4,160,320]{2,1,0:T(8,128)(2,1)}, u32[]{:S(2)}, u32[]{:S(2)}) async-start(bf16[4,160,320]{2,1,0:T(8,128)(2,1)} %copy.330), calls=%async_computation.1 | async-start | bytes 983040 | tf_op jit(solution)/shard_map/density_columns/all_to_all | solution.py:107
  75.0 10.7 %collective-permute-start.10 = (bf16[320,640]{1,0:T(8,128)(2,1)}, bf16[320,640]{1,0:T(8,128)(2,1)}, u32[]{:S(2)}, u32[]{:S(2)}) collective-permute-start(bf16[320,640]{1,0:T(8,128)(2,1)} %slice.178), channel_id=1, source_target_pairs={{0,4},{1,5},{2,6},{3,7},{4,0},{5,1},{6,2},{7,3},{8,12},{9,13},{10,... | collective-permute-start | bytes 1228808 | tf_op jit(solution)/shard_map/left_gather/ppermute | solution.py:26
  79.2 9.7 %collective-permute-start.11 = (bf16[320,640]{1,0:T(8,128)(2,1)}, bf16[320,640]{1,0:T(8,128)(2,1)}, u32[]{:S(2)}, u32[]{:S(2)}) collective-permute-start(bf16[320,640]{1,0:T(8,128)(2,1)} %slice.179), channel_id=1, source_target_pairs={{0,5},{1,4},{2,7},{3,6},{4,1},{5,0},{6,3},{7,2},{8,13},{9,12},{10,... | collective-permute-start | bytes 1228808 | tf_op jit(solution)/shard_map/left_gather/ppermute | solution.py:26
  95.6 5.4 %collective-permute-start.12 = (f32[160,1280]{1,0:T(8,128)S(1)}, f32[160,1280]{1,0:T(8,128)S(1)}, u32[]{:S(2)}, u32[]{:S(2)}) collective-permute-start(f32[160,1280]{1,0:T(8,128)S(1)} %get-tuple-element.59), channel_id=1, source_target_pairs={{0,2},{1,3},{2,0},{3,1},{4,6},{5,7},{6,4},{7,5},{8,10},{9,11},{10,... | collective-permute-start | bytes 2457608 | tf_op jit(solution)/shard_map/mixed_sum/ppermute | solution.py:26
  96.4 5.2 %collective-permute-start.17 = (f32[160,1280]{1,0:T(8,128)S(1)}, f32[160,1280]{1,0:T(8,128)S(1)}, u32[]{:S(2)}, u32[]{:S(2)}) collective-permute-start(f32[160,1280]{1,0:T(8,128)S(1)} %get-tuple-element.60), channel_id=1, source_target_pairs={{0,2},{1,3},{2,0},{3,1},{4,6},{5,7},{6,4},{7,5},{8,10},{9,11},{10,... | collective-permute-start | bytes 2457608 | tf_op jit(solution)/shard_map/mixed_sum/ppermute | solution.py:26
  102.2 12.1 %collective-permute-start.18 = (f32[80,1280]{1,0:T(8,128)S(1)}, f32[80,1280]{1,0:T(8,128)S(1)}, u32[]{:S(2)}, u32[]{:S(2)}) collective-permute-start(f32[80,1280]{1,0:T(8,128)S(1)} %get-tuple-element.103), channel_id=1, source_target_pairs={{0,8},{1,9},{2,10},{3,11},{4,12},{5,13},{6,14},{7,15},{8,0},{9,1},... | collective-permute-start | bytes 1228808 | tf_op jit(solution)/shard_map/mixed_sum/ppermute | solution.py:26
  104.0 13.4 %collective-permute-start.15 = (f32[80,1280]{1,0:T(8,128)S(1)}, f32[80,1280]{1,0:T(8,128)S(1)}, u32[]{:S(2)}, u32[]{:S(2)}) collective-permute-start(f32[80,1280]{1,0:T(8,128)S(1)} %get-tuple-element.104), channel_id=1, source_target_pairs={{0,24},{1,25},{2,26},{3,27},{4,28},{5,29},{6,30},{7,31},{8,16},{9,... | collective-permute-start | bytes 1228808 | tf_op jit(solution)/shard_map/mixed_sum/ppermute | solution.py:26
  114.4 29.5 %collective-permute-start.19 = (f32[160,1280]{1,0:T(8,128)S(1)}, f32[160,1280]{1,0:T(8,128)S(1)}, u32[]{:S(2)}, u32[]{:S(2)}) collective-permute-start(f32[160,1280]{1,0:T(8,128)S(1)} %pad_maximum_fusion.13), channel_id=1, source_target_pairs={{0,24},{1,25},{2,26},{3,27},{4,28},{5,29},{6,30},{7,31},{8,16},{9,... | collective-permute-start | bytes 2457608 | tf_op jit(solution)/shard_map/mixed_sum/ppermute | solution.py:26
  117.6 27.1 %collective-permute-start.16 = (f32[160,1280]{1,0:T(8,128)S(1)}, f32[160,1280]{1,0:T(8,128)S(1)}, u32[]{:S(2)}, u32[]{:S(2)}) collective-permute-start(f32[160,1280]{1,0:T(8,128)S(1)} %pad_maximum_fusion.12), channel_id=1, source_target_pairs={{0,8},{1,9},{2,10},{3,11},{4,12},{5,13},{6,14},{7,15},{8,0},{9,1},... | collective-permute-start | bytes 2457608 | tf_op jit(solution)/shard_map/mixed_sum/ppermute | solution.py:26
  117.9 14.4 %collective-permute-start.20 = (bf16[4,160,320]{2,1,0:T(8,128)(2,1)}, bf16[4,160,320]{2,1,0:T(8,128)(2,1)S(1)}, u32[]{:S(2)}, u32[]{:S(2)}) collective-permute-start(bf16[4,160,320]{2,1,0:T(8,128)(2,1)} %all-to-all-done.1), channel_id=1, source_target_pairs={{0,32},{1,33},{2,34},{3,35},{4,36},{5,37},{6,38},{7,39},{8,40},{9,... | collective-permute-start | bytes 1228808 | tf_op jit(solution)/shard_map/density_gather/ppermute | solution.py:26
  119.0 22.3 %collective-permute-start.21 = (bf16[4,160,320]{2,1,0:T(8,128)(2,1)}, bf16[4,160,320]{2,1,0:T(8,128)(2,1)S(1)}, u32[]{:S(2)}, u32[]{:S(2)}) collective-permute-start(bf16[4,160,320]{2,1,0:T(8,128)(2,1)} %all-to-all-done.1), channel_id=1, source_target_pairs={{0,64},{1,65},{2,66},{3,67},{4,68},{5,69},{6,70},{7,71},{8,72},{9,... | collective-permute-start | bytes 1228808 | tf_op jit(solution)/shard_map/density_gather/ppermute | solution.py:26
  120.0 23.9 %collective-permute-start.22 = (bf16[4,160,320]{2,1,0:T(8,128)(2,1)}, bf16[4,160,320]{2,1,0:T(8,128)(2,1)S(1)}, u32[]{:S(2)}, u32[]{:S(2)}) collective-permute-start(bf16[4,160,320]{2,1,0:T(8,128)(2,1)} %all-to-all-done.1), channel_id=1, source_target_pairs={{0,96},{1,97},{2,98},{3,99},{4,100},{5,101},{6,102},{7,103},{8,104... | collective-permute-start | bytes 1228808 | tf_op jit(solution)/shard_map/density_gather/ppermute | solution.py:26
  144.8 12.5 %collective-permute-start.23 = (bf16[160,1280]{1,0:T(8,128)(2,1)S(1)}, bf16[160,1280]{1,0:T(8,128)(2,1)S(1)}, u32[]{:S(2)}, u32[]{:S(2)}) collective-permute-start(bf16[160,1280]{1,0:T(8,128)(2,1)S(1)} %add_convert_fusion), channel_id=1, source_target_pairs={{0,8},{1,9},{2,10},{3,11},{4,12},{5,13},{6,14},{7,15},{8,0},{9,1},... | collective-permute-start | bytes 1228808 | tf_op jit(solution)/shard_map/mixed_gather/ppermute | solution.py:26
  146.6 17.6 %collective-permute-start.24 = (bf16[160,1280]{1,0:T(8,128)(2,1)S(1)}, bf16[160,1280]{1,0:T(8,128)(2,1)S(1)}, u32[]{:S(2)}, u32[]{:S(2)}) collective-permute-start(bf16[160,1280]{1,0:T(8,128)(2,1)S(1)} %add_convert_fusion), channel_id=1, source_target_pairs={{0,16},{1,17},{2,18},{3,19},{4,20},{5,21},{6,22},{7,23},{8,24},{9,... | collective-permute-start | bytes 1228808 | tf_op jit(solution)/shard_map/mixed_gather/ppermute | solution.py:26
  147.9 18.8 %collective-permute-start.25 = (bf16[160,1280]{1,0:T(8,128)(2,1)S(1)}, bf16[160,1280]{1,0:T(8,128)(2,1)S(1)}, u32[]{:S(2)}, u32[]{:S(2)}) collective-permute-start(bf16[160,1280]{1,0:T(8,128)(2,1)S(1)} %add_convert_fusion), channel_id=1, source_target_pairs={{0,24},{1,25},{2,26},{3,27},{4,28},{5,29},{6,30},{7,31},{8,16},{9,... | collective-permute-start | bytes 1228808 | tf_op jit(solution)/shard_map/mixed_gather/ppermute | solution.py:26
  177.8 13.2 %collective-permute-start.28 = (bf16[320,640]{1,0:T(8,128)(2,1)}, bf16[320,640]{1,0:T(8,128)(2,1)}, u32[]{:S(2)}, u32[]{:S(2)}) collective-permute-start(bf16[320,640]{1,0:T(8,128)(2,1)} %bitcast.56), channel_id=1, source_target_pairs={{0,4},{1,5},{2,6},{3,7},{4,0},{5,1},{6,2},{7,3},{8,12},{9,13},{10,... | collective-permute-start | bytes 1228808 | tf_op jit(solution)/shard_map/second_product/ppermute | solution.py:26
  180.5 20.4 %collective-permute-start.29 = (bf16[320,640]{1,0:T(8,128)(2,1)}, bf16[320,640]{1,0:T(8,128)(2,1)}, u32[]{:S(2)}, u32[]{:S(2)}) collective-permute-start(bf16[320,640]{1,0:T(8,128)(2,1)} %bitcast.57), channel_id=1, source_target_pairs={{0,5},{1,4},{2,7},{3,6},{4,1},{5,0},{6,3},{7,2},{8,13},{9,12},{10,... | collective-permute-start | bytes 1228808 | tf_op jit(solution)/shard_map/second_product/ppermute | solution.py:26
  181.8 19.1 %collective-permute-start.27 = (bf16[320,640]{1,0:T(8,128)(2,1)}, bf16[320,640]{1,0:T(8,128)(2,1)}, u32[]{:S(2)}, u32[]{:S(2)}) collective-permute-start(bf16[320,640]{1,0:T(8,128)(2,1)} %bitcast.54), channel_id=1, source_target_pairs={{0,1},{1,0},{2,3},{3,2},{4,5},{5,4},{6,7},{7,6},{8,9},{9,8},{10,11... | collective-permute-start | bytes 1228808 | tf_op jit(solution)/shard_map/second_product/ppermute | solution.py:26
  207.8 15.8 %collective-permute-start.31 = (f32[40,1280]{1,0:T(8,128)}, f32[40,1280]{1,0:T(8,128)}, u32[]{:S(2)}, u32[]{:S(2)}) collective-permute-start(f32[40,1280]{1,0:T(8,128)} %get-tuple-element.95), channel_id=1, source_target_pairs={{0,8},{1,9},{2,10},{3,11},{4,12},{5,13},{6,14},{7,15},{8,0},{9,1},... | collective-permute-start | bytes 614408 | tf_op jit(solution)/shard_map/direct/ppermute | solution.py:26
  207.8 16.9 %collective-permute-start.32 = (f32[40,1280]{1,0:T(8,128)}, f32[40,1280]{1,0:T(8,128)}, u32[]{:S(2)}, u32[]{:S(2)}) collective-permute-start(f32[40,1280]{1,0:T(8,128)} %get-tuple-element.94), channel_id=1, source_target_pairs={{0,16},{1,17},{2,18},{3,19},{4,20},{5,21},{6,22},{7,23},{8,24},{9,... | collective-permute-start | bytes 614408 | tf_op jit(solution)/shard_map/direct/ppermute | solution.py:26
  213.8 23.8 %all-to-all-start.2 = ((bf16[32,40,160]{2,1,0:T(8,128)(2,1)}), bf16[32,40,160]{2,1,0:T(8,128)(2,1)}, u32[]{:S(2)}, u32[]{:S(2)}) async-start(bf16[32,40,160]{2,1,0:T(8,128)(2,1)} %bitcast.166), calls=%async_computation.2 | async-start | bytes 1310720 | tf_op jit(solution)/shard_map/transposed/all_to_all | solution.py:185
  221.2 8.7 %collective-permute-start.33 = (f32[40,1280]{1,0:T(8,128)}, f32[40,1280]{1,0:T(8,128)}, u32[]{:S(2)}, u32[]{:S(2)}) collective-permute-start(f32[40,1280]{1,0:T(8,128)} %get-tuple-element.93), channel_id=1, source_target_pairs={{0,24},{1,25},{2,26},{3,27},{4,28},{5,29},{6,30},{7,31},{8,16},{9,... | collective-permute-start | bytes 614408 | tf_op jit(solution)/shard_map/direct/ppermute | solution.py:26
  (25 other events, 222.1 us)

commit v2 on v1

--- a/solution.py
+++ b/solution.py
@@ -65,36 +65,39 @@
         keep = jnp.where(core == 0, dens_resp, density)
         send = jnp.where(core == 0, density, dens_resp)
         came = flip(send, core=1)
-    with jax.named_scope("right_pair"):
-        rounds = []
-        for turn in range(2):
-            chosen = jnp.where((xl ^ turn) == 0, fock, fock_resp)
-            chosen, _ = lax.optimization_barrier((chosen, send))
-            rounds.append(
-                remap(chosen, lambda a, b, c, d, e: (a, b, d, c ^ turn, e))
-            )
+    with jax.named_scope("right_columns"):
+        at = jnp.arange(1280, dtype=jnp.int32)
+        to = at // 160 % 2 * 640 + at // 40 % 2 * 320 + at // 320 * 80 + at // 80 % 2 * 40 + at % 40
+        order = (to[:, None] == at[None, :]).astype(bf16)
+        both_right = jnp.concatenate((fock, fock_resp))
+        parts = [
+            dot(both_right, order[:, j * 320 : (j + 1) * 320]).astype(bf16).reshape(2, 1, 160, 320)
+            for j in range(4)
+        ]
+        parts = jnp.concatenate(
+            [jnp.concatenate((parts[2 * j], parts[2 * j + 1]), axis=1) for j in range(2)]
+        )
+        parts, _ = lax.optimization_barrier((parts, send))
+        rounds = lax.all_to_all(
+            parts.reshape(8, 160, 320), ("xl", "core", "xh"), split_axis=0, concat_axis=0, tiled=True
+        )
+    with jax.named_scope("density_turn"):
+        halves, _ = lax.optimization_barrier((density.reshape(2, 2, 40, 1280), send))
+        same = lax.dynamic_index_in_dim(halves, xh, 1, keepdims=False).reshape(80, 4, 320)
+        other = lax.dynamic_index_in_dim(halves, 1 - xh, 1, keepdims=False).reshape(80, 1280)
+        other = flip(other, xh=1).reshape(80, 4, 320)
     with jax.named_scope("left_columns"):
         low = jnp.where(core == 0, keep, came).reshape(160, 4, 320)
         high = jnp.where(core == 0, came, keep).reshape(160, 4, 320)
         pieces = jnp.stack(
             [jnp.concatenate((low[:, j], high[:, j]), axis=1) for j in range(4)]
         )
-        left = lax.all_to_all(pieces, "y", split_axis=0, concat_axis=0, tiled=True)
-        left = left.reshape(640, 640)
-    with jax.named_scope("density_turn"):
-        turned, _ = lax.optimization_barrier((density, send))
-        turned = remap(
-            turned,
-            lambda a, b, c, d, e: (c * 2 + e, b, a // 2, d, a % 2),
+        left = jnp.concatenate(
+            [pick(pieces, y)] + [flip(pick(pieces, y ^ q), y=q) for q in (1, 2, 3)]
         )
     with jax.named_scope("right_gather"):
-        rounds, left = lax.optimization_barrier((rounds, left))
-        right = jnp.where(
-            core == 0,
-            jnp.concatenate((rounds[0], rounds[1])),
-            jnp.concatenate((rounds[1], rounds[0])),
-        )
-        right, left, turned = lax.optimization_barrier((right, left, turned))
+        right = rounds.reshape(2, 4, 160, 320).transpose(0, 2, 1, 3).reshape(320, 1280)
+        right, left = lax.optimization_barrier((right, left))
         one, three, two = ring_gather(right, ({"z": 1}, {"z": 3}))
         rights = [right, one, two, three]
     with jax.named_scope("left_gather"):
@@ -102,9 +105,14 @@
         lefts = {(0, 0): left, (1, 0): one, (0, 1): two, (1, 1): three}
 
     with jax.named_scope("density_columns"):
-        turned, rights[1], rights[3] = lax.optimization_barrier((turned, rights[1], rights[3]))
-        cols = turned.reshape(160, 4, 320).transpose(1, 0, 2)
+        same, other, rights[2] = lax.optimization_barrier((same, other, rights[2]))
+        first = jnp.where(xh == 0, same, other)
+        second = jnp.where(xh == 0, other, same)
+        cols = jnp.stack(
+            [jnp.concatenate((first[:, j], second[:, j]), axis=1) for j in range(4)]
+        )
         dslots = lax.all_to_all(cols, "y", split_axis=0, concat_axis=0, tiled=True)
+        dslots = dslots.reshape(320, 640)
 
     with jax.named_scope("swap_matrix"):
         at = jnp.arange(1280, dtype=jnp.int32)
@@ -114,18 +122,21 @@
     with jax.named_scope("first_product"):
         rights, dslots, swap = lax.optimization_barrier((rights, dslots, swap))
         rights = jnp.stack(rights)
-        rsel = [
-            jnp.concatenate([pick(rights, z ^ (nzh * 2 + (xh ^ r))) for nzh in range(2)])
-            for r in range(2)
-        ]
+        rsel = jnp.concatenate(
+            [
+                pick(rights, z ^ (nzh * 2 + (xh ^ r)))
+                for r in range(2)
+                for nzh in range(2)
+            ]
+        )
         theirs = [jnp.where(core == 0, lefts[1, r], lefts[0, r]) for r in range(2)]
         mine = [jnp.where(core == 0, lefts[0, r], lefts[1, r]) for r in range(2)]
-        theirs = (dot(theirs[0], rsel[0]) + dot(theirs[1], rsel[1])).reshape(4, 160, 1280)
-        mine = (dot(mine[0], rsel[0]) + dot(mine[1], rsel[1])).reshape(4, 160, 1280)
+        theirs = dot(jnp.concatenate(theirs, axis=1), rsel).reshape(4, 160, 1280)
+        mine = dot(jnp.concatenate(mine, axis=1), rsel).reshape(4, 160, 1280)
     with jax.named_scope("mixed_sum"):
         both = [None] * 4
         for q in (2, 1, 3, 0):
-            both[q] = pick(mine, y ^ q) + flip(pick(theirs, y ^ q), core=1)
+            both[q] = mine[q] + flip(theirs[q], core=1)
         upper = flip(both[2][:80], y=1)
         lower = flip(both[2][80:], y=3)
         third = jnp.concatenate((both[3][:80] + upper, both[3][80:]))
@@ -143,16 +154,7 @@
 
     with jax.named_scope("density_rows"):
         dparts = jnp.stack(dparts)
-        dfull = jnp.concatenate(
-            [
-                jnp.concatenate(
-                    [pick(dparts, z ^ (nxl * 2 + nzl))[ny] for nzl in range(2)],
-                    axis=1,
-                )
-                for ny in range(4)
-                for nxl in range(2)
-            ]
-        )
+        dfull = jnp.concatenate([pick(dparts, z ^ nz) for nz in range(4)])
 
     with jax.named_scope("mixed_gather"):
         mslots = jnp.concatenate([mixed] + [flip(mixed, y=q) for q in (1, 2, 3)])

time: 248 us -> 246 us (level)
  waiting for transfers between devices: 105 us -> 93.2 us
  local copies, waits for them, and re-layouts: 41.1 us -> 51.1 us
  other arithmetic: 18.7 us -> 27.1 us
  starting transfers between devices: 64.8 us -> 57.2 us
    ppermute x3 -> x0, waiting for transfers between devices: 17.6 us -> none  [remap(): return lax.ppermute(value, AXES, pairs)]
    ppermute x3 -> x0, starting transfers between devices: 9.32 us -> none  [remap(): return lax.ppermute(value, AXES, pairs)]
    select_n x2 -> x3, other arithmetic: 0.27 us -> 5.25 us  [the longest x2 5.2 us: shards(): mine = [jnp.where(core == 0, lefts[0, r], lefts[1, r]) for r in range(2)]]
    reshape x1 -> x4, local copies, waits for them, and re-layouts: 0.54 us -> 5.31 us  [the longest x2 2.17 us: shards(): rounds.reshape(2, 4, 160, 320).transpose(0, 2, 1, 3).reshape(320, 1280)]
    all_to_all x1, waiting for transfers between devices: 0.01 us -> 2.94 us  [shards(): dslots = lax.all_to_all(cols, 'y', split_axis=0, concat_axis=0, tiled=True)]
    ppermute x31 -> x35, waiting for transfers between devices: 87.6 us -> 90.2 us  [flip(): return lax.ppermute(value, AXES, pairs)]
    ppermute x31 -> x35, starting transfers between devices: 39.5 us -> 41.6 us  [flip(): return lax.ppermute(value, AXES, pairs)]
    dot_general x7 -> x9, matrix products: 15.4 us -> 14 us  [dot(): return jnp.dot(a, b, preferred_element_type=f32)]
  transfers between devices with their start and end apart: 37 -> 38, of which waited for: 20 -> 20; matrix products, arithmetic and copies ran while one was open for 16% -> 26% of each run, Pallas kernels for 0% -> 0%
where the time goes in v2:
time: 246 us; the launch traced here: 244 us
  waiting for transfers between devices  93.2 us (38%)
  starting transfers between devices  57.2 us (23%)
  local copies, waits for them, and re-layouts  51.1 us (21%)
  other arithmetic  27.1 us (11%)
  matrix products  14.2 us (6%)
    ppermute x35, waiting for transfers between devices, flip(): return lax.ppermute(value, AXES, pairs)  90.2 us
    ppermute x35, starting transfers between devices, flip(): return lax.ppermute(value, AXES, pairs)  41.6 us
    dot_general x9, matrix products, dot(): return jnp.dot(a, b, preferred_element_type=f32)  14 us
    unnamed x57, local copies, waits for them, and re-layouts  7.21 us
    all_to_all x1, starting transfers between devices, shards(): lax.all_to_all(turned, ('z', 'xl', 'core', 'xh'), split_axis=0, concat_ax...  6.63 us
    another operation x5, local copies, waits for them, and re-layouts, shards(): direct = jnp.stack([rows[0]] + [flip(rows[q], y=q) for q in (1, 2, 3)])  5.86 us
    select_n x2, other arithmetic, shards(): mine = [jnp.where(core == 0, lefts[0, r], lefts[1, r]) for r in range(2)]  5.2 us
    all_to_all x1, starting transfers between devices, shards(): lax.all_to_all(parts.reshape(8, 160, 320), ('xl', 'core', 'xh'), split_ax...  4.94 us
  transfers between devices with their start and end apart: 38, of which 20 were waited for; matrix products, arithmetic and copies ran while one was open for 26% of the time, Pallas kernels for 0%

profile of v2, /device:TPU:2, one launch (start us, length us, event | category | flops | bytes accessed | tf_op | source)
XLA Modules:
  0.0 243.5 jit_solution(5549729960793986815)
XLA Ops:
  8.8 4.9 %all-to-all-start = ((bf16[8,160,320]{2,1,0:T(8,128)(2,1)}), bf16[8,160,320]{2,1,0:T(8,128)(2,1)S(1)}, u32[]{:S(2)}, u32[]{:S(2)}) async-start(bf16[8,160,320]{2,1,0:T(8,128)(2,1)} %bitcast.8), calls=%async_computation | async-start | bytes 1966080 | tf_op jit(solution)/shard_map/right_columns/all_to_all | solution.py:81
  19.8 2.9 %collective-permute-start.2 = (bf16[160,640]{1,0:T(8,128)(2,1)S(1)}, bf16[160,640]{1,0:T(8,128)(2,1)S(1)}, u32[]{:S(2)}, u32[]{:S(2)}) collective-permute-start(bf16[160,640]{1,0:T(8,128)(2,1)S(1)} %get-tuple-element.91), channel_id=1, source_target_pairs={{0,16},{1,17},{2,18},{3,19},{4,20},{5,21},{6,22},{7,23},{8,24},{9,... | collective-permute-start | bytes 614408 | tf_op jit(solution)/shard_map/left_columns/ppermute | solution.py:26
  26.2 6.2 %collective-permute-done.2 = bf16[160,640]{1,0:T(8,128)(2,1)S(1)} collective-permute-done((bf16[160,640]{1,0:T(8,128)(2,1)S(1)}, bf16[160,640]{1,0:T(8,128)(2,1)S(1)}, u32[]{:S(2)}, u32[]{:S(2)}) %collective-permute-start.2) | collective-permute-done | bytes 204832 | tf_op jit(solution)/shard_map/left_columns/ppermute | solution.py:26
  32.3 2.6 %collective-permute-done.3 = bf16[160,640]{1,0:T(8,128)(2,1)S(1)} collective-permute-done((bf16[160,640]{1,0:T(8,128)(2,1)S(1)}, bf16[160,640]{1,0:T(8,128)(2,1)S(1)}, u32[]{:S(2)}, u32[]{:S(2)}) %collective-permute-start.3) | collective-permute-done | bytes 204832 | tf_op jit(solution)/shard_map/left_columns/ppermute | solution.py:26
  38.0 4.0 %collective-permute-start.10 = (bf16[320,1280]{1,0:T(8,128)(2,1)}, bf16[320,1280]{1,0:T(8,128)(2,1)}, u32[]{:S(2)}, u32[]{:S(2)}) collective-permute-start(bf16[320,1280]{1,0:T(8,128)(2,1)} %reshape.247), channel_id=1, source_target_pairs={{0,96},{1,97},{2,98},{3,99},{4,100},{5,101},{6,102},{7,103},{8,104... | collective-permute-start | bytes 2457608 | tf_op jit(solution)/shard_map/right_gather/ppermute | solution.py:26
  42.4 2.3 collective-permute-start.5
  45.3 14.4 %collective-permute-done.10 = bf16[320,1280]{1,0:T(8,128)(2,1)} collective-permute-done((bf16[320,1280]{1,0:T(8,128)(2,1)}, bf16[320,1280]{1,0:T(8,128)(2,1)}, u32[]{:S(2)}, u32[]{:S(2)}) %collective-permute-start.10) | collective-permute-done | bytes 819232 | tf_op jit(solution)/shard_map/right_gather/ppermute | solution.py:26
  63.3 3.0 %collective-permute-start.12 = (bf16[160,1280]{1,0:T(8,128)(2,1)}, bf16[160,1280]{1,0:T(8,128)(2,1)}, u32[]{:S(2)}, u32[]{:S(2)}) collective-permute-start(bf16[160,1280]{1,0:T(8,128)(2,1)} %slice.191), channel_id=1, source_target_pairs={{0,96},{1,97},{2,98},{3,99},{4,100},{5,101},{6,102},{7,103},{8,104... | collective-permute-start | bytes 1228808 | tf_op jit(solution)/shard_map/right_gather/ppermute | solution.py:26
  75.3 2.1 collective-permute-start.7
  77.5 2.7 %broadcast_select_fusion.5 = (bf16[640,640]{1,0:T(8,128)(2,1)}, bf16[640,640]{1,0:T(8,128)(2,1)}) fusion(bf16[640,640]{1,0:T(8,128)(2,1)} %pad_maximum_fusion.7, bf16[640,640]{1,0:T(8,128)(2,1)} %collective-permute-done.4, pred[]{:T(512)S(6)} %eq.85), kind=kLoop, calls=%fused_computation.61 | loop fusion | flops 819200 | bytes 3276801 | tf_op jit(solution)/shard_map/first_product/jit(_where)/select_n | solution.py:133
  84.4 4.1 %all-to-all-start.1 = ((bf16[4,80,640]{2,1,0:T(8,128)(2,1)}), bf16[4,80,640]{2,1,0:T(8,128)(2,1)}, u32[]{:S(2)}, u32[]{:S(2)}) async-start(bf16[4,80,640]{2,1,0:T(8,128)(2,1)} %pad_maximum_fusion.13), calls=%async_computation.1 | async-start | bytes 819200 | tf_op jit(solution)/shard_map/density_columns/all_to_all | solution.py:114
  90.7 2.5 %broadcast_select_fusion.4 = (bf16[640,640]{1,0:T(8,128)(2,1)}, bf16[640,640]{1,0:T(8,128)(2,1)}) fusion(bf16[640,640]{1,0:T(8,128)(2,1)S(1)} %constant_dynamic-update-slice_fusion.2, bf16[640,640]{1,0:T(8,128)(2,1)} %collective-permute-done.5, pred[]{:T(512)S(6)} %eq.85), kind=kLoop, calls=%fused_computation.60 | loop fusion | flops 819200 | bytes 3276801 | tf_op jit(solution)/shard_map/first_product/jit(_where)/select_n | solution.py:133
  93.1 2.9 %all-to-all-done.1 = bf16[4,80,640]{2,1,0:T(8,128)(2,1)} async-done(((bf16[4,80,640]{2,1,0:T(8,128)(2,1)}), bf16[4,80,640]{2,1,0:T(8,128)(2,1)}, u32[]{:S(2)}, u32[]{:S(2)}) %all-to-all-start.1) | async-done | bytes 409632 | tf_op jit(solution)/shard_map/density_columns/all_to_all | solution.py:114
  96.1 2.1 pad_maximum_fusion
  99.6 2.3 fusion.18
  103.3 2.3 fusion.14
  109.9 10.2 %collective-permute-done.19 = f32[80,1280]{1,0:T(8,128)S(1)} collective-permute-done((f32[80,1280]{1,0:T(8,128)S(1)}, f32[80,1280]{1,0:T(8,128)S(1)}, u32[]{:S(2)}, u32[]{:S(2)}) %collective-permute-start.19) | collective-permute-done | bytes 409632 | tf_op jit(solution)/shard_map/mixed_sum/ppermute | solution.py:26
  123.9 3.0 %collective-permute-start.23 = (bf16[320,640]{1,0:T(8,128)(2,1)}, bf16[320,640]{1,0:T(8,128)(2,1)S(1)}, u32[]{:S(2)}, u32[]{:S(2)}) collective-permute-start(bf16[320,640]{1,0:T(8,128)(2,1)} %bitcast.33), channel_id=1, source_target_pairs={{0,96},{1,97},{2,98},{3,99},{4,100},{5,101},{6,102},{7,103},{8,104... | collective-permute-start | bytes 1228808 | tf_op jit(solution)/shard_map/density_gather/ppermute | solution.py:26
  126.8 7.9 %collective-permute-done.21 = bf16[320,640]{1,0:T(8,128)(2,1)S(1)} collective-permute-done((bf16[320,640]{1,0:T(8,128)(2,1)}, bf16[320,640]{1,0:T(8,128)(2,1)S(1)}, u32[]{:S(2)}, u32[]{:S(2)}) %collective-permute-start.21) | collective-permute-done | bytes 409632 | tf_op jit(solution)/shard_map/density_gather/ppermute | solution.py:26
  134.7 6.4 %collective-permute-done.22 = bf16[320,640]{1,0:T(8,128)(2,1)S(1)} collective-permute-done((bf16[320,640]{1,0:T(8,128)(2,1)}, bf16[320,640]{1,0:T(8,128)(2,1)S(1)}, u32[]{:S(2)}, u32[]{:S(2)}) %collective-permute-start.22) | collective-permute-done | bytes 409632 | tf_op jit(solution)/shard_map/density_gather/ppermute | solution.py:26
  141.1 2.7 %collective-permute-done.23 = bf16[320,640]{1,0:T(8,128)(2,1)S(1)} collective-permute-done((bf16[320,640]{1,0:T(8,128)(2,1)}, bf16[320,640]{1,0:T(8,128)(2,1)S(1)}, u32[]{:S(2)}, u32[]{:S(2)}) %collective-permute-start.23) | collective-permute-done | bytes 409632 | tf_op jit(solution)/shard_map/density_gather/ppermute | solution.py:26
  149.5 6.3 %collective-permute-done.24 = bf16[160,1280]{1,0:T(8,128)(2,1)S(1)} collective-permute-done((bf16[160,1280]{1,0:T(8,128)(2,1)S(1)}, bf16[160,1280]{1,0:T(8,128)(2,1)S(1)}, u32[]{:S(2)}, u32[]{:S(2)}) %collective-permute-start.24) | collective-permute-done | bytes 409632 | tf_op jit(solution)/shard_map/mixed_gather/ppermute | solution.py:26
  155.8 8.3 %collective-permute-done.25 = bf16[160,1280]{1,0:T(8,128)(2,1)S(1)} collective-permute-done((bf16[160,1280]{1,0:T(8,128)(2,1)S(1)}, bf16[160,1280]{1,0:T(8,128)(2,1)S(1)}, u32[]{:S(2)}, u32[]{:S(2)}) %collective-permute-start.25) | collective-permute-done | bytes 409632 | tf_op jit(solution)/shard_map/mixed_gather/ppermute | solution.py:26
  164.2 2.6 %collective-permute-done.26 = bf16[160,1280]{1,0:T(8,128)(2,1)S(1)} collective-permute-done((bf16[160,1280]{1,0:T(8,128)(2,1)S(1)}, bf16[160,1280]{1,0:T(8,128)(2,1)S(1)}, u32[]{:S(2)}, u32[]{:S(2)}) %collective-permute-start.26) | collective-permute-done | bytes 409632 | tf_op jit(solution)/shard_map/mixed_gather/ppermute | solution.py:26
  172.0 3.0 %fusion.36 = f32[640,640]{1,0:T(8,128)S(1)} fusion(bf16[640,1280]{1,0:T(8,128)(2,1)} %collective-permute-done.27, bf16[320,640]{1,0:T(8,128)(2,1)S(1)} %get-tuple-element.58, bf16[320,640]{1,0:T(8,128)(2,1)S(1)} %get-tuple-element.59, bf16[320,640]{1,0:T(8,128)(2,1)S(1)} %get-tuple-element.60, bf16[320,640]{1,0:T(8,128)(2,1)S(1)} %get-tuple-element.57), kind=kOutput, calls=%fused_computation.76 | convolution fusion | flops 1055129600 | bytes 4915200 | tf_op jit(solution)/shard_map/second_product/dot_general | solution.py:58
  180.7 2.1 collective-permute-start.28
  184.0 6.5 %collective-permute-done.29 = bf16[320,640]{1,0:T(8,128)(2,1)} collective-permute-done((bf16[320,640]{1,0:T(8,128)(2,1)}, bf16[320,640]{1,0:T(8,128)(2,1)}, u32[]{:S(2)}, u32[]{:S(2)}) %collective-permute-start.29) | collective-permute-done | bytes 409632 | tf_op jit(solution)/shard_map/second_product/ppermute | solution.py:26
  190.5 9.2 %collective-permute-done.30 = bf16[320,640]{1,0:T(8,128)(2,1)} collective-permute-done((bf16[320,640]{1,0:T(8,128)(2,1)}, bf16[320,640]{1,0:T(8,128)(2,1)}, u32[]{:S(2)}, u32[]{:S(2)}) %collective-permute-start.30) | collective-permute-done | bytes 409632 | tf_op jit(solution)/shard_map/second_product/ppermute | solution.py:26
  211.2 6.6 %all-to-all-start.2 = ((bf16[32,40,160]{2,1,0:T(8,128)(2,1)}), bf16[32,40,160]{2,1,0:T(8,128)(2,1)}, u32[]{:S(2)}, u32[]{:S(2)}) async-start(bf16[32,40,160]{2,1,0:T(8,128)(2,1)} %bitcast.193), calls=%async_computation.2 | async-start | bytes 1310720 | tf_op jit(solution)/shard_map/transposed/all_to_all | solution.py:187
  219.0 3.0 %collective-permute-start.34 = (f32[40,1280]{1,0:T(8,128)}, f32[40,1280]{1,0:T(8,128)}, u32[]{:S(2)}, u32[]{:S(2)}) collective-permute-start(f32[40,1280]{1,0:T(8,128)} %get-tuple-element.75), channel_id=1, source_target_pairs={{0,24},{1,25},{2,26},{3,27},{4,28},{5,29},{6,30},{7,31},{8,16},{9,... | collective-permute-start | bytes 614408 | tf_op jit(solution)/shard_map/direct/ppermute | solution.py:26
  232.7 2.9 %reshape.257 = f32[40,5120]{1,0:T(8,128)} reshape(f32[40,4,4,320]{3,2,1,0:T(4,128)} %copy.193) | data formatting | bytes 1638400 | tf_op jit(solution)/shard_map/direct/reshape | solution.py:197
  237.7 2.5 %dot_general.40 = bf16[4,40,1280]{2,1,0:T(8,128)(2,1)} reshape(bf16[4,40,8,160]{3,2,1,0:T(8,128)(2,1)} %copy.195) | data formatting | bytes 819200 | tf_op jit(solution)/shard_map/transposed/dot_general | solution.py:58
  (199 shorter events, 98.2 us)
Async XLA Ops:
  1.9 11.9 %collective-permute-start = (bf16[160,1280]{1,0:T(8,128)(2,1)}, bf16[160,1280]{1,0:T(8,128)(2,1)}, u32[]{:S(2)}, u32[]{:S(2)}) collective-permute-start(bf16[160,1280]{1,0:T(8,128)(2,1)} %broadcast_select_fusion.9), channel_id=1, source_target_pairs={{0,2},{1,3},{2,0},{3,1},{4,6},{5,7},{6,4},{7,5},{8,10},{9,11},{10,... | collective-permute-start | bytes 1228808 | tf_op jit(solution)/shard_map/left_columns/ppermute | solution.py:26
  8.8 27.1 %all-to-all-start = ((bf16[8,160,320]{2,1,0:T(8,128)(2,1)}), bf16[8,160,320]{2,1,0:T(8,128)(2,1)S(1)}, u32[]{:S(2)}, u32[]{:S(2)}) async-start(bf16[8,160,320]{2,1,0:T(8,128)(2,1)} %bitcast.8), calls=%async_computation | async-start | bytes 1966080 | tf_op jit(solution)/shard_map/right_columns/all_to_all | solution.py:81
  18.2 8.0 %collective-permute-start.1 = (bf16[160,640]{1,0:T(8,128)(2,1)S(1)}, bf16[160,640]{1,0:T(8,128)(2,1)S(1)}, u32[]{:S(2)}, u32[]{:S(2)}) collective-permute-start(bf16[160,640]{1,0:T(8,128)(2,1)S(1)} %get-tuple-element.92), channel_id=1, source_target_pairs={{0,8},{1,9},{2,10},{3,11},{4,12},{5,13},{6,14},{7,15},{8,0},{9,1},... | collective-permute-start | bytes 614408 | tf_op jit(solution)/shard_map/left_columns/ppermute | solution.py:26
  19.8 12.5 %collective-permute-start.2 = (bf16[160,640]{1,0:T(8,128)(2,1)S(1)}, bf16[160,640]{1,0:T(8,128)(2,1)S(1)}, u32[]{:S(2)}, u32[]{:S(2)}) collective-permute-start(bf16[160,640]{1,0:T(8,128)(2,1)S(1)} %get-tuple-element.91), channel_id=1, source_target_pairs={{0,16},{1,17},{2,18},{3,19},{4,20},{5,21},{6,22},{7,23},{8,24},{9,... | collective-permute-start | bytes 614408 | tf_op jit(solution)/shard_map/left_columns/ppermute | solution.py:26
  22.7 12.2 %collective-permute-start.3 = (bf16[160,640]{1,0:T(8,128)(2,1)S(1)}, bf16[160,640]{1,0:T(8,128)(2,1)S(1)}, u32[]{:S(2)}, u32[]{:S(2)}) collective-permute-start(bf16[160,640]{1,0:T(8,128)(2,1)S(1)} %get-tuple-element.90), channel_id=1, source_target_pairs={{0,24},{1,25},{2,26},{3,27},{4,28},{5,29},{6,30},{7,31},{8,16},{9,... | collective-permute-start | bytes 614408 | tf_op jit(solution)/shard_map/left_columns/ppermute | solution.py:26
  23.7 45.5 %collective-permute-start.9 = (bf16[80,1280]{1,0:T(8,128)(2,1)}, bf16[80,1280]{1,0:T(8,128)(2,1)}, u32[]{:S(2)}, u32[]{:S(2)}) collective-permute-start(bf16[80,1280]{1,0:T(8,128)(2,1)} %bitcast.28), channel_id=1, source_target_pairs={{0,1},{1,0},{2,3},{3,2},{4,5},{5,4},{6,7},{7,6},{8,9},{9,8},{10,11... | collective-permute-start | bytes 614408 | tf_op jit(solution)/shard_map/density_turn/ppermute | solution.py:26
  38.0 21.7 %collective-permute-start.10 = (bf16[320,1280]{1,0:T(8,128)(2,1)}, bf16[320,1280]{1,0:T(8,128)(2,1)}, u32[]{:S(2)}, u32[]{:S(2)}) collective-permute-start(bf16[320,1280]{1,0:T(8,128)(2,1)} %reshape.247), channel_id=1, source_target_pairs={{0,96},{1,97},{2,98},{3,99},{4,100},{5,101},{6,102},{7,103},{8,104... | collective-permute-start | bytes 2457608 | tf_op jit(solution)/shard_map/right_gather/ppermute | solution.py:26
  42.1 19.4 %collective-permute-start.8 = (bf16[320,1280]{1,0:T(8,128)(2,1)}, bf16[320,1280]{1,0:T(8,128)(2,1)}, u32[]{:S(2)}, u32[]{:S(2)}) collective-permute-start(bf16[320,1280]{1,0:T(8,128)(2,1)} %reshape.247), channel_id=1, source_target_pairs={{0,32},{1,33},{2,34},{3,35},{4,36},{5,37},{6,38},{7,39},{8,40},{9,... | collective-permute-start | bytes 2457608 | tf_op jit(solution)/shard_map/right_gather/ppermute | solution.py:26
  42.1 31.4 %collective-permute-start.4 = (bf16[640,640]{1,0:T(8,128)(2,1)}, bf16[640,640]{1,0:T(8,128)(2,1)}, u32[]{:S(2)}, u32[]{:S(2)}) collective-permute-start(bf16[640,640]{1,0:T(8,128)(2,1)} %pad_maximum_fusion.7), channel_id=1, source_target_pairs={{0,4},{1,5},{2,6},{3,7},{4,0},{5,1},{6,2},{7,3},{8,12},{9,13},{10,... | collective-permute-start | bytes 2457608 | tf_op jit(solution)/shard_map/left_gather/ppermute | solution.py:26
  42.4 28.6 %collective-permute-start.5 = (bf16[640,640]{1,0:T(8,128)(2,1)}, bf16[640,640]{1,0:T(8,128)(2,1)}, u32[]{:S(2)}, u32[]{:S(2)}) collective-permute-start(bf16[640,640]{1,0:T(8,128)(2,1)} %pad_maximum_fusion.7), channel_id=1, source_target_pairs={{0,5},{1,4},{2,7},{3,6},{4,1},{5,0},{6,3},{7,2},{8,13},{9,12},{10,... | collective-permute-start | bytes 2457608 | tf_op jit(solution)/shard_map/left_gather/ppermute | solution.py:26
  61.5 18.7 %collective-permute-start.11 = (bf16[160,1280]{1,0:T(8,128)(2,1)}, bf16[160,1280]{1,0:T(8,128)(2,1)}, u32[]{:S(2)}, u32[]{:S(2)}) collective-permute-start(bf16[160,1280]{1,0:T(8,128)(2,1)} %slice.190), channel_id=1, source_target_pairs={{0,32},{1,33},{2,34},{3,35},{4,36},{5,37},{6,38},{7,39},{8,40},{9,... | collective-permute-start | bytes 1228808 | tf_op jit(solution)/shard_map/right_gather/ppermute | solution.py:26
  63.3 16.9 %collective-permute-start.12 = (bf16[160,1280]{1,0:T(8,128)(2,1)}, bf16[160,1280]{1,0:T(8,128)(2,1)}, u32[]{:S(2)}, u32[]{:S(2)}) collective-permute-start(bf16[160,1280]{1,0:T(8,128)(2,1)} %slice.191), channel_id=1, source_target_pairs={{0,96},{1,97},{2,98},{3,99},{4,100},{5,101},{6,102},{7,103},{8,104... | collective-permute-start | bytes 1228808 | tf_op jit(solution)/shard_map/right_gather/ppermute | solution.py:26
  73.0 15.6 %collective-permute-start.6 = (bf16[320,640]{1,0:T(8,128)(2,1)}, bf16[320,640]{1,0:T(8,128)(2,1)}, u32[]{:S(2)}, u32[]{:S(2)}) collective-permute-start(bf16[320,640]{1,0:T(8,128)(2,1)} %slice.188), channel_id=1, source_target_pairs={{0,4},{1,5},{2,6},{3,7},{4,0},{5,1},{6,2},{7,3},{8,12},{9,13},{10,... | collective-permute-start | bytes 1228808 | tf_op jit(solution)/shard_map/left_gather/ppermute | solution.py:26
  75.3 14.2 %collective-permute-start.7 = (bf16[320,640]{1,0:T(8,128)(2,1)}, bf16[320,640]{1,0:T(8,128)(2,1)}, u32[]{:S(2)}, u32[]{:S(2)}) collective-permute-start(bf16[320,640]{1,0:T(8,128)(2,1)} %slice.189), channel_id=1, source_target_pairs={{0,5},{1,4},{2,7},{3,6},{4,1},{5,0},{6,3},{7,2},{8,13},{9,12},{10,... | collective-permute-start | bytes 1228808 | tf_op jit(solution)/shard_map/left_gather/ppermute | solution.py:26
  84.4 11.7 %all-to-all-start.1 = ((bf16[4,80,640]{2,1,0:T(8,128)(2,1)}), bf16[4,80,640]{2,1,0:T(8,128)(2,1)}, u32[]{:S(2)}, u32[]{:S(2)}) async-start(bf16[4,80,640]{2,1,0:T(8,128)(2,1)} %pad_maximum_fusion.13), calls=%async_computation.1 | async-start | bytes 819200 | tf_op jit(solution)/shard_map/density_columns/all_to_all | solution.py:114
  108.5 11.6 %collective-permute-start.19 = (f32[80,1280]{1,0:T(8,128)S(1)}, f32[80,1280]{1,0:T(8,128)S(1)}, u32[]{:S(2)}, u32[]{:S(2)}) collective-permute-start(f32[80,1280]{1,0:T(8,128)S(1)} %get-tuple-element.85), channel_id=1, source_target_pairs={{0,8},{1,9},{2,10},{3,11},{4,12},{5,13},{6,14},{7,15},{8,0},{9,1},... | collective-permute-start | bytes 1228808 | tf_op jit(solution)/shard_map/mixed_sum/ppermute | solution.py:26
  109.2 12.4 %collective-permute-start.16 = (f32[80,1280]{1,0:T(8,128)S(1)}, f32[80,1280]{1,0:T(8,128)S(1)}, u32[]{:S(2)}, u32[]{:S(2)}) collective-permute-start(f32[80,1280]{1,0:T(8,128)S(1)} %get-tuple-element.86), channel_id=1, source_target_pairs={{0,24},{1,25},{2,26},{3,27},{4,28},{5,29},{6,30},{7,31},{8,16},{9,... | collective-permute-start | bytes 1228808 | tf_op jit(solution)/shard_map/mixed_sum/ppermute | solution.py:26
  120.3 23.5 %collective-permute-start.20 = (f32[160,1280]{1,0:T(8,128)S(1)}, f32[160,1280]{1,0:T(8,128)S(1)}, u32[]{:S(2)}, u32[]{:S(2)}) collective-permute-start(f32[160,1280]{1,0:T(8,128)S(1)} %pad_maximum_fusion.10), channel_id=1, source_target_pairs={{0,24},{1,25},{2,26},{3,27},{4,28},{5,29},{6,30},{7,31},{8,16},{9,... | collective-permute-start | bytes 2457608 | tf_op jit(solution)/shard_map/mixed_sum/ppermute | solution.py:26
  121.8 22.8 %collective-permute-start.17 = (f32[160,1280]{1,0:T(8,128)S(1)}, f32[160,1280]{1,0:T(8,128)S(1)}, u32[]{:S(2)}, u32[]{:S(2)}) collective-permute-start(f32[160,1280]{1,0:T(8,128)S(1)} %pad_maximum_fusion.9), channel_id=1, source_target_pairs={{0,8},{1,9},{2,10},{3,11},{4,12},{5,13},{6,14},{7,15},{8,0},{9,1},... | collective-permute-start | bytes 2457608 | tf_op jit(solution)/shard_map/mixed_sum/ppermute | solution.py:26
  122.1 12.6 %collective-permute-start.21 = (bf16[320,640]{1,0:T(8,128)(2,1)}, bf16[320,640]{1,0:T(8,128)(2,1)S(1)}, u32[]{:S(2)}, u32[]{:S(2)}) collective-permute-start(bf16[320,640]{1,0:T(8,128)(2,1)} %bitcast.33), channel_id=1, source_target_pairs={{0,32},{1,33},{2,34},{3,35},{4,36},{5,37},{6,38},{7,39},{8,40},{9,... | collective-permute-start | bytes 1228808 | tf_op jit(solution)/shard_map/density_gather/ppermute | solution.py:26
  123.5 17.6 %collective-permute-start.22 = (bf16[320,640]{1,0:T(8,128)(2,1)}, bf16[320,640]{1,0:T(8,128)(2,1)S(1)}, u32[]{:S(2)}, u32[]{:S(2)}) collective-permute-start(bf16[320,640]{1,0:T(8,128)(2,1)} %bitcast.33), channel_id=1, source_target_pairs={{0,64},{1,65},{2,66},{3,67},{4,68},{5,69},{6,70},{7,71},{8,72},{9,... | collective-permute-start | bytes 1228808 | tf_op jit(solution)/shard_map/density_gather/ppermute | solution.py:26
  123.9 19.9 %collective-permute-start.23 = (bf16[320,640]{1,0:T(8,128)(2,1)}, bf16[320,640]{1,0:T(8,128)(2,1)S(1)}, u32[]{:S(2)}, u32[]{:S(2)}) collective-permute-start(bf16[320,640]{1,0:T(8,128)(2,1)} %bitcast.33), channel_id=1, source_target_pairs={{0,96},{1,97},{2,98},{3,99},{4,100},{5,101},{6,102},{7,103},{8,104... | collective-permute-start | bytes 1228808 | tf_op jit(solution)/shard_map/density_gather/ppermute | solution.py:26
  144.7 11.1 %collective-permute-start.24 = (bf16[160,1280]{1,0:T(8,128)(2,1)S(1)}, bf16[160,1280]{1,0:T(8,128)(2,1)S(1)}, u32[]{:S(2)}, u32[]{:S(2)}) collective-permute-start(bf16[160,1280]{1,0:T(8,128)(2,1)S(1)} %add_convert_fusion), channel_id=1, source_target_pairs={{0,8},{1,9},{2,10},{3,11},{4,12},{5,13},{6,14},{7,15},{8,0},{9,1},... | collective-permute-start | bytes 1228808 | tf_op jit(solution)/shard_map/mixed_gather/ppermute | solution.py:26
  146.4 17.8 %collective-permute-start.25 = (bf16[160,1280]{1,0:T(8,128)(2,1)S(1)}, bf16[160,1280]{1,0:T(8,128)(2,1)S(1)}, u32[]{:S(2)}, u32[]{:S(2)}) collective-permute-start(bf16[160,1280]{1,0:T(8,128)(2,1)S(1)} %add_convert_fusion), channel_id=1, source_target_pairs={{0,16},{1,17},{2,18},{3,19},{4,20},{5,21},{6,22},{7,23},{8,24},{9,... | collective-permute-start | bytes 1228808 | tf_op jit(solution)/shard_map/mixed_gather/ppermute | solution.py:26
  148.3 18.4 %collective-permute-start.26 = (bf16[160,1280]{1,0:T(8,128)(2,1)S(1)}, bf16[160,1280]{1,0:T(8,128)(2,1)S(1)}, u32[]{:S(2)}, u32[]{:S(2)}) collective-permute-start(bf16[160,1280]{1,0:T(8,128)(2,1)S(1)} %add_convert_fusion), channel_id=1, source_target_pairs={{0,24},{1,25},{2,26},{3,27},{4,28},{5,29},{6,30},{7,31},{8,16},{9,... | collective-permute-start | bytes 1228808 | tf_op jit(solution)/shard_map/mixed_gather/ppermute | solution.py:26
  177.9 12.6 %collective-permute-start.29 = (bf16[320,640]{1,0:T(8,128)(2,1)}, bf16[320,640]{1,0:T(8,128)(2,1)}, u32[]{:S(2)}, u32[]{:S(2)}) collective-permute-start(bf16[320,640]{1,0:T(8,128)(2,1)} %bitcast.54), channel_id=1, source_target_pairs={{0,4},{1,5},{2,6},{3,7},{4,0},{5,1},{6,2},{7,3},{8,12},{9,13},{10,... | collective-permute-start | bytes 1228808 | tf_op jit(solution)/shard_map/second_product/ppermute | solution.py:26
  179.3 20.3 %collective-permute-start.30 = (bf16[320,640]{1,0:T(8,128)(2,1)}, bf16[320,640]{1,0:T(8,128)(2,1)}, u32[]{:S(2)}, u32[]{:S(2)}) collective-permute-start(bf16[320,640]{1,0:T(8,128)(2,1)} %bitcast.55), channel_id=1, source_target_pairs={{0,5},{1,4},{2,7},{3,6},{4,1},{5,0},{6,3},{7,2},{8,13},{9,12},{10,... | collective-permute-start | bytes 1228808 | tf_op jit(solution)/shard_map/second_product/ppermute | solution.py:26
  180.7 19.0 %collective-permute-start.28 = (bf16[320,640]{1,0:T(8,128)(2,1)}, bf16[320,640]{1,0:T(8,128)(2,1)}, u32[]{:S(2)}, u32[]{:S(2)}) collective-permute-start(bf16[320,640]{1,0:T(8,128)(2,1)} %bitcast.52), channel_id=1, source_target_pairs={{0,1},{1,0},{2,3},{3,2},{4,5},{5,4},{6,7},{7,6},{8,9},{9,8},{10,11... | collective-permute-start | bytes 1228808 | tf_op jit(solution)/shard_map/second_product/ppermute | solution.py:26
  206.6 16.1 %collective-permute-start.32 = (f32[40,1280]{1,0:T(8,128)}, f32[40,1280]{1,0:T(8,128)}, u32[]{:S(2)}, u32[]{:S(2)}) collective-permute-start(f32[40,1280]{1,0:T(8,128)} %get-tuple-element.77), channel_id=1, source_target_pairs={{0,8},{1,9},{2,10},{3,11},{4,12},{5,13},{6,14},{7,15},{8,0},{9,1},... | collective-permute-start | bytes 614408 | tf_op jit(solution)/shard_map/direct/ppermute | solution.py:26
  206.6 17.2 %collective-permute-start.33 = (f32[40,1280]{1,0:T(8,128)}, f32[40,1280]{1,0:T(8,128)}, u32[]{:S(2)}, u32[]{:S(2)}) collective-permute-start(f32[40,1280]{1,0:T(8,128)} %get-tuple-element.76), channel_id=1, source_target_pairs={{0,16},{1,17},{2,18},{3,19},{4,20},{5,21},{6,22},{7,23},{8,24},{9,... | collective-permute-start | bytes 614408 | tf_op jit(solution)/shard_map/direct/ppermute | solution.py:26
  211.2 24.4 %all-to-all-start.2 = ((bf16[32,40,160]{2,1,0:T(8,128)(2,1)}), bf16[32,40,160]{2,1,0:T(8,128)(2,1)}, u32[]{:S(2)}, u32[]{:S(2)}) async-start(bf16[32,40,160]{2,1,0:T(8,128)(2,1)} %bitcast.193), calls=%async_computation.2 | async-start | bytes 1310720 | tf_op jit(solution)/shard_map/transposed/all_to_all | solution.py:187
  219.0 9.0 %collective-permute-start.34 = (f32[40,1280]{1,0:T(8,128)}, f32[40,1280]{1,0:T(8,128)}, u32[]{:S(2)}, u32[]{:S(2)}) collective-permute-start(f32[40,1280]{1,0:T(8,128)} %get-tuple-element.75), channel_id=1, source_target_pairs={{0,24},{1,25},{2,26},{3,27},{4,28},{5,29},{6,30},{7,31},{8,16},{9,... | collective-permute-start | bytes 614408 | tf_op jit(solution)/shard_map/direct/ppermute | solution.py:26
  (28 other events, 195.8 us)

commit v3 on v2

v3 whole, which is shorter than its diff:
```python
import jax
import jax.numpy as jnp
from jax import lax
from jax.experimental import pallas as pl
from jax.experimental.pallas import tpu as pltpu
from jax.sharding import Mesh
from jax.sharding import PartitionSpec as P

BLK = 128
AXES = ("z", "y", "xl", "core", "xh")
SIZES = (4, 4, 2, 2, 2)
f32 = jnp.float32
bf16 = jnp.bfloat16


def flip(value, z=0, y=0, xl=0, core=0, xh=0):
    masks = (z, y, xl, core, xh)
    pairs = []
    for source in range(128):
        rest, digits = source, []
        for size in reversed(SIZES):
            digits.append(rest % size)
            rest //= size
        target = 0
        for digit, size, mask in zip(reversed(digits), SIZES, masks):
            target = target * size + (digit ^ mask)
        pairs.append((source, target))
    return lax.ppermute(value, AXES, pairs)


def remap(value, rule):
    pairs = []
    for source in range(128):
        rest, digits = source, []
        for size in reversed(SIZES):
            digits.append(rest % size)
            rest //= size
        target = 0
        for digit, size in zip(rule(*reversed(digits)), SIZES):
            target = target * size + digit
        pairs.append((source, target))
    return lax.ppermute(value, AXES, pairs)


def pick(stack, index):
    return lax.dynamic_index_in_dim(stack, index, 0, keepdims=False)


def dot(a, b):
    return jnp.dot(a, b, preferred_element_type=f32)


VMEM = pl.BlockSpec(memory_space=pltpu.VMEM)
SMEM = pl.BlockSpec(memory_space=pltpu.SMEM)


def local_call(kernel, name, outs, coords, *operands, scratch=()):
    return pl.pallas_call(
        kernel,
        out_shape=outs,
        in_specs=[SMEM] + [VMEM] * len(operands),
        out_specs=jax.tree.map(lambda _: VMEM, outs),
        scratch_shapes=list(scratch),
        name=name,
    )(coords, *operands)


def shape(dtype, *dims):
    return jax.ShapeDtypeStruct(dims, dtype)


def left_kernel(at_ref, keep_ref, came_ref, *outs):
    y, core = at_ref[1], at_ref[3]
    low = jnp.where(core == 0, keep_ref[...], came_ref[...])
    high = jnp.where(core == 0, came_ref[...], keep_ref[...])
    for ny in range(4):
        cut = slice(ny * 320, ny * 320 + 320)
        piece = jnp.concatenate((low[:, cut], high[:, cut]), axis=1)
        for q in range(4):

            @pl.when((y ^ q) == ny)
            def _():
                outs[q][...] = piece


def right_kernel(at_ref, first_ref, second_ref, out_ref):
    for m, ref in enumerate((first_ref, second_ref)):
        whole = ref[...]
        for xl in range(2):
            for xh in range(2):
                out_ref[xl * 4 + m * 2 + xh] = jnp.concatenate(
                    [
                        whole[:, start : start + 40]
                        for ny in range(4)
                        for start in (
                            ny * 320 + xl * 160 + xh * 40,
                            ny * 320 + xl * 160 + 80 + xh * 40,
                        )
                    ],
                    axis=1,
                )


def density_kernel(at_ref, same_ref, other_ref, out_ref):
    xh = at_ref[4]
    first = jnp.where(xh == 0, same_ref[...], other_ref[...])
    second = jnp.where(xh == 0, other_ref[...], same_ref[...])
    for ny in range(4):
        cut = slice(ny * 320, ny * 320 + 320)
        out_ref[ny] = jnp.concatenate((first[:, cut], second[:, cut]), axis=1)


def combine_kernel(at_ref, own_ref, a_ref, b_ref, c_ref, stay_ref, away_ref):
    core = at_ref[3]
    for q in range(4):
        halves = []
        for nc in range(2):
            rows = slice((q * 2 + nc) * 40, (q * 2 + nc) * 40 + 40)
            halves.append(
                own_ref[rows]
                + a_ref[q * 2 + nc].astype(f32)
                + b_ref[q * 2 + nc].astype(f32)
                + c_ref[q * 2 + nc].astype(f32)
            )
        stay_ref[q] = jnp.where(core == 0, halves[0], halves[1])
        away_ref[q] = jnp.where(core == 0, halves[1], halves[0])


def spread_kernel(at_ref, stay_ref, came_ref, turned_ref, d0, d1, d2, d3, slots):
    y, core = at_ref[1], at_ref[3]
    for q, ref in enumerate((d0, d1, d2, d3)):
        low = jnp.where(core == 0, stay_ref[q], came_ref[q])
        high = jnp.where(core == 0, came_ref[q], stay_ref[q])
        ref[:, :640] = low
        ref[:, 640:] = high
        slots[y ^ q, :, :640] = low
        slots[y ^ q, :, 640:] = high
    for nz in range(4):
        part = jnp.concatenate(
            [slots[ny, :, nz * 320 : nz * 320 + 320] for ny in range(4)], axis=0
        )
        part = part.T
        for j in range(8):
            turned_ref[nz * 8 + j] = part[j * 40 : j * 40 + 40].astype(bf16)


def finish_kernel(at_ref, d0, d1, d2, d3, t_ref, kept_ref, out_ref, slots):
    for q, ref in enumerate((d0, d1, d2, d3)):
        slots[q] = ref[...]
    y = at_ref[1]
    for nz in range(4):
        blocks = []
        for ny in range(4):
            other = jnp.concatenate(
                [
                    t_ref[nz * 8 + s, :, ny * 40 : (ny + 1) * 40].astype(f32)
                    for s in range(8)
                ],
                axis=1,
            )
            blocks.append(slots[y ^ ny, :, nz * 320 : (nz + 1) * 320] + other)
        block = 0.5 * jnp.concatenate(blocks, axis=1)
        kept = jnp.concatenate(
            [
                jnp.broadcast_to(kept_ref[:, j : j + 1], (40, BLK))
                for j in range(nz * 10, nz * 10 + 10)
            ],
            axis=1,
        )
        out_ref[:, nz * 1280 : (nz + 1) * 1280] = block * kept


def shards(dens_resp, density, fock, fock_resp, pattern):
    z, y, xl, core, xh = (lax.axis_index(name) for name in AXES)
    coords = jnp.stack((z, y, xl, core, xh)).astype(jnp.int32)

    with jax.named_scope("left_columns"):
        keep = jnp.where(core == 0, dens_resp, density)
        send = jnp.where(core == 0, density, dens_resp)
        came = flip(send, core=1)
    with jax.named_scope("right_columns"):
        first, second, _ = lax.optimization_barrier((fock, fock_resp, send))
        parts = local_call(
            right_kernel, "right_columns", shape(bf16, 8, 160, 320), coords, first, second
        )
        rounds = lax.all_to_all(
            parts, ("xl", "core", "xh"), split_axis=0, concat_axis=0, tiled=True
        )
    with jax.named_scope("density_turn"):
        halves, _ = lax.optimization_barrier((density.reshape(2, 2, 40, 1280), send))
        same = lax.dynamic_index_in_dim(halves, xh, 1, keepdims=False).reshape(80, 1280)
        other = lax.dynamic_index_in_dim(halves, 1 - xh, 1, keepdims=False).reshape(80, 1280)
        other = flip(other, xh=1)
    with jax.named_scope("left_columns"):
        pieces = local_call(
            left_kernel, "left_columns", [shape(bf16, 160, 640)] * 4, coords, keep, came
        )
        left = jnp.concatenate([pieces[0]] + [flip(pieces[q], y=q) for q in (1, 2, 3)])
    with jax.named_scope("right_gather"):
        right = rounds.reshape(2, 4, 160, 320).transpose(0, 2, 1, 3).reshape(320, 1280)
        right, left = lax.optimization_barrier((right, left))
        rights = [right] + [flip(right, z=q) for q in (1, 2, 3)]
    with jax.named_scope("left_gather"):
        lefts = {
            (0, 0): left,
            (1, 0): flip(left, xl=1),
            (0, 1): flip(left, xh=1),
            (1, 1): flip(left, xl=1, xh=1),
        }

    with jax.named_scope("density_columns"):
        same, other, lefts[1, 0], lefts[1, 1] = lax.optimization_barrier(
            (same, other, lefts[1, 0], lefts[1, 1])
        )
        cols = local_call(
            density_kernel, "density_columns", shape(bf16, 4, 80, 640), coords, same, other
        )
        dslots = lax.all_to_all(cols, "y", split_axis=0, concat_axis=0, tiled=True)
        dslots = dslots.reshape(320, 640)

    with jax.named_scope("first_product"):
        rights, dslots = lax.optimization_barrier((rights, dslots))
        rights = jnp.stack(rights)
        rsel = jnp.concatenate(
            [
                pick(rights, z ^ (nzh * 2 + (xh ^ r)))
                for r in range(2)
                for nzh in range(2)
            ]
        )
        theirs = [jnp.where(core == 0, lefts[1, r], lefts[0, r]) for r in range(2)]
        mine = [jnp.where(core == 0, lefts[0, r], lefts[1, r]) for r in range(2)]
        theirs = dot(jnp.concatenate(theirs, axis=1), rsel).reshape(4, 160, 1280)
        mine = dot(jnp.concatenate(mine, axis=1), rsel).reshape(4, 160, 1280)
    with jax.named_scope("mixed_sum"):
        both = [None] * 4
        for q in (2, 1, 3, 0):
            both[q] = mine[q] + flip(theirs[q], core=1)
        upper = flip(both[2][:80], y=1)
        lower = flip(both[2][80:], y=3)
        third = jnp.concatenate((both[3][:80] + upper, both[3][80:]))
        first = jnp.concatenate((both[1][:80], both[1][80:] + lower))
        sums = [flip(first, y=1), flip(third, y=3)]

    with jax.named_scope("density_gather"):
        dslots, _ = lax.optimization_barrier((dslots, both))
        dparts = [dslots] + [flip(dslots, z=q) for q in (1, 2, 3)]

    with jax.named_scope("mixed_sum"):
        sums, dparts = lax.optimization_barrier((sums, dparts))
        total = both[0] + sums[0] + sums[1]
        mixed = total.astype(bf16)

    with jax.named_scope("density_rows"):
        dparts = jnp.stack(dparts)
        dfull = jnp.concatenate([pick(dparts, z ^ nz) for nz in range(4)])

    with jax.named_scope("mixed_gather"):
        mslots = jnp.concatenate([mixed] + [flip(mixed, y=q) for q in (1, 2, 3)])
        mother = flip(mslots, core=1)

    with jax.named_scope("second_product"):
        near = dot(mslots, dfull).reshape(4, 160, 640)
        far = dot(mother, dfull).reshape(4, 160, 640)

        def piece(h, r):
            rows = jnp.where(core == h, near, far).reshape(8, 2, 40, 640)
            return lax.dynamic_index_in_dim(rows, xh ^ r, 1, keepdims=False).reshape(320, 640)

        came = [
            flip(piece(h, r).astype(bf16), xl=h, xh=r).reshape(8, 40, 640)
            for h, r in ((0, 1), (1, 0), (1, 1))
        ]
        stay, away = local_call(
            combine_kernel, "combine", [shape(f32, 4, 40, 640)] * 2, coords, piece(0, 0), *came
        )
        away = flip(away, core=1)
        turned, *rows = local_call(
            spread_kernel,
            "spread",
            [shape(bf16, 32, 40, 160)] + [shape(f32, 40, 1280)] * 4,
            coords,
            stay,
            away,
            scratch=[pltpu.VMEM((4, 40, 1280), f32)],
        )

    with jax.named_scope("transposed"):
        turned = lax.all_to_all(
            turned, ("z", "xl", "core", "xh"), split_axis=0, concat_axis=0, tiled=True
        )
    with jax.named_scope("direct"):
        direct = [rows[0]] + [flip(rows[q], y=q) for q in (1, 2, 3)]

    first_row = ((((z * 4 + y) * 2 + xl) * 2 + core) * 2 + xh) * 40
    block_rows = (first_row + jnp.arange(40, dtype=jnp.int32)) // BLK
    block_count = pattern.shape[0]
    onehot = (
        block_rows[:, None] == jnp.arange(block_count, dtype=jnp.int32)[None, :]
    ).astype(f32)
    kept_blocks = jnp.dot(onehot, pattern.astype(f32), preferred_element_type=f32)
    return local_call(
        finish_kernel,
        "finish",
        shape(f32, 40, 5120),
        coords,
        *direct,
        turned,
        kept_blocks,
        scratch=[pltpu.VMEM((4, 40, 1280), f32)],
    )


def solution(mesh):
    fine = Mesh(mesh.devices.reshape(SIZES), AXES)
    split = P(("z", "y", "xl"), ("core", "xh"))
    return jax.shard_map(
        shards,
        mesh=fine,
        in_specs=(split, split, split, split, P()),
        out_specs=P(AXES, None),
        check_vma=False,
    )
```

time: 246 us -> 251 us (1.020)
  waiting for transfers between devices: 93.2 us -> 146 us
  local copies, waits for them, and re-layouts: 51.1 us -> 10.1 us
  Pallas kernels: 0 us -> 16.2 us
  other arithmetic: 27.1 us -> 11.1 us
  matrix products: 14.2 us -> 9.81 us
    ppermute x35 -> x33, waiting for transfers between devices: 90.2 us -> 146 us  [flip(): return lax.ppermute(value, AXES, pairs)]
    pallas_call x0 -> x6, Pallas kernels: none -> 16.2 us  [local_call(): pl.pallas_call(kernel, out_shape=outs, in_specs=[SMEM] + [VMEM] * len(ope...]
    slice x8 -> x0, local copies, waits for them, and re-layouts: 9.45 us -> none  [the longest x2 3.7 us: ring_gather(): upper = flip(three[:half], **near)]
    reshape x6 -> x0, local copies, waits for them, and re-layouts: 7.18 us -> none  [the longest x1 2.89 us: shards(): long_rows = long_rows.reshape(40, 5120)]
    another operation x6 -> x1, local copies, waits for them, and re-layouts: 7.08 us -> 0.61 us  [shards(): coords = jnp.stack((z, y, xl, core, xh)).astype(jnp.int32)]
    dot_general x9 -> x4, matrix products: 14 us -> 9.02 us  [dot(): return jnp.dot(a, b, preferred_element_type=f32)]
    transpose x2 -> x0, local copies, waits for them, and re-layouts: 4.16 us -> none  [the longest x1 2.09 us: shards(): turned = sorted_rows.astype(bf16).T.reshape(32, 40, 160)]
    concatenate x3 -> x1, other arithmetic: 4.21 us -> 1 us  [shards(): jnp.concatenate([pieces[0]] + [flip(pieces[q], y=q) for q in (1, 2, 3)])]
  transfers between devices with their start and end apart: 38 -> 36, of which waited for: 20 -> 24; matrix products, arithmetic and copies ran while one was open for 26% -> 5% of each run, Pallas kernels for 0% -> 3%
where the time goes in v3:
time: 251 us; the launch traced here: 250 us
  waiting for transfers between devices  146 us (58%)
  starting transfers between devices  56.4 us (22%)
  Pallas kernels  16.2 us (6%)
  other arithmetic  11.1 us (4%)
  local copies, waits for them, and re-layouts  10.1 us (4%)
  matrix products  9.81 us (4%)
    ppermute x33, waiting for transfers between devices, flip(): return lax.ppermute(value, AXES, pairs)  146 us
    ppermute x33, starting transfers between devices, flip(): return lax.ppermute(value, AXES, pairs)  41.7 us
    pallas_call x6, Pallas kernels, local_call(): pl.pallas_call(kernel, out_shape=outs, in_specs=[SMEM] + [VMEM] * len(ope...  16.2 us
    dot_general x4, matrix products, dot(): return jnp.dot(a, b, preferred_element_type=f32)  9.02 us
    all_to_all x1, starting transfers between devices, shards(): lax.all_to_all(turned, ('z', 'xl', 'core', 'xh'), split_axis=0, concat_ax...  6.35 us
    unnamed x44, local copies, waits for them, and re-layouts  5.7 us
  transfers between devices with their start and end apart: 36, of which 24 were waited for; matrix products, arithmetic and copies ran while one was open for 5% of the time, Pallas kernels for 3%

profile of v3, /device:TPU:2, one launch (start us, length us, event | category | flops | bytes accessed | tf_op | source)
XLA Modules:
  0.0 250.2 jit_solution(16691104722447056864)
XLA Ops:
  2.5 2.8 %right_columns.1 = bf16[8,160,320]{2,1,0:T(8,128)(2,1)} custom-call(s32[5]{0:T(128)} %stack.53.at_ref, bf16[160,1280]{1,0:T(8,128)(2,1)} %first_ref, bf16[160,1280]{1,0:T(8,128)(2,1)} %second_ref), custom_call_target="tpu_custom_call" | custom-call | tf_op jit(solution)/shard_map/right_columns/right_columns/pallas_call | solution.py:58
  5.3 4.9 %all-to-all-start = ((bf16[8,160,320]{2,1,0:T(8,128)(2,1)}), bf16[8,160,320]{2,1,0:T(8,128)(2,1)S(1)}, u32[]{:S(2)}, u32[]{:S(2)}) async-start(bf16[8,160,320]{2,1,0:T(8,128)(2,1)} %right_columns.1), calls=%async_computation | async-start | bytes 1966080 | tf_op jit(solution)/shard_map/right_columns/all_to_all | solution.py:186
  11.0 2.5 %left_columns.1 = (bf16[160,640]{1,0:T(8,128)(2,1)}, bf16[160,640]{1,0:T(8,128)(2,1)}, bf16[160,640]{1,0:T(8,128)(2,1)}, bf16[160,640]{1,0:T(8,128)(2,1)}) custom-call(s32[5]{0:T(128)} %stack.53.at_ref, bf16[160,1280]{1,0:T(8,128)(2,1)} %get-tuple-element.97.keep_ref, bf16[160,1280]{1,0:T(8,128)(2,1)} %copy-done.12), custom_call_target="tpu_custom_call" | custom-call | tf_op jit(solution)/shard_map/left_columns/left_columns/pallas_call | solution.py:58
  15.2 2.9 %collective-permute-start.2 = (bf16[160,640]{1,0:T(8,128)(2,1)}, bf16[160,640]{1,0:T(8,128)(2,1)S(1)}, u32[]{:S(2)}, u32[]{:S(2)}) collective-permute-start(bf16[160,640]{1,0:T(8,128)(2,1)} %get-tuple-element.41), channel_id=1, source_target_pairs={{0,16},{1,17},{2,18},{3,19},{4,20},{5,21},{6,22},{7,23},{8,24},{9,... | collective-permute-start | bytes 614408 | tf_op jit(solution)/shard_map/left_columns/ppermute | solution.py:28
  18.3 3.4 %collective-permute-done.1 = bf16[160,640]{1,0:T(8,128)(2,1)S(1)} collective-permute-done((bf16[160,640]{1,0:T(8,128)(2,1)}, bf16[160,640]{1,0:T(8,128)(2,1)S(1)}, u32[]{:S(2)}, u32[]{:S(2)}) %collective-permute-start.1) | collective-permute-done | bytes 204832 | tf_op jit(solution)/shard_map/left_columns/ppermute | solution.py:28
  21.7 6.2 %collective-permute-done.2 = bf16[160,640]{1,0:T(8,128)(2,1)S(1)} collective-permute-done((bf16[160,640]{1,0:T(8,128)(2,1)}, bf16[160,640]{1,0:T(8,128)(2,1)S(1)}, u32[]{:S(2)}, u32[]{:S(2)}) %collective-permute-start.2) | collective-permute-done | bytes 204832 | tf_op jit(solution)/shard_map/left_columns/ppermute | solution.py:28
  27.9 2.6 %collective-permute-done.3 = bf16[160,640]{1,0:T(8,128)(2,1)S(1)} collective-permute-done((bf16[160,640]{1,0:T(8,128)(2,1)}, bf16[160,640]{1,0:T(8,128)(2,1)S(1)}, u32[]{:S(2)}, u32[]{:S(2)}) %collective-permute-start.3) | collective-permute-done | bytes 204832 | tf_op jit(solution)/shard_map/left_columns/ppermute | solution.py:28
  39.7 4.0 %collective-permute-start.10 = (bf16[320,1280]{1,0:T(8,128)(2,1)S(1)}, bf16[320,1280]{1,0:T(8,128)(2,1)}, u32[]{:S(2)}, u32[]{:S(2)}) collective-permute-start(bf16[320,1280]{1,0:T(8,128)(2,1)S(1)} %reshape.94), channel_id=1, source_target_pairs={{0,96},{1,97},{2,98},{3,99},{4,100},{5,101},{6,102},{7,103},{8,104... | collective-permute-start | bytes 2457608 | tf_op jit(solution)/shard_map/right_gather/ppermute | solution.py:28
  43.7 31.0 %collective-permute-done.4.other_ref = bf16[80,1280]{1,0:T(8,128)(2,1)S(1)} collective-permute-done((bf16[80,1280]{1,0:T(8,128)(2,1)S(1)}, bf16[80,1280]{1,0:T(8,128)(2,1)S(1)}, u32[]{:S(2)}, u32[]{:S(2)}) %collective-permute-start.4) | collective-permute-done | bytes 204832 | tf_op jit(solution)/shard_map/density_turn/ppermute | solution.py:28
  76.6 3.6 %collective-permute-start.9 = (bf16[320,1280]{1,0:T(8,128)(2,1)S(1)}, bf16[320,1280]{1,0:T(8,128)(2,1)}, u32[]{:S(2)}, u32[]{:S(2)}) collective-permute-start(bf16[320,1280]{1,0:T(8,128)(2,1)S(1)} %reshape.94), channel_id=1, source_target_pairs={{0,64},{1,65},{2,66},{3,67},{4,68},{5,69},{6,70},{7,71},{8,72},{9,... | collective-permute-start | bytes 2457608 | tf_op jit(solution)/shard_map/right_gather/ppermute | solution.py:28
  82.2 3.5 %all-to-all-start.1 = ((bf16[4,80,640]{2,1,0:T(8,128)(2,1)}), bf16[4,80,640]{2,1,0:T(8,128)(2,1)S(1)}, u32[]{:S(2)}, u32[]{:S(2)}) async-start(bf16[4,80,640]{2,1,0:T(8,128)(2,1)} %density_columns.1), calls=%async_computation.1 | async-start | bytes 819200 | tf_op jit(solution)/shard_map/density_columns/all_to_all | solution.py:218
  85.6 2.5 broadcast_select_fusion.5
  89.7 6.3 %collective-permute-done.8 = bf16[320,1280]{1,0:T(8,128)(2,1)} collective-permute-done((bf16[320,1280]{1,0:T(8,128)(2,1)S(1)}, bf16[320,1280]{1,0:T(8,128)(2,1)}, u32[]{:S(2)}, u32[]{:S(2)}) %collective-permute-start.8) | collective-permute-done | bytes 819232 | tf_op jit(solution)/shard_map/right_gather/ppermute | solution.py:28
  96.0 18.0 %collective-permute-done.9 = bf16[320,1280]{1,0:T(8,128)(2,1)} collective-permute-done((bf16[320,1280]{1,0:T(8,128)(2,1)S(1)}, bf16[320,1280]{1,0:T(8,128)(2,1)}, u32[]{:S(2)}, u32[]{:S(2)}) %collective-permute-start.9) | collective-permute-done | bytes 819232 | tf_op jit(solution)/shard_map/right_gather/ppermute | solution.py:28
  126.5 11.0 %collective-permute-done.17 = f32[80,1280]{1,0:T(8,128)S(1)} collective-permute-done((f32[80,1280]{1,0:T(8,128)S(1)}, f32[80,1280]{1,0:T(8,128)S(1)}, u32[]{:S(2)}, u32[]{:S(2)}) %collective-permute-start.17) | collective-permute-done | bytes 409632 | tf_op jit(solution)/shard_map/mixed_sum/ppermute | solution.py:28
  140.3 3.9 %collective-permute-start.21 = (bf16[320,640]{1,0:T(8,128)(2,1)S(1)}, bf16[320,640]{1,0:T(8,128)(2,1)S(1)}, u32[]{:S(2)}, u32[]{:S(2)}) collective-permute-start(bf16[320,640]{1,0:T(8,128)(2,1)S(1)} %bitcast.56), channel_id=1, source_target_pairs={{0,96},{1,97},{2,98},{3,99},{4,100},{5,101},{6,102},{7,103},{8,104... | collective-permute-start | bytes 1228808 | tf_op jit(solution)/shard_map/density_gather/ppermute | solution.py:28
  144.2 7.7 %collective-permute-done.19 = bf16[320,640]{1,0:T(8,128)(2,1)S(1)} collective-permute-done((bf16[320,640]{1,0:T(8,128)(2,1)S(1)}, bf16[320,640]{1,0:T(8,128)(2,1)S(1)}, u32[]{:S(2)}, u32[]{:S(2)}) %collective-permute-start.19) | collective-permute-done | bytes 409632 | tf_op jit(solution)/shard_map/density_gather/ppermute | solution.py:28
  151.9 5.6 %collective-permute-done.20 = bf16[320,640]{1,0:T(8,128)(2,1)S(1)} collective-permute-done((bf16[320,640]{1,0:T(8,128)(2,1)S(1)}, bf16[320,640]{1,0:T(8,128)(2,1)S(1)}, u32[]{:S(2)}, u32[]{:S(2)}) %collective-permute-start.20) | collective-permute-done | bytes 409632 | tf_op jit(solution)/shard_map/density_gather/ppermute | solution.py:28
  157.5 3.5 %collective-permute-done.21 = bf16[320,640]{1,0:T(8,128)(2,1)S(1)} collective-permute-done((bf16[320,640]{1,0:T(8,128)(2,1)S(1)}, bf16[320,640]{1,0:T(8,128)(2,1)S(1)}, u32[]{:S(2)}, u32[]{:S(2)}) %collective-permute-start.21) | collective-permute-done | bytes 409632 | tf_op jit(solution)/shard_map/density_gather/ppermute | solution.py:28
  166.7 7.7 %collective-permute-done.22 = bf16[160,1280]{1,0:T(8,128)(2,1)S(1)} collective-permute-done((bf16[160,1280]{1,0:T(8,128)(2,1)S(1)}, bf16[160,1280]{1,0:T(8,128)(2,1)S(1)}, u32[]{:S(2)}, u32[]{:S(2)}) %collective-permute-start.22) | collective-permute-done | bytes 409632 | tf_op jit(solution)/shard_map/mixed_gather/ppermute | solution.py:28
  174.4 7.0 %collective-permute-done.23 = bf16[160,1280]{1,0:T(8,128)(2,1)S(1)} collective-permute-done((bf16[160,1280]{1,0:T(8,128)(2,1)S(1)}, bf16[160,1280]{1,0:T(8,128)(2,1)S(1)}, u32[]{:S(2)}, u32[]{:S(2)}) %collective-permute-start.23) | collective-permute-done | bytes 409632 | tf_op jit(solution)/shard_map/mixed_gather/ppermute | solution.py:28
  181.4 2.6 %collective-permute-done.24 = bf16[160,1280]{1,0:T(8,128)(2,1)S(1)} collective-permute-done((bf16[160,1280]{1,0:T(8,128)(2,1)S(1)}, bf16[160,1280]{1,0:T(8,128)(2,1)S(1)}, u32[]{:S(2)}, u32[]{:S(2)}) %collective-permute-start.24) | collective-permute-done | bytes 409632 | tf_op jit(solution)/shard_map/mixed_gather/ppermute | solution.py:28
  188.4 3.0 %fusion.8 = f32[640,640]{1,0:T(8,128)S(1)} fusion(bf16[640,1280]{1,0:T(8,128)(2,1)} %collective-permute-done.25, bf16[320,640]{1,0:T(8,128)(2,1)S(1)} %get-tuple-element.82, bf16[320,640]{1,0:T(8,128)(2,1)S(1)} %get-tuple-element.83, bf16[320,640]{1,0:T(8,128)(2,1)S(1)} %get-tuple-element.84, bf16[320,640]{1,0:T(8,128)(2,1)S(1)} %get-tuple-element.81), kind=kOutput, calls=%fused_computation.43 | convolution fusion | flops 1055129600 | bytes 4915200 | tf_op jit(solution)/shard_map/second_product/dot_general | solution.py:50
  198.3 7.1 %collective-permute-done.27 = bf16[320,640]{1,0:T(8,128)(2,1)S(1)} collective-permute-done((bf16[320,640]{1,0:T(8,128)(2,1)S(1)}, bf16[320,640]{1,0:T(8,128)(2,1)S(1)}, u32[]{:S(2)}, u32[]{:S(2)}) %collective-permute-start.27) | collective-permute-done | bytes 409632 | tf_op jit(solution)/shard_map/second_product/ppermute | solution.py:28
  205.5 9.5 %collective-permute-done.28 = bf16[320,640]{1,0:T(8,128)(2,1)S(1)} collective-permute-done((bf16[320,640]{1,0:T(8,128)(2,1)S(1)}, bf16[320,640]{1,0:T(8,128)(2,1)S(1)}, u32[]{:S(2)}, u32[]{:S(2)}) %collective-permute-start.28) | collective-permute-done | bytes 409632 | tf_op jit(solution)/shard_map/second_product/ppermute | solution.py:28
  215.9 2.6 %combine.1 = (f32[4,40,640]{2,1,0:T(8,128)}, f32[4,40,640]{2,1,0:T(8,128)}) custom-call(s32[5]{0:T(128)} %stack.53.at_ref, f32[320,640]{1,0:T(8,128)} %bitcast.52, bf16[8,40,640]{2,1,0:T(8,128)(2,1)} %bitcast.70, bf16[8,40,640]{2,1,0:T(8,128)(2,1)} %bitcast.68, bf16[8,40,640]{2,1,0:T(8,128)(2,1)} %bitcast.69), custom_call_target="tpu_custom_call" | custom-call | tf_op jit(solution)/shard_map/second_product/combine/pallas_call | solution.py:58
  223.7 6.3 %all-to-all-start.2 = ((bf16[32,40,160]{2,1,0:T(8,128)(2,1)}), bf16[32,40,160]{2,1,0:T(8,128)(2,1)S(1)}, u32[]{:S(2)}, u32[]{:S(2)}) async-start(bf16[32,40,160]{2,1,0:T(8,128)(2,1)} %get-tuple-element.68), calls=%async_computation.2 | async-start | bytes 1310720 | tf_op jit(solution)/shard_map/transposed/all_to_all | solution.py:289
  230.2 2.8 %collective-permute-start.31 = (f32[40,1280]{1,0:T(8,128)}, f32[40,1280]{1,0:T(8,128)S(1)}, u32[]{:S(2)}, u32[]{:S(2)}) collective-permute-start(f32[40,1280]{1,0:T(8,128)} %get-tuple-element.66), channel_id=1, source_target_pairs={{0,16},{1,17},{2,18},{3,19},{4,20},{5,21},{6,22},{7,23},{8,24},{9,... | collective-permute-start | bytes 614408 | tf_op jit(solution)/shard_map/direct/ppermute | solution.py:28
  235.6 2.6 %collective-permute-done.30.d1 = f32[40,1280]{1,0:T(8,128)S(1)} collective-permute-done((f32[40,1280]{1,0:T(8,128)}, f32[40,1280]{1,0:T(8,128)S(1)}, u32[]{:S(2)}, u32[]{:S(2)}) %collective-permute-start.30) | collective-permute-done | bytes 204832 | tf_op jit(solution)/shard_map/direct/ppermute | solution.py:28
  238.3 4.5 %collective-permute-done.31.d2 = f32[40,1280]{1,0:T(8,128)S(1)} collective-permute-done((f32[40,1280]{1,0:T(8,128)}, f32[40,1280]{1,0:T(8,128)S(1)}, u32[]{:S(2)}, u32[]{:S(2)}) %collective-permute-start.31) | collective-permute-done | bytes 204832 | tf_op jit(solution)/shard_map/direct/ppermute | solution.py:28
  242.8 2.6 %collective-permute-done.32.d3 = f32[40,1280]{1,0:T(8,128)S(1)} collective-permute-done((f32[40,1280]{1,0:T(8,128)}, f32[40,1280]{1,0:T(8,128)S(1)}, u32[]{:S(2)}, u32[]{:S(2)}) %collective-permute-start.32) | collective-permute-done | bytes 204832 | tf_op jit(solution)/shard_map/direct/ppermute | solution.py:28
  246.3 3.9 %finish.1 = f32[40,5120]{1,0:T(8,128)} custom-call(s32[5]{0:T(128)} %stack.53.at_ref, f32[40,1280]{1,0:T(8,128)} %get-tuple-element.64.d0, f32[40,1280]{1,0:T(8,128)} %copy-done.17, f32[40,1280]{1,0:T(8,128)} %copy-done.18, f32[40,1280]{1,0:T(8,128)} %copy-done.19, bf16[32,40,160]{2,1,0:T(8,128)(2,1)} %copy-done, f32[40,40]{1,0:T(8,128)} %fusion.10.kept_ref), custom_call_target="tpu_custom_call" | custom-call | tf_op jit(solution)/shard_map/finish/pallas_call | solution.py:58
  (121 shorter events, 61.8 us)
Async XLA Ops:
  1.9 8.3 %collective-permute-start = (bf16[160,1280]{1,0:T(8,128)(2,1)S(1)}, bf16[160,1280]{1,0:T(8,128)(2,1)S(1)}, u32[]{:S(2)}, u32[]{:S(2)}) collective-permute-start(bf16[160,1280]{1,0:T(8,128)(2,1)S(1)} %get-tuple-element.98), channel_id=1, source_target_pairs={{0,2},{1,3},{2,0},{3,1},{4,6},{5,7},{6,4},{7,5},{8,10},{9,11},{10,... | collective-permute-start | bytes 1228808 | tf_op jit(solution)/shard_map/left_columns/ppermute | solution.py:28
  5.3 26.1 %all-to-all-start = ((bf16[8,160,320]{2,1,0:T(8,128)(2,1)}), bf16[8,160,320]{2,1,0:T(8,128)(2,1)S(1)}, u32[]{:S(2)}, u32[]{:S(2)}) async-start(bf16[8,160,320]{2,1,0:T(8,128)(2,1)} %right_columns.1), calls=%async_computation | async-start | bytes 1966080 | tf_op jit(solution)/shard_map/right_columns/all_to_all | solution.py:186
  13.6 8.1 %collective-permute-start.1 = (bf16[160,640]{1,0:T(8,128)(2,1)}, bf16[160,640]{1,0:T(8,128)(2,1)S(1)}, u32[]{:S(2)}, u32[]{:S(2)}) collective-permute-start(bf16[160,640]{1,0:T(8,128)(2,1)} %get-tuple-element.40), channel_id=1, source_target_pairs={{0,8},{1,9},{2,10},{3,11},{4,12},{5,13},{6,14},{7,15},{8,0},{9,1},... | collective-permute-start | bytes 614408 | tf_op jit(solution)/shard_map/left_columns/ppermute | solution.py:28
  15.2 12.7 %collective-permute-start.2 = (bf16[160,640]{1,0:T(8,128)(2,1)}, bf16[160,640]{1,0:T(8,128)(2,1)S(1)}, u32[]{:S(2)}, u32[]{:S(2)}) collective-permute-start(bf16[160,640]{1,0:T(8,128)(2,1)} %get-tuple-element.41), channel_id=1, source_target_pairs={{0,16},{1,17},{2,18},{3,19},{4,20},{5,21},{6,22},{7,23},{8,24},{9,... | collective-permute-start | bytes 614408 | tf_op jit(solution)/shard_map/left_columns/ppermute | solution.py:28
  18.0 12.4 %collective-permute-start.3 = (bf16[160,640]{1,0:T(8,128)(2,1)}, bf16[160,640]{1,0:T(8,128)(2,1)S(1)}, u32[]{:S(2)}, u32[]{:S(2)}) collective-permute-start(bf16[160,640]{1,0:T(8,128)(2,1)} %get-tuple-element.42), channel_id=1, source_target_pairs={{0,24},{1,25},{2,26},{3,27},{4,28},{5,29},{6,30},{7,31},{8,16},{9,... | collective-permute-start | bytes 614408 | tf_op jit(solution)/shard_map/left_columns/ppermute | solution.py:28
  32.7 43.9 %collective-permute-start.5 = (bf16[640,640]{1,0:T(8,128)(2,1)S(1)}, bf16[640,640]{1,0:T(8,128)(2,1)S(1)}, u32[]{:S(2)}, u32[]{:S(2)}) collective-permute-start(bf16[640,640]{1,0:T(8,128)(2,1)S(1)} %pad_maximum_fusion.5), channel_id=1, source_target_pairs={{0,4},{1,5},{2,6},{3,7},{4,0},{5,1},{6,2},{7,3},{8,12},{9,13},{10,... | collective-permute-start | bytes 2457608 | tf_op jit(solution)/shard_map/left_gather/ppermute | solution.py:28
  33.2 47.1 %collective-permute-start.6 = (bf16[640,640]{1,0:T(8,128)(2,1)S(1)}, bf16[640,640]{1,0:T(8,128)(2,1)}, u32[]{:S(2)}, u32[]{:S(2)}) collective-permute-start(bf16[640,640]{1,0:T(8,128)(2,1)S(1)} %pad_maximum_fusion.5), channel_id=1, source_target_pairs={{0,5},{1,4},{2,7},{3,6},{4,1},{5,0},{6,3},{7,2},{8,13},{9,12},{10,... | collective-permute-start | bytes 2457608 | tf_op jit(solution)/shard_map/left_gather/ppermute | solution.py:28
  35.4 52.7 %collective-permute-start.7 = (bf16[640,640]{1,0:T(8,128)(2,1)S(1)}, bf16[640,640]{1,0:T(8,128)(2,1)}, u32[]{:S(2)}, u32[]{:S(2)}) collective-permute-start(bf16[640,640]{1,0:T(8,128)(2,1)S(1)} %pad_maximum_fusion.5), channel_id=1, source_target_pairs={{0,1},{1,0},{2,3},{3,2},{4,5},{5,4},{6,7},{7,6},{8,9},{9,8},{10,11... | collective-permute-start | bytes 2457608 | tf_op jit(solution)/shard_map/left_gather/ppermute | solution.py:28
  37.6 37.1 %collective-permute-start.4 = (bf16[80,1280]{1,0:T(8,128)(2,1)S(1)}, bf16[80,1280]{1,0:T(8,128)(2,1)S(1)}, u32[]{:S(2)}, u32[]{:S(2)}) collective-permute-start(bf16[80,1280]{1,0:T(8,128)(2,1)S(1)} %bitcast.71), channel_id=1, source_target_pairs={{0,1},{1,0},{2,3},{3,2},{4,5},{5,4},{6,7},{7,6},{8,9},{9,8},{10,11... | collective-permute-start | bytes 614408 | tf_op jit(solution)/shard_map/density_turn/ppermute | solution.py:28
  39.7 50.0 %collective-permute-start.10 = (bf16[320,1280]{1,0:T(8,128)(2,1)S(1)}, bf16[320,1280]{1,0:T(8,128)(2,1)}, u32[]{:S(2)}, u32[]{:S(2)}) collective-permute-start(bf16[320,1280]{1,0:T(8,128)(2,1)S(1)} %reshape.94), channel_id=1, source_target_pairs={{0,96},{1,97},{2,98},{3,99},{4,100},{5,101},{6,102},{7,103},{8,104... | collective-permute-start | bytes 2457608 | tf_op jit(solution)/shard_map/right_gather/ppermute | solution.py:28
  74.7 21.3 %collective-permute-start.8 = (bf16[320,1280]{1,0:T(8,128)(2,1)S(1)}, bf16[320,1280]{1,0:T(8,128)(2,1)}, u32[]{:S(2)}, u32[]{:S(2)}) collective-permute-start(bf16[320,1280]{1,0:T(8,128)(2,1)S(1)} %reshape.94), channel_id=1, source_target_pairs={{0,32},{1,33},{2,34},{3,35},{4,36},{5,37},{6,38},{7,39},{8,40},{9,... | collective-permute-start | bytes 2457608 | tf_op jit(solution)/shard_map/right_gather/ppermute | solution.py:28
  76.6 37.4 %collective-permute-start.9 = (bf16[320,1280]{1,0:T(8,128)(2,1)S(1)}, bf16[320,1280]{1,0:T(8,128)(2,1)}, u32[]{:S(2)}, u32[]{:S(2)}) collective-permute-start(bf16[320,1280]{1,0:T(8,128)(2,1)S(1)} %reshape.94), channel_id=1, source_target_pairs={{0,64},{1,65},{2,66},{3,67},{4,68},{5,69},{6,70},{7,71},{8,72},{9,... | collective-permute-start | bytes 2457608 | tf_op jit(solution)/shard_map/right_gather/ppermute | solution.py:28
  82.2 31.8 %all-to-all-start.1 = ((bf16[4,80,640]{2,1,0:T(8,128)(2,1)}), bf16[4,80,640]{2,1,0:T(8,128)(2,1)S(1)}, u32[]{:S(2)}, u32[]{:S(2)}) async-start(bf16[4,80,640]{2,1,0:T(8,128)(2,1)} %density_columns.1), calls=%async_computation.1 | async-start | bytes 819200 | tf_op jit(solution)/shard_map/density_columns/all_to_all | solution.py:218
  120.2 4.2 %collective-permute-start.13 = (f32[160,1280]{1,0:T(8,128)S(1)}, f32[160,1280]{1,0:T(8,128)S(1)}, u32[]{:S(2)}, u32[]{:S(2)}) collective-permute-start(f32[160,1280]{1,0:T(8,128)S(1)} %get-tuple-element.75), channel_id=1, source_target_pairs={{0,2},{1,3},{2,0},{3,1},{4,6},{5,7},{6,4},{7,5},{8,10},{9,11},{10,... | collective-permute-start | bytes 2457608 | tf_op jit(solution)/shard_map/mixed_sum/ppermute | solution.py:28
  120.3 5.2 %collective-permute-start.16 = (f32[160,1280]{1,0:T(8,128)S(1)}, f32[160,1280]{1,0:T(8,128)S(1)}, u32[]{:S(2)}, u32[]{:S(2)}) collective-permute-start(f32[160,1280]{1,0:T(8,128)S(1)} %get-tuple-element.74), channel_id=1, source_target_pairs={{0,2},{1,3},{2,0},{3,1},{4,6},{5,7},{6,4},{7,5},{8,10},{9,11},{10,... | collective-permute-start | bytes 2457608 | tf_op jit(solution)/shard_map/mixed_sum/ppermute | solution.py:28
  126.0 11.6 %collective-permute-start.17 = (f32[80,1280]{1,0:T(8,128)S(1)}, f32[80,1280]{1,0:T(8,128)S(1)}, u32[]{:S(2)}, u32[]{:S(2)}) collective-permute-start(f32[80,1280]{1,0:T(8,128)S(1)} %get-tuple-element.93), channel_id=1, source_target_pairs={{0,8},{1,9},{2,10},{3,11},{4,12},{5,13},{6,14},{7,15},{8,0},{9,1},... | collective-permute-start | bytes 1228808 | tf_op jit(solution)/shard_map/mixed_sum/ppermute | solution.py:28
  126.0 12.8 %collective-permute-start.14 = (f32[80,1280]{1,0:T(8,128)S(1)}, f32[80,1280]{1,0:T(8,128)S(1)}, u32[]{:S(2)}, u32[]{:S(2)}) collective-permute-start(f32[80,1280]{1,0:T(8,128)S(1)} %get-tuple-element.94), channel_id=1, source_target_pairs={{0,24},{1,25},{2,26},{3,27},{4,28},{5,29},{6,30},{7,31},{8,16},{9,... | collective-permute-start | bytes 1228808 | tf_op jit(solution)/shard_map/mixed_sum/ppermute | solution.py:28
  137.7 23.3 %collective-permute-start.18 = (f32[160,1280]{1,0:T(8,128)S(1)}, f32[160,1280]{1,0:T(8,128)S(1)}, u32[]{:S(2)}, u32[]{:S(2)}) collective-permute-start(f32[160,1280]{1,0:T(8,128)S(1)} %pad_maximum_fusion.7), channel_id=1, source_target_pairs={{0,24},{1,25},{2,26},{3,27},{4,28},{5,29},{6,30},{7,31},{8,16},{9,... | collective-permute-start | bytes 2457608 | tf_op jit(solution)/shard_map/mixed_sum/ppermute | solution.py:28
  139.0 22.8 %collective-permute-start.15 = (f32[160,1280]{1,0:T(8,128)S(1)}, f32[160,1280]{1,0:T(8,128)S(1)}, u32[]{:S(2)}, u32[]{:S(2)}) collective-permute-start(f32[160,1280]{1,0:T(8,128)S(1)} %pad_maximum_fusion.6), channel_id=1, source_target_pairs={{0,8},{1,9},{2,10},{3,11},{4,12},{5,13},{6,14},{7,15},{8,0},{9,1},... | collective-permute-start | bytes 2457608 | tf_op jit(solution)/shard_map/mixed_sum/ppermute | solution.py:28
  139.5 12.4 %collective-permute-start.19 = (bf16[320,640]{1,0:T(8,128)(2,1)S(1)}, bf16[320,640]{1,0:T(8,128)(2,1)S(1)}, u32[]{:S(2)}, u32[]{:S(2)}) collective-permute-start(bf16[320,640]{1,0:T(8,128)(2,1)S(1)} %bitcast.54), channel_id=1, source_target_pairs={{0,32},{1,33},{2,34},{3,35},{4,36},{5,37},{6,38},{7,39},{8,40},{9,... | collective-permute-start | bytes 1228808 | tf_op jit(solution)/shard_map/density_gather/ppermute | solution.py:28
  139.5 18.0 %collective-permute-start.20 = (bf16[320,640]{1,0:T(8,128)(2,1)S(1)}, bf16[320,640]{1,0:T(8,128)(2,1)S(1)}, u32[]{:S(2)}, u32[]{:S(2)}) collective-permute-start(bf16[320,640]{1,0:T(8,128)(2,1)S(1)} %bitcast.55), channel_id=1, source_target_pairs={{0,64},{1,65},{2,66},{3,67},{4,68},{5,69},{6,70},{7,71},{8,72},{9,... | collective-permute-start | bytes 1228808 | tf_op jit(solution)/shard_map/density_gather/ppermute | solution.py:28
  140.3 20.7 %collective-permute-start.21 = (bf16[320,640]{1,0:T(8,128)(2,1)S(1)}, bf16[320,640]{1,0:T(8,128)(2,1)S(1)}, u32[]{:S(2)}, u32[]{:S(2)}) collective-permute-start(bf16[320,640]{1,0:T(8,128)(2,1)S(1)} %bitcast.56), channel_id=1, source_target_pairs={{0,96},{1,97},{2,98},{3,99},{4,100},{5,101},{6,102},{7,103},{8,104... | collective-permute-start | bytes 1228808 | tf_op jit(solution)/shard_map/density_gather/ppermute | solution.py:28
  161.9 12.5 %collective-permute-start.22 = (bf16[160,1280]{1,0:T(8,128)(2,1)S(1)}, bf16[160,1280]{1,0:T(8,128)(2,1)S(1)}, u32[]{:S(2)}, u32[]{:S(2)}) collective-permute-start(bf16[160,1280]{1,0:T(8,128)(2,1)S(1)} %add_convert_fusion), channel_id=1, source_target_pairs={{0,8},{1,9},{2,10},{3,11},{4,12},{5,13},{6,14},{7,15},{8,0},{9,1},... | collective-permute-start | bytes 1228808 | tf_op jit(solution)/shard_map/mixed_gather/ppermute | solution.py:28
  163.6 17.7 %collective-permute-start.23 = (bf16[160,1280]{1,0:T(8,128)(2,1)S(1)}, bf16[160,1280]{1,0:T(8,128)(2,1)S(1)}, u32[]{:S(2)}, u32[]{:S(2)}) collective-permute-start(bf16[160,1280]{1,0:T(8,128)(2,1)S(1)} %add_convert_fusion), channel_id=1, source_target_pairs={{0,16},{1,17},{2,18},{3,19},{4,20},{5,21},{6,22},{7,23},{8,24},{9,... | collective-permute-start | bytes 1228808 | tf_op jit(solution)/shard_map/mixed_gather/ppermute | solution.py:28
  165.3 18.6 %collective-permute-start.24 = (bf16[160,1280]{1,0:T(8,128)(2,1)S(1)}, bf16[160,1280]{1,0:T(8,128)(2,1)S(1)}, u32[]{:S(2)}, u32[]{:S(2)}) collective-permute-start(bf16[160,1280]{1,0:T(8,128)(2,1)S(1)} %add_convert_fusion), channel_id=1, source_target_pairs={{0,24},{1,25},{2,26},{3,27},{4,28},{5,29},{6,30},{7,31},{8,16},{9,... | collective-permute-start | bytes 1228808 | tf_op jit(solution)/shard_map/mixed_gather/ppermute | solution.py:28
  193.1 12.4 %collective-permute-start.27 = (bf16[320,640]{1,0:T(8,128)(2,1)S(1)}, bf16[320,640]{1,0:T(8,128)(2,1)S(1)}, u32[]{:S(2)}, u32[]{:S(2)}) collective-permute-start(bf16[320,640]{1,0:T(8,128)(2,1)S(1)} %bitcast.66), channel_id=1, source_target_pairs={{0,4},{1,5},{2,6},{3,7},{4,0},{5,1},{6,2},{7,3},{8,12},{9,13},{10,... | collective-permute-start | bytes 1228808 | tf_op jit(solution)/shard_map/second_product/ppermute | solution.py:28
  195.0 20.0 %collective-permute-start.28 = (bf16[320,640]{1,0:T(8,128)(2,1)S(1)}, bf16[320,640]{1,0:T(8,128)(2,1)S(1)}, u32[]{:S(2)}, u32[]{:S(2)}) collective-permute-start(bf16[320,640]{1,0:T(8,128)(2,1)S(1)} %bitcast.65), channel_id=1, source_target_pairs={{0,5},{1,4},{2,7},{3,6},{4,1},{5,0},{6,3},{7,2},{8,13},{9,12},{10,... | collective-permute-start | bytes 1228808 | tf_op jit(solution)/shard_map/second_product/ppermute | solution.py:28
  195.2 19.8 %collective-permute-start.26 = (bf16[320,640]{1,0:T(8,128)(2,1)S(1)}, bf16[320,640]{1,0:T(8,128)(2,1)S(1)}, u32[]{:S(2)}, u32[]{:S(2)}) collective-permute-start(bf16[320,640]{1,0:T(8,128)(2,1)S(1)} %bitcast.67), channel_id=1, source_target_pairs={{0,1},{1,0},{2,3},{3,2},{4,5},{5,4},{6,7},{7,6},{8,9},{9,8},{10,11... | collective-permute-start | bytes 1228808 | tf_op jit(solution)/shard_map/second_product/ppermute | solution.py:28
  223.7 21.7 %all-to-all-start.2 = ((bf16[32,40,160]{2,1,0:T(8,128)(2,1)}), bf16[32,40,160]{2,1,0:T(8,128)(2,1)S(1)}, u32[]{:S(2)}, u32[]{:S(2)}) async-start(bf16[32,40,160]{2,1,0:T(8,128)(2,1)} %get-tuple-element.68), calls=%async_computation.2 | async-start | bytes 1310720 | tf_op jit(solution)/shard_map/transposed/all_to_all | solution.py:289
  230.1 8.2 %collective-permute-start.30 = (f32[40,1280]{1,0:T(8,128)}, f32[40,1280]{1,0:T(8,128)S(1)}, u32[]{:S(2)}, u32[]{:S(2)}) collective-permute-start(f32[40,1280]{1,0:T(8,128)} %get-tuple-element.65), channel_id=1, source_target_pairs={{0,8},{1,9},{2,10},{3,11},{4,12},{5,13},{6,14},{7,15},{8,0},{9,1},... | collective-permute-start | bytes 614408 | tf_op jit(solution)/shard_map/direct/ppermute | solution.py:28
  230.2 12.6 %collective-permute-start.31 = (f32[40,1280]{1,0:T(8,128)}, f32[40,1280]{1,0:T(8,128)S(1)}, u32[]{:S(2)}, u32[]{:S(2)}) collective-permute-start(f32[40,1280]{1,0:T(8,128)} %get-tuple-element.66), channel_id=1, source_target_pairs={{0,16},{1,17},{2,18},{3,19},{4,20},{5,21},{6,22},{7,23},{8,24},{9,... | collective-permute-start | bytes 614408 | tf_op jit(solution)/shard_map/direct/ppermute | solution.py:28
  233.0 12.4 %collective-permute-start.32 = (f32[40,1280]{1,0:T(8,128)}, f32[40,1280]{1,0:T(8,128)S(1)}, u32[]{:S(2)}, u32[]{:S(2)}) collective-permute-start(f32[40,1280]{1,0:T(8,128)} %get-tuple-element.67), channel_id=1, source_target_pairs={{0,24},{1,25},{2,26},{3,27},{4,28},{5,29},{6,30},{7,31},{8,16},{9,... | collective-permute-start | bytes 614408 | tf_op jit(solution)/shard_map/direct/ppermute | solution.py:28
  (26 other events, 139.3 us)

commit v4 on v3

--- a/solution.py
+++ b/solution.py
@@ -198,7 +198,7 @@
         left = jnp.concatenate([pieces[0]] + [flip(pieces[q], y=q) for q in (1, 2, 3)])
     with jax.named_scope("right_gather"):
         right = rounds.reshape(2, 4, 160, 320).transpose(0, 2, 1, 3).reshape(320, 1280)
-        right, left = lax.optimization_barrier((right, left))
+        right, left, other = lax.optimization_barrier((right, left, other))
         rights = [right] + [flip(right, z=q) for q in (1, 2, 3)]
     with jax.named_scope("left_gather"):
         lefts = {

time: 251 us -> 223 us (0.89)
  waiting for transfers between devices: 146 us -> 117 us
    ppermute x33, waiting for transfers between devices: 146 us -> 114 us  [flip(): return lax.ppermute(value, AXES, pairs)]
    all_to_all x1, waiting for transfers between devices: 0.01 us -> 3.45 us  [shards(): dslots = lax.all_to_all(cols, 'y', split_axis=0, concat_axis=0, tiled=True)]
    unnamed x44 -> x46, local copies, waits for them, and re-layouts: 5.7 us -> 5.69 us
  transfers between devices with their start and end apart: 36 -> 36, of which waited for: 24 -> 24; matrix products, arithmetic and copies ran while one was open for 5% -> 6% of each run, Pallas kernels for 3% -> 3%
where the time goes in v4:
time: 223 us; the launch traced here: 222 us
  waiting for transfers between devices  117 us (52%)
  starting transfers between devices  57 us (26%)
  Pallas kernels  16.5 us (7%)
  other arithmetic  11.1 us (5%)
  local copies, waits for them, and re-layouts  10.1 us (5%)
  matrix products  9.8 us (4%)
    ppermute x33, waiting for transfers between devices, flip(): return lax.ppermute(value, AXES, pairs)  114 us
    ppermute x33, starting transfers between devices, flip(): return lax.ppermute(value, AXES, pairs)  43.3 us
    pallas_call x6, Pallas kernels, local_call(): pl.pallas_call(kernel, out_shape=outs, in_specs=[SMEM] + [VMEM] * len(ope...  16.5 us
    dot_general x4, matrix products, dot(): return jnp.dot(a, b, preferred_element_type=f32)  9.02 us
    unnamed x46, local copies, waits for them, and re-layouts  5.69 us
    all_to_all x1, starting transfers between devices, shards(): lax.all_to_all(turned, ('z', 'xl', 'core', 'xh'), split_axis=0, concat_ax...  5.25 us
    all_to_all x1, starting transfers between devices, shards(): lax.all_to_all(parts, ('xl', 'core', 'xh'), split_axis=0, concat_axis=0,...  4.94 us
  transfers between devices with their start and end apart: 36, of which 24 were waited for; matrix products, arithmetic and copies ran while one was open for 6% of the time, Pallas kernels for 3%

profile of v4, /device:TPU:2, one launch (start us, length us, event | category | flops | bytes accessed | tf_op | source)
XLA Modules:
  0.0 221.9 jit_solution(1456267437710048999)
XLA Ops:
  2.6 2.8 %right_columns.1 = bf16[8,160,320]{2,1,0:T(8,128)(2,1)} custom-call(s32[5]{0:T(128)} %stack.53.at_ref, bf16[160,1280]{1,0:T(8,128)(2,1)} %first_ref, bf16[160,1280]{1,0:T(8,128)(2,1)} %second_ref), custom_call_target="tpu_custom_call" | custom-call | tf_op jit(solution)/shard_map/right_columns/right_columns/pallas_call | solution.py:58
  5.4 4.9 %all-to-all-start = ((bf16[8,160,320]{2,1,0:T(8,128)(2,1)}), bf16[8,160,320]{2,1,0:T(8,128)(2,1)S(1)}, u32[]{:S(2)}, u32[]{:S(2)}) async-start(bf16[8,160,320]{2,1,0:T(8,128)(2,1)} %right_columns.1), calls=%async_computation | async-start | bytes 1966080 | tf_op jit(solution)/shard_map/right_columns/all_to_all | solution.py:186
  11.1 2.5 %left_columns.1 = (bf16[160,640]{1,0:T(8,128)(2,1)}, bf16[160,640]{1,0:T(8,128)(2,1)}, bf16[160,640]{1,0:T(8,128)(2,1)}, bf16[160,640]{1,0:T(8,128)(2,1)}) custom-call(s32[5]{0:T(128)} %stack.53.at_ref, bf16[160,1280]{1,0:T(8,128)(2,1)} %get-tuple-element.99.keep_ref, bf16[160,1280]{1,0:T(8,128)(2,1)} %copy-done.13), custom_call_target="tpu_custom_call" | custom-call | tf_op jit(solution)/shard_map/left_columns/left_columns/pallas_call | solution.py:58
  15.2 2.9 %collective-permute-start.2 = (bf16[160,640]{1,0:T(8,128)(2,1)}, bf16[160,640]{1,0:T(8,128)(2,1)S(1)}, u32[]{:S(2)}, u32[]{:S(2)}) collective-permute-start(bf16[160,640]{1,0:T(8,128)(2,1)} %get-tuple-element.42), channel_id=1, source_target_pairs={{0,16},{1,17},{2,18},{3,19},{4,20},{5,21},{6,22},{7,23},{8,24},{9,... | collective-permute-start | bytes 614408 | tf_op jit(solution)/shard_map/left_columns/ppermute | solution.py:28
  21.8 6.2 %collective-permute-done.2 = bf16[160,640]{1,0:T(8,128)(2,1)S(1)} collective-permute-done((bf16[160,640]{1,0:T(8,128)(2,1)}, bf16[160,640]{1,0:T(8,128)(2,1)S(1)}, u32[]{:S(2)}, u32[]{:S(2)}) %collective-permute-start.2) | collective-permute-done | bytes 204832 | tf_op jit(solution)/shard_map/left_columns/ppermute | solution.py:28
  27.9 2.6 %collective-permute-done.3 = bf16[160,640]{1,0:T(8,128)(2,1)S(1)} collective-permute-done((bf16[160,640]{1,0:T(8,128)(2,1)}, bf16[160,640]{1,0:T(8,128)(2,1)S(1)}, u32[]{:S(2)}, u32[]{:S(2)}) %collective-permute-start.3) | collective-permute-done | bytes 204832 | tf_op jit(solution)/shard_map/left_columns/ppermute | solution.py:28
  37.0 4.0 %collective-permute-start.10 = (bf16[320,1280]{1,0:T(8,128)(2,1)S(1)}, bf16[320,1280]{1,0:T(8,128)(2,1)}, u32[]{:S(2)}, u32[]{:S(2)}) collective-permute-start(bf16[320,1280]{1,0:T(8,128)(2,1)S(1)} %reshape.94), channel_id=1, source_target_pairs={{0,96},{1,97},{2,98},{3,99},{4,100},{5,101},{6,102},{7,103},{8,104... | collective-permute-start | bytes 2457608 | tf_op jit(solution)/shard_map/right_gather/ppermute | solution.py:28
  41.0 13.1 %collective-permute-done.5 = bf16[640,640]{1,0:T(8,128)(2,1)} collective-permute-done((bf16[640,640]{1,0:T(8,128)(2,1)S(1)}, bf16[640,640]{1,0:T(8,128)(2,1)}, u32[]{:S(2)}, u32[]{:S(2)}) %collective-permute-start.5) | collective-permute-done | bytes 819232 | tf_op jit(solution)/shard_map/left_gather/ppermute | solution.py:28
  54.2 3.9 %collective-permute-start.9 = (bf16[320,1280]{1,0:T(8,128)(2,1)S(1)}, bf16[320,1280]{1,0:T(8,128)(2,1)}, u32[]{:S(2)}, u32[]{:S(2)}) collective-permute-start(bf16[320,1280]{1,0:T(8,128)(2,1)S(1)} %reshape.94), channel_id=1, source_target_pairs={{0,64},{1,65},{2,66},{3,67},{4,68},{5,69},{6,70},{7,71},{8,72},{9,... | collective-permute-start | bytes 2457608 | tf_op jit(solution)/shard_map/right_gather/ppermute | solution.py:28
  58.0 11.3 %collective-permute-done.6 = bf16[640,640]{1,0:T(8,128)(2,1)S(1)} collective-permute-done((bf16[640,640]{1,0:T(8,128)(2,1)S(1)}, bf16[640,640]{1,0:T(8,128)(2,1)S(1)}, u32[]{:S(2)}, u32[]{:S(2)}) %collective-permute-start.6) | collective-permute-done | bytes 819232 | tf_op jit(solution)/shard_map/left_gather/ppermute | solution.py:28
  71.6 3.5 %all-to-all-start.1 = ((bf16[4,80,640]{2,1,0:T(8,128)(2,1)}), bf16[4,80,640]{2,1,0:T(8,128)(2,1)S(1)}, u32[]{:S(2)}, u32[]{:S(2)}) async-start(bf16[4,80,640]{2,1,0:T(8,128)(2,1)} %density_columns.1), calls=%async_computation.1 | async-start | bytes 819200 | tf_op jit(solution)/shard_map/density_columns/all_to_all | solution.py:218
  75.1 2.6 %broadcast_select_fusion.5 = (bf16[640,640]{1,0:T(8,128)(2,1)}, bf16[640,640]{1,0:T(8,128)(2,1)}) fusion(bf16[640,640]{1,0:T(8,128)(2,1)S(1)} %pad_maximum_fusion.5, bf16[640,640]{1,0:T(8,128)(2,1)} %collective-permute-done.5, pred[]{:T(512)S(6)} %eq.10), kind=kLoop, calls=%fused_computation.34 | loop fusion | flops 819200 | bytes 3276801 | tf_op jit(solution)/shard_map/first_product/jit(_where)/select_n | solution.py:232
  79.1 3.5 %all-to-all-done.1 = bf16[4,80,640]{2,1,0:T(8,128)(2,1)S(1)} async-done(((bf16[4,80,640]{2,1,0:T(8,128)(2,1)}), bf16[4,80,640]{2,1,0:T(8,128)(2,1)S(1)}, u32[]{:S(2)}, u32[]{:S(2)}) %all-to-all-start.1) | async-done | bytes 409632 | tf_op jit(solution)/shard_map/density_columns/all_to_all | solution.py:218
  95.8 10.2 %collective-permute-done.17 = f32[80,1280]{1,0:T(8,128)S(1)} collective-permute-done((f32[80,1280]{1,0:T(8,128)S(1)}, f32[80,1280]{1,0:T(8,128)S(1)}, u32[]{:S(2)}, u32[]{:S(2)}) %collective-permute-start.17) | collective-permute-done | bytes 409632 | tf_op jit(solution)/shard_map/mixed_sum/ppermute | solution.py:28
  110.0 3.6 %collective-permute-start.20 = (bf16[320,640]{1,0:T(8,128)(2,1)S(1)}, bf16[320,640]{1,0:T(8,128)(2,1)S(1)}, u32[]{:S(2)}, u32[]{:S(2)}) collective-permute-start(bf16[320,640]{1,0:T(8,128)(2,1)S(1)} %bitcast.55), channel_id=1, source_target_pairs={{0,64},{1,65},{2,66},{3,67},{4,68},{5,69},{6,70},{7,71},{8,72},{9,... | collective-permute-start | bytes 1228808 | tf_op jit(solution)/shard_map/density_gather/ppermute | solution.py:28
  113.5 6.9 %collective-permute-done.19 = bf16[320,640]{1,0:T(8,128)(2,1)S(1)} collective-permute-done((bf16[320,640]{1,0:T(8,128)(2,1)S(1)}, bf16[320,640]{1,0:T(8,128)(2,1)S(1)}, u32[]{:S(2)}, u32[]{:S(2)}) %collective-permute-start.19) | collective-permute-done | bytes 409632 | tf_op jit(solution)/shard_map/density_gather/ppermute | solution.py:28
  120.4 10.2 %collective-permute-done.20 = bf16[320,640]{1,0:T(8,128)(2,1)S(1)} collective-permute-done((bf16[320,640]{1,0:T(8,128)(2,1)S(1)}, bf16[320,640]{1,0:T(8,128)(2,1)S(1)}, u32[]{:S(2)}, u32[]{:S(2)}) %collective-permute-start.20) | collective-permute-done | bytes 409632 | tf_op jit(solution)/shard_map/density_gather/ppermute | solution.py:28
  130.6 2.6 %collective-permute-done.21 = bf16[320,640]{1,0:T(8,128)(2,1)S(1)} collective-permute-done((bf16[320,640]{1,0:T(8,128)(2,1)S(1)}, bf16[320,640]{1,0:T(8,128)(2,1)S(1)}, u32[]{:S(2)}, u32[]{:S(2)}) %collective-permute-start.21) | collective-permute-done | bytes 409632 | tf_op jit(solution)/shard_map/density_gather/ppermute | solution.py:28
  138.8 6.4 %collective-permute-done.22 = bf16[160,1280]{1,0:T(8,128)(2,1)S(1)} collective-permute-done((bf16[160,1280]{1,0:T(8,128)(2,1)S(1)}, bf16[160,1280]{1,0:T(8,128)(2,1)S(1)}, u32[]{:S(2)}, u32[]{:S(2)}) %collective-permute-start.22) | collective-permute-done | bytes 409632 | tf_op jit(solution)/shard_map/mixed_gather/ppermute | solution.py:28
  145.2 8.2 %collective-permute-done.23 = bf16[160,1280]{1,0:T(8,128)(2,1)S(1)} collective-permute-done((bf16[160,1280]{1,0:T(8,128)(2,1)S(1)}, bf16[160,1280]{1,0:T(8,128)(2,1)S(1)}, u32[]{:S(2)}, u32[]{:S(2)}) %collective-permute-start.23) | collective-permute-done | bytes 409632 | tf_op jit(solution)/shard_map/mixed_gather/ppermute | solution.py:28
  153.4 2.6 %collective-permute-done.24 = bf16[160,1280]{1,0:T(8,128)(2,1)S(1)} collective-permute-done((bf16[160,1280]{1,0:T(8,128)(2,1)S(1)}, bf16[160,1280]{1,0:T(8,128)(2,1)S(1)}, u32[]{:S(2)}, u32[]{:S(2)}) %collective-permute-start.24) | collective-permute-done | bytes 409632 | tf_op jit(solution)/shard_map/mixed_gather/ppermute | solution.py:28
  160.4 3.0 %fusion.8 = f32[640,640]{1,0:T(8,128)S(1)} fusion(bf16[640,1280]{1,0:T(8,128)(2,1)} %collective-permute-done.25, bf16[320,640]{1,0:T(8,128)(2,1)S(1)} %get-tuple-element.84, bf16[320,640]{1,0:T(8,128)(2,1)S(1)} %get-tuple-element.85, bf16[320,640]{1,0:T(8,128)(2,1)S(1)} %get-tuple-element.86, bf16[320,640]{1,0:T(8,128)(2,1)S(1)} %get-tuple-element.83), kind=kOutput, calls=%fused_computation.43 | convolution fusion | flops 1055129600 | bytes 4915200 | tf_op jit(solution)/shard_map/second_product/dot_general | solution.py:50
  165.1 3.2 %collective-permute-start.27 = (bf16[320,640]{1,0:T(8,128)(2,1)S(1)}, bf16[320,640]{1,0:T(8,128)(2,1)S(1)}, u32[]{:S(2)}, u32[]{:S(2)}) collective-permute-start(bf16[320,640]{1,0:T(8,128)(2,1)S(1)} %bitcast.66), channel_id=1, source_target_pairs={{0,4},{1,5},{2,6},{3,7},{4,0},{5,1},{6,2},{7,3},{8,12},{9,13},{10,... | collective-permute-start | bytes 1228808 | tf_op jit(solution)/shard_map/second_product/ppermute | solution.py:28
  171.5 7.0 %collective-permute-done.27 = bf16[320,640]{1,0:T(8,128)(2,1)S(1)} collective-permute-done((bf16[320,640]{1,0:T(8,128)(2,1)S(1)}, bf16[320,640]{1,0:T(8,128)(2,1)S(1)}, u32[]{:S(2)}, u32[]{:S(2)}) %collective-permute-start.27) | collective-permute-done | bytes 409632 | tf_op jit(solution)/shard_map/second_product/ppermute | solution.py:28
  178.5 9.7 %collective-permute-done.28 = bf16[320,640]{1,0:T(8,128)(2,1)S(1)} collective-permute-done((bf16[320,640]{1,0:T(8,128)(2,1)S(1)}, bf16[320,640]{1,0:T(8,128)(2,1)S(1)}, u32[]{:S(2)}, u32[]{:S(2)}) %collective-permute-start.28) | collective-permute-done | bytes 409632 | tf_op jit(solution)/shard_map/second_product/ppermute | solution.py:28
  189.2 2.6 %combine.1 = (f32[4,40,640]{2,1,0:T(8,128)}, f32[4,40,640]{2,1,0:T(8,128)}) custom-call(s32[5]{0:T(128)} %stack.53.at_ref, f32[320,640]{1,0:T(8,128)} %bitcast.52, bf16[8,40,640]{2,1,0:T(8,128)(2,1)} %bitcast.70, bf16[8,40,640]{2,1,0:T(8,128)(2,1)} %bitcast.68, bf16[8,40,640]{2,1,0:T(8,128)(2,1)} %bitcast.69), custom_call_target="tpu_custom_call" | custom-call | tf_op jit(solution)/shard_map/second_product/combine/pallas_call | solution.py:58
  194.5 2.5 %spread.1 = (bf16[32,40,160]{2,1,0:T(8,128)(2,1)}, f32[40,1280]{1,0:T(8,128)}, f32[40,1280]{1,0:T(8,128)}, f32[40,1280]{1,0:T(8,128)}, f32[40,1280]{1,0:T(8,128)}) custom-call(s32[5]{0:T(128)} %stack.53.at_ref, f32[4,40,640]{2,1,0:T(8,128)} %get-tuple-element.64.stay_ref, f32[4,40,640]{2,1,0:T(8,128)} %copy-done.14), custom_call_target="tpu_custom_call" | custom-call | tf_op jit(solution)/shard_map/second_product/spread/pallas_call | solution.py:58
  196.9 5.3 %all-to-all-start.2 = ((bf16[32,40,160]{2,1,0:T(8,128)(2,1)}), bf16[32,40,160]{2,1,0:T(8,128)(2,1)S(1)}, u32[]{:S(2)}, u32[]{:S(2)}) async-start(bf16[32,40,160]{2,1,0:T(8,128)(2,1)} %get-tuple-element.70), calls=%async_computation.2 | async-start | bytes 1310720 | tf_op jit(solution)/shard_map/transposed/all_to_all | solution.py:289
  207.8 2.6 %collective-permute-done.30.d1 = f32[40,1280]{1,0:T(8,128)S(1)} collective-permute-done((f32[40,1280]{1,0:T(8,128)}, f32[40,1280]{1,0:T(8,128)S(1)}, u32[]{:S(2)}, u32[]{:S(2)}) %collective-permute-start.30) | collective-permute-done | bytes 204832 | tf_op jit(solution)/shard_map/direct/ppermute | solution.py:28
  210.4 4.0 %collective-permute-done.31.d2 = f32[40,1280]{1,0:T(8,128)S(1)} collective-permute-done((f32[40,1280]{1,0:T(8,128)}, f32[40,1280]{1,0:T(8,128)S(1)}, u32[]{:S(2)}, u32[]{:S(2)}) %collective-permute-start.31) | collective-permute-done | bytes 204832 | tf_op jit(solution)/shard_map/direct/ppermute | solution.py:28
  214.5 2.6 %collective-permute-done.32.d3 = f32[40,1280]{1,0:T(8,128)S(1)} collective-permute-done((f32[40,1280]{1,0:T(8,128)}, f32[40,1280]{1,0:T(8,128)S(1)}, u32[]{:S(2)}, u32[]{:S(2)}) %collective-permute-start.32) | collective-permute-done | bytes 204832 | tf_op jit(solution)/shard_map/direct/ppermute | solution.py:28
  218.0 3.9 %finish.1 = f32[40,5120]{1,0:T(8,128)} custom-call(s32[5]{0:T(128)} %stack.53.at_ref, f32[40,1280]{1,0:T(8,128)} %get-tuple-element.66.d0, f32[40,1280]{1,0:T(8,128)} %copy-done.18, f32[40,1280]{1,0:T(8,128)} %copy-done.19, f32[40,1280]{1,0:T(8,128)} %copy-done.20, bf16[32,40,160]{2,1,0:T(8,128)(2,1)} %copy-done, f32[40,40]{1,0:T(8,128)} %fusion.10.kept_ref), custom_call_target="tpu_custom_call" | custom-call | tf_op jit(solution)/shard_map/finish/pallas_call | solution.py:58
  (123 shorter events, 60.8 us)
Async XLA Ops:
  2.0 8.4 %collective-permute-start = (bf16[160,1280]{1,0:T(8,128)(2,1)S(1)}, bf16[160,1280]{1,0:T(8,128)(2,1)S(1)}, u32[]{:S(2)}, u32[]{:S(2)}) collective-permute-start(bf16[160,1280]{1,0:T(8,128)(2,1)S(1)} %get-tuple-element.100), channel_id=1, source_target_pairs={{0,2},{1,3},{2,0},{3,1},{4,6},{5,7},{6,4},{7,5},{8,10},{9,11},{10,... | collective-permute-start | bytes 1228808 | tf_op jit(solution)/shard_map/left_columns/ppermute | solution.py:28
  5.4 26.1 %all-to-all-start = ((bf16[8,160,320]{2,1,0:T(8,128)(2,1)}), bf16[8,160,320]{2,1,0:T(8,128)(2,1)S(1)}, u32[]{:S(2)}, u32[]{:S(2)}) async-start(bf16[8,160,320]{2,1,0:T(8,128)(2,1)} %right_columns.1), calls=%async_computation | async-start | bytes 1966080 | tf_op jit(solution)/shard_map/right_columns/all_to_all | solution.py:186
  13.6 8.1 %collective-permute-start.1 = (bf16[160,640]{1,0:T(8,128)(2,1)}, bf16[160,640]{1,0:T(8,128)(2,1)S(1)}, u32[]{:S(2)}, u32[]{:S(2)}) collective-permute-start(bf16[160,640]{1,0:T(8,128)(2,1)} %get-tuple-element.41), channel_id=1, source_target_pairs={{0,8},{1,9},{2,10},{3,11},{4,12},{5,13},{6,14},{7,15},{8,0},{9,1},... | collective-permute-start | bytes 614408 | tf_op jit(solution)/shard_map/left_columns/ppermute | solution.py:28
  15.2 12.7 %collective-permute-start.2 = (bf16[160,640]{1,0:T(8,128)(2,1)}, bf16[160,640]{1,0:T(8,128)(2,1)S(1)}, u32[]{:S(2)}, u32[]{:S(2)}) collective-permute-start(bf16[160,640]{1,0:T(8,128)(2,1)} %get-tuple-element.42), channel_id=1, source_target_pairs={{0,16},{1,17},{2,18},{3,19},{4,20},{5,21},{6,22},{7,23},{8,24},{9,... | collective-permute-start | bytes 614408 | tf_op jit(solution)/shard_map/left_columns/ppermute | solution.py:28
  18.1 12.4 %collective-permute-start.3 = (bf16[160,640]{1,0:T(8,128)(2,1)}, bf16[160,640]{1,0:T(8,128)(2,1)S(1)}, u32[]{:S(2)}, u32[]{:S(2)}) collective-permute-start(bf16[160,640]{1,0:T(8,128)(2,1)} %get-tuple-element.43), channel_id=1, source_target_pairs={{0,24},{1,25},{2,26},{3,27},{4,28},{5,29},{6,30},{7,31},{8,16},{9,... | collective-permute-start | bytes 614408 | tf_op jit(solution)/shard_map/left_columns/ppermute | solution.py:28
  19.0 13.7 %collective-permute-start.4 = (bf16[80,1280]{1,0:T(8,128)(2,1)S(1)}, bf16[80,1280]{1,0:T(8,128)(2,1)S(1)}, u32[]{:S(2)}, u32[]{:S(2)}) collective-permute-start(bf16[80,1280]{1,0:T(8,128)(2,1)S(1)} %bitcast.71), channel_id=1, source_target_pairs={{0,1},{1,0},{2,3},{3,2},{4,5},{5,4},{6,7},{7,6},{8,9},{9,8},{10,11... | collective-permute-start | bytes 614408 | tf_op jit(solution)/shard_map/density_turn/ppermute | solution.py:28
  32.8 21.4 %collective-permute-start.5 = (bf16[640,640]{1,0:T(8,128)(2,1)S(1)}, bf16[640,640]{1,0:T(8,128)(2,1)}, u32[]{:S(2)}, u32[]{:S(2)}) collective-permute-start(bf16[640,640]{1,0:T(8,128)(2,1)S(1)} %pad_maximum_fusion.5), channel_id=1, source_target_pairs={{0,4},{1,5},{2,6},{3,7},{4,0},{5,1},{6,2},{7,3},{8,12},{9,13},{10,... | collective-permute-start | bytes 2457608 | tf_op jit(solution)/shard_map/left_gather/ppermute | solution.py:28
  33.2 36.1 %collective-permute-start.6 = (bf16[640,640]{1,0:T(8,128)(2,1)S(1)}, bf16[640,640]{1,0:T(8,128)(2,1)S(1)}, u32[]{:S(2)}, u32[]{:S(2)}) collective-permute-start(bf16[640,640]{1,0:T(8,128)(2,1)S(1)} %pad_maximum_fusion.5), channel_id=1, source_target_pairs={{0,5},{1,4},{2,7},{3,6},{4,1},{5,0},{6,3},{7,2},{8,13},{9,12},{10,... | collective-permute-start | bytes 2457608 | tf_op jit(solution)/shard_map/left_gather/ppermute | solution.py:28
  35.5 42.2 %collective-permute-start.7 = (bf16[640,640]{1,0:T(8,128)(2,1)S(1)}, bf16[640,640]{1,0:T(8,128)(2,1)}, u32[]{:S(2)}, u32[]{:S(2)}) collective-permute-start(bf16[640,640]{1,0:T(8,128)(2,1)S(1)} %pad_maximum_fusion.5), channel_id=1, source_target_pairs={{0,1},{1,0},{2,3},{3,2},{4,5},{5,4},{6,7},{7,6},{8,9},{9,8},{10,11... | collective-permute-start | bytes 2457608 | tf_op jit(solution)/shard_map/left_gather/ppermute | solution.py:28
  37.0 42.1 %collective-permute-start.10 = (bf16[320,1280]{1,0:T(8,128)(2,1)S(1)}, bf16[320,1280]{1,0:T(8,128)(2,1)}, u32[]{:S(2)}, u32[]{:S(2)}) collective-permute-start(bf16[320,1280]{1,0:T(8,128)(2,1)S(1)} %reshape.94), channel_id=1, source_target_pairs={{0,96},{1,97},{2,98},{3,99},{4,100},{5,101},{6,102},{7,103},{8,104... | collective-permute-start | bytes 2457608 | tf_op jit(solution)/shard_map/right_gather/ppermute | solution.py:28
  41.0 38.0 %collective-permute-start.8 = (bf16[320,1280]{1,0:T(8,128)(2,1)S(1)}, bf16[320,1280]{1,0:T(8,128)(2,1)}, u32[]{:S(2)}, u32[]{:S(2)}) collective-permute-start(bf16[320,1280]{1,0:T(8,128)(2,1)S(1)} %reshape.94), channel_id=1, source_target_pairs={{0,32},{1,33},{2,34},{3,35},{4,36},{5,37},{6,38},{7,39},{8,40},{9,... | collective-permute-start | bytes 2457608 | tf_op jit(solution)/shard_map/right_gather/ppermute | solution.py:28
  54.2 24.9 %collective-permute-start.9 = (bf16[320,1280]{1,0:T(8,128)(2,1)S(1)}, bf16[320,1280]{1,0:T(8,128)(2,1)}, u32[]{:S(2)}, u32[]{:S(2)}) collective-permute-start(bf16[320,1280]{1,0:T(8,128)(2,1)S(1)} %reshape.94), channel_id=1, source_target_pairs={{0,64},{1,65},{2,66},{3,67},{4,68},{5,69},{6,70},{7,71},{8,72},{9,... | collective-permute-start | bytes 2457608 | tf_op jit(solution)/shard_map/right_gather/ppermute | solution.py:28
  71.6 10.9 %all-to-all-start.1 = ((bf16[4,80,640]{2,1,0:T(8,128)(2,1)}), bf16[4,80,640]{2,1,0:T(8,128)(2,1)S(1)}, u32[]{:S(2)}, u32[]{:S(2)}) async-start(bf16[4,80,640]{2,1,0:T(8,128)(2,1)} %density_columns.1), calls=%async_computation.1 | async-start | bytes 819200 | tf_op jit(solution)/shard_map/density_columns/all_to_all | solution.py:218
  88.7 4.2 %collective-permute-start.13 = (f32[160,1280]{1,0:T(8,128)S(1)}, f32[160,1280]{1,0:T(8,128)S(1)}, u32[]{:S(2)}, u32[]{:S(2)}) collective-permute-start(f32[160,1280]{1,0:T(8,128)S(1)} %get-tuple-element.77), channel_id=1, source_target_pairs={{0,2},{1,3},{2,0},{3,1},{4,6},{5,7},{6,4},{7,5},{8,10},{9,11},{10,... | collective-permute-start | bytes 2457608 | tf_op jit(solution)/shard_map/mixed_sum/ppermute | solution.py:28
  88.8 5.2 %collective-permute-start.16 = (f32[160,1280]{1,0:T(8,128)S(1)}, f32[160,1280]{1,0:T(8,128)S(1)}, u32[]{:S(2)}, u32[]{:S(2)}) collective-permute-start(f32[160,1280]{1,0:T(8,128)S(1)} %get-tuple-element.76), channel_id=1, source_target_pairs={{0,2},{1,3},{2,0},{3,1},{4,6},{5,7},{6,4},{7,5},{8,10},{9,11},{10,... | collective-permute-start | bytes 2457608 | tf_op jit(solution)/shard_map/mixed_sum/ppermute | solution.py:28
  94.5 11.6 %collective-permute-start.17 = (f32[80,1280]{1,0:T(8,128)S(1)}, f32[80,1280]{1,0:T(8,128)S(1)}, u32[]{:S(2)}, u32[]{:S(2)}) collective-permute-start(f32[80,1280]{1,0:T(8,128)S(1)} %get-tuple-element.95), channel_id=1, source_target_pairs={{0,8},{1,9},{2,10},{3,11},{4,12},{5,13},{6,14},{7,15},{8,0},{9,1},... | collective-permute-start | bytes 1228808 | tf_op jit(solution)/shard_map/mixed_sum/ppermute | solution.py:28
  95.1 12.4 %collective-permute-start.14 = (f32[80,1280]{1,0:T(8,128)S(1)}, f32[80,1280]{1,0:T(8,128)S(1)}, u32[]{:S(2)}, u32[]{:S(2)}) collective-permute-start(f32[80,1280]{1,0:T(8,128)S(1)} %get-tuple-element.96), channel_id=1, source_target_pairs={{0,24},{1,25},{2,26},{3,27},{4,28},{5,29},{6,30},{7,31},{8,16},{9,... | collective-permute-start | bytes 1228808 | tf_op jit(solution)/shard_map/mixed_sum/ppermute | solution.py:28
  106.2 27.0 %collective-permute-start.18 = (f32[160,1280]{1,0:T(8,128)S(1)}, f32[160,1280]{1,0:T(8,128)S(1)}, u32[]{:S(2)}, u32[]{:S(2)}) collective-permute-start(f32[160,1280]{1,0:T(8,128)S(1)} %pad_maximum_fusion.7), channel_id=1, source_target_pairs={{0,24},{1,25},{2,26},{3,27},{4,28},{5,29},{6,30},{7,31},{8,16},{9,... | collective-permute-start | bytes 2457608 | tf_op jit(solution)/shard_map/mixed_sum/ppermute | solution.py:28
  107.7 26.2 %collective-permute-start.15 = (f32[160,1280]{1,0:T(8,128)S(1)}, f32[160,1280]{1,0:T(8,128)S(1)}, u32[]{:S(2)}, u32[]{:S(2)}) collective-permute-start(f32[160,1280]{1,0:T(8,128)S(1)} %pad_maximum_fusion.6), channel_id=1, source_target_pairs={{0,8},{1,9},{2,10},{3,11},{4,12},{5,13},{6,14},{7,15},{8,0},{9,1},... | collective-permute-start | bytes 2457608 | tf_op jit(solution)/shard_map/mixed_sum/ppermute | solution.py:28
  108.0 12.4 %collective-permute-start.19 = (bf16[320,640]{1,0:T(8,128)(2,1)S(1)}, bf16[320,640]{1,0:T(8,128)(2,1)S(1)}, u32[]{:S(2)}, u32[]{:S(2)}) collective-permute-start(bf16[320,640]{1,0:T(8,128)(2,1)S(1)} %bitcast.54), channel_id=1, source_target_pairs={{0,32},{1,33},{2,34},{3,35},{4,36},{5,37},{6,38},{7,39},{8,40},{9,... | collective-permute-start | bytes 1228808 | tf_op jit(solution)/shard_map/density_gather/ppermute | solution.py:28
  110.0 20.6 %collective-permute-start.20 = (bf16[320,640]{1,0:T(8,128)(2,1)S(1)}, bf16[320,640]{1,0:T(8,128)(2,1)S(1)}, u32[]{:S(2)}, u32[]{:S(2)}) collective-permute-start(bf16[320,640]{1,0:T(8,128)(2,1)S(1)} %bitcast.55), channel_id=1, source_target_pairs={{0,64},{1,65},{2,66},{3,67},{4,68},{5,69},{6,70},{7,71},{8,72},{9,... | collective-permute-start | bytes 1228808 | tf_op jit(solution)/shard_map/density_gather/ppermute | solution.py:28
  113.5 19.6 %collective-permute-start.21 = (bf16[320,640]{1,0:T(8,128)(2,1)S(1)}, bf16[320,640]{1,0:T(8,128)(2,1)S(1)}, u32[]{:S(2)}, u32[]{:S(2)}) collective-permute-start(bf16[320,640]{1,0:T(8,128)(2,1)S(1)} %bitcast.56), channel_id=1, source_target_pairs={{0,96},{1,97},{2,98},{3,99},{4,100},{5,101},{6,102},{7,103},{8,104... | collective-permute-start | bytes 1228808 | tf_op jit(solution)/shard_map/density_gather/ppermute | solution.py:28
  134.1 11.2 %collective-permute-start.22 = (bf16[160,1280]{1,0:T(8,128)(2,1)S(1)}, bf16[160,1280]{1,0:T(8,128)(2,1)S(1)}, u32[]{:S(2)}, u32[]{:S(2)}) collective-permute-start(bf16[160,1280]{1,0:T(8,128)(2,1)S(1)} %add_convert_fusion), channel_id=1, source_target_pairs={{0,8},{1,9},{2,10},{3,11},{4,12},{5,13},{6,14},{7,15},{8,0},{9,1},... | collective-permute-start | bytes 1228808 | tf_op jit(solution)/shard_map/mixed_gather/ppermute | solution.py:28
  135.8 17.6 %collective-permute-start.23 = (bf16[160,1280]{1,0:T(8,128)(2,1)S(1)}, bf16[160,1280]{1,0:T(8,128)(2,1)S(1)}, u32[]{:S(2)}, u32[]{:S(2)}) collective-permute-start(bf16[160,1280]{1,0:T(8,128)(2,1)S(1)} %add_convert_fusion), channel_id=1, source_target_pairs={{0,16},{1,17},{2,18},{3,19},{4,20},{5,21},{6,22},{7,23},{8,24},{9,... | collective-permute-start | bytes 1228808 | tf_op jit(solution)/shard_map/mixed_gather/ppermute | solution.py:28
  137.6 18.3 %collective-permute-start.24 = (bf16[160,1280]{1,0:T(8,128)(2,1)S(1)}, bf16[160,1280]{1,0:T(8,128)(2,1)S(1)}, u32[]{:S(2)}, u32[]{:S(2)}) collective-permute-start(bf16[160,1280]{1,0:T(8,128)(2,1)S(1)} %add_convert_fusion), channel_id=1, source_target_pairs={{0,24},{1,25},{2,26},{3,27},{4,28},{5,29},{6,30},{7,31},{8,16},{9,... | collective-permute-start | bytes 1228808 | tf_op jit(solution)/shard_map/mixed_gather/ppermute | solution.py:28
  165.1 13.4 %collective-permute-start.27 = (bf16[320,640]{1,0:T(8,128)(2,1)S(1)}, bf16[320,640]{1,0:T(8,128)(2,1)S(1)}, u32[]{:S(2)}, u32[]{:S(2)}) collective-permute-start(bf16[320,640]{1,0:T(8,128)(2,1)S(1)} %bitcast.66), channel_id=1, source_target_pairs={{0,4},{1,5},{2,6},{3,7},{4,0},{5,1},{6,2},{7,3},{8,12},{9,13},{10,... | collective-permute-start | bytes 1228808 | tf_op jit(solution)/shard_map/second_product/ppermute | solution.py:28
  168.3 20.0 %collective-permute-start.28 = (bf16[320,640]{1,0:T(8,128)(2,1)S(1)}, bf16[320,640]{1,0:T(8,128)(2,1)S(1)}, u32[]{:S(2)}, u32[]{:S(2)}) collective-permute-start(bf16[320,640]{1,0:T(8,128)(2,1)S(1)} %bitcast.65), channel_id=1, source_target_pairs={{0,5},{1,4},{2,7},{3,6},{4,1},{5,0},{6,3},{7,2},{8,13},{9,12},{10,... | collective-permute-start | bytes 1228808 | tf_op jit(solution)/shard_map/second_product/ppermute | solution.py:28
  169.8 18.5 %collective-permute-start.26 = (bf16[320,640]{1,0:T(8,128)(2,1)S(1)}, bf16[320,640]{1,0:T(8,128)(2,1)S(1)}, u32[]{:S(2)}, u32[]{:S(2)}) collective-permute-start(bf16[320,640]{1,0:T(8,128)(2,1)S(1)} %bitcast.67), channel_id=1, source_target_pairs={{0,1},{1,0},{2,3},{3,2},{4,5},{5,4},{6,7},{7,6},{8,9},{9,8},{10,11... | collective-permute-start | bytes 1228808 | tf_op jit(solution)/shard_map/second_product/ppermute | solution.py:28
  196.9 20.1 %all-to-all-start.2 = ((bf16[32,40,160]{2,1,0:T(8,128)(2,1)}), bf16[32,40,160]{2,1,0:T(8,128)(2,1)S(1)}, u32[]{:S(2)}, u32[]{:S(2)}) async-start(bf16[32,40,160]{2,1,0:T(8,128)(2,1)} %get-tuple-element.70), calls=%async_computation.2 | async-start | bytes 1310720 | tf_op jit(solution)/shard_map/transposed/all_to_all | solution.py:289
  202.2 8.2 %collective-permute-start.30 = (f32[40,1280]{1,0:T(8,128)}, f32[40,1280]{1,0:T(8,128)S(1)}, u32[]{:S(2)}, u32[]{:S(2)}) collective-permute-start(f32[40,1280]{1,0:T(8,128)} %get-tuple-element.67), channel_id=1, source_target_pairs={{0,8},{1,9},{2,10},{3,11},{4,12},{5,13},{6,14},{7,15},{8,0},{9,1},... | collective-permute-start | bytes 614408 | tf_op jit(solution)/shard_map/direct/ppermute | solution.py:28
  202.3 12.1 %collective-permute-start.31 = (f32[40,1280]{1,0:T(8,128)}, f32[40,1280]{1,0:T(8,128)S(1)}, u32[]{:S(2)}, u32[]{:S(2)}) collective-permute-start(f32[40,1280]{1,0:T(8,128)} %get-tuple-element.68), channel_id=1, source_target_pairs={{0,16},{1,17},{2,18},{3,19},{4,20},{5,21},{6,22},{7,23},{8,24},{9,... | collective-permute-start | bytes 614408 | tf_op jit(solution)/shard_map/direct/ppermute | solution.py:28
  204.7 12.4 %collective-permute-start.32 = (f32[40,1280]{1,0:T(8,128)}, f32[40,1280]{1,0:T(8,128)S(1)}, u32[]{:S(2)}, u32[]{:S(2)}) collective-permute-start(f32[40,1280]{1,0:T(8,128)} %get-tuple-element.69), channel_id=1, source_target_pairs={{0,24},{1,25},{2,26},{3,27},{4,28},{5,29},{6,30},{7,31},{8,16},{9,... | collective-permute-start | bytes 614408 | tf_op jit(solution)/shard_map/direct/ppermute | solution.py:28
  (27 other events, 159.8 us)

commit v5 on v4

--- a/solution.py
+++ b/solution.py
@@ -110,31 +110,18 @@
         out_ref[ny] = jnp.concatenate((first[:, cut], second[:, cut]), axis=1)
 
 
-def combine_kernel(at_ref, own_ref, a_ref, b_ref, c_ref, stay_ref, away_ref):
-    core = at_ref[3]
+def spread_kernel(at_ref, *refs):
+    many, last = refs[:4], refs[4:8]
+    turned_ref, outs, slots = refs[8], refs[9:13], refs[13]
+    y = at_ref[1]
     for q in range(4):
-        halves = []
-        for nc in range(2):
-            rows = slice((q * 2 + nc) * 40, (q * 2 + nc) * 40 + 40)
-            halves.append(
-                own_ref[rows]
-                + a_ref[q * 2 + nc].astype(f32)
-                + b_ref[q * 2 + nc].astype(f32)
-                + c_ref[q * 2 + nc].astype(f32)
-            )
-        stay_ref[q] = jnp.where(core == 0, halves[0], halves[1])
-        away_ref[q] = jnp.where(core == 0, halves[1], halves[0])
-
-
-def spread_kernel(at_ref, stay_ref, came_ref, turned_ref, d0, d1, d2, d3, slots):
-    y, core = at_ref[1], at_ref[3]
-    for q, ref in enumerate((d0, d1, d2, d3)):
-        low = jnp.where(core == 0, stay_ref[q], came_ref[q])
-        high = jnp.where(core == 0, came_ref[q], stay_ref[q])
-        ref[:, :640] = low
-        ref[:, 640:] = high
-        slots[y ^ q, :, :640] = low
-        slots[y ^ q, :, 640:] = high
+        parts = last if q == 2 else many
+        place = 0 if q == 2 else (0, 1, None, 2)[q]
+        total = parts[0][place].astype(f32)
+        for ref in parts[1:]:
+            total = total + ref[place].astype(f32)
+        outs[q][...] = total
+        slots[y ^ q] = total
     for nz in range(4):
         part = jnp.concatenate(
             [slots[ny, :, nz * 320 : nz * 320 + 320] for ny in range(4)], axis=0
@@ -209,9 +196,7 @@
         }
 
     with jax.named_scope("density_columns"):
-        same, other, lefts[1, 0], lefts[1, 1] = lax.optimization_barrier(
-            (same, other, lefts[1, 0], lefts[1, 1])
-        )
+        same, other, lefts[1, 0] = lax.optimization_barrier((same, other, lefts[1, 0]))
         cols = local_call(
             density_kernel, "density_columns", shape(bf16, 4, 80, 640), coords, same, other
         )
@@ -252,36 +237,47 @@
         mixed = total.astype(bf16)
 
     with jax.named_scope("density_rows"):
-        dparts = jnp.stack(dparts)
-        dfull = jnp.concatenate([pick(dparts, z ^ nz) for nz in range(4)])
+        mixed, dparts = lax.optimization_barrier((mixed, dparts))
+        dmine = jnp.concatenate([pick(jnp.stack(dparts), z ^ nz) for nz in range(4)])
+        dother = flip(dmine, core=1)
+        dfull = jnp.where(
+            core == 0,
+            jnp.concatenate((dmine, dother), axis=1),
+            jnp.concatenate((dother, dmine), axis=1),
+        )
 
     with jax.named_scope("mixed_gather"):
-        mslots = jnp.concatenate([mixed] + [flip(mixed, y=q) for q in (1, 2, 3)])
-        mother = flip(mslots, core=1)
+        mslots = [mixed] + [flip(mixed, y=q) for q in (1, 2, 3)]
 
     with jax.named_scope("second_product"):
-        near = dot(mslots, dfull).reshape(4, 160, 640)
-        far = dot(mother, dfull).reshape(4, 160, 640)
-
-        def piece(h, r):
-            rows = jnp.where(core == h, near, far).reshape(8, 2, 40, 640)
-            return lax.dynamic_index_in_dim(rows, xh ^ r, 1, keepdims=False).reshape(320, 640)
-
-        came = [
-            flip(piece(h, r).astype(bf16), xl=h, xh=r).reshape(8, 40, 640)
-            for h, r in ((0, 1), (1, 0), (1, 1))
-        ]
-        stay, away = local_call(
-            combine_kernel, "combine", [shape(f32, 4, 40, 640)] * 2, coords, piece(0, 0), *came
-        )
-        away = flip(away, core=1)
+        turns = [(r, t) for r in range(2) for t in range(2)]
+
+        def pieces_of(rows, count):
+            resp = dot(rows, dfull).reshape(count, 2, 2, 40, 1280)
+            cut = []
+            for r, t in turns:
+                piece = lax.dynamic_index_in_dim(resp, core ^ t, 1, keepdims=False)
+                piece = lax.dynamic_index_in_dim(piece, xh ^ r, 1, keepdims=False)
+                cut.append(piece.astype(bf16))
+            return cut
+
+        def scatter(cut):
+            return [
+                remap(piece, lambda a, b, c, d, e: (a, b, c ^ d, d ^ t, e ^ r))
+                for piece, (r, t) in zip(cut, turns)
+            ]
+
+        many = pieces_of(jnp.concatenate((mslots[0], mslots[1], mslots[3])), 3)
+        many = scatter(many)
+        many[0], mslots[2] = lax.optimization_barrier((many[0], mslots[2]))
+        last = scatter(pieces_of(mslots[2], 1))
         turned, *rows = local_call(
             spread_kernel,
             "spread",
             [shape(bf16, 32, 40, 160)] + [shape(f32, 40, 1280)] * 4,
             coords,
-            stay,
-            away,
+            *many,
+            *last,
             scratch=[pltpu.VMEM((4, 40, 1280), f32)],
         )
 

time: 223 us -> 218 us (0.978)
  waiting for transfers between devices: 117 us -> 80.5 us
  other arithmetic: 11.1 us -> 40.7 us
  starting transfers between devices: 57 us -> 66.9 us
  local copies, waits for them, and re-layouts: 10.1 us -> 6.7 us
  Pallas kernels: 16.5 us -> 14 us
    ppermute x33 -> x29, waiting for transfers between devices: 114 us -> 75.5 us  [flip(): return lax.ppermute(value, AXES, pairs)]
    select_n x1, other arithmetic: 0.16 us -> 26.7 us  [shards(): jnp.where(core == 0, jnp.concatenate((dmine, dother), axis=1), jnp.concat...]
    ppermute x0 -> x8, starting transfers between devices: none -> 18.7 us  [remap(): return lax.ppermute(value, AXES, pairs)]
    ppermute x33 -> x29, starting transfers between devices: 43.3 us -> 34.5 us  [flip(): return lax.ppermute(value, AXES, pairs)]
    ppermute x0 -> x8, waiting for transfers between devices: none -> 4.99 us  [remap(): return lax.ppermute(value, AXES, pairs)]
    all_to_all x1, waiting for transfers between devices: 3.45 us -> 0.01 us  [shards(): dslots = lax.all_to_all(cols, 'y', split_axis=0, concat_axis=0, tiled=True)]
    pallas_call x6 -> x5, Pallas kernels: 16.5 us -> 14 us  [local_call(): pl.pallas_call(kernel, out_shape=outs, in_specs=[SMEM] + [VMEM] * len(ope...]
    unnamed x46 -> x40, local copies, waits for them, and re-layouts: 5.69 us -> 3.26 us
  transfers between devices with their start and end apart: 36 -> 40, of which waited for: 24 -> 21; matrix products, arithmetic and copies ran while one was open for 6% -> 19% of each run, Pallas kernels for 3% -> 3%
where the time goes in v5:
time: 218 us; the launch traced here: 217 us
  waiting for transfers between devices  80.5 us (37%)
  starting transfers between devices  66.9 us (31%)
  other arithmetic  40.7 us (19%)
  Pallas kernels  14 us (6%)
  matrix products  7.84 us (4%)
  local copies, waits for them, and re-layouts  6.7 us (3%)
    ppermute x29, waiting for transfers between devices, flip(): return lax.ppermute(value, AXES, pairs)  75.5 us
    ppermute x29, starting transfers between devices, flip(): return lax.ppermute(value, AXES, pairs)  34.5 us
    select_n x1, other arithmetic, shards(): jnp.where(core == 0, jnp.concatenate((dmine, dother), axis=1), jnp.concat...  26.7 us
    ppermute x8, starting transfers between devices, remap(): return lax.ppermute(value, AXES, pairs)  18.7 us
    pallas_call x5, Pallas kernels, local_call(): pl.pallas_call(kernel, out_shape=outs, in_specs=[SMEM] + [VMEM] * len(ope...  14 us
    dot_general x4, matrix products, dot(): return jnp.dot(a, b, preferred_element_type=f32)  7.05 us
    all_to_all x1, starting transfers between devices, shards(): lax.all_to_all(turned, ('z', 'xl', 'core', 'xh'), split_axis=0, concat_ax...  5.35 us
    ppermute x8, waiting for transfers between devices, remap(): return lax.ppermute(value, AXES, pairs)  4.99 us
  transfers between devices with their start and end apart: 40, of which 21 were waited for; matrix products, arithmetic and copies ran while one was open for 19% of the time, Pallas kernels for 3%

profile of v5, /device:TPU:2, one launch (start us, length us, event | category | flops | bytes accessed | tf_op | source)
XLA Modules:
  0.0 217.1 jit_solution(652148703946092776)
XLA Ops:
  2.6 2.8 %right_columns.1 = bf16[8,160,320]{2,1,0:T(8,128)(2,1)} custom-call(s32[5]{0:T(128)} %stack.68.at_ref, bf16[160,1280]{1,0:T(8,128)(2,1)} %first_ref, bf16[160,1280]{1,0:T(8,128)(2,1)} %second_ref), custom_call_target="tpu_custom_call" | custom-call | tf_op jit(solution)/shard_map/right_columns/right_columns/pallas_call | solution.py:58
  5.4 4.9 %all-to-all-start = ((bf16[8,160,320]{2,1,0:T(8,128)(2,1)}), bf16[8,160,320]{2,1,0:T(8,128)(2,1)S(1)}, u32[]{:S(2)}, u32[]{:S(2)}) async-start(bf16[8,160,320]{2,1,0:T(8,128)(2,1)} %right_columns.1), calls=%async_computation | async-start | bytes 1966080 | tf_op jit(solution)/shard_map/right_columns/all_to_all | solution.py:173
  11.1 2.5 %left_columns.1 = (bf16[160,640]{1,0:T(8,128)(2,1)}, bf16[160,640]{1,0:T(8,128)(2,1)}, bf16[160,640]{1,0:T(8,128)(2,1)}, bf16[160,640]{1,0:T(8,128)(2,1)}) custom-call(s32[5]{0:T(128)} %stack.68.at_ref, bf16[160,1280]{1,0:T(8,128)(2,1)} %get-tuple-element.109.keep_ref, bf16[160,1280]{1,0:T(8,128)(2,1)} %copy-done.5), custom_call_target="tpu_custom_call" | custom-call | tf_op jit(solution)/shard_map/left_columns/left_columns/pallas_call | solution.py:58
  15.2 2.9 %collective-permute-start.2 = (bf16[160,640]{1,0:T(8,128)(2,1)}, bf16[160,640]{1,0:T(8,128)(2,1)S(1)}, u32[]{:S(2)}, u32[]{:S(2)}) collective-permute-start(bf16[160,640]{1,0:T(8,128)(2,1)} %get-tuple-element.46), channel_id=1, source_target_pairs={{0,16},{1,17},{2,18},{3,19},{4,20},{5,21},{6,22},{7,23},{8,24},{9,... | collective-permute-start | bytes 614408 | tf_op jit(solution)/shard_map/left_columns/ppermute | solution.py:28
  21.8 6.2 %collective-permute-done.2 = bf16[160,640]{1,0:T(8,128)(2,1)S(1)} collective-permute-done((bf16[160,640]{1,0:T(8,128)(2,1)}, bf16[160,640]{1,0:T(8,128)(2,1)S(1)}, u32[]{:S(2)}, u32[]{:S(2)}) %collective-permute-start.2) | collective-permute-done | bytes 204832 | tf_op jit(solution)/shard_map/left_columns/ppermute | solution.py:28
  27.9 2.6 %collective-permute-done.3 = bf16[160,640]{1,0:T(8,128)(2,1)S(1)} collective-permute-done((bf16[160,640]{1,0:T(8,128)(2,1)}, bf16[160,640]{1,0:T(8,128)(2,1)S(1)}, u32[]{:S(2)}, u32[]{:S(2)}) %collective-permute-start.3) | collective-permute-done | bytes 204832 | tf_op jit(solution)/shard_map/left_columns/ppermute | solution.py:28
  33.2 2.6 %collective-permute-start.6 = (bf16[640,640]{1,0:T(8,128)(2,1)S(1)}, bf16[640,640]{1,0:T(8,128)(2,1)}, u32[]{:S(2)}, u32[]{:S(2)}) collective-permute-start(bf16[640,640]{1,0:T(8,128)(2,1)S(1)} %pad_maximum_fusion.4), channel_id=1, source_target_pairs={{0,1},{1,0},{2,3},{3,2},{4,5},{5,4},{6,7},{7,6},{8,9},{9,8},{10,11... | collective-permute-start | bytes 2457608 | tf_op jit(solution)/shard_map/left_gather/ppermute | solution.py:28
  36.4 4.0 %collective-permute-start.10 = (bf16[320,1280]{1,0:T(8,128)(2,1)S(1)}, bf16[320,1280]{1,0:T(8,128)(2,1)}, u32[]{:S(2)}, u32[]{:S(2)}) collective-permute-start(bf16[320,1280]{1,0:T(8,128)(2,1)S(1)} %reshape.136), channel_id=1, source_target_pairs={{0,96},{1,97},{2,98},{3,99},{4,100},{5,101},{6,102},{7,103},{8,104... | collective-permute-start | bytes 2457608 | tf_op jit(solution)/shard_map/right_gather/ppermute | solution.py:28
  40.4 13.6 %collective-permute-done.5 = bf16[640,640]{1,0:T(8,128)(2,1)S(1)} collective-permute-done((bf16[640,640]{1,0:T(8,128)(2,1)S(1)}, bf16[640,640]{1,0:T(8,128)(2,1)S(1)}, u32[]{:S(2)}, u32[]{:S(2)}) %collective-permute-start.5) | collective-permute-done | bytes 819232 | tf_op jit(solution)/shard_map/left_gather/ppermute | solution.py:28
  54.1 3.9 %collective-permute-start.9 = (bf16[320,1280]{1,0:T(8,128)(2,1)S(1)}, bf16[320,1280]{1,0:T(8,128)(2,1)}, u32[]{:S(2)}, u32[]{:S(2)}) collective-permute-start(bf16[320,1280]{1,0:T(8,128)(2,1)S(1)} %reshape.136), channel_id=1, source_target_pairs={{0,64},{1,65},{2,66},{3,67},{4,68},{5,69},{6,70},{7,71},{8,72},{9,... | collective-permute-start | bytes 2457608 | tf_op jit(solution)/shard_map/right_gather/ppermute | solution.py:28
  59.9 3.5 %all-to-all-start.1 = ((bf16[4,80,640]{2,1,0:T(8,128)(2,1)}), bf16[4,80,640]{2,1,0:T(8,128)(2,1)S(1)}, u32[]{:S(2)}, u32[]{:S(2)}) async-start(bf16[4,80,640]{2,1,0:T(8,128)(2,1)} %density_columns.1), calls=%async_computation.1 | async-start | bytes 819200 | tf_op jit(solution)/shard_map/density_columns/all_to_all | solution.py:203
  63.4 2.5 %broadcast_select_fusion.3 = (bf16[640,640]{1,0:T(8,128)(2,1)}, bf16[640,640]{1,0:T(8,128)(2,1)}) fusion(bf16[640,640]{1,0:T(8,128)(2,1)S(1)} %pad_maximum_fusion.4, bf16[640,640]{1,0:T(8,128)(2,1)} %copy-done.3, pred[]{:T(512)S(6)} %eq.8), kind=kLoop, calls=%fused_computation.35 | loop fusion | flops 819200 | bytes 3276801 | tf_op jit(solution)/shard_map/first_product/jit(_where)/select_n | solution.py:217
  65.8 4.7 %collective-permute-done.6 = bf16[640,640]{1,0:T(8,128)(2,1)} collective-permute-done((bf16[640,640]{1,0:T(8,128)(2,1)S(1)}, bf16[640,640]{1,0:T(8,128)(2,1)}, u32[]{:S(2)}, u32[]{:S(2)}) %collective-permute-start.6) | collective-permute-done | bytes 819232 | tf_op jit(solution)/shard_map/left_gather/ppermute | solution.py:28
  73.5 2.2 %collective-permute-done.9 = bf16[320,1280]{1,0:T(8,128)(2,1)} collective-permute-done((bf16[320,1280]{1,0:T(8,128)(2,1)S(1)}, bf16[320,1280]{1,0:T(8,128)(2,1)}, u32[]{:S(2)}, u32[]{:S(2)}) %collective-permute-start.9) | collective-permute-done | bytes 819232 | tf_op jit(solution)/shard_map/right_gather/ppermute | solution.py:28
  78.7 2.3 %fusion.4 = f32[640,1280]{1,0:T(8,128)S(1)} fusion(bf16[640,640]{1,0:T(8,128)(2,1)S(1)} %get-tuple-element.98, bf16[640,640]{1,0:T(8,128)(2,1)S(1)} %copy-done.4, bf16[320,1280]{1,0:T(8,128)(2,1)S(1)} %get-tuple-element.88, bf16[320,1280]{1,0:T(8,128)(2,1)S(1)} %get-tuple-element.89, bf16[320,1280]{1,0:T(8,128)(2,1)S(1)} %get-tuple-element.90, ...), kind=kOutput, calls=%fused_computation.7 | convolution fusion | flops 2113536000 | bytes 8192000 | tf_op jit(solution)/shard_map/first_product/dot_general | solution.py:50
  82.4 2.3 %fusion = f32[640,1280]{1,0:T(8,128)S(1)} fusion(bf16[640,640]{1,0:T(8,128)(2,1)S(1)} %get-tuple-element.97, bf16[640,640]{1,0:T(8,128)(2,1)S(1)} %copy-done.2, bf16[320,1280]{1,0:T(8,128)(2,1)S(1)} %get-tuple-element.88, bf16[320,1280]{1,0:T(8,128)(2,1)S(1)} %get-tuple-element.89, bf16[320,1280]{1,0:T(8,128)(2,1)S(1)} %get-tuple-element.90, ...), kind=kOutput, calls=%fused_computation.3 | convolution fusion | flops 2113536000 | bytes 8192000 | tf_op jit(solution)/shard_map/first_product/dot_general | solution.py:50
  88.2 11.1 %collective-permute-done.17 = f32[80,1280]{1,0:T(8,128)S(1)} collective-permute-done((f32[80,1280]{1,0:T(8,128)S(1)}, f32[80,1280]{1,0:T(8,128)S(1)}, u32[]{:S(2)}, u32[]{:S(2)}) %collective-permute-start.17) | collective-permute-done | bytes 409632 | tf_op jit(solution)/shard_map/mixed_sum/ppermute | solution.py:28
  102.1 4.4 %collective-permute-start.20 = (bf16[320,640]{1,0:T(8,128)(2,1)S(1)}, bf16[320,640]{1,0:T(8,128)(2,1)}, u32[]{:S(2)}, u32[]{:S(2)}) collective-permute-start(bf16[320,640]{1,0:T(8,128)(2,1)S(1)} %bitcast.78), channel_id=1, source_target_pairs={{0,64},{1,65},{2,66},{3,67},{4,68},{5,69},{6,70},{7,71},{8,72},{9,... | collective-permute-start | bytes 1228808 | tf_op jit(solution)/shard_map/density_gather/ppermute | solution.py:28
  106.8 7.7 %collective-permute-done.19 = bf16[320,640]{1,0:T(8,128)(2,1)S(1)} collective-permute-done((bf16[320,640]{1,0:T(8,128)(2,1)S(1)}, bf16[320,640]{1,0:T(8,128)(2,1)S(1)}, u32[]{:S(2)}, u32[]{:S(2)}) %collective-permute-start.19) | collective-permute-done | bytes 409632 | tf_op jit(solution)/shard_map/density_gather/ppermute | solution.py:28
  114.5 9.2 %collective-permute-done.20 = bf16[320,640]{1,0:T(8,128)(2,1)} collective-permute-done((bf16[320,640]{1,0:T(8,128)(2,1)S(1)}, bf16[320,640]{1,0:T(8,128)(2,1)}, u32[]{:S(2)}, u32[]{:S(2)}) %collective-permute-start.20) | collective-permute-done | bytes 409632 | tf_op jit(solution)/shard_map/density_gather/ppermute | solution.py:28
  123.7 2.6 %collective-permute-done.21 = bf16[320,640]{1,0:T(8,128)(2,1)} collective-permute-done((bf16[320,640]{1,0:T(8,128)(2,1)S(1)}, bf16[320,640]{1,0:T(8,128)(2,1)}, u32[]{:S(2)}, u32[]{:S(2)}) %collective-permute-start.21) | collective-permute-done | bytes 409632 | tf_op jit(solution)/shard_map/density_gather/ppermute | solution.py:28
  134.3 26.7 %maximum_select_fusion = bf16[1280,1280]{1,0:T(8,128)(2,1)S(1)} fusion(bf16[1280,640]{1,0:T(8,128)(2,1)} %collective-permute-done.24, bf16[320,640]{1,0:T(8,128)(2,1)S(1)} %get-tuple-element.92, bf16[320,640]{1,0:T(8,128)(2,1)S(1)} %get-tuple-element.93, bf16[320,640]{1,0:T(8,128)(2,1)S(1)} %get-tuple-element.94, bf16[320,640]{1,0:T(8,128)(2,1)S(1)} %get-tuple-element.91, ...), kind=kLoop, calls=%fused_computation.2 | loop fusion | flops 34406400 | bytes 6553601 | tf_op jit(solution)/shard_map/density_rows/jit(_where)/select_n | solution.py:243
  163.6 2.4 %collective-permute-start.27 = (bf16[3,40,1280]{2,1,0:T(8,128)(2,1)S(1)}, bf16[3,40,1280]{2,1,0:T(8,128)(2,1)S(1)}, u32[]{:S(2)}, u32[]{:S(2)}) collective-permute-start(bf16[3,40,1280]{2,1,0:T(8,128)(2,1)S(1)} %get-tuple-element.101), channel_id=1, source_target_pairs={{0,2},{1,3},{2,4},{3,5},{4,6},{5,7},{6,0},{7,1},{8,10},{9,11},{10,... | collective-permute-start | bytes 921608 | tf_op jit(solution)/shard_map/second_product/ppermute | solution.py:42
  169.3 6.2 %collective-permute-start.31 = (bf16[1,40,1280]{2,1,0:T(8,128)(2,1)S(1)}, bf16[1,40,1280]{2,1,0:T(8,128)(2,1)S(1)}, u32[]{:S(2)}, u32[]{:S(2)}) collective-permute-start(bf16[1,40,1280]{2,1,0:T(8,128)(2,1)S(1)} %get-tuple-element.113), channel_id=1, source_target_pairs={{0,2},{1,3},{2,4},{3,5},{4,6},{5,7},{6,0},{7,1},{8,10},{9,11},{10,... | collective-permute-start | bytes 307208 | tf_op jit(solution)/shard_map/second_product/ppermute | solution.py:42
  175.7 6.9 %collective-permute-start.32 = (bf16[1,40,1280]{2,1,0:T(8,128)(2,1)S(1)}, bf16[1,40,1280]{2,1,0:T(8,128)(2,1)S(1)}, u32[]{:S(2)}, u32[]{:S(2)}) collective-permute-start(bf16[1,40,1280]{2,1,0:T(8,128)(2,1)S(1)} %get-tuple-element.112), channel_id=1, source_target_pairs={{0,1},{1,0},{2,7},{3,6},{4,5},{5,4},{6,3},{7,2},{8,9},{9,8},{10,15... | collective-permute-start | bytes 307208 | tf_op jit(solution)/shard_map/second_product/ppermute | solution.py:42
  182.7 2.6 %collective-permute-done.32.refs_6_ = bf16[1,40,1280]{2,1,0:T(8,128)(2,1)S(1)} collective-permute-done((bf16[1,40,1280]{2,1,0:T(8,128)(2,1)S(1)}, bf16[1,40,1280]{2,1,0:T(8,128)(2,1)S(1)}, u32[]{:S(2)}, u32[]{:S(2)}) %collective-permute-start.32) | collective-permute-done | bytes 102432 | tf_op jit(solution)/shard_map/second_product/ppermute | solution.py:42
  188.1 2.8 %spread.1 = (bf16[32,40,160]{2,1,0:T(8,128)(2,1)}, f32[40,1280]{1,0:T(8,128)}, f32[40,1280]{1,0:T(8,128)}, f32[40,1280]{1,0:T(8,128)}, f32[40,1280]{1,0:T(8,128)}) custom-call(s32[5]{0:T(128)} %stack.68.at_ref, bf16[3,40,1280]{2,1,0:T(8,128)(2,1)} %copy-done.7, bf16[3,40,1280]{2,1,0:T(8,128)(2,1)} %copy-done.8, bf16[3,40,1280]{2,1,0:T(8,128)(2,1)} %copy-done.9, ...), custom_call_target="tpu_custom_call" | custom-call | tf_op jit(solution)/shard_map/second_product/spread/pallas_call | solution.py:58
  191.0 5.3 %all-to-all-start.2 = ((bf16[32,40,160]{2,1,0:T(8,128)(2,1)}), bf16[32,40,160]{2,1,0:T(8,128)(2,1)S(1)}, u32[]{:S(2)}, u32[]{:S(2)}) async-start(bf16[32,40,160]{2,1,0:T(8,128)(2,1)} %get-tuple-element.78), calls=%async_computation.2 | async-start | bytes 1310720 | tf_op jit(solution)/shard_map/transposed/all_to_all | solution.py:285
  201.9 2.6 %collective-permute-done.34.d1 = f32[40,1280]{1,0:T(8,128)S(1)} collective-permute-done((f32[40,1280]{1,0:T(8,128)}, f32[40,1280]{1,0:T(8,128)S(1)}, u32[]{:S(2)}, u32[]{:S(2)}) %collective-permute-start.34) | collective-permute-done | bytes 204832 | tf_op jit(solution)/shard_map/direct/ppermute | solution.py:28
  204.6 5.0 %collective-permute-done.35.d2 = f32[40,1280]{1,0:T(8,128)S(1)} collective-permute-done((f32[40,1280]{1,0:T(8,128)}, f32[40,1280]{1,0:T(8,128)S(1)}, u32[]{:S(2)}, u32[]{:S(2)}) %collective-permute-start.35) | collective-permute-done | bytes 204832 | tf_op jit(solution)/shard_map/direct/ppermute | solution.py:28
  209.6 2.7 %collective-permute-done.36.d3 = f32[40,1280]{1,0:T(8,128)S(1)} collective-permute-done((f32[40,1280]{1,0:T(8,128)}, f32[40,1280]{1,0:T(8,128)S(1)}, u32[]{:S(2)}, u32[]{:S(2)}) %collective-permute-start.36) | collective-permute-done | bytes 204832 | tf_op jit(solution)/shard_map/direct/ppermute | solution.py:28
  213.2 3.9 %finish.1 = f32[40,5120]{1,0:T(8,128)} custom-call(s32[5]{0:T(128)} %stack.68.at_ref, f32[40,1280]{1,0:T(8,128)} %get-tuple-element.74.d0, f32[40,1280]{1,0:T(8,128)} %copy-done.11, f32[40,1280]{1,0:T(8,128)} %copy-done.12, f32[40,1280]{1,0:T(8,128)} %copy-done.13, bf16[32,40,160]{2,1,0:T(8,128)(2,1)} %copy-done, f32[40,40]{1,0:T(8,128)} %fusion.22.kept_ref), custom_call_target="tpu_custom_call" | custom-call | tf_op jit(solution)/shard_map/finish/pallas_call | solution.py:58
  (123 shorter events, 50.9 us)
Async XLA Ops:
  2.0 8.4 %collective-permute-start = (bf16[160,1280]{1,0:T(8,128)(2,1)S(1)}, bf16[160,1280]{1,0:T(8,128)(2,1)S(1)}, u32[]{:S(2)}, u32[]{:S(2)}) collective-permute-start(bf16[160,1280]{1,0:T(8,128)(2,1)S(1)} %get-tuple-element.110), channel_id=1, source_target_pairs={{0,2},{1,3},{2,0},{3,1},{4,6},{5,7},{6,4},{7,5},{8,10},{9,11},{10,... | collective-permute-start | bytes 1228808 | tf_op jit(solution)/shard_map/left_columns/ppermute | solution.py:28
  5.4 26.1 %all-to-all-start = ((bf16[8,160,320]{2,1,0:T(8,128)(2,1)}), bf16[8,160,320]{2,1,0:T(8,128)(2,1)S(1)}, u32[]{:S(2)}, u32[]{:S(2)}) async-start(bf16[8,160,320]{2,1,0:T(8,128)(2,1)} %right_columns.1), calls=%async_computation | async-start | bytes 1966080 | tf_op jit(solution)/shard_map/right_columns/all_to_all | solution.py:173
  15.2 12.7 %collective-permute-start.2 = (bf16[160,640]{1,0:T(8,128)(2,1)}, bf16[160,640]{1,0:T(8,128)(2,1)S(1)}, u32[]{:S(2)}, u32[]{:S(2)}) collective-permute-start(bf16[160,640]{1,0:T(8,128)(2,1)} %get-tuple-element.46), channel_id=1, source_target_pairs={{0,16},{1,17},{2,18},{3,19},{4,20},{5,21},{6,22},{7,23},{8,24},{9,... | collective-permute-start | bytes 614408 | tf_op jit(solution)/shard_map/left_columns/ppermute | solution.py:28
  18.1 12.4 %collective-permute-start.3 = (bf16[160,640]{1,0:T(8,128)(2,1)}, bf16[160,640]{1,0:T(8,128)(2,1)S(1)}, u32[]{:S(2)}, u32[]{:S(2)}) collective-permute-start(bf16[160,640]{1,0:T(8,128)(2,1)} %get-tuple-element.47), channel_id=1, source_target_pairs={{0,24},{1,25},{2,26},{3,27},{4,28},{5,29},{6,30},{7,31},{8,16},{9,... | collective-permute-start | bytes 614408 | tf_op jit(solution)/shard_map/left_columns/ppermute | solution.py:28
  19.0 13.8 %collective-permute-start.4 = (bf16[80,1280]{1,0:T(8,128)(2,1)S(1)}, bf16[80,1280]{1,0:T(8,128)(2,1)S(1)}, u32[]{:S(2)}, u32[]{:S(2)}) collective-permute-start(bf16[80,1280]{1,0:T(8,128)(2,1)S(1)} %bitcast.86), channel_id=1, source_target_pairs={{0,1},{1,0},{2,3},{3,2},{4,5},{5,4},{6,7},{7,6},{8,9},{9,8},{10,11... | collective-permute-start | bytes 614408 | tf_op jit(solution)/shard_map/density_turn/ppermute | solution.py:28
  32.8 21.3 %collective-permute-start.5 = (bf16[640,640]{1,0:T(8,128)(2,1)S(1)}, bf16[640,640]{1,0:T(8,128)(2,1)S(1)}, u32[]{:S(2)}, u32[]{:S(2)}) collective-permute-start(bf16[640,640]{1,0:T(8,128)(2,1)S(1)} %pad_maximum_fusion.4), channel_id=1, source_target_pairs={{0,4},{1,5},{2,6},{3,7},{4,0},{5,1},{6,2},{7,3},{8,12},{9,13},{10,... | collective-permute-start | bytes 2457608 | tf_op jit(solution)/shard_map/left_gather/ppermute | solution.py:28
  33.2 37.4 %collective-permute-start.6 = (bf16[640,640]{1,0:T(8,128)(2,1)S(1)}, bf16[640,640]{1,0:T(8,128)(2,1)}, u32[]{:S(2)}, u32[]{:S(2)}) collective-permute-start(bf16[640,640]{1,0:T(8,128)(2,1)S(1)} %pad_maximum_fusion.4), channel_id=1, source_target_pairs={{0,1},{1,0},{2,3},{3,2},{4,5},{5,4},{6,7},{7,6},{8,9},{9,8},{10,11... | collective-permute-start | bytes 2457608 | tf_op jit(solution)/shard_map/left_gather/ppermute | solution.py:28
  35.8 36.2 %collective-permute-start.7 = (bf16[640,640]{1,0:T(8,128)(2,1)S(1)}, bf16[640,640]{1,0:T(8,128)(2,1)}, u32[]{:S(2)}, u32[]{:S(2)}) collective-permute-start(bf16[640,640]{1,0:T(8,128)(2,1)S(1)} %pad_maximum_fusion.4), channel_id=1, source_target_pairs={{0,5},{1,4},{2,7},{3,6},{4,1},{5,0},{6,3},{7,2},{8,13},{9,12},{10,... | collective-permute-start | bytes 2457608 | tf_op jit(solution)/shard_map/left_gather/ppermute | solution.py:28
  36.4 37.1 %collective-permute-start.10 = (bf16[320,1280]{1,0:T(8,128)(2,1)S(1)}, bf16[320,1280]{1,0:T(8,128)(2,1)}, u32[]{:S(2)}, u32[]{:S(2)}) collective-permute-start(bf16[320,1280]{1,0:T(8,128)(2,1)S(1)} %reshape.136), channel_id=1, source_target_pairs={{0,96},{1,97},{2,98},{3,99},{4,100},{5,101},{6,102},{7,103},{8,104... | collective-permute-start | bytes 2457608 | tf_op jit(solution)/shard_map/right_gather/ppermute | solution.py:28
  40.4 33.1 %collective-permute-start.8 = (bf16[320,1280]{1,0:T(8,128)(2,1)S(1)}, bf16[320,1280]{1,0:T(8,128)(2,1)}, u32[]{:S(2)}, u32[]{:S(2)}) collective-permute-start(bf16[320,1280]{1,0:T(8,128)(2,1)S(1)} %reshape.136), channel_id=1, source_target_pairs={{0,32},{1,33},{2,34},{3,35},{4,36},{5,37},{6,38},{7,39},{8,40},{9,... | collective-permute-start | bytes 2457608 | tf_op jit(solution)/shard_map/right_gather/ppermute | solution.py:28
  54.1 21.7 %collective-permute-start.9 = (bf16[320,1280]{1,0:T(8,128)(2,1)S(1)}, bf16[320,1280]{1,0:T(8,128)(2,1)}, u32[]{:S(2)}, u32[]{:S(2)}) collective-permute-start(bf16[320,1280]{1,0:T(8,128)(2,1)S(1)} %reshape.136), channel_id=1, source_target_pairs={{0,64},{1,65},{2,66},{3,67},{4,68},{5,69},{6,70},{7,71},{8,72},{9,... | collective-permute-start | bytes 2457608 | tf_op jit(solution)/shard_map/right_gather/ppermute | solution.py:28
  59.9 15.8 %all-to-all-start.1 = ((bf16[4,80,640]{2,1,0:T(8,128)(2,1)}), bf16[4,80,640]{2,1,0:T(8,128)(2,1)S(1)}, u32[]{:S(2)}, u32[]{:S(2)}) async-start(bf16[4,80,640]{2,1,0:T(8,128)(2,1)} %density_columns.1), calls=%async_computation.1 | async-start | bytes 819200 | tf_op jit(solution)/shard_map/density_columns/all_to_all | solution.py:203
  87.7 11.6 %collective-permute-start.17 = (f32[80,1280]{1,0:T(8,128)S(1)}, f32[80,1280]{1,0:T(8,128)S(1)}, u32[]{:S(2)}, u32[]{:S(2)}) collective-permute-start(f32[80,1280]{1,0:T(8,128)S(1)} %get-tuple-element.105), channel_id=1, source_target_pairs={{0,8},{1,9},{2,10},{3,11},{4,12},{5,13},{6,14},{7,15},{8,0},{9,1},... | collective-permute-start | bytes 1228808 | tf_op jit(solution)/shard_map/mixed_sum/ppermute | solution.py:28
  87.8 12.8 %collective-permute-start.14 = (f32[80,1280]{1,0:T(8,128)S(1)}, f32[80,1280]{1,0:T(8,128)S(1)}, u32[]{:S(2)}, u32[]{:S(2)}) collective-permute-start(f32[80,1280]{1,0:T(8,128)S(1)} %get-tuple-element.106), channel_id=1, source_target_pairs={{0,24},{1,25},{2,26},{3,27},{4,28},{5,29},{6,30},{7,31},{8,16},{9,... | collective-permute-start | bytes 1228808 | tf_op jit(solution)/shard_map/mixed_sum/ppermute | solution.py:28
  99.4 26.8 %collective-permute-start.18 = (f32[160,1280]{1,0:T(8,128)S(1)}, f32[160,1280]{1,0:T(8,128)S(1)}, u32[]{:S(2)}, u32[]{:S(2)}) collective-permute-start(f32[160,1280]{1,0:T(8,128)S(1)} %pad_maximum_fusion.6), channel_id=1, source_target_pairs={{0,24},{1,25},{2,26},{3,27},{4,28},{5,29},{6,30},{7,31},{8,16},{9,... | collective-permute-start | bytes 2457608 | tf_op jit(solution)/shard_map/mixed_sum/ppermute | solution.py:28
  101.6 24.6 %collective-permute-start.15 = (f32[160,1280]{1,0:T(8,128)}, f32[160,1280]{1,0:T(8,128)}, u32[]{:S(2)}, u32[]{:S(2)}) collective-permute-start(f32[160,1280]{1,0:T(8,128)} %pad_maximum_fusion.5), channel_id=1, source_target_pairs={{0,8},{1,9},{2,10},{3,11},{4,12},{5,13},{6,14},{7,15},{8,0},{9,1},... | collective-permute-start | bytes 2457608 | tf_op jit(solution)/shard_map/mixed_sum/ppermute | solution.py:28
  102.1 12.4 %collective-permute-start.19 = (bf16[320,640]{1,0:T(8,128)(2,1)S(1)}, bf16[320,640]{1,0:T(8,128)(2,1)S(1)}, u32[]{:S(2)}, u32[]{:S(2)}) collective-permute-start(bf16[320,640]{1,0:T(8,128)(2,1)S(1)} %bitcast.77), channel_id=1, source_target_pairs={{0,32},{1,33},{2,34},{3,35},{4,36},{5,37},{6,38},{7,39},{8,40},{9,... | collective-permute-start | bytes 1228808 | tf_op jit(solution)/shard_map/density_gather/ppermute | solution.py:28
  102.1 21.6 %collective-permute-start.20 = (bf16[320,640]{1,0:T(8,128)(2,1)S(1)}, bf16[320,640]{1,0:T(8,128)(2,1)}, u32[]{:S(2)}, u32[]{:S(2)}) collective-permute-start(bf16[320,640]{1,0:T(8,128)(2,1)S(1)} %bitcast.78), channel_id=1, source_target_pairs={{0,64},{1,65},{2,66},{3,67},{4,68},{5,69},{6,70},{7,71},{8,72},{9,... | collective-permute-start | bytes 1228808 | tf_op jit(solution)/shard_map/density_gather/ppermute | solution.py:28
  106.5 19.8 %collective-permute-start.21 = (bf16[320,640]{1,0:T(8,128)(2,1)S(1)}, bf16[320,640]{1,0:T(8,128)(2,1)}, u32[]{:S(2)}, u32[]{:S(2)}) collective-permute-start(bf16[320,640]{1,0:T(8,128)(2,1)S(1)} %bitcast.79), channel_id=1, source_target_pairs={{0,96},{1,97},{2,98},{3,99},{4,100},{5,101},{6,102},{7,103},{8,104... | collective-permute-start | bytes 1228808 | tf_op jit(solution)/shard_map/density_gather/ppermute | solution.py:28
  130.1 30.9 %collective-permute-start.22 = (bf16[160,1280]{1,0:T(8,128)(2,1)}, bf16[160,1280]{1,0:T(8,128)(2,1)S(1)}, u32[]{:S(2)}, u32[]{:S(2)}) collective-permute-start(bf16[160,1280]{1,0:T(8,128)(2,1)} %add_convert_fusion), channel_id=1, source_target_pairs={{0,8},{1,9},{2,10},{3,11},{4,12},{5,13},{6,14},{7,15},{8,0},{9,1},... | collective-permute-start | bytes 1228808 | tf_op jit(solution)/shard_map/mixed_gather/ppermute | solution.py:28
  131.9 29.1 %collective-permute-start.23 = (bf16[160,1280]{1,0:T(8,128)(2,1)}, bf16[160,1280]{1,0:T(8,128)(2,1)S(1)}, u32[]{:S(2)}, u32[]{:S(2)}) collective-permute-start(bf16[160,1280]{1,0:T(8,128)(2,1)} %add_convert_fusion), channel_id=1, source_target_pairs={{0,24},{1,25},{2,26},{3,27},{4,28},{5,29},{6,30},{7,31},{8,16},{9,... | collective-permute-start | bytes 1228808 | tf_op jit(solution)/shard_map/mixed_gather/ppermute | solution.py:28
  133.8 34.0 %collective-permute-start.26 = (bf16[160,1280]{1,0:T(8,128)(2,1)}, bf16[160,1280]{1,0:T(8,128)(2,1)S(1)}, u32[]{:S(2)}, u32[]{:S(2)}) collective-permute-start(bf16[160,1280]{1,0:T(8,128)(2,1)} %add_convert_fusion), channel_id=1, source_target_pairs={{0,16},{1,17},{2,18},{3,19},{4,20},{5,21},{6,22},{7,23},{8,24},{9,... | collective-permute-start | bytes 1228808 | tf_op jit(solution)/shard_map/mixed_gather/ppermute | solution.py:28
  163.6 12.1 %collective-permute-start.27 = (bf16[3,40,1280]{2,1,0:T(8,128)(2,1)S(1)}, bf16[3,40,1280]{2,1,0:T(8,128)(2,1)S(1)}, u32[]{:S(2)}, u32[]{:S(2)}) collective-permute-start(bf16[3,40,1280]{2,1,0:T(8,128)(2,1)S(1)} %get-tuple-element.101), channel_id=1, source_target_pairs={{0,2},{1,3},{2,4},{3,5},{4,6},{5,7},{6,0},{7,1},{8,10},{9,11},{10,... | collective-permute-start | bytes 921608 | tf_op jit(solution)/shard_map/second_product/ppermute | solution.py:42
  166.0 16.6 %collective-permute-start.28 = (bf16[3,40,1280]{2,1,0:T(8,128)(2,1)S(1)}, bf16[3,40,1280]{2,1,0:T(8,128)(2,1)S(1)}, u32[]{:S(2)}, u32[]{:S(2)}) collective-permute-start(bf16[3,40,1280]{2,1,0:T(8,128)(2,1)S(1)} %get-tuple-element.100), channel_id=1, source_target_pairs={{0,1},{1,0},{2,7},{3,6},{4,5},{5,4},{6,3},{7,2},{8,9},{9,8},{10,15... | collective-permute-start | bytes 921608 | tf_op jit(solution)/shard_map/second_product/ppermute | solution.py:42
  167.7 14.9 %collective-permute-start.29 = (bf16[3,40,1280]{2,1,0:T(8,128)(2,1)S(1)}, bf16[3,40,1280]{2,1,0:T(8,128)(2,1)S(1)}, u32[]{:S(2)}, u32[]{:S(2)}) collective-permute-start(bf16[3,40,1280]{2,1,0:T(8,128)(2,1)S(1)} %get-tuple-element.99), channel_id=1, source_target_pairs={{0,3},{1,2},{2,5},{3,4},{4,7},{5,6},{6,1},{7,0},{8,11},{9,10},{10,... | collective-permute-start | bytes 921608 | tf_op jit(solution)/shard_map/second_product/ppermute | solution.py:42
  168.6 14.0 %collective-permute-start.30 = (bf16[1,40,1280]{2,1,0:T(8,128)(2,1)S(1)}, bf16[1,40,1280]{2,1,0:T(8,128)(2,1)S(1)}, u32[]{:S(2)}, u32[]{:S(2)}) collective-permute-start(bf16[1,40,1280]{2,1,0:T(8,128)(2,1)S(1)} %get-tuple-element.114), channel_id=1, source_target_pairs={{0,0},{1,1},{2,6},{3,7},{4,4},{5,5},{6,2},{7,3},{8,8},{9,9},{10,14... | collective-permute-start | bytes 307208 | tf_op jit(solution)/shard_map/second_product/ppermute | solution.py:42
  169.3 13.4 %collective-permute-start.31 = (bf16[1,40,1280]{2,1,0:T(8,128)(2,1)S(1)}, bf16[1,40,1280]{2,1,0:T(8,128)(2,1)S(1)}, u32[]{:S(2)}, u32[]{:S(2)}) collective-permute-start(bf16[1,40,1280]{2,1,0:T(8,128)(2,1)S(1)} %get-tuple-element.113), channel_id=1, source_target_pairs={{0,2},{1,3},{2,4},{3,5},{4,6},{5,7},{6,0},{7,1},{8,10},{9,11},{10,... | collective-permute-start | bytes 307208 | tf_op jit(solution)/shard_map/second_product/ppermute | solution.py:42
  175.7 9.5 %collective-permute-start.32 = (bf16[1,40,1280]{2,1,0:T(8,128)(2,1)S(1)}, bf16[1,40,1280]{2,1,0:T(8,128)(2,1)S(1)}, u32[]{:S(2)}, u32[]{:S(2)}) collective-permute-start(bf16[1,40,1280]{2,1,0:T(8,128)(2,1)S(1)} %get-tuple-element.112), channel_id=1, source_target_pairs={{0,1},{1,0},{2,7},{3,6},{4,5},{5,4},{6,3},{7,2},{8,9},{9,8},{10,15... | collective-permute-start | bytes 307208 | tf_op jit(solution)/shard_map/second_product/ppermute | solution.py:42
  191.0 21.3 %all-to-all-start.2 = ((bf16[32,40,160]{2,1,0:T(8,128)(2,1)}), bf16[32,40,160]{2,1,0:T(8,128)(2,1)S(1)}, u32[]{:S(2)}, u32[]{:S(2)}) async-start(bf16[32,40,160]{2,1,0:T(8,128)(2,1)} %get-tuple-element.78), calls=%async_computation.2 | async-start | bytes 1310720 | tf_op jit(solution)/shard_map/transposed/all_to_all | solution.py:285
  196.4 8.2 %collective-permute-start.34 = (f32[40,1280]{1,0:T(8,128)}, f32[40,1280]{1,0:T(8,128)S(1)}, u32[]{:S(2)}, u32[]{:S(2)}) collective-permute-start(f32[40,1280]{1,0:T(8,128)} %get-tuple-element.75), channel_id=1, source_target_pairs={{0,8},{1,9},{2,10},{3,11},{4,12},{5,13},{6,14},{7,15},{8,0},{9,1},... | collective-permute-start | bytes 614408 | tf_op jit(solution)/shard_map/direct/ppermute | solution.py:28
  198.2 11.4 %collective-permute-start.35 = (f32[40,1280]{1,0:T(8,128)}, f32[40,1280]{1,0:T(8,128)S(1)}, u32[]{:S(2)}, u32[]{:S(2)}) collective-permute-start(f32[40,1280]{1,0:T(8,128)} %get-tuple-element.76), channel_id=1, source_target_pairs={{0,16},{1,17},{2,18},{3,19},{4,20},{5,21},{6,22},{7,23},{8,24},{9,... | collective-permute-start | bytes 614408 | tf_op jit(solution)/shard_map/direct/ppermute | solution.py:28
  199.8 12.5 %collective-permute-start.36 = (f32[40,1280]{1,0:T(8,128)}, f32[40,1280]{1,0:T(8,128)S(1)}, u32[]{:S(2)}, u32[]{:S(2)}) collective-permute-start(f32[40,1280]{1,0:T(8,128)} %get-tuple-element.77), channel_id=1, source_target_pairs={{0,24},{1,25},{2,26},{3,27},{4,28},{5,29},{6,30},{7,31},{8,16},{9,... | collective-permute-start | bytes 614408 | tf_op jit(solution)/shard_map/direct/ppermute | solution.py:28
  (28 other events, 220.9 us)

commit v6 on v5

--- a/solution.py
+++ b/solution.py
@@ -69,10 +69,10 @@
     return jax.ShapeDtypeStruct(dims, dtype)
 
 
-def left_kernel(at_ref, keep_ref, came_ref, *outs):
+def left_kernel(at_ref, first_ref, second_ref, came_ref, *outs):
     y, core = at_ref[1], at_ref[3]
-    low = jnp.where(core == 0, keep_ref[...], came_ref[...])
-    high = jnp.where(core == 0, came_ref[...], keep_ref[...])
+    low = jnp.where(core == 0, first_ref[...], came_ref[...])
+    high = jnp.where(core == 0, came_ref[...], second_ref[...])
     for ny in range(4):
         cut = slice(ny * 320, ny * 320 + 320)
         piece = jnp.concatenate((low[:, cut], high[:, cut]), axis=1)
@@ -108,6 +108,19 @@
     for ny in range(4):
         cut = slice(ny * 320, ny * 320 + 320)
         out_ref[ny] = jnp.concatenate((first[:, cut], second[:, cut]), axis=1)
+
+
+def rows_kernel(at_ref, *refs):
+    out_ref = refs[4]
+    z = at_ref[0]
+    for q in range(4):
+        out_ref[pl.ds(pl.multiple_of((z ^ q) * 320, 320), 320), :] = refs[q][...]
+
+
+def join_kernel(at_ref, mine_ref, other_ref, out_ref):
+    core = at_ref[3]
+    out_ref[:, :640] = jnp.where(core == 0, mine_ref[...], other_ref[...])
+    out_ref[:, 640:] = jnp.where(core == 0, other_ref[...], mine_ref[...])
 
 
 def spread_kernel(at_ref, *refs):
@@ -162,16 +175,12 @@
     coords = jnp.stack((z, y, xl, core, xh)).astype(jnp.int32)
 
     with jax.named_scope("left_columns"):
-        keep = jnp.where(core == 0, dens_resp, density)
         send = jnp.where(core == 0, density, dens_resp)
         came = flip(send, core=1)
     with jax.named_scope("right_columns"):
         first, second, _ = lax.optimization_barrier((fock, fock_resp, send))
         parts = local_call(
             right_kernel, "right_columns", shape(bf16, 8, 160, 320), coords, first, second
-        )
-        rounds = lax.all_to_all(
-            parts, ("xl", "core", "xh"), split_axis=0, concat_axis=0, tiled=True
         )
     with jax.named_scope("density_turn"):
         halves, _ = lax.optimization_barrier((density.reshape(2, 2, 40, 1280), send))
@@ -180,12 +189,17 @@
         other = flip(other, xh=1)
     with jax.named_scope("left_columns"):
         pieces = local_call(
-            left_kernel, "left_columns", [shape(bf16, 160, 640)] * 4, coords, keep, came
-        )
+            left_kernel, "left_columns", [shape(bf16, 160, 640)] * 4, coords, dens_resp, density, came
+        )
+        parts, pieces = lax.optimization_barrier((parts, pieces))
         left = jnp.concatenate([pieces[0]] + [flip(pieces[q], y=q) for q in (1, 2, 3)])
+        left, other = lax.optimization_barrier((left, other))
     with jax.named_scope("right_gather"):
+        rounds = lax.all_to_all(
+            parts, ("xl", "core", "xh"), split_axis=0, concat_axis=0, tiled=True
+        )
         right = rounds.reshape(2, 4, 160, 320).transpose(0, 2, 1, 3).reshape(320, 1280)
-        right, left, other = lax.optimization_barrier((right, left, other))
+        right, left = lax.optimization_barrier((right, left))
         rights = [right] + [flip(right, z=q) for q in (1, 2, 3)]
     with jax.named_scope("left_gather"):
         lefts = {
@@ -237,15 +251,10 @@
         mixed = total.astype(bf16)
 
     with jax.named_scope("density_rows"):
-        mixed, dparts = lax.optimization_barrier((mixed, dparts))
-        dmine = jnp.concatenate([pick(jnp.stack(dparts), z ^ nz) for nz in range(4)])
-        dother = flip(dmine, core=1)
-        dfull = jnp.where(
-            core == 0,
-            jnp.concatenate((dmine, dother), axis=1),
-            jnp.concatenate((dother, dmine), axis=1),
-        )
-
+        dmine = local_call(rows_kernel, "density_rows", shape(bf16, 1280, 640), coords, *dparts)
+        dfull = local_call(
+            join_kernel, "density_join", shape(bf16, 1280, 1280), coords, dmine, flip(dmine, core=1)
+        )
     with jax.named_scope("mixed_gather"):
         mslots = [mixed] + [flip(mixed, y=q) for q in (1, 2, 3)]
 

time: 218 us -> 215 us (0.986)
  other arithmetic: 40.7 us -> 11.3 us
  waiting for transfers between devices: 80.5 us -> 89.1 us
  Pallas kernels: 14 us -> 20.8 us
  starting transfers between devices: 66.9 us -> 72.7 us
  local copies, waits for them, and re-layouts: 6.7 us -> 10.6 us
    select_n x2 -> x1, other arithmetic: 28.7 us -> 1.12 us  [shards(): send = jnp.where(core == 0, density, dens_resp)]
    ppermute x29, waiting for transfers between devices: 75.5 us -> 83.8 us  [flip(): return lax.ppermute(value, AXES, pairs)]
    pallas_call x5 -> x7, Pallas kernels: 14 us -> 20.8 us  [local_call(): pl.pallas_call(kernel, out_shape=outs, in_specs=[SMEM] + [VMEM] * len(ope...]
    ppermute x29, starting transfers between devices: 34.5 us -> 40.2 us  [flip(): return lax.ppermute(value, AXES, pairs)]
    unnamed x40 -> x56, local copies, waits for them, and re-layouts: 3.26 us -> 7.26 us
  transfers between devices with their start and end apart: 40 -> 40, of which waited for: 21 -> 24; matrix products, arithmetic and copies ran while one was open for 19% -> 8% of each run, Pallas kernels for 3% -> 4%
where the time goes in v6:
time: 215 us
  waiting for transfers between devices  89.1 us (41%)
  starting transfers between devices  72.7 us (34%)
  Pallas kernels  20.8 us (10%)
  other arithmetic  11.3 us (5%)
  local copies, waits for them, and re-layouts  10.6 us (5%)
  matrix products  9.76 us (5%)
    ppermute x29, waiting for transfers between devices, flip(): return lax.ppermute(value, AXES, pairs)  83.8 us
    ppermute x29, starting transfers between devices, flip(): return lax.ppermute(value, AXES, pairs)  40.2 us
    pallas_call x7, Pallas kernels, local_call(): pl.pallas_call(kernel, out_shape=outs, in_specs=[SMEM] + [VMEM] * len(ope...  20.8 us
    ppermute x8, starting transfers between devices, remap(): return lax.ppermute(value, AXES, pairs)  18 us
    dot_general x4, matrix products, dot(): return jnp.dot(a, b, preferred_element_type=f32)  8.97 us
    unnamed x56, local copies, waits for them, and re-layouts  7.26 us
    ppermute x8, waiting for transfers between devices, remap(): return lax.ppermute(value, AXES, pairs)  5.27 us
    select_n x2, other arithmetic, shards(): mine = [jnp.where(core == 0, lefts[0, r], lefts[1, r]) for r in range(2)]  5.24 us
  transfers between devices with their start and end apart: 40, of which 24 were waited for; matrix products, arithmetic and copies ran while one was open for 8% of the time, Pallas kernels for 4%

profile of v6, /device:TPU:2, one launch (start us, length us, event | category | flops | bytes accessed | tf_op | source)
XLA Modules:
  0.0 214.7 jit_solution(3792214688721433584)
XLA Ops:
  1.9 2.8 %right_columns.1 = bf16[8,160,320]{2,1,0:T(8,128)(2,1)} custom-call(s32[5]{0:T(128)} %stack.38.at_ref, bf16[160,1280]{1,0:T(8,128)(2,1)} %first_ref.1, bf16[160,1280]{1,0:T(8,128)(2,1)} %second_ref.1), custom_call_target="tpu_custom_call" | custom-call | tf_op jit(solution)/shard_map/right_columns/right_columns/pallas_call | solution.py:58
  5.4 2.7 %left_columns.1 = (bf16[160,640]{1,0:T(8,128)(2,1)}, bf16[160,640]{1,0:T(8,128)(2,1)}, bf16[160,640]{1,0:T(8,128)(2,1)}, bf16[160,640]{1,0:T(8,128)(2,1)}) custom-call(s32[5]{0:T(128)} %stack.38.at_ref, bf16[160,1280]{1,0:T(8,128)(2,1)} %first_ref.2, bf16[160,1280]{1,0:T(8,128)(2,1)} %second_ref.2, bf16[160,1280]{1,0:T(8,128)(2,1)} %copy-done.11), custom_call_target="tpu_custom_call" | custom-call | tf_op jit(solution)/shard_map/left_columns/left_columns/pallas_call | solution.py:58
  8.1 4.9 %all-to-all-start = ((bf16[8,160,320]{2,1,0:T(8,128)(2,1)}), bf16[8,160,320]{2,1,0:T(8,128)(2,1)S(1)}, u32[]{:S(2)}, u32[]{:S(2)}) async-start(bf16[8,160,320]{2,1,0:T(8,128)(2,1)} %right_columns.1), calls=%async_computation | async-start | bytes 1966080 | tf_op jit(solution)/shard_map/right_gather/all_to_all | solution.py:198
  14.6 2.9 %collective-permute-start.2 = (bf16[160,640]{1,0:T(8,128)(2,1)}, bf16[160,640]{1,0:T(8,128)(2,1)S(1)}, u32[]{:S(2)}, u32[]{:S(2)}) collective-permute-start(bf16[160,640]{1,0:T(8,128)(2,1)} %get-tuple-element.52), channel_id=1, source_target_pairs={{0,16},{1,17},{2,18},{3,19},{4,20},{5,21},{6,22},{7,23},{8,24},{9,... | collective-permute-start | bytes 614408 | tf_op jit(solution)/shard_map/left_columns/ppermute | solution.py:28
  21.1 6.1 %collective-permute-done.2 = bf16[160,640]{1,0:T(8,128)(2,1)S(1)} collective-permute-done((bf16[160,640]{1,0:T(8,128)(2,1)}, bf16[160,640]{1,0:T(8,128)(2,1)S(1)}, u32[]{:S(2)}, u32[]{:S(2)}) %collective-permute-start.2) | collective-permute-done | bytes 204832 | tf_op jit(solution)/shard_map/left_columns/ppermute | solution.py:28
  27.3 2.6 %collective-permute-done.3 = bf16[160,640]{1,0:T(8,128)(2,1)S(1)} collective-permute-done((bf16[160,640]{1,0:T(8,128)(2,1)}, bf16[160,640]{1,0:T(8,128)(2,1)S(1)}, u32[]{:S(2)}, u32[]{:S(2)}) %collective-permute-start.3) | collective-permute-done | bytes 204832 | tf_op jit(solution)/shard_map/left_columns/ppermute | solution.py:28
  36.1 4.0 %collective-permute-start.10 = (bf16[320,1280]{1,0:T(8,128)(2,1)S(1)}, bf16[320,1280]{1,0:T(8,128)(2,1)S(1)}, u32[]{:S(2)}, u32[]{:S(2)}) collective-permute-start(bf16[320,1280]{1,0:T(8,128)(2,1)S(1)} %reshape.136), channel_id=1, source_target_pairs={{0,96},{1,97},{2,98},{3,99},{4,100},{5,101},{6,102},{7,103},{8,104... | collective-permute-start | bytes 2457608 | tf_op jit(solution)/shard_map/right_gather/ppermute | solution.py:28
  40.2 13.7 %collective-permute-done.5 = bf16[640,640]{1,0:T(8,128)(2,1)} collective-permute-done((bf16[640,640]{1,0:T(8,128)(2,1)S(1)}, bf16[640,640]{1,0:T(8,128)(2,1)}, u32[]{:S(2)}, u32[]{:S(2)}) %collective-permute-start.5) | collective-permute-done | bytes 819232 | tf_op jit(solution)/shard_map/left_gather/ppermute | solution.py:28
  53.9 3.9 %collective-permute-start.9 = (bf16[320,1280]{1,0:T(8,128)(2,1)S(1)}, bf16[320,1280]{1,0:T(8,128)(2,1)}, u32[]{:S(2)}, u32[]{:S(2)}) collective-permute-start(bf16[320,1280]{1,0:T(8,128)(2,1)S(1)} %reshape.136), channel_id=1, source_target_pairs={{0,64},{1,65},{2,66},{3,67},{4,68},{5,69},{6,70},{7,71},{8,72},{9,... | collective-permute-start | bytes 2457608 | tf_op jit(solution)/shard_map/right_gather/ppermute | solution.py:28
  59.7 4.5 %all-to-all-start.1 = ((bf16[4,80,640]{2,1,0:T(8,128)(2,1)}), bf16[4,80,640]{2,1,0:T(8,128)(2,1)S(1)}, u32[]{:S(2)}, u32[]{:S(2)}) async-start(bf16[4,80,640]{2,1,0:T(8,128)(2,1)} %density_columns.1), calls=%async_computation.1 | async-start | bytes 819200 | tf_op jit(solution)/shard_map/density_columns/all_to_all | solution.py:217
  66.7 3.3 %collective-permute-done.6 = bf16[640,640]{1,0:T(8,128)(2,1)} collective-permute-done((bf16[640,640]{1,0:T(8,128)(2,1)S(1)}, bf16[640,640]{1,0:T(8,128)(2,1)}, u32[]{:S(2)}, u32[]{:S(2)}) %collective-permute-start.6) | collective-permute-done | bytes 819232 | tf_op jit(solution)/shard_map/left_gather/ppermute | solution.py:28
  71.4 2.7 %broadcast_select_fusion.2 = (bf16[640,640]{1,0:T(8,128)(2,1)}, bf16[640,640]{1,0:T(8,128)(2,1)}) fusion(bf16[640,640]{1,0:T(8,128)(2,1)} %collective-permute-done.6, bf16[640,640]{1,0:T(8,128)(2,1)} %collective-permute-done.7, pred[]{:T(512)S(6)} %eq.8), kind=kLoop, calls=%fused_computation.31 | loop fusion | flops 819200 | bytes 3276801 | tf_op jit(solution)/shard_map/first_product/jit(_where)/select_n | solution.py:231
  92.2 7.8 %collective-permute-done.17 = f32[80,1280]{1,0:T(8,128)S(1)} collective-permute-done((f32[80,1280]{1,0:T(8,128)S(1)}, f32[80,1280]{1,0:T(8,128)S(1)}, u32[]{:S(2)}, u32[]{:S(2)}) %collective-permute-start.17) | collective-permute-done | bytes 409632 | tf_op jit(solution)/shard_map/mixed_sum/ppermute | solution.py:28
  100.1 3.1 %collective-permute-start.18 = (f32[160,1280]{1,0:T(8,128)S(1)}, f32[160,1280]{1,0:T(8,128)S(1)}, u32[]{:S(2)}, u32[]{:S(2)}) collective-permute-start(f32[160,1280]{1,0:T(8,128)S(1)} %pad_maximum_fusion.4), channel_id=1, source_target_pairs={{0,24},{1,25},{2,26},{3,27},{4,28},{5,29},{6,30},{7,31},{8,16},{9,... | collective-permute-start | bytes 2457608 | tf_op jit(solution)/shard_map/mixed_sum/ppermute | solution.py:28
  103.6 4.4 %collective-permute-start.20 = (bf16[320,640]{1,0:T(8,128)(2,1)S(1)}, bf16[320,640]{1,0:T(8,128)(2,1)S(1)}, u32[]{:S(2)}, u32[]{:S(2)}) collective-permute-start(bf16[320,640]{1,0:T(8,128)(2,1)S(1)} %bitcast.67), channel_id=1, source_target_pairs={{0,64},{1,65},{2,66},{3,67},{4,68},{5,69},{6,70},{7,71},{8,72},{9,... | collective-permute-start | bytes 1228808 | tf_op jit(solution)/shard_map/density_gather/ppermute | solution.py:28
  108.3 7.7 %collective-permute-done.19.refs_1_ = bf16[320,640]{1,0:T(8,128)(2,1)S(1)} collective-permute-done((bf16[320,640]{1,0:T(8,128)(2,1)S(1)}, bf16[320,640]{1,0:T(8,128)(2,1)S(1)}, u32[]{:S(2)}, u32[]{:S(2)}) %collective-permute-start.19) | collective-permute-done | bytes 409632 | tf_op jit(solution)/shard_map/density_gather/ppermute | solution.py:28
  116.0 9.2 %collective-permute-done.20.refs_2_ = bf16[320,640]{1,0:T(8,128)(2,1)S(1)} collective-permute-done((bf16[320,640]{1,0:T(8,128)(2,1)S(1)}, bf16[320,640]{1,0:T(8,128)(2,1)S(1)}, u32[]{:S(2)}, u32[]{:S(2)}) %collective-permute-start.20) | collective-permute-done | bytes 409632 | tf_op jit(solution)/shard_map/density_gather/ppermute | solution.py:28
  125.2 2.6 %collective-permute-done.21.refs_3_ = bf16[320,640]{1,0:T(8,128)(2,1)S(1)} collective-permute-done((bf16[320,640]{1,0:T(8,128)(2,1)S(1)}, bf16[320,640]{1,0:T(8,128)(2,1)S(1)}, u32[]{:S(2)}, u32[]{:S(2)}) %collective-permute-start.21) | collective-permute-done | bytes 409632 | tf_op jit(solution)/shard_map/density_gather/ppermute | solution.py:28
  130.3 2.7 %density_rows.1.mine_ref = bf16[1280,640]{1,0:T(8,128)(2,1)} custom-call(s32[5]{0:T(128)} %stack.38.at_ref, bf16[320,640]{1,0:T(8,128)(2,1)} %bitcast.69, bf16[320,640]{1,0:T(8,128)(2,1)} %copy-done.12, bf16[320,640]{1,0:T(8,128)(2,1)} %copy-done.13, bf16[320,640]{1,0:T(8,128)(2,1)} %copy-done.14), custom_call_target="tpu_custom_call" | custom-call | tf_op jit(solution)/shard_map/density_rows/density_rows/pallas_call | solution.py:58
  139.9 4.0 %density_join.1 = bf16[1280,1280]{1,0:T(8,128)(2,1)} custom-call(s32[5]{0:T(128)} %stack.38.at_ref, bf16[1280,640]{1,0:T(8,128)(2,1)} %density_rows.1.mine_ref, bf16[1280,640]{1,0:T(8,128)(2,1)} %copy-done.4), custom_call_target="tpu_custom_call" | custom-call | tf_op jit(solution)/shard_map/density_rows/density_join/pallas_call | solution.py:58
  143.9 3.0 %collective-permute-done.22 = bf16[160,1280]{1,0:T(8,128)(2,1)S(1)} collective-permute-done((bf16[160,1280]{1,0:T(8,128)(2,1)S(1)}, bf16[160,1280]{1,0:T(8,128)(2,1)S(1)}, u32[]{:S(2)}, u32[]{:S(2)}) %collective-permute-start.22) | collective-permute-done | bytes 409632 | tf_op jit(solution)/shard_map/mixed_gather/ppermute | solution.py:28
  146.9 11.0 %collective-permute-done.23 = bf16[160,1280]{1,0:T(8,128)(2,1)S(1)} collective-permute-done((bf16[160,1280]{1,0:T(8,128)(2,1)S(1)}, bf16[160,1280]{1,0:T(8,128)(2,1)S(1)}, u32[]{:S(2)}, u32[]{:S(2)}) %collective-permute-start.23) | collective-permute-done | bytes 409632 | tf_op jit(solution)/shard_map/mixed_gather/ppermute | solution.py:28
  157.9 3.7 %fusion.8 = bf16[480,1280]{1,0:T(8,128)(2,1)S(1)} fusion(bf16[1280,1280]{1,0:T(8,128)(2,1)} %density_join.1, bf16[160,1280]{1,0:T(8,128)(2,1)S(1)} %collective-permute-done.23, bf16[160,1280]{1,0:T(8,128)(2,1)S(1)} %collective-permute-done.22, bf16[160,1280]{1,0:T(8,128)(2,1)S(1)} %add_convert_fusion), kind=kOutput, calls=%fused_computation.10 | convolution fusion | flops 1576550400 | bytes 5734400 | tf_op jit(solution)/shard_map/second_product/dot_general | solution.py:50
  162.4 3.1 %collective-permute-start.27 = (bf16[3,40,1280]{2,1,0:T(8,128)(2,1)S(1)}, bf16[3,40,1280]{2,1,0:T(8,128)(2,1)S(1)}, u32[]{:S(2)}, u32[]{:S(2)}) collective-permute-start(bf16[3,40,1280]{2,1,0:T(8,128)(2,1)S(1)} %get-tuple-element.99), channel_id=1, source_target_pairs={{0,2},{1,3},{2,4},{3,5},{4,6},{5,7},{6,0},{7,1},{8,10},{9,11},{10,... | collective-permute-start | bytes 921608 | tf_op jit(solution)/shard_map/second_product/ppermute | solution.py:42
  168.7 6.9 %collective-permute-start.31 = (bf16[1,40,1280]{2,1,0:T(8,128)(2,1)S(1)}, bf16[1,40,1280]{2,1,0:T(8,128)(2,1)S(1)}, u32[]{:S(2)}, u32[]{:S(2)}) collective-permute-start(bf16[1,40,1280]{2,1,0:T(8,128)(2,1)S(1)} %get-tuple-element.109), channel_id=1, source_target_pairs={{0,2},{1,3},{2,4},{3,5},{4,6},{5,7},{6,0},{7,1},{8,10},{9,11},{10,... | collective-permute-start | bytes 307208 | tf_op jit(solution)/shard_map/second_product/ppermute | solution.py:42
  175.8 4.9 %collective-permute-start.32 = (bf16[1,40,1280]{2,1,0:T(8,128)(2,1)S(1)}, bf16[1,40,1280]{2,1,0:T(8,128)(2,1)S(1)}, u32[]{:S(2)}, u32[]{:S(2)}) collective-permute-start(bf16[1,40,1280]{2,1,0:T(8,128)(2,1)S(1)} %get-tuple-element.108), channel_id=1, source_target_pairs={{0,1},{1,0},{2,7},{3,6},{4,5},{5,4},{6,3},{7,2},{8,9},{9,8},{10,15... | collective-permute-start | bytes 307208 | tf_op jit(solution)/shard_map/second_product/ppermute | solution.py:42
  186.5 2.8 %spread.1 = (bf16[32,40,160]{2,1,0:T(8,128)(2,1)}, f32[40,1280]{1,0:T(8,128)}, f32[40,1280]{1,0:T(8,128)}, f32[40,1280]{1,0:T(8,128)}, f32[40,1280]{1,0:T(8,128)}) custom-call(s32[5]{0:T(128)} %stack.38.at_ref, bf16[3,40,1280]{2,1,0:T(8,128)(2,1)} %copy-done.15, bf16[3,40,1280]{2,1,0:T(8,128)(2,1)} %copy-done.16, bf16[3,40,1280]{2,1,0:T(8,128)(2,1)} %copy-done.17, ...), custom_call_target="tpu_custom_call" | custom-call | tf_op jit(solution)/shard_map/second_product/spread/pallas_call | solution.py:58
  189.4 5.1 %all-to-all-start.2 = ((bf16[32,40,160]{2,1,0:T(8,128)(2,1)}), bf16[32,40,160]{2,1,0:T(8,128)(2,1)S(1)}, u32[]{:S(2)}, u32[]{:S(2)}) async-start(bf16[32,40,160]{2,1,0:T(8,128)(2,1)} %get-tuple-element.80), calls=%async_computation.2 | async-start | bytes 1310720 | tf_op jit(solution)/shard_map/transposed/all_to_all | solution.py:294
  194.6 2.8 %collective-permute-start.35 = (f32[40,1280]{1,0:T(8,128)}, f32[40,1280]{1,0:T(8,128)S(1)}, u32[]{:S(2)}, u32[]{:S(2)}) collective-permute-start(f32[40,1280]{1,0:T(8,128)} %get-tuple-element.78), channel_id=1, source_target_pairs={{0,16},{1,17},{2,18},{3,19},{4,20},{5,21},{6,22},{7,23},{8,24},{9,... | collective-permute-start | bytes 614408 | tf_op jit(solution)/shard_map/direct/ppermute | solution.py:28
  200.0 2.6 %collective-permute-done.34.d1 = f32[40,1280]{1,0:T(8,128)S(1)} collective-permute-done((f32[40,1280]{1,0:T(8,128)}, f32[40,1280]{1,0:T(8,128)S(1)}, u32[]{:S(2)}, u32[]{:S(2)}) %collective-permute-start.34) | collective-permute-done | bytes 204832 | tf_op jit(solution)/shard_map/direct/ppermute | solution.py:28
  202.7 4.5 %collective-permute-done.35.d2 = f32[40,1280]{1,0:T(8,128)S(1)} collective-permute-done((f32[40,1280]{1,0:T(8,128)}, f32[40,1280]{1,0:T(8,128)S(1)}, u32[]{:S(2)}, u32[]{:S(2)}) %collective-permute-start.35) | collective-permute-done | bytes 204832 | tf_op jit(solution)/shard_map/direct/ppermute | solution.py:28
  210.8 3.9 %finish.1 = f32[40,5120]{1,0:T(8,128)} custom-call(s32[5]{0:T(128)} %stack.38.at_ref, f32[40,1280]{1,0:T(8,128)} %get-tuple-element.76.d0, f32[40,1280]{1,0:T(8,128)} %copy-done.19, f32[40,1280]{1,0:T(8,128)} %copy-done.20, f32[40,1280]{1,0:T(8,128)} %copy-done.21, bf16[32,40,160]{2,1,0:T(8,128)(2,1)} %copy-done.2, f32[40,40]{1,0:T(8,128)} %fusion.22.kept_ref), custom_call_target="tpu_custom_call" | custom-call | tf_op jit(solution)/shard_map/finish/pallas_call | solution.py:58
  (137 shorter events, 64.4 us)
Async XLA Ops:
  8.1 23.2 %all-to-all-start = ((bf16[8,160,320]{2,1,0:T(8,128)(2,1)}), bf16[8,160,320]{2,1,0:T(8,128)(2,1)S(1)}, u32[]{:S(2)}, u32[]{:S(2)}) async-start(bf16[8,160,320]{2,1,0:T(8,128)(2,1)} %right_columns.1), calls=%async_computation | async-start | bytes 1966080 | tf_op jit(solution)/shard_map/right_gather/all_to_all | solution.py:198
  13.0 8.1 %collective-permute-start.1 = (bf16[160,640]{1,0:T(8,128)(2,1)}, bf16[160,640]{1,0:T(8,128)(2,1)S(1)}, u32[]{:S(2)}, u32[]{:S(2)}) collective-permute-start(bf16[160,640]{1,0:T(8,128)(2,1)} %get-tuple-element.51), channel_id=1, source_target_pairs={{0,8},{1,9},{2,10},{3,11},{4,12},{5,13},{6,14},{7,15},{8,0},{9,1},... | collective-permute-start | bytes 614408 | tf_op jit(solution)/shard_map/left_columns/ppermute | solution.py:28
  14.6 12.7 %collective-permute-start.2 = (bf16[160,640]{1,0:T(8,128)(2,1)}, bf16[160,640]{1,0:T(8,128)(2,1)S(1)}, u32[]{:S(2)}, u32[]{:S(2)}) collective-permute-start(bf16[160,640]{1,0:T(8,128)(2,1)} %get-tuple-element.52), channel_id=1, source_target_pairs={{0,16},{1,17},{2,18},{3,19},{4,20},{5,21},{6,22},{7,23},{8,24},{9,... | collective-permute-start | bytes 614408 | tf_op jit(solution)/shard_map/left_columns/ppermute | solution.py:28
  17.5 12.4 %collective-permute-start.3 = (bf16[160,640]{1,0:T(8,128)(2,1)}, bf16[160,640]{1,0:T(8,128)(2,1)S(1)}, u32[]{:S(2)}, u32[]{:S(2)}) collective-permute-start(bf16[160,640]{1,0:T(8,128)(2,1)} %get-tuple-element.53), channel_id=1, source_target_pairs={{0,24},{1,25},{2,26},{3,27},{4,28},{5,29},{6,30},{7,31},{8,16},{9,... | collective-permute-start | bytes 614408 | tf_op jit(solution)/shard_map/left_columns/ppermute | solution.py:28
  18.4 12.9 %collective-permute-start.4 = (bf16[80,1280]{1,0:T(8,128)(2,1)S(1)}, bf16[80,1280]{1,0:T(8,128)(2,1)S(1)}, u32[]{:S(2)}, u32[]{:S(2)}) collective-permute-start(bf16[80,1280]{1,0:T(8,128)(2,1)S(1)} %bitcast.74), channel_id=1, source_target_pairs={{0,1},{1,0},{2,3},{3,2},{4,5},{5,4},{6,7},{7,6},{8,9},{9,8},{10,11... | collective-permute-start | bytes 614408 | tf_op jit(solution)/shard_map/density_turn/ppermute | solution.py:28
  32.6 21.3 %collective-permute-start.5 = (bf16[640,640]{1,0:T(8,128)(2,1)S(1)}, bf16[640,640]{1,0:T(8,128)(2,1)}, u32[]{:S(2)}, u32[]{:S(2)}) collective-permute-start(bf16[640,640]{1,0:T(8,128)(2,1)S(1)} %pad_maximum_fusion.2), channel_id=1, source_target_pairs={{0,4},{1,5},{2,6},{3,7},{4,0},{5,1},{6,2},{7,3},{8,12},{9,13},{10,... | collective-permute-start | bytes 2457608 | tf_op jit(solution)/shard_map/left_gather/ppermute | solution.py:28
  34.1 35.9 %collective-permute-start.6 = (bf16[640,640]{1,0:T(8,128)(2,1)S(1)}, bf16[640,640]{1,0:T(8,128)(2,1)}, u32[]{:S(2)}, u32[]{:S(2)}) collective-permute-start(bf16[640,640]{1,0:T(8,128)(2,1)S(1)} %pad_maximum_fusion.2), channel_id=1, source_target_pairs={{0,1},{1,0},{2,3},{3,2},{4,5},{5,4},{6,7},{7,6},{8,9},{9,8},{10,11... | collective-permute-start | bytes 2457608 | tf_op jit(solution)/shard_map/left_gather/ppermute | solution.py:28
  35.2 36.2 %collective-permute-start.7 = (bf16[640,640]{1,0:T(8,128)(2,1)S(1)}, bf16[640,640]{1,0:T(8,128)(2,1)}, u32[]{:S(2)}, u32[]{:S(2)}) collective-permute-start(bf16[640,640]{1,0:T(8,128)(2,1)S(1)} %pad_maximum_fusion.2), channel_id=1, source_target_pairs={{0,5},{1,4},{2,7},{3,6},{4,1},{5,0},{6,3},{7,2},{8,13},{9,12},{10,... | collective-permute-start | bytes 2457608 | tf_op jit(solution)/shard_map/left_gather/ppermute | solution.py:28
  36.1 37.9 %collective-permute-start.10 = (bf16[320,1280]{1,0:T(8,128)(2,1)S(1)}, bf16[320,1280]{1,0:T(8,128)(2,1)S(1)}, u32[]{:S(2)}, u32[]{:S(2)}) collective-permute-start(bf16[320,1280]{1,0:T(8,128)(2,1)S(1)} %reshape.136), channel_id=1, source_target_pairs={{0,96},{1,97},{2,98},{3,99},{4,100},{5,101},{6,102},{7,103},{8,104... | collective-permute-start | bytes 2457608 | tf_op jit(solution)/shard_map/right_gather/ppermute | solution.py:28
  40.2 33.9 %collective-permute-start.8 = (bf16[320,1280]{1,0:T(8,128)(2,1)S(1)}, bf16[320,1280]{1,0:T(8,128)(2,1)}, u32[]{:S(2)}, u32[]{:S(2)}) collective-permute-start(bf16[320,1280]{1,0:T(8,128)(2,1)S(1)} %reshape.136), channel_id=1, source_target_pairs={{0,32},{1,33},{2,34},{3,35},{4,36},{5,37},{6,38},{7,39},{8,40},{9,... | collective-permute-start | bytes 2457608 | tf_op jit(solution)/shard_map/right_gather/ppermute | solution.py:28
  53.9 22.3 %collective-permute-start.9 = (bf16[320,1280]{1,0:T(8,128)(2,1)S(1)}, bf16[320,1280]{1,0:T(8,128)(2,1)}, u32[]{:S(2)}, u32[]{:S(2)}) collective-permute-start(bf16[320,1280]{1,0:T(8,128)(2,1)S(1)} %reshape.136), channel_id=1, source_target_pairs={{0,64},{1,65},{2,66},{3,67},{4,68},{5,69},{6,70},{7,71},{8,72},{9,... | collective-permute-start | bytes 2457608 | tf_op jit(solution)/shard_map/right_gather/ppermute | solution.py:28
  59.7 16.5 %all-to-all-start.1 = ((bf16[4,80,640]{2,1,0:T(8,128)(2,1)}), bf16[4,80,640]{2,1,0:T(8,128)(2,1)S(1)}, u32[]{:S(2)}, u32[]{:S(2)}) async-start(bf16[4,80,640]{2,1,0:T(8,128)(2,1)} %density_columns.1), calls=%async_computation.1 | async-start | bytes 819200 | tf_op jit(solution)/shard_map/density_columns/all_to_all | solution.py:217
  88.4 11.6 %collective-permute-start.17 = (f32[80,1280]{1,0:T(8,128)S(1)}, f32[80,1280]{1,0:T(8,128)S(1)}, u32[]{:S(2)}, u32[]{:S(2)}) collective-permute-start(f32[80,1280]{1,0:T(8,128)S(1)} %get-tuple-element.103), channel_id=1, source_target_pairs={{0,8},{1,9},{2,10},{3,11},{4,12},{5,13},{6,14},{7,15},{8,0},{9,1},... | collective-permute-start | bytes 1228808 | tf_op jit(solution)/shard_map/mixed_sum/ppermute | solution.py:28
  90.0 13.2 %collective-permute-start.14 = (f32[80,1280]{1,0:T(8,128)S(1)}, f32[80,1280]{1,0:T(8,128)S(1)}, u32[]{:S(2)}, u32[]{:S(2)}) collective-permute-start(f32[80,1280]{1,0:T(8,128)S(1)} %get-tuple-element.104), channel_id=1, source_target_pairs={{0,24},{1,25},{2,26},{3,27},{4,28},{5,29},{6,30},{7,31},{8,16},{9,... | collective-permute-start | bytes 1228808 | tf_op jit(solution)/shard_map/mixed_sum/ppermute | solution.py:28
  100.1 27.7 %collective-permute-start.18 = (f32[160,1280]{1,0:T(8,128)S(1)}, f32[160,1280]{1,0:T(8,128)S(1)}, u32[]{:S(2)}, u32[]{:S(2)}) collective-permute-start(f32[160,1280]{1,0:T(8,128)S(1)} %pad_maximum_fusion.4), channel_id=1, source_target_pairs={{0,24},{1,25},{2,26},{3,27},{4,28},{5,29},{6,30},{7,31},{8,16},{9,... | collective-permute-start | bytes 2457608 | tf_op jit(solution)/shard_map/mixed_sum/ppermute | solution.py:28
  103.3 25.2 %collective-permute-start.15 = (f32[160,1280]{1,0:T(8,128)S(1)}, f32[160,1280]{1,0:T(8,128)S(1)}, u32[]{:S(2)}, u32[]{:S(2)}) collective-permute-start(f32[160,1280]{1,0:T(8,128)S(1)} %pad_maximum_fusion.3), channel_id=1, source_target_pairs={{0,8},{1,9},{2,10},{3,11},{4,12},{5,13},{6,14},{7,15},{8,0},{9,1},... | collective-permute-start | bytes 2457608 | tf_op jit(solution)/shard_map/mixed_sum/ppermute | solution.py:28
  103.6 12.4 %collective-permute-start.19 = (bf16[320,640]{1,0:T(8,128)(2,1)S(1)}, bf16[320,640]{1,0:T(8,128)(2,1)S(1)}, u32[]{:S(2)}, u32[]{:S(2)}) collective-permute-start(bf16[320,640]{1,0:T(8,128)(2,1)S(1)} %bitcast.66), channel_id=1, source_target_pairs={{0,32},{1,33},{2,34},{3,35},{4,36},{5,37},{6,38},{7,39},{8,40},{9,... | collective-permute-start | bytes 1228808 | tf_op jit(solution)/shard_map/density_gather/ppermute | solution.py:28
  103.6 21.6 %collective-permute-start.20 = (bf16[320,640]{1,0:T(8,128)(2,1)S(1)}, bf16[320,640]{1,0:T(8,128)(2,1)S(1)}, u32[]{:S(2)}, u32[]{:S(2)}) collective-permute-start(bf16[320,640]{1,0:T(8,128)(2,1)S(1)} %bitcast.67), channel_id=1, source_target_pairs={{0,64},{1,65},{2,66},{3,67},{4,68},{5,69},{6,70},{7,71},{8,72},{9,... | collective-permute-start | bytes 1228808 | tf_op jit(solution)/shard_map/density_gather/ppermute | solution.py:28
  108.0 19.8 %collective-permute-start.21 = (bf16[320,640]{1,0:T(8,128)(2,1)S(1)}, bf16[320,640]{1,0:T(8,128)(2,1)S(1)}, u32[]{:S(2)}, u32[]{:S(2)}) collective-permute-start(bf16[320,640]{1,0:T(8,128)(2,1)S(1)} %bitcast.68), channel_id=1, source_target_pairs={{0,96},{1,97},{2,98},{3,99},{4,100},{5,101},{6,102},{7,103},{8,104... | collective-permute-start | bytes 1228808 | tf_op jit(solution)/shard_map/density_gather/ppermute | solution.py:28
  134.5 12.3 %collective-permute-start.22 = (bf16[160,1280]{1,0:T(8,128)(2,1)S(1)}, bf16[160,1280]{1,0:T(8,128)(2,1)S(1)}, u32[]{:S(2)}, u32[]{:S(2)}) collective-permute-start(bf16[160,1280]{1,0:T(8,128)(2,1)S(1)} %add_convert_fusion), channel_id=1, source_target_pairs={{0,8},{1,9},{2,10},{3,11},{4,12},{5,13},{6,14},{7,15},{8,0},{9,1},... | collective-permute-start | bytes 1228808 | tf_op jit(solution)/shard_map/mixed_gather/ppermute | solution.py:28
  136.3 21.6 %collective-permute-start.23 = (bf16[160,1280]{1,0:T(8,128)(2,1)S(1)}, bf16[160,1280]{1,0:T(8,128)(2,1)S(1)}, u32[]{:S(2)}, u32[]{:S(2)}) collective-permute-start(bf16[160,1280]{1,0:T(8,128)(2,1)S(1)} %add_convert_fusion), channel_id=1, source_target_pairs={{0,24},{1,25},{2,26},{3,27},{4,28},{5,29},{6,30},{7,31},{8,16},{9,... | collective-permute-start | bytes 1228808 | tf_op jit(solution)/shard_map/mixed_gather/ppermute | solution.py:28
  137.7 29.6 %collective-permute-start.26 = (bf16[160,1280]{1,0:T(8,128)(2,1)S(1)}, bf16[160,1280]{1,0:T(8,128)(2,1)S(1)}, u32[]{:S(2)}, u32[]{:S(2)}) collective-permute-start(bf16[160,1280]{1,0:T(8,128)(2,1)S(1)} %add_convert_fusion), channel_id=1, source_target_pairs={{0,16},{1,17},{2,18},{3,19},{4,20},{5,21},{6,22},{7,23},{8,24},{9,... | collective-permute-start | bytes 1228808 | tf_op jit(solution)/shard_map/mixed_gather/ppermute | solution.py:28
  162.4 13.5 %collective-permute-start.27 = (bf16[3,40,1280]{2,1,0:T(8,128)(2,1)S(1)}, bf16[3,40,1280]{2,1,0:T(8,128)(2,1)S(1)}, u32[]{:S(2)}, u32[]{:S(2)}) collective-permute-start(bf16[3,40,1280]{2,1,0:T(8,128)(2,1)S(1)} %get-tuple-element.99), channel_id=1, source_target_pairs={{0,2},{1,3},{2,4},{3,5},{4,6},{5,7},{6,0},{7,1},{8,10},{9,11},{10,... | collective-permute-start | bytes 921608 | tf_op jit(solution)/shard_map/second_product/ppermute | solution.py:42
  165.5 15.3 %collective-permute-start.28 = (bf16[3,40,1280]{2,1,0:T(8,128)(2,1)S(1)}, bf16[3,40,1280]{2,1,0:T(8,128)(2,1)S(1)}, u32[]{:S(2)}, u32[]{:S(2)}) collective-permute-start(bf16[3,40,1280]{2,1,0:T(8,128)(2,1)S(1)} %get-tuple-element.98), channel_id=1, source_target_pairs={{0,1},{1,0},{2,7},{3,6},{4,5},{5,4},{6,3},{7,2},{8,9},{9,8},{10,15... | collective-permute-start | bytes 921608 | tf_op jit(solution)/shard_map/second_product/ppermute | solution.py:42
  166.4 14.3 %collective-permute-start.29 = (bf16[3,40,1280]{2,1,0:T(8,128)(2,1)S(1)}, bf16[3,40,1280]{2,1,0:T(8,128)(2,1)S(1)}, u32[]{:S(2)}, u32[]{:S(2)}) collective-permute-start(bf16[3,40,1280]{2,1,0:T(8,128)(2,1)S(1)} %get-tuple-element.97), channel_id=1, source_target_pairs={{0,3},{1,2},{2,5},{3,4},{4,7},{5,6},{6,1},{7,0},{8,11},{9,10},{10,... | collective-permute-start | bytes 921608 | tf_op jit(solution)/shard_map/second_product/ppermute | solution.py:42
  168.0 12.7 %collective-permute-start.30 = (bf16[1,40,1280]{2,1,0:T(8,128)(2,1)S(1)}, bf16[1,40,1280]{2,1,0:T(8,128)(2,1)S(1)}, u32[]{:S(2)}, u32[]{:S(2)}) collective-permute-start(bf16[1,40,1280]{2,1,0:T(8,128)(2,1)S(1)} %get-tuple-element.110), channel_id=1, source_target_pairs={{0,0},{1,1},{2,6},{3,7},{4,4},{5,5},{6,2},{7,3},{8,8},{9,9},{10,14... | collective-permute-start | bytes 307208 | tf_op jit(solution)/shard_map/second_product/ppermute | solution.py:42
  168.7 12.4 %collective-permute-start.31 = (bf16[1,40,1280]{2,1,0:T(8,128)(2,1)S(1)}, bf16[1,40,1280]{2,1,0:T(8,128)(2,1)S(1)}, u32[]{:S(2)}, u32[]{:S(2)}) collective-permute-start(bf16[1,40,1280]{2,1,0:T(8,128)(2,1)S(1)} %get-tuple-element.109), channel_id=1, source_target_pairs={{0,2},{1,3},{2,4},{3,5},{4,6},{5,7},{6,0},{7,1},{8,10},{9,11},{10,... | collective-permute-start | bytes 307208 | tf_op jit(solution)/shard_map/second_product/ppermute | solution.py:42
  175.8 7.8 %collective-permute-start.32 = (bf16[1,40,1280]{2,1,0:T(8,128)(2,1)S(1)}, bf16[1,40,1280]{2,1,0:T(8,128)(2,1)S(1)}, u32[]{:S(2)}, u32[]{:S(2)}) collective-permute-start(bf16[1,40,1280]{2,1,0:T(8,128)(2,1)S(1)} %get-tuple-element.108), channel_id=1, source_target_pairs={{0,1},{1,0},{2,7},{3,6},{4,5},{5,4},{6,3},{7,2},{8,9},{9,8},{10,15... | collective-permute-start | bytes 307208 | tf_op jit(solution)/shard_map/second_product/ppermute | solution.py:42
  189.4 20.4 %all-to-all-start.2 = ((bf16[32,40,160]{2,1,0:T(8,128)(2,1)}), bf16[32,40,160]{2,1,0:T(8,128)(2,1)S(1)}, u32[]{:S(2)}, u32[]{:S(2)}) async-start(bf16[32,40,160]{2,1,0:T(8,128)(2,1)} %get-tuple-element.80), calls=%async_computation.2 | async-start | bytes 1310720 | tf_op jit(solution)/shard_map/transposed/all_to_all | solution.py:294
  194.5 8.2 %collective-permute-start.34 = (f32[40,1280]{1,0:T(8,128)}, f32[40,1280]{1,0:T(8,128)S(1)}, u32[]{:S(2)}, u32[]{:S(2)}) collective-permute-start(f32[40,1280]{1,0:T(8,128)} %get-tuple-element.77), channel_id=1, source_target_pairs={{0,8},{1,9},{2,10},{3,11},{4,12},{5,13},{6,14},{7,15},{8,0},{9,1},... | collective-permute-start | bytes 614408 | tf_op jit(solution)/shard_map/direct/ppermute | solution.py:28
  194.6 12.7 %collective-permute-start.35 = (f32[40,1280]{1,0:T(8,128)}, f32[40,1280]{1,0:T(8,128)S(1)}, u32[]{:S(2)}, u32[]{:S(2)}) collective-permute-start(f32[40,1280]{1,0:T(8,128)} %get-tuple-element.78), channel_id=1, source_target_pairs={{0,16},{1,17},{2,18},{3,19},{4,20},{5,21},{6,22},{7,23},{8,24},{9,... | collective-permute-start | bytes 614408 | tf_op jit(solution)/shard_map/direct/ppermute | solution.py:28
  197.4 12.4 %collective-permute-start.36 = (f32[40,1280]{1,0:T(8,128)}, f32[40,1280]{1,0:T(8,128)S(1)}, u32[]{:S(2)}, u32[]{:S(2)}) collective-permute-start(f32[40,1280]{1,0:T(8,128)} %get-tuple-element.79), channel_id=1, source_target_pairs={{0,24},{1,25},{2,26},{3,27},{4,28},{5,29},{6,30},{7,31},{8,16},{9,... | collective-permute-start | bytes 614408 | tf_op jit(solution)/shard_map/direct/ppermute | solution.py:28
  (36 other events, 255.5 us)

commit v7 on v6

--- a/solution.py
+++ b/solution.py
@@ -110,31 +110,57 @@
         out_ref[ny] = jnp.concatenate((first[:, cut], second[:, cut]), axis=1)
 
 
-def rows_kernel(at_ref, *refs):
-    out_ref = refs[4]
+def rows_kernel(at_ref, own_ref, one_ref, upper_ref, lower_ref, three_ref, out_ref):
     z = at_ref[0]
-    for q in range(4):
-        out_ref[pl.ds(pl.multiple_of((z ^ q) * 320, 320), 320), :] = refs[q][...]
-
-
-def join_kernel(at_ref, mine_ref, other_ref, out_ref):
-    core = at_ref[3]
-    out_ref[:, :640] = jnp.where(core == 0, mine_ref[...], other_ref[...])
-    out_ref[:, 640:] = jnp.where(core == 0, other_ref[...], mine_ref[...])
+
+    def place(q, start, count, ref):
+        first = pl.multiple_of((z ^ q) * 320 + start, 160)
+        out_ref[pl.ds(first, count), :] = ref[...]
+
+    place(0, 0, 320, own_ref)
+    place(1, 0, 320, one_ref)
+    place(2, 0, 160, upper_ref)
+    place(2, 160, 160, lower_ref)
+    place(3, 0, 320, three_ref)
+
+
+def second_kernel(at_ref, mine_ref, other_ref, *refs):
+    rows, outs, whole = refs[:-5], refs[-5:-1], refs[-1]
+    core, xh = at_ref[3], at_ref[4]
+    for side, right in enumerate((mine_ref, other_ref)):
+        first = 0
+        for ref in rows:
+            count = ref.shape[0] // 80
+            whole[side, first : first + count] = dot(ref[...], right[...]).reshape(
+                count, 2, 40, 640
+            )
+            first += count
+    for i, out in enumerate(outs):
+        r, t = i // 2, i % 2
+        for side in range(2):
+            for slot in range(out.shape[1]):
+                out[side, slot] = whole[side, slot * 2 + (core ^ t), xh ^ r].astype(bf16)
 
 
 def spread_kernel(at_ref, *refs):
     many, last = refs[:4], refs[4:8]
     turned_ref, outs, slots = refs[8], refs[9:13], refs[13]
-    y = at_ref[1]
+    y, core = at_ref[1], at_ref[3]
     for q in range(4):
         parts = last if q == 2 else many
         place = 0 if q == 2 else (0, 1, None, 2)[q]
-        total = parts[0][place].astype(f32)
-        for ref in parts[1:]:
-            total = total + ref[place].astype(f32)
-        outs[q][...] = total
-        slots[y ^ q] = total
+
+        def total(side):
+            terms = [parts[i][side ^ (i % 2), place].astype(f32) for i in range(4)]
+            return (terms[0] + terms[1]) + (terms[2] + terms[3])
+
+        mine, other = total(0), total(1)
+        low = jnp.where(core == 0, mine, other)
+        high = jnp.where(core == 0, other, mine)
+        outs[q][:, :640] = low
+        outs[q][:, 640:] = high
+        slots[y ^ q, :, :640] = low
+        slots[y ^ q, :, 640:] = high
     for nz in range(4):
         part = jnp.concatenate(
             [slots[ny, :, nz * 320 : nz * 320 + 320] for ny in range(4)], axis=0
@@ -237,49 +263,57 @@
             both[q] = mine[q] + flip(theirs[q], core=1)
         upper = flip(both[2][:80], y=1)
         lower = flip(both[2][80:], y=3)
+
+    with jax.named_scope("density_gather"):
+        done = flip(dslots, z=1)
+        dthree = flip(dslots, z=3)
+        upper, lower, done, dthree = lax.optimization_barrier((upper, lower, done, dthree))
+        dtwo = (flip(dthree[:160], z=1), flip(done[160:], z=3))
+
+    with jax.named_scope("mixed_sum"):
         third = jnp.concatenate((both[3][:80] + upper, both[3][80:]))
         first = jnp.concatenate((both[1][:80], both[1][80:] + lower))
         sums = [flip(first, y=1), flip(third, y=3)]
 
-    with jax.named_scope("density_gather"):
-        dslots, _ = lax.optimization_barrier((dslots, both))
-        dparts = [dslots] + [flip(dslots, z=q) for q in (1, 2, 3)]
+    with jax.named_scope("density_rows"):
+        dmine = local_call(
+            rows_kernel, "density_rows", shape(bf16, 1280, 640), coords, dslots, done, *dtwo, dthree
+        )
 
     with jax.named_scope("mixed_sum"):
-        sums, dparts = lax.optimization_barrier((sums, dparts))
+        sums, dmine = lax.optimization_barrier((sums, dmine))
         total = both[0] + sums[0] + sums[1]
         mixed = total.astype(bf16)
 
-    with jax.named_scope("density_rows"):
-        dmine = local_call(rows_kernel, "density_rows", shape(bf16, 1280, 640), coords, *dparts)
-        dfull = local_call(
-            join_kernel, "density_join", shape(bf16, 1280, 1280), coords, dmine, flip(dmine, core=1)
-        )
     with jax.named_scope("mixed_gather"):
-        mslots = [mixed] + [flip(mixed, y=q) for q in (1, 2, 3)]
+        one, three = flip(mixed, y=1), flip(mixed, y=3)
+        dother = flip(dmine, core=1)
+        two = (three[:80], one[80:])
+        two, one, three = lax.optimization_barrier((two, one, three))
+        two = (flip(two[0], y=1), flip(two[1], y=3))
 
     with jax.named_scope("second_product"):
-        turns = [(r, t) for r in range(2) for t in range(2)]
-
-        def pieces_of(rows, count):
-            resp = dot(rows, dfull).reshape(count, 2, 2, 40, 1280)
-            cut = []
-            for r, t in turns:
-                piece = lax.dynamic_index_in_dim(resp, core ^ t, 1, keepdims=False)
-                piece = lax.dynamic_index_in_dim(piece, xh ^ r, 1, keepdims=False)
-                cut.append(piece.astype(bf16))
-            return cut
-
-        def scatter(cut):
+
+        def scatter(count, *rows):
+            cut = local_call(
+                second_kernel,
+                "second_product",
+                [shape(bf16, 2, count, 40, 640)] * 4,
+                coords,
+                dmine,
+                dother,
+                *rows,
+                scratch=[pltpu.VMEM((2, count * 2, 2, 40, 640), f32)],
+            )
+            turns = [(r, t) for r in range(2) for t in range(2)]
             return [
                 remap(piece, lambda a, b, c, d, e: (a, b, c ^ d, d ^ t, e ^ r))
                 for piece, (r, t) in zip(cut, turns)
             ]
 
-        many = pieces_of(jnp.concatenate((mslots[0], mslots[1], mslots[3])), 3)
-        many = scatter(many)
-        many[0], mslots[2] = lax.optimization_barrier((many[0], mslots[2]))
-        last = scatter(pieces_of(mslots[2], 1))
+        many = scatter(3, mixed, one, three)
+        many[0], two = lax.optimization_barrier((many[0], two))
+        last = scatter(1, *two)
         turned, *rows = local_call(
             spread_kernel,
             "spread",

time: 215 us -> 208 us (0.967)
  starting transfers between devices: 72.7 us -> 64.1 us
  Pallas kernels: 20.8 us -> 26.3 us
  matrix products: 9.76 us -> 5.34 us
    ppermute x8, starting transfers between devices: 18 us -> 10.4 us  [remap(): return lax.ppermute(value, AXES, pairs)]
    pallas_call x7 -> x8, Pallas kernels: 20.8 us -> 26.3 us  [local_call(): pl.pallas_call(kernel, out_shape=outs, in_specs=[SMEM] + [VMEM] * len(ope...]
    dot_general x4 -> x2, matrix products: 8.97 us -> 4.56 us  [dot(): return jnp.dot(a, b, preferred_element_type=f32)]
    ppermute x29 -> x31, starting transfers between devices: 40.2 us -> 38 us  [flip(): return lax.ppermute(value, AXES, pairs)]
    ppermute x29 -> x31, waiting for transfers between devices: 83.8 us -> 82.4 us  [flip(): return lax.ppermute(value, AXES, pairs)]
    unnamed x56 -> x62, local copies, waits for them, and re-layouts: 7.26 us -> 8.17 us
  transfers between devices with their start and end apart: 40 -> 42, of which waited for: 24 -> 24; matrix products, arithmetic and copies ran while one was open for 8% -> 6% of each run, Pallas kernels for 4% -> 8%
where the time goes in v7:
time: 208 us; the launch traced here: 207 us
  waiting for transfers between devices  87.5 us (42%)
  starting transfers between devices  64.1 us (31%)
  Pallas kernels  26.3 us (13%)
  other arithmetic  12.1 us (6%)
  local copies, waits for them, and re-layouts  11.4 us (5%)
  matrix products  5.34 us (3%)
    ppermute x31, waiting for transfers between devices, flip(): return lax.ppermute(value, AXES, pairs)  82.4 us
    ppermute x31, starting transfers between devices, flip(): return lax.ppermute(value, AXES, pairs)  38 us
    pallas_call x8, Pallas kernels, local_call(): pl.pallas_call(kernel, out_shape=outs, in_specs=[SMEM] + [VMEM] * len(ope...  26.3 us
    ppermute x8, starting transfers between devices, remap(): return lax.ppermute(value, AXES, pairs)  10.4 us
    unnamed x62, local copies, waits for them, and re-layouts  8.17 us
    all_to_all x1, starting transfers between devices, shards(): lax.all_to_all(turned, ('z', 'xl', 'core', 'xh'), split_axis=0, concat_ax...  6.32 us
    ppermute x8, waiting for transfers between devices, remap(): return lax.ppermute(value, AXES, pairs)  5.09 us
    all_to_all x1, starting transfers between devices, shards(): lax.all_to_all(parts, ('xl', 'core', 'xh'), split_axis=0, concat_axis=0,...  4.92 us
  transfers between devices with their start and end apart: 42, of which 24 were waited for; matrix products, arithmetic and copies ran while one was open for 6% of the time, Pallas kernels for 8%

profile of v7, /device:TPU:2, one launch (start us, length us, event | category | flops | bytes accessed | tf_op | source)
XLA Modules:
  0.0 207.2 jit_solution(16678734867715386335)
XLA Ops:
  1.8 2.8 %right_columns.1 = bf16[8,160,320]{2,1,0:T(8,128)(2,1)} custom-call(s32[5]{0:T(128)} %stack.38.at_ref, bf16[160,1280]{1,0:T(8,128)(2,1)} %first_ref.1, bf16[160,1280]{1,0:T(8,128)(2,1)} %second_ref.1), custom_call_target="tpu_custom_call" | custom-call | tf_op jit(solution)/shard_map/right_columns/right_columns/pallas_call | solution.py:58
  5.4 2.7 %left_columns.1 = (bf16[160,640]{1,0:T(8,128)(2,1)}, bf16[160,640]{1,0:T(8,128)(2,1)}, bf16[160,640]{1,0:T(8,128)(2,1)}, bf16[160,640]{1,0:T(8,128)(2,1)}) custom-call(s32[5]{0:T(128)} %stack.38.at_ref, bf16[160,1280]{1,0:T(8,128)(2,1)} %first_ref.2, bf16[160,1280]{1,0:T(8,128)(2,1)} %second_ref.2, bf16[160,1280]{1,0:T(8,128)(2,1)} %copy-done.13), custom_call_target="tpu_custom_call" | custom-call | tf_op jit(solution)/shard_map/left_columns/left_columns/pallas_call | solution.py:58
  8.0 4.9 %all-to-all-start = ((bf16[8,160,320]{2,1,0:T(8,128)(2,1)}), bf16[8,160,320]{2,1,0:T(8,128)(2,1)S(1)}, u32[]{:S(2)}, u32[]{:S(2)}) async-start(bf16[8,160,320]{2,1,0:T(8,128)(2,1)} %right_columns.1), calls=%async_computation | async-start | bytes 1966080 | tf_op jit(solution)/shard_map/right_gather/all_to_all | solution.py:224
  14.5 2.9 %collective-permute-start.2 = (bf16[160,640]{1,0:T(8,128)(2,1)}, bf16[160,640]{1,0:T(8,128)(2,1)S(1)}, u32[]{:S(2)}, u32[]{:S(2)}) collective-permute-start(bf16[160,640]{1,0:T(8,128)(2,1)} %get-tuple-element.65), channel_id=1, source_target_pairs={{0,16},{1,17},{2,18},{3,19},{4,20},{5,21},{6,22},{7,23},{8,24},{9,... | collective-permute-start | bytes 614408 | tf_op jit(solution)/shard_map/left_columns/ppermute | solution.py:28
  21.1 6.1 %collective-permute-done.2 = bf16[160,640]{1,0:T(8,128)(2,1)S(1)} collective-permute-done((bf16[160,640]{1,0:T(8,128)(2,1)}, bf16[160,640]{1,0:T(8,128)(2,1)S(1)}, u32[]{:S(2)}, u32[]{:S(2)}) %collective-permute-start.2) | collective-permute-done | bytes 204832 | tf_op jit(solution)/shard_map/left_columns/ppermute | solution.py:28
  27.2 2.6 %collective-permute-done.3 = bf16[160,640]{1,0:T(8,128)(2,1)S(1)} collective-permute-done((bf16[160,640]{1,0:T(8,128)(2,1)}, bf16[160,640]{1,0:T(8,128)(2,1)S(1)}, u32[]{:S(2)}, u32[]{:S(2)}) %collective-permute-start.3) | collective-permute-done | bytes 204832 | tf_op jit(solution)/shard_map/left_columns/ppermute | solution.py:28
  36.1 4.0 %collective-permute-start.10 = (bf16[320,1280]{1,0:T(8,128)(2,1)S(1)}, bf16[320,1280]{1,0:T(8,128)(2,1)S(1)}, u32[]{:S(2)}, u32[]{:S(2)}) collective-permute-start(bf16[320,1280]{1,0:T(8,128)(2,1)S(1)} %reshape.58), channel_id=1, source_target_pairs={{0,96},{1,97},{2,98},{3,99},{4,100},{5,101},{6,102},{7,103},{8,104... | collective-permute-start | bytes 2457608 | tf_op jit(solution)/shard_map/right_gather/ppermute | solution.py:28
  40.1 13.7 %collective-permute-done.5 = bf16[640,640]{1,0:T(8,128)(2,1)} collective-permute-done((bf16[640,640]{1,0:T(8,128)(2,1)S(1)}, bf16[640,640]{1,0:T(8,128)(2,1)}, u32[]{:S(2)}, u32[]{:S(2)}) %collective-permute-start.5) | collective-permute-done | bytes 819232 | tf_op jit(solution)/shard_map/left_gather/ppermute | solution.py:28
  53.8 3.9 %collective-permute-start.9 = (bf16[320,1280]{1,0:T(8,128)(2,1)S(1)}, bf16[320,1280]{1,0:T(8,128)(2,1)}, u32[]{:S(2)}, u32[]{:S(2)}) collective-permute-start(bf16[320,1280]{1,0:T(8,128)(2,1)S(1)} %reshape.58), channel_id=1, source_target_pairs={{0,64},{1,65},{2,66},{3,67},{4,68},{5,69},{6,70},{7,71},{8,72},{9,... | collective-permute-start | bytes 2457608 | tf_op jit(solution)/shard_map/right_gather/ppermute | solution.py:28
  59.7 4.5 %all-to-all-start.1 = ((bf16[4,80,640]{2,1,0:T(8,128)(2,1)}), bf16[4,80,640]{2,1,0:T(8,128)(2,1)S(1)}, u32[]{:S(2)}, u32[]{:S(2)}) async-start(bf16[4,80,640]{2,1,0:T(8,128)(2,1)} %density_columns.1), calls=%async_computation.1 | async-start | bytes 819200 | tf_op jit(solution)/shard_map/density_columns/all_to_all | solution.py:243
  64.1 2.5 %broadcast_select_fusion.3 = (bf16[640,640]{1,0:T(8,128)(2,1)}, bf16[640,640]{1,0:T(8,128)(2,1)}) fusion(bf16[640,640]{1,0:T(8,128)(2,1)S(1)} %pad_maximum_fusion.2, bf16[640,640]{1,0:T(8,128)(2,1)} %collective-permute-done.5, pred[]{:T(512)S(6)} %eq.8), kind=kLoop, calls=%fused_computation.28 | loop fusion | flops 819200 | bytes 3276801 | tf_op jit(solution)/shard_map/first_product/jit(_where)/select_n | solution.py:257
  66.6 3.3 %collective-permute-done.6 = bf16[640,640]{1,0:T(8,128)(2,1)} collective-permute-done((bf16[640,640]{1,0:T(8,128)(2,1)S(1)}, bf16[640,640]{1,0:T(8,128)(2,1)}, u32[]{:S(2)}, u32[]{:S(2)}) %collective-permute-start.6) | collective-permute-done | bytes 819232 | tf_op jit(solution)/shard_map/left_gather/ppermute | solution.py:28
  71.3 2.4 %broadcast_select_fusion.2 = (bf16[640,640]{1,0:T(8,128)(2,1)S(1)}, bf16[640,640]{1,0:T(8,128)(2,1)}) fusion(bf16[640,640]{1,0:T(8,128)(2,1)} %collective-permute-done.6, bf16[640,640]{1,0:T(8,128)(2,1)} %collective-permute-done.7, pred[]{:T(512)S(6)} %eq.8), kind=kLoop, calls=%fused_computation.27 | loop fusion | flops 819200 | bytes 3276801 | tf_op jit(solution)/shard_map/first_product/jit(_where)/select_n | solution.py:257
  73.7 2.4 %collective-permute-done.9 = bf16[320,1280]{1,0:T(8,128)(2,1)} collective-permute-done((bf16[320,1280]{1,0:T(8,128)(2,1)S(1)}, bf16[320,1280]{1,0:T(8,128)(2,1)}, u32[]{:S(2)}, u32[]{:S(2)}) %collective-permute-start.9) | collective-permute-done | bytes 819232 | tf_op jit(solution)/shard_map/right_gather/ppermute | solution.py:28
  82.6 3.1 %collective-permute-start.16 = (bf16[320,640]{1,0:T(8,128)(2,1)S(1)}, bf16[320,640]{1,0:T(8,128)(2,1)S(1)}, u32[]{:S(2)}, u32[]{:S(2)}) collective-permute-start(bf16[320,640]{1,0:T(8,128)(2,1)S(1)} %bitcast.30), channel_id=1, source_target_pairs={{0,96},{1,97},{2,98},{3,99},{4,100},{5,101},{6,102},{7,103},{8,104... | collective-permute-start | bytes 1228808 | tf_op jit(solution)/shard_map/density_gather/ppermute | solution.py:28
  95.6 5.6 %collective-permute-done.13 = f32[80,1280]{1,0:T(8,128)S(1)} collective-permute-done((f32[80,1280]{1,0:T(8,128)S(1)}, f32[80,1280]{1,0:T(8,128)S(1)}, u32[]{:S(2)}, u32[]{:S(2)}) %collective-permute-start.13) | collective-permute-done | bytes 409632 | tf_op jit(solution)/shard_map/mixed_sum/ppermute | solution.py:28
  101.2 2.5 %collective-permute-done.14 = f32[80,1280]{1,0:T(8,128)S(1)} collective-permute-done((f32[80,1280]{1,0:T(8,128)S(1)}, f32[80,1280]{1,0:T(8,128)S(1)}, u32[]{:S(2)}, u32[]{:S(2)}) %collective-permute-start.14) | collective-permute-done | bytes 409632 | tf_op jit(solution)/shard_map/mixed_sum/ppermute | solution.py:28
  109.4 5.3 %collective-permute-done.20.upper_ref = bf16[160,640]{1,0:T(8,128)(2,1)S(1)} collective-permute-done((bf16[160,640]{1,0:T(8,128)(2,1)S(1)}, bf16[160,640]{1,0:T(8,128)(2,1)S(1)}, u32[]{:S(2)}, u32[]{:S(2)}) %collective-permute-start.20) | collective-permute-done | bytes 204832 | tf_op jit(solution)/shard_map/density_gather/ppermute | solution.py:28
  117.6 2.7 %density_rows.1.mine_ref = bf16[1280,640]{1,0:T(8,128)(2,1)} custom-call(s32[5]{0:T(128)} %stack.38.at_ref, bf16[320,640]{1,0:T(8,128)(2,1)} %bitcast.31, bf16[320,640]{1,0:T(8,128)(2,1)} %copy-done.8, bf16[160,640]{1,0:T(8,128)(2,1)} %copy-done.24, bf16[160,640]{1,0:T(8,128)(2,1)} %copy-done.25, bf16[320,640]{1,0:T(8,128)(2,1)} %copy-done.9), custom_call_target="tpu_custom_call" | custom-call | tf_op jit(solution)/shard_map/density_rows/density_rows/pallas_call | solution.py:58
  120.4 3.8 %collective-permute-done.19 = f32[160,1280]{1,0:T(8,128)S(1)} collective-permute-done((f32[160,1280]{1,0:T(8,128)S(1)}, f32[160,1280]{1,0:T(8,128)S(1)}, u32[]{:S(2)}, u32[]{:S(2)}) %collective-permute-start.19) | collective-permute-done | bytes 819232 | tf_op jit(solution)/shard_map/mixed_sum/ppermute | solution.py:28
  129.1 12.0 %collective-permute-done.24.refs_2_ = bf16[160,1280]{1,0:T(8,128)(2,1)S(1)} collective-permute-done((bf16[160,1280]{1,0:T(8,128)(2,1)S(1)}, bf16[160,1280]{1,0:T(8,128)(2,1)S(1)}, u32[]{:S(2)}, u32[]{:S(2)}) %collective-permute-start.24) | collective-permute-done | bytes 409632 | tf_op jit(solution)/shard_map/mixed_gather/ppermute | solution.py:28
  143.2 5.4 %second_product.2 = (bf16[2,3,40,640]{3,2,1,0:T(8,128)(2,1)}, bf16[2,3,40,640]{3,2,1,0:T(8,128)(2,1)}, bf16[2,3,40,640]{3,2,1,0:T(8,128)(2,1)}, bf16[2,3,40,640]{3,2,1,0:T(8,128)(2,1)}) custom-call(s32[5]{0:T(128)} %stack.38.at_ref, bf16[1280,640]{1,0:T(8,128)(2,1)} %density_rows.1.mine_ref, bf16[1280,640]{1,0:T(8,128)(2,1)} %copy-done, ...), custom_call_target="tpu_custom_call" | custom-call | tf_op jit(solution)/shard_map/second_product/second_product/pallas_call | solution.py:58
  150.2 2.5 %collective-permute-start.29 = (bf16[2,3,40,640]{3,2,1,0:T(8,128)(2,1)}, bf16[2,3,40,640]{3,2,1,0:T(8,128)(2,1)S(1)}, u32[]{:S(2)}, u32[]{:S(2)}) collective-permute-start(bf16[2,3,40,640]{3,2,1,0:T(8,128)(2,1)} %get-tuple-element.93), channel_id=1, source_target_pairs={{0,2},{1,3},{2,4},{3,5},{4,6},{5,7},{6,0},{7,1},{8,10},{9,11},{10,... | collective-permute-start | bytes 921608 | tf_op jit(solution)/shard_map/second_product/ppermute | solution.py:42
  155.4 6.4 %collective-permute-done.28.refs_1_ = bf16[80,1280]{1,0:T(8,128)(2,1)S(1)} collective-permute-done((bf16[80,1280]{1,0:T(8,128)(2,1)S(1)}, bf16[80,1280]{1,0:T(8,128)(2,1)S(1)}, u32[]{:S(2)}, u32[]{:S(2)}) %collective-permute-start.28) | collective-permute-done | bytes 204832 | tf_op jit(solution)/shard_map/mixed_gather/ppermute | solution.py:28
  162.6 4.0 %second_product.3 = (bf16[2,1,40,640]{3,2,1,0:T(8,128)(2,1)}, bf16[2,1,40,640]{3,2,1,0:T(8,128)(2,1)}, bf16[2,1,40,640]{3,2,1,0:T(8,128)(2,1)}, bf16[2,1,40,640]{3,2,1,0:T(8,128)(2,1)}) custom-call(s32[5]{0:T(128)} %stack.38.at_ref, bf16[1280,640]{1,0:T(8,128)(2,1)} %density_rows.1.mine_ref, bf16[1280,640]{1,0:T(8,128)(2,1)} %copy-done, ...), custom_call_target="tpu_custom_call" | custom-call | tf_op jit(solution)/shard_map/second_product/second_product/pallas_call | solution.py:58
  177.5 2.9 %spread.1 = (bf16[32,40,160]{2,1,0:T(8,128)(2,1)}, f32[40,1280]{1,0:T(8,128)}, f32[40,1280]{1,0:T(8,128)}, f32[40,1280]{1,0:T(8,128)}, f32[40,1280]{1,0:T(8,128)}) custom-call(s32[5]{0:T(128)} %stack.38.at_ref, bf16[2,3,40,640]{3,2,1,0:T(8,128)(2,1)} %copy-done.14, bf16[2,3,40,640]{3,2,1,0:T(8,128)(2,1)} %copy-done.15, bf16[2,3,40,640]{3,2,1,0:T(8,128)(2,1)} %copy-done.16, ...), custom_call_target="tpu_custom_call" | custom-call | tf_op jit(solution)/shard_map/second_product/spread/pallas_call | solution.py:58
  180.4 6.3 %all-to-all-start.2 = ((bf16[32,40,160]{2,1,0:T(8,128)(2,1)}), bf16[32,40,160]{2,1,0:T(8,128)(2,1)S(1)}, u32[]{:S(2)}, u32[]{:S(2)}) async-start(bf16[32,40,160]{2,1,0:T(8,128)(2,1)} %get-tuple-element.106), calls=%async_computation.2 | async-start | bytes 1310720 | tf_op jit(solution)/shard_map/transposed/all_to_all | solution.py:328
  186.9 3.0 %collective-permute-start.37 = (f32[40,1280]{1,0:T(8,128)}, f32[40,1280]{1,0:T(8,128)S(1)}, u32[]{:S(2)}, u32[]{:S(2)}) collective-permute-start(f32[40,1280]{1,0:T(8,128)} %get-tuple-element.104), channel_id=1, source_target_pairs={{0,16},{1,17},{2,18},{3,19},{4,20},{5,21},{6,22},{7,23},{8,24},{9,... | collective-permute-start | bytes 614408 | tf_op jit(solution)/shard_map/direct/ppermute | solution.py:28
  192.3 2.6 %collective-permute-done.36.d1 = f32[40,1280]{1,0:T(8,128)S(1)} collective-permute-done((f32[40,1280]{1,0:T(8,128)}, f32[40,1280]{1,0:T(8,128)S(1)}, u32[]{:S(2)}, u32[]{:S(2)}) %collective-permute-start.36) | collective-permute-done | bytes 204832 | tf_op jit(solution)/shard_map/direct/ppermute | solution.py:28
  195.0 4.8 %collective-permute-done.37.d2 = f32[40,1280]{1,0:T(8,128)S(1)} collective-permute-done((f32[40,1280]{1,0:T(8,128)}, f32[40,1280]{1,0:T(8,128)S(1)}, u32[]{:S(2)}, u32[]{:S(2)}) %collective-permute-start.37) | collective-permute-done | bytes 204832 | tf_op jit(solution)/shard_map/direct/ppermute | solution.py:28
  199.7 2.6 %collective-permute-done.38.d3 = f32[40,1280]{1,0:T(8,128)S(1)} collective-permute-done((f32[40,1280]{1,0:T(8,128)}, f32[40,1280]{1,0:T(8,128)S(1)}, u32[]{:S(2)}, u32[]{:S(2)}) %collective-permute-start.38) | collective-permute-done | bytes 204832 | tf_op jit(solution)/shard_map/direct/ppermute | solution.py:28
  203.3 3.9 %finish.1 = f32[40,5120]{1,0:T(8,128)} custom-call(s32[5]{0:T(128)} %stack.38.at_ref, f32[40,1280]{1,0:T(8,128)} %get-tuple-element.102.d0, f32[40,1280]{1,0:T(8,128)} %copy-done.18, f32[40,1280]{1,0:T(8,128)} %copy-done.19, f32[40,1280]{1,0:T(8,128)} %copy-done.20, bf16[32,40,160]{2,1,0:T(8,128)(2,1)} %copy-done.3, f32[40,40]{1,0:T(8,128)} %fusion.11.kept_ref), custom_call_target="tpu_custom_call" | custom-call | tf_op jit(solution)/shard_map/finish/pallas_call | solution.py:58
  (147 shorter events, 68.6 us)
Async XLA Ops:
  8.0 23.2 %all-to-all-start = ((bf16[8,160,320]{2,1,0:T(8,128)(2,1)}), bf16[8,160,320]{2,1,0:T(8,128)(2,1)S(1)}, u32[]{:S(2)}, u32[]{:S(2)}) async-start(bf16[8,160,320]{2,1,0:T(8,128)(2,1)} %right_columns.1), calls=%async_computation | async-start | bytes 1966080 | tf_op jit(solution)/shard_map/right_gather/all_to_all | solution.py:224
  14.5 12.7 %collective-permute-start.2 = (bf16[160,640]{1,0:T(8,128)(2,1)}, bf16[160,640]{1,0:T(8,128)(2,1)S(1)}, u32[]{:S(2)}, u32[]{:S(2)}) collective-permute-start(bf16[160,640]{1,0:T(8,128)(2,1)} %get-tuple-element.65), channel_id=1, source_target_pairs={{0,16},{1,17},{2,18},{3,19},{4,20},{5,21},{6,22},{7,23},{8,24},{9,... | collective-permute-start | bytes 614408 | tf_op jit(solution)/shard_map/left_columns/ppermute | solution.py:28
  17.4 12.4 %collective-permute-start.3 = (bf16[160,640]{1,0:T(8,128)(2,1)}, bf16[160,640]{1,0:T(8,128)(2,1)S(1)}, u32[]{:S(2)}, u32[]{:S(2)}) collective-permute-start(bf16[160,640]{1,0:T(8,128)(2,1)} %get-tuple-element.66), channel_id=1, source_target_pairs={{0,24},{1,25},{2,26},{3,27},{4,28},{5,29},{6,30},{7,31},{8,16},{9,... | collective-permute-start | bytes 614408 | tf_op jit(solution)/shard_map/left_columns/ppermute | solution.py:28
  18.4 12.9 %collective-permute-start.4 = (bf16[80,1280]{1,0:T(8,128)(2,1)S(1)}, bf16[80,1280]{1,0:T(8,128)(2,1)S(1)}, u32[]{:S(2)}, u32[]{:S(2)}) collective-permute-start(bf16[80,1280]{1,0:T(8,128)(2,1)S(1)} %bitcast.34), channel_id=1, source_target_pairs={{0,1},{1,0},{2,3},{3,2},{4,5},{5,4},{6,7},{7,6},{8,9},{9,8},{10,11... | collective-permute-start | bytes 614408 | tf_op jit(solution)/shard_map/density_turn/ppermute | solution.py:28
  32.5 21.3 %collective-permute-start.5 = (bf16[640,640]{1,0:T(8,128)(2,1)S(1)}, bf16[640,640]{1,0:T(8,128)(2,1)}, u32[]{:S(2)}, u32[]{:S(2)}) collective-permute-start(bf16[640,640]{1,0:T(8,128)(2,1)S(1)} %pad_maximum_fusion.2), channel_id=1, source_target_pairs={{0,4},{1,5},{2,6},{3,7},{4,0},{5,1},{6,2},{7,3},{8,12},{9,13},{10,... | collective-permute-start | bytes 2457608 | tf_op jit(solution)/shard_map/left_gather/ppermute | solution.py:28
  34.0 35.9 %collective-permute-start.6 = (bf16[640,640]{1,0:T(8,128)(2,1)S(1)}, bf16[640,640]{1,0:T(8,128)(2,1)}, u32[]{:S(2)}, u32[]{:S(2)}) collective-permute-start(bf16[640,640]{1,0:T(8,128)(2,1)S(1)} %pad_maximum_fusion.2), channel_id=1, source_target_pairs={{0,1},{1,0},{2,3},{3,2},{4,5},{5,4},{6,7},{7,6},{8,9},{9,8},{10,11... | collective-permute-start | bytes 2457608 | tf_op jit(solution)/shard_map/left_gather/ppermute | solution.py:28
  35.1 36.2 %collective-permute-start.7 = (bf16[640,640]{1,0:T(8,128)(2,1)S(1)}, bf16[640,640]{1,0:T(8,128)(2,1)}, u32[]{:S(2)}, u32[]{:S(2)}) collective-permute-start(bf16[640,640]{1,0:T(8,128)(2,1)S(1)} %pad_maximum_fusion.2), channel_id=1, source_target_pairs={{0,5},{1,4},{2,7},{3,6},{4,1},{5,0},{6,3},{7,2},{8,13},{9,12},{10,... | collective-permute-start | bytes 2457608 | tf_op jit(solution)/shard_map/left_gather/ppermute | solution.py:28
  36.1 37.7 %collective-permute-start.10 = (bf16[320,1280]{1,0:T(8,128)(2,1)S(1)}, bf16[320,1280]{1,0:T(8,128)(2,1)S(1)}, u32[]{:S(2)}, u32[]{:S(2)}) collective-permute-start(bf16[320,1280]{1,0:T(8,128)(2,1)S(1)} %reshape.58), channel_id=1, source_target_pairs={{0,96},{1,97},{2,98},{3,99},{4,100},{5,101},{6,102},{7,103},{8,104... | collective-permute-start | bytes 2457608 | tf_op jit(solution)/shard_map/right_gather/ppermute | solution.py:28
  40.1 33.6 %collective-permute-start.8 = (bf16[320,1280]{1,0:T(8,128)(2,1)S(1)}, bf16[320,1280]{1,0:T(8,128)(2,1)}, u32[]{:S(2)}, u32[]{:S(2)}) collective-permute-start(bf16[320,1280]{1,0:T(8,128)(2,1)S(1)} %reshape.58), channel_id=1, source_target_pairs={{0,32},{1,33},{2,34},{3,35},{4,36},{5,37},{6,38},{7,39},{8,40},{9,... | collective-permute-start | bytes 2457608 | tf_op jit(solution)/shard_map/right_gather/ppermute | solution.py:28
  53.8 22.3 %collective-permute-start.9 = (bf16[320,1280]{1,0:T(8,128)(2,1)S(1)}, bf16[320,1280]{1,0:T(8,128)(2,1)}, u32[]{:S(2)}, u32[]{:S(2)}) collective-permute-start(bf16[320,1280]{1,0:T(8,128)(2,1)S(1)} %reshape.58), channel_id=1, source_target_pairs={{0,64},{1,65},{2,66},{3,67},{4,68},{5,69},{6,70},{7,71},{8,72},{9,... | collective-permute-start | bytes 2457608 | tf_op jit(solution)/shard_map/right_gather/ppermute | solution.py:28
  59.7 16.5 %all-to-all-start.1 = ((bf16[4,80,640]{2,1,0:T(8,128)(2,1)}), bf16[4,80,640]{2,1,0:T(8,128)(2,1)S(1)}, u32[]{:S(2)}, u32[]{:S(2)}) async-start(bf16[4,80,640]{2,1,0:T(8,128)(2,1)} %density_columns.1), calls=%async_computation.1 | async-start | bytes 819200 | tf_op jit(solution)/shard_map/density_columns/all_to_all | solution.py:243
  82.6 11.8 %collective-permute-start.15 = (bf16[320,640]{1,0:T(8,128)(2,1)S(1)}, bf16[320,640]{1,0:T(8,128)(2,1)S(1)}, u32[]{:S(2)}, u32[]{:S(2)}) collective-permute-start(bf16[320,640]{1,0:T(8,128)(2,1)S(1)} %bitcast.29), channel_id=1, source_target_pairs={{0,32},{1,33},{2,34},{3,35},{4,36},{5,37},{6,38},{7,39},{8,40},{9,... | collective-permute-start | bytes 1228808 | tf_op jit(solution)/shard_map/density_gather/ppermute | solution.py:28
  82.6 13.0 %collective-permute-start.16 = (bf16[320,640]{1,0:T(8,128)(2,1)S(1)}, bf16[320,640]{1,0:T(8,128)(2,1)S(1)}, u32[]{:S(2)}, u32[]{:S(2)}) collective-permute-start(bf16[320,640]{1,0:T(8,128)(2,1)S(1)} %bitcast.30), channel_id=1, source_target_pairs={{0,96},{1,97},{2,98},{3,99},{4,100},{5,101},{6,102},{7,103},{8,104... | collective-permute-start | bytes 1228808 | tf_op jit(solution)/shard_map/density_gather/ppermute | solution.py:28
  89.8 11.4 %collective-permute-start.13 = (f32[80,1280]{1,0:T(8,128)S(1)}, f32[80,1280]{1,0:T(8,128)S(1)}, u32[]{:S(2)}, u32[]{:S(2)}) collective-permute-start(f32[80,1280]{1,0:T(8,128)S(1)} %get-tuple-element.127), channel_id=1, source_target_pairs={{0,8},{1,9},{2,10},{3,11},{4,12},{5,13},{6,14},{7,15},{8,0},{9,1},... | collective-permute-start | bytes 1228808 | tf_op jit(solution)/shard_map/mixed_sum/ppermute | solution.py:28
  91.4 12.3 %collective-permute-start.14 = (f32[80,1280]{1,0:T(8,128)S(1)}, f32[80,1280]{1,0:T(8,128)S(1)}, u32[]{:S(2)}, u32[]{:S(2)}) collective-permute-start(f32[80,1280]{1,0:T(8,128)S(1)} %get-tuple-element.126), channel_id=1, source_target_pairs={{0,24},{1,25},{2,26},{3,27},{4,28},{5,29},{6,30},{7,31},{8,16},{9,... | collective-permute-start | bytes 1228808 | tf_op jit(solution)/shard_map/mixed_sum/ppermute | solution.py:28
  104.0 20.2 %collective-permute-start.19 = (f32[160,1280]{1,0:T(8,128)S(1)}, f32[160,1280]{1,0:T(8,128)S(1)}, u32[]{:S(2)}, u32[]{:S(2)}) collective-permute-start(f32[160,1280]{1,0:T(8,128)S(1)} %pad_maximum_fusion.4), channel_id=1, source_target_pairs={{0,24},{1,25},{2,26},{3,27},{4,28},{5,29},{6,30},{7,31},{8,16},{9,... | collective-permute-start | bytes 2457608 | tf_op jit(solution)/shard_map/mixed_sum/ppermute | solution.py:28
  107.2 19.0 %collective-permute-start.17 = (f32[160,1280]{1,0:T(8,128)}, f32[160,1280]{1,0:T(8,128)}, u32[]{:S(2)}, u32[]{:S(2)}) collective-permute-start(f32[160,1280]{1,0:T(8,128)} %pad_maximum_fusion.3), channel_id=1, source_target_pairs={{0,8},{1,9},{2,10},{3,11},{4,12},{5,13},{6,14},{7,15},{8,0},{9,1},... | collective-permute-start | bytes 2457608 | tf_op jit(solution)/shard_map/mixed_sum/ppermute | solution.py:28
  107.2 19.0 %collective-permute-start.23 = (f32[160,1280]{1,0:T(8,128)S(1)}, f32[160,1280]{1,0:T(8,128)}, u32[]{:S(2)}, u32[]{:S(2)}) collective-permute-start(f32[160,1280]{1,0:T(8,128)S(1)} %get-tuple-element.107), channel_id=1, source_target_pairs={{0,2},{1,3},{2,0},{3,1},{4,6},{5,7},{6,4},{7,5},{8,10},{9,11},{10,... | collective-permute-start | bytes 2457608 | tf_op jit(solution)/shard_map/mixed_sum/ppermute | solution.py:28
  108.4 8.5 %collective-permute-start.21 = (bf16[160,640]{1,0:T(8,128)(2,1)S(1)}, bf16[160,640]{1,0:T(8,128)(2,1)S(1)}, u32[]{:S(2)}, u32[]{:S(2)}) collective-permute-start(bf16[160,640]{1,0:T(8,128)(2,1)S(1)} %slice.75), channel_id=1, source_target_pairs={{0,96},{1,97},{2,98},{3,99},{4,100},{5,101},{6,102},{7,103},{8,104... | collective-permute-start | bytes 614408 | tf_op jit(solution)/shard_map/density_gather/ppermute | solution.py:28
  126.1 15.1 %collective-permute-start.22 = (bf16[1280,640]{1,0:T(8,128)(2,1)}, bf16[1280,640]{1,0:T(8,128)(2,1)S(1)}, u32[]{:S(2)}, u32[]{:S(2)}) collective-permute-start(bf16[1280,640]{1,0:T(8,128)(2,1)} %density_rows.1.mine_ref), channel_id=1, source_target_pairs={{0,2},{1,3},{2,0},{3,1},{4,6},{5,7},{6,4},{7,5},{8,10},{9,11},{10,... | collective-permute-start | bytes 4915208 | tf_op jit(solution)/shard_map/mixed_gather/ppermute | solution.py:28
  127.9 13.2 %collective-permute-start.24 = (bf16[160,1280]{1,0:T(8,128)(2,1)S(1)}, bf16[160,1280]{1,0:T(8,128)(2,1)S(1)}, u32[]{:S(2)}, u32[]{:S(2)}) collective-permute-start(bf16[160,1280]{1,0:T(8,128)(2,1)S(1)} %fusion.10.refs_0_), channel_id=1, source_target_pairs={{0,24},{1,25},{2,26},{3,27},{4,28},{5,29},{6,30},{7,31},{8,16},{9,... | collective-permute-start | bytes 1228808 | tf_op jit(solution)/shard_map/mixed_gather/ppermute | solution.py:28
  129.1 12.0 %collective-permute-start.25 = (bf16[160,1280]{1,0:T(8,128)(2,1)S(1)}, bf16[160,1280]{1,0:T(8,128)(2,1)S(1)}, u32[]{:S(2)}, u32[]{:S(2)}) collective-permute-start(bf16[160,1280]{1,0:T(8,128)(2,1)S(1)} %fusion.10.refs_0_), channel_id=1, source_target_pairs={{0,8},{1,9},{2,10},{3,11},{4,12},{5,13},{6,14},{7,15},{8,0},{9,1},... | collective-permute-start | bytes 1228808 | tf_op jit(solution)/shard_map/mixed_gather/ppermute | solution.py:28
  141.2 13.7 %collective-permute-start.27 = (bf16[80,1280]{1,0:T(8,128)(2,1)S(1)}, bf16[80,1280]{1,0:T(8,128)(2,1)S(1)}, u32[]{:S(2)}, u32[]{:S(2)}) collective-permute-start(bf16[80,1280]{1,0:T(8,128)(2,1)S(1)} %slice.94), channel_id=1, source_target_pairs={{0,8},{1,9},{2,10},{3,11},{4,12},{5,13},{6,14},{7,15},{8,0},{9,1},... | collective-permute-start | bytes 614408 | tf_op jit(solution)/shard_map/mixed_gather/ppermute | solution.py:28
  148.6 13.3 %collective-permute-start.26 = (bf16[2,3,40,640]{3,2,1,0:T(8,128)(2,1)}, bf16[2,3,40,640]{3,2,1,0:T(8,128)(2,1)S(1)}, u32[]{:S(2)}, u32[]{:S(2)}) collective-permute-start(bf16[2,3,40,640]{3,2,1,0:T(8,128)(2,1)} %get-tuple-element.89), channel_id=1, source_target_pairs={{0,0},{1,1},{2,6},{3,7},{4,4},{5,5},{6,2},{7,3},{8,8},{9,9},{10,14... | collective-permute-start | bytes 921608 | tf_op jit(solution)/shard_map/second_product/ppermute | solution.py:42
  150.2 18.0 %collective-permute-start.29 = (bf16[2,3,40,640]{3,2,1,0:T(8,128)(2,1)}, bf16[2,3,40,640]{3,2,1,0:T(8,128)(2,1)S(1)}, u32[]{:S(2)}, u32[]{:S(2)}) collective-permute-start(bf16[2,3,40,640]{3,2,1,0:T(8,128)(2,1)} %get-tuple-element.93), channel_id=1, source_target_pairs={{0,2},{1,3},{2,4},{3,5},{4,6},{5,7},{6,0},{7,1},{8,10},{9,11},{10,... | collective-permute-start | bytes 921608 | tf_op jit(solution)/shard_map/second_product/ppermute | solution.py:42
  152.7 17.6 %collective-permute-start.30 = (bf16[2,3,40,640]{3,2,1,0:T(8,128)(2,1)}, bf16[2,3,40,640]{3,2,1,0:T(8,128)(2,1)S(1)}, u32[]{:S(2)}, u32[]{:S(2)}) collective-permute-start(bf16[2,3,40,640]{3,2,1,0:T(8,128)(2,1)} %get-tuple-element.94), channel_id=1, source_target_pairs={{0,1},{1,0},{2,7},{3,6},{4,5},{5,4},{6,3},{7,2},{8,9},{9,8},{10,15... | collective-permute-start | bytes 921608 | tf_op jit(solution)/shard_map/second_product/ppermute | solution.py:42
  153.4 8.5 %collective-permute-start.28 = (bf16[80,1280]{1,0:T(8,128)(2,1)S(1)}, bf16[80,1280]{1,0:T(8,128)(2,1)S(1)}, u32[]{:S(2)}, u32[]{:S(2)}) collective-permute-start(bf16[80,1280]{1,0:T(8,128)(2,1)S(1)} %slice.95), channel_id=1, source_target_pairs={{0,24},{1,25},{2,26},{3,27},{4,28},{5,29},{6,30},{7,31},{8,16},{9,... | collective-permute-start | bytes 614408 | tf_op jit(solution)/shard_map/mixed_gather/ppermute | solution.py:28
  154.9 16.8 %collective-permute-start.31 = (bf16[2,3,40,640]{3,2,1,0:T(8,128)(2,1)}, bf16[2,3,40,640]{3,2,1,0:T(8,128)(2,1)S(1)}, u32[]{:S(2)}, u32[]{:S(2)}) collective-permute-start(bf16[2,3,40,640]{3,2,1,0:T(8,128)(2,1)} %get-tuple-element.95), channel_id=1, source_target_pairs={{0,3},{1,2},{2,5},{3,4},{4,7},{5,6},{6,1},{7,0},{8,11},{9,10},{10,... | collective-permute-start | bytes 921608 | tf_op jit(solution)/shard_map/second_product/ppermute | solution.py:42
  180.4 21.9 %all-to-all-start.2 = ((bf16[32,40,160]{2,1,0:T(8,128)(2,1)}), bf16[32,40,160]{2,1,0:T(8,128)(2,1)S(1)}, u32[]{:S(2)}, u32[]{:S(2)}) async-start(bf16[32,40,160]{2,1,0:T(8,128)(2,1)} %get-tuple-element.106), calls=%async_computation.2 | async-start | bytes 1310720 | tf_op jit(solution)/shard_map/transposed/all_to_all | solution.py:328
  186.8 8.2 %collective-permute-start.36 = (f32[40,1280]{1,0:T(8,128)}, f32[40,1280]{1,0:T(8,128)S(1)}, u32[]{:S(2)}, u32[]{:S(2)}) collective-permute-start(f32[40,1280]{1,0:T(8,128)} %get-tuple-element.103), channel_id=1, source_target_pairs={{0,8},{1,9},{2,10},{3,11},{4,12},{5,13},{6,14},{7,15},{8,0},{9,1},... | collective-permute-start | bytes 614408 | tf_op jit(solution)/shard_map/direct/ppermute | solution.py:28
  186.9 12.8 %collective-permute-start.37 = (f32[40,1280]{1,0:T(8,128)}, f32[40,1280]{1,0:T(8,128)S(1)}, u32[]{:S(2)}, u32[]{:S(2)}) collective-permute-start(f32[40,1280]{1,0:T(8,128)} %get-tuple-element.104), channel_id=1, source_target_pairs={{0,16},{1,17},{2,18},{3,19},{4,20},{5,21},{6,22},{7,23},{8,24},{9,... | collective-permute-start | bytes 614408 | tf_op jit(solution)/shard_map/direct/ppermute | solution.py:28
  189.9 12.4 %collective-permute-start.38 = (f32[40,1280]{1,0:T(8,128)}, f32[40,1280]{1,0:T(8,128)S(1)}, u32[]{:S(2)}, u32[]{:S(2)}) collective-permute-start(f32[40,1280]{1,0:T(8,128)} %get-tuple-element.105), channel_id=1, source_target_pairs={{0,24},{1,25},{2,26},{3,27},{4,28},{5,29},{6,30},{7,31},{8,16},{9,... | collective-permute-start | bytes 614408 | tf_op jit(solution)/shard_map/direct/ppermute | solution.py:28
  (41 other events, 266.4 us)

commit v8 on v7

--- a/solution.py
+++ b/solution.py
@@ -125,16 +125,14 @@
 
 
 def second_kernel(at_ref, mine_ref, other_ref, *refs):
-    rows, outs, whole = refs[:-5], refs[-5:-1], refs[-1]
+    rows, outs, stack, whole = refs[:-6], refs[-6:-2], refs[-2], refs[-1]
     core, xh = at_ref[3], at_ref[4]
+    first = 0
+    for ref in rows:
+        stack[first : first + ref.shape[0]] = ref[...]
+        first += ref.shape[0]
     for side, right in enumerate((mine_ref, other_ref)):
-        first = 0
-        for ref in rows:
-            count = ref.shape[0] // 80
-            whole[side, first : first + count] = dot(ref[...], right[...]).reshape(
-                count, 2, 40, 640
-            )
-            first += count
+        whole[side] = dot(stack[...], right[...]).reshape(first // 80, 2, 40, 640)
     for i, out in enumerate(outs):
         r, t = i // 2, i % 2
         for side in range(2):
@@ -294,8 +292,8 @@
 
     with jax.named_scope("second_product"):
 
-        def scatter(count, *rows):
-            cut = local_call(
+        def pieces_of(count, *rows):
+            return local_call(
                 second_kernel,
                 "second_product",
                 [shape(bf16, 2, count, 40, 640)] * 4,
@@ -303,17 +301,24 @@
                 dmine,
                 dother,
                 *rows,
-                scratch=[pltpu.VMEM((2, count * 2, 2, 40, 640), f32)],
+                scratch=[
+                    pltpu.VMEM((count * 160, 1280), bf16),
+                    pltpu.VMEM((2, count * 2, 2, 40, 640), f32),
+                ],
             )
+
+        def scatter(cut):
             turns = [(r, t) for r in range(2) for t in range(2)]
             return [
                 remap(piece, lambda a, b, c, d, e: (a, b, c ^ d, d ^ t, e ^ r))
                 for piece, (r, t) in zip(cut, turns)
             ]
 
-        many = scatter(3, mixed, one, three)
+        cut = list(pieces_of(3, mixed, one, three))
+        cut[3], two = lax.optimization_barrier((cut[3], two))
+        many = scatter(cut)
         many[0], two = lax.optimization_barrier((many[0], two))
-        last = scatter(1, *two)
+        last = scatter(pieces_of(1, *two))
         turned, *rows = local_call(
             spread_kernel,
             "spread",

time: 208 us -> 206 us (level)
  waiting for transfers between devices: 87.5 us -> 80.6 us
  starting transfers between devices: 64.1 us -> 70.1 us
    ppermute x31, waiting for transfers between devices: 82.4 us -> 76 us  [flip(): return lax.ppermute(value, AXES, pairs)]
    ppermute x8, starting transfers between devices: 10.4 us -> 15.5 us  [remap(): return lax.ppermute(value, AXES, pairs)]
    unnamed x62 -> x60, local copies, waits for them, and re-layouts: 8.17 us -> 7.27 us
  transfers between devices with their start and end apart: 42 -> 42, of which waited for: 24 -> 22; matrix products, arithmetic and copies ran while one was open for 6% -> 7% of each run, Pallas kernels for 8% -> 8%
where the time goes in v8:
time: 206 us; the launch traced here: 205 us
  waiting for transfers between devices  80.6 us (39%)
  starting transfers between devices  70.1 us (34%)
  Pallas kernels  25.9 us (13%)
  other arithmetic  12.1 us (6%)
  local copies, waits for them, and re-layouts  10.6 us (5%)
  matrix products  5.35 us (3%)
    ppermute x31, waiting for transfers between devices, flip(): return lax.ppermute(value, AXES, pairs)  76 us
    ppermute x31, starting transfers between devices, flip(): return lax.ppermute(value, AXES, pairs)  38.4 us
    pallas_call x8, Pallas kernels, local_call(): pl.pallas_call(kernel, out_shape=outs, in_specs=[SMEM] + [VMEM] * len(ope...  25.9 us
    ppermute x8, starting transfers between devices, remap(): return lax.ppermute(value, AXES, pairs)  15.5 us
    unnamed x60, local copies, waits for them, and re-layouts  7.27 us
    all_to_all x1, starting transfers between devices, shards(): lax.all_to_all(turned, ('z', 'xl', 'core', 'xh'), split_axis=0, concat_ax...  6.79 us
    select_n x2, other arithmetic, shards(): mine = [jnp.where(core == 0, lefts[0, r], lefts[1, r]) for r in range(2)]  4.92 us
    all_to_all x1, starting transfers between devices, shards(): lax.all_to_all(parts, ('xl', 'core', 'xh'), split_axis=0, concat_axis=0,...  4.92 us
  transfers between devices with their start and end apart: 42, of which 22 were waited for; matrix products, arithmetic and copies ran while one was open for 7% of the time, Pallas kernels for 8%

profile of v8, /device:TPU:2, one launch (start us, length us, event | category | flops | bytes accessed | tf_op | source)
XLA Modules:
  0.0 205.0 jit_solution(9283657159269920679)
XLA Ops:
  1.9 2.7 %right_columns.1 = bf16[8,160,320]{2,1,0:T(8,128)(2,1)} custom-call(s32[5]{0:T(128)} %stack.38.at_ref, bf16[160,1280]{1,0:T(8,128)(2,1)} %first_ref.1, bf16[160,1280]{1,0:T(8,128)(2,1)} %second_ref.1), custom_call_target="tpu_custom_call" | custom-call | tf_op jit(solution)/shard_map/right_columns/right_columns/pallas_call | solution.py:58
  5.4 2.6 %left_columns.1 = (bf16[160,640]{1,0:T(8,128)(2,1)}, bf16[160,640]{1,0:T(8,128)(2,1)}, bf16[160,640]{1,0:T(8,128)(2,1)}, bf16[160,640]{1,0:T(8,128)(2,1)}) custom-call(s32[5]{0:T(128)} %stack.38.at_ref, bf16[160,1280]{1,0:T(8,128)(2,1)} %first_ref.2, bf16[160,1280]{1,0:T(8,128)(2,1)} %second_ref.2, bf16[160,1280]{1,0:T(8,128)(2,1)} %copy-done.13), custom_call_target="tpu_custom_call" | custom-call | tf_op jit(solution)/shard_map/left_columns/left_columns/pallas_call | solution.py:58
  8.0 4.9 %all-to-all-start = ((bf16[8,160,320]{2,1,0:T(8,128)(2,1)}), bf16[8,160,320]{2,1,0:T(8,128)(2,1)S(1)}, u32[]{:S(2)}, u32[]{:S(2)}) async-start(bf16[8,160,320]{2,1,0:T(8,128)(2,1)} %right_columns.1), calls=%async_computation | async-start | bytes 1966080 | tf_op jit(solution)/shard_map/right_gather/all_to_all | solution.py:222
  14.5 2.9 %collective-permute-start.2 = (bf16[160,640]{1,0:T(8,128)(2,1)}, bf16[160,640]{1,0:T(8,128)(2,1)S(1)}, u32[]{:S(2)}, u32[]{:S(2)}) collective-permute-start(bf16[160,640]{1,0:T(8,128)(2,1)} %get-tuple-element.68), channel_id=1, source_target_pairs={{0,16},{1,17},{2,18},{3,19},{4,20},{5,21},{6,22},{7,23},{8,24},{9,... | collective-permute-start | bytes 614408 | tf_op jit(solution)/shard_map/left_columns/ppermute | solution.py:28
  21.1 6.1 %collective-permute-done.2 = bf16[160,640]{1,0:T(8,128)(2,1)S(1)} collective-permute-done((bf16[160,640]{1,0:T(8,128)(2,1)}, bf16[160,640]{1,0:T(8,128)(2,1)S(1)}, u32[]{:S(2)}, u32[]{:S(2)}) %collective-permute-start.2) | collective-permute-done | bytes 204832 | tf_op jit(solution)/shard_map/left_columns/ppermute | solution.py:28
  27.2 2.6 %collective-permute-done.3 = bf16[160,640]{1,0:T(8,128)(2,1)S(1)} collective-permute-done((bf16[160,640]{1,0:T(8,128)(2,1)}, bf16[160,640]{1,0:T(8,128)(2,1)S(1)}, u32[]{:S(2)}, u32[]{:S(2)}) %collective-permute-start.3) | collective-permute-done | bytes 204832 | tf_op jit(solution)/shard_map/left_columns/ppermute | solution.py:28
  36.1 4.0 %collective-permute-start.10 = (bf16[320,1280]{1,0:T(8,128)(2,1)S(1)}, bf16[320,1280]{1,0:T(8,128)(2,1)S(1)}, u32[]{:S(2)}, u32[]{:S(2)}) collective-permute-start(bf16[320,1280]{1,0:T(8,128)(2,1)S(1)} %reshape.58), channel_id=1, source_target_pairs={{0,96},{1,97},{2,98},{3,99},{4,100},{5,101},{6,102},{7,103},{8,104... | collective-permute-start | bytes 2457608 | tf_op jit(solution)/shard_map/right_gather/ppermute | solution.py:28
  40.1 13.7 %collective-permute-done.5 = bf16[640,640]{1,0:T(8,128)(2,1)} collective-permute-done((bf16[640,640]{1,0:T(8,128)(2,1)S(1)}, bf16[640,640]{1,0:T(8,128)(2,1)}, u32[]{:S(2)}, u32[]{:S(2)}) %collective-permute-start.5) | collective-permute-done | bytes 819232 | tf_op jit(solution)/shard_map/left_gather/ppermute | solution.py:28
  53.9 3.9 %collective-permute-start.9 = (bf16[320,1280]{1,0:T(8,128)(2,1)S(1)}, bf16[320,1280]{1,0:T(8,128)(2,1)}, u32[]{:S(2)}, u32[]{:S(2)}) collective-permute-start(bf16[320,1280]{1,0:T(8,128)(2,1)S(1)} %reshape.58), channel_id=1, source_target_pairs={{0,64},{1,65},{2,66},{3,67},{4,68},{5,69},{6,70},{7,71},{8,72},{9,... | collective-permute-start | bytes 2457608 | tf_op jit(solution)/shard_map/right_gather/ppermute | solution.py:28
  59.7 4.5 %all-to-all-start.1 = ((bf16[4,80,640]{2,1,0:T(8,128)(2,1)}), bf16[4,80,640]{2,1,0:T(8,128)(2,1)S(1)}, u32[]{:S(2)}, u32[]{:S(2)}) async-start(bf16[4,80,640]{2,1,0:T(8,128)(2,1)} %density_columns.1), calls=%async_computation.1 | async-start | bytes 819200 | tf_op jit(solution)/shard_map/density_columns/all_to_all | solution.py:241
  64.1 2.5 %broadcast_select_fusion.3 = (bf16[640,640]{1,0:T(8,128)(2,1)}, bf16[640,640]{1,0:T(8,128)(2,1)}) fusion(bf16[640,640]{1,0:T(8,128)(2,1)S(1)} %pad_maximum_fusion.2, bf16[640,640]{1,0:T(8,128)(2,1)} %collective-permute-done.5, pred[]{:T(512)S(6)} %eq.8), kind=kLoop, calls=%fused_computation.28 | loop fusion | flops 819200 | bytes 3276801 | tf_op jit(solution)/shard_map/first_product/jit(_where)/select_n | solution.py:255
  66.6 3.3 %collective-permute-done.6 = bf16[640,640]{1,0:T(8,128)(2,1)} collective-permute-done((bf16[640,640]{1,0:T(8,128)(2,1)S(1)}, bf16[640,640]{1,0:T(8,128)(2,1)}, u32[]{:S(2)}, u32[]{:S(2)}) %collective-permute-start.6) | collective-permute-done | bytes 819232 | tf_op jit(solution)/shard_map/left_gather/ppermute | solution.py:28
  71.3 2.4 %broadcast_select_fusion.2 = (bf16[640,640]{1,0:T(8,128)(2,1)S(1)}, bf16[640,640]{1,0:T(8,128)(2,1)}) fusion(bf16[640,640]{1,0:T(8,128)(2,1)} %collective-permute-done.6, bf16[640,640]{1,0:T(8,128)(2,1)} %collective-permute-done.7, pred[]{:T(512)S(6)} %eq.8), kind=kLoop, calls=%fused_computation.27 | loop fusion | flops 819200 | bytes 3276801 | tf_op jit(solution)/shard_map/first_product/jit(_where)/select_n | solution.py:255
  73.8 2.4 %collective-permute-done.9 = bf16[320,1280]{1,0:T(8,128)(2,1)} collective-permute-done((bf16[320,1280]{1,0:T(8,128)(2,1)S(1)}, bf16[320,1280]{1,0:T(8,128)(2,1)}, u32[]{:S(2)}, u32[]{:S(2)}) %collective-permute-start.9) | collective-permute-done | bytes 819232 | tf_op jit(solution)/shard_map/right_gather/ppermute | solution.py:28
  82.7 3.1 %collective-permute-start.16 = (bf16[320,640]{1,0:T(8,128)(2,1)S(1)}, bf16[320,640]{1,0:T(8,128)(2,1)S(1)}, u32[]{:S(2)}, u32[]{:S(2)}) collective-permute-start(bf16[320,640]{1,0:T(8,128)(2,1)S(1)} %bitcast.30), channel_id=1, source_target_pairs={{0,96},{1,97},{2,98},{3,99},{4,100},{5,101},{6,102},{7,103},{8,104... | collective-permute-start | bytes 1228808 | tf_op jit(solution)/shard_map/density_gather/ppermute | solution.py:28
  95.7 5.5 %collective-permute-done.13 = f32[80,1280]{1,0:T(8,128)S(1)} collective-permute-done((f32[80,1280]{1,0:T(8,128)S(1)}, f32[80,1280]{1,0:T(8,128)S(1)}, u32[]{:S(2)}, u32[]{:S(2)}) %collective-permute-start.13) | collective-permute-done | bytes 409632 | tf_op jit(solution)/shard_map/mixed_sum/ppermute | solution.py:28
  101.2 2.5 %collective-permute-done.14 = f32[80,1280]{1,0:T(8,128)S(1)} collective-permute-done((f32[80,1280]{1,0:T(8,128)S(1)}, f32[80,1280]{1,0:T(8,128)S(1)}, u32[]{:S(2)}, u32[]{:S(2)}) %collective-permute-start.14) | collective-permute-done | bytes 409632 | tf_op jit(solution)/shard_map/mixed_sum/ppermute | solution.py:28
  109.4 5.3 %collective-permute-done.20.upper_ref = bf16[160,640]{1,0:T(8,128)(2,1)S(1)} collective-permute-done((bf16[160,640]{1,0:T(8,128)(2,1)S(1)}, bf16[160,640]{1,0:T(8,128)(2,1)S(1)}, u32[]{:S(2)}, u32[]{:S(2)}) %collective-permute-start.20) | collective-permute-done | bytes 204832 | tf_op jit(solution)/shard_map/density_gather/ppermute | solution.py:28
  117.7 2.7 %density_rows.1.mine_ref = bf16[1280,640]{1,0:T(8,128)(2,1)} custom-call(s32[5]{0:T(128)} %stack.38.at_ref, bf16[320,640]{1,0:T(8,128)(2,1)} %bitcast.31, bf16[320,640]{1,0:T(8,128)(2,1)} %copy-done.8, bf16[160,640]{1,0:T(8,128)(2,1)} %copy-done.23, bf16[160,640]{1,0:T(8,128)(2,1)} %copy-done.24, bf16[320,640]{1,0:T(8,128)(2,1)} %copy-done.9), custom_call_target="tpu_custom_call" | custom-call | tf_op jit(solution)/shard_map/density_rows/density_rows/pallas_call | solution.py:58
  120.4 3.8 %collective-permute-done.19 = f32[160,1280]{1,0:T(8,128)S(1)} collective-permute-done((f32[160,1280]{1,0:T(8,128)S(1)}, f32[160,1280]{1,0:T(8,128)S(1)}, u32[]{:S(2)}, u32[]{:S(2)}) %collective-permute-start.19) | collective-permute-done | bytes 819232 | tf_op jit(solution)/shard_map/mixed_sum/ppermute | solution.py:28
  129.1 12.0 %collective-permute-done.24.refs_2_ = bf16[160,1280]{1,0:T(8,128)(2,1)S(1)} collective-permute-done((bf16[160,1280]{1,0:T(8,128)(2,1)S(1)}, bf16[160,1280]{1,0:T(8,128)(2,1)S(1)}, u32[]{:S(2)}, u32[]{:S(2)}) %collective-permute-start.24) | collective-permute-done | bytes 409632 | tf_op jit(solution)/shard_map/mixed_gather/ppermute | solution.py:28
  144.4 5.4 %second_product.2 = (bf16[2,3,40,640]{3,2,1,0:T(8,128)(2,1)}, bf16[2,3,40,640]{3,2,1,0:T(8,128)(2,1)}, bf16[2,3,40,640]{3,2,1,0:T(8,128)(2,1)}, bf16[2,3,40,640]{3,2,1,0:T(8,128)(2,1)}) custom-call(s32[5]{0:T(128)} %stack.38.at_ref, bf16[1280,640]{1,0:T(8,128)(2,1)} %density_rows.1.mine_ref, bf16[1280,640]{1,0:T(8,128)(2,1)} %copy-done, ...), custom_call_target="tpu_custom_call" | custom-call | tf_op jit(solution)/shard_map/second_product/second_product/pallas_call | solution.py:58
  153.7 2.8 %collective-permute-start.30 = (bf16[2,3,40,640]{3,2,1,0:T(8,128)(2,1)}, bf16[2,3,40,640]{3,2,1,0:T(8,128)(2,1)S(1)}, u32[]{:S(2)}, u32[]{:S(2)}) collective-permute-start(bf16[2,3,40,640]{3,2,1,0:T(8,128)(2,1)} %get-tuple-element.100), channel_id=1, source_target_pairs={{0,1},{1,0},{2,7},{3,6},{4,5},{5,4},{6,3},{7,2},{8,9},{9,8},{10,15... | collective-permute-start | bytes 921608 | tf_op jit(solution)/shard_map/second_product/ppermute | solution.py:42
  156.5 3.7 %second_product.3 = (bf16[2,1,40,640]{3,2,1,0:T(8,128)(2,1)}, bf16[2,1,40,640]{3,2,1,0:T(8,128)(2,1)}, bf16[2,1,40,640]{3,2,1,0:T(8,128)(2,1)}, bf16[2,1,40,640]{3,2,1,0:T(8,128)(2,1)}) custom-call(s32[5]{0:T(128)} %stack.38.at_ref, bf16[1280,640]{1,0:T(8,128)(2,1)} %density_rows.1.mine_ref, bf16[1280,640]{1,0:T(8,128)(2,1)} %copy-done, ...), custom_call_target="tpu_custom_call" | custom-call | tf_op jit(solution)/shard_map/second_product/second_product/pallas_call | solution.py:58
  161.8 5.5 %collective-permute-start.33 = (bf16[2,1,40,640]{3,2,1,0:T(8,128)(2,1)}, bf16[2,1,40,640]{3,2,1,0:T(8,128)(2,1)S(1)}, u32[]{:S(2)}, u32[]{:S(2)}) collective-permute-start(bf16[2,1,40,640]{3,2,1,0:T(8,128)(2,1)} %get-tuple-element.105), channel_id=1, source_target_pairs={{0,2},{1,3},{2,4},{3,5},{4,6},{5,7},{6,0},{7,1},{8,10},{9,11},{10,... | collective-permute-start | bytes 307208 | tf_op jit(solution)/shard_map/second_product/ppermute | solution.py:42
  170.7 2.9 %collective-permute-done.34.refs_6_ = bf16[2,1,40,640]{3,2,1,0:T(8,128)(2,1)S(1)} collective-permute-done((bf16[2,1,40,640]{3,2,1,0:T(8,128)(2,1)}, bf16[2,1,40,640]{3,2,1,0:T(8,128)(2,1)S(1)}, u32[]{:S(2)}, u32[]{:S(2)}) %collective-permute-start.34) | collective-permute-done | bytes 102432 | tf_op jit(solution)/shard_map/second_product/ppermute | solution.py:42
  174.9 2.9 %spread.1 = (bf16[32,40,160]{2,1,0:T(8,128)(2,1)}, f32[40,1280]{1,0:T(8,128)}, f32[40,1280]{1,0:T(8,128)}, f32[40,1280]{1,0:T(8,128)}, f32[40,1280]{1,0:T(8,128)}) custom-call(s32[5]{0:T(128)} %stack.38.at_ref, bf16[2,3,40,640]{3,2,1,0:T(8,128)(2,1)} %copy-done.14, bf16[2,3,40,640]{3,2,1,0:T(8,128)(2,1)} %copy-done.16, bf16[2,3,40,640]{3,2,1,0:T(8,128)(2,1)} %copy-done.17, ...), custom_call_target="tpu_custom_call" | custom-call | tf_op jit(solution)/shard_map/second_product/spread/pallas_call | solution.py:58
  177.8 6.8 %all-to-all-start.2 = ((bf16[32,40,160]{2,1,0:T(8,128)(2,1)}), bf16[32,40,160]{2,1,0:T(8,128)(2,1)S(1)}, u32[]{:S(2)}, u32[]{:S(2)}) async-start(bf16[32,40,160]{2,1,0:T(8,128)(2,1)} %get-tuple-element.112), calls=%async_computation.2 | async-start | bytes 1310720 | tf_op jit(solution)/shard_map/transposed/all_to_all | solution.py:333
  190.2 2.6 %collective-permute-done.36.d1 = f32[40,1280]{1,0:T(8,128)S(1)} collective-permute-done((f32[40,1280]{1,0:T(8,128)}, f32[40,1280]{1,0:T(8,128)S(1)}, u32[]{:S(2)}, u32[]{:S(2)}) %collective-permute-start.36) | collective-permute-done | bytes 204832 | tf_op jit(solution)/shard_map/direct/ppermute | solution.py:28
  192.9 4.8 %collective-permute-done.37.d2 = f32[40,1280]{1,0:T(8,128)S(1)} collective-permute-done((f32[40,1280]{1,0:T(8,128)}, f32[40,1280]{1,0:T(8,128)S(1)}, u32[]{:S(2)}, u32[]{:S(2)}) %collective-permute-start.37) | collective-permute-done | bytes 204832 | tf_op jit(solution)/shard_map/direct/ppermute | solution.py:28
  197.6 2.6 %collective-permute-done.38.d3 = f32[40,1280]{1,0:T(8,128)S(1)} collective-permute-done((f32[40,1280]{1,0:T(8,128)}, f32[40,1280]{1,0:T(8,128)S(1)}, u32[]{:S(2)}, u32[]{:S(2)}) %collective-permute-start.38) | collective-permute-done | bytes 204832 | tf_op jit(solution)/shard_map/direct/ppermute | solution.py:28
  201.2 3.9 %finish.1 = f32[40,5120]{1,0:T(8,128)} custom-call(s32[5]{0:T(128)} %stack.38.at_ref, f32[40,1280]{1,0:T(8,128)} %get-tuple-element.108.d0, f32[40,1280]{1,0:T(8,128)} %copy-done.18, f32[40,1280]{1,0:T(8,128)} %copy-done.19, f32[40,1280]{1,0:T(8,128)} %copy-done.20, bf16[32,40,160]{2,1,0:T(8,128)(2,1)} %copy-done.3, f32[40,40]{1,0:T(8,128)} %fusion.11.kept_ref), custom_call_target="tpu_custom_call" | custom-call | tf_op jit(solution)/shard_map/finish/pallas_call | solution.py:58
  (145 shorter events, 67.0 us)
Async XLA Ops:
  8.0 23.2 %all-to-all-start = ((bf16[8,160,320]{2,1,0:T(8,128)(2,1)}), bf16[8,160,320]{2,1,0:T(8,128)(2,1)S(1)}, u32[]{:S(2)}, u32[]{:S(2)}) async-start(bf16[8,160,320]{2,1,0:T(8,128)(2,1)} %right_columns.1), calls=%async_computation | async-start | bytes 1966080 | tf_op jit(solution)/shard_map/right_gather/all_to_all | solution.py:222
  14.5 12.7 %collective-permute-start.2 = (bf16[160,640]{1,0:T(8,128)(2,1)}, bf16[160,640]{1,0:T(8,128)(2,1)S(1)}, u32[]{:S(2)}, u32[]{:S(2)}) collective-permute-start(bf16[160,640]{1,0:T(8,128)(2,1)} %get-tuple-element.68), channel_id=1, source_target_pairs={{0,16},{1,17},{2,18},{3,19},{4,20},{5,21},{6,22},{7,23},{8,24},{9,... | collective-permute-start | bytes 614408 | tf_op jit(solution)/shard_map/left_columns/ppermute | solution.py:28
  17.4 12.4 %collective-permute-start.3 = (bf16[160,640]{1,0:T(8,128)(2,1)}, bf16[160,640]{1,0:T(8,128)(2,1)S(1)}, u32[]{:S(2)}, u32[]{:S(2)}) collective-permute-start(bf16[160,640]{1,0:T(8,128)(2,1)} %get-tuple-element.69), channel_id=1, source_target_pairs={{0,24},{1,25},{2,26},{3,27},{4,28},{5,29},{6,30},{7,31},{8,16},{9,... | collective-permute-start | bytes 614408 | tf_op jit(solution)/shard_map/left_columns/ppermute | solution.py:28
  18.4 12.9 %collective-permute-start.4 = (bf16[80,1280]{1,0:T(8,128)(2,1)S(1)}, bf16[80,1280]{1,0:T(8,128)(2,1)S(1)}, u32[]{:S(2)}, u32[]{:S(2)}) collective-permute-start(bf16[80,1280]{1,0:T(8,128)(2,1)S(1)} %bitcast.34), channel_id=1, source_target_pairs={{0,1},{1,0},{2,3},{3,2},{4,5},{5,4},{6,7},{7,6},{8,9},{9,8},{10,11... | collective-permute-start | bytes 614408 | tf_op jit(solution)/shard_map/density_turn/ppermute | solution.py:28
  32.5 21.3 %collective-permute-start.5 = (bf16[640,640]{1,0:T(8,128)(2,1)S(1)}, bf16[640,640]{1,0:T(8,128)(2,1)}, u32[]{:S(2)}, u32[]{:S(2)}) collective-permute-start(bf16[640,640]{1,0:T(8,128)(2,1)S(1)} %pad_maximum_fusion.2), channel_id=1, source_target_pairs={{0,4},{1,5},{2,6},{3,7},{4,0},{5,1},{6,2},{7,3},{8,12},{9,13},{10,... | collective-permute-start | bytes 2457608 | tf_op jit(solution)/shard_map/left_gather/ppermute | solution.py:28
  34.1 35.9 %collective-permute-start.6 = (bf16[640,640]{1,0:T(8,128)(2,1)S(1)}, bf16[640,640]{1,0:T(8,128)(2,1)}, u32[]{:S(2)}, u32[]{:S(2)}) collective-permute-start(bf16[640,640]{1,0:T(8,128)(2,1)S(1)} %pad_maximum_fusion.2), channel_id=1, source_target_pairs={{0,1},{1,0},{2,3},{3,2},{4,5},{5,4},{6,7},{7,6},{8,9},{9,8},{10,11... | collective-permute-start | bytes 2457608 | tf_op jit(solution)/shard_map/left_gather/ppermute | solution.py:28
  35.1 36.2 %collective-permute-start.7 = (bf16[640,640]{1,0:T(8,128)(2,1)S(1)}, bf16[640,640]{1,0:T(8,128)(2,1)}, u32[]{:S(2)}, u32[]{:S(2)}) collective-permute-start(bf16[640,640]{1,0:T(8,128)(2,1)S(1)} %pad_maximum_fusion.2), channel_id=1, source_target_pairs={{0,5},{1,4},{2,7},{3,6},{4,1},{5,0},{6,3},{7,2},{8,13},{9,12},{10,... | collective-permute-start | bytes 2457608 | tf_op jit(solution)/shard_map/left_gather/ppermute | solution.py:28
  36.1 37.7 %collective-permute-start.10 = (bf16[320,1280]{1,0:T(8,128)(2,1)S(1)}, bf16[320,1280]{1,0:T(8,128)(2,1)S(1)}, u32[]{:S(2)}, u32[]{:S(2)}) collective-permute-start(bf16[320,1280]{1,0:T(8,128)(2,1)S(1)} %reshape.58), channel_id=1, source_target_pairs={{0,96},{1,97},{2,98},{3,99},{4,100},{5,101},{6,102},{7,103},{8,104... | collective-permute-start | bytes 2457608 | tf_op jit(solution)/shard_map/right_gather/ppermute | solution.py:28
  40.1 33.6 %collective-permute-start.8 = (bf16[320,1280]{1,0:T(8,128)(2,1)S(1)}, bf16[320,1280]{1,0:T(8,128)(2,1)}, u32[]{:S(2)}, u32[]{:S(2)}) collective-permute-start(bf16[320,1280]{1,0:T(8,128)(2,1)S(1)} %reshape.58), channel_id=1, source_target_pairs={{0,32},{1,33},{2,34},{3,35},{4,36},{5,37},{6,38},{7,39},{8,40},{9,... | collective-permute-start | bytes 2457608 | tf_op jit(solution)/shard_map/right_gather/ppermute | solution.py:28
  53.9 22.3 %collective-permute-start.9 = (bf16[320,1280]{1,0:T(8,128)(2,1)S(1)}, bf16[320,1280]{1,0:T(8,128)(2,1)}, u32[]{:S(2)}, u32[]{:S(2)}) collective-permute-start(bf16[320,1280]{1,0:T(8,128)(2,1)S(1)} %reshape.58), channel_id=1, source_target_pairs={{0,64},{1,65},{2,66},{3,67},{4,68},{5,69},{6,70},{7,71},{8,72},{9,... | collective-permute-start | bytes 2457608 | tf_op jit(solution)/shard_map/right_gather/ppermute | solution.py:28
  59.7 16.5 %all-to-all-start.1 = ((bf16[4,80,640]{2,1,0:T(8,128)(2,1)}), bf16[4,80,640]{2,1,0:T(8,128)(2,1)S(1)}, u32[]{:S(2)}, u32[]{:S(2)}) async-start(bf16[4,80,640]{2,1,0:T(8,128)(2,1)} %density_columns.1), calls=%async_computation.1 | async-start | bytes 819200 | tf_op jit(solution)/shard_map/density_columns/all_to_all | solution.py:241
  82.7 11.8 %collective-permute-start.15 = (bf16[320,640]{1,0:T(8,128)(2,1)S(1)}, bf16[320,640]{1,0:T(8,128)(2,1)S(1)}, u32[]{:S(2)}, u32[]{:S(2)}) collective-permute-start(bf16[320,640]{1,0:T(8,128)(2,1)S(1)} %bitcast.29), channel_id=1, source_target_pairs={{0,32},{1,33},{2,34},{3,35},{4,36},{5,37},{6,38},{7,39},{8,40},{9,... | collective-permute-start | bytes 1228808 | tf_op jit(solution)/shard_map/density_gather/ppermute | solution.py:28
  82.7 13.0 %collective-permute-start.16 = (bf16[320,640]{1,0:T(8,128)(2,1)S(1)}, bf16[320,640]{1,0:T(8,128)(2,1)S(1)}, u32[]{:S(2)}, u32[]{:S(2)}) collective-permute-start(bf16[320,640]{1,0:T(8,128)(2,1)S(1)} %bitcast.30), channel_id=1, source_target_pairs={{0,96},{1,97},{2,98},{3,99},{4,100},{5,101},{6,102},{7,103},{8,104... | collective-permute-start | bytes 1228808 | tf_op jit(solution)/shard_map/density_gather/ppermute | solution.py:28
  89.8 11.4 %collective-permute-start.13 = (f32[80,1280]{1,0:T(8,128)S(1)}, f32[80,1280]{1,0:T(8,128)S(1)}, u32[]{:S(2)}, u32[]{:S(2)}) collective-permute-start(f32[80,1280]{1,0:T(8,128)S(1)} %get-tuple-element.133), channel_id=1, source_target_pairs={{0,8},{1,9},{2,10},{3,11},{4,12},{5,13},{6,14},{7,15},{8,0},{9,1},... | collective-permute-start | bytes 1228808 | tf_op jit(solution)/shard_map/mixed_sum/ppermute | solution.py:28
  91.4 12.3 %collective-permute-start.14 = (f32[80,1280]{1,0:T(8,128)S(1)}, f32[80,1280]{1,0:T(8,128)S(1)}, u32[]{:S(2)}, u32[]{:S(2)}) collective-permute-start(f32[80,1280]{1,0:T(8,128)S(1)} %get-tuple-element.132), channel_id=1, source_target_pairs={{0,24},{1,25},{2,26},{3,27},{4,28},{5,29},{6,30},{7,31},{8,16},{9,... | collective-permute-start | bytes 1228808 | tf_op jit(solution)/shard_map/mixed_sum/ppermute | solution.py:28
  104.0 20.2 %collective-permute-start.19 = (f32[160,1280]{1,0:T(8,128)S(1)}, f32[160,1280]{1,0:T(8,128)S(1)}, u32[]{:S(2)}, u32[]{:S(2)}) collective-permute-start(f32[160,1280]{1,0:T(8,128)S(1)} %pad_maximum_fusion.4), channel_id=1, source_target_pairs={{0,24},{1,25},{2,26},{3,27},{4,28},{5,29},{6,30},{7,31},{8,16},{9,... | collective-permute-start | bytes 2457608 | tf_op jit(solution)/shard_map/mixed_sum/ppermute | solution.py:28
  107.2 19.0 %collective-permute-start.17 = (f32[160,1280]{1,0:T(8,128)}, f32[160,1280]{1,0:T(8,128)}, u32[]{:S(2)}, u32[]{:S(2)}) collective-permute-start(f32[160,1280]{1,0:T(8,128)} %pad_maximum_fusion.3), channel_id=1, source_target_pairs={{0,8},{1,9},{2,10},{3,11},{4,12},{5,13},{6,14},{7,15},{8,0},{9,1},... | collective-permute-start | bytes 2457608 | tf_op jit(solution)/shard_map/mixed_sum/ppermute | solution.py:28
  107.2 19.0 %collective-permute-start.23 = (f32[160,1280]{1,0:T(8,128)S(1)}, f32[160,1280]{1,0:T(8,128)}, u32[]{:S(2)}, u32[]{:S(2)}) collective-permute-start(f32[160,1280]{1,0:T(8,128)S(1)} %get-tuple-element.113), channel_id=1, source_target_pairs={{0,2},{1,3},{2,0},{3,1},{4,6},{5,7},{6,4},{7,5},{8,10},{9,11},{10,... | collective-permute-start | bytes 2457608 | tf_op jit(solution)/shard_map/mixed_sum/ppermute | solution.py:28
  108.5 8.5 %collective-permute-start.21 = (bf16[160,640]{1,0:T(8,128)(2,1)S(1)}, bf16[160,640]{1,0:T(8,128)(2,1)S(1)}, u32[]{:S(2)}, u32[]{:S(2)}) collective-permute-start(bf16[160,640]{1,0:T(8,128)(2,1)S(1)} %slice.75), channel_id=1, source_target_pairs={{0,96},{1,97},{2,98},{3,99},{4,100},{5,101},{6,102},{7,103},{8,104... | collective-permute-start | bytes 614408 | tf_op jit(solution)/shard_map/density_gather/ppermute | solution.py:28
  126.2 17.1 %collective-permute-start.22 = (bf16[1280,640]{1,0:T(8,128)(2,1)}, bf16[1280,640]{1,0:T(8,128)(2,1)S(1)}, u32[]{:S(2)}, u32[]{:S(2)}) collective-permute-start(bf16[1280,640]{1,0:T(8,128)(2,1)} %density_rows.1.mine_ref), channel_id=1, source_target_pairs={{0,2},{1,3},{2,0},{3,1},{4,6},{5,7},{6,4},{7,5},{8,10},{9,11},{10,... | collective-permute-start | bytes 4915208 | tf_op jit(solution)/shard_map/mixed_gather/ppermute | solution.py:28
  128.0 13.2 %collective-permute-start.24 = (bf16[160,1280]{1,0:T(8,128)(2,1)S(1)}, bf16[160,1280]{1,0:T(8,128)(2,1)S(1)}, u32[]{:S(2)}, u32[]{:S(2)}) collective-permute-start(bf16[160,1280]{1,0:T(8,128)(2,1)S(1)} %fusion.10.refs_0_), channel_id=1, source_target_pairs={{0,24},{1,25},{2,26},{3,27},{4,28},{5,29},{6,30},{7,31},{8,16},{9,... | collective-permute-start | bytes 1228808 | tf_op jit(solution)/shard_map/mixed_gather/ppermute | solution.py:28
  129.1 12.1 %collective-permute-start.25 = (bf16[160,1280]{1,0:T(8,128)(2,1)S(1)}, bf16[160,1280]{1,0:T(8,128)(2,1)S(1)}, u32[]{:S(2)}, u32[]{:S(2)}) collective-permute-start(bf16[160,1280]{1,0:T(8,128)(2,1)S(1)} %fusion.10.refs_0_), channel_id=1, source_target_pairs={{0,8},{1,9},{2,10},{3,11},{4,12},{5,13},{6,14},{7,15},{8,0},{9,1},... | collective-permute-start | bytes 1228808 | tf_op jit(solution)/shard_map/mixed_gather/ppermute | solution.py:28
  141.2 10.3 %collective-permute-start.27 = (bf16[80,1280]{1,0:T(8,128)(2,1)S(1)}, bf16[80,1280]{1,0:T(8,128)(2,1)S(1)}, u32[]{:S(2)}, u32[]{:S(2)}) collective-permute-start(bf16[80,1280]{1,0:T(8,128)(2,1)S(1)} %slice.94), channel_id=1, source_target_pairs={{0,8},{1,9},{2,10},{3,11},{4,12},{5,13},{6,14},{7,15},{8,0},{9,1},... | collective-permute-start | bytes 614408 | tf_op jit(solution)/shard_map/mixed_gather/ppermute | solution.py:28
  141.3 10.2 %collective-permute-start.28 = (bf16[80,1280]{1,0:T(8,128)(2,1)S(1)}, bf16[80,1280]{1,0:T(8,128)(2,1)}, u32[]{:S(2)}, u32[]{:S(2)}) collective-permute-start(bf16[80,1280]{1,0:T(8,128)(2,1)S(1)} %slice.95), channel_id=1, source_target_pairs={{0,24},{1,25},{2,26},{3,27},{4,28},{5,29},{6,30},{7,31},{8,16},{9,... | collective-permute-start | bytes 614408 | tf_op jit(solution)/shard_map/mixed_gather/ppermute | solution.py:28
  151.5 15.8 %collective-permute-start.31 = (bf16[2,3,40,640]{3,2,1,0:T(8,128)(2,1)}, bf16[2,3,40,640]{3,2,1,0:T(8,128)(2,1)S(1)}, u32[]{:S(2)}, u32[]{:S(2)}) collective-permute-start(bf16[2,3,40,640]{3,2,1,0:T(8,128)(2,1)} %get-tuple-element.101), channel_id=1, source_target_pairs={{0,3},{1,2},{2,5},{3,4},{4,7},{5,6},{6,1},{7,0},{8,11},{9,10},{10,... | collective-permute-start | bytes 921608 | tf_op jit(solution)/shard_map/second_product/ppermute | solution.py:42
  153.7 14.2 %collective-permute-start.29 = (bf16[2,3,40,640]{3,2,1,0:T(8,128)(2,1)}, bf16[2,3,40,640]{3,2,1,0:T(8,128)(2,1)S(1)}, u32[]{:S(2)}, u32[]{:S(2)}) collective-permute-start(bf16[2,3,40,640]{3,2,1,0:T(8,128)(2,1)} %get-tuple-element.99), channel_id=1, source_target_pairs={{0,2},{1,3},{2,4},{3,5},{4,6},{5,7},{6,0},{7,1},{8,10},{9,11},{10,... | collective-permute-start | bytes 921608 | tf_op jit(solution)/shard_map/second_product/ppermute | solution.py:42
  153.7 15.4 %collective-permute-start.30 = (bf16[2,3,40,640]{3,2,1,0:T(8,128)(2,1)}, bf16[2,3,40,640]{3,2,1,0:T(8,128)(2,1)S(1)}, u32[]{:S(2)}, u32[]{:S(2)}) collective-permute-start(bf16[2,3,40,640]{3,2,1,0:T(8,128)(2,1)} %get-tuple-element.100), channel_id=1, source_target_pairs={{0,1},{1,0},{2,7},{3,6},{4,5},{5,4},{6,3},{7,2},{8,9},{9,8},{10,15... | collective-permute-start | bytes 921608 | tf_op jit(solution)/shard_map/second_product/ppermute | solution.py:42
  160.2 8.9 %collective-permute-start.32 = (bf16[2,1,40,640]{3,2,1,0:T(8,128)(2,1)}, bf16[2,1,40,640]{3,2,1,0:T(8,128)(2,1)S(1)}, u32[]{:S(2)}, u32[]{:S(2)}) collective-permute-start(bf16[2,1,40,640]{3,2,1,0:T(8,128)(2,1)} %get-tuple-element.104), channel_id=1, source_target_pairs={{0,0},{1,1},{2,6},{3,7},{4,4},{5,5},{6,2},{7,3},{8,8},{9,9},{10,14... | collective-permute-start | bytes 307208 | tf_op jit(solution)/shard_map/second_product/ppermute | solution.py:42
  161.8 9.0 %collective-permute-start.33 = (bf16[2,1,40,640]{3,2,1,0:T(8,128)(2,1)}, bf16[2,1,40,640]{3,2,1,0:T(8,128)(2,1)S(1)}, u32[]{:S(2)}, u32[]{:S(2)}) collective-permute-start(bf16[2,1,40,640]{3,2,1,0:T(8,128)(2,1)} %get-tuple-element.105), channel_id=1, source_target_pairs={{0,2},{1,3},{2,4},{3,5},{4,6},{5,7},{6,0},{7,1},{8,10},{9,11},{10,... | collective-permute-start | bytes 307208 | tf_op jit(solution)/shard_map/second_product/ppermute | solution.py:42
  177.8 22.4 %all-to-all-start.2 = ((bf16[32,40,160]{2,1,0:T(8,128)(2,1)}), bf16[32,40,160]{2,1,0:T(8,128)(2,1)S(1)}, u32[]{:S(2)}, u32[]{:S(2)}) async-start(bf16[32,40,160]{2,1,0:T(8,128)(2,1)} %get-tuple-element.112), calls=%async_computation.2 | async-start | bytes 1310720 | tf_op jit(solution)/shard_map/transposed/all_to_all | solution.py:333
  185.6 12.1 %collective-permute-start.37 = (f32[40,1280]{1,0:T(8,128)}, f32[40,1280]{1,0:T(8,128)S(1)}, u32[]{:S(2)}, u32[]{:S(2)}) collective-permute-start(f32[40,1280]{1,0:T(8,128)} %get-tuple-element.110), channel_id=1, source_target_pairs={{0,16},{1,17},{2,18},{3,19},{4,20},{5,21},{6,22},{7,23},{8,24},{9,... | collective-permute-start | bytes 614408 | tf_op jit(solution)/shard_map/direct/ppermute | solution.py:28
  187.8 12.4 %collective-permute-start.38 = (f32[40,1280]{1,0:T(8,128)}, f32[40,1280]{1,0:T(8,128)S(1)}, u32[]{:S(2)}, u32[]{:S(2)}) collective-permute-start(f32[40,1280]{1,0:T(8,128)} %get-tuple-element.111), channel_id=1, source_target_pairs={{0,24},{1,25},{2,26},{3,27},{4,28},{5,29},{6,30},{7,31},{8,16},{9,... | collective-permute-start | bytes 614408 | tf_op jit(solution)/shard_map/direct/ppermute | solution.py:28
  (40 other events, 267.8 us)

commit v9 on v8

--- a/solution.py
+++ b/solution.py
@@ -124,20 +124,13 @@
     place(3, 0, 320, three_ref)
 
 
-def second_kernel(at_ref, mine_ref, other_ref, *refs):
-    rows, outs, stack, whole = refs[:-6], refs[-6:-2], refs[-2], refs[-1]
+def cut_kernel(at_ref, mine_ref, other_ref, *outs):
     core, xh = at_ref[3], at_ref[4]
-    first = 0
-    for ref in rows:
-        stack[first : first + ref.shape[0]] = ref[...]
-        first += ref.shape[0]
-    for side, right in enumerate((mine_ref, other_ref)):
-        whole[side] = dot(stack[...], right[...]).reshape(first // 80, 2, 40, 640)
     for i, out in enumerate(outs):
         r, t = i // 2, i % 2
-        for side in range(2):
+        for side, ref in enumerate((mine_ref, other_ref)):
             for slot in range(out.shape[1]):
-                out[side, slot] = whole[side, slot * 2 + (core ^ t), xh ^ r].astype(bf16)
+                out[side, slot] = ref[slot * 2 + (core ^ t), xh ^ r]
 
 
 def spread_kernel(at_ref, *refs):
@@ -216,7 +209,18 @@
             left_kernel, "left_columns", [shape(bf16, 160, 640)] * 4, coords, dens_resp, density, came
         )
         parts, pieces = lax.optimization_barrier((parts, pieces))
-        left = jnp.concatenate([pieces[0]] + [flip(pieces[q], y=q) for q in (1, 2, 3)])
+        slots = [pieces[0]] + [flip(pieces[q], y=q) for q in (1, 2, 3)]
+        left = jnp.concatenate(
+            (
+                slots[2][:80],
+                slots[1][:80],
+                slots[2][80:],
+                slots[3][80:],
+                slots[3][:80],
+                slots[1][80:],
+                slots[0],
+            )
+        )
         left, other = lax.optimization_barrier((left, other))
     with jax.named_scope("right_gather"):
         rounds = lax.all_to_all(
@@ -256,11 +260,9 @@
         theirs = dot(jnp.concatenate(theirs, axis=1), rsel).reshape(4, 160, 1280)
         mine = dot(jnp.concatenate(mine, axis=1), rsel).reshape(4, 160, 1280)
     with jax.named_scope("mixed_sum"):
-        both = [None] * 4
-        for q in (2, 1, 3, 0):
-            both[q] = mine[q] + flip(theirs[q], core=1)
-        upper = flip(both[2][:80], y=1)
-        lower = flip(both[2][80:], y=3)
+        both = [mine[g] + flip(theirs[g], core=1) for g in range(4)]
+        upper = flip(both[0], y=1)
+        lower = flip(both[1], y=3)
 
     with jax.named_scope("density_gather"):
         done = flip(dslots, z=1)
@@ -269,9 +271,10 @@
         dtwo = (flip(dthree[:160], z=1), flip(done[160:], z=3))
 
     with jax.named_scope("mixed_sum"):
-        third = jnp.concatenate((both[3][:80] + upper, both[3][80:]))
-        first = jnp.concatenate((both[1][:80], both[1][80:] + lower))
-        sums = [flip(first, y=1), flip(third, y=3)]
+        sums = [
+            flip(both[2][:80] + upper[:80], y=3),
+            flip(both[2][80:] + lower[:80], y=1),
+        ]
 
     with jax.named_scope("density_rows"):
         dmine = local_call(
@@ -280,7 +283,7 @@
 
     with jax.named_scope("mixed_sum"):
         sums, dmine = lax.optimization_barrier((sums, dmine))
-        total = both[0] + sums[0] + sums[1]
+        total = both[3] + jnp.concatenate((upper[80:] + sums[0], lower[80:] + sums[1]))
         mixed = total.astype(bf16)
 
     with jax.named_scope("mixed_gather"):
@@ -293,18 +296,13 @@
     with jax.named_scope("second_product"):
 
         def pieces_of(count, *rows):
+            rows = jnp.concatenate(rows)
+            parts = [
+                dot(rows, right).astype(bf16).reshape(count * 2, 2, 40, 640)
+                for right in (dmine, dother)
+            ]
             return local_call(
-                second_kernel,
-                "second_product",
-                [shape(bf16, 2, count, 40, 640)] * 4,
-                coords,
-                dmine,
-                dother,
-                *rows,
-                scratch=[
-                    pltpu.VMEM((count * 160, 1280), bf16),
-                    pltpu.VMEM((2, count * 2, 2, 40, 640), f32),
-                ],
+                cut_kernel, "cut", [shape(bf16, 2, count, 40, 640)] * 4, coords, *parts
             )
 
         def scatter(cut):
@@ -315,7 +313,7 @@
             ]
 
         cut = list(pieces_of(3, mixed, one, three))
-        cut[3], two = lax.optimization_barrier((cut[3], two))
+        cut, two = lax.optimization_barrier((cut, two))
         many = scatter(cut)
         many[0], two = lax.optimization_barrier((many[0], two))
         last = scatter(pieces_of(1, *two))

time: 206 us -> 214 us (1.039)
  matrix products: 5.35 us -> 11.6 us
  waiting for transfers between devices: 80.6 us -> 86.1 us
  Pallas kernels: 25.9 us -> 21.2 us
  local copies, waits for them, and re-layouts: 10.6 us -> 13.2 us
    all_to_all x1, waiting for transfers between devices: 0.01 us -> 9.82 us  [shards(): lax.all_to_all(parts, ('xl', 'core', 'xh'), split_axis=0, concat_axis=0,...]
    ppermute x31, waiting for transfers between devices: 76 us -> 67.8 us  [flip(): return lax.ppermute(value, AXES, pairs)]
    dot_general x2 -> x6, matrix products: 4.56 us -> 10.8 us  [dot(): return jnp.dot(a, b, preferred_element_type=f32)]
    pallas_call x8, Pallas kernels: 25.9 us -> 21.2 us  [local_call(): pl.pallas_call(kernel, out_shape=outs, in_specs=[SMEM] + [VMEM] * len(ope...]
    ppermute x8, waiting for transfers between devices: 4.57 us -> 8.45 us  [remap(): return lax.ppermute(value, AXES, pairs)]
    unnamed x60 -> x61, local copies, waits for them, and re-layouts: 7.27 us -> 6.8 us
  transfers between devices with their start and end apart: 42 -> 42, of which waited for: 22 -> 21; matrix products, arithmetic and copies ran while one was open for 7% -> 10% of each run, Pallas kernels for 8% -> 5%
where the time goes in v9:
time: 214 us; the launch traced here: 213 us
  waiting for transfers between devices  86.1 us (40%)
  starting transfers between devices  69.8 us (33%)
  Pallas kernels  21.2 us (10%)
  local copies, waits for them, and re-layouts  13.2 us (6%)
  matrix products  11.6 us (5%)
  other arithmetic  11.2 us (5%)
    ppermute x31, waiting for transfers between devices, flip(): return lax.ppermute(value, AXES, pairs)  67.8 us
    ppermute x31, starting transfers between devices, flip(): return lax.ppermute(value, AXES, pairs)  40.4 us
    pallas_call x8, Pallas kernels, local_call(): pl.pallas_call(kernel, out_shape=outs, in_specs=[SMEM] + [VMEM] * len(ope...  21.2 us
    ppermute x8, starting transfers between devices, remap(): return lax.ppermute(value, AXES, pairs)  13.4 us
    dot_general x6, matrix products, dot(): return jnp.dot(a, b, preferred_element_type=f32)  10.8 us
    all_to_all x1, waiting for transfers between devices, shards(): lax.all_to_all(parts, ('xl', 'core', 'xh'), split_axis=0, concat_axis=0,...  9.82 us
    ppermute x8, waiting for transfers between devices, remap(): return lax.ppermute(value, AXES, pairs)  8.45 us
    unnamed x61, local copies, waits for them, and re-layouts  6.8 us
  transfers between devices with their start and end apart: 42, of which 21 were waited for; matrix products, arithmetic and copies ran while one was open for 10% of the time, Pallas kernels for 5%

profile of v9, /device:TPU:2, one launch (start us, length us, event | category | flops | bytes accessed | tf_op | source)
XLA Modules:
  0.0 213.5 jit_solution(8483381629795436108)
XLA Ops:
  1.8 2.8 %right_columns.1 = bf16[8,160,320]{2,1,0:T(8,128)(2,1)} custom-call(s32[5]{0:T(128)} %stack.38.at_ref, bf16[160,1280]{1,0:T(8,128)(2,1)} %first_ref.1, bf16[160,1280]{1,0:T(8,128)(2,1)} %second_ref.1), custom_call_target="tpu_custom_call" | custom-call | tf_op jit(solution)/shard_map/right_columns/right_columns/pallas_call | solution.py:58
  5.3 2.7 %left_columns.1 = (bf16[160,640]{1,0:T(8,128)(2,1)}, bf16[160,640]{1,0:T(8,128)(2,1)}, bf16[160,640]{1,0:T(8,128)(2,1)}, bf16[160,640]{1,0:T(8,128)(2,1)}) custom-call(s32[5]{0:T(128)} %stack.38.at_ref, bf16[160,1280]{1,0:T(8,128)(2,1)} %first_ref.2, bf16[160,1280]{1,0:T(8,128)(2,1)} %second_ref.2, bf16[160,1280]{1,0:T(8,128)(2,1)} %copy-done.14), custom_call_target="tpu_custom_call" | custom-call | tf_op jit(solution)/shard_map/left_columns/left_columns/pallas_call | solution.py:58
  8.0 3.2 %collective-permute-start.1 = (bf16[160,640]{1,0:T(8,128)(2,1)}, bf16[160,640]{1,0:T(8,128)(2,1)S(1)}, u32[]{:S(2)}, u32[]{:S(2)}) collective-permute-start(bf16[160,640]{1,0:T(8,128)(2,1)} %get-tuple-element.69), channel_id=1, source_target_pairs={{0,16},{1,17},{2,18},{3,19},{4,20},{5,21},{6,22},{7,23},{8,24},{9,... | collective-permute-start | bytes 614408 | tf_op jit(solution)/shard_map/left_columns/ppermute | solution.py:28
  15.1 4.9 %all-to-all-start = ((bf16[8,160,320]{2,1,0:T(8,128)(2,1)}), bf16[8,160,320]{2,1,0:T(8,128)(2,1)S(1)}, u32[]{:S(2)}, u32[]{:S(2)}) async-start(bf16[8,160,320]{2,1,0:T(8,128)(2,1)} %right_columns.1), calls=%async_computation | async-start | bytes 1966080 | tf_op jit(solution)/shard_map/right_gather/all_to_all | solution.py:226
  22.9 9.8 %all-to-all-done = bf16[8,160,320]{2,1,0:T(8,128)(2,1)S(1)} async-done(((bf16[8,160,320]{2,1,0:T(8,128)(2,1)}), bf16[8,160,320]{2,1,0:T(8,128)(2,1)S(1)}, u32[]{:S(2)}, u32[]{:S(2)}) %all-to-all-start) | async-done | bytes 819232 | tf_op jit(solution)/shard_map/right_gather/all_to_all | solution.py:226
  37.6 4.0 %collective-permute-start.10 = (bf16[320,1280]{1,0:T(8,128)(2,1)S(1)}, bf16[320,1280]{1,0:T(8,128)(2,1)}, u32[]{:S(2)}, u32[]{:S(2)}) collective-permute-start(bf16[320,1280]{1,0:T(8,128)(2,1)S(1)} %reshape.70), channel_id=1, source_target_pairs={{0,96},{1,97},{2,98},{3,99},{4,100},{5,101},{6,102},{7,103},{8,104... | collective-permute-start | bytes 2457608 | tf_op jit(solution)/shard_map/right_gather/ppermute | solution.py:28
  41.7 13.5 %collective-permute-done.5 = bf16[640,640]{1,0:T(8,128)(2,1)S(1)} collective-permute-done((bf16[640,640]{1,0:T(8,128)(2,1)S(1)}, bf16[640,640]{1,0:T(8,128)(2,1)S(1)}, u32[]{:S(2)}, u32[]{:S(2)}) %collective-permute-start.5) | collective-permute-done | bytes 819232 | tf_op jit(solution)/shard_map/left_gather/ppermute | solution.py:28
  56.1 3.9 %collective-permute-start.9 = (bf16[320,1280]{1,0:T(8,128)(2,1)S(1)}, bf16[320,1280]{1,0:T(8,128)(2,1)S(1)}, u32[]{:S(2)}, u32[]{:S(2)}) collective-permute-start(bf16[320,1280]{1,0:T(8,128)(2,1)S(1)} %reshape.70), channel_id=1, source_target_pairs={{0,64},{1,65},{2,66},{3,67},{4,68},{5,69},{6,70},{7,71},{8,72},{9,... | collective-permute-start | bytes 2457608 | tf_op jit(solution)/shard_map/right_gather/ppermute | solution.py:28
  61.9 4.3 %all-to-all-start.1 = ((bf16[4,80,640]{2,1,0:T(8,128)(2,1)}), bf16[4,80,640]{2,1,0:T(8,128)(2,1)S(1)}, u32[]{:S(2)}, u32[]{:S(2)}) async-start(bf16[4,80,640]{2,1,0:T(8,128)(2,1)} %density_columns.1), calls=%async_computation.1 | async-start | bytes 819200 | tf_op jit(solution)/shard_map/density_columns/all_to_all | solution.py:245
  66.2 2.5 %broadcast_select_fusion.3 = (bf16[640,640]{1,0:T(8,128)(2,1)}, bf16[640,640]{1,0:T(8,128)(2,1)}) fusion(bf16[640,640]{1,0:T(8,128)(2,1)S(1)} %constant_dynamic-update-slice_fusion, bf16[640,640]{1,0:T(8,128)(2,1)} %copy-done.9, pred[]{:T(512)S(6)} %eq.8), kind=kLoop, calls=%fused_computation.29 | loop fusion | flops 819200 | bytes 3276801 | tf_op jit(solution)/shard_map/first_product/jit(_where)/select_n | solution.py:259
  68.7 4.2 %collective-permute-done.6 = bf16[640,640]{1,0:T(8,128)(2,1)} collective-permute-done((bf16[640,640]{1,0:T(8,128)(2,1)S(1)}, bf16[640,640]{1,0:T(8,128)(2,1)}, u32[]{:S(2)}, u32[]{:S(2)}) %collective-permute-start.6) | collective-permute-done | bytes 819232 | tf_op jit(solution)/shard_map/left_gather/ppermute | solution.py:28
  74.2 2.4 %broadcast_select_fusion.2 = (bf16[640,640]{1,0:T(8,128)(2,1)S(1)}, bf16[640,640]{1,0:T(8,128)(2,1)}) fusion(bf16[640,640]{1,0:T(8,128)(2,1)} %collective-permute-done.6, bf16[640,640]{1,0:T(8,128)(2,1)} %collective-permute-done.7, pred[]{:T(512)S(6)} %eq.8), kind=kLoop, calls=%fused_computation.28 | loop fusion | flops 819200 | bytes 3276801 | tf_op jit(solution)/shard_map/first_product/jit(_where)/select_n | solution.py:259
  94.2 2.6 %collective-permute-start.17 = (bf16[320,640]{1,0:T(8,128)(2,1)S(1)}, bf16[320,640]{1,0:T(8,128)(2,1)S(1)}, u32[]{:S(2)}, u32[]{:S(2)}) collective-permute-start(bf16[320,640]{1,0:T(8,128)(2,1)S(1)} %bitcast.40), channel_id=1, source_target_pairs={{0,96},{1,97},{2,98},{3,99},{4,100},{5,101},{6,102},{7,103},{8,104... | collective-permute-start | bytes 1228808 | tf_op jit(solution)/shard_map/density_gather/ppermute | solution.py:28
  96.8 8.0 %collective-permute-done.16.one_ref = bf16[320,640]{1,0:T(8,128)(2,1)S(1)} collective-permute-done((bf16[320,640]{1,0:T(8,128)(2,1)S(1)}, bf16[320,640]{1,0:T(8,128)(2,1)S(1)}, u32[]{:S(2)}, u32[]{:S(2)}) %collective-permute-start.16) | collective-permute-done | bytes 409632 | tf_op jit(solution)/shard_map/density_gather/ppermute | solution.py:28
  106.1 4.5 %collective-permute-done.13 = f32[160,1280]{1,0:T(8,128)S(1)} collective-permute-done((f32[160,1280]{1,0:T(8,128)S(1)}, f32[160,1280]{1,0:T(8,128)S(1)}, u32[]{:S(2)}, u32[]{:S(2)}) %collective-permute-start.13) | collective-permute-done | bytes 819232 | tf_op jit(solution)/shard_map/mixed_sum/ppermute | solution.py:28
  110.6 2.3 %collective-permute-done.15 = f32[160,1280]{1,0:T(8,128)S(1)} collective-permute-done((f32[160,1280]{1,0:T(8,128)S(1)}, f32[160,1280]{1,0:T(8,128)S(1)}, u32[]{:S(2)}, u32[]{:S(2)}) %collective-permute-start.15) | collective-permute-done | bytes 819232 | tf_op jit(solution)/shard_map/mixed_sum/ppermute | solution.py:28
  116.5 2.7 %collective-permute-start.22 = (bf16[160,640]{1,0:T(8,128)(2,1)S(1)}, bf16[160,640]{1,0:T(8,128)(2,1)S(1)}, u32[]{:S(2)}, u32[]{:S(2)}) collective-permute-start(bf16[160,640]{1,0:T(8,128)(2,1)S(1)} %slice.100), channel_id=1, source_target_pairs={{0,96},{1,97},{2,98},{3,99},{4,100},{5,101},{6,102},{7,103},{8,104... | collective-permute-start | bytes 614408 | tf_op jit(solution)/shard_map/density_gather/ppermute | solution.py:28
  119.2 4.4 %collective-permute-done.21.upper_ref = bf16[160,640]{1,0:T(8,128)(2,1)S(1)} collective-permute-done((bf16[160,640]{1,0:T(8,128)(2,1)S(1)}, bf16[160,640]{1,0:T(8,128)(2,1)S(1)}, u32[]{:S(2)}, u32[]{:S(2)}) %collective-permute-start.21) | collective-permute-done | bytes 204832 | tf_op jit(solution)/shard_map/density_gather/ppermute | solution.py:28
  125.7 2.7 %density_rows.1 = bf16[1280,640]{1,0:T(8,128)(2,1)} custom-call(s32[5]{0:T(128)} %stack.38.at_ref, bf16[320,640]{1,0:T(8,128)(2,1)} %bitcast.41, bf16[320,640]{1,0:T(8,128)(2,1)} %copy-done.5, bf16[160,640]{1,0:T(8,128)(2,1)} %copy-done.20, bf16[160,640]{1,0:T(8,128)(2,1)} %copy-done.21, bf16[320,640]{1,0:T(8,128)(2,1)} %copy-done.6), custom_call_target="tpu_custom_call" | custom-call | tf_op jit(solution)/shard_map/density_rows/density_rows/pallas_call | solution.py:58
  134.8 10.6 %collective-permute-done.23 = bf16[160,1280]{1,0:T(8,128)(2,1)S(1)} collective-permute-done((bf16[160,1280]{1,0:T(8,128)(2,1)S(1)}, bf16[160,1280]{1,0:T(8,128)(2,1)S(1)}, u32[]{:S(2)}, u32[]{:S(2)}) %collective-permute-start.23) | collective-permute-done | bytes 409632 | tf_op jit(solution)/shard_map/mixed_gather/ppermute | solution.py:28
  153.2 2.4 %cut.2 = (bf16[2,3,40,640]{3,2,1,0:T(8,128)(2,1)}, bf16[2,3,40,640]{3,2,1,0:T(8,128)(2,1)}, bf16[2,3,40,640]{3,2,1,0:T(8,128)(2,1)}, bf16[2,3,40,640]{3,2,1,0:T(8,128)(2,1)}) custom-call(s32[5]{0:T(128)} %stack.38.at_ref, bf16[6,2,40,640]{3,2,1,0:T(8,128)(2,1)} %bitcast.46, bf16[6,2,40,640]{3,2,1,0:T(8,128)(2,1)} %bitcast.47), custom_call_target="tpu_custom_call" | custom-call | tf_op jit(solution)/shard_map/second_product/cut/pallas_call | solution.py:58
  155.6 3.8 %collective-permute-start.28 = (bf16[2,3,40,640]{3,2,1,0:T(8,128)(2,1)}, bf16[2,3,40,640]{3,2,1,0:T(8,128)(2,1)}, u32[]{:S(2)}, u32[]{:S(2)}) collective-permute-start(bf16[2,3,40,640]{3,2,1,0:T(8,128)(2,1)} %get-tuple-element.101), channel_id=1, source_target_pairs={{0,0},{1,1},{2,6},{3,7},{4,4},{5,5},{6,2},{7,3},{8,8},{9,9},{10,14... | collective-permute-start | bytes 921608 | tf_op jit(solution)/shard_map/second_product/ppermute | solution.py:42
  159.5 3.8 %collective-permute-start.30 = (bf16[2,3,40,640]{3,2,1,0:T(8,128)(2,1)}, bf16[2,3,40,640]{3,2,1,0:T(8,128)(2,1)}, u32[]{:S(2)}, u32[]{:S(2)}) collective-permute-start(bf16[2,3,40,640]{3,2,1,0:T(8,128)(2,1)} %get-tuple-element.106), channel_id=1, source_target_pairs={{0,1},{1,0},{2,7},{3,6},{4,5},{5,4},{6,3},{7,2},{8,9},{9,8},{10,15... | collective-permute-start | bytes 921608 | tf_op jit(solution)/shard_map/second_product/ppermute | solution.py:42
  174.2 5.3 %collective-permute-done.31.refs_3_ = bf16[2,3,40,640]{3,2,1,0:T(8,128)(2,1)} collective-permute-done((bf16[2,3,40,640]{3,2,1,0:T(8,128)(2,1)}, bf16[2,3,40,640]{3,2,1,0:T(8,128)(2,1)}, u32[]{:S(2)}, u32[]{:S(2)}) %collective-permute-start.31) | collective-permute-done | bytes 307232 | tf_op jit(solution)/shard_map/second_product/ppermute | solution.py:42
  179.6 3.1 %collective-permute-done.35.refs_7_ = bf16[2,1,40,640]{3,2,1,0:T(8,128)(2,1)S(1)} collective-permute-done((bf16[2,1,40,640]{3,2,1,0:T(8,128)(2,1)}, bf16[2,1,40,640]{3,2,1,0:T(8,128)(2,1)S(1)}, u32[]{:S(2)}, u32[]{:S(2)}) %collective-permute-start.35) | collective-permute-done | bytes 102432 | tf_op jit(solution)/shard_map/second_product/ppermute | solution.py:42
  183.3 2.9 %spread.1 = (bf16[32,40,160]{2,1,0:T(8,128)(2,1)}, f32[40,1280]{1,0:T(8,128)}, f32[40,1280]{1,0:T(8,128)}, f32[40,1280]{1,0:T(8,128)}, f32[40,1280]{1,0:T(8,128)}) custom-call(s32[5]{0:T(128)} %stack.38.at_ref, bf16[2,3,40,640]{3,2,1,0:T(8,128)(2,1)} %collective-permute-done.28.refs_0_, bf16[2,3,40,640]{3,2,1,0:T(8,128)(2,1)} %collective-permute-done.29.refs_1_, ...), custom_call_target="tpu_custom_call" | custom-call | tf_op jit(solution)/shard_map/second_product/spread/pallas_call | solution.py:58
  186.2 6.8 %all-to-all-start.2 = ((bf16[32,40,160]{2,1,0:T(8,128)(2,1)}), bf16[32,40,160]{2,1,0:T(8,128)(2,1)S(1)}, u32[]{:S(2)}, u32[]{:S(2)}) async-start(bf16[32,40,160]{2,1,0:T(8,128)(2,1)} %get-tuple-element.118), calls=%async_computation.2 | async-start | bytes 1310720 | tf_op jit(solution)/shard_map/transposed/all_to_all | solution.py:331
  193.2 3.0 %collective-permute-start.37 = (f32[40,1280]{1,0:T(8,128)}, f32[40,1280]{1,0:T(8,128)S(1)}, u32[]{:S(2)}, u32[]{:S(2)}) collective-permute-start(f32[40,1280]{1,0:T(8,128)} %get-tuple-element.116), channel_id=1, source_target_pairs={{0,16},{1,17},{2,18},{3,19},{4,20},{5,21},{6,22},{7,23},{8,24},{9,... | collective-permute-start | bytes 614408 | tf_op jit(solution)/shard_map/direct/ppermute | solution.py:28
  198.6 2.6 %collective-permute-done.36.d1 = f32[40,1280]{1,0:T(8,128)S(1)} collective-permute-done((f32[40,1280]{1,0:T(8,128)}, f32[40,1280]{1,0:T(8,128)S(1)}, u32[]{:S(2)}, u32[]{:S(2)}) %collective-permute-start.36) | collective-permute-done | bytes 204832 | tf_op jit(solution)/shard_map/direct/ppermute | solution.py:28
  201.3 4.8 %collective-permute-done.37.d2 = f32[40,1280]{1,0:T(8,128)S(1)} collective-permute-done((f32[40,1280]{1,0:T(8,128)}, f32[40,1280]{1,0:T(8,128)S(1)}, u32[]{:S(2)}, u32[]{:S(2)}) %collective-permute-start.37) | collective-permute-done | bytes 204832 | tf_op jit(solution)/shard_map/direct/ppermute | solution.py:28
  206.0 2.6 %collective-permute-done.38.d3 = f32[40,1280]{1,0:T(8,128)S(1)} collective-permute-done((f32[40,1280]{1,0:T(8,128)}, f32[40,1280]{1,0:T(8,128)S(1)}, u32[]{:S(2)}, u32[]{:S(2)}) %collective-permute-start.38) | collective-permute-done | bytes 204832 | tf_op jit(solution)/shard_map/direct/ppermute | solution.py:28
  209.6 3.9 %finish.1 = f32[40,5120]{1,0:T(8,128)} custom-call(s32[5]{0:T(128)} %stack.38.at_ref, f32[40,1280]{1,0:T(8,128)} %get-tuple-element.114.d0, f32[40,1280]{1,0:T(8,128)} %copy-done.15, f32[40,1280]{1,0:T(8,128)} %copy-done.16, f32[40,1280]{1,0:T(8,128)} %copy-done.17, bf16[32,40,160]{2,1,0:T(8,128)(2,1)} %copy-done.3, f32[40,40]{1,0:T(8,128)} %fusion.10.kept_ref), custom_call_target="tpu_custom_call" | custom-call | tf_op jit(solution)/shard_map/finish/pallas_call | solution.py:58
  (149 shorter events, 72.0 us)
Async XLA Ops:
  8.0 12.0 %collective-permute-start.1 = (bf16[160,640]{1,0:T(8,128)(2,1)}, bf16[160,640]{1,0:T(8,128)(2,1)S(1)}, u32[]{:S(2)}, u32[]{:S(2)}) collective-permute-start(bf16[160,640]{1,0:T(8,128)(2,1)} %get-tuple-element.69), channel_id=1, source_target_pairs={{0,16},{1,17},{2,18},{3,19},{4,20},{5,21},{6,22},{7,23},{8,24},{9,... | collective-permute-start | bytes 614408 | tf_op jit(solution)/shard_map/left_columns/ppermute | solution.py:28
  11.9 11.0 %collective-permute-start.4 = (bf16[80,1280]{1,0:T(8,128)(2,1)S(1)}, bf16[80,1280]{1,0:T(8,128)(2,1)S(1)}, u32[]{:S(2)}, u32[]{:S(2)}) collective-permute-start(bf16[80,1280]{1,0:T(8,128)(2,1)S(1)} %bitcast.48), channel_id=1, source_target_pairs={{0,1},{1,0},{2,3},{3,2},{4,5},{5,4},{6,7},{7,6},{8,9},{9,8},{10,11... | collective-permute-start | bytes 614408 | tf_op jit(solution)/shard_map/density_turn/ppermute | solution.py:28
  15.1 17.6 %all-to-all-start = ((bf16[8,160,320]{2,1,0:T(8,128)(2,1)}), bf16[8,160,320]{2,1,0:T(8,128)(2,1)S(1)}, u32[]{:S(2)}, u32[]{:S(2)}) async-start(bf16[8,160,320]{2,1,0:T(8,128)(2,1)} %right_columns.1), calls=%async_computation | async-start | bytes 1966080 | tf_op jit(solution)/shard_map/right_gather/all_to_all | solution.py:226
  34.0 21.1 %collective-permute-start.5 = (bf16[640,640]{1,0:T(8,128)(2,1)S(1)}, bf16[640,640]{1,0:T(8,128)(2,1)S(1)}, u32[]{:S(2)}, u32[]{:S(2)}) collective-permute-start(bf16[640,640]{1,0:T(8,128)(2,1)S(1)} %constant_dynamic-update-slice_fusion), channel_id=1, source_target_pairs={{0,4},{1,5},{2,6},{3,7},{4,0},{5,1},{6,2},{7,3},{8,12},{9,13},{10,... | collective-permute-start | bytes 2457608 | tf_op jit(solution)/shard_map/left_gather/ppermute | solution.py:28
  36.1 36.8 %collective-permute-start.6 = (bf16[640,640]{1,0:T(8,128)(2,1)S(1)}, bf16[640,640]{1,0:T(8,128)(2,1)}, u32[]{:S(2)}, u32[]{:S(2)}) collective-permute-start(bf16[640,640]{1,0:T(8,128)(2,1)S(1)} %constant_dynamic-update-slice_fusion), channel_id=1, source_target_pairs={{0,1},{1,0},{2,3},{3,2},{4,5},{5,4},{6,7},{7,6},{8,9},{9,8},{10,11... | collective-permute-start | bytes 2457608 | tf_op jit(solution)/shard_map/left_gather/ppermute | solution.py:28
  37.3 36.9 %collective-permute-start.7 = (bf16[640,640]{1,0:T(8,128)(2,1)S(1)}, bf16[640,640]{1,0:T(8,128)(2,1)}, u32[]{:S(2)}, u32[]{:S(2)}) collective-permute-start(bf16[640,640]{1,0:T(8,128)(2,1)S(1)} %constant_dynamic-update-slice_fusion), channel_id=1, source_target_pairs={{0,5},{1,4},{2,7},{3,6},{4,1},{5,0},{6,3},{7,2},{8,13},{9,12},{10,... | collective-permute-start | bytes 2457608 | tf_op jit(solution)/shard_map/left_gather/ppermute | solution.py:28
  37.6 39.0 %collective-permute-start.10 = (bf16[320,1280]{1,0:T(8,128)(2,1)S(1)}, bf16[320,1280]{1,0:T(8,128)(2,1)}, u32[]{:S(2)}, u32[]{:S(2)}) collective-permute-start(bf16[320,1280]{1,0:T(8,128)(2,1)S(1)} %reshape.70), channel_id=1, source_target_pairs={{0,96},{1,97},{2,98},{3,99},{4,100},{5,101},{6,102},{7,103},{8,104... | collective-permute-start | bytes 2457608 | tf_op jit(solution)/shard_map/right_gather/ppermute | solution.py:28
  41.7 35.0 %collective-permute-start.8 = (bf16[320,1280]{1,0:T(8,128)(2,1)S(1)}, bf16[320,1280]{1,0:T(8,128)(2,1)}, u32[]{:S(2)}, u32[]{:S(2)}) collective-permute-start(bf16[320,1280]{1,0:T(8,128)(2,1)S(1)} %reshape.70), channel_id=1, source_target_pairs={{0,32},{1,33},{2,34},{3,35},{4,36},{5,37},{6,38},{7,39},{8,40},{9,... | collective-permute-start | bytes 2457608 | tf_op jit(solution)/shard_map/right_gather/ppermute | solution.py:28
  56.1 22.3 %collective-permute-start.9 = (bf16[320,1280]{1,0:T(8,128)(2,1)S(1)}, bf16[320,1280]{1,0:T(8,128)(2,1)S(1)}, u32[]{:S(2)}, u32[]{:S(2)}) collective-permute-start(bf16[320,1280]{1,0:T(8,128)(2,1)S(1)} %reshape.70), channel_id=1, source_target_pairs={{0,64},{1,65},{2,66},{3,67},{4,68},{5,69},{6,70},{7,71},{8,72},{9,... | collective-permute-start | bytes 2457608 | tf_op jit(solution)/shard_map/right_gather/ppermute | solution.py:28
  61.9 16.5 %all-to-all-start.1 = ((bf16[4,80,640]{2,1,0:T(8,128)(2,1)}), bf16[4,80,640]{2,1,0:T(8,128)(2,1)S(1)}, u32[]{:S(2)}, u32[]{:S(2)}) async-start(bf16[4,80,640]{2,1,0:T(8,128)(2,1)} %density_columns.1), calls=%async_computation.1 | async-start | bytes 819200 | tf_op jit(solution)/shard_map/density_columns/all_to_all | solution.py:245
  90.0 20.5 %collective-permute-start.13 = (f32[160,1280]{1,0:T(8,128)S(1)}, f32[160,1280]{1,0:T(8,128)S(1)}, u32[]{:S(2)}, u32[]{:S(2)}) collective-permute-start(f32[160,1280]{1,0:T(8,128)S(1)} %get-tuple-element.125), channel_id=1, source_target_pairs={{0,8},{1,9},{2,10},{3,11},{4,12},{5,13},{6,14},{7,15},{8,0},{9,1},... | collective-permute-start | bytes 2457608 | tf_op jit(solution)/shard_map/mixed_sum/ppermute | solution.py:28
  91.7 21.2 %collective-permute-start.15 = (f32[160,1280]{1,0:T(8,128)S(1)}, f32[160,1280]{1,0:T(8,128)S(1)}, u32[]{:S(2)}, u32[]{:S(2)}) collective-permute-start(f32[160,1280]{1,0:T(8,128)S(1)} %get-tuple-element.123), channel_id=1, source_target_pairs={{0,24},{1,25},{2,26},{3,27},{4,28},{5,29},{6,30},{7,31},{8,16},{9,... | collective-permute-start | bytes 2457608 | tf_op jit(solution)/shard_map/mixed_sum/ppermute | solution.py:28
  93.9 10.9 %collective-permute-start.16 = (bf16[320,640]{1,0:T(8,128)(2,1)S(1)}, bf16[320,640]{1,0:T(8,128)(2,1)S(1)}, u32[]{:S(2)}, u32[]{:S(2)}) collective-permute-start(bf16[320,640]{1,0:T(8,128)(2,1)S(1)} %bitcast.39), channel_id=1, source_target_pairs={{0,32},{1,33},{2,34},{3,35},{4,36},{5,37},{6,38},{7,39},{8,40},{9,... | collective-permute-start | bytes 1228808 | tf_op jit(solution)/shard_map/density_gather/ppermute | solution.py:28
  94.2 11.9 %collective-permute-start.17 = (bf16[320,640]{1,0:T(8,128)(2,1)S(1)}, bf16[320,640]{1,0:T(8,128)(2,1)S(1)}, u32[]{:S(2)}, u32[]{:S(2)}) collective-permute-start(bf16[320,640]{1,0:T(8,128)(2,1)S(1)} %bitcast.40), channel_id=1, source_target_pairs={{0,96},{1,97},{2,98},{3,99},{4,100},{5,101},{6,102},{7,103},{8,104... | collective-permute-start | bytes 1228808 | tf_op jit(solution)/shard_map/density_gather/ppermute | solution.py:28
  113.8 14.6 %collective-permute-start.19 = (f32[80,1280]{1,0:T(8,128)S(1)}, f32[80,1280]{1,0:T(8,128)S(1)}, u32[]{:S(2)}, u32[]{:S(2)}) collective-permute-start(f32[80,1280]{1,0:T(8,128)S(1)} %get-tuple-element.135), channel_id=1, source_target_pairs={{0,24},{1,25},{2,26},{3,27},{4,28},{5,29},{6,30},{7,31},{8,16},{9,... | collective-permute-start | bytes 1228808 | tf_op jit(solution)/shard_map/mixed_sum/ppermute | solution.py:28
  116.0 13.2 %collective-permute-start.20 = (f32[80,1280]{1,0:T(8,128)S(1)}, f32[80,1280]{1,0:T(8,128)}, u32[]{:S(2)}, u32[]{:S(2)}) collective-permute-start(f32[80,1280]{1,0:T(8,128)S(1)} %get-tuple-element.134), channel_id=1, source_target_pairs={{0,8},{1,9},{2,10},{3,11},{4,12},{5,13},{6,14},{7,15},{8,0},{9,1},... | collective-permute-start | bytes 1228808 | tf_op jit(solution)/shard_map/mixed_sum/ppermute | solution.py:28
  116.0 14.7 %collective-permute-start.11 = (f32[160,1280]{1,0:T(8,128)}, f32[160,1280]{1,0:T(8,128)}, u32[]{:S(2)}, u32[]{:S(2)}) collective-permute-start(f32[160,1280]{1,0:T(8,128)} %get-tuple-element.119), channel_id=1, source_target_pairs={{0,2},{1,3},{2,0},{3,1},{4,6},{5,7},{6,4},{7,5},{8,10},{9,11},{10,... | collective-permute-start | bytes 2457608 | tf_op jit(solution)/shard_map/mixed_sum/ppermute | solution.py:28
  116.5 8.5 %collective-permute-start.22 = (bf16[160,640]{1,0:T(8,128)(2,1)S(1)}, bf16[160,640]{1,0:T(8,128)(2,1)S(1)}, u32[]{:S(2)}, u32[]{:S(2)}) collective-permute-start(bf16[160,640]{1,0:T(8,128)(2,1)S(1)} %slice.100), channel_id=1, source_target_pairs={{0,96},{1,97},{2,98},{3,99},{4,100},{5,101},{6,102},{7,103},{8,104... | collective-permute-start | bytes 614408 | tf_op jit(solution)/shard_map/density_gather/ppermute | solution.py:28
  129.2 22.0 %collective-permute-start.25 = (bf16[1280,640]{1,0:T(8,128)(2,1)}, bf16[1280,640]{1,0:T(8,128)(2,1)S(1)}, u32[]{:S(2)}, u32[]{:S(2)}) collective-permute-start(bf16[1280,640]{1,0:T(8,128)(2,1)} %density_rows.1), channel_id=1, source_target_pairs={{0,2},{1,3},{2,0},{3,1},{4,6},{5,7},{6,4},{7,5},{8,10},{9,11},{10,... | collective-permute-start | bytes 4915208 | tf_op jit(solution)/shard_map/mixed_gather/ppermute | solution.py:28
  132.2 13.2 %collective-permute-start.23 = (bf16[160,1280]{1,0:T(8,128)(2,1)S(1)}, bf16[160,1280]{1,0:T(8,128)(2,1)S(1)}, u32[]{:S(2)}, u32[]{:S(2)}) collective-permute-start(bf16[160,1280]{1,0:T(8,128)(2,1)S(1)} %fusion.9), channel_id=1, source_target_pairs={{0,24},{1,25},{2,26},{3,27},{4,28},{5,29},{6,30},{7,31},{8,16},{9,... | collective-permute-start | bytes 1228808 | tf_op jit(solution)/shard_map/mixed_gather/ppermute | solution.py:28
  133.4 12.7 %collective-permute-start.24 = (bf16[160,1280]{1,0:T(8,128)(2,1)S(1)}, bf16[160,1280]{1,0:T(8,128)(2,1)S(1)}, u32[]{:S(2)}, u32[]{:S(2)}) collective-permute-start(bf16[160,1280]{1,0:T(8,128)(2,1)S(1)} %fusion.9), channel_id=1, source_target_pairs={{0,8},{1,9},{2,10},{3,11},{4,12},{5,13},{6,14},{7,15},{8,0},{9,1},... | collective-permute-start | bytes 1228808 | tf_op jit(solution)/shard_map/mixed_gather/ppermute | solution.py:28
  146.8 8.8 %collective-permute-start.26 = (bf16[80,1280]{1,0:T(8,128)(2,1)}, bf16[80,1280]{1,0:T(8,128)(2,1)S(1)}, u32[]{:S(2)}, u32[]{:S(2)}) collective-permute-start(bf16[80,1280]{1,0:T(8,128)(2,1)} %slice.120), channel_id=1, source_target_pairs={{0,8},{1,9},{2,10},{3,11},{4,12},{5,13},{6,14},{7,15},{8,0},{9,1},... | collective-permute-start | bytes 614408 | tf_op jit(solution)/shard_map/mixed_gather/ppermute | solution.py:28
  159.4 12.6 %collective-permute-start.29 = (bf16[2,3,40,640]{3,2,1,0:T(8,128)(2,1)}, bf16[2,3,40,640]{3,2,1,0:T(8,128)(2,1)}, u32[]{:S(2)}, u32[]{:S(2)}) collective-permute-start(bf16[2,3,40,640]{3,2,1,0:T(8,128)(2,1)} %get-tuple-element.105), channel_id=1, source_target_pairs={{0,2},{1,3},{2,4},{3,5},{4,6},{5,7},{6,0},{7,1},{8,10},{9,11},{10,... | collective-permute-start | bytes 921608 | tf_op jit(solution)/shard_map/second_product/ppermute | solution.py:42
  159.5 14.3 %collective-permute-start.30 = (bf16[2,3,40,640]{3,2,1,0:T(8,128)(2,1)}, bf16[2,3,40,640]{3,2,1,0:T(8,128)(2,1)}, u32[]{:S(2)}, u32[]{:S(2)}) collective-permute-start(bf16[2,3,40,640]{3,2,1,0:T(8,128)(2,1)} %get-tuple-element.106), channel_id=1, source_target_pairs={{0,1},{1,0},{2,7},{3,6},{4,5},{5,4},{6,3},{7,2},{8,9},{9,8},{10,15... | collective-permute-start | bytes 921608 | tf_op jit(solution)/shard_map/second_product/ppermute | solution.py:42
  163.3 16.2 %collective-permute-start.31 = (bf16[2,3,40,640]{3,2,1,0:T(8,128)(2,1)}, bf16[2,3,40,640]{3,2,1,0:T(8,128)(2,1)}, u32[]{:S(2)}, u32[]{:S(2)}) collective-permute-start(bf16[2,3,40,640]{3,2,1,0:T(8,128)(2,1)} %get-tuple-element.107), channel_id=1, source_target_pairs={{0,3},{1,2},{2,5},{3,4},{4,7},{5,6},{6,1},{7,0},{8,11},{9,10},{10,... | collective-permute-start | bytes 921608 | tf_op jit(solution)/shard_map/second_product/ppermute | solution.py:42
  168.5 11.1 %collective-permute-start.32 = (bf16[2,1,40,640]{3,2,1,0:T(8,128)(2,1)}, bf16[2,1,40,640]{3,2,1,0:T(8,128)(2,1)S(1)}, u32[]{:S(2)}, u32[]{:S(2)}) collective-permute-start(bf16[2,1,40,640]{3,2,1,0:T(8,128)(2,1)} %get-tuple-element.110), channel_id=1, source_target_pairs={{0,0},{1,1},{2,6},{3,7},{4,4},{5,5},{6,2},{7,3},{8,8},{9,9},{10,14... | collective-permute-start | bytes 307208 | tf_op jit(solution)/shard_map/second_product/ppermute | solution.py:42
  170.0 9.5 %collective-permute-start.33 = (bf16[2,1,40,640]{3,2,1,0:T(8,128)(2,1)}, bf16[2,1,40,640]{3,2,1,0:T(8,128)(2,1)S(1)}, u32[]{:S(2)}, u32[]{:S(2)}) collective-permute-start(bf16[2,1,40,640]{3,2,1,0:T(8,128)(2,1)} %get-tuple-element.111), channel_id=1, source_target_pairs={{0,2},{1,3},{2,4},{3,5},{4,6},{5,7},{6,0},{7,1},{8,10},{9,11},{10,... | collective-permute-start | bytes 307208 | tf_op jit(solution)/shard_map/second_product/ppermute | solution.py:42
  173.8 8.9 %collective-permute-start.35 = (bf16[2,1,40,640]{3,2,1,0:T(8,128)(2,1)}, bf16[2,1,40,640]{3,2,1,0:T(8,128)(2,1)S(1)}, u32[]{:S(2)}, u32[]{:S(2)}) collective-permute-start(bf16[2,1,40,640]{3,2,1,0:T(8,128)(2,1)} %get-tuple-element.113), channel_id=1, source_target_pairs={{0,3},{1,2},{2,5},{3,4},{4,7},{5,6},{6,1},{7,0},{8,11},{9,10},{10,... | collective-permute-start | bytes 307208 | tf_op jit(solution)/shard_map/second_product/ppermute | solution.py:42
  186.2 22.4 %all-to-all-start.2 = ((bf16[32,40,160]{2,1,0:T(8,128)(2,1)}), bf16[32,40,160]{2,1,0:T(8,128)(2,1)S(1)}, u32[]{:S(2)}, u32[]{:S(2)}) async-start(bf16[32,40,160]{2,1,0:T(8,128)(2,1)} %get-tuple-element.118), calls=%async_computation.2 | async-start | bytes 1310720 | tf_op jit(solution)/shard_map/transposed/all_to_all | solution.py:331
  193.1 8.2 %collective-permute-start.36 = (f32[40,1280]{1,0:T(8,128)}, f32[40,1280]{1,0:T(8,128)S(1)}, u32[]{:S(2)}, u32[]{:S(2)}) collective-permute-start(f32[40,1280]{1,0:T(8,128)} %get-tuple-element.115), channel_id=1, source_target_pairs={{0,8},{1,9},{2,10},{3,11},{4,12},{5,13},{6,14},{7,15},{8,0},{9,1},... | collective-permute-start | bytes 614408 | tf_op jit(solution)/shard_map/direct/ppermute | solution.py:28
  193.2 12.8 %collective-permute-start.37 = (f32[40,1280]{1,0:T(8,128)}, f32[40,1280]{1,0:T(8,128)S(1)}, u32[]{:S(2)}, u32[]{:S(2)}) collective-permute-start(f32[40,1280]{1,0:T(8,128)} %get-tuple-element.116), channel_id=1, source_target_pairs={{0,16},{1,17},{2,18},{3,19},{4,20},{5,21},{6,22},{7,23},{8,24},{9,... | collective-permute-start | bytes 614408 | tf_op jit(solution)/shard_map/direct/ppermute | solution.py:28
  196.2 12.4 %collective-permute-start.38 = (f32[40,1280]{1,0:T(8,128)}, f32[40,1280]{1,0:T(8,128)S(1)}, u32[]{:S(2)}, u32[]{:S(2)}) collective-permute-start(f32[40,1280]{1,0:T(8,128)} %get-tuple-element.117), channel_id=1, source_target_pairs={{0,24},{1,25},{2,26},{3,27},{4,28},{5,29},{6,30},{7,31},{8,16},{9,... | collective-permute-start | bytes 614408 | tf_op jit(solution)/shard_map/direct/ppermute | solution.py:28
  (37 other events, 267.8 us)

commit v10 on v8

--- a/solution.py
+++ b/solution.py
@@ -69,18 +69,41 @@
     return jax.ShapeDtypeStruct(dims, dtype)
 
 
-def left_kernel(at_ref, first_ref, second_ref, came_ref, *outs):
-    y, core = at_ref[1], at_ref[3]
-    low = jnp.where(core == 0, first_ref[...], came_ref[...])
-    high = jnp.where(core == 0, came_ref[...], second_ref[...])
+def left_kernel(at_ref, first_ref, second_ref, *outs):
+    y = at_ref[1]
+    first, second = first_ref[...], second_ref[...]
+    pieces = []
     for ny in range(4):
         cut = slice(ny * 320, ny * 320 + 320)
-        piece = jnp.concatenate((low[:, cut], high[:, cut]), axis=1)
-        for q in range(4):
-
-            @pl.when((y ^ q) == ny)
-            def _():
-                outs[q][...] = piece
+        pieces.append(jnp.concatenate((first[:, cut], second[:, cut]), axis=1))
+    for q in range(4):
+        low = jnp.where((y & 1) == 0, pieces[q], pieces[q ^ 1])
+        high = jnp.where((y & 1) == 0, pieces[q ^ 2], pieces[q ^ 3])
+        outs[q][...] = jnp.where((y & 2) == 0, low, high)
+
+
+def pass_kernel(at_ref, *refs):
+    core, out = at_ref[3], refs[4]
+    for c in range(2):
+
+        @pl.when(core == c)
+        def _():
+            for q in range(4):
+                cut = slice(320 - c * 320, 640 - c * 320)
+                out[q * 160 : q * 160 + 160] = refs[q][:, cut]
+
+
+def pair_kernel(at_ref, *refs):
+    core, came_ref, out = at_ref[3], refs[4], refs[5]
+    for c in range(2):
+
+        @pl.when(core == c)
+        def _():
+            for q in range(4):
+                rows = slice(q * 160, q * 160 + 160)
+                pair = [came_ref[rows], came_ref[rows]]
+                pair[c] = refs[q][:, c * 320 : c * 320 + 320]
+                out[rows] = jnp.concatenate(pair, axis=1)
 
 
 def right_kernel(at_ref, first_ref, second_ref, out_ref):
@@ -199,25 +222,25 @@
     coords = jnp.stack((z, y, xl, core, xh)).astype(jnp.int32)
 
     with jax.named_scope("left_columns"):
-        send = jnp.where(core == 0, density, dens_resp)
-        came = flip(send, core=1)
-    with jax.named_scope("right_columns"):
-        first, second, _ = lax.optimization_barrier((fock, fock_resp, send))
-        parts = local_call(
-            right_kernel, "right_columns", shape(bf16, 8, 160, 320), coords, first, second
-        )
+        pieces = local_call(
+            left_kernel, "left_columns", [shape(bf16, 160, 640)] * 4, coords, dens_resp, density
+        )
+        slots = [pieces[0]] + [flip(pieces[q], y=q) for q in (1, 2, 3)]
     with jax.named_scope("density_turn"):
-        halves, _ = lax.optimization_barrier((density.reshape(2, 2, 40, 1280), send))
+        halves = density.reshape(2, 2, 40, 1280)
         same = lax.dynamic_index_in_dim(halves, xh, 1, keepdims=False).reshape(80, 1280)
         other = lax.dynamic_index_in_dim(halves, 1 - xh, 1, keepdims=False).reshape(80, 1280)
         other = flip(other, xh=1)
-    with jax.named_scope("left_columns"):
-        pieces = local_call(
-            left_kernel, "left_columns", [shape(bf16, 160, 640)] * 4, coords, dens_resp, density, came
-        )
-        parts, pieces = lax.optimization_barrier((parts, pieces))
-        left = jnp.concatenate([pieces[0]] + [flip(pieces[q], y=q) for q in (1, 2, 3)])
-        left, other = lax.optimization_barrier((left, other))
+    with jax.named_scope("right_columns"):
+        first, second, _ = lax.optimization_barrier((fock, fock_resp, pieces))
+        parts = local_call(
+            right_kernel, "right_columns", shape(bf16, 8, 160, 320), coords, first, second
+        )
+        parts, other = lax.optimization_barrier((parts, other))
+    with jax.named_scope("left_pair"):
+        came = local_call(pass_kernel, "left_pass", shape(bf16, 640, 320), coords, *slots)
+        came = flip(came, core=1)
+        left = local_call(pair_kernel, "left_pair", shape(bf16, 640, 640), coords, *slots, came)
     with jax.named_scope("right_gather"):
         rounds = lax.all_to_all(
             parts, ("xl", "core", "xh"), split_axis=0, concat_axis=0, tiled=True

time: 206 us -> 213 us (1.034)
  waiting for transfers between devices: 80.6 us -> 91.9 us
  other arithmetic: 12.1 us -> 7.27 us
  Pallas kernels: 25.9 us -> 30.4 us
  starting transfers between devices: 70.1 us -> 65.8 us
    ppermute x31, waiting for transfers between devices: 76 us -> 87.2 us  [flip(): return lax.ppermute(value, AXES, pairs)]
    pallas_call x8 -> x10, Pallas kernels: 25.9 us -> 30.4 us  [local_call(): pl.pallas_call(kernel, out_shape=outs, in_specs=[SMEM] + [VMEM] * len(ope...]
    ppermute x31, starting transfers between devices: 38.4 us -> 34.2 us  [flip(): return lax.ppermute(value, AXES, pairs)]
    unnamed x60 -> x68, local copies, waits for them, and re-layouts: 7.27 us -> 6.53 us
  transfers between devices with their start and end apart: 42 -> 42, of which waited for: 22 -> 24; matrix products, arithmetic and copies ran while one was open for 7% -> 4% of each run, Pallas kernels for 8% -> 11%
where the time goes in v10:
time: 213 us; the launch traced here: 212 us
  waiting for transfers between devices  91.9 us (43%)
  starting transfers between devices  65.8 us (31%)
  Pallas kernels  30.4 us (14%)
  local copies, waits for them, and re-layouts  10.8 us (5%)
  other arithmetic  7.27 us (3%)
  matrix products  5.34 us (3%)
    ppermute x31, waiting for transfers between devices, flip(): return lax.ppermute(value, AXES, pairs)  87.2 us
    ppermute x31, starting transfers between devices, flip(): return lax.ppermute(value, AXES, pairs)  34.2 us
    pallas_call x10, Pallas kernels, local_call(): pl.pallas_call(kernel, out_shape=outs, in_specs=[SMEM] + [VMEM] * len(ope...  30.4 us
    ppermute x8, starting transfers between devices, remap(): return lax.ppermute(value, AXES, pairs)  15.8 us
    all_to_all x1, starting transfers between devices, shards(): lax.all_to_all(turned, ('z', 'xl', 'core', 'xh'), split_axis=0, concat_ax...  7.54 us
    unnamed x68, local copies, waits for them, and re-layouts  6.53 us
    all_to_all x1, starting transfers between devices, shards(): lax.all_to_all(parts, ('xl', 'core', 'xh'), split_axis=0, concat_axis=0,...  4.83 us
    ppermute x8, waiting for transfers between devices, remap(): return lax.ppermute(value, AXES, pairs)  4.69 us
  transfers between devices with their start and end apart: 42, of which 24 were waited for; matrix products, arithmetic and copies ran while one was open for 4% of the time, Pallas kernels for 11%

profile of v10, /device:TPU:2, one launch (start us, length us, event | category | flops | bytes accessed | tf_op | source)
XLA Modules:
  0.0 211.9 jit_solution(2970596109018330066)
XLA Ops:
  6.8 2.8 %right_columns.1 = bf16[8,160,320]{2,1,0:T(8,128)(2,1)} custom-call(s32[5]{0:T(128)} %stack.38.at_ref, bf16[160,1280]{1,0:T(8,128)(2,1)} %first_ref.2, bf16[160,1280]{1,0:T(8,128)(2,1)} %second_ref.2), custom_call_target="tpu_custom_call" | custom-call | tf_op jit(solution)/shard_map/right_columns/right_columns/pallas_call | solution.py:58
  10.1 4.8 %all-to-all-start = ((bf16[8,160,320]{2,1,0:T(8,128)(2,1)}), bf16[8,160,320]{2,1,0:T(8,128)(2,1)S(1)}, u32[]{:S(2)}, u32[]{:S(2)}) async-start(bf16[8,160,320]{2,1,0:T(8,128)(2,1)} %right_columns.1), calls=%async_computation | async-start | bytes 1966080 | tf_op jit(solution)/shard_map/right_gather/all_to_all | solution.py:245
  16.5 2.9 %collective-permute-start.2 = (bf16[160,640]{1,0:T(8,128)(2,1)S(1)}, bf16[160,640]{1,0:T(8,128)(2,1)S(1)}, u32[]{:S(2)}, u32[]{:S(2)}) collective-permute-start(bf16[160,640]{1,0:T(8,128)(2,1)S(1)} %copy-done.31), channel_id=1, source_target_pairs={{0,16},{1,17},{2,18},{3,19},{4,20},{5,21},{6,22},{7,23},{8,24},{9,... | collective-permute-start | bytes 614408 | tf_op jit(solution)/shard_map/left_columns/ppermute | solution.py:28
  19.6 3.2 %collective-permute-done.1.refs_1_ = bf16[160,640]{1,0:T(8,128)(2,1)S(1)} collective-permute-done((bf16[160,640]{1,0:T(8,128)(2,1)S(1)}, bf16[160,640]{1,0:T(8,128)(2,1)S(1)}, u32[]{:S(2)}, u32[]{:S(2)}) %collective-permute-start.1) | collective-permute-done | bytes 204832 | tf_op jit(solution)/shard_map/left_columns/ppermute | solution.py:28
  22.8 6.2 %collective-permute-done.2.refs_2_ = bf16[160,640]{1,0:T(8,128)(2,1)S(1)} collective-permute-done((bf16[160,640]{1,0:T(8,128)(2,1)S(1)}, bf16[160,640]{1,0:T(8,128)(2,1)S(1)}, u32[]{:S(2)}, u32[]{:S(2)}) %collective-permute-start.2) | collective-permute-done | bytes 204832 | tf_op jit(solution)/shard_map/left_columns/ppermute | solution.py:28
  29.0 2.6 %collective-permute-done.3.refs_3_ = bf16[160,640]{1,0:T(8,128)(2,1)S(1)} collective-permute-done((bf16[160,640]{1,0:T(8,128)(2,1)S(1)}, bf16[160,640]{1,0:T(8,128)(2,1)S(1)}, u32[]{:S(2)}, u32[]{:S(2)}) %collective-permute-start.3) | collective-permute-done | bytes 204832 | tf_op jit(solution)/shard_map/left_columns/ppermute | solution.py:28
  37.3 2.5 %left_pair.1 = bf16[640,640]{1,0:T(8,128)(2,1)} custom-call(s32[5]{0:T(128)} %stack.38.at_ref, bf16[160,640]{1,0:T(8,128)(2,1)} %get-tuple-element.53.refs_0_, bf16[160,640]{1,0:T(8,128)(2,1)} %copy-done.10, bf16[160,640]{1,0:T(8,128)(2,1)} %copy-done.11, bf16[160,640]{1,0:T(8,128)(2,1)} %copy-done.12, bf16[640,320]{1,0:T(8,128)(2,1)} %copy-done.15), custom_call_target="tpu_custom_call" | custom-call | tf_op jit(solution)/shard_map/left_pair/left_pair/pallas_call | solution.py:58
  41.6 2.5 %collective-permute-start.6 = (bf16[640,640]{1,0:T(8,128)(2,1)S(1)}, bf16[640,640]{1,0:T(8,128)(2,1)}, u32[]{:S(2)}, u32[]{:S(2)}) collective-permute-start(bf16[640,640]{1,0:T(8,128)(2,1)S(1)} %copy-done.2), channel_id=1, source_target_pairs={{0,1},{1,0},{2,3},{3,2},{4,5},{5,4},{6,7},{7,6},{8,9},{9,8},{10,11... | collective-permute-start | bytes 2457608 | tf_op jit(solution)/shard_map/left_gather/ppermute | solution.py:28
  44.7 4.0 %collective-permute-start.10 = (bf16[320,1280]{1,0:T(8,128)(2,1)S(1)}, bf16[320,1280]{1,0:T(8,128)(2,1)}, u32[]{:S(2)}, u32[]{:S(2)}) collective-permute-start(bf16[320,1280]{1,0:T(8,128)(2,1)S(1)} %reshape.60), channel_id=1, source_target_pairs={{0,96},{1,97},{2,98},{3,99},{4,100},{5,101},{6,102},{7,103},{8,104... | collective-permute-start | bytes 2457608 | tf_op jit(solution)/shard_map/right_gather/ppermute | solution.py:28
  48.7 13.6 %collective-permute-done.5 = bf16[640,640]{1,0:T(8,128)(2,1)S(1)} collective-permute-done((bf16[640,640]{1,0:T(8,128)(2,1)S(1)}, bf16[640,640]{1,0:T(8,128)(2,1)S(1)}, u32[]{:S(2)}, u32[]{:S(2)}) %collective-permute-start.5) | collective-permute-done | bytes 819232 | tf_op jit(solution)/shard_map/left_gather/ppermute | solution.py:28
  62.3 3.9 %collective-permute-start.9 = (bf16[320,1280]{1,0:T(8,128)(2,1)S(1)}, bf16[320,1280]{1,0:T(8,128)(2,1)}, u32[]{:S(2)}, u32[]{:S(2)}) collective-permute-start(bf16[320,1280]{1,0:T(8,128)(2,1)S(1)} %reshape.60), channel_id=1, source_target_pairs={{0,64},{1,65},{2,66},{3,67},{4,68},{5,69},{6,70},{7,71},{8,72},{9,... | collective-permute-start | bytes 2457608 | tf_op jit(solution)/shard_map/right_gather/ppermute | solution.py:28
  68.1 3.5 %all-to-all-start.1 = ((bf16[4,80,640]{2,1,0:T(8,128)(2,1)}), bf16[4,80,640]{2,1,0:T(8,128)(2,1)S(1)}, u32[]{:S(2)}, u32[]{:S(2)}) async-start(bf16[4,80,640]{2,1,0:T(8,128)(2,1)} %density_columns.1), calls=%async_computation.1 | async-start | bytes 819200 | tf_op jit(solution)/shard_map/density_columns/all_to_all | solution.py:264
  72.9 7.1 %collective-permute-done.6 = bf16[640,640]{1,0:T(8,128)(2,1)} collective-permute-done((bf16[640,640]{1,0:T(8,128)(2,1)S(1)}, bf16[640,640]{1,0:T(8,128)(2,1)}, u32[]{:S(2)}, u32[]{:S(2)}) %collective-permute-start.6) | collective-permute-done | bytes 819232 | tf_op jit(solution)/shard_map/left_gather/ppermute | solution.py:28
  91.6 3.1 %collective-permute-start.16 = (bf16[320,640]{1,0:T(8,128)(2,1)S(1)}, bf16[320,640]{1,0:T(8,128)(2,1)S(1)}, u32[]{:S(2)}, u32[]{:S(2)}) collective-permute-start(bf16[320,640]{1,0:T(8,128)(2,1)S(1)} %bitcast.34), channel_id=1, source_target_pairs={{0,96},{1,97},{2,98},{3,99},{4,100},{5,101},{6,102},{7,103},{8,104... | collective-permute-start | bytes 1228808 | tf_op jit(solution)/shard_map/density_gather/ppermute | solution.py:28
  99.3 4.2 %collective-permute-done.15.one_ref = bf16[320,640]{1,0:T(8,128)(2,1)S(1)} collective-permute-done((bf16[320,640]{1,0:T(8,128)(2,1)S(1)}, bf16[320,640]{1,0:T(8,128)(2,1)S(1)}, u32[]{:S(2)}, u32[]{:S(2)}) %collective-permute-start.15) | collective-permute-done | bytes 409632 | tf_op jit(solution)/shard_map/density_gather/ppermute | solution.py:28
  104.6 5.6 %collective-permute-done.13 = f32[80,1280]{1,0:T(8,128)S(1)} collective-permute-done((f32[80,1280]{1,0:T(8,128)S(1)}, f32[80,1280]{1,0:T(8,128)S(1)}, u32[]{:S(2)}, u32[]{:S(2)}) %collective-permute-start.13) | collective-permute-done | bytes 409632 | tf_op jit(solution)/shard_map/mixed_sum/ppermute | solution.py:28
  115.0 5.3 %collective-permute-done.20.upper_ref = bf16[160,640]{1,0:T(8,128)(2,1)S(1)} collective-permute-done((bf16[160,640]{1,0:T(8,128)(2,1)S(1)}, bf16[160,640]{1,0:T(8,128)(2,1)S(1)}, u32[]{:S(2)}, u32[]{:S(2)}) %collective-permute-start.20) | collective-permute-done | bytes 204832 | tf_op jit(solution)/shard_map/density_gather/ppermute | solution.py:28
  122.6 2.7 %density_rows.1.mine_ref = bf16[1280,640]{1,0:T(8,128)(2,1)} custom-call(s32[5]{0:T(128)} %stack.38.at_ref, bf16[320,640]{1,0:T(8,128)(2,1)} %bitcast.35, bf16[320,640]{1,0:T(8,128)(2,1)} %copy-done.8, bf16[160,640]{1,0:T(8,128)(2,1)} %copy-done.25, bf16[160,640]{1,0:T(8,128)(2,1)} %collective-permute-done.21.lower_ref, bf16[320,640]{1,0:T(8,128)(2,1)} %copy-done.9), custom_call_target="tpu_custom_call" | custom-call | tf_op jit(solution)/shard_map/density_rows/density_rows/pallas_call | solution.py:58
  125.3 7.0 %collective-permute-done.19 = f32[160,1280]{1,0:T(8,128)S(1)} collective-permute-done((f32[160,1280]{1,0:T(8,128)S(1)}, f32[160,1280]{1,0:T(8,128)S(1)}, u32[]{:S(2)}, u32[]{:S(2)}) %collective-permute-start.19) | collective-permute-done | bytes 819232 | tf_op jit(solution)/shard_map/mixed_sum/ppermute | solution.py:28
  136.2 11.1 %collective-permute-done.24.refs_2_ = bf16[160,1280]{1,0:T(8,128)(2,1)S(1)} collective-permute-done((bf16[160,1280]{1,0:T(8,128)(2,1)S(1)}, bf16[160,1280]{1,0:T(8,128)(2,1)S(1)}, u32[]{:S(2)}, u32[]{:S(2)}) %collective-permute-start.24) | collective-permute-done | bytes 409632 | tf_op jit(solution)/shard_map/mixed_gather/ppermute | solution.py:28
  150.7 5.4 %second_product.2 = (bf16[2,3,40,640]{3,2,1,0:T(8,128)(2,1)}, bf16[2,3,40,640]{3,2,1,0:T(8,128)(2,1)}, bf16[2,3,40,640]{3,2,1,0:T(8,128)(2,1)}, bf16[2,3,40,640]{3,2,1,0:T(8,128)(2,1)}) custom-call(s32[5]{0:T(128)} %stack.38.at_ref, bf16[1280,640]{1,0:T(8,128)(2,1)} %density_rows.1.mine_ref, bf16[1280,640]{1,0:T(8,128)(2,1)} %copy-done, ...), custom_call_target="tpu_custom_call" | custom-call | tf_op jit(solution)/shard_map/second_product/second_product/pallas_call | solution.py:58
  157.7 2.7 %collective-permute-start.31 = (bf16[2,3,40,640]{3,2,1,0:T(8,128)(2,1)}, bf16[2,3,40,640]{3,2,1,0:T(8,128)(2,1)S(1)}, u32[]{:S(2)}, u32[]{:S(2)}) collective-permute-start(bf16[2,3,40,640]{3,2,1,0:T(8,128)(2,1)} %get-tuple-element.89), channel_id=1, source_target_pairs={{0,3},{1,2},{2,5},{3,4},{4,7},{5,6},{6,1},{7,0},{8,11},{9,10},{10,... | collective-permute-start | bytes 921608 | tf_op jit(solution)/shard_map/second_product/ppermute | solution.py:42
  162.4 3.7 %second_product.3 = (bf16[2,1,40,640]{3,2,1,0:T(8,128)(2,1)}, bf16[2,1,40,640]{3,2,1,0:T(8,128)(2,1)}, bf16[2,1,40,640]{3,2,1,0:T(8,128)(2,1)}, bf16[2,1,40,640]{3,2,1,0:T(8,128)(2,1)}) custom-call(s32[5]{0:T(128)} %stack.38.at_ref, bf16[1280,640]{1,0:T(8,128)(2,1)} %density_rows.1.mine_ref, bf16[1280,640]{1,0:T(8,128)(2,1)} %copy-done, ...), custom_call_target="tpu_custom_call" | custom-call | tf_op jit(solution)/shard_map/second_product/second_product/pallas_call | solution.py:58
  167.6 4.5 %collective-permute-start.33 = (bf16[2,1,40,640]{3,2,1,0:T(8,128)(2,1)}, bf16[2,1,40,640]{3,2,1,0:T(8,128)(2,1)S(1)}, u32[]{:S(2)}, u32[]{:S(2)}) collective-permute-start(bf16[2,1,40,640]{3,2,1,0:T(8,128)(2,1)} %get-tuple-element.93), channel_id=1, source_target_pairs={{0,2},{1,3},{2,4},{3,5},{4,6},{5,7},{6,0},{7,1},{8,10},{9,11},{10,... | collective-permute-start | bytes 307208 | tf_op jit(solution)/shard_map/second_product/ppermute | solution.py:42
  172.2 3.5 %collective-permute-start.34 = (bf16[2,1,40,640]{3,2,1,0:T(8,128)(2,1)}, bf16[2,1,40,640]{3,2,1,0:T(8,128)(2,1)S(1)}, u32[]{:S(2)}, u32[]{:S(2)}) collective-permute-start(bf16[2,1,40,640]{3,2,1,0:T(8,128)(2,1)} %get-tuple-element.94), channel_id=1, source_target_pairs={{0,1},{1,0},{2,7},{3,6},{4,5},{5,4},{6,3},{7,2},{8,9},{9,8},{10,15... | collective-permute-start | bytes 307208 | tf_op jit(solution)/shard_map/second_product/ppermute | solution.py:42
  175.9 3.8 %collective-permute-done.34.refs_6_ = bf16[2,1,40,640]{3,2,1,0:T(8,128)(2,1)S(1)} collective-permute-done((bf16[2,1,40,640]{3,2,1,0:T(8,128)(2,1)}, bf16[2,1,40,640]{3,2,1,0:T(8,128)(2,1)S(1)}, u32[]{:S(2)}, u32[]{:S(2)}) %collective-permute-start.34) | collective-permute-done | bytes 102432 | tf_op jit(solution)/shard_map/second_product/ppermute | solution.py:42
  181.1 2.9 %spread.1 = (bf16[32,40,160]{2,1,0:T(8,128)(2,1)}, f32[40,1280]{1,0:T(8,128)}, f32[40,1280]{1,0:T(8,128)}, f32[40,1280]{1,0:T(8,128)}, f32[40,1280]{1,0:T(8,128)}) custom-call(s32[5]{0:T(128)} %stack.38.at_ref, bf16[2,3,40,640]{3,2,1,0:T(8,128)(2,1)} %copy-done.16, bf16[2,3,40,640]{3,2,1,0:T(8,128)(2,1)} %copy-done.18, bf16[2,3,40,640]{3,2,1,0:T(8,128)(2,1)} %copy-done.19, ...), custom_call_target="tpu_custom_call" | custom-call | tf_op jit(solution)/shard_map/second_product/spread/pallas_call | solution.py:58
  184.0 7.5 %all-to-all-start.2 = ((bf16[32,40,160]{2,1,0:T(8,128)(2,1)}), bf16[32,40,160]{2,1,0:T(8,128)(2,1)S(1)}, u32[]{:S(2)}, u32[]{:S(2)}) async-start(bf16[32,40,160]{2,1,0:T(8,128)(2,1)} %get-tuple-element.100), calls=%async_computation.2 | async-start | bytes 1310720 | tf_op jit(solution)/shard_map/transposed/all_to_all | solution.py:356
  197.1 2.6 %collective-permute-done.36.d1 = f32[40,1280]{1,0:T(8,128)S(1)} collective-permute-done((f32[40,1280]{1,0:T(8,128)}, f32[40,1280]{1,0:T(8,128)S(1)}, u32[]{:S(2)}, u32[]{:S(2)}) %collective-permute-start.36) | collective-permute-done | bytes 204832 | tf_op jit(solution)/shard_map/direct/ppermute | solution.py:28
  199.8 4.8 %collective-permute-done.37.d2 = f32[40,1280]{1,0:T(8,128)S(1)} collective-permute-done((f32[40,1280]{1,0:T(8,128)}, f32[40,1280]{1,0:T(8,128)S(1)}, u32[]{:S(2)}, u32[]{:S(2)}) %collective-permute-start.37) | collective-permute-done | bytes 204832 | tf_op jit(solution)/shard_map/direct/ppermute | solution.py:28
  204.5 2.6 %collective-permute-done.38.d3 = f32[40,1280]{1,0:T(8,128)S(1)} collective-permute-done((f32[40,1280]{1,0:T(8,128)}, f32[40,1280]{1,0:T(8,128)S(1)}, u32[]{:S(2)}, u32[]{:S(2)}) %collective-permute-start.38) | collective-permute-done | bytes 204832 | tf_op jit(solution)/shard_map/direct/ppermute | solution.py:28
  208.0 3.9 %finish.1 = f32[40,5120]{1,0:T(8,128)} custom-call(s32[5]{0:T(128)} %stack.38.at_ref, f32[40,1280]{1,0:T(8,128)} %get-tuple-element.96.d0, f32[40,1280]{1,0:T(8,128)} %copy-done.20, f32[40,1280]{1,0:T(8,128)} %copy-done.21, f32[40,1280]{1,0:T(8,128)} %copy-done.22, bf16[32,40,160]{2,1,0:T(8,128)(2,1)} %copy-done.3, f32[40,40]{1,0:T(8,128)} %fusion.11.kept_ref), custom_call_target="tpu_custom_call" | custom-call | tf_op jit(solution)/shard_map/finish/pallas_call | solution.py:58
  (153 shorter events, 65.0 us)
Async XLA Ops:
  1.7 8.3 %collective-permute-start = (bf16[80,1280]{1,0:T(8,128)(2,1)S(1)}, bf16[80,1280]{1,0:T(8,128)(2,1)S(1)}, u32[]{:S(2)}, u32[]{:S(2)}) collective-permute-start(bf16[80,1280]{1,0:T(8,128)(2,1)S(1)} %bitcast.37), channel_id=1, source_target_pairs={{0,1},{1,0},{2,3},{3,2},{4,5},{5,4},{6,7},{7,6},{8,9},{9,8},{10,11... | collective-permute-start | bytes 614408 | tf_op jit(solution)/shard_map/density_turn/ppermute | solution.py:28
  10.1 29.8 %all-to-all-start = ((bf16[8,160,320]{2,1,0:T(8,128)(2,1)}), bf16[8,160,320]{2,1,0:T(8,128)(2,1)S(1)}, u32[]{:S(2)}, u32[]{:S(2)}) async-start(bf16[8,160,320]{2,1,0:T(8,128)(2,1)} %right_columns.1), calls=%async_computation | async-start | bytes 1966080 | tf_op jit(solution)/shard_map/right_gather/all_to_all | solution.py:245
  16.5 12.5 %collective-permute-start.2 = (bf16[160,640]{1,0:T(8,128)(2,1)S(1)}, bf16[160,640]{1,0:T(8,128)(2,1)S(1)}, u32[]{:S(2)}, u32[]{:S(2)}) collective-permute-start(bf16[160,640]{1,0:T(8,128)(2,1)S(1)} %copy-done.31), channel_id=1, source_target_pairs={{0,16},{1,17},{2,18},{3,19},{4,20},{5,21},{6,22},{7,23},{8,24},{9,... | collective-permute-start | bytes 614408 | tf_op jit(solution)/shard_map/left_columns/ppermute | solution.py:28
  19.4 12.2 %collective-permute-start.3 = (bf16[160,640]{1,0:T(8,128)(2,1)S(1)}, bf16[160,640]{1,0:T(8,128)(2,1)S(1)}, u32[]{:S(2)}, u32[]{:S(2)}) collective-permute-start(bf16[160,640]{1,0:T(8,128)(2,1)S(1)} %copy-done.30), channel_id=1, source_target_pairs={{0,24},{1,25},{2,26},{3,27},{4,28},{5,29},{6,30},{7,31},{8,16},{9,... | collective-permute-start | bytes 614408 | tf_op jit(solution)/shard_map/left_columns/ppermute | solution.py:28
  41.1 21.2 %collective-permute-start.5 = (bf16[640,640]{1,0:T(8,128)(2,1)S(1)}, bf16[640,640]{1,0:T(8,128)(2,1)S(1)}, u32[]{:S(2)}, u32[]{:S(2)}) collective-permute-start(bf16[640,640]{1,0:T(8,128)(2,1)S(1)} %copy-done.2), channel_id=1, source_target_pairs={{0,4},{1,5},{2,6},{3,7},{4,0},{5,1},{6,2},{7,3},{8,12},{9,13},{10,... | collective-permute-start | bytes 2457608 | tf_op jit(solution)/shard_map/left_gather/ppermute | solution.py:28
  41.6 38.5 %collective-permute-start.6 = (bf16[640,640]{1,0:T(8,128)(2,1)S(1)}, bf16[640,640]{1,0:T(8,128)(2,1)}, u32[]{:S(2)}, u32[]{:S(2)}) collective-permute-start(bf16[640,640]{1,0:T(8,128)(2,1)S(1)} %copy-done.2), channel_id=1, source_target_pairs={{0,1},{1,0},{2,3},{3,2},{4,5},{5,4},{6,7},{7,6},{8,9},{9,8},{10,11... | collective-permute-start | bytes 2457608 | tf_op jit(solution)/shard_map/left_gather/ppermute | solution.py:28
  44.1 37.3 %collective-permute-start.7 = (bf16[640,640]{1,0:T(8,128)(2,1)S(1)}, bf16[640,640]{1,0:T(8,128)(2,1)}, u32[]{:S(2)}, u32[]{:S(2)}) collective-permute-start(bf16[640,640]{1,0:T(8,128)(2,1)S(1)} %copy-done.2), channel_id=1, source_target_pairs={{0,5},{1,4},{2,7},{3,6},{4,1},{5,0},{6,3},{7,2},{8,13},{9,12},{10,... | collective-permute-start | bytes 2457608 | tf_op jit(solution)/shard_map/left_gather/ppermute | solution.py:28
  44.7 38.3 %collective-permute-start.10 = (bf16[320,1280]{1,0:T(8,128)(2,1)S(1)}, bf16[320,1280]{1,0:T(8,128)(2,1)}, u32[]{:S(2)}, u32[]{:S(2)}) collective-permute-start(bf16[320,1280]{1,0:T(8,128)(2,1)S(1)} %reshape.60), channel_id=1, source_target_pairs={{0,96},{1,97},{2,98},{3,99},{4,100},{5,101},{6,102},{7,103},{8,104... | collective-permute-start | bytes 2457608 | tf_op jit(solution)/shard_map/right_gather/ppermute | solution.py:28
  48.7 34.2 %collective-permute-start.8 = (bf16[320,1280]{1,0:T(8,128)(2,1)S(1)}, bf16[320,1280]{1,0:T(8,128)(2,1)}, u32[]{:S(2)}, u32[]{:S(2)}) collective-permute-start(bf16[320,1280]{1,0:T(8,128)(2,1)S(1)} %reshape.60), channel_id=1, source_target_pairs={{0,32},{1,33},{2,34},{3,35},{4,36},{5,37},{6,38},{7,39},{8,40},{9,... | collective-permute-start | bytes 2457608 | tf_op jit(solution)/shard_map/right_gather/ppermute | solution.py:28
  62.3 22.8 %collective-permute-start.9 = (bf16[320,1280]{1,0:T(8,128)(2,1)S(1)}, bf16[320,1280]{1,0:T(8,128)(2,1)}, u32[]{:S(2)}, u32[]{:S(2)}) collective-permute-start(bf16[320,1280]{1,0:T(8,128)(2,1)S(1)} %reshape.60), channel_id=1, source_target_pairs={{0,64},{1,65},{2,66},{3,67},{4,68},{5,69},{6,70},{7,71},{8,72},{9,... | collective-permute-start | bytes 2457608 | tf_op jit(solution)/shard_map/right_gather/ppermute | solution.py:28
  68.1 17.0 %all-to-all-start.1 = ((bf16[4,80,640]{2,1,0:T(8,128)(2,1)}), bf16[4,80,640]{2,1,0:T(8,128)(2,1)S(1)}, u32[]{:S(2)}, u32[]{:S(2)}) async-start(bf16[4,80,640]{2,1,0:T(8,128)(2,1)} %density_columns.1), calls=%async_computation.1 | async-start | bytes 819200 | tf_op jit(solution)/shard_map/density_columns/all_to_all | solution.py:264
  91.6 11.8 %collective-permute-start.15 = (bf16[320,640]{1,0:T(8,128)(2,1)S(1)}, bf16[320,640]{1,0:T(8,128)(2,1)S(1)}, u32[]{:S(2)}, u32[]{:S(2)}) collective-permute-start(bf16[320,640]{1,0:T(8,128)(2,1)S(1)} %bitcast.33), channel_id=1, source_target_pairs={{0,32},{1,33},{2,34},{3,35},{4,36},{5,37},{6,38},{7,39},{8,40},{9,... | collective-permute-start | bytes 1228808 | tf_op jit(solution)/shard_map/density_gather/ppermute | solution.py:28
  91.6 13.0 %collective-permute-start.16 = (bf16[320,640]{1,0:T(8,128)(2,1)S(1)}, bf16[320,640]{1,0:T(8,128)(2,1)S(1)}, u32[]{:S(2)}, u32[]{:S(2)}) collective-permute-start(bf16[320,640]{1,0:T(8,128)(2,1)S(1)} %bitcast.34), channel_id=1, source_target_pairs={{0,96},{1,97},{2,98},{3,99},{4,100},{5,101},{6,102},{7,103},{8,104... | collective-permute-start | bytes 1228808 | tf_op jit(solution)/shard_map/density_gather/ppermute | solution.py:28
  98.8 11.4 %collective-permute-start.13 = (f32[80,1280]{1,0:T(8,128)S(1)}, f32[80,1280]{1,0:T(8,128)S(1)}, u32[]{:S(2)}, u32[]{:S(2)}) collective-permute-start(f32[80,1280]{1,0:T(8,128)S(1)} %get-tuple-element.121), channel_id=1, source_target_pairs={{0,8},{1,9},{2,10},{3,11},{4,12},{5,13},{6,14},{7,15},{8,0},{9,1},... | collective-permute-start | bytes 1228808 | tf_op jit(solution)/shard_map/mixed_sum/ppermute | solution.py:28
  98.9 12.6 %collective-permute-start.14 = (f32[80,1280]{1,0:T(8,128)S(1)}, f32[80,1280]{1,0:T(8,128)S(1)}, u32[]{:S(2)}, u32[]{:S(2)}) collective-permute-start(f32[80,1280]{1,0:T(8,128)S(1)} %get-tuple-element.120), channel_id=1, source_target_pairs={{0,24},{1,25},{2,26},{3,27},{4,28},{5,29},{6,30},{7,31},{8,16},{9,... | collective-permute-start | bytes 1228808 | tf_op jit(solution)/shard_map/mixed_sum/ppermute | solution.py:28
  111.8 20.6 %collective-permute-start.19 = (f32[160,1280]{1,0:T(8,128)S(1)}, f32[160,1280]{1,0:T(8,128)S(1)}, u32[]{:S(2)}, u32[]{:S(2)}) collective-permute-start(f32[160,1280]{1,0:T(8,128)S(1)} %pad_maximum_fusion.3), channel_id=1, source_target_pairs={{0,24},{1,25},{2,26},{3,27},{4,28},{5,29},{6,30},{7,31},{8,16},{9,... | collective-permute-start | bytes 2457608 | tf_op jit(solution)/shard_map/mixed_sum/ppermute | solution.py:28
  112.2 20.1 %collective-permute-start.17 = (f32[160,1280]{1,0:T(8,128)S(1)}, f32[160,1280]{1,0:T(8,128)}, u32[]{:S(2)}, u32[]{:S(2)}) collective-permute-start(f32[160,1280]{1,0:T(8,128)S(1)} %pad_maximum_fusion.2), channel_id=1, source_target_pairs={{0,8},{1,9},{2,10},{3,11},{4,12},{5,13},{6,14},{7,15},{8,0},{9,1},... | collective-permute-start | bytes 2457608 | tf_op jit(solution)/shard_map/mixed_sum/ppermute | solution.py:28
  112.7 19.6 %collective-permute-start.23 = (f32[160,1280]{1,0:T(8,128)S(1)}, f32[160,1280]{1,0:T(8,128)}, u32[]{:S(2)}, u32[]{:S(2)}) collective-permute-start(f32[160,1280]{1,0:T(8,128)S(1)} %get-tuple-element.101), channel_id=1, source_target_pairs={{0,2},{1,3},{2,0},{3,1},{4,6},{5,7},{6,4},{7,5},{8,10},{9,11},{10,... | collective-permute-start | bytes 2457608 | tf_op jit(solution)/shard_map/mixed_sum/ppermute | solution.py:28
  114.0 8.6 %collective-permute-start.21 = (bf16[160,640]{1,0:T(8,128)(2,1)S(1)}, bf16[160,640]{1,0:T(8,128)(2,1)}, u32[]{:S(2)}, u32[]{:S(2)}) collective-permute-start(bf16[160,640]{1,0:T(8,128)(2,1)S(1)} %slice.75), channel_id=1, source_target_pairs={{0,96},{1,97},{2,98},{3,99},{4,100},{5,101},{6,102},{7,103},{8,104... | collective-permute-start | bytes 614408 | tf_op jit(solution)/shard_map/density_gather/ppermute | solution.py:28
  132.3 17.2 %collective-permute-start.22 = (bf16[1280,640]{1,0:T(8,128)(2,1)}, bf16[1280,640]{1,0:T(8,128)(2,1)S(1)}, u32[]{:S(2)}, u32[]{:S(2)}) collective-permute-start(bf16[1280,640]{1,0:T(8,128)(2,1)} %density_rows.1.mine_ref), channel_id=1, source_target_pairs={{0,2},{1,3},{2,0},{3,1},{4,6},{5,7},{6,4},{7,5},{8,10},{9,11},{10,... | collective-permute-start | bytes 4915208 | tf_op jit(solution)/shard_map/mixed_gather/ppermute | solution.py:28
  134.2 13.2 %collective-permute-start.24 = (bf16[160,1280]{1,0:T(8,128)(2,1)S(1)}, bf16[160,1280]{1,0:T(8,128)(2,1)S(1)}, u32[]{:S(2)}, u32[]{:S(2)}) collective-permute-start(bf16[160,1280]{1,0:T(8,128)(2,1)S(1)} %fusion.10.refs_0_), channel_id=1, source_target_pairs={{0,24},{1,25},{2,26},{3,27},{4,28},{5,29},{6,30},{7,31},{8,16},{9,... | collective-permute-start | bytes 1228808 | tf_op jit(solution)/shard_map/mixed_gather/ppermute | solution.py:28
  136.2 11.6 %collective-permute-start.25 = (bf16[160,1280]{1,0:T(8,128)(2,1)S(1)}, bf16[160,1280]{1,0:T(8,128)(2,1)S(1)}, u32[]{:S(2)}, u32[]{:S(2)}) collective-permute-start(bf16[160,1280]{1,0:T(8,128)(2,1)S(1)} %fusion.10.refs_0_), channel_id=1, source_target_pairs={{0,8},{1,9},{2,10},{3,11},{4,12},{5,13},{6,14},{7,15},{8,0},{9,1},... | collective-permute-start | bytes 1228808 | tf_op jit(solution)/shard_map/mixed_gather/ppermute | solution.py:28
  147.8 9.9 %collective-permute-start.27 = (bf16[80,1280]{1,0:T(8,128)(2,1)S(1)}, bf16[80,1280]{1,0:T(8,128)(2,1)S(1)}, u32[]{:S(2)}, u32[]{:S(2)}) collective-permute-start(bf16[80,1280]{1,0:T(8,128)(2,1)S(1)} %slice.94), channel_id=1, source_target_pairs={{0,8},{1,9},{2,10},{3,11},{4,12},{5,13},{6,14},{7,15},{8,0},{9,1},... | collective-permute-start | bytes 614408 | tf_op jit(solution)/shard_map/mixed_gather/ppermute | solution.py:28
  148.2 9.5 %collective-permute-start.28 = (bf16[80,1280]{1,0:T(8,128)(2,1)S(1)}, bf16[80,1280]{1,0:T(8,128)(2,1)}, u32[]{:S(2)}, u32[]{:S(2)}) collective-permute-start(bf16[80,1280]{1,0:T(8,128)(2,1)S(1)} %slice.95), channel_id=1, source_target_pairs={{0,24},{1,25},{2,26},{3,27},{4,28},{5,29},{6,30},{7,31},{8,16},{9,... | collective-permute-start | bytes 614408 | tf_op jit(solution)/shard_map/mixed_gather/ppermute | solution.py:28
  157.7 14.4 %collective-permute-start.31 = (bf16[2,3,40,640]{3,2,1,0:T(8,128)(2,1)}, bf16[2,3,40,640]{3,2,1,0:T(8,128)(2,1)S(1)}, u32[]{:S(2)}, u32[]{:S(2)}) collective-permute-start(bf16[2,3,40,640]{3,2,1,0:T(8,128)(2,1)} %get-tuple-element.89), channel_id=1, source_target_pairs={{0,3},{1,2},{2,5},{3,4},{4,7},{5,6},{6,1},{7,0},{8,11},{9,10},{10,... | collective-permute-start | bytes 921608 | tf_op jit(solution)/shard_map/second_product/ppermute | solution.py:42
  160.5 15.2 %collective-permute-start.29 = (bf16[2,3,40,640]{3,2,1,0:T(8,128)(2,1)}, bf16[2,3,40,640]{3,2,1,0:T(8,128)(2,1)S(1)}, u32[]{:S(2)}, u32[]{:S(2)}) collective-permute-start(bf16[2,3,40,640]{3,2,1,0:T(8,128)(2,1)} %get-tuple-element.87), channel_id=1, source_target_pairs={{0,2},{1,3},{2,4},{3,5},{4,6},{5,7},{6,0},{7,1},{8,10},{9,11},{10,... | collective-permute-start | bytes 921608 | tf_op jit(solution)/shard_map/second_product/ppermute | solution.py:42
  160.5 15.2 %collective-permute-start.30 = (bf16[2,3,40,640]{3,2,1,0:T(8,128)(2,1)}, bf16[2,3,40,640]{3,2,1,0:T(8,128)(2,1)S(1)}, u32[]{:S(2)}, u32[]{:S(2)}) collective-permute-start(bf16[2,3,40,640]{3,2,1,0:T(8,128)(2,1)} %get-tuple-element.88), channel_id=1, source_target_pairs={{0,1},{1,0},{2,7},{3,6},{4,5},{5,4},{6,3},{7,2},{8,9},{9,8},{10,15... | collective-permute-start | bytes 921608 | tf_op jit(solution)/shard_map/second_product/ppermute | solution.py:42
  166.1 9.6 %collective-permute-start.32 = (bf16[2,1,40,640]{3,2,1,0:T(8,128)(2,1)}, bf16[2,1,40,640]{3,2,1,0:T(8,128)(2,1)S(1)}, u32[]{:S(2)}, u32[]{:S(2)}) collective-permute-start(bf16[2,1,40,640]{3,2,1,0:T(8,128)(2,1)} %get-tuple-element.92), channel_id=1, source_target_pairs={{0,0},{1,1},{2,6},{3,7},{4,4},{5,5},{6,2},{7,3},{8,8},{9,9},{10,14... | collective-permute-start | bytes 307208 | tf_op jit(solution)/shard_map/second_product/ppermute | solution.py:42
  167.6 8.2 %collective-permute-start.33 = (bf16[2,1,40,640]{3,2,1,0:T(8,128)(2,1)}, bf16[2,1,40,640]{3,2,1,0:T(8,128)(2,1)S(1)}, u32[]{:S(2)}, u32[]{:S(2)}) collective-permute-start(bf16[2,1,40,640]{3,2,1,0:T(8,128)(2,1)} %get-tuple-element.93), channel_id=1, source_target_pairs={{0,2},{1,3},{2,4},{3,5},{4,6},{5,7},{6,0},{7,1},{8,10},{9,11},{10,... | collective-permute-start | bytes 307208 | tf_op jit(solution)/shard_map/second_product/ppermute | solution.py:42
  184.0 23.1 %all-to-all-start.2 = ((bf16[32,40,160]{2,1,0:T(8,128)(2,1)}), bf16[32,40,160]{2,1,0:T(8,128)(2,1)S(1)}, u32[]{:S(2)}, u32[]{:S(2)}) async-start(bf16[32,40,160]{2,1,0:T(8,128)(2,1)} %get-tuple-element.100), calls=%async_computation.2 | async-start | bytes 1310720 | tf_op jit(solution)/shard_map/transposed/all_to_all | solution.py:356
  192.7 11.8 %collective-permute-start.37 = (f32[40,1280]{1,0:T(8,128)}, f32[40,1280]{1,0:T(8,128)S(1)}, u32[]{:S(2)}, u32[]{:S(2)}) collective-permute-start(f32[40,1280]{1,0:T(8,128)} %get-tuple-element.98), channel_id=1, source_target_pairs={{0,16},{1,17},{2,18},{3,19},{4,20},{5,21},{6,22},{7,23},{8,24},{9,... | collective-permute-start | bytes 614408 | tf_op jit(solution)/shard_map/direct/ppermute | solution.py:28
  194.7 12.4 %collective-permute-start.38 = (f32[40,1280]{1,0:T(8,128)}, f32[40,1280]{1,0:T(8,128)S(1)}, u32[]{:S(2)}, u32[]{:S(2)}) collective-permute-start(f32[40,1280]{1,0:T(8,128)} %get-tuple-element.99), channel_id=1, source_target_pairs={{0,24},{1,25},{2,26},{3,27},{4,28},{5,29},{6,30},{7,31},{8,16},{9,... | collective-permute-start | bytes 614408 | tf_op jit(solution)/shard_map/direct/ppermute | solution.py:28
  (44 other events, 290.1 us)

commit v11 on v10

--- a/solution.py
+++ b/solution.py
@@ -227,7 +227,7 @@
         )
         slots = [pieces[0]] + [flip(pieces[q], y=q) for q in (1, 2, 3)]
     with jax.named_scope("density_turn"):
-        halves = density.reshape(2, 2, 40, 1280)
+        halves, _ = lax.optimization_barrier((density.reshape(2, 2, 40, 1280), pieces))
         same = lax.dynamic_index_in_dim(halves, xh, 1, keepdims=False).reshape(80, 1280)
         other = lax.dynamic_index_in_dim(halves, 1 - xh, 1, keepdims=False).reshape(80, 1280)
         other = flip(other, xh=1)
@@ -236,8 +236,9 @@
         parts = local_call(
             right_kernel, "right_columns", shape(bf16, 8, 160, 320), coords, first, second
         )
-        parts, other = lax.optimization_barrier((parts, other))
+        parts, slots[1] = lax.optimization_barrier((parts, slots[1]))
     with jax.named_scope("left_pair"):
+        slots[2], other = lax.optimization_barrier((slots[2], other))
         came = local_call(pass_kernel, "left_pass", shape(bf16, 640, 320), coords, *slots)
         came = flip(came, core=1)
         left = local_call(pair_kernel, "left_pair", shape(bf16, 640, 640), coords, *slots, came)

time: 213 us -> 217 us (1.019)
  starting transfers between devices: 65.8 us -> 71.1 us
  waiting for transfers between devices: 91.9 us -> 87.2 us
  other arithmetic: 7.27 us -> 10.2 us
    ppermute x31, starting transfers between devices: 34.2 us -> 39.5 us  [flip(): return lax.ppermute(value, AXES, pairs)]
    ppermute x31, waiting for transfers between devices: 87.2 us -> 82.6 us  [flip(): return lax.ppermute(value, AXES, pairs)]
    unnamed x68 -> x74, local copies, waits for them, and re-layouts: 6.53 us -> 8.71 us
  transfers between devices with their start and end apart: 42 -> 42, of which waited for: 24 -> 21; matrix products, arithmetic and copies ran while one was open for 4% -> 5% of each run, Pallas kernels for 11% -> 10%
where the time goes in v11:
time: 217 us
  waiting for transfers between devices  87.2 us (40%)
  starting transfers between devices  71.1 us (33%)
  Pallas kernels  30.3 us (14%)
  local copies, waits for them, and re-layouts  12 us (6%)
  other arithmetic  10.2 us (5%)
  matrix products  5.35 us (2%)
    ppermute x31, waiting for transfers between devices, flip(): return lax.ppermute(value, AXES, pairs)  82.6 us
    ppermute x31, starting transfers between devices, flip(): return lax.ppermute(value, AXES, pairs)  39.5 us
    pallas_call x10, Pallas kernels, local_call(): pl.pallas_call(kernel, out_shape=outs, in_specs=[SMEM] + [VMEM] * len(ope...  30.3 us
    ppermute x8, starting transfers between devices, remap(): return lax.ppermute(value, AXES, pairs)  15.5 us
    unnamed x74, local copies, waits for them, and re-layouts  8.71 us
    all_to_all x1, starting transfers between devices, shards(): lax.all_to_all(turned, ('z', 'xl', 'core', 'xh'), split_axis=0, concat_ax...  6.79 us
    select_n x2, other arithmetic, shards(): mine = [jnp.where(core == 0, lefts[0, r], lefts[1, r]) for r in range(2)]  4.93 us
    all_to_all x1, starting transfers between devices, shards(): lax.all_to_all(parts, ('xl', 'core', 'xh'), split_axis=0, concat_axis=0,...  4.83 us
  transfers between devices with their start and end apart: 42, of which 21 were waited for; matrix products, arithmetic and copies ran while one was open for 5% of the time, Pallas kernels for 10%

profile of v11, /device:TPU:2, one launch (start us, length us, event | category | flops | bytes accessed | tf_op | source)
XLA Modules:
  0.0 216.5 jit_solution(4360349662668165626)
XLA Ops:
  4.5 2.7 %right_columns.1 = bf16[8,160,320]{2,1,0:T(8,128)(2,1)} custom-call(s32[5]{0:T(128)} %stack.38.at_ref, bf16[160,1280]{1,0:T(8,128)(2,1)} %first_ref.2, bf16[160,1280]{1,0:T(8,128)(2,1)} %second_ref.2), custom_call_target="tpu_custom_call" | custom-call | tf_op jit(solution)/shard_map/right_columns/right_columns/pallas_call | solution.py:58
  7.2 2.7 %collective-permute-done.refs_1_ = bf16[160,640]{1,0:T(8,128)(2,1)S(1)} collective-permute-done((bf16[160,640]{1,0:T(8,128)(2,1)}, bf16[160,640]{1,0:T(8,128)(2,1)S(1)}, u32[]{:S(2)}, u32[]{:S(2)}) %collective-permute-start) | collective-permute-done | bytes 204832 | tf_op jit(solution)/shard_map/left_columns/ppermute | solution.py:28
  9.9 4.8 %all-to-all-start = ((bf16[8,160,320]{2,1,0:T(8,128)(2,1)}), bf16[8,160,320]{2,1,0:T(8,128)(2,1)S(1)}, u32[]{:S(2)}, u32[]{:S(2)}) async-start(bf16[8,160,320]{2,1,0:T(8,128)(2,1)} %right_columns.1), calls=%async_computation | async-start | bytes 1966080 | tf_op jit(solution)/shard_map/right_gather/all_to_all | solution.py:246
  17.6 3.2 %collective-permute-start.1 = (bf16[160,640]{1,0:T(8,128)(2,1)S(1)}, bf16[160,640]{1,0:T(8,128)(2,1)S(1)}, u32[]{:S(2)}, u32[]{:S(2)}) collective-permute-start(bf16[160,640]{1,0:T(8,128)(2,1)S(1)} %copy-done.35), channel_id=1, source_target_pairs={{0,16},{1,17},{2,18},{3,19},{4,20},{5,21},{6,22},{7,23},{8,24},{9,... | collective-permute-start | bytes 614408 | tf_op jit(solution)/shard_map/left_columns/ppermute | solution.py:28
  21.8 11.2 %collective-permute-done.2.other_ref = bf16[80,1280]{1,0:T(8,128)(2,1)S(1)} collective-permute-done((bf16[80,1280]{1,0:T(8,128)(2,1)S(1)}, bf16[80,1280]{1,0:T(8,128)(2,1)S(1)}, u32[]{:S(2)}, u32[]{:S(2)}) %collective-permute-start.2) | collective-permute-done | bytes 204832 | tf_op jit(solution)/shard_map/density_turn/ppermute | solution.py:28
  39.6 2.5 %left_pair.1 = bf16[640,640]{1,0:T(8,128)(2,1)} custom-call(s32[5]{0:T(128)} %stack.38.at_ref, bf16[160,640]{1,0:T(8,128)(2,1)} %get-tuple-element.56.refs_0_, bf16[160,640]{1,0:T(8,128)(2,1)} %copy-done.11, bf16[160,640]{1,0:T(8,128)(2,1)} %copy-done.12, bf16[160,640]{1,0:T(8,128)(2,1)} %copy-done.13, bf16[640,320]{1,0:T(8,128)(2,1)} %copy-done.18), custom_call_target="tpu_custom_call" | custom-call | tf_op jit(solution)/shard_map/left_pair/left_pair/pallas_call | solution.py:58
  47.0 4.0 %collective-permute-start.10 = (bf16[320,1280]{1,0:T(8,128)(2,1)S(1)}, bf16[320,1280]{1,0:T(8,128)(2,1)}, u32[]{:S(2)}, u32[]{:S(2)}) collective-permute-start(bf16[320,1280]{1,0:T(8,128)(2,1)S(1)} %reshape.58), channel_id=1, source_target_pairs={{0,96},{1,97},{2,98},{3,99},{4,100},{5,101},{6,102},{7,103},{8,104... | collective-permute-start | bytes 2457608 | tf_op jit(solution)/shard_map/right_gather/ppermute | solution.py:28
  51.0 13.6 %collective-permute-done.5 = bf16[640,640]{1,0:T(8,128)(2,1)S(1)} collective-permute-done((bf16[640,640]{1,0:T(8,128)(2,1)S(1)}, bf16[640,640]{1,0:T(8,128)(2,1)S(1)}, u32[]{:S(2)}, u32[]{:S(2)}) %collective-permute-start.5) | collective-permute-done | bytes 819232 | tf_op jit(solution)/shard_map/left_gather/ppermute | solution.py:28
  64.6 3.9 %collective-permute-start.9 = (bf16[320,1280]{1,0:T(8,128)(2,1)S(1)}, bf16[320,1280]{1,0:T(8,128)(2,1)}, u32[]{:S(2)}, u32[]{:S(2)}) collective-permute-start(bf16[320,1280]{1,0:T(8,128)(2,1)S(1)} %reshape.58), channel_id=1, source_target_pairs={{0,64},{1,65},{2,66},{3,67},{4,68},{5,69},{6,70},{7,71},{8,72},{9,... | collective-permute-start | bytes 2457608 | tf_op jit(solution)/shard_map/right_gather/ppermute | solution.py:28
  70.4 4.5 %all-to-all-start.1 = ((bf16[4,80,640]{2,1,0:T(8,128)(2,1)}), bf16[4,80,640]{2,1,0:T(8,128)(2,1)S(1)}, u32[]{:S(2)}, u32[]{:S(2)}) async-start(bf16[4,80,640]{2,1,0:T(8,128)(2,1)} %density_columns.1), calls=%async_computation.1 | async-start | bytes 819200 | tf_op jit(solution)/shard_map/density_columns/all_to_all | solution.py:265
  74.9 2.5 %broadcast_select_fusion.3 = (bf16[640,640]{1,0:T(8,128)(2,1)}, bf16[640,640]{1,0:T(8,128)(2,1)}) fusion(bf16[640,640]{1,0:T(8,128)(2,1)S(1)} %copy-done.2, bf16[640,640]{1,0:T(8,128)(2,1)} %copy-done.15, pred[]{:T(512)S(6)} %eq.8), kind=kLoop, calls=%fused_computation.27 | loop fusion | flops 819200 | bytes 3276801 | tf_op jit(solution)/shard_map/first_product/jit(_where)/select_n | solution.py:279
  77.4 3.8 %collective-permute-done.6 = bf16[640,640]{1,0:T(8,128)(2,1)} collective-permute-done((bf16[640,640]{1,0:T(8,128)(2,1)S(1)}, bf16[640,640]{1,0:T(8,128)(2,1)}, u32[]{:S(2)}, u32[]{:S(2)}) %collective-permute-start.6) | collective-permute-done | bytes 819232 | tf_op jit(solution)/shard_map/left_gather/ppermute | solution.py:28
  82.6 2.4 %broadcast_select_fusion.2 = (bf16[640,640]{1,0:T(8,128)(2,1)S(1)}, bf16[640,640]{1,0:T(8,128)(2,1)}) fusion(bf16[640,640]{1,0:T(8,128)(2,1)} %collective-permute-done.6, bf16[640,640]{1,0:T(8,128)(2,1)} %collective-permute-done.7, pred[]{:T(512)S(6)} %eq.8), kind=kLoop, calls=%fused_computation.26 | loop fusion | flops 819200 | bytes 3276801 | tf_op jit(solution)/shard_map/first_product/jit(_where)/select_n | solution.py:279
  85.0 2.4 %collective-permute-done.9 = bf16[320,1280]{1,0:T(8,128)(2,1)} collective-permute-done((bf16[320,1280]{1,0:T(8,128)(2,1)S(1)}, bf16[320,1280]{1,0:T(8,128)(2,1)}, u32[]{:S(2)}, u32[]{:S(2)}) %collective-permute-start.9) | collective-permute-done | bytes 819232 | tf_op jit(solution)/shard_map/right_gather/ppermute | solution.py:28
  94.1 3.1 %collective-permute-start.16 = (bf16[320,640]{1,0:T(8,128)(2,1)S(1)}, bf16[320,640]{1,0:T(8,128)(2,1)S(1)}, u32[]{:S(2)}, u32[]{:S(2)}) collective-permute-start(bf16[320,640]{1,0:T(8,128)(2,1)S(1)} %bitcast.30), channel_id=1, source_target_pairs={{0,96},{1,97},{2,98},{3,99},{4,100},{5,101},{6,102},{7,103},{8,104... | collective-permute-start | bytes 1228808 | tf_op jit(solution)/shard_map/density_gather/ppermute | solution.py:28
  107.1 5.6 %collective-permute-done.13 = f32[80,1280]{1,0:T(8,128)S(1)} collective-permute-done((f32[80,1280]{1,0:T(8,128)S(1)}, f32[80,1280]{1,0:T(8,128)S(1)}, u32[]{:S(2)}, u32[]{:S(2)}) %collective-permute-start.13) | collective-permute-done | bytes 409632 | tf_op jit(solution)/shard_map/mixed_sum/ppermute | solution.py:28
  112.7 2.5 %collective-permute-done.14 = f32[80,1280]{1,0:T(8,128)S(1)} collective-permute-done((f32[80,1280]{1,0:T(8,128)S(1)}, f32[80,1280]{1,0:T(8,128)S(1)}, u32[]{:S(2)}, u32[]{:S(2)}) %collective-permute-start.14) | collective-permute-done | bytes 409632 | tf_op jit(solution)/shard_map/mixed_sum/ppermute | solution.py:28
  121.0 5.3 %collective-permute-done.20.upper_ref = bf16[160,640]{1,0:T(8,128)(2,1)S(1)} collective-permute-done((bf16[160,640]{1,0:T(8,128)(2,1)S(1)}, bf16[160,640]{1,0:T(8,128)(2,1)S(1)}, u32[]{:S(2)}, u32[]{:S(2)}) %collective-permute-start.20) | collective-permute-done | bytes 204832 | tf_op jit(solution)/shard_map/density_gather/ppermute | solution.py:28
  129.2 2.7 %density_rows.1.mine_ref = bf16[1280,640]{1,0:T(8,128)(2,1)} custom-call(s32[5]{0:T(128)} %stack.38.at_ref, bf16[320,640]{1,0:T(8,128)(2,1)} %bitcast.31, bf16[320,640]{1,0:T(8,128)(2,1)} %copy-done.9, bf16[160,640]{1,0:T(8,128)(2,1)} %copy-done.28, bf16[160,640]{1,0:T(8,128)(2,1)} %copy-done.29, bf16[320,640]{1,0:T(8,128)(2,1)} %copy-done.10), custom_call_target="tpu_custom_call" | custom-call | tf_op jit(solution)/shard_map/density_rows/density_rows/pallas_call | solution.py:58
  131.9 3.8 %collective-permute-done.19 = f32[160,1280]{1,0:T(8,128)S(1)} collective-permute-done((f32[160,1280]{1,0:T(8,128)S(1)}, f32[160,1280]{1,0:T(8,128)S(1)}, u32[]{:S(2)}, u32[]{:S(2)}) %collective-permute-start.19) | collective-permute-done | bytes 819232 | tf_op jit(solution)/shard_map/mixed_sum/ppermute | solution.py:28
  140.6 12.0 %collective-permute-done.24.refs_2_ = bf16[160,1280]{1,0:T(8,128)(2,1)S(1)} collective-permute-done((bf16[160,1280]{1,0:T(8,128)(2,1)S(1)}, bf16[160,1280]{1,0:T(8,128)(2,1)S(1)}, u32[]{:S(2)}, u32[]{:S(2)}) %collective-permute-start.24) | collective-permute-done | bytes 409632 | tf_op jit(solution)/shard_map/mixed_gather/ppermute | solution.py:28
  156.0 5.4 %second_product.2 = (bf16[2,3,40,640]{3,2,1,0:T(8,128)(2,1)}, bf16[2,3,40,640]{3,2,1,0:T(8,128)(2,1)}, bf16[2,3,40,640]{3,2,1,0:T(8,128)(2,1)}, bf16[2,3,40,640]{3,2,1,0:T(8,128)(2,1)}) custom-call(s32[5]{0:T(128)} %stack.38.at_ref, bf16[1280,640]{1,0:T(8,128)(2,1)} %density_rows.1.mine_ref, bf16[1280,640]{1,0:T(8,128)(2,1)} %copy-done, ...), custom_call_target="tpu_custom_call" | custom-call | tf_op jit(solution)/shard_map/second_product/second_product/pallas_call | solution.py:58
  165.2 2.8 %collective-permute-start.30 = (bf16[2,3,40,640]{3,2,1,0:T(8,128)(2,1)}, bf16[2,3,40,640]{3,2,1,0:T(8,128)(2,1)S(1)}, u32[]{:S(2)}, u32[]{:S(2)}) collective-permute-start(bf16[2,3,40,640]{3,2,1,0:T(8,128)(2,1)} %get-tuple-element.94), channel_id=1, source_target_pairs={{0,1},{1,0},{2,7},{3,6},{4,5},{5,4},{6,3},{7,2},{8,9},{9,8},{10,15... | collective-permute-start | bytes 921608 | tf_op jit(solution)/shard_map/second_product/ppermute | solution.py:42
  168.0 3.7 %second_product.3 = (bf16[2,1,40,640]{3,2,1,0:T(8,128)(2,1)}, bf16[2,1,40,640]{3,2,1,0:T(8,128)(2,1)}, bf16[2,1,40,640]{3,2,1,0:T(8,128)(2,1)}, bf16[2,1,40,640]{3,2,1,0:T(8,128)(2,1)}) custom-call(s32[5]{0:T(128)} %stack.38.at_ref, bf16[1280,640]{1,0:T(8,128)(2,1)} %density_rows.1.mine_ref, bf16[1280,640]{1,0:T(8,128)(2,1)} %copy-done, ...), custom_call_target="tpu_custom_call" | custom-call | tf_op jit(solution)/shard_map/second_product/second_product/pallas_call | solution.py:58
  173.3 5.5 %collective-permute-start.33 = (bf16[2,1,40,640]{3,2,1,0:T(8,128)(2,1)}, bf16[2,1,40,640]{3,2,1,0:T(8,128)(2,1)S(1)}, u32[]{:S(2)}, u32[]{:S(2)}) collective-permute-start(bf16[2,1,40,640]{3,2,1,0:T(8,128)(2,1)} %get-tuple-element.99), channel_id=1, source_target_pairs={{0,2},{1,3},{2,4},{3,5},{4,6},{5,7},{6,0},{7,1},{8,10},{9,11},{10,... | collective-permute-start | bytes 307208 | tf_op jit(solution)/shard_map/second_product/ppermute | solution.py:42
  182.3 2.9 %collective-permute-done.34.refs_6_ = bf16[2,1,40,640]{3,2,1,0:T(8,128)(2,1)S(1)} collective-permute-done((bf16[2,1,40,640]{3,2,1,0:T(8,128)(2,1)}, bf16[2,1,40,640]{3,2,1,0:T(8,128)(2,1)S(1)}, u32[]{:S(2)}, u32[]{:S(2)}) %collective-permute-start.34) | collective-permute-done | bytes 102432 | tf_op jit(solution)/shard_map/second_product/ppermute | solution.py:42
  186.5 2.9 %spread.1 = (bf16[32,40,160]{2,1,0:T(8,128)(2,1)}, f32[40,1280]{1,0:T(8,128)}, f32[40,1280]{1,0:T(8,128)}, f32[40,1280]{1,0:T(8,128)}, f32[40,1280]{1,0:T(8,128)}) custom-call(s32[5]{0:T(128)} %stack.38.at_ref, bf16[2,3,40,640]{3,2,1,0:T(8,128)(2,1)} %copy-done.19, bf16[2,3,40,640]{3,2,1,0:T(8,128)(2,1)} %copy-done.21, bf16[2,3,40,640]{3,2,1,0:T(8,128)(2,1)} %copy-done.22, ...), custom_call_target="tpu_custom_call" | custom-call | tf_op jit(solution)/shard_map/second_product/spread/pallas_call | solution.py:58
  189.4 6.8 %all-to-all-start.2 = ((bf16[32,40,160]{2,1,0:T(8,128)(2,1)}), bf16[32,40,160]{2,1,0:T(8,128)(2,1)S(1)}, u32[]{:S(2)}, u32[]{:S(2)}) async-start(bf16[32,40,160]{2,1,0:T(8,128)(2,1)} %get-tuple-element.106), calls=%async_computation.2 | async-start | bytes 1310720 | tf_op jit(solution)/shard_map/transposed/all_to_all | solution.py:357
  201.8 2.6 %collective-permute-done.36.d1 = f32[40,1280]{1,0:T(8,128)S(1)} collective-permute-done((f32[40,1280]{1,0:T(8,128)}, f32[40,1280]{1,0:T(8,128)S(1)}, u32[]{:S(2)}, u32[]{:S(2)}) %collective-permute-start.36) | collective-permute-done | bytes 204832 | tf_op jit(solution)/shard_map/direct/ppermute | solution.py:28
  204.4 4.8 %collective-permute-done.37.d2 = f32[40,1280]{1,0:T(8,128)S(1)} collective-permute-done((f32[40,1280]{1,0:T(8,128)}, f32[40,1280]{1,0:T(8,128)S(1)}, u32[]{:S(2)}, u32[]{:S(2)}) %collective-permute-start.37) | collective-permute-done | bytes 204832 | tf_op jit(solution)/shard_map/direct/ppermute | solution.py:28
  209.2 2.6 %collective-permute-done.38.d3 = f32[40,1280]{1,0:T(8,128)S(1)} collective-permute-done((f32[40,1280]{1,0:T(8,128)}, f32[40,1280]{1,0:T(8,128)S(1)}, u32[]{:S(2)}, u32[]{:S(2)}) %collective-permute-start.38) | collective-permute-done | bytes 204832 | tf_op jit(solution)/shard_map/direct/ppermute | solution.py:28
  212.7 3.9 %finish.1 = f32[40,5120]{1,0:T(8,128)} custom-call(s32[5]{0:T(128)} %stack.38.at_ref, f32[40,1280]{1,0:T(8,128)} %get-tuple-element.102.d0, f32[40,1280]{1,0:T(8,128)} %copy-done.23, f32[40,1280]{1,0:T(8,128)} %copy-done.24, f32[40,1280]{1,0:T(8,128)} %copy-done.25, bf16[32,40,160]{2,1,0:T(8,128)(2,1)} %copy-done.3, f32[40,40]{1,0:T(8,128)} %fusion.11.kept_ref), custom_call_target="tpu_custom_call" | custom-call | tf_op jit(solution)/shard_map/finish/pallas_call | solution.py:58
  (159 shorter events, 72.9 us)
Async XLA Ops:
  9.9 32.2 %all-to-all-start = ((bf16[8,160,320]{2,1,0:T(8,128)(2,1)}), bf16[8,160,320]{2,1,0:T(8,128)(2,1)S(1)}, u32[]{:S(2)}, u32[]{:S(2)}) async-start(bf16[8,160,320]{2,1,0:T(8,128)(2,1)} %right_columns.1), calls=%async_computation | async-start | bytes 1966080 | tf_op jit(solution)/shard_map/right_gather/all_to_all | solution.py:246
  15.5 17.6 %collective-permute-start.2 = (bf16[80,1280]{1,0:T(8,128)(2,1)S(1)}, bf16[80,1280]{1,0:T(8,128)(2,1)S(1)}, u32[]{:S(2)}, u32[]{:S(2)}) collective-permute-start(bf16[80,1280]{1,0:T(8,128)(2,1)S(1)} %bitcast.33), channel_id=1, source_target_pairs={{0,1},{1,0},{2,3},{3,2},{4,5},{5,4},{6,7},{7,6},{8,9},{9,8},{10,11... | collective-permute-start | bytes 614408 | tf_op jit(solution)/shard_map/density_turn/ppermute | solution.py:28
  17.6 15.5 %collective-permute-start.1 = (bf16[160,640]{1,0:T(8,128)(2,1)S(1)}, bf16[160,640]{1,0:T(8,128)(2,1)S(1)}, u32[]{:S(2)}, u32[]{:S(2)}) collective-permute-start(bf16[160,640]{1,0:T(8,128)(2,1)S(1)} %copy-done.35), channel_id=1, source_target_pairs={{0,16},{1,17},{2,18},{3,19},{4,20},{5,21},{6,22},{7,23},{8,24},{9,... | collective-permute-start | bytes 614408 | tf_op jit(solution)/shard_map/left_columns/ppermute | solution.py:28
  20.8 12.3 %collective-permute-start.3 = (bf16[160,640]{1,0:T(8,128)(2,1)S(1)}, bf16[160,640]{1,0:T(8,128)(2,1)S(1)}, u32[]{:S(2)}, u32[]{:S(2)}) collective-permute-start(bf16[160,640]{1,0:T(8,128)(2,1)S(1)} %copy-done.34), channel_id=1, source_target_pairs={{0,24},{1,25},{2,26},{3,27},{4,28},{5,29},{6,30},{7,31},{8,16},{9,... | collective-permute-start | bytes 614408 | tf_op jit(solution)/shard_map/left_columns/ppermute | solution.py:28
  43.4 21.2 %collective-permute-start.5 = (bf16[640,640]{1,0:T(8,128)(2,1)S(1)}, bf16[640,640]{1,0:T(8,128)(2,1)S(1)}, u32[]{:S(2)}, u32[]{:S(2)}) collective-permute-start(bf16[640,640]{1,0:T(8,128)(2,1)S(1)} %copy-done.2), channel_id=1, source_target_pairs={{0,4},{1,5},{2,6},{3,7},{4,0},{5,1},{6,2},{7,3},{8,12},{9,13},{10,... | collective-permute-start | bytes 2457608 | tf_op jit(solution)/shard_map/left_gather/ppermute | solution.py:28
  44.9 36.2 %collective-permute-start.6 = (bf16[640,640]{1,0:T(8,128)(2,1)S(1)}, bf16[640,640]{1,0:T(8,128)(2,1)}, u32[]{:S(2)}, u32[]{:S(2)}) collective-permute-start(bf16[640,640]{1,0:T(8,128)(2,1)S(1)} %copy-done.2), channel_id=1, source_target_pairs={{0,1},{1,0},{2,3},{3,2},{4,5},{5,4},{6,7},{7,6},{8,9},{9,8},{10,11... | collective-permute-start | bytes 2457608 | tf_op jit(solution)/shard_map/left_gather/ppermute | solution.py:28
  45.0 37.5 %collective-permute-start.7 = (bf16[640,640]{1,0:T(8,128)(2,1)S(1)}, bf16[640,640]{1,0:T(8,128)(2,1)}, u32[]{:S(2)}, u32[]{:S(2)}) collective-permute-start(bf16[640,640]{1,0:T(8,128)(2,1)S(1)} %copy-done.2), channel_id=1, source_target_pairs={{0,5},{1,4},{2,7},{3,6},{4,1},{5,0},{6,3},{7,2},{8,13},{9,12},{10,... | collective-permute-start | bytes 2457608 | tf_op jit(solution)/shard_map/left_gather/ppermute | solution.py:28
  47.0 38.0 %collective-permute-start.10 = (bf16[320,1280]{1,0:T(8,128)(2,1)S(1)}, bf16[320,1280]{1,0:T(8,128)(2,1)}, u32[]{:S(2)}, u32[]{:S(2)}) collective-permute-start(bf16[320,1280]{1,0:T(8,128)(2,1)S(1)} %reshape.58), channel_id=1, source_target_pairs={{0,96},{1,97},{2,98},{3,99},{4,100},{5,101},{6,102},{7,103},{8,104... | collective-permute-start | bytes 2457608 | tf_op jit(solution)/shard_map/right_gather/ppermute | solution.py:28
  51.0 34.0 %collective-permute-start.8 = (bf16[320,1280]{1,0:T(8,128)(2,1)S(1)}, bf16[320,1280]{1,0:T(8,128)(2,1)}, u32[]{:S(2)}, u32[]{:S(2)}) collective-permute-start(bf16[320,1280]{1,0:T(8,128)(2,1)S(1)} %reshape.58), channel_id=1, source_target_pairs={{0,32},{1,33},{2,34},{3,35},{4,36},{5,37},{6,38},{7,39},{8,40},{9,... | collective-permute-start | bytes 2457608 | tf_op jit(solution)/shard_map/right_gather/ppermute | solution.py:28
  64.6 22.8 %collective-permute-start.9 = (bf16[320,1280]{1,0:T(8,128)(2,1)S(1)}, bf16[320,1280]{1,0:T(8,128)(2,1)}, u32[]{:S(2)}, u32[]{:S(2)}) collective-permute-start(bf16[320,1280]{1,0:T(8,128)(2,1)S(1)} %reshape.58), channel_id=1, source_target_pairs={{0,64},{1,65},{2,66},{3,67},{4,68},{5,69},{6,70},{7,71},{8,72},{9,... | collective-permute-start | bytes 2457608 | tf_op jit(solution)/shard_map/right_gather/ppermute | solution.py:28
  70.4 17.0 %all-to-all-start.1 = ((bf16[4,80,640]{2,1,0:T(8,128)(2,1)}), bf16[4,80,640]{2,1,0:T(8,128)(2,1)S(1)}, u32[]{:S(2)}, u32[]{:S(2)}) async-start(bf16[4,80,640]{2,1,0:T(8,128)(2,1)} %density_columns.1), calls=%async_computation.1 | async-start | bytes 819200 | tf_op jit(solution)/shard_map/density_columns/all_to_all | solution.py:265
  94.1 11.8 %collective-permute-start.15 = (bf16[320,640]{1,0:T(8,128)(2,1)S(1)}, bf16[320,640]{1,0:T(8,128)(2,1)S(1)}, u32[]{:S(2)}, u32[]{:S(2)}) collective-permute-start(bf16[320,640]{1,0:T(8,128)(2,1)S(1)} %bitcast.29), channel_id=1, source_target_pairs={{0,32},{1,33},{2,34},{3,35},{4,36},{5,37},{6,38},{7,39},{8,40},{9,... | collective-permute-start | bytes 1228808 | tf_op jit(solution)/shard_map/density_gather/ppermute | solution.py:28
  94.1 13.0 %collective-permute-start.16 = (bf16[320,640]{1,0:T(8,128)(2,1)S(1)}, bf16[320,640]{1,0:T(8,128)(2,1)S(1)}, u32[]{:S(2)}, u32[]{:S(2)}) collective-permute-start(bf16[320,640]{1,0:T(8,128)(2,1)S(1)} %bitcast.30), channel_id=1, source_target_pairs={{0,96},{1,97},{2,98},{3,99},{4,100},{5,101},{6,102},{7,103},{8,104... | collective-permute-start | bytes 1228808 | tf_op jit(solution)/shard_map/density_gather/ppermute | solution.py:28
  101.3 11.4 %collective-permute-start.13 = (f32[80,1280]{1,0:T(8,128)S(1)}, f32[80,1280]{1,0:T(8,128)S(1)}, u32[]{:S(2)}, u32[]{:S(2)}) collective-permute-start(f32[80,1280]{1,0:T(8,128)S(1)} %get-tuple-element.127), channel_id=1, source_target_pairs={{0,8},{1,9},{2,10},{3,11},{4,12},{5,13},{6,14},{7,15},{8,0},{9,1},... | collective-permute-start | bytes 1228808 | tf_op jit(solution)/shard_map/mixed_sum/ppermute | solution.py:28
  103.0 12.3 %collective-permute-start.14 = (f32[80,1280]{1,0:T(8,128)S(1)}, f32[80,1280]{1,0:T(8,128)S(1)}, u32[]{:S(2)}, u32[]{:S(2)}) collective-permute-start(f32[80,1280]{1,0:T(8,128)S(1)} %get-tuple-element.126), channel_id=1, source_target_pairs={{0,24},{1,25},{2,26},{3,27},{4,28},{5,29},{6,30},{7,31},{8,16},{9,... | collective-permute-start | bytes 1228808 | tf_op jit(solution)/shard_map/mixed_sum/ppermute | solution.py:28
  115.5 20.2 %collective-permute-start.19 = (f32[160,1280]{1,0:T(8,128)S(1)}, f32[160,1280]{1,0:T(8,128)S(1)}, u32[]{:S(2)}, u32[]{:S(2)}) collective-permute-start(f32[160,1280]{1,0:T(8,128)S(1)} %pad_maximum_fusion.3), channel_id=1, source_target_pairs={{0,24},{1,25},{2,26},{3,27},{4,28},{5,29},{6,30},{7,31},{8,16},{9,... | collective-permute-start | bytes 2457608 | tf_op jit(solution)/shard_map/mixed_sum/ppermute | solution.py:28
  118.7 19.0 %collective-permute-start.17 = (f32[160,1280]{1,0:T(8,128)}, f32[160,1280]{1,0:T(8,128)}, u32[]{:S(2)}, u32[]{:S(2)}) collective-permute-start(f32[160,1280]{1,0:T(8,128)} %pad_maximum_fusion.2), channel_id=1, source_target_pairs={{0,8},{1,9},{2,10},{3,11},{4,12},{5,13},{6,14},{7,15},{8,0},{9,1},... | collective-permute-start | bytes 2457608 | tf_op jit(solution)/shard_map/mixed_sum/ppermute | solution.py:28
  118.7 19.0 %collective-permute-start.23 = (f32[160,1280]{1,0:T(8,128)S(1)}, f32[160,1280]{1,0:T(8,128)}, u32[]{:S(2)}, u32[]{:S(2)}) collective-permute-start(f32[160,1280]{1,0:T(8,128)S(1)} %get-tuple-element.107), channel_id=1, source_target_pairs={{0,2},{1,3},{2,0},{3,1},{4,6},{5,7},{6,4},{7,5},{8,10},{9,11},{10,... | collective-permute-start | bytes 2457608 | tf_op jit(solution)/shard_map/mixed_sum/ppermute | solution.py:28
  120.0 8.5 %collective-permute-start.21 = (bf16[160,640]{1,0:T(8,128)(2,1)S(1)}, bf16[160,640]{1,0:T(8,128)(2,1)S(1)}, u32[]{:S(2)}, u32[]{:S(2)}) collective-permute-start(bf16[160,640]{1,0:T(8,128)(2,1)S(1)} %slice.75), channel_id=1, source_target_pairs={{0,96},{1,97},{2,98},{3,99},{4,100},{5,101},{6,102},{7,103},{8,104... | collective-permute-start | bytes 614408 | tf_op jit(solution)/shard_map/density_gather/ppermute | solution.py:28
  137.7 17.1 %collective-permute-start.22 = (bf16[1280,640]{1,0:T(8,128)(2,1)}, bf16[1280,640]{1,0:T(8,128)(2,1)S(1)}, u32[]{:S(2)}, u32[]{:S(2)}) collective-permute-start(bf16[1280,640]{1,0:T(8,128)(2,1)} %density_rows.1.mine_ref), channel_id=1, source_target_pairs={{0,2},{1,3},{2,0},{3,1},{4,6},{5,7},{6,4},{7,5},{8,10},{9,11},{10,... | collective-permute-start | bytes 4915208 | tf_op jit(solution)/shard_map/mixed_gather/ppermute | solution.py:28
  139.5 13.2 %collective-permute-start.24 = (bf16[160,1280]{1,0:T(8,128)(2,1)S(1)}, bf16[160,1280]{1,0:T(8,128)(2,1)S(1)}, u32[]{:S(2)}, u32[]{:S(2)}) collective-permute-start(bf16[160,1280]{1,0:T(8,128)(2,1)S(1)} %fusion.10.refs_0_), channel_id=1, source_target_pairs={{0,24},{1,25},{2,26},{3,27},{4,28},{5,29},{6,30},{7,31},{8,16},{9,... | collective-permute-start | bytes 1228808 | tf_op jit(solution)/shard_map/mixed_gather/ppermute | solution.py:28
  140.6 12.1 %collective-permute-start.25 = (bf16[160,1280]{1,0:T(8,128)(2,1)S(1)}, bf16[160,1280]{1,0:T(8,128)(2,1)S(1)}, u32[]{:S(2)}, u32[]{:S(2)}) collective-permute-start(bf16[160,1280]{1,0:T(8,128)(2,1)S(1)} %fusion.10.refs_0_), channel_id=1, source_target_pairs={{0,8},{1,9},{2,10},{3,11},{4,12},{5,13},{6,14},{7,15},{8,0},{9,1},... | collective-permute-start | bytes 1228808 | tf_op jit(solution)/shard_map/mixed_gather/ppermute | solution.py:28
  152.7 10.2 %collective-permute-start.27 = (bf16[80,1280]{1,0:T(8,128)(2,1)S(1)}, bf16[80,1280]{1,0:T(8,128)(2,1)S(1)}, u32[]{:S(2)}, u32[]{:S(2)}) collective-permute-start(bf16[80,1280]{1,0:T(8,128)(2,1)S(1)} %slice.94), channel_id=1, source_target_pairs={{0,8},{1,9},{2,10},{3,11},{4,12},{5,13},{6,14},{7,15},{8,0},{9,1},... | collective-permute-start | bytes 614408 | tf_op jit(solution)/shard_map/mixed_gather/ppermute | solution.py:28
  152.8 10.2 %collective-permute-start.28 = (bf16[80,1280]{1,0:T(8,128)(2,1)S(1)}, bf16[80,1280]{1,0:T(8,128)(2,1)}, u32[]{:S(2)}, u32[]{:S(2)}) collective-permute-start(bf16[80,1280]{1,0:T(8,128)(2,1)S(1)} %slice.95), channel_id=1, source_target_pairs={{0,24},{1,25},{2,26},{3,27},{4,28},{5,29},{6,30},{7,31},{8,16},{9,... | collective-permute-start | bytes 614408 | tf_op jit(solution)/shard_map/mixed_gather/ppermute | solution.py:28
  163.0 15.8 %collective-permute-start.31 = (bf16[2,3,40,640]{3,2,1,0:T(8,128)(2,1)}, bf16[2,3,40,640]{3,2,1,0:T(8,128)(2,1)S(1)}, u32[]{:S(2)}, u32[]{:S(2)}) collective-permute-start(bf16[2,3,40,640]{3,2,1,0:T(8,128)(2,1)} %get-tuple-element.95), channel_id=1, source_target_pairs={{0,3},{1,2},{2,5},{3,4},{4,7},{5,6},{6,1},{7,0},{8,11},{9,10},{10,... | collective-permute-start | bytes 921608 | tf_op jit(solution)/shard_map/second_product/ppermute | solution.py:42
  165.2 14.3 %collective-permute-start.29 = (bf16[2,3,40,640]{3,2,1,0:T(8,128)(2,1)}, bf16[2,3,40,640]{3,2,1,0:T(8,128)(2,1)S(1)}, u32[]{:S(2)}, u32[]{:S(2)}) collective-permute-start(bf16[2,3,40,640]{3,2,1,0:T(8,128)(2,1)} %get-tuple-element.93), channel_id=1, source_target_pairs={{0,2},{1,3},{2,4},{3,5},{4,6},{5,7},{6,0},{7,1},{8,10},{9,11},{10,... | collective-permute-start | bytes 921608 | tf_op jit(solution)/shard_map/second_product/ppermute | solution.py:42
  165.2 15.4 %collective-permute-start.30 = (bf16[2,3,40,640]{3,2,1,0:T(8,128)(2,1)}, bf16[2,3,40,640]{3,2,1,0:T(8,128)(2,1)S(1)}, u32[]{:S(2)}, u32[]{:S(2)}) collective-permute-start(bf16[2,3,40,640]{3,2,1,0:T(8,128)(2,1)} %get-tuple-element.94), channel_id=1, source_target_pairs={{0,1},{1,0},{2,7},{3,6},{4,5},{5,4},{6,3},{7,2},{8,9},{9,8},{10,15... | collective-permute-start | bytes 921608 | tf_op jit(solution)/shard_map/second_product/ppermute | solution.py:42
  171.8 8.9 %collective-permute-start.32 = (bf16[2,1,40,640]{3,2,1,0:T(8,128)(2,1)}, bf16[2,1,40,640]{3,2,1,0:T(8,128)(2,1)S(1)}, u32[]{:S(2)}, u32[]{:S(2)}) collective-permute-start(bf16[2,1,40,640]{3,2,1,0:T(8,128)(2,1)} %get-tuple-element.98), channel_id=1, source_target_pairs={{0,0},{1,1},{2,6},{3,7},{4,4},{5,5},{6,2},{7,3},{8,8},{9,9},{10,14... | collective-permute-start | bytes 307208 | tf_op jit(solution)/shard_map/second_product/ppermute | solution.py:42
  173.3 9.0 %collective-permute-start.33 = (bf16[2,1,40,640]{3,2,1,0:T(8,128)(2,1)}, bf16[2,1,40,640]{3,2,1,0:T(8,128)(2,1)S(1)}, u32[]{:S(2)}, u32[]{:S(2)}) collective-permute-start(bf16[2,1,40,640]{3,2,1,0:T(8,128)(2,1)} %get-tuple-element.99), channel_id=1, source_target_pairs={{0,2},{1,3},{2,4},{3,5},{4,6},{5,7},{6,0},{7,1},{8,10},{9,11},{10,... | collective-permute-start | bytes 307208 | tf_op jit(solution)/shard_map/second_product/ppermute | solution.py:42
  189.4 22.4 %all-to-all-start.2 = ((bf16[32,40,160]{2,1,0:T(8,128)(2,1)}), bf16[32,40,160]{2,1,0:T(8,128)(2,1)S(1)}, u32[]{:S(2)}, u32[]{:S(2)}) async-start(bf16[32,40,160]{2,1,0:T(8,128)(2,1)} %get-tuple-element.106), calls=%async_computation.2 | async-start | bytes 1310720 | tf_op jit(solution)/shard_map/transposed/all_to_all | solution.py:357
  197.1 12.1 %collective-permute-start.37 = (f32[40,1280]{1,0:T(8,128)}, f32[40,1280]{1,0:T(8,128)S(1)}, u32[]{:S(2)}, u32[]{:S(2)}) collective-permute-start(f32[40,1280]{1,0:T(8,128)} %get-tuple-element.104), channel_id=1, source_target_pairs={{0,16},{1,17},{2,18},{3,19},{4,20},{5,21},{6,22},{7,23},{8,24},{9,... | collective-permute-start | bytes 614408 | tf_op jit(solution)/shard_map/direct/ppermute | solution.py:28
  199.4 12.4 %collective-permute-start.38 = (f32[40,1280]{1,0:T(8,128)}, f32[40,1280]{1,0:T(8,128)S(1)}, u32[]{:S(2)}, u32[]{:S(2)}) collective-permute-start(f32[40,1280]{1,0:T(8,128)} %get-tuple-element.105), channel_id=1, source_target_pairs={{0,24},{1,25},{2,26},{3,27},{4,28},{5,29},{6,30},{7,31},{8,16},{9,... | collective-permute-start | bytes 614408 | tf_op jit(solution)/shard_map/direct/ppermute | solution.py:28
  (47 other events, 336.0 us)

commit v12 on v6

--- a/solution.py
+++ b/solution.py
@@ -110,11 +110,18 @@
         out_ref[ny] = jnp.concatenate((first[:, cut], second[:, cut]), axis=1)
 
 
-def rows_kernel(at_ref, *refs):
-    out_ref = refs[4]
+def rows_kernel(at_ref, own_ref, one_ref, upper_ref, lower_ref, three_ref, out_ref):
     z = at_ref[0]
-    for q in range(4):
-        out_ref[pl.ds(pl.multiple_of((z ^ q) * 320, 320), 320), :] = refs[q][...]
+
+    def place(q, start, count, ref):
+        first = pl.multiple_of((z ^ q) * 320 + start, 160)
+        out_ref[pl.ds(first, count), :] = ref[...]
+
+    place(0, 0, 320, own_ref)
+    place(1, 0, 320, one_ref)
+    place(2, 0, 160, upper_ref)
+    place(2, 160, 160, lower_ref)
+    place(3, 0, 320, three_ref)
 
 
 def join_kernel(at_ref, mine_ref, other_ref, out_ref):
@@ -237,32 +244,44 @@
             both[q] = mine[q] + flip(theirs[q], core=1)
         upper = flip(both[2][:80], y=1)
         lower = flip(both[2][80:], y=3)
+
+    with jax.named_scope("density_gather"):
+        done = flip(dslots, z=1)
+        dthree = flip(dslots, z=3)
+        upper, lower, done, dthree = lax.optimization_barrier((upper, lower, done, dthree))
+        dtwo = (flip(dthree[:160], z=1), flip(done[160:], z=3))
+
+    with jax.named_scope("mixed_sum"):
         third = jnp.concatenate((both[3][:80] + upper, both[3][80:]))
         first = jnp.concatenate((both[1][:80], both[1][80:] + lower))
         sums = [flip(first, y=1), flip(third, y=3)]
 
-    with jax.named_scope("density_gather"):
-        dslots, _ = lax.optimization_barrier((dslots, both))
-        dparts = [dslots] + [flip(dslots, z=q) for q in (1, 2, 3)]
+    with jax.named_scope("density_rows"):
+        dmine = local_call(
+            rows_kernel, "density_rows", shape(bf16, 1280, 640), coords, dslots, done, *dtwo, dthree
+        )
 
     with jax.named_scope("mixed_sum"):
-        sums, dparts = lax.optimization_barrier((sums, dparts))
+        sums, dmine = lax.optimization_barrier((sums, dmine))
         total = both[0] + sums[0] + sums[1]
         mixed = total.astype(bf16)
 
-    with jax.named_scope("density_rows"):
-        dmine = local_call(rows_kernel, "density_rows", shape(bf16, 1280, 640), coords, *dparts)
+    with jax.named_scope("mixed_gather"):
+        one, three = flip(mixed, y=1), flip(mixed, y=3)
+        dother = flip(dmine, core=1)
+        two = (three[:80], one[80:])
         dfull = local_call(
-            join_kernel, "density_join", shape(bf16, 1280, 1280), coords, dmine, flip(dmine, core=1)
-        )
-    with jax.named_scope("mixed_gather"):
-        mslots = [mixed] + [flip(mixed, y=q) for q in (1, 2, 3)]
+            join_kernel, "density_join", shape(bf16, 1280, 1280), coords, dmine, dother
+        )
+        two, one, three, dfull = lax.optimization_barrier((two, one, three, dfull))
+        two = (flip(two[0], y=1), flip(two[1], y=3))
 
     with jax.named_scope("second_product"):
+
         turns = [(r, t) for r in range(2) for t in range(2)]
 
-        def pieces_of(rows, count):
-            resp = dot(rows, dfull).reshape(count, 2, 2, 40, 1280)
+        def pieces_of(count, *rows):
+            resp = dot(jnp.concatenate(rows), dfull).reshape(count, 2, 2, 40, 1280)
             cut = []
             for r, t in turns:
                 piece = lax.dynamic_index_in_dim(resp, core ^ t, 1, keepdims=False)
@@ -276,10 +295,10 @@
                 for piece, (r, t) in zip(cut, turns)
             ]
 
-        many = pieces_of(jnp.concatenate((mslots[0], mslots[1], mslots[3])), 3)
-        many = scatter(many)
-        many[0], mslots[2] = lax.optimization_barrier((many[0], mslots[2]))
-        last = scatter(pieces_of(mslots[2], 1))
+        cut = list(pieces_of(3, mixed, one, three))
+        many = scatter(cut)
+        many[0], two = lax.optimization_barrier((many[0], two))
+        last = scatter(pieces_of(1, *two))
         turned, *rows = local_call(
             spread_kernel,
             "spread",

time: 215 us -> 219 us (1.019)
  waiting for transfers between devices: 89.1 us -> 102 us
  starting transfers between devices: 72.7 us -> 64.8 us
  local copies, waits for them, and re-layouts: 10.6 us -> 7.62 us
    ppermute x29 -> x31, waiting for transfers between devices: 83.8 us -> 93.9 us  [flip(): return lax.ppermute(value, AXES, pairs)]
    ppermute x8, starting transfers between devices: 18 us -> 10.9 us  [remap(): return lax.ppermute(value, AXES, pairs)]
    unnamed x56 -> x44, local copies, waits for them, and re-layouts: 7.26 us -> 3.27 us
    ppermute x8, waiting for transfers between devices: 5.27 us -> 8.38 us  [remap(): return lax.ppermute(value, AXES, pairs)]
    ppermute x29 -> x31, starting transfers between devices: 40.2 us -> 38.8 us  [flip(): return lax.ppermute(value, AXES, pairs)]
  transfers between devices with their start and end apart: 40 -> 42, of which waited for: 24 -> 25; matrix products, arithmetic and copies ran while one was open for 8% -> 6% of each run, Pallas kernels for 4% -> 3%
where the time goes in v12:
time: 219 us; the launch traced here: 218 us
  waiting for transfers between devices  102 us (47%)
  starting transfers between devices  64.8 us (30%)
  Pallas kernels  20.9 us (10%)
  other arithmetic  12.4 us (6%)
  matrix products  10 us (5%)
  local copies, waits for them, and re-layouts  7.62 us (3%)
    ppermute x31, waiting for transfers between devices, flip(): return lax.ppermute(value, AXES, pairs)  93.9 us
    ppermute x31, starting transfers between devices, flip(): return lax.ppermute(value, AXES, pairs)  38.8 us
    pallas_call x7, Pallas kernels, local_call(): pl.pallas_call(kernel, out_shape=outs, in_specs=[SMEM] + [VMEM] * len(ope...  20.9 us
    ppermute x8, starting transfers between devices, remap(): return lax.ppermute(value, AXES, pairs)  10.9 us
    dot_general x4, matrix products, dot(): return jnp.dot(a, b, preferred_element_type=f32)  9.23 us
    ppermute x8, waiting for transfers between devices, remap(): return lax.ppermute(value, AXES, pairs)  8.38 us
    all_to_all x1, starting transfers between devices, shards(): lax.all_to_all(turned, ('z', 'xl', 'core', 'xh'), split_axis=0, concat_ax...  5.69 us
    all_to_all x1, starting transfers between devices, shards(): lax.all_to_all(parts, ('xl', 'core', 'xh'), split_axis=0, concat_axis=0,...  4.92 us
  transfers between devices with their start and end apart: 42, of which 25 were waited for; matrix products, arithmetic and copies ran while one was open for 6% of the time, Pallas kernels for 3%

profile of v12, /device:TPU:2, one launch (start us, length us, event | category | flops | bytes accessed | tf_op | source)
XLA Modules:
  0.0 218.4 jit_solution(4353444336818315894)
XLA Ops:
  1.8 2.8 %right_columns.1 = bf16[8,160,320]{2,1,0:T(8,128)(2,1)} custom-call(s32[5]{0:T(128)} %stack.38.at_ref, bf16[160,1280]{1,0:T(8,128)(2,1)} %first_ref.1, bf16[160,1280]{1,0:T(8,128)(2,1)} %second_ref.1), custom_call_target="tpu_custom_call" | custom-call | tf_op jit(solution)/shard_map/right_columns/right_columns/pallas_call | solution.py:58
  5.4 2.6 %left_columns.1 = (bf16[160,640]{1,0:T(8,128)(2,1)}, bf16[160,640]{1,0:T(8,128)(2,1)}, bf16[160,640]{1,0:T(8,128)(2,1)}, bf16[160,640]{1,0:T(8,128)(2,1)}) custom-call(s32[5]{0:T(128)} %stack.38.at_ref, bf16[160,1280]{1,0:T(8,128)(2,1)} %first_ref.2, bf16[160,1280]{1,0:T(8,128)(2,1)} %second_ref.2, bf16[160,1280]{1,0:T(8,128)(2,1)} %copy-done.8), custom_call_target="tpu_custom_call" | custom-call | tf_op jit(solution)/shard_map/left_columns/left_columns/pallas_call | solution.py:58
  8.0 4.9 %all-to-all-start = ((bf16[8,160,320]{2,1,0:T(8,128)(2,1)}), bf16[8,160,320]{2,1,0:T(8,128)(2,1)S(1)}, u32[]{:S(2)}, u32[]{:S(2)}) async-start(bf16[8,160,320]{2,1,0:T(8,128)(2,1)} %right_columns.1), calls=%async_computation | async-start | bytes 1966080 | tf_op jit(solution)/shard_map/right_gather/all_to_all | solution.py:205
  12.9 3.0 %collective-permute-start.3 = (bf16[160,640]{1,0:T(8,128)(2,1)}, bf16[160,640]{1,0:T(8,128)(2,1)S(1)}, u32[]{:S(2)}, u32[]{:S(2)}) collective-permute-start(bf16[160,640]{1,0:T(8,128)(2,1)} %get-tuple-element.59), channel_id=1, source_target_pairs={{0,24},{1,25},{2,26},{3,27},{4,28},{5,29},{6,30},{7,31},{8,16},{9,... | collective-permute-start | bytes 614408 | tf_op jit(solution)/shard_map/left_columns/ppermute | solution.py:28
  19.8 6.1 %collective-permute-done.3 = bf16[160,640]{1,0:T(8,128)(2,1)S(1)} collective-permute-done((bf16[160,640]{1,0:T(8,128)(2,1)}, bf16[160,640]{1,0:T(8,128)(2,1)S(1)}, u32[]{:S(2)}, u32[]{:S(2)}) %collective-permute-start.3) | collective-permute-done | bytes 204832 | tf_op jit(solution)/shard_map/left_columns/ppermute | solution.py:28
  27.6 3.8 %collective-permute-done.4.other_ref = bf16[80,1280]{1,0:T(8,128)(2,1)} collective-permute-done((bf16[80,1280]{1,0:T(8,128)(2,1)S(1)}, bf16[80,1280]{1,0:T(8,128)(2,1)}, u32[]{:S(2)}, u32[]{:S(2)}) %collective-permute-start.4) | collective-permute-done | bytes 204832 | tf_op jit(solution)/shard_map/density_turn/ppermute | solution.py:28
  38.1 3.6 %collective-permute-start.9 = (bf16[320,1280]{1,0:T(8,128)(2,1)S(1)}, bf16[320,1280]{1,0:T(8,128)(2,1)}, u32[]{:S(2)}, u32[]{:S(2)}) collective-permute-start(bf16[320,1280]{1,0:T(8,128)(2,1)S(1)} %reshape.136), channel_id=1, source_target_pairs={{0,64},{1,65},{2,66},{3,67},{4,68},{5,69},{6,70},{7,71},{8,72},{9,... | collective-permute-start | bytes 2457608 | tf_op jit(solution)/shard_map/right_gather/ppermute | solution.py:28
  41.7 12.2 %collective-permute-done.5 = bf16[640,640]{1,0:T(8,128)(2,1)S(1)} collective-permute-done((bf16[640,640]{1,0:T(8,128)(2,1)S(1)}, bf16[640,640]{1,0:T(8,128)(2,1)S(1)}, u32[]{:S(2)}, u32[]{:S(2)}) %collective-permute-start.5) | collective-permute-done | bytes 819232 | tf_op jit(solution)/shard_map/left_gather/ppermute | solution.py:28
  53.8 4.0 %collective-permute-start.10 = (bf16[320,1280]{1,0:T(8,128)(2,1)S(1)}, bf16[320,1280]{1,0:T(8,128)(2,1)}, u32[]{:S(2)}, u32[]{:S(2)}) collective-permute-start(bf16[320,1280]{1,0:T(8,128)(2,1)S(1)} %reshape.136), channel_id=1, source_target_pairs={{0,96},{1,97},{2,98},{3,99},{4,100},{5,101},{6,102},{7,103},{8,104... | collective-permute-start | bytes 2457608 | tf_op jit(solution)/shard_map/right_gather/ppermute | solution.py:28
  59.8 4.5 %all-to-all-start.1 = ((bf16[4,80,640]{2,1,0:T(8,128)(2,1)}), bf16[4,80,640]{2,1,0:T(8,128)(2,1)}, u32[]{:S(2)}, u32[]{:S(2)}) async-start(bf16[4,80,640]{2,1,0:T(8,128)(2,1)} %density_columns.1), calls=%async_computation.1 | async-start | bytes 819200 | tf_op jit(solution)/shard_map/density_columns/all_to_all | solution.py:224
  65.6 4.3 %collective-permute-done.6 = bf16[640,640]{1,0:T(8,128)(2,1)} collective-permute-done((bf16[640,640]{1,0:T(8,128)(2,1)S(1)}, bf16[640,640]{1,0:T(8,128)(2,1)}, u32[]{:S(2)}, u32[]{:S(2)}) %collective-permute-start.6) | collective-permute-done | bytes 819232 | tf_op jit(solution)/shard_map/left_gather/ppermute | solution.py:28
  73.8 2.5 %collective-permute-done.9 = bf16[320,1280]{1,0:T(8,128)(2,1)} collective-permute-done((bf16[320,1280]{1,0:T(8,128)(2,1)S(1)}, bf16[320,1280]{1,0:T(8,128)(2,1)}, u32[]{:S(2)}, u32[]{:S(2)}) %collective-permute-start.9) | collective-permute-done | bytes 819232 | tf_op jit(solution)/shard_map/right_gather/ppermute | solution.py:28
  76.4 15.1 %collective-permute-done.10 = bf16[320,1280]{1,0:T(8,128)(2,1)} collective-permute-done((bf16[320,1280]{1,0:T(8,128)(2,1)S(1)}, bf16[320,1280]{1,0:T(8,128)(2,1)}, u32[]{:S(2)}, u32[]{:S(2)}) %collective-permute-start.10) | collective-permute-done | bytes 819232 | tf_op jit(solution)/shard_map/right_gather/ppermute | solution.py:28
  106.6 3.7 %collective-permute-done.16.one_ref = bf16[320,640]{1,0:T(8,128)(2,1)S(1)} collective-permute-done((bf16[320,640]{1,0:T(8,128)(2,1)}, bf16[320,640]{1,0:T(8,128)(2,1)S(1)}, u32[]{:S(2)}, u32[]{:S(2)}) %collective-permute-start.16) | collective-permute-done | bytes 409632 | tf_op jit(solution)/shard_map/density_gather/ppermute | solution.py:28
  111.6 2.8 %collective-permute-done.14 = f32[80,1280]{1,0:T(8,128)S(1)} collective-permute-done((f32[80,1280]{1,0:T(8,128)S(1)}, f32[80,1280]{1,0:T(8,128)S(1)}, u32[]{:S(2)}, u32[]{:S(2)}) %collective-permute-start.14) | collective-permute-done | bytes 409632 | tf_op jit(solution)/shard_map/mixed_sum/ppermute | solution.py:28
  114.4 2.5 %collective-permute-done.15 = f32[80,1280]{1,0:T(8,128)S(1)} collective-permute-done((f32[80,1280]{1,0:T(8,128)S(1)}, f32[80,1280]{1,0:T(8,128)S(1)}, u32[]{:S(2)}, u32[]{:S(2)}) %collective-permute-start.15) | collective-permute-done | bytes 409632 | tf_op jit(solution)/shard_map/mixed_sum/ppermute | solution.py:28
  124.1 3.0 %collective-permute-done.21.upper_ref = bf16[160,640]{1,0:T(8,128)(2,1)S(1)} collective-permute-done((bf16[160,640]{1,0:T(8,128)(2,1)S(1)}, bf16[160,640]{1,0:T(8,128)(2,1)S(1)}, u32[]{:S(2)}, u32[]{:S(2)}) %collective-permute-start.21) | collective-permute-done | bytes 204832 | tf_op jit(solution)/shard_map/density_gather/ppermute | solution.py:28
  129.2 2.8 %density_rows.1.mine_ref = bf16[1280,640]{1,0:T(8,128)(2,1)} custom-call(s32[5]{0:T(128)} %stack.38.at_ref, bf16[320,640]{1,0:T(8,128)(2,1)} %bitcast.10.own_ref, bf16[320,640]{1,0:T(8,128)(2,1)} %copy-done.3, bf16[160,640]{1,0:T(8,128)(2,1)} %copy-done.16, bf16[160,640]{1,0:T(8,128)(2,1)} %collective-permute-done.22.lower_ref, bf16[320,640]{1,0:T(8,128)(2,1)} %copy-done.4), custom_call_target="tpu_custom_call" | custom-call | tf_op jit(solution)/shard_map/density_rows/density_rows/pallas_call | solution.py:58
  132.0 5.5 %collective-permute-done.18 = f32[160,1280]{1,0:T(8,128)} collective-permute-done((f32[160,1280]{1,0:T(8,128)}, f32[160,1280]{1,0:T(8,128)}, u32[]{:S(2)}, u32[]{:S(2)}) %collective-permute-start.18) | collective-permute-done | bytes 819232 | tf_op jit(solution)/shard_map/mixed_sum/ppermute | solution.py:28
  139.6 2.5 %fusion.16 = bf16[160,1280]{1,0:T(8,128)(2,1)} fusion(f32[160,1280]{1,0:T(8,128)} %collective-permute-done.20, f32[160,1280]{1,0:T(8,128)} %collective-permute-done.18, f32[160,1280]{1,0:T(8,128)} %collective-permute-done.11, f32[640,1280]{1,0:T(8,128)S(1)} %fusion), kind=kLoop, calls=%fused_computation.23 | loop fusion | flops 819200 | bytes 3686400 | tf_op jit(solution)/shard_map/mixed_sum/convert_element_type | solution.py:267
  144.4 11.1 %collective-permute-done.23 = bf16[160,1280]{1,0:T(8,128)(2,1)S(1)} collective-permute-done((bf16[160,1280]{1,0:T(8,128)(2,1)}, bf16[160,1280]{1,0:T(8,128)(2,1)S(1)}, u32[]{:S(2)}, u32[]{:S(2)}) %collective-permute-start.23) | collective-permute-done | bytes 409632 | tf_op jit(solution)/shard_map/mixed_gather/ppermute | solution.py:28
  156.2 4.0 %density_join.1 = bf16[1280,1280]{1,0:T(8,128)(2,1)} custom-call(s32[5]{0:T(128)} %stack.38.at_ref, bf16[1280,640]{1,0:T(8,128)(2,1)} %density_rows.1.mine_ref, bf16[1280,640]{1,0:T(8,128)(2,1)} %collective-permute-done.25.other_ref), custom_call_target="tpu_custom_call" | custom-call | tf_op jit(solution)/shard_map/mixed_gather/density_join/pallas_call | solution.py:58
  160.2 4.0 %fusion.8 = bf16[480,1280]{1,0:T(8,128)(2,1)S(1)} fusion(bf16[1280,1280]{1,0:T(8,128)(2,1)} %density_join.1, bf16[160,1280]{1,0:T(8,128)(2,1)S(1)} %collective-permute-done.23, bf16[160,1280]{1,0:T(8,128)(2,1)S(1)} %collective-permute-done.24, bf16[160,1280]{1,0:T(8,128)(2,1)} %fusion.16), kind=kOutput, calls=%fused_computation.10 | convolution fusion | flops 1576550400 | bytes 5734400 | tf_op jit(solution)/shard_map/second_product/dot_general | solution.py:50
  169.1 2.8 %collective-permute-done.27 = bf16[80,1280]{1,0:T(8,128)(2,1)S(1)} collective-permute-done((bf16[80,1280]{1,0:T(8,128)(2,1)S(1)}, bf16[80,1280]{1,0:T(8,128)(2,1)S(1)}, u32[]{:S(2)}, u32[]{:S(2)}) %collective-permute-start.27) | collective-permute-done | bytes 204832 | tf_op jit(solution)/shard_map/mixed_gather/ppermute | solution.py:28
  175.4 2.9 %collective-permute-start.33 = (bf16[1,40,1280]{2,1,0:T(8,128)(2,1)S(1)}, bf16[1,40,1280]{2,1,0:T(8,128)(2,1)S(1)}, u32[]{:S(2)}, u32[]{:S(2)}) collective-permute-start(bf16[1,40,1280]{2,1,0:T(8,128)(2,1)S(1)} %get-tuple-element.120), channel_id=1, source_target_pairs={{0,2},{1,3},{2,4},{3,5},{4,6},{5,7},{6,0},{7,1},{8,10},{9,11},{10,... | collective-permute-start | bytes 307208 | tf_op jit(solution)/shard_map/second_product/ppermute | solution.py:42
  180.5 6.2 %collective-permute-done.31.refs_3_ = bf16[3,40,1280]{2,1,0:T(8,128)(2,1)S(1)} collective-permute-done((bf16[3,40,1280]{2,1,0:T(8,128)(2,1)S(1)}, bf16[3,40,1280]{2,1,0:T(8,128)(2,1)S(1)}, u32[]{:S(2)}, u32[]{:S(2)}) %collective-permute-start.31) | collective-permute-done | bytes 307232 | tf_op jit(solution)/shard_map/second_product/ppermute | solution.py:42
  189.6 2.8 %spread.1 = (bf16[32,40,160]{2,1,0:T(8,128)(2,1)}, f32[40,1280]{1,0:T(8,128)}, f32[40,1280]{1,0:T(8,128)}, f32[40,1280]{1,0:T(8,128)}, f32[40,1280]{1,0:T(8,128)}) custom-call(s32[5]{0:T(128)} %stack.38.at_ref, bf16[3,40,1280]{2,1,0:T(8,128)(2,1)} %copy-done.9, bf16[3,40,1280]{2,1,0:T(8,128)(2,1)} %copy-done.10, bf16[3,40,1280]{2,1,0:T(8,128)(2,1)} %copy-done.11, ...), custom_call_target="tpu_custom_call" | custom-call | tf_op jit(solution)/shard_map/second_product/spread/pallas_call | solution.py:58
  192.5 5.7 %all-to-all-start.2 = ((bf16[32,40,160]{2,1,0:T(8,128)(2,1)}), bf16[32,40,160]{2,1,0:T(8,128)(2,1)S(1)}, u32[]{:S(2)}, u32[]{:S(2)}) async-start(bf16[32,40,160]{2,1,0:T(8,128)(2,1)} %get-tuple-element.92), calls=%async_computation.2 | async-start | bytes 1310720 | tf_op jit(solution)/shard_map/transposed/all_to_all | solution.py:313
  203.8 2.6 %collective-permute-done.36.d1 = f32[40,1280]{1,0:T(8,128)S(1)} collective-permute-done((f32[40,1280]{1,0:T(8,128)}, f32[40,1280]{1,0:T(8,128)S(1)}, u32[]{:S(2)}, u32[]{:S(2)}) %collective-permute-start.36) | collective-permute-done | bytes 204832 | tf_op jit(solution)/shard_map/direct/ppermute | solution.py:28
  206.4 4.6 %collective-permute-done.37.d2 = f32[40,1280]{1,0:T(8,128)S(1)} collective-permute-done((f32[40,1280]{1,0:T(8,128)}, f32[40,1280]{1,0:T(8,128)S(1)}, u32[]{:S(2)}, u32[]{:S(2)}) %collective-permute-start.37) | collective-permute-done | bytes 204832 | tf_op jit(solution)/shard_map/direct/ppermute | solution.py:28
  211.0 2.6 %collective-permute-done.38.d3 = f32[40,1280]{1,0:T(8,128)S(1)} collective-permute-done((f32[40,1280]{1,0:T(8,128)}, f32[40,1280]{1,0:T(8,128)S(1)}, u32[]{:S(2)}, u32[]{:S(2)}) %collective-permute-start.38) | collective-permute-done | bytes 204832 | tf_op jit(solution)/shard_map/direct/ppermute | solution.py:28
  214.5 3.9 %finish.1 = f32[40,5120]{1,0:T(8,128)} custom-call(s32[5]{0:T(128)} %stack.38.at_ref, f32[40,1280]{1,0:T(8,128)} %get-tuple-element.88.d0, f32[40,1280]{1,0:T(8,128)} %copy-done.13, f32[40,1280]{1,0:T(8,128)} %copy-done.14, f32[40,1280]{1,0:T(8,128)} %copy-done.15, bf16[32,40,160]{2,1,0:T(8,128)(2,1)} %copy-done.2, f32[40,40]{1,0:T(8,128)} %fusion.29.kept_ref), custom_call_target="tpu_custom_call" | custom-call | tf_op jit(solution)/shard_map/finish/pallas_call | solution.py:58
  (132 shorter events, 72.6 us)
Async XLA Ops:
  8.0 23.3 %all-to-all-start = ((bf16[8,160,320]{2,1,0:T(8,128)(2,1)}), bf16[8,160,320]{2,1,0:T(8,128)(2,1)S(1)}, u32[]{:S(2)}, u32[]{:S(2)}) async-start(bf16[8,160,320]{2,1,0:T(8,128)(2,1)} %right_columns.1), calls=%async_computation | async-start | bytes 1966080 | tf_op jit(solution)/shard_map/right_gather/all_to_all | solution.py:205
  12.9 13.0 %collective-permute-start.3 = (bf16[160,640]{1,0:T(8,128)(2,1)}, bf16[160,640]{1,0:T(8,128)(2,1)S(1)}, u32[]{:S(2)}, u32[]{:S(2)}) collective-permute-start(bf16[160,640]{1,0:T(8,128)(2,1)} %get-tuple-element.59), channel_id=1, source_target_pairs={{0,24},{1,25},{2,26},{3,27},{4,28},{5,29},{6,30},{7,31},{8,16},{9,... | collective-permute-start | bytes 614408 | tf_op jit(solution)/shard_map/left_columns/ppermute | solution.py:28
  15.9 10.0 %collective-permute-start.2 = (bf16[160,640]{1,0:T(8,128)(2,1)}, bf16[160,640]{1,0:T(8,128)(2,1)S(1)}, u32[]{:S(2)}, u32[]{:S(2)}) collective-permute-start(bf16[160,640]{1,0:T(8,128)(2,1)} %get-tuple-element.58), channel_id=1, source_target_pairs={{0,16},{1,17},{2,18},{3,19},{4,20},{5,21},{6,22},{7,23},{8,24},{9,... | collective-permute-start | bytes 614408 | tf_op jit(solution)/shard_map/left_columns/ppermute | solution.py:28
  16.6 10.0 %collective-permute-start.1 = (bf16[160,640]{1,0:T(8,128)(2,1)}, bf16[160,640]{1,0:T(8,128)(2,1)S(1)}, u32[]{:S(2)}, u32[]{:S(2)}) collective-permute-start(bf16[160,640]{1,0:T(8,128)(2,1)} %get-tuple-element.57), channel_id=1, source_target_pairs={{0,8},{1,9},{2,10},{3,11},{4,12},{5,13},{6,14},{7,15},{8,0},{9,1},... | collective-permute-start | bytes 614408 | tf_op jit(solution)/shard_map/left_columns/ppermute | solution.py:28
  17.7 13.6 %collective-permute-start.4 = (bf16[80,1280]{1,0:T(8,128)(2,1)S(1)}, bf16[80,1280]{1,0:T(8,128)(2,1)}, u32[]{:S(2)}, u32[]{:S(2)}) collective-permute-start(bf16[80,1280]{1,0:T(8,128)(2,1)S(1)} %bitcast.69), channel_id=1, source_target_pairs={{0,1},{1,0},{2,3},{3,2},{4,5},{5,4},{6,7},{7,6},{8,9},{9,8},{10,11... | collective-permute-start | bytes 614408 | tf_op jit(solution)/shard_map/density_turn/ppermute | solution.py:28
  32.6 21.2 %collective-permute-start.5 = (bf16[640,640]{1,0:T(8,128)(2,1)S(1)}, bf16[640,640]{1,0:T(8,128)(2,1)S(1)}, u32[]{:S(2)}, u32[]{:S(2)}) collective-permute-start(bf16[640,640]{1,0:T(8,128)(2,1)S(1)} %pad_maximum_fusion.2), channel_id=1, source_target_pairs={{0,4},{1,5},{2,6},{3,7},{4,0},{5,1},{6,2},{7,3},{8,12},{9,13},{10,... | collective-permute-start | bytes 2457608 | tf_op jit(solution)/shard_map/left_gather/ppermute | solution.py:28
  34.1 35.8 %collective-permute-start.6 = (bf16[640,640]{1,0:T(8,128)(2,1)S(1)}, bf16[640,640]{1,0:T(8,128)(2,1)}, u32[]{:S(2)}, u32[]{:S(2)}) collective-permute-start(bf16[640,640]{1,0:T(8,128)(2,1)S(1)} %pad_maximum_fusion.2), channel_id=1, source_target_pairs={{0,1},{1,0},{2,3},{3,2},{4,5},{5,4},{6,7},{7,6},{8,9},{9,8},{10,11... | collective-permute-start | bytes 2457608 | tf_op jit(solution)/shard_map/left_gather/ppermute | solution.py:28
  34.2 37.2 %collective-permute-start.7 = (bf16[640,640]{1,0:T(8,128)(2,1)S(1)}, bf16[640,640]{1,0:T(8,128)(2,1)}, u32[]{:S(2)}, u32[]{:S(2)}) collective-permute-start(bf16[640,640]{1,0:T(8,128)(2,1)S(1)} %pad_maximum_fusion.2), channel_id=1, source_target_pairs={{0,5},{1,4},{2,7},{3,6},{4,1},{5,0},{6,3},{7,2},{8,13},{9,12},{10,... | collective-permute-start | bytes 2457608 | tf_op jit(solution)/shard_map/left_gather/ppermute | solution.py:28
  36.2 37.7 %collective-permute-start.8 = (bf16[320,1280]{1,0:T(8,128)(2,1)S(1)}, bf16[320,1280]{1,0:T(8,128)(2,1)S(1)}, u32[]{:S(2)}, u32[]{:S(2)}) collective-permute-start(bf16[320,1280]{1,0:T(8,128)(2,1)S(1)} %reshape.136), channel_id=1, source_target_pairs={{0,32},{1,33},{2,34},{3,35},{4,36},{5,37},{6,38},{7,39},{8,40},{9,... | collective-permute-start | bytes 2457608 | tf_op jit(solution)/shard_map/right_gather/ppermute | solution.py:28
  38.1 38.3 %collective-permute-start.9 = (bf16[320,1280]{1,0:T(8,128)(2,1)S(1)}, bf16[320,1280]{1,0:T(8,128)(2,1)}, u32[]{:S(2)}, u32[]{:S(2)}) collective-permute-start(bf16[320,1280]{1,0:T(8,128)(2,1)S(1)} %reshape.136), channel_id=1, source_target_pairs={{0,64},{1,65},{2,66},{3,67},{4,68},{5,69},{6,70},{7,71},{8,72},{9,... | collective-permute-start | bytes 2457608 | tf_op jit(solution)/shard_map/right_gather/ppermute | solution.py:28
  53.8 37.6 %collective-permute-start.10 = (bf16[320,1280]{1,0:T(8,128)(2,1)S(1)}, bf16[320,1280]{1,0:T(8,128)(2,1)}, u32[]{:S(2)}, u32[]{:S(2)}) collective-permute-start(bf16[320,1280]{1,0:T(8,128)(2,1)S(1)} %reshape.136), channel_id=1, source_target_pairs={{0,96},{1,97},{2,98},{3,99},{4,100},{5,101},{6,102},{7,103},{8,104... | collective-permute-start | bytes 2457608 | tf_op jit(solution)/shard_map/right_gather/ppermute | solution.py:28
  59.8 31.6 %all-to-all-start.1 = ((bf16[4,80,640]{2,1,0:T(8,128)(2,1)}), bf16[4,80,640]{2,1,0:T(8,128)(2,1)}, u32[]{:S(2)}, u32[]{:S(2)}) async-start(bf16[4,80,640]{2,1,0:T(8,128)(2,1)} %density_columns.1), calls=%async_computation.1 | async-start | bytes 819200 | tf_op jit(solution)/shard_map/density_columns/all_to_all | solution.py:224
  98.3 12.1 %collective-permute-start.16 = (bf16[320,640]{1,0:T(8,128)(2,1)}, bf16[320,640]{1,0:T(8,128)(2,1)S(1)}, u32[]{:S(2)}, u32[]{:S(2)}) collective-permute-start(bf16[320,640]{1,0:T(8,128)(2,1)} %bitcast.10.own_ref), channel_id=1, source_target_pairs={{0,32},{1,33},{2,34},{3,35},{4,36},{5,37},{6,38},{7,39},{8,40},{9,... | collective-permute-start | bytes 1228808 | tf_op jit(solution)/shard_map/density_gather/ppermute | solution.py:28
  98.3 13.3 %collective-permute-start.17 = (bf16[320,640]{1,0:T(8,128)(2,1)}, bf16[320,640]{1,0:T(8,128)(2,1)S(1)}, u32[]{:S(2)}, u32[]{:S(2)}) collective-permute-start(bf16[320,640]{1,0:T(8,128)(2,1)} %bitcast.10.own_ref), channel_id=1, source_target_pairs={{0,96},{1,97},{2,98},{3,99},{4,100},{5,101},{6,102},{7,103},{8,104... | collective-permute-start | bytes 1228808 | tf_op jit(solution)/shard_map/density_gather/ppermute | solution.py:28
  102.8 11.6 %collective-permute-start.14 = (f32[80,1280]{1,0:T(8,128)S(1)}, f32[80,1280]{1,0:T(8,128)S(1)}, u32[]{:S(2)}, u32[]{:S(2)}) collective-permute-start(f32[80,1280]{1,0:T(8,128)S(1)} %get-tuple-element.117), channel_id=1, source_target_pairs={{0,8},{1,9},{2,10},{3,11},{4,12},{5,13},{6,14},{7,15},{8,0},{9,1},... | collective-permute-start | bytes 1228808 | tf_op jit(solution)/shard_map/mixed_sum/ppermute | solution.py:28
  104.4 12.4 %collective-permute-start.15 = (f32[80,1280]{1,0:T(8,128)S(1)}, f32[80,1280]{1,0:T(8,128)S(1)}, u32[]{:S(2)}, u32[]{:S(2)}) collective-permute-start(f32[80,1280]{1,0:T(8,128)S(1)} %get-tuple-element.116), channel_id=1, source_target_pairs={{0,24},{1,25},{2,26},{3,27},{4,28},{5,29},{6,30},{7,31},{8,16},{9,... | collective-permute-start | bytes 1228808 | tf_op jit(solution)/shard_map/mixed_sum/ppermute | solution.py:28
  118.0 19.4 %collective-permute-start.18 = (f32[160,1280]{1,0:T(8,128)}, f32[160,1280]{1,0:T(8,128)}, u32[]{:S(2)}, u32[]{:S(2)}) collective-permute-start(f32[160,1280]{1,0:T(8,128)} %pad_maximum_fusion.3), channel_id=1, source_target_pairs={{0,8},{1,9},{2,10},{3,11},{4,12},{5,13},{6,14},{7,15},{8,0},{9,1},... | collective-permute-start | bytes 2457608 | tf_op jit(solution)/shard_map/mixed_sum/ppermute | solution.py:28
  119.0 20.7 %collective-permute-start.20 = (f32[160,1280]{1,0:T(8,128)}, f32[160,1280]{1,0:T(8,128)}, u32[]{:S(2)}, u32[]{:S(2)}) collective-permute-start(f32[160,1280]{1,0:T(8,128)} %pad_maximum_fusion.4), channel_id=1, source_target_pairs={{0,24},{1,25},{2,26},{3,27},{4,28},{5,29},{6,30},{7,31},{8,16},{9,... | collective-permute-start | bytes 2457608 | tf_op jit(solution)/shard_map/mixed_sum/ppermute | solution.py:28
  124.1 15.6 %collective-permute-start.11 = (f32[160,1280]{1,0:T(8,128)}, f32[160,1280]{1,0:T(8,128)}, u32[]{:S(2)}, u32[]{:S(2)}) collective-permute-start(f32[160,1280]{1,0:T(8,128)} %get-tuple-element.93), channel_id=1, source_target_pairs={{0,2},{1,3},{2,0},{3,1},{4,6},{5,7},{6,4},{7,5},{8,10},{9,11},{10,... | collective-permute-start | bytes 2457608 | tf_op jit(solution)/shard_map/mixed_sum/ppermute | solution.py:28
  139.6 16.6 %collective-permute-start.25 = (bf16[1280,640]{1,0:T(8,128)(2,1)}, bf16[1280,640]{1,0:T(8,128)(2,1)}, u32[]{:S(2)}, u32[]{:S(2)}) collective-permute-start(bf16[1280,640]{1,0:T(8,128)(2,1)} %density_rows.1.mine_ref), channel_id=1, source_target_pairs={{0,2},{1,3},{2,0},{3,1},{4,6},{5,7},{6,4},{7,5},{8,10},{9,11},{10,... | collective-permute-start | bytes 4915208 | tf_op jit(solution)/shard_map/mixed_gather/ppermute | solution.py:28
  142.2 13.3 %collective-permute-start.23 = (bf16[160,1280]{1,0:T(8,128)(2,1)}, bf16[160,1280]{1,0:T(8,128)(2,1)S(1)}, u32[]{:S(2)}, u32[]{:S(2)}) collective-permute-start(bf16[160,1280]{1,0:T(8,128)(2,1)} %fusion.16), channel_id=1, source_target_pairs={{0,24},{1,25},{2,26},{3,27},{4,28},{5,29},{6,30},{7,31},{8,16},{9,... | collective-permute-start | bytes 1228808 | tf_op jit(solution)/shard_map/mixed_gather/ppermute | solution.py:28
  144.4 11.8 %collective-permute-start.24 = (bf16[160,1280]{1,0:T(8,128)(2,1)}, bf16[160,1280]{1,0:T(8,128)(2,1)S(1)}, u32[]{:S(2)}, u32[]{:S(2)}) collective-permute-start(bf16[160,1280]{1,0:T(8,128)(2,1)} %fusion.16), channel_id=1, source_target_pairs={{0,8},{1,9},{2,10},{3,11},{4,12},{5,13},{6,14},{7,15},{8,0},{9,1},... | collective-permute-start | bytes 1228808 | tf_op jit(solution)/shard_map/mixed_gather/ppermute | solution.py:28
  164.3 9.6 %collective-permute-start.26 = (bf16[3,40,1280]{2,1,0:T(8,128)(2,1)S(1)}, bf16[3,40,1280]{2,1,0:T(8,128)(2,1)S(1)}, u32[]{:S(2)}, u32[]{:S(2)}) collective-permute-start(bf16[3,40,1280]{2,1,0:T(8,128)(2,1)S(1)} %get-tuple-element.111), channel_id=1, source_target_pairs={{0,0},{1,1},{2,6},{3,7},{4,4},{5,5},{6,2},{7,3},{8,8},{9,9},{10,14... | collective-permute-start | bytes 921608 | tf_op jit(solution)/shard_map/second_product/ppermute | solution.py:42
  166.7 11.7 %collective-permute-start.29 = (bf16[3,40,1280]{2,1,0:T(8,128)(2,1)S(1)}, bf16[3,40,1280]{2,1,0:T(8,128)(2,1)S(1)}, u32[]{:S(2)}, u32[]{:S(2)}) collective-permute-start(bf16[3,40,1280]{2,1,0:T(8,128)(2,1)S(1)} %get-tuple-element.110), channel_id=1, source_target_pairs={{0,2},{1,3},{2,4},{3,5},{4,6},{5,7},{6,0},{7,1},{8,10},{9,11},{10,... | collective-permute-start | bytes 921608 | tf_op jit(solution)/shard_map/second_product/ppermute | solution.py:42
  168.8 10.6 %collective-permute-start.30 = (bf16[3,40,1280]{2,1,0:T(8,128)(2,1)S(1)}, bf16[3,40,1280]{2,1,0:T(8,128)(2,1)S(1)}, u32[]{:S(2)}, u32[]{:S(2)}) collective-permute-start(bf16[3,40,1280]{2,1,0:T(8,128)(2,1)S(1)} %get-tuple-element.109), channel_id=1, source_target_pairs={{0,1},{1,0},{2,7},{3,6},{4,5},{5,4},{6,3},{7,2},{8,9},{9,8},{10,15... | collective-permute-start | bytes 921608 | tf_op jit(solution)/shard_map/second_product/ppermute | solution.py:42
  171.9 14.8 %collective-permute-start.31 = (bf16[3,40,1280]{2,1,0:T(8,128)(2,1)S(1)}, bf16[3,40,1280]{2,1,0:T(8,128)(2,1)S(1)}, u32[]{:S(2)}, u32[]{:S(2)}) collective-permute-start(bf16[3,40,1280]{2,1,0:T(8,128)(2,1)S(1)} %get-tuple-element.108), channel_id=1, source_target_pairs={{0,3},{1,2},{2,5},{3,4},{4,7},{5,6},{6,1},{7,0},{8,11},{9,10},{10,... | collective-permute-start | bytes 921608 | tf_op jit(solution)/shard_map/second_product/ppermute | solution.py:42
  174.7 12.0 %collective-permute-start.32 = (bf16[1,40,1280]{2,1,0:T(8,128)(2,1)S(1)}, bf16[1,40,1280]{2,1,0:T(8,128)(2,1)S(1)}, u32[]{:S(2)}, u32[]{:S(2)}) collective-permute-start(bf16[1,40,1280]{2,1,0:T(8,128)(2,1)S(1)} %get-tuple-element.121), channel_id=1, source_target_pairs={{0,0},{1,1},{2,6},{3,7},{4,4},{5,5},{6,2},{7,3},{8,8},{9,9},{10,14... | collective-permute-start | bytes 307208 | tf_op jit(solution)/shard_map/second_product/ppermute | solution.py:42
  175.4 11.4 %collective-permute-start.33 = (bf16[1,40,1280]{2,1,0:T(8,128)(2,1)S(1)}, bf16[1,40,1280]{2,1,0:T(8,128)(2,1)S(1)}, u32[]{:S(2)}, u32[]{:S(2)}) collective-permute-start(bf16[1,40,1280]{2,1,0:T(8,128)(2,1)S(1)} %get-tuple-element.120), channel_id=1, source_target_pairs={{0,2},{1,3},{2,4},{3,5},{4,6},{5,7},{6,0},{7,1},{8,10},{9,11},{10,... | collective-permute-start | bytes 307208 | tf_op jit(solution)/shard_map/second_product/ppermute | solution.py:42
  179.4 9.5 %collective-permute-start.35 = (bf16[1,40,1280]{2,1,0:T(8,128)(2,1)S(1)}, bf16[1,40,1280]{2,1,0:T(8,128)(2,1)S(1)}, u32[]{:S(2)}, u32[]{:S(2)}) collective-permute-start(bf16[1,40,1280]{2,1,0:T(8,128)(2,1)S(1)} %get-tuple-element.118), channel_id=1, source_target_pairs={{0,3},{1,2},{2,5},{3,4},{4,7},{5,6},{6,1},{7,0},{8,11},{9,10},{10,... | collective-permute-start | bytes 307208 | tf_op jit(solution)/shard_map/second_product/ppermute | solution.py:42
  192.5 21.2 %all-to-all-start.2 = ((bf16[32,40,160]{2,1,0:T(8,128)(2,1)}), bf16[32,40,160]{2,1,0:T(8,128)(2,1)S(1)}, u32[]{:S(2)}, u32[]{:S(2)}) async-start(bf16[32,40,160]{2,1,0:T(8,128)(2,1)} %get-tuple-element.92), calls=%async_computation.2 | async-start | bytes 1310720 | tf_op jit(solution)/shard_map/transposed/all_to_all | solution.py:313
  199.1 12.0 %collective-permute-start.37 = (f32[40,1280]{1,0:T(8,128)}, f32[40,1280]{1,0:T(8,128)S(1)}, u32[]{:S(2)}, u32[]{:S(2)}) collective-permute-start(f32[40,1280]{1,0:T(8,128)} %get-tuple-element.90), channel_id=1, source_target_pairs={{0,16},{1,17},{2,18},{3,19},{4,20},{5,21},{6,22},{7,23},{8,24},{9,... | collective-permute-start | bytes 614408 | tf_op jit(solution)/shard_map/direct/ppermute | solution.py:28
  201.2 12.4 %collective-permute-start.38 = (f32[40,1280]{1,0:T(8,128)}, f32[40,1280]{1,0:T(8,128)S(1)}, u32[]{:S(2)}, u32[]{:S(2)}) collective-permute-start(f32[40,1280]{1,0:T(8,128)} %get-tuple-element.91), channel_id=1, source_target_pairs={{0,24},{1,25},{2,26},{3,27},{4,28},{5,29},{6,30},{7,31},{8,16},{9,... | collective-permute-start | bytes 614408 | tf_op jit(solution)/shard_map/direct/ppermute | solution.py:28
  (32 other events, 210.8 us)

commit v13 on v8

--- a/solution.py
+++ b/solution.py
@@ -155,8 +155,8 @@
         mine, other = total(0), total(1)
         low = jnp.where(core == 0, mine, other)
         high = jnp.where(core == 0, other, mine)
-        outs[q][:, :640] = low
-        outs[q][:, 640:] = high
+        outs[q][:, :640] = low.astype(outs[q].dtype)
+        outs[q][:, 640:] = high.astype(outs[q].dtype)
         slots[y ^ q, :, :640] = low
         slots[y ^ q, :, 640:] = high
     for nz in range(4):
@@ -170,7 +170,7 @@
 
 def finish_kernel(at_ref, d0, d1, d2, d3, t_ref, kept_ref, out_ref, slots):
     for q, ref in enumerate((d0, d1, d2, d3)):
-        slots[q] = ref[...]
+        slots[q] = ref[...].astype(f32)
     y = at_ref[1]
     for nz in range(4):
         blocks = []
@@ -322,7 +322,7 @@
         turned, *rows = local_call(
             spread_kernel,
             "spread",
-            [shape(bf16, 32, 40, 160)] + [shape(f32, 40, 1280)] * 4,
+            [shape(bf16, 32, 40, 160), shape(f32, 40, 1280)] + [shape(bf16, 40, 1280)] * 3,
             coords,
             *many,
             *last,

time: 206 us -> 203 us (0.985)
  waiting for transfers between devices: 80.6 us -> 76.8 us
    ppermute x31, waiting for transfers between devices: 76 us -> 71 us  [flip(): return lax.ppermute(value, AXES, pairs)]
  transfers between devices with their start and end apart: 42 -> 42, of which waited for: 22 -> 23; matrix products, arithmetic and copies ran while one was open for 7% -> 7% of each run, Pallas kernels for 8% -> 8%
where the time goes in v13:
time: 203 us; the launch traced here: 201 us
  waiting for transfers between devices  76.8 us (38%)
  starting transfers between devices  70.1 us (35%)
  Pallas kernels  25.8 us (13%)
  other arithmetic  12.1 us (6%)
  local copies, waits for them, and re-layouts  10.5 us (5%)
  matrix products  5.35 us (3%)
    ppermute x31, waiting for transfers between devices, flip(): return lax.ppermute(value, AXES, pairs)  71 us
    ppermute x31, starting transfers between devices, flip(): return lax.ppermute(value, AXES, pairs)  38.4 us
    pallas_call x8, Pallas kernels, local_call(): pl.pallas_call(kernel, out_shape=outs, in_specs=[SMEM] + [VMEM] * len(ope...  25.8 us
    ppermute x8, starting transfers between devices, remap(): return lax.ppermute(value, AXES, pairs)  15.5 us
    unnamed x60, local copies, waits for them, and re-layouts  7.23 us
    all_to_all x1, starting transfers between devices, shards(): lax.all_to_all(turned, ('z', 'xl', 'core', 'xh'), split_axis=0, concat_ax...  6.79 us
    select_n x2, other arithmetic, shards(): mine = [jnp.where(core == 0, lefts[0, r], lefts[1, r]) for r in range(2)]  4.92 us
    all_to_all x1, starting transfers between devices, shards(): lax.all_to_all(parts, ('xl', 'core', 'xh'), split_axis=0, concat_axis=0,...  4.92 us
  transfers between devices with their start and end apart: 42, of which 23 were waited for; matrix products, arithmetic and copies ran while one was open for 7% of the time, Pallas kernels for 8%

profile of v13, /device:TPU:2, one launch (start us, length us, event | category | flops | bytes accessed | tf_op | source)
XLA Modules:
  0.0 201.1 jit_solution(12722559464012597828)
XLA Ops:
  1.9 2.7 %right_columns.1 = bf16[8,160,320]{2,1,0:T(8,128)(2,1)} custom-call(s32[5]{0:T(128)} %stack.38.at_ref, bf16[160,1280]{1,0:T(8,128)(2,1)} %first_ref.1, bf16[160,1280]{1,0:T(8,128)(2,1)} %second_ref.1), custom_call_target="tpu_custom_call" | custom-call | tf_op jit(solution)/shard_map/right_columns/right_columns/pallas_call | solution.py:58
  5.4 2.6 %left_columns.1 = (bf16[160,640]{1,0:T(8,128)(2,1)}, bf16[160,640]{1,0:T(8,128)(2,1)}, bf16[160,640]{1,0:T(8,128)(2,1)}, bf16[160,640]{1,0:T(8,128)(2,1)}) custom-call(s32[5]{0:T(128)} %stack.38.at_ref, bf16[160,1280]{1,0:T(8,128)(2,1)} %first_ref.2, bf16[160,1280]{1,0:T(8,128)(2,1)} %second_ref.2, bf16[160,1280]{1,0:T(8,128)(2,1)} %copy-done.13), custom_call_target="tpu_custom_call" | custom-call | tf_op jit(solution)/shard_map/left_columns/left_columns/pallas_call | solution.py:58
  8.0 4.9 %all-to-all-start = ((bf16[8,160,320]{2,1,0:T(8,128)(2,1)}), bf16[8,160,320]{2,1,0:T(8,128)(2,1)S(1)}, u32[]{:S(2)}, u32[]{:S(2)}) async-start(bf16[8,160,320]{2,1,0:T(8,128)(2,1)} %right_columns.1), calls=%async_computation | async-start | bytes 1966080 | tf_op jit(solution)/shard_map/right_gather/all_to_all | solution.py:222
  14.5 2.9 %collective-permute-start.2 = (bf16[160,640]{1,0:T(8,128)(2,1)}, bf16[160,640]{1,0:T(8,128)(2,1)S(1)}, u32[]{:S(2)}, u32[]{:S(2)}) collective-permute-start(bf16[160,640]{1,0:T(8,128)(2,1)} %get-tuple-element.68), channel_id=1, source_target_pairs={{0,16},{1,17},{2,18},{3,19},{4,20},{5,21},{6,22},{7,23},{8,24},{9,... | collective-permute-start | bytes 614408 | tf_op jit(solution)/shard_map/left_columns/ppermute | solution.py:28
  21.1 6.1 %collective-permute-done.2 = bf16[160,640]{1,0:T(8,128)(2,1)S(1)} collective-permute-done((bf16[160,640]{1,0:T(8,128)(2,1)}, bf16[160,640]{1,0:T(8,128)(2,1)S(1)}, u32[]{:S(2)}, u32[]{:S(2)}) %collective-permute-start.2) | collective-permute-done | bytes 204832 | tf_op jit(solution)/shard_map/left_columns/ppermute | solution.py:28
  27.2 2.6 %collective-permute-done.3 = bf16[160,640]{1,0:T(8,128)(2,1)S(1)} collective-permute-done((bf16[160,640]{1,0:T(8,128)(2,1)}, bf16[160,640]{1,0:T(8,128)(2,1)S(1)}, u32[]{:S(2)}, u32[]{:S(2)}) %collective-permute-start.3) | collective-permute-done | bytes 204832 | tf_op jit(solution)/shard_map/left_columns/ppermute | solution.py:28
  36.1 4.0 %collective-permute-start.10 = (bf16[320,1280]{1,0:T(8,128)(2,1)S(1)}, bf16[320,1280]{1,0:T(8,128)(2,1)S(1)}, u32[]{:S(2)}, u32[]{:S(2)}) collective-permute-start(bf16[320,1280]{1,0:T(8,128)(2,1)S(1)} %reshape.58), channel_id=1, source_target_pairs={{0,96},{1,97},{2,98},{3,99},{4,100},{5,101},{6,102},{7,103},{8,104... | collective-permute-start | bytes 2457608 | tf_op jit(solution)/shard_map/right_gather/ppermute | solution.py:28
  40.1 13.7 %collective-permute-done.5 = bf16[640,640]{1,0:T(8,128)(2,1)} collective-permute-done((bf16[640,640]{1,0:T(8,128)(2,1)S(1)}, bf16[640,640]{1,0:T(8,128)(2,1)}, u32[]{:S(2)}, u32[]{:S(2)}) %collective-permute-start.5) | collective-permute-done | bytes 819232 | tf_op jit(solution)/shard_map/left_gather/ppermute | solution.py:28
  53.9 3.9 %collective-permute-start.9 = (bf16[320,1280]{1,0:T(8,128)(2,1)S(1)}, bf16[320,1280]{1,0:T(8,128)(2,1)}, u32[]{:S(2)}, u32[]{:S(2)}) collective-permute-start(bf16[320,1280]{1,0:T(8,128)(2,1)S(1)} %reshape.58), channel_id=1, source_target_pairs={{0,64},{1,65},{2,66},{3,67},{4,68},{5,69},{6,70},{7,71},{8,72},{9,... | collective-permute-start | bytes 2457608 | tf_op jit(solution)/shard_map/right_gather/ppermute | solution.py:28
  59.7 4.5 %all-to-all-start.1 = ((bf16[4,80,640]{2,1,0:T(8,128)(2,1)}), bf16[4,80,640]{2,1,0:T(8,128)(2,1)S(1)}, u32[]{:S(2)}, u32[]{:S(2)}) async-start(bf16[4,80,640]{2,1,0:T(8,128)(2,1)} %density_columns.1), calls=%async_computation.1 | async-start | bytes 819200 | tf_op jit(solution)/shard_map/density_columns/all_to_all | solution.py:241
  64.1 2.5 %broadcast_select_fusion.3 = (bf16[640,640]{1,0:T(8,128)(2,1)}, bf16[640,640]{1,0:T(8,128)(2,1)}) fusion(bf16[640,640]{1,0:T(8,128)(2,1)S(1)} %pad_maximum_fusion.2, bf16[640,640]{1,0:T(8,128)(2,1)} %collective-permute-done.5, pred[]{:T(512)S(6)} %eq.8), kind=kLoop, calls=%fused_computation.28 | loop fusion | flops 819200 | bytes 3276801 | tf_op jit(solution)/shard_map/first_product/jit(_where)/select_n | solution.py:255
  66.6 3.3 %collective-permute-done.6 = bf16[640,640]{1,0:T(8,128)(2,1)} collective-permute-done((bf16[640,640]{1,0:T(8,128)(2,1)S(1)}, bf16[640,640]{1,0:T(8,128)(2,1)}, u32[]{:S(2)}, u32[]{:S(2)}) %collective-permute-start.6) | collective-permute-done | bytes 819232 | tf_op jit(solution)/shard_map/left_gather/ppermute | solution.py:28
  71.3 2.4 %broadcast_select_fusion.2 = (bf16[640,640]{1,0:T(8,128)(2,1)S(1)}, bf16[640,640]{1,0:T(8,128)(2,1)}) fusion(bf16[640,640]{1,0:T(8,128)(2,1)} %collective-permute-done.6, bf16[640,640]{1,0:T(8,128)(2,1)} %collective-permute-done.7, pred[]{:T(512)S(6)} %eq.8), kind=kLoop, calls=%fused_computation.27 | loop fusion | flops 819200 | bytes 3276801 | tf_op jit(solution)/shard_map/first_product/jit(_where)/select_n | solution.py:255
  73.8 2.4 %collective-permute-done.9 = bf16[320,1280]{1,0:T(8,128)(2,1)} collective-permute-done((bf16[320,1280]{1,0:T(8,128)(2,1)S(1)}, bf16[320,1280]{1,0:T(8,128)(2,1)}, u32[]{:S(2)}, u32[]{:S(2)}) %collective-permute-start.9) | collective-permute-done | bytes 819232 | tf_op jit(solution)/shard_map/right_gather/ppermute | solution.py:28
  79.3 2.3 %fusion.4 = f32[640,1280]{1,0:T(8,128)S(1)} fusion(bf16[640,640]{1,0:T(8,128)(2,1)S(1)} %copy-done.12, bf16[640,640]{1,0:T(8,128)(2,1)S(1)} %copy-done.11, bf16[320,1280]{1,0:T(8,128)(2,1)S(1)} %get-tuple-element.121, bf16[320,1280]{1,0:T(8,128)(2,1)S(1)} %get-tuple-element.122, bf16[320,1280]{1,0:T(8,128)(2,1)S(1)} %get-tuple-element.123, ...), kind=kOutput, calls=%fused_computation.6 | convolution fusion | flops 2113536000 | bytes 8192000 | tf_op jit(solution)/shard_map/first_product/dot_general | solution.py:50
  82.7 3.1 %collective-permute-start.16 = (bf16[320,640]{1,0:T(8,128)(2,1)S(1)}, bf16[320,640]{1,0:T(8,128)(2,1)S(1)}, u32[]{:S(2)}, u32[]{:S(2)}) collective-permute-start(bf16[320,640]{1,0:T(8,128)(2,1)S(1)} %bitcast.30), channel_id=1, source_target_pairs={{0,96},{1,97},{2,98},{3,99},{4,100},{5,101},{6,102},{7,103},{8,104... | collective-permute-start | bytes 1228808 | tf_op jit(solution)/shard_map/density_gather/ppermute | solution.py:28
  85.8 2.3 %fusion = f32[640,1280]{1,0:T(8,128)S(1)} fusion(bf16[640,640]{1,0:T(8,128)(2,1)S(1)} %get-tuple-element.126, bf16[640,640]{1,0:T(8,128)(2,1)S(1)} %copy-done.10, bf16[320,1280]{1,0:T(8,128)(2,1)S(1)} %get-tuple-element.121, bf16[320,1280]{1,0:T(8,128)(2,1)S(1)} %get-tuple-element.122, bf16[320,1280]{1,0:T(8,128)(2,1)S(1)} %get-tuple-element.123, ...), kind=kOutput, calls=%fused_computation.2 | convolution fusion | flops 2113536000 | bytes 8192000 | tf_op jit(solution)/shard_map/first_product/dot_general | solution.py:50
  95.7 5.5 %collective-permute-done.13 = f32[80,1280]{1,0:T(8,128)S(1)} collective-permute-done((f32[80,1280]{1,0:T(8,128)S(1)}, f32[80,1280]{1,0:T(8,128)S(1)}, u32[]{:S(2)}, u32[]{:S(2)}) %collective-permute-start.13) | collective-permute-done | bytes 409632 | tf_op jit(solution)/shard_map/mixed_sum/ppermute | solution.py:28
  101.2 2.5 %collective-permute-done.14 = f32[80,1280]{1,0:T(8,128)S(1)} collective-permute-done((f32[80,1280]{1,0:T(8,128)S(1)}, f32[80,1280]{1,0:T(8,128)S(1)}, u32[]{:S(2)}, u32[]{:S(2)}) %collective-permute-start.14) | collective-permute-done | bytes 409632 | tf_op jit(solution)/shard_map/mixed_sum/ppermute | solution.py:28
  109.4 5.3 %collective-permute-done.20.upper_ref = bf16[160,640]{1,0:T(8,128)(2,1)S(1)} collective-permute-done((bf16[160,640]{1,0:T(8,128)(2,1)S(1)}, bf16[160,640]{1,0:T(8,128)(2,1)S(1)}, u32[]{:S(2)}, u32[]{:S(2)}) %collective-permute-start.20) | collective-permute-done | bytes 204832 | tf_op jit(solution)/shard_map/density_gather/ppermute | solution.py:28
  117.7 2.7 %density_rows.1.mine_ref = bf16[1280,640]{1,0:T(8,128)(2,1)} custom-call(s32[5]{0:T(128)} %stack.38.at_ref, bf16[320,640]{1,0:T(8,128)(2,1)} %bitcast.31, bf16[320,640]{1,0:T(8,128)(2,1)} %copy-done.8, bf16[160,640]{1,0:T(8,128)(2,1)} %copy-done.20, bf16[160,640]{1,0:T(8,128)(2,1)} %copy-done.21, bf16[320,640]{1,0:T(8,128)(2,1)} %copy-done.9), custom_call_target="tpu_custom_call" | custom-call | tf_op jit(solution)/shard_map/density_rows/density_rows/pallas_call | solution.py:58
  120.4 3.8 %collective-permute-done.19 = f32[160,1280]{1,0:T(8,128)S(1)} collective-permute-done((f32[160,1280]{1,0:T(8,128)S(1)}, f32[160,1280]{1,0:T(8,128)S(1)}, u32[]{:S(2)}, u32[]{:S(2)}) %collective-permute-start.19) | collective-permute-done | bytes 819232 | tf_op jit(solution)/shard_map/mixed_sum/ppermute | solution.py:28
  129.1 12.0 %collective-permute-done.24.refs_2_ = bf16[160,1280]{1,0:T(8,128)(2,1)S(1)} collective-permute-done((bf16[160,1280]{1,0:T(8,128)(2,1)S(1)}, bf16[160,1280]{1,0:T(8,128)(2,1)S(1)}, u32[]{:S(2)}, u32[]{:S(2)}) %collective-permute-start.24) | collective-permute-done | bytes 409632 | tf_op jit(solution)/shard_map/mixed_gather/ppermute | solution.py:28
  144.4 5.4 %second_product.2 = (bf16[2,3,40,640]{3,2,1,0:T(8,128)(2,1)}, bf16[2,3,40,640]{3,2,1,0:T(8,128)(2,1)}, bf16[2,3,40,640]{3,2,1,0:T(8,128)(2,1)}, bf16[2,3,40,640]{3,2,1,0:T(8,128)(2,1)}) custom-call(s32[5]{0:T(128)} %stack.38.at_ref, bf16[1280,640]{1,0:T(8,128)(2,1)} %density_rows.1.mine_ref, bf16[1280,640]{1,0:T(8,128)(2,1)} %copy-done, ...), custom_call_target="tpu_custom_call" | custom-call | tf_op jit(solution)/shard_map/second_product/second_product/pallas_call | solution.py:58
  153.7 2.8 %collective-permute-start.30 = (bf16[2,3,40,640]{3,2,1,0:T(8,128)(2,1)}, bf16[2,3,40,640]{3,2,1,0:T(8,128)(2,1)S(1)}, u32[]{:S(2)}, u32[]{:S(2)}) collective-permute-start(bf16[2,3,40,640]{3,2,1,0:T(8,128)(2,1)} %get-tuple-element.100), channel_id=1, source_target_pairs={{0,1},{1,0},{2,7},{3,6},{4,5},{5,4},{6,3},{7,2},{8,9},{9,8},{10,15... | collective-permute-start | bytes 921608 | tf_op jit(solution)/shard_map/second_product/ppermute | solution.py:42
  156.5 3.7 %second_product.3 = (bf16[2,1,40,640]{3,2,1,0:T(8,128)(2,1)}, bf16[2,1,40,640]{3,2,1,0:T(8,128)(2,1)}, bf16[2,1,40,640]{3,2,1,0:T(8,128)(2,1)}, bf16[2,1,40,640]{3,2,1,0:T(8,128)(2,1)}) custom-call(s32[5]{0:T(128)} %stack.38.at_ref, bf16[1280,640]{1,0:T(8,128)(2,1)} %density_rows.1.mine_ref, bf16[1280,640]{1,0:T(8,128)(2,1)} %copy-done, ...), custom_call_target="tpu_custom_call" | custom-call | tf_op jit(solution)/shard_map/second_product/second_product/pallas_call | solution.py:58
  161.8 5.5 %collective-permute-start.33 = (bf16[2,1,40,640]{3,2,1,0:T(8,128)(2,1)}, bf16[2,1,40,640]{3,2,1,0:T(8,128)(2,1)S(1)}, u32[]{:S(2)}, u32[]{:S(2)}) collective-permute-start(bf16[2,1,40,640]{3,2,1,0:T(8,128)(2,1)} %get-tuple-element.105), channel_id=1, source_target_pairs={{0,2},{1,3},{2,4},{3,5},{4,6},{5,7},{6,0},{7,1},{8,10},{9,11},{10,... | collective-permute-start | bytes 307208 | tf_op jit(solution)/shard_map/second_product/ppermute | solution.py:42
  170.7 2.9 %collective-permute-done.34.refs_6_ = bf16[2,1,40,640]{3,2,1,0:T(8,128)(2,1)S(1)} collective-permute-done((bf16[2,1,40,640]{3,2,1,0:T(8,128)(2,1)}, bf16[2,1,40,640]{3,2,1,0:T(8,128)(2,1)S(1)}, u32[]{:S(2)}, u32[]{:S(2)}) %collective-permute-start.34) | collective-permute-done | bytes 102432 | tf_op jit(solution)/shard_map/second_product/ppermute | solution.py:42
  174.9 2.9 %spread.1 = (bf16[32,40,160]{2,1,0:T(8,128)(2,1)}, f32[40,1280]{1,0:T(8,128)}, bf16[40,1280]{1,0:T(8,128)(2,1)}, bf16[40,1280]{1,0:T(8,128)(2,1)}, bf16[40,1280]{1,0:T(8,128)(2,1)}) custom-call(s32[5]{0:T(128)} %stack.38.at_ref, bf16[2,3,40,640]{3,2,1,0:T(8,128)(2,1)} %copy-done.14, bf16[2,3,40,640]{3,2,1,0:T(8,128)(2,1)} %copy-done.16, ...), custom_call_target="tpu_custom_call" | custom-call | tf_op jit(solution)/shard_map/second_product/spread/pallas_call | solution.py:58
  177.9 6.8 %all-to-all-start.2 = ((bf16[32,40,160]{2,1,0:T(8,128)(2,1)}), bf16[32,40,160]{2,1,0:T(8,128)(2,1)S(1)}, u32[]{:S(2)}, u32[]{:S(2)}) async-start(bf16[32,40,160]{2,1,0:T(8,128)(2,1)} %get-tuple-element.112), calls=%async_computation.2 | async-start | bytes 1310720 | tf_op jit(solution)/shard_map/transposed/all_to_all | solution.py:333
  190.7 2.6 %collective-permute-done.37.d2 = bf16[40,1280]{1,0:T(8,128)(2,1)S(1)} collective-permute-done((bf16[40,1280]{1,0:T(8,128)(2,1)}, bf16[40,1280]{1,0:T(8,128)(2,1)S(1)}, u32[]{:S(2)}, u32[]{:S(2)}) %collective-permute-start.37) | collective-permute-done | bytes 102432 | tf_op jit(solution)/shard_map/direct/ppermute | solution.py:28
  197.3 3.8 %finish.1 = f32[40,5120]{1,0:T(8,128)} custom-call(s32[5]{0:T(128)} %stack.38.at_ref, f32[40,1280]{1,0:T(8,128)} %get-tuple-element.108.d0, bf16[40,1280]{1,0:T(8,128)(2,1)} %copy-done.26, bf16[40,1280]{1,0:T(8,128)(2,1)} %copy-done.27, bf16[40,1280]{1,0:T(8,128)(2,1)} %copy-done.28, bf16[32,40,160]{2,1,0:T(8,128)(2,1)} %copy-done.3, f32[40,40]{1,0:T(8,128)} %fusion.11.kept_ref), custom_call_target="tpu_custom_call" | custom-call | tf_op jit(solution)/shard_map/finish/pallas_call | solution.py:58
  (145 shorter events, 66.0 us)
Async XLA Ops:
  8.0 23.2 %all-to-all-start = ((bf16[8,160,320]{2,1,0:T(8,128)(2,1)}), bf16[8,160,320]{2,1,0:T(8,128)(2,1)S(1)}, u32[]{:S(2)}, u32[]{:S(2)}) async-start(bf16[8,160,320]{2,1,0:T(8,128)(2,1)} %right_columns.1), calls=%async_computation | async-start | bytes 1966080 | tf_op jit(solution)/shard_map/right_gather/all_to_all | solution.py:222
  13.0 8.1 %collective-permute-start.1 = (bf16[160,640]{1,0:T(8,128)(2,1)}, bf16[160,640]{1,0:T(8,128)(2,1)S(1)}, u32[]{:S(2)}, u32[]{:S(2)}) collective-permute-start(bf16[160,640]{1,0:T(8,128)(2,1)} %get-tuple-element.67), channel_id=1, source_target_pairs={{0,8},{1,9},{2,10},{3,11},{4,12},{5,13},{6,14},{7,15},{8,0},{9,1},... | collective-permute-start | bytes 614408 | tf_op jit(solution)/shard_map/left_columns/ppermute | solution.py:28
  14.5 12.7 %collective-permute-start.2 = (bf16[160,640]{1,0:T(8,128)(2,1)}, bf16[160,640]{1,0:T(8,128)(2,1)S(1)}, u32[]{:S(2)}, u32[]{:S(2)}) collective-permute-start(bf16[160,640]{1,0:T(8,128)(2,1)} %get-tuple-element.68), channel_id=1, source_target_pairs={{0,16},{1,17},{2,18},{3,19},{4,20},{5,21},{6,22},{7,23},{8,24},{9,... | collective-permute-start | bytes 614408 | tf_op jit(solution)/shard_map/left_columns/ppermute | solution.py:28
  17.4 12.4 %collective-permute-start.3 = (bf16[160,640]{1,0:T(8,128)(2,1)}, bf16[160,640]{1,0:T(8,128)(2,1)S(1)}, u32[]{:S(2)}, u32[]{:S(2)}) collective-permute-start(bf16[160,640]{1,0:T(8,128)(2,1)} %get-tuple-element.69), channel_id=1, source_target_pairs={{0,24},{1,25},{2,26},{3,27},{4,28},{5,29},{6,30},{7,31},{8,16},{9,... | collective-permute-start | bytes 614408 | tf_op jit(solution)/shard_map/left_columns/ppermute | solution.py:28
  18.4 12.9 %collective-permute-start.4 = (bf16[80,1280]{1,0:T(8,128)(2,1)S(1)}, bf16[80,1280]{1,0:T(8,128)(2,1)S(1)}, u32[]{:S(2)}, u32[]{:S(2)}) collective-permute-start(bf16[80,1280]{1,0:T(8,128)(2,1)S(1)} %bitcast.34), channel_id=1, source_target_pairs={{0,1},{1,0},{2,3},{3,2},{4,5},{5,4},{6,7},{7,6},{8,9},{9,8},{10,11... | collective-permute-start | bytes 614408 | tf_op jit(solution)/shard_map/density_turn/ppermute | solution.py:28
  32.5 21.3 %collective-permute-start.5 = (bf16[640,640]{1,0:T(8,128)(2,1)S(1)}, bf16[640,640]{1,0:T(8,128)(2,1)}, u32[]{:S(2)}, u32[]{:S(2)}) collective-permute-start(bf16[640,640]{1,0:T(8,128)(2,1)S(1)} %pad_maximum_fusion.2), channel_id=1, source_target_pairs={{0,4},{1,5},{2,6},{3,7},{4,0},{5,1},{6,2},{7,3},{8,12},{9,13},{10,... | collective-permute-start | bytes 2457608 | tf_op jit(solution)/shard_map/left_gather/ppermute | solution.py:28
  34.1 35.9 %collective-permute-start.6 = (bf16[640,640]{1,0:T(8,128)(2,1)S(1)}, bf16[640,640]{1,0:T(8,128)(2,1)}, u32[]{:S(2)}, u32[]{:S(2)}) collective-permute-start(bf16[640,640]{1,0:T(8,128)(2,1)S(1)} %pad_maximum_fusion.2), channel_id=1, source_target_pairs={{0,1},{1,0},{2,3},{3,2},{4,5},{5,4},{6,7},{7,6},{8,9},{9,8},{10,11... | collective-permute-start | bytes 2457608 | tf_op jit(solution)/shard_map/left_gather/ppermute | solution.py:28
  35.1 36.2 %collective-permute-start.7 = (bf16[640,640]{1,0:T(8,128)(2,1)S(1)}, bf16[640,640]{1,0:T(8,128)(2,1)}, u32[]{:S(2)}, u32[]{:S(2)}) collective-permute-start(bf16[640,640]{1,0:T(8,128)(2,1)S(1)} %pad_maximum_fusion.2), channel_id=1, source_target_pairs={{0,5},{1,4},{2,7},{3,6},{4,1},{5,0},{6,3},{7,2},{8,13},{9,12},{10,... | collective-permute-start | bytes 2457608 | tf_op jit(solution)/shard_map/left_gather/ppermute | solution.py:28
  36.1 37.7 %collective-permute-start.10 = (bf16[320,1280]{1,0:T(8,128)(2,1)S(1)}, bf16[320,1280]{1,0:T(8,128)(2,1)S(1)}, u32[]{:S(2)}, u32[]{:S(2)}) collective-permute-start(bf16[320,1280]{1,0:T(8,128)(2,1)S(1)} %reshape.58), channel_id=1, source_target_pairs={{0,96},{1,97},{2,98},{3,99},{4,100},{5,101},{6,102},{7,103},{8,104... | collective-permute-start | bytes 2457608 | tf_op jit(solution)/shard_map/right_gather/ppermute | solution.py:28
  40.1 33.6 %collective-permute-start.8 = (bf16[320,1280]{1,0:T(8,128)(2,1)S(1)}, bf16[320,1280]{1,0:T(8,128)(2,1)}, u32[]{:S(2)}, u32[]{:S(2)}) collective-permute-start(bf16[320,1280]{1,0:T(8,128)(2,1)S(1)} %reshape.58), channel_id=1, source_target_pairs={{0,32},{1,33},{2,34},{3,35},{4,36},{5,37},{6,38},{7,39},{8,40},{9,... | collective-permute-start | bytes 2457608 | tf_op jit(solution)/shard_map/right_gather/ppermute | solution.py:28
  53.9 22.3 %collective-permute-start.9 = (bf16[320,1280]{1,0:T(8,128)(2,1)S(1)}, bf16[320,1280]{1,0:T(8,128)(2,1)}, u32[]{:S(2)}, u32[]{:S(2)}) collective-permute-start(bf16[320,1280]{1,0:T(8,128)(2,1)S(1)} %reshape.58), channel_id=1, source_target_pairs={{0,64},{1,65},{2,66},{3,67},{4,68},{5,69},{6,70},{7,71},{8,72},{9,... | collective-permute-start | bytes 2457608 | tf_op jit(solution)/shard_map/right_gather/ppermute | solution.py:28
  59.7 16.5 %all-to-all-start.1 = ((bf16[4,80,640]{2,1,0:T(8,128)(2,1)}), bf16[4,80,640]{2,1,0:T(8,128)(2,1)S(1)}, u32[]{:S(2)}, u32[]{:S(2)}) async-start(bf16[4,80,640]{2,1,0:T(8,128)(2,1)} %density_columns.1), calls=%async_computation.1 | async-start | bytes 819200 | tf_op jit(solution)/shard_map/density_columns/all_to_all | solution.py:241
  82.7 11.8 %collective-permute-start.15 = (bf16[320,640]{1,0:T(8,128)(2,1)S(1)}, bf16[320,640]{1,0:T(8,128)(2,1)S(1)}, u32[]{:S(2)}, u32[]{:S(2)}) collective-permute-start(bf16[320,640]{1,0:T(8,128)(2,1)S(1)} %bitcast.29), channel_id=1, source_target_pairs={{0,32},{1,33},{2,34},{3,35},{4,36},{5,37},{6,38},{7,39},{8,40},{9,... | collective-permute-start | bytes 1228808 | tf_op jit(solution)/shard_map/density_gather/ppermute | solution.py:28
  82.7 13.0 %collective-permute-start.16 = (bf16[320,640]{1,0:T(8,128)(2,1)S(1)}, bf16[320,640]{1,0:T(8,128)(2,1)S(1)}, u32[]{:S(2)}, u32[]{:S(2)}) collective-permute-start(bf16[320,640]{1,0:T(8,128)(2,1)S(1)} %bitcast.30), channel_id=1, source_target_pairs={{0,96},{1,97},{2,98},{3,99},{4,100},{5,101},{6,102},{7,103},{8,104... | collective-permute-start | bytes 1228808 | tf_op jit(solution)/shard_map/density_gather/ppermute | solution.py:28
  89.8 11.4 %collective-permute-start.13 = (f32[80,1280]{1,0:T(8,128)S(1)}, f32[80,1280]{1,0:T(8,128)S(1)}, u32[]{:S(2)}, u32[]{:S(2)}) collective-permute-start(f32[80,1280]{1,0:T(8,128)S(1)} %get-tuple-element.133), channel_id=1, source_target_pairs={{0,8},{1,9},{2,10},{3,11},{4,12},{5,13},{6,14},{7,15},{8,0},{9,1},... | collective-permute-start | bytes 1228808 | tf_op jit(solution)/shard_map/mixed_sum/ppermute | solution.py:28
  91.4 12.3 %collective-permute-start.14 = (f32[80,1280]{1,0:T(8,128)S(1)}, f32[80,1280]{1,0:T(8,128)S(1)}, u32[]{:S(2)}, u32[]{:S(2)}) collective-permute-start(f32[80,1280]{1,0:T(8,128)S(1)} %get-tuple-element.132), channel_id=1, source_target_pairs={{0,24},{1,25},{2,26},{3,27},{4,28},{5,29},{6,30},{7,31},{8,16},{9,... | collective-permute-start | bytes 1228808 | tf_op jit(solution)/shard_map/mixed_sum/ppermute | solution.py:28
  104.0 20.2 %collective-permute-start.19 = (f32[160,1280]{1,0:T(8,128)S(1)}, f32[160,1280]{1,0:T(8,128)S(1)}, u32[]{:S(2)}, u32[]{:S(2)}) collective-permute-start(f32[160,1280]{1,0:T(8,128)S(1)} %pad_maximum_fusion.4), channel_id=1, source_target_pairs={{0,24},{1,25},{2,26},{3,27},{4,28},{5,29},{6,30},{7,31},{8,16},{9,... | collective-permute-start | bytes 2457608 | tf_op jit(solution)/shard_map/mixed_sum/ppermute | solution.py:28
  107.2 19.0 %collective-permute-start.17 = (f32[160,1280]{1,0:T(8,128)}, f32[160,1280]{1,0:T(8,128)}, u32[]{:S(2)}, u32[]{:S(2)}) collective-permute-start(f32[160,1280]{1,0:T(8,128)} %pad_maximum_fusion.3), channel_id=1, source_target_pairs={{0,8},{1,9},{2,10},{3,11},{4,12},{5,13},{6,14},{7,15},{8,0},{9,1},... | collective-permute-start | bytes 2457608 | tf_op jit(solution)/shard_map/mixed_sum/ppermute | solution.py:28
  107.2 19.0 %collective-permute-start.23 = (f32[160,1280]{1,0:T(8,128)S(1)}, f32[160,1280]{1,0:T(8,128)}, u32[]{:S(2)}, u32[]{:S(2)}) collective-permute-start(f32[160,1280]{1,0:T(8,128)S(1)} %get-tuple-element.113), channel_id=1, source_target_pairs={{0,2},{1,3},{2,0},{3,1},{4,6},{5,7},{6,4},{7,5},{8,10},{9,11},{10,... | collective-permute-start | bytes 2457608 | tf_op jit(solution)/shard_map/mixed_sum/ppermute | solution.py:28
  108.5 8.5 %collective-permute-start.21 = (bf16[160,640]{1,0:T(8,128)(2,1)S(1)}, bf16[160,640]{1,0:T(8,128)(2,1)S(1)}, u32[]{:S(2)}, u32[]{:S(2)}) collective-permute-start(bf16[160,640]{1,0:T(8,128)(2,1)S(1)} %slice.75), channel_id=1, source_target_pairs={{0,96},{1,97},{2,98},{3,99},{4,100},{5,101},{6,102},{7,103},{8,104... | collective-permute-start | bytes 614408 | tf_op jit(solution)/shard_map/density_gather/ppermute | solution.py:28
  126.2 17.1 %collective-permute-start.22 = (bf16[1280,640]{1,0:T(8,128)(2,1)}, bf16[1280,640]{1,0:T(8,128)(2,1)S(1)}, u32[]{:S(2)}, u32[]{:S(2)}) collective-permute-start(bf16[1280,640]{1,0:T(8,128)(2,1)} %density_rows.1.mine_ref), channel_id=1, source_target_pairs={{0,2},{1,3},{2,0},{3,1},{4,6},{5,7},{6,4},{7,5},{8,10},{9,11},{10,... | collective-permute-start | bytes 4915208 | tf_op jit(solution)/shard_map/mixed_gather/ppermute | solution.py:28
  128.0 13.2 %collective-permute-start.24 = (bf16[160,1280]{1,0:T(8,128)(2,1)S(1)}, bf16[160,1280]{1,0:T(8,128)(2,1)S(1)}, u32[]{:S(2)}, u32[]{:S(2)}) collective-permute-start(bf16[160,1280]{1,0:T(8,128)(2,1)S(1)} %fusion.10.refs_0_), channel_id=1, source_target_pairs={{0,24},{1,25},{2,26},{3,27},{4,28},{5,29},{6,30},{7,31},{8,16},{9,... | collective-permute-start | bytes 1228808 | tf_op jit(solution)/shard_map/mixed_gather/ppermute | solution.py:28
  129.1 12.1 %collective-permute-start.25 = (bf16[160,1280]{1,0:T(8,128)(2,1)S(1)}, bf16[160,1280]{1,0:T(8,128)(2,1)S(1)}, u32[]{:S(2)}, u32[]{:S(2)}) collective-permute-start(bf16[160,1280]{1,0:T(8,128)(2,1)S(1)} %fusion.10.refs_0_), channel_id=1, source_target_pairs={{0,8},{1,9},{2,10},{3,11},{4,12},{5,13},{6,14},{7,15},{8,0},{9,1},... | collective-permute-start | bytes 1228808 | tf_op jit(solution)/shard_map/mixed_gather/ppermute | solution.py:28
  141.2 10.3 %collective-permute-start.27 = (bf16[80,1280]{1,0:T(8,128)(2,1)S(1)}, bf16[80,1280]{1,0:T(8,128)(2,1)S(1)}, u32[]{:S(2)}, u32[]{:S(2)}) collective-permute-start(bf16[80,1280]{1,0:T(8,128)(2,1)S(1)} %slice.94), channel_id=1, source_target_pairs={{0,8},{1,9},{2,10},{3,11},{4,12},{5,13},{6,14},{7,15},{8,0},{9,1},... | collective-permute-start | bytes 614408 | tf_op jit(solution)/shard_map/mixed_gather/ppermute | solution.py:28
  141.3 10.2 %collective-permute-start.28 = (bf16[80,1280]{1,0:T(8,128)(2,1)S(1)}, bf16[80,1280]{1,0:T(8,128)(2,1)}, u32[]{:S(2)}, u32[]{:S(2)}) collective-permute-start(bf16[80,1280]{1,0:T(8,128)(2,1)S(1)} %slice.95), channel_id=1, source_target_pairs={{0,24},{1,25},{2,26},{3,27},{4,28},{5,29},{6,30},{7,31},{8,16},{9,... | collective-permute-start | bytes 614408 | tf_op jit(solution)/shard_map/mixed_gather/ppermute | solution.py:28
  151.5 15.8 %collective-permute-start.31 = (bf16[2,3,40,640]{3,2,1,0:T(8,128)(2,1)}, bf16[2,3,40,640]{3,2,1,0:T(8,128)(2,1)S(1)}, u32[]{:S(2)}, u32[]{:S(2)}) collective-permute-start(bf16[2,3,40,640]{3,2,1,0:T(8,128)(2,1)} %get-tuple-element.101), channel_id=1, source_target_pairs={{0,3},{1,2},{2,5},{3,4},{4,7},{5,6},{6,1},{7,0},{8,11},{9,10},{10,... | collective-permute-start | bytes 921608 | tf_op jit(solution)/shard_map/second_product/ppermute | solution.py:42
  153.7 14.2 %collective-permute-start.29 = (bf16[2,3,40,640]{3,2,1,0:T(8,128)(2,1)}, bf16[2,3,40,640]{3,2,1,0:T(8,128)(2,1)S(1)}, u32[]{:S(2)}, u32[]{:S(2)}) collective-permute-start(bf16[2,3,40,640]{3,2,1,0:T(8,128)(2,1)} %get-tuple-element.99), channel_id=1, source_target_pairs={{0,2},{1,3},{2,4},{3,5},{4,6},{5,7},{6,0},{7,1},{8,10},{9,11},{10,... | collective-permute-start | bytes 921608 | tf_op jit(solution)/shard_map/second_product/ppermute | solution.py:42
  153.7 15.4 %collective-permute-start.30 = (bf16[2,3,40,640]{3,2,1,0:T(8,128)(2,1)}, bf16[2,3,40,640]{3,2,1,0:T(8,128)(2,1)S(1)}, u32[]{:S(2)}, u32[]{:S(2)}) collective-permute-start(bf16[2,3,40,640]{3,2,1,0:T(8,128)(2,1)} %get-tuple-element.100), channel_id=1, source_target_pairs={{0,1},{1,0},{2,7},{3,6},{4,5},{5,4},{6,3},{7,2},{8,9},{9,8},{10,15... | collective-permute-start | bytes 921608 | tf_op jit(solution)/shard_map/second_product/ppermute | solution.py:42
  160.2 8.9 %collective-permute-start.32 = (bf16[2,1,40,640]{3,2,1,0:T(8,128)(2,1)}, bf16[2,1,40,640]{3,2,1,0:T(8,128)(2,1)S(1)}, u32[]{:S(2)}, u32[]{:S(2)}) collective-permute-start(bf16[2,1,40,640]{3,2,1,0:T(8,128)(2,1)} %get-tuple-element.104), channel_id=1, source_target_pairs={{0,0},{1,1},{2,6},{3,7},{4,4},{5,5},{6,2},{7,3},{8,8},{9,9},{10,14... | collective-permute-start | bytes 307208 | tf_op jit(solution)/shard_map/second_product/ppermute | solution.py:42
  161.8 9.0 %collective-permute-start.33 = (bf16[2,1,40,640]{3,2,1,0:T(8,128)(2,1)}, bf16[2,1,40,640]{3,2,1,0:T(8,128)(2,1)S(1)}, u32[]{:S(2)}, u32[]{:S(2)}) collective-permute-start(bf16[2,1,40,640]{3,2,1,0:T(8,128)(2,1)} %get-tuple-element.105), channel_id=1, source_target_pairs={{0,2},{1,3},{2,4},{3,5},{4,6},{5,7},{6,0},{7,1},{8,10},{9,11},{10,... | collective-permute-start | bytes 307208 | tf_op jit(solution)/shard_map/second_product/ppermute | solution.py:42
  177.9 18.6 %all-to-all-start.2 = ((bf16[32,40,160]{2,1,0:T(8,128)(2,1)}), bf16[32,40,160]{2,1,0:T(8,128)(2,1)S(1)}, u32[]{:S(2)}, u32[]{:S(2)}) async-start(bf16[32,40,160]{2,1,0:T(8,128)(2,1)} %get-tuple-element.112), calls=%async_computation.2 | async-start | bytes 1310720 | tf_op jit(solution)/shard_map/transposed/all_to_all | solution.py:333
  185.6 7.7 %collective-permute-start.37 = (bf16[40,1280]{1,0:T(8,128)(2,1)}, bf16[40,1280]{1,0:T(8,128)(2,1)S(1)}, u32[]{:S(2)}, u32[]{:S(2)}) collective-permute-start(bf16[40,1280]{1,0:T(8,128)(2,1)} %get-tuple-element.110), channel_id=1, source_target_pairs={{0,16},{1,17},{2,18},{3,19},{4,20},{5,21},{6,22},{7,23},{8,24},{9,... | collective-permute-start | bytes 307208 | tf_op jit(solution)/shard_map/direct/ppermute | solution.py:28
  (40 other events, 264.3 us)

commit v14 on v13

--- a/solution.py
+++ b/solution.py
@@ -177,11 +177,11 @@
         for ny in range(4):
             other = jnp.concatenate(
                 [
-                    t_ref[nz * 8 + s, :, ny * 40 : (ny + 1) * 40].astype(f32)
+                    t_ref[nz * 8 + s, :, ny * 40 : (ny + 1) * 40]
                     for s in range(8)
                 ],
                 axis=1,
-            )
+            ).astype(f32)
             blocks.append(slots[y ^ ny, :, nz * 320 : (nz + 1) * 320] + other)
         block = 0.5 * jnp.concatenate(blocks, axis=1)
         kept = jnp.concatenate(

time: 203 us -> 203 us (level)
  no operation moved by 1% of the time
where the time goes in v14:
time: 203 us; the launch traced here: 201 us
  waiting for transfers between devices  76.8 us (38%)
  starting transfers between devices  70.1 us (35%)
  Pallas kernels  25.9 us (13%)
  other arithmetic  12.1 us (6%)
  local copies, waits for them, and re-layouts  10.5 us (5%)
  matrix products  5.35 us (3%)
    ppermute x31, waiting for transfers between devices, flip(): return lax.ppermute(value, AXES, pairs)  71 us
    ppermute x31, starting transfers between devices, flip(): return lax.ppermute(value, AXES, pairs)  38.4 us
    pallas_call x8, Pallas kernels, local_call(): pl.pallas_call(kernel, out_shape=outs, in_specs=[SMEM] + [VMEM] * len(ope...  25.9 us
    ppermute x8, starting transfers between devices, remap(): return lax.ppermute(value, AXES, pairs)  15.5 us
    unnamed x60, local copies, waits for them, and re-layouts  7.23 us
    all_to_all x1, starting transfers between devices, shards(): lax.all_to_all(turned, ('z', 'xl', 'core', 'xh'), split_axis=0, concat_ax...  6.79 us
    select_n x2, other arithmetic, shards(): mine = [jnp.where(core == 0, lefts[0, r], lefts[1, r]) for r in range(2)]  4.92 us
    all_to_all x1, starting transfers between devices, shards(): lax.all_to_all(parts, ('xl', 'core', 'xh'), split_axis=0, concat_axis=0,...  4.92 us
  transfers between devices with their start and end apart: 42, of which 23 were waited for; matrix products, arithmetic and copies ran while one was open for 7% of the time, Pallas kernels for 8%

profile of v14, /device:TPU:2, one launch (start us, length us, event | category | flops | bytes accessed | tf_op | source)
XLA Modules:
  0.0 201.1 jit_solution(12916486456904953337)
XLA Ops:
  1.9 2.7 %right_columns.1 = bf16[8,160,320]{2,1,0:T(8,128)(2,1)} custom-call(s32[5]{0:T(128)} %stack.38.at_ref, bf16[160,1280]{1,0:T(8,128)(2,1)} %first_ref.1, bf16[160,1280]{1,0:T(8,128)(2,1)} %second_ref.1), custom_call_target="tpu_custom_call" | custom-call | tf_op jit(solution)/shard_map/right_columns/right_columns/pallas_call | solution.py:58
  5.4 2.6 %left_columns.1 = (bf16[160,640]{1,0:T(8,128)(2,1)}, bf16[160,640]{1,0:T(8,128)(2,1)}, bf16[160,640]{1,0:T(8,128)(2,1)}, bf16[160,640]{1,0:T(8,128)(2,1)}) custom-call(s32[5]{0:T(128)} %stack.38.at_ref, bf16[160,1280]{1,0:T(8,128)(2,1)} %first_ref.2, bf16[160,1280]{1,0:T(8,128)(2,1)} %second_ref.2, bf16[160,1280]{1,0:T(8,128)(2,1)} %copy-done.13), custom_call_target="tpu_custom_call" | custom-call | tf_op jit(solution)/shard_map/left_columns/left_columns/pallas_call | solution.py:58
  8.0 4.9 %all-to-all-start = ((bf16[8,160,320]{2,1,0:T(8,128)(2,1)}), bf16[8,160,320]{2,1,0:T(8,128)(2,1)S(1)}, u32[]{:S(2)}, u32[]{:S(2)}) async-start(bf16[8,160,320]{2,1,0:T(8,128)(2,1)} %right_columns.1), calls=%async_computation | async-start | bytes 1966080 | tf_op jit(solution)/shard_map/right_gather/all_to_all | solution.py:222
  14.5 2.9 %collective-permute-start.2 = (bf16[160,640]{1,0:T(8,128)(2,1)}, bf16[160,640]{1,0:T(8,128)(2,1)S(1)}, u32[]{:S(2)}, u32[]{:S(2)}) collective-permute-start(bf16[160,640]{1,0:T(8,128)(2,1)} %get-tuple-element.68), channel_id=1, source_target_pairs={{0,16},{1,17},{2,18},{3,19},{4,20},{5,21},{6,22},{7,23},{8,24},{9,... | collective-permute-start | bytes 614408 | tf_op jit(solution)/shard_map/left_columns/ppermute | solution.py:28
  21.1 6.1 %collective-permute-done.2 = bf16[160,640]{1,0:T(8,128)(2,1)S(1)} collective-permute-done((bf16[160,640]{1,0:T(8,128)(2,1)}, bf16[160,640]{1,0:T(8,128)(2,1)S(1)}, u32[]{:S(2)}, u32[]{:S(2)}) %collective-permute-start.2) | collective-permute-done | bytes 204832 | tf_op jit(solution)/shard_map/left_columns/ppermute | solution.py:28
  27.2 2.6 %collective-permute-done.3 = bf16[160,640]{1,0:T(8,128)(2,1)S(1)} collective-permute-done((bf16[160,640]{1,0:T(8,128)(2,1)}, bf16[160,640]{1,0:T(8,128)(2,1)S(1)}, u32[]{:S(2)}, u32[]{:S(2)}) %collective-permute-start.3) | collective-permute-done | bytes 204832 | tf_op jit(solution)/shard_map/left_columns/ppermute | solution.py:28
  36.1 4.0 %collective-permute-start.10 = (bf16[320,1280]{1,0:T(8,128)(2,1)S(1)}, bf16[320,1280]{1,0:T(8,128)(2,1)S(1)}, u32[]{:S(2)}, u32[]{:S(2)}) collective-permute-start(bf16[320,1280]{1,0:T(8,128)(2,1)S(1)} %reshape.58), channel_id=1, source_target_pairs={{0,96},{1,97},{2,98},{3,99},{4,100},{5,101},{6,102},{7,103},{8,104... | collective-permute-start | bytes 2457608 | tf_op jit(solution)/shard_map/right_gather/ppermute | solution.py:28
  40.1 13.7 %collective-permute-done.5 = bf16[640,640]{1,0:T(8,128)(2,1)} collective-permute-done((bf16[640,640]{1,0:T(8,128)(2,1)S(1)}, bf16[640,640]{1,0:T(8,128)(2,1)}, u32[]{:S(2)}, u32[]{:S(2)}) %collective-permute-start.5) | collective-permute-done | bytes 819232 | tf_op jit(solution)/shard_map/left_gather/ppermute | solution.py:28
  53.9 3.9 %collective-permute-start.9 = (bf16[320,1280]{1,0:T(8,128)(2,1)S(1)}, bf16[320,1280]{1,0:T(8,128)(2,1)}, u32[]{:S(2)}, u32[]{:S(2)}) collective-permute-start(bf16[320,1280]{1,0:T(8,128)(2,1)S(1)} %reshape.58), channel_id=1, source_target_pairs={{0,64},{1,65},{2,66},{3,67},{4,68},{5,69},{6,70},{7,71},{8,72},{9,... | collective-permute-start | bytes 2457608 | tf_op jit(solution)/shard_map/right_gather/ppermute | solution.py:28
  59.7 4.5 %all-to-all-start.1 = ((bf16[4,80,640]{2,1,0:T(8,128)(2,1)}), bf16[4,80,640]{2,1,0:T(8,128)(2,1)S(1)}, u32[]{:S(2)}, u32[]{:S(2)}) async-start(bf16[4,80,640]{2,1,0:T(8,128)(2,1)} %density_columns.1), calls=%async_computation.1 | async-start | bytes 819200 | tf_op jit(solution)/shard_map/density_columns/all_to_all | solution.py:241
  64.1 2.5 %broadcast_select_fusion.3 = (bf16[640,640]{1,0:T(8,128)(2,1)}, bf16[640,640]{1,0:T(8,128)(2,1)}) fusion(bf16[640,640]{1,0:T(8,128)(2,1)S(1)} %pad_maximum_fusion.2, bf16[640,640]{1,0:T(8,128)(2,1)} %collective-permute-done.5, pred[]{:T(512)S(6)} %eq.8), kind=kLoop, calls=%fused_computation.28 | loop fusion | flops 819200 | bytes 3276801 | tf_op jit(solution)/shard_map/first_product/jit(_where)/select_n | solution.py:255
  66.6 3.3 %collective-permute-done.6 = bf16[640,640]{1,0:T(8,128)(2,1)} collective-permute-done((bf16[640,640]{1,0:T(8,128)(2,1)S(1)}, bf16[640,640]{1,0:T(8,128)(2,1)}, u32[]{:S(2)}, u32[]{:S(2)}) %collective-permute-start.6) | collective-permute-done | bytes 819232 | tf_op jit(solution)/shard_map/left_gather/ppermute | solution.py:28
  71.3 2.4 %broadcast_select_fusion.2 = (bf16[640,640]{1,0:T(8,128)(2,1)S(1)}, bf16[640,640]{1,0:T(8,128)(2,1)}) fusion(bf16[640,640]{1,0:T(8,128)(2,1)} %collective-permute-done.6, bf16[640,640]{1,0:T(8,128)(2,1)} %collective-permute-done.7, pred[]{:T(512)S(6)} %eq.8), kind=kLoop, calls=%fused_computation.27 | loop fusion | flops 819200 | bytes 3276801 | tf_op jit(solution)/shard_map/first_product/jit(_where)/select_n | solution.py:255
  73.8 2.4 %collective-permute-done.9 = bf16[320,1280]{1,0:T(8,128)(2,1)} collective-permute-done((bf16[320,1280]{1,0:T(8,128)(2,1)S(1)}, bf16[320,1280]{1,0:T(8,128)(2,1)}, u32[]{:S(2)}, u32[]{:S(2)}) %collective-permute-start.9) | collective-permute-done | bytes 819232 | tf_op jit(solution)/shard_map/right_gather/ppermute | solution.py:28
  79.3 2.3 %fusion.4 = f32[640,1280]{1,0:T(8,128)S(1)} fusion(bf16[640,640]{1,0:T(8,128)(2,1)S(1)} %copy-done.12, bf16[640,640]{1,0:T(8,128)(2,1)S(1)} %copy-done.11, bf16[320,1280]{1,0:T(8,128)(2,1)S(1)} %get-tuple-element.121, bf16[320,1280]{1,0:T(8,128)(2,1)S(1)} %get-tuple-element.122, bf16[320,1280]{1,0:T(8,128)(2,1)S(1)} %get-tuple-element.123, ...), kind=kOutput, calls=%fused_computation.6 | convolution fusion | flops 2113536000 | bytes 8192000 | tf_op jit(solution)/shard_map/first_product/dot_general | solution.py:50
  82.7 3.1 %collective-permute-start.16 = (bf16[320,640]{1,0:T(8,128)(2,1)S(1)}, bf16[320,640]{1,0:T(8,128)(2,1)S(1)}, u32[]{:S(2)}, u32[]{:S(2)}) collective-permute-start(bf16[320,640]{1,0:T(8,128)(2,1)S(1)} %bitcast.30), channel_id=1, source_target_pairs={{0,96},{1,97},{2,98},{3,99},{4,100},{5,101},{6,102},{7,103},{8,104... | collective-permute-start | bytes 1228808 | tf_op jit(solution)/shard_map/density_gather/ppermute | solution.py:28
  85.8 2.3 %fusion = f32[640,1280]{1,0:T(8,128)S(1)} fusion(bf16[640,640]{1,0:T(8,128)(2,1)S(1)} %get-tuple-element.126, bf16[640,640]{1,0:T(8,128)(2,1)S(1)} %copy-done.10, bf16[320,1280]{1,0:T(8,128)(2,1)S(1)} %get-tuple-element.121, bf16[320,1280]{1,0:T(8,128)(2,1)S(1)} %get-tuple-element.122, bf16[320,1280]{1,0:T(8,128)(2,1)S(1)} %get-tuple-element.123, ...), kind=kOutput, calls=%fused_computation.2 | convolution fusion | flops 2113536000 | bytes 8192000 | tf_op jit(solution)/shard_map/first_product/dot_general | solution.py:50
  95.7 5.5 %collective-permute-done.13 = f32[80,1280]{1,0:T(8,128)S(1)} collective-permute-done((f32[80,1280]{1,0:T(8,128)S(1)}, f32[80,1280]{1,0:T(8,128)S(1)}, u32[]{:S(2)}, u32[]{:S(2)}) %collective-permute-start.13) | collective-permute-done | bytes 409632 | tf_op jit(solution)/shard_map/mixed_sum/ppermute | solution.py:28
  101.2 2.5 %collective-permute-done.14 = f32[80,1280]{1,0:T(8,128)S(1)} collective-permute-done((f32[80,1280]{1,0:T(8,128)S(1)}, f32[80,1280]{1,0:T(8,128)S(1)}, u32[]{:S(2)}, u32[]{:S(2)}) %collective-permute-start.14) | collective-permute-done | bytes 409632 | tf_op jit(solution)/shard_map/mixed_sum/ppermute | solution.py:28
  109.4 5.3 %collective-permute-done.20.upper_ref = bf16[160,640]{1,0:T(8,128)(2,1)S(1)} collective-permute-done((bf16[160,640]{1,0:T(8,128)(2,1)S(1)}, bf16[160,640]{1,0:T(8,128)(2,1)S(1)}, u32[]{:S(2)}, u32[]{:S(2)}) %collective-permute-start.20) | collective-permute-done | bytes 204832 | tf_op jit(solution)/shard_map/density_gather/ppermute | solution.py:28
  117.7 2.7 %density_rows.1.mine_ref = bf16[1280,640]{1,0:T(8,128)(2,1)} custom-call(s32[5]{0:T(128)} %stack.38.at_ref, bf16[320,640]{1,0:T(8,128)(2,1)} %bitcast.31, bf16[320,640]{1,0:T(8,128)(2,1)} %copy-done.8, bf16[160,640]{1,0:T(8,128)(2,1)} %copy-done.20, bf16[160,640]{1,0:T(8,128)(2,1)} %copy-done.21, bf16[320,640]{1,0:T(8,128)(2,1)} %copy-done.9), custom_call_target="tpu_custom_call" | custom-call | tf_op jit(solution)/shard_map/density_rows/density_rows/pallas_call | solution.py:58
  120.4 3.8 %collective-permute-done.19 = f32[160,1280]{1,0:T(8,128)S(1)} collective-permute-done((f32[160,1280]{1,0:T(8,128)S(1)}, f32[160,1280]{1,0:T(8,128)S(1)}, u32[]{:S(2)}, u32[]{:S(2)}) %collective-permute-start.19) | collective-permute-done | bytes 819232 | tf_op jit(solution)/shard_map/mixed_sum/ppermute | solution.py:28
  129.1 12.0 %collective-permute-done.24.refs_2_ = bf16[160,1280]{1,0:T(8,128)(2,1)S(1)} collective-permute-done((bf16[160,1280]{1,0:T(8,128)(2,1)S(1)}, bf16[160,1280]{1,0:T(8,128)(2,1)S(1)}, u32[]{:S(2)}, u32[]{:S(2)}) %collective-permute-start.24) | collective-permute-done | bytes 409632 | tf_op jit(solution)/shard_map/mixed_gather/ppermute | solution.py:28
  144.4 5.4 %second_product.2 = (bf16[2,3,40,640]{3,2,1,0:T(8,128)(2,1)}, bf16[2,3,40,640]{3,2,1,0:T(8,128)(2,1)}, bf16[2,3,40,640]{3,2,1,0:T(8,128)(2,1)}, bf16[2,3,40,640]{3,2,1,0:T(8,128)(2,1)}) custom-call(s32[5]{0:T(128)} %stack.38.at_ref, bf16[1280,640]{1,0:T(8,128)(2,1)} %density_rows.1.mine_ref, bf16[1280,640]{1,0:T(8,128)(2,1)} %copy-done, ...), custom_call_target="tpu_custom_call" | custom-call | tf_op jit(solution)/shard_map/second_product/second_product/pallas_call | solution.py:58
  153.7 2.8 %collective-permute-start.30 = (bf16[2,3,40,640]{3,2,1,0:T(8,128)(2,1)}, bf16[2,3,40,640]{3,2,1,0:T(8,128)(2,1)S(1)}, u32[]{:S(2)}, u32[]{:S(2)}) collective-permute-start(bf16[2,3,40,640]{3,2,1,0:T(8,128)(2,1)} %get-tuple-element.100), channel_id=1, source_target_pairs={{0,1},{1,0},{2,7},{3,6},{4,5},{5,4},{6,3},{7,2},{8,9},{9,8},{10,15... | collective-permute-start | bytes 921608 | tf_op jit(solution)/shard_map/second_product/ppermute | solution.py:42
  156.5 3.7 %second_product.3 = (bf16[2,1,40,640]{3,2,1,0:T(8,128)(2,1)}, bf16[2,1,40,640]{3,2,1,0:T(8,128)(2,1)}, bf16[2,1,40,640]{3,2,1,0:T(8,128)(2,1)}, bf16[2,1,40,640]{3,2,1,0:T(8,128)(2,1)}) custom-call(s32[5]{0:T(128)} %stack.38.at_ref, bf16[1280,640]{1,0:T(8,128)(2,1)} %density_rows.1.mine_ref, bf16[1280,640]{1,0:T(8,128)(2,1)} %copy-done, ...), custom_call_target="tpu_custom_call" | custom-call | tf_op jit(solution)/shard_map/second_product/second_product/pallas_call | solution.py:58
  161.8 5.5 %collective-permute-start.33 = (bf16[2,1,40,640]{3,2,1,0:T(8,128)(2,1)}, bf16[2,1,40,640]{3,2,1,0:T(8,128)(2,1)S(1)}, u32[]{:S(2)}, u32[]{:S(2)}) collective-permute-start(bf16[2,1,40,640]{3,2,1,0:T(8,128)(2,1)} %get-tuple-element.105), channel_id=1, source_target_pairs={{0,2},{1,3},{2,4},{3,5},{4,6},{5,7},{6,0},{7,1},{8,10},{9,11},{10,... | collective-permute-start | bytes 307208 | tf_op jit(solution)/shard_map/second_product/ppermute | solution.py:42
  170.7 2.9 %collective-permute-done.34.refs_6_ = bf16[2,1,40,640]{3,2,1,0:T(8,128)(2,1)S(1)} collective-permute-done((bf16[2,1,40,640]{3,2,1,0:T(8,128)(2,1)}, bf16[2,1,40,640]{3,2,1,0:T(8,128)(2,1)S(1)}, u32[]{:S(2)}, u32[]{:S(2)}) %collective-permute-start.34) | collective-permute-done | bytes 102432 | tf_op jit(solution)/shard_map/second_product/ppermute | solution.py:42
  174.9 2.9 %spread.1 = (bf16[32,40,160]{2,1,0:T(8,128)(2,1)}, f32[40,1280]{1,0:T(8,128)}, bf16[40,1280]{1,0:T(8,128)(2,1)}, bf16[40,1280]{1,0:T(8,128)(2,1)}, bf16[40,1280]{1,0:T(8,128)(2,1)}) custom-call(s32[5]{0:T(128)} %stack.38.at_ref, bf16[2,3,40,640]{3,2,1,0:T(8,128)(2,1)} %copy-done.14, bf16[2,3,40,640]{3,2,1,0:T(8,128)(2,1)} %copy-done.16, ...), custom_call_target="tpu_custom_call" | custom-call | tf_op jit(solution)/shard_map/second_product/spread/pallas_call | solution.py:58
  177.9 6.8 %all-to-all-start.2 = ((bf16[32,40,160]{2,1,0:T(8,128)(2,1)}), bf16[32,40,160]{2,1,0:T(8,128)(2,1)S(1)}, u32[]{:S(2)}, u32[]{:S(2)}) async-start(bf16[32,40,160]{2,1,0:T(8,128)(2,1)} %get-tuple-element.112), calls=%async_computation.2 | async-start | bytes 1310720 | tf_op jit(solution)/shard_map/transposed/all_to_all | solution.py:333
  190.7 2.6 %collective-permute-done.37.d2 = bf16[40,1280]{1,0:T(8,128)(2,1)S(1)} collective-permute-done((bf16[40,1280]{1,0:T(8,128)(2,1)}, bf16[40,1280]{1,0:T(8,128)(2,1)S(1)}, u32[]{:S(2)}, u32[]{:S(2)}) %collective-permute-start.37) | collective-permute-done | bytes 102432 | tf_op jit(solution)/shard_map/direct/ppermute | solution.py:28
  197.3 3.8 %finish.1 = f32[40,5120]{1,0:T(8,128)} custom-call(s32[5]{0:T(128)} %stack.38.at_ref, f32[40,1280]{1,0:T(8,128)} %get-tuple-element.108.d0, bf16[40,1280]{1,0:T(8,128)(2,1)} %copy-done.26, bf16[40,1280]{1,0:T(8,128)(2,1)} %copy-done.27, bf16[40,1280]{1,0:T(8,128)(2,1)} %copy-done.28, bf16[32,40,160]{2,1,0:T(8,128)(2,1)} %copy-done.3, f32[40,40]{1,0:T(8,128)} %fusion.11.kept_ref), custom_call_target="tpu_custom_call" | custom-call | tf_op jit(solution)/shard_map/finish/pallas_call | solution.py:58
  (145 shorter events, 66.0 us)
Async XLA Ops:
  8.0 23.2 %all-to-all-start = ((bf16[8,160,320]{2,1,0:T(8,128)(2,1)}), bf16[8,160,320]{2,1,0:T(8,128)(2,1)S(1)}, u32[]{:S(2)}, u32[]{:S(2)}) async-start(bf16[8,160,320]{2,1,0:T(8,128)(2,1)} %right_columns.1), calls=%async_computation | async-start | bytes 1966080 | tf_op jit(solution)/shard_map/right_gather/all_to_all | solution.py:222
  13.0 8.1 %collective-permute-start.1 = (bf16[160,640]{1,0:T(8,128)(2,1)}, bf16[160,640]{1,0:T(8,128)(2,1)S(1)}, u32[]{:S(2)}, u32[]{:S(2)}) collective-permute-start(bf16[160,640]{1,0:T(8,128)(2,1)} %get-tuple-element.67), channel_id=1, source_target_pairs={{0,8},{1,9},{2,10},{3,11},{4,12},{5,13},{6,14},{7,15},{8,0},{9,1},... | collective-permute-start | bytes 614408 | tf_op jit(solution)/shard_map/left_columns/ppermute | solution.py:28
  14.5 12.7 %collective-permute-start.2 = (bf16[160,640]{1,0:T(8,128)(2,1)}, bf16[160,640]{1,0:T(8,128)(2,1)S(1)}, u32[]{:S(2)}, u32[]{:S(2)}) collective-permute-start(bf16[160,640]{1,0:T(8,128)(2,1)} %get-tuple-element.68), channel_id=1, source_target_pairs={{0,16},{1,17},{2,18},{3,19},{4,20},{5,21},{6,22},{7,23},{8,24},{9,... | collective-permute-start | bytes 614408 | tf_op jit(solution)/shard_map/left_columns/ppermute | solution.py:28
  17.4 12.4 %collective-permute-start.3 = (bf16[160,640]{1,0:T(8,128)(2,1)}, bf16[160,640]{1,0:T(8,128)(2,1)S(1)}, u32[]{:S(2)}, u32[]{:S(2)}) collective-permute-start(bf16[160,640]{1,0:T(8,128)(2,1)} %get-tuple-element.69), channel_id=1, source_target_pairs={{0,24},{1,25},{2,26},{3,27},{4,28},{5,29},{6,30},{7,31},{8,16},{9,... | collective-permute-start | bytes 614408 | tf_op jit(solution)/shard_map/left_columns/ppermute | solution.py:28
  18.4 12.9 %collective-permute-start.4 = (bf16[80,1280]{1,0:T(8,128)(2,1)S(1)}, bf16[80,1280]{1,0:T(8,128)(2,1)S(1)}, u32[]{:S(2)}, u32[]{:S(2)}) collective-permute-start(bf16[80,1280]{1,0:T(8,128)(2,1)S(1)} %bitcast.34), channel_id=1, source_target_pairs={{0,1},{1,0},{2,3},{3,2},{4,5},{5,4},{6,7},{7,6},{8,9},{9,8},{10,11... | collective-permute-start | bytes 614408 | tf_op jit(solution)/shard_map/density_turn/ppermute | solution.py:28
  32.5 21.3 %collective-permute-start.5 = (bf16[640,640]{1,0:T(8,128)(2,1)S(1)}, bf16[640,640]{1,0:T(8,128)(2,1)}, u32[]{:S(2)}, u32[]{:S(2)}) collective-permute-start(bf16[640,640]{1,0:T(8,128)(2,1)S(1)} %pad_maximum_fusion.2), channel_id=1, source_target_pairs={{0,4},{1,5},{2,6},{3,7},{4,0},{5,1},{6,2},{7,3},{8,12},{9,13},{10,... | collective-permute-start | bytes 2457608 | tf_op jit(solution)/shard_map/left_gather/ppermute | solution.py:28
  34.1 35.9 %collective-permute-start.6 = (bf16[640,640]{1,0:T(8,128)(2,1)S(1)}, bf16[640,640]{1,0:T(8,128)(2,1)}, u32[]{:S(2)}, u32[]{:S(2)}) collective-permute-start(bf16[640,640]{1,0:T(8,128)(2,1)S(1)} %pad_maximum_fusion.2), channel_id=1, source_target_pairs={{0,1},{1,0},{2,3},{3,2},{4,5},{5,4},{6,7},{7,6},{8,9},{9,8},{10,11... | collective-permute-start | bytes 2457608 | tf_op jit(solution)/shard_map/left_gather/ppermute | solution.py:28
  35.1 36.2 %collective-permute-start.7 = (bf16[640,640]{1,0:T(8,128)(2,1)S(1)}, bf16[640,640]{1,0:T(8,128)(2,1)}, u32[]{:S(2)}, u32[]{:S(2)}) collective-permute-start(bf16[640,640]{1,0:T(8,128)(2,1)S(1)} %pad_maximum_fusion.2), channel_id=1, source_target_pairs={{0,5},{1,4},{2,7},{3,6},{4,1},{5,0},{6,3},{7,2},{8,13},{9,12},{10,... | collective-permute-start | bytes 2457608 | tf_op jit(solution)/shard_map/left_gather/ppermute | solution.py:28
  36.1 37.7 %collective-permute-start.10 = (bf16[320,1280]{1,0:T(8,128)(2,1)S(1)}, bf16[320,1280]{1,0:T(8,128)(2,1)S(1)}, u32[]{:S(2)}, u32[]{:S(2)}) collective-permute-start(bf16[320,1280]{1,0:T(8,128)(2,1)S(1)} %reshape.58), channel_id=1, source_target_pairs={{0,96},{1,97},{2,98},{3,99},{4,100},{5,101},{6,102},{7,103},{8,104... | collective-permute-start | bytes 2457608 | tf_op jit(solution)/shard_map/right_gather/ppermute | solution.py:28
  40.1 33.6 %collective-permute-start.8 = (bf16[320,1280]{1,0:T(8,128)(2,1)S(1)}, bf16[320,1280]{1,0:T(8,128)(2,1)}, u32[]{:S(2)}, u32[]{:S(2)}) collective-permute-start(bf16[320,1280]{1,0:T(8,128)(2,1)S(1)} %reshape.58), channel_id=1, source_target_pairs={{0,32},{1,33},{2,34},{3,35},{4,36},{5,37},{6,38},{7,39},{8,40},{9,... | collective-permute-start | bytes 2457608 | tf_op jit(solution)/shard_map/right_gather/ppermute | solution.py:28
  53.9 22.3 %collective-permute-start.9 = (bf16[320,1280]{1,0:T(8,128)(2,1)S(1)}, bf16[320,1280]{1,0:T(8,128)(2,1)}, u32[]{:S(2)}, u32[]{:S(2)}) collective-permute-start(bf16[320,1280]{1,0:T(8,128)(2,1)S(1)} %reshape.58), channel_id=1, source_target_pairs={{0,64},{1,65},{2,66},{3,67},{4,68},{5,69},{6,70},{7,71},{8,72},{9,... | collective-permute-start | bytes 2457608 | tf_op jit(solution)/shard_map/right_gather/ppermute | solution.py:28
  59.7 16.5 %all-to-all-start.1 = ((bf16[4,80,640]{2,1,0:T(8,128)(2,1)}), bf16[4,80,640]{2,1,0:T(8,128)(2,1)S(1)}, u32[]{:S(2)}, u32[]{:S(2)}) async-start(bf16[4,80,640]{2,1,0:T(8,128)(2,1)} %density_columns.1), calls=%async_computation.1 | async-start | bytes 819200 | tf_op jit(solution)/shard_map/density_columns/all_to_all | solution.py:241
  82.7 11.8 %collective-permute-start.15 = (bf16[320,640]{1,0:T(8,128)(2,1)S(1)}, bf16[320,640]{1,0:T(8,128)(2,1)S(1)}, u32[]{:S(2)}, u32[]{:S(2)}) collective-permute-start(bf16[320,640]{1,0:T(8,128)(2,1)S(1)} %bitcast.29), channel_id=1, source_target_pairs={{0,32},{1,33},{2,34},{3,35},{4,36},{5,37},{6,38},{7,39},{8,40},{9,... | collective-permute-start | bytes 1228808 | tf_op jit(solution)/shard_map/density_gather/ppermute | solution.py:28
  82.7 13.0 %collective-permute-start.16 = (bf16[320,640]{1,0:T(8,128)(2,1)S(1)}, bf16[320,640]{1,0:T(8,128)(2,1)S(1)}, u32[]{:S(2)}, u32[]{:S(2)}) collective-permute-start(bf16[320,640]{1,0:T(8,128)(2,1)S(1)} %bitcast.30), channel_id=1, source_target_pairs={{0,96},{1,97},{2,98},{3,99},{4,100},{5,101},{6,102},{7,103},{8,104... | collective-permute-start | bytes 1228808 | tf_op jit(solution)/shard_map/density_gather/ppermute | solution.py:28
  89.8 11.4 %collective-permute-start.13 = (f32[80,1280]{1,0:T(8,128)S(1)}, f32[80,1280]{1,0:T(8,128)S(1)}, u32[]{:S(2)}, u32[]{:S(2)}) collective-permute-start(f32[80,1280]{1,0:T(8,128)S(1)} %get-tuple-element.133), channel_id=1, source_target_pairs={{0,8},{1,9},{2,10},{3,11},{4,12},{5,13},{6,14},{7,15},{8,0},{9,1},... | collective-permute-start | bytes 1228808 | tf_op jit(solution)/shard_map/mixed_sum/ppermute | solution.py:28
  91.4 12.3 %collective-permute-start.14 = (f32[80,1280]{1,0:T(8,128)S(1)}, f32[80,1280]{1,0:T(8,128)S(1)}, u32[]{:S(2)}, u32[]{:S(2)}) collective-permute-start(f32[80,1280]{1,0:T(8,128)S(1)} %get-tuple-element.132), channel_id=1, source_target_pairs={{0,24},{1,25},{2,26},{3,27},{4,28},{5,29},{6,30},{7,31},{8,16},{9,... | collective-permute-start | bytes 1228808 | tf_op jit(solution)/shard_map/mixed_sum/ppermute | solution.py:28
  104.0 20.2 %collective-permute-start.19 = (f32[160,1280]{1,0:T(8,128)S(1)}, f32[160,1280]{1,0:T(8,128)S(1)}, u32[]{:S(2)}, u32[]{:S(2)}) collective-permute-start(f32[160,1280]{1,0:T(8,128)S(1)} %pad_maximum_fusion.4), channel_id=1, source_target_pairs={{0,24},{1,25},{2,26},{3,27},{4,28},{5,29},{6,30},{7,31},{8,16},{9,... | collective-permute-start | bytes 2457608 | tf_op jit(solution)/shard_map/mixed_sum/ppermute | solution.py:28
  107.2 19.0 %collective-permute-start.17 = (f32[160,1280]{1,0:T(8,128)}, f32[160,1280]{1,0:T(8,128)}, u32[]{:S(2)}, u32[]{:S(2)}) collective-permute-start(f32[160,1280]{1,0:T(8,128)} %pad_maximum_fusion.3), channel_id=1, source_target_pairs={{0,8},{1,9},{2,10},{3,11},{4,12},{5,13},{6,14},{7,15},{8,0},{9,1},... | collective-permute-start | bytes 2457608 | tf_op jit(solution)/shard_map/mixed_sum/ppermute | solution.py:28
  107.2 19.0 %collective-permute-start.23 = (f32[160,1280]{1,0:T(8,128)S(1)}, f32[160,1280]{1,0:T(8,128)}, u32[]{:S(2)}, u32[]{:S(2)}) collective-permute-start(f32[160,1280]{1,0:T(8,128)S(1)} %get-tuple-element.113), channel_id=1, source_target_pairs={{0,2},{1,3},{2,0},{3,1},{4,6},{5,7},{6,4},{7,5},{8,10},{9,11},{10,... | collective-permute-start | bytes 2457608 | tf_op jit(solution)/shard_map/mixed_sum/ppermute | solution.py:28
  108.5 8.5 %collective-permute-start.21 = (bf16[160,640]{1,0:T(8,128)(2,1)S(1)}, bf16[160,640]{1,0:T(8,128)(2,1)S(1)}, u32[]{:S(2)}, u32[]{:S(2)}) collective-permute-start(bf16[160,640]{1,0:T(8,128)(2,1)S(1)} %slice.75), channel_id=1, source_target_pairs={{0,96},{1,97},{2,98},{3,99},{4,100},{5,101},{6,102},{7,103},{8,104... | collective-permute-start | bytes 614408 | tf_op jit(solution)/shard_map/density_gather/ppermute | solution.py:28
  126.2 17.1 %collective-permute-start.22 = (bf16[1280,640]{1,0:T(8,128)(2,1)}, bf16[1280,640]{1,0:T(8,128)(2,1)S(1)}, u32[]{:S(2)}, u32[]{:S(2)}) collective-permute-start(bf16[1280,640]{1,0:T(8,128)(2,1)} %density_rows.1.mine_ref), channel_id=1, source_target_pairs={{0,2},{1,3},{2,0},{3,1},{4,6},{5,7},{6,4},{7,5},{8,10},{9,11},{10,... | collective-permute-start | bytes 4915208 | tf_op jit(solution)/shard_map/mixed_gather/ppermute | solution.py:28
  128.0 13.2 %collective-permute-start.24 = (bf16[160,1280]{1,0:T(8,128)(2,1)S(1)}, bf16[160,1280]{1,0:T(8,128)(2,1)S(1)}, u32[]{:S(2)}, u32[]{:S(2)}) collective-permute-start(bf16[160,1280]{1,0:T(8,128)(2,1)S(1)} %fusion.10.refs_0_), channel_id=1, source_target_pairs={{0,24},{1,25},{2,26},{3,27},{4,28},{5,29},{6,30},{7,31},{8,16},{9,... | collective-permute-start | bytes 1228808 | tf_op jit(solution)/shard_map/mixed_gather/ppermute | solution.py:28
  129.1 12.1 %collective-permute-start.25 = (bf16[160,1280]{1,0:T(8,128)(2,1)S(1)}, bf16[160,1280]{1,0:T(8,128)(2,1)S(1)}, u32[]{:S(2)}, u32[]{:S(2)}) collective-permute-start(bf16[160,1280]{1,0:T(8,128)(2,1)S(1)} %fusion.10.refs_0_), channel_id=1, source_target_pairs={{0,8},{1,9},{2,10},{3,11},{4,12},{5,13},{6,14},{7,15},{8,0},{9,1},... | collective-permute-start | bytes 1228808 | tf_op jit(solution)/shard_map/mixed_gather/ppermute | solution.py:28
  141.2 10.3 %collective-permute-start.27 = (bf16[80,1280]{1,0:T(8,128)(2,1)S(1)}, bf16[80,1280]{1,0:T(8,128)(2,1)S(1)}, u32[]{:S(2)}, u32[]{:S(2)}) collective-permute-start(bf16[80,1280]{1,0:T(8,128)(2,1)S(1)} %slice.94), channel_id=1, source_target_pairs={{0,8},{1,9},{2,10},{3,11},{4,12},{5,13},{6,14},{7,15},{8,0},{9,1},... | collective-permute-start | bytes 614408 | tf_op jit(solution)/shard_map/mixed_gather/ppermute | solution.py:28
  141.3 10.2 %collective-permute-start.28 = (bf16[80,1280]{1,0:T(8,128)(2,1)S(1)}, bf16[80,1280]{1,0:T(8,128)(2,1)}, u32[]{:S(2)}, u32[]{:S(2)}) collective-permute-start(bf16[80,1280]{1,0:T(8,128)(2,1)S(1)} %slice.95), channel_id=1, source_target_pairs={{0,24},{1,25},{2,26},{3,27},{4,28},{5,29},{6,30},{7,31},{8,16},{9,... | collective-permute-start | bytes 614408 | tf_op jit(solution)/shard_map/mixed_gather/ppermute | solution.py:28
  151.5 15.8 %collective-permute-start.31 = (bf16[2,3,40,640]{3,2,1,0:T(8,128)(2,1)}, bf16[2,3,40,640]{3,2,1,0:T(8,128)(2,1)S(1)}, u32[]{:S(2)}, u32[]{:S(2)}) collective-permute-start(bf16[2,3,40,640]{3,2,1,0:T(8,128)(2,1)} %get-tuple-element.101), channel_id=1, source_target_pairs={{0,3},{1,2},{2,5},{3,4},{4,7},{5,6},{6,1},{7,0},{8,11},{9,10},{10,... | collective-permute-start | bytes 921608 | tf_op jit(solution)/shard_map/second_product/ppermute | solution.py:42
  153.7 14.2 %collective-permute-start.29 = (bf16[2,3,40,640]{3,2,1,0:T(8,128)(2,1)}, bf16[2,3,40,640]{3,2,1,0:T(8,128)(2,1)S(1)}, u32[]{:S(2)}, u32[]{:S(2)}) collective-permute-start(bf16[2,3,40,640]{3,2,1,0:T(8,128)(2,1)} %get-tuple-element.99), channel_id=1, source_target_pairs={{0,2},{1,3},{2,4},{3,5},{4,6},{5,7},{6,0},{7,1},{8,10},{9,11},{10,... | collective-permute-start | bytes 921608 | tf_op jit(solution)/shard_map/second_product/ppermute | solution.py:42
  153.7 15.4 %collective-permute-start.30 = (bf16[2,3,40,640]{3,2,1,0:T(8,128)(2,1)}, bf16[2,3,40,640]{3,2,1,0:T(8,128)(2,1)S(1)}, u32[]{:S(2)}, u32[]{:S(2)}) collective-permute-start(bf16[2,3,40,640]{3,2,1,0:T(8,128)(2,1)} %get-tuple-element.100), channel_id=1, source_target_pairs={{0,1},{1,0},{2,7},{3,6},{4,5},{5,4},{6,3},{7,2},{8,9},{9,8},{10,15... | collective-permute-start | bytes 921608 | tf_op jit(solution)/shard_map/second_product/ppermute | solution.py:42
  160.2 8.9 %collective-permute-start.32 = (bf16[2,1,40,640]{3,2,1,0:T(8,128)(2,1)}, bf16[2,1,40,640]{3,2,1,0:T(8,128)(2,1)S(1)}, u32[]{:S(2)}, u32[]{:S(2)}) collective-permute-start(bf16[2,1,40,640]{3,2,1,0:T(8,128)(2,1)} %get-tuple-element.104), channel_id=1, source_target_pairs={{0,0},{1,1},{2,6},{3,7},{4,4},{5,5},{6,2},{7,3},{8,8},{9,9},{10,14... | collective-permute-start | bytes 307208 | tf_op jit(solution)/shard_map/second_product/ppermute | solution.py:42
  161.8 9.0 %collective-permute-start.33 = (bf16[2,1,40,640]{3,2,1,0:T(8,128)(2,1)}, bf16[2,1,40,640]{3,2,1,0:T(8,128)(2,1)S(1)}, u32[]{:S(2)}, u32[]{:S(2)}) collective-permute-start(bf16[2,1,40,640]{3,2,1,0:T(8,128)(2,1)} %get-tuple-element.105), channel_id=1, source_target_pairs={{0,2},{1,3},{2,4},{3,5},{4,6},{5,7},{6,0},{7,1},{8,10},{9,11},{10,... | collective-permute-start | bytes 307208 | tf_op jit(solution)/shard_map/second_product/ppermute | solution.py:42
  177.9 18.6 %all-to-all-start.2 = ((bf16[32,40,160]{2,1,0:T(8,128)(2,1)}), bf16[32,40,160]{2,1,0:T(8,128)(2,1)S(1)}, u32[]{:S(2)}, u32[]{:S(2)}) async-start(bf16[32,40,160]{2,1,0:T(8,128)(2,1)} %get-tuple-element.112), calls=%async_computation.2 | async-start | bytes 1310720 | tf_op jit(solution)/shard_map/transposed/all_to_all | solution.py:333
  185.6 7.7 %collective-permute-start.37 = (bf16[40,1280]{1,0:T(8,128)(2,1)}, bf16[40,1280]{1,0:T(8,128)(2,1)S(1)}, u32[]{:S(2)}, u32[]{:S(2)}) collective-permute-start(bf16[40,1280]{1,0:T(8,128)(2,1)} %get-tuple-element.110), channel_id=1, source_target_pairs={{0,16},{1,17},{2,18},{3,19},{4,20},{5,21},{6,22},{7,23},{8,24},{9,... | collective-permute-start | bytes 307208 | tf_op jit(solution)/shard_map/direct/ppermute | solution.py:28
  (40 other events, 264.3 us)

commit v15 on v14

--- a/solution.py
+++ b/solution.py
@@ -51,26 +51,28 @@
 
 
 VMEM = pl.BlockSpec(memory_space=pltpu.VMEM)
-SMEM = pl.BlockSpec(memory_space=pltpu.SMEM)
-
-
-def local_call(kernel, name, outs, coords, *operands, scratch=()):
+
+
+def local_call(kernel, name, outs, *operands, scratch=()):
+    def body(*refs):
+        kernel([lax.axis_index(axis) for axis in AXES], *refs)
+
     return pl.pallas_call(
-        kernel,
+        body,
         out_shape=outs,
-        in_specs=[SMEM] + [VMEM] * len(operands),
+        in_specs=[VMEM] * len(operands),
         out_specs=jax.tree.map(lambda _: VMEM, outs),
         scratch_shapes=list(scratch),
         name=name,
-    )(coords, *operands)
+    )(*operands)
 
 
 def shape(dtype, *dims):
     return jax.ShapeDtypeStruct(dims, dtype)
 
 
-def left_kernel(at_ref, first_ref, second_ref, came_ref, *outs):
-    y, core = at_ref[1], at_ref[3]
+def left_kernel(at, first_ref, second_ref, came_ref, *outs):
+    y, core = at[1], at[3]
     low = jnp.where(core == 0, first_ref[...], came_ref[...])
     high = jnp.where(core == 0, came_ref[...], second_ref[...])
     for ny in range(4):
@@ -83,7 +85,7 @@
                 outs[q][...] = piece
 
 
-def right_kernel(at_ref, first_ref, second_ref, out_ref):
+def right_kernel(at, first_ref, second_ref, out_ref):
     for m, ref in enumerate((first_ref, second_ref)):
         whole = ref[...]
         for xl in range(2):
@@ -101,8 +103,8 @@
                 )
 
 
-def density_kernel(at_ref, same_ref, other_ref, out_ref):
-    xh = at_ref[4]
+def density_kernel(at, same_ref, other_ref, out_ref):
+    xh = at[4]
     first = jnp.where(xh == 0, same_ref[...], other_ref[...])
     second = jnp.where(xh == 0, other_ref[...], same_ref[...])
     for ny in range(4):
@@ -110,8 +112,8 @@
         out_ref[ny] = jnp.concatenate((first[:, cut], second[:, cut]), axis=1)
 
 
-def rows_kernel(at_ref, own_ref, one_ref, upper_ref, lower_ref, three_ref, out_ref):
-    z = at_ref[0]
+def rows_kernel(at, own_ref, one_ref, upper_ref, lower_ref, three_ref, out_ref):
+    z = at[0]
 
     def place(q, start, count, ref):
         first = pl.multiple_of((z ^ q) * 320 + start, 160)
@@ -124,9 +126,9 @@
     place(3, 0, 320, three_ref)
 
 
-def second_kernel(at_ref, mine_ref, other_ref, *refs):
+def second_kernel(at, mine_ref, other_ref, *refs):
     rows, outs, stack, whole = refs[:-6], refs[-6:-2], refs[-2], refs[-1]
-    core, xh = at_ref[3], at_ref[4]
+    core, xh = at[3], at[4]
     first = 0
     for ref in rows:
         stack[first : first + ref.shape[0]] = ref[...]
@@ -140,10 +142,10 @@
                 out[side, slot] = whole[side, slot * 2 + (core ^ t), xh ^ r].astype(bf16)
 
 
-def spread_kernel(at_ref, *refs):
+def spread_kernel(at, *refs):
     many, last = refs[:4], refs[4:8]
     turned_ref, outs, slots = refs[8], refs[9:13], refs[13]
-    y, core = at_ref[1], at_ref[3]
+    y, core = at[1], at[3]
     for q in range(4):
         parts = last if q == 2 else many
         place = 0 if q == 2 else (0, 1, None, 2)[q]
@@ -168,10 +170,10 @@
             turned_ref[nz * 8 + j] = part[j * 40 : j * 40 + 40].astype(bf16)
 
 
-def finish_kernel(at_ref, d0, d1, d2, d3, t_ref, kept_ref, out_ref, slots):
+def finish_kernel(at, d0, d1, d2, d3, t_ref, kept_ref, out_ref, slots):
     for q, ref in enumerate((d0, d1, d2, d3)):
         slots[q] = ref[...].astype(f32)
-    y = at_ref[1]
+    y = at[1]
     for nz in range(4):
         blocks = []
         for ny in range(4):
@@ -196,7 +198,6 @@
 
 def shards(dens_resp, density, fock, fock_resp, pattern):
     z, y, xl, core, xh = (lax.axis_index(name) for name in AXES)
-    coords = jnp.stack((z, y, xl, core, xh)).astype(jnp.int32)
 
     with jax.named_scope("left_columns"):
         send = jnp.where(core == 0, density, dens_resp)
@@ -204,7 +205,7 @@
     with jax.named_scope("right_columns"):
         first, second, _ = lax.optimization_barrier((fock, fock_resp, send))
         parts = local_call(
-            right_kernel, "right_columns", shape(bf16, 8, 160, 320), coords, first, second
+            right_kernel, "right_columns", shape(bf16, 8, 160, 320), first, second
         )
     with jax.named_scope("density_turn"):
         halves, _ = lax.optimization_barrier((density.reshape(2, 2, 40, 1280), send))
@@ -213,7 +214,7 @@
         other = flip(other, xh=1)
     with jax.named_scope("left_columns"):
         pieces = local_call(
-            left_kernel, "left_columns", [shape(bf16, 160, 640)] * 4, coords, dens_resp, density, came
+            left_kernel, "left_columns", [shape(bf16, 160, 640)] * 4, dens_resp, density, came
         )
         parts, pieces = lax.optimization_barrier((parts, pieces))
         left = jnp.concatenate([pieces[0]] + [flip(pieces[q], y=q) for q in (1, 2, 3)])
@@ -236,7 +237,7 @@
     with jax.named_scope("density_columns"):
         same, other, lefts[1, 0] = lax.optimization_barrier((same, other, lefts[1, 0]))
         cols = local_call(
-            density_kernel, "density_columns", shape(bf16, 4, 80, 640), coords, same, other
+            density_kernel, "density_columns", shape(bf16, 4, 80, 640), same, other
         )
         dslots = lax.all_to_all(cols, "y", split_axis=0, concat_axis=0, tiled=True)
         dslots = dslots.reshape(320, 640)
@@ -275,7 +276,7 @@
 
     with jax.named_scope("density_rows"):
         dmine = local_call(
-            rows_kernel, "density_rows", shape(bf16, 1280, 640), coords, dslots, done, *dtwo, dthree
+            rows_kernel, "density_rows", shape(bf16, 1280, 640), dslots, done, *dtwo, dthree
         )
 
     with jax.named_scope("mixed_sum"):
@@ -297,7 +298,6 @@
                 second_kernel,
                 "second_product",
                 [shape(bf16, 2, count, 40, 640)] * 4,
-                coords,
                 dmine,
                 dother,
                 *rows,
@@ -323,7 +323,6 @@
             spread_kernel,
             "spread",
             [shape(bf16, 32, 40, 160), shape(f32, 40, 1280)] + [shape(bf16, 40, 1280)] * 3,
-            coords,
             *many,
             *last,
             scratch=[pltpu.VMEM((4, 40, 1280), f32)],
@@ -347,7 +346,6 @@
         finish_kernel,
         "finish",
         shape(f32, 40, 5120),
-        coords,
         *direct,
         turned,
         kept_blocks,

time: 203 us -> 203 us (level)
    unnamed x60 -> x62, local copies, waits for them, and re-layouts: 7.23 us -> 7.24 us
where the time goes in v15:
time: 203 us; the launch traced here: 201 us
  waiting for transfers between devices  76.7 us (38%)
  starting transfers between devices  70 us (34%)
  Pallas kernels  26 us (13%)
  other arithmetic  12.1 us (6%)
  local copies, waits for them, and re-layouts  10.6 us (5%)
  matrix products  5.35 us (3%)
    ppermute x31, waiting for transfers between devices, flip(): return lax.ppermute(value, AXES, pairs)  70.9 us
    ppermute x31, starting transfers between devices, flip(): return lax.ppermute(value, AXES, pairs)  38.4 us
    pallas_call x8, Pallas kernels, local_call(): pl.pallas_call(body, out_shape=outs, in_specs=[VMEM] * len(operands), out...  26 us
    ppermute x8, starting transfers between devices, remap(): return lax.ppermute(value, AXES, pairs)  15.5 us
    unnamed x62, local copies, waits for them, and re-layouts  7.24 us
    all_to_all x1, starting transfers between devices, shards(): lax.all_to_all(turned, ('z', 'xl', 'core', 'xh'), split_axis=0, concat_ax...  6.78 us
    all_to_all x1, starting transfers between devices, shards(): lax.all_to_all(parts, ('xl', 'core', 'xh'), split_axis=0, concat_axis=0,...  4.93 us
    select_n x2, other arithmetic, shards(): mine = [jnp.where(core == 0, lefts[0, r], lefts[1, r]) for r in range(2)]  4.92 us
  transfers between devices with their start and end apart: 42, of which 23 were waited for; matrix products, arithmetic and copies ran while one was open for 7% of the time, Pallas kernels for 8%

profile of v15, /device:TPU:2, one launch (start us, length us, event | category | flops | bytes accessed | tf_op | source)
XLA Modules:
  0.0 201.2 jit_solution(765505552919866627)
XLA Ops:
  1.2 2.8 %right_columns.1 = bf16[8,160,320]{2,1,0:T(8,128)(2,1)} custom-call(bf16[160,1280]{1,0:T(8,128)(2,1)} %refs_0_.1, bf16[160,1280]{1,0:T(8,128)(2,1)} %refs_1_.1), custom_call_target="tpu_custom_call" | custom-call | tf_op jit(solution)/shard_map/right_columns/right_columns/pallas_call | solution.py:60
  4.7 2.7 %left_columns.1 = (bf16[160,640]{1,0:T(8,128)(2,1)}, bf16[160,640]{1,0:T(8,128)(2,1)}, bf16[160,640]{1,0:T(8,128)(2,1)}, bf16[160,640]{1,0:T(8,128)(2,1)}) custom-call(bf16[160,1280]{1,0:T(8,128)(2,1)} %refs_0_.2, bf16[160,1280]{1,0:T(8,128)(2,1)} %refs_1_.2, bf16[160,1280]{1,0:T(8,128)(2,1)} %copy-done.13), custom_call_target="tpu_custom_call" | custom-call | tf_op jit(solution)/shard_map/left_columns/left_columns/pallas_call | solution.py:60
  7.4 4.9 %all-to-all-start = ((bf16[8,160,320]{2,1,0:T(8,128)(2,1)}), bf16[8,160,320]{2,1,0:T(8,128)(2,1)S(1)}, u32[]{:S(2)}, u32[]{:S(2)}) async-start(bf16[8,160,320]{2,1,0:T(8,128)(2,1)} %right_columns.1), calls=%async_computation | async-start | bytes 1966080 | tf_op jit(solution)/shard_map/right_gather/all_to_all | solution.py:223
  13.9 2.9 %collective-permute-start.2 = (bf16[160,640]{1,0:T(8,128)(2,1)}, bf16[160,640]{1,0:T(8,128)(2,1)S(1)}, u32[]{:S(2)}, u32[]{:S(2)}) collective-permute-start(bf16[160,640]{1,0:T(8,128)(2,1)} %get-tuple-element.68), channel_id=1, source_target_pairs={{0,16},{1,17},{2,18},{3,19},{4,20},{5,21},{6,22},{7,23},{8,24},{9,... | collective-permute-start | bytes 614408 | tf_op jit(solution)/shard_map/left_columns/ppermute | solution.py:28
  20.5 6.2 %collective-permute-done.2 = bf16[160,640]{1,0:T(8,128)(2,1)S(1)} collective-permute-done((bf16[160,640]{1,0:T(8,128)(2,1)}, bf16[160,640]{1,0:T(8,128)(2,1)S(1)}, u32[]{:S(2)}, u32[]{:S(2)}) %collective-permute-start.2) | collective-permute-done | bytes 204832 | tf_op jit(solution)/shard_map/left_columns/ppermute | solution.py:28
  26.6 2.6 %collective-permute-done.3 = bf16[160,640]{1,0:T(8,128)(2,1)S(1)} collective-permute-done((bf16[160,640]{1,0:T(8,128)(2,1)}, bf16[160,640]{1,0:T(8,128)(2,1)S(1)}, u32[]{:S(2)}, u32[]{:S(2)}) %collective-permute-start.3) | collective-permute-done | bytes 204832 | tf_op jit(solution)/shard_map/left_columns/ppermute | solution.py:28
  35.5 4.0 %collective-permute-start.10 = (bf16[320,1280]{1,0:T(8,128)(2,1)S(1)}, bf16[320,1280]{1,0:T(8,128)(2,1)S(1)}, u32[]{:S(2)}, u32[]{:S(2)}) collective-permute-start(bf16[320,1280]{1,0:T(8,128)(2,1)S(1)} %reshape.58), channel_id=1, source_target_pairs={{0,96},{1,97},{2,98},{3,99},{4,100},{5,101},{6,102},{7,103},{8,104... | collective-permute-start | bytes 2457608 | tf_op jit(solution)/shard_map/right_gather/ppermute | solution.py:28
  39.5 13.7 %collective-permute-done.5 = bf16[640,640]{1,0:T(8,128)(2,1)} collective-permute-done((bf16[640,640]{1,0:T(8,128)(2,1)S(1)}, bf16[640,640]{1,0:T(8,128)(2,1)}, u32[]{:S(2)}, u32[]{:S(2)}) %collective-permute-start.5) | collective-permute-done | bytes 819232 | tf_op jit(solution)/shard_map/left_gather/ppermute | solution.py:28
  53.3 3.9 %collective-permute-start.9 = (bf16[320,1280]{1,0:T(8,128)(2,1)S(1)}, bf16[320,1280]{1,0:T(8,128)(2,1)}, u32[]{:S(2)}, u32[]{:S(2)}) collective-permute-start(bf16[320,1280]{1,0:T(8,128)(2,1)S(1)} %reshape.58), channel_id=1, source_target_pairs={{0,64},{1,65},{2,66},{3,67},{4,68},{5,69},{6,70},{7,71},{8,72},{9,... | collective-permute-start | bytes 2457608 | tf_op jit(solution)/shard_map/right_gather/ppermute | solution.py:28
  59.1 4.5 %all-to-all-start.1 = ((bf16[4,80,640]{2,1,0:T(8,128)(2,1)}), bf16[4,80,640]{2,1,0:T(8,128)(2,1)S(1)}, u32[]{:S(2)}, u32[]{:S(2)}) async-start(bf16[4,80,640]{2,1,0:T(8,128)(2,1)} %density_columns.1), calls=%async_computation.1 | async-start | bytes 819200 | tf_op jit(solution)/shard_map/density_columns/all_to_all | solution.py:242
  63.5 2.5 %broadcast_select_fusion.3 = (bf16[640,640]{1,0:T(8,128)(2,1)}, bf16[640,640]{1,0:T(8,128)(2,1)}) fusion(bf16[640,640]{1,0:T(8,128)(2,1)S(1)} %pad_maximum_fusion.2, bf16[640,640]{1,0:T(8,128)(2,1)} %collective-permute-done.5, pred[]{:T(512)S(6)} %eq.8), kind=kLoop, calls=%fused_computation.28 | loop fusion | flops 819200 | bytes 3276801 | tf_op jit(solution)/shard_map/first_product/jit(_where)/select_n | solution.py:256
  66.0 3.3 %collective-permute-done.6 = bf16[640,640]{1,0:T(8,128)(2,1)} collective-permute-done((bf16[640,640]{1,0:T(8,128)(2,1)S(1)}, bf16[640,640]{1,0:T(8,128)(2,1)}, u32[]{:S(2)}, u32[]{:S(2)}) %collective-permute-start.6) | collective-permute-done | bytes 819232 | tf_op jit(solution)/shard_map/left_gather/ppermute | solution.py:28
  70.7 2.4 %broadcast_select_fusion.2 = (bf16[640,640]{1,0:T(8,128)(2,1)S(1)}, bf16[640,640]{1,0:T(8,128)(2,1)}) fusion(bf16[640,640]{1,0:T(8,128)(2,1)} %collective-permute-done.6, bf16[640,640]{1,0:T(8,128)(2,1)} %collective-permute-done.7, pred[]{:T(512)S(6)} %eq.8), kind=kLoop, calls=%fused_computation.27 | loop fusion | flops 819200 | bytes 3276801 | tf_op jit(solution)/shard_map/first_product/jit(_where)/select_n | solution.py:256
  73.2 2.4 %collective-permute-done.9 = bf16[320,1280]{1,0:T(8,128)(2,1)} collective-permute-done((bf16[320,1280]{1,0:T(8,128)(2,1)S(1)}, bf16[320,1280]{1,0:T(8,128)(2,1)}, u32[]{:S(2)}, u32[]{:S(2)}) %collective-permute-start.9) | collective-permute-done | bytes 819232 | tf_op jit(solution)/shard_map/right_gather/ppermute | solution.py:28
  78.7 2.3 %fusion.4 = f32[640,1280]{1,0:T(8,128)S(1)} fusion(bf16[640,640]{1,0:T(8,128)(2,1)S(1)} %copy-done.12, bf16[640,640]{1,0:T(8,128)(2,1)S(1)} %copy-done.11, bf16[320,1280]{1,0:T(8,128)(2,1)S(1)} %get-tuple-element.121, bf16[320,1280]{1,0:T(8,128)(2,1)S(1)} %get-tuple-element.122, bf16[320,1280]{1,0:T(8,128)(2,1)S(1)} %get-tuple-element.123, ...), kind=kOutput, calls=%fused_computation.6 | convolution fusion | flops 2113536000 | bytes 8192000 | tf_op jit(solution)/shard_map/first_product/dot_general | solution.py:50
  82.0 3.1 %collective-permute-start.16 = (bf16[320,640]{1,0:T(8,128)(2,1)S(1)}, bf16[320,640]{1,0:T(8,128)(2,1)S(1)}, u32[]{:S(2)}, u32[]{:S(2)}) collective-permute-start(bf16[320,640]{1,0:T(8,128)(2,1)S(1)} %bitcast.25), channel_id=1, source_target_pairs={{0,96},{1,97},{2,98},{3,99},{4,100},{5,101},{6,102},{7,103},{8,104... | collective-permute-start | bytes 1228808 | tf_op jit(solution)/shard_map/density_gather/ppermute | solution.py:28
  85.2 2.3 %fusion = f32[640,1280]{1,0:T(8,128)S(1)} fusion(bf16[640,640]{1,0:T(8,128)(2,1)S(1)} %get-tuple-element.126, bf16[640,640]{1,0:T(8,128)(2,1)S(1)} %copy-done.10, bf16[320,1280]{1,0:T(8,128)(2,1)S(1)} %get-tuple-element.121, bf16[320,1280]{1,0:T(8,128)(2,1)S(1)} %get-tuple-element.122, bf16[320,1280]{1,0:T(8,128)(2,1)S(1)} %get-tuple-element.123, ...), kind=kOutput, calls=%fused_computation.2 | convolution fusion | flops 2113536000 | bytes 8192000 | tf_op jit(solution)/shard_map/first_product/dot_general | solution.py:50
  95.0 5.5 %collective-permute-done.13 = f32[80,1280]{1,0:T(8,128)S(1)} collective-permute-done((f32[80,1280]{1,0:T(8,128)S(1)}, f32[80,1280]{1,0:T(8,128)S(1)}, u32[]{:S(2)}, u32[]{:S(2)}) %collective-permute-start.13) | collective-permute-done | bytes 409632 | tf_op jit(solution)/shard_map/mixed_sum/ppermute | solution.py:28
  100.6 2.5 %collective-permute-done.14 = f32[80,1280]{1,0:T(8,128)S(1)} collective-permute-done((f32[80,1280]{1,0:T(8,128)S(1)}, f32[80,1280]{1,0:T(8,128)S(1)}, u32[]{:S(2)}, u32[]{:S(2)}) %collective-permute-start.14) | collective-permute-done | bytes 409632 | tf_op jit(solution)/shard_map/mixed_sum/ppermute | solution.py:28
  108.8 5.3 %collective-permute-done.20.refs_2_ = bf16[160,640]{1,0:T(8,128)(2,1)S(1)} collective-permute-done((bf16[160,640]{1,0:T(8,128)(2,1)S(1)}, bf16[160,640]{1,0:T(8,128)(2,1)S(1)}, u32[]{:S(2)}, u32[]{:S(2)}) %collective-permute-start.20) | collective-permute-done | bytes 204832 | tf_op jit(solution)/shard_map/density_gather/ppermute | solution.py:28
  117.1 2.7 %density_rows.1.refs_0_ = bf16[1280,640]{1,0:T(8,128)(2,1)} custom-call(bf16[320,640]{1,0:T(8,128)(2,1)} %bitcast.26, bf16[320,640]{1,0:T(8,128)(2,1)} %copy-done.6, bf16[160,640]{1,0:T(8,128)(2,1)} %copy-done.20, bf16[160,640]{1,0:T(8,128)(2,1)} %copy-done.21, bf16[320,640]{1,0:T(8,128)(2,1)} %copy-done.7), custom_call_target="tpu_custom_call" | custom-call | tf_op jit(solution)/shard_map/density_rows/density_rows/pallas_call | solution.py:60
  119.8 3.8 %collective-permute-done.19 = f32[160,1280]{1,0:T(8,128)S(1)} collective-permute-done((f32[160,1280]{1,0:T(8,128)S(1)}, f32[160,1280]{1,0:T(8,128)S(1)}, u32[]{:S(2)}, u32[]{:S(2)}) %collective-permute-start.19) | collective-permute-done | bytes 819232 | tf_op jit(solution)/shard_map/mixed_sum/ppermute | solution.py:28
  128.5 12.0 %collective-permute-done.24.refs_4_ = bf16[160,1280]{1,0:T(8,128)(2,1)S(1)} collective-permute-done((bf16[160,1280]{1,0:T(8,128)(2,1)S(1)}, bf16[160,1280]{1,0:T(8,128)(2,1)S(1)}, u32[]{:S(2)}, u32[]{:S(2)}) %collective-permute-start.24) | collective-permute-done | bytes 409632 | tf_op jit(solution)/shard_map/mixed_gather/ppermute | solution.py:28
  144.5 5.4 %second_product.2 = (bf16[2,3,40,640]{3,2,1,0:T(8,128)(2,1)}, bf16[2,3,40,640]{3,2,1,0:T(8,128)(2,1)}, bf16[2,3,40,640]{3,2,1,0:T(8,128)(2,1)}, bf16[2,3,40,640]{3,2,1,0:T(8,128)(2,1)}) custom-call(bf16[1280,640]{1,0:T(8,128)(2,1)} %density_rows.1.refs_0_, bf16[1280,640]{1,0:T(8,128)(2,1)} %copy-done, bf16[160,1280]{1,0:T(8,128)(2,1)} %copy-done.4, ...), custom_call_target="tpu_custom_call" | custom-call | tf_op jit(solution)/shard_map/second_product/second_product/pallas_call | solution.py:60
  153.8 2.8 %collective-permute-start.30 = (bf16[2,3,40,640]{3,2,1,0:T(8,128)(2,1)}, bf16[2,3,40,640]{3,2,1,0:T(8,128)(2,1)S(1)}, u32[]{:S(2)}, u32[]{:S(2)}) collective-permute-start(bf16[2,3,40,640]{3,2,1,0:T(8,128)(2,1)} %get-tuple-element.100), channel_id=1, source_target_pairs={{0,1},{1,0},{2,7},{3,6},{4,5},{5,4},{6,3},{7,2},{8,9},{9,8},{10,15... | collective-permute-start | bytes 921608 | tf_op jit(solution)/shard_map/second_product/ppermute | solution.py:42
  156.7 3.7 %second_product.3 = (bf16[2,1,40,640]{3,2,1,0:T(8,128)(2,1)}, bf16[2,1,40,640]{3,2,1,0:T(8,128)(2,1)}, bf16[2,1,40,640]{3,2,1,0:T(8,128)(2,1)}, bf16[2,1,40,640]{3,2,1,0:T(8,128)(2,1)}) custom-call(bf16[1280,640]{1,0:T(8,128)(2,1)} %density_rows.1.refs_0_, bf16[1280,640]{1,0:T(8,128)(2,1)} %copy-done, bf16[80,1280]{1,0:T(8,128)(2,1)} %copy-done.18, ...), custom_call_target="tpu_custom_call" | custom-call | tf_op jit(solution)/shard_map/second_product/second_product/pallas_call | solution.py:60
  161.9 5.5 %collective-permute-start.33 = (bf16[2,1,40,640]{3,2,1,0:T(8,128)(2,1)}, bf16[2,1,40,640]{3,2,1,0:T(8,128)(2,1)S(1)}, u32[]{:S(2)}, u32[]{:S(2)}) collective-permute-start(bf16[2,1,40,640]{3,2,1,0:T(8,128)(2,1)} %get-tuple-element.105), channel_id=1, source_target_pairs={{0,2},{1,3},{2,4},{3,5},{4,6},{5,7},{6,0},{7,1},{8,10},{9,11},{10,... | collective-permute-start | bytes 307208 | tf_op jit(solution)/shard_map/second_product/ppermute | solution.py:42
  170.8 2.9 %collective-permute-done.34.refs_6_ = bf16[2,1,40,640]{3,2,1,0:T(8,128)(2,1)S(1)} collective-permute-done((bf16[2,1,40,640]{3,2,1,0:T(8,128)(2,1)}, bf16[2,1,40,640]{3,2,1,0:T(8,128)(2,1)S(1)}, u32[]{:S(2)}, u32[]{:S(2)}) %collective-permute-start.34) | collective-permute-done | bytes 102432 | tf_op jit(solution)/shard_map/second_product/ppermute | solution.py:42
  175.0 2.9 %spread.1 = (bf16[32,40,160]{2,1,0:T(8,128)(2,1)}, f32[40,1280]{1,0:T(8,128)}, bf16[40,1280]{1,0:T(8,128)(2,1)}, bf16[40,1280]{1,0:T(8,128)(2,1)}, bf16[40,1280]{1,0:T(8,128)(2,1)}) custom-call(bf16[2,3,40,640]{3,2,1,0:T(8,128)(2,1)} %copy-done.14, bf16[2,3,40,640]{3,2,1,0:T(8,128)(2,1)} %copy-done.16, bf16[2,3,40,640]{3,2,1,0:T(8,128)(2,1)} %copy-done.17, ...), custom_call_target="tpu_custom_call" | custom-call | tf_op jit(solution)/shard_map/second_product/spread/pallas_call | solution.py:60
  177.9 6.8 %all-to-all-start.2 = ((bf16[32,40,160]{2,1,0:T(8,128)(2,1)}), bf16[32,40,160]{2,1,0:T(8,128)(2,1)S(1)}, u32[]{:S(2)}, u32[]{:S(2)}) async-start(bf16[32,40,160]{2,1,0:T(8,128)(2,1)} %get-tuple-element.112), calls=%async_computation.2 | async-start | bytes 1310720 | tf_op jit(solution)/shard_map/transposed/all_to_all | solution.py:332
  190.8 2.5 %collective-permute-done.37.refs_2_ = bf16[40,1280]{1,0:T(8,128)(2,1)S(1)} collective-permute-done((bf16[40,1280]{1,0:T(8,128)(2,1)}, bf16[40,1280]{1,0:T(8,128)(2,1)S(1)}, u32[]{:S(2)}, u32[]{:S(2)}) %collective-permute-start.37) | collective-permute-done | bytes 102432 | tf_op jit(solution)/shard_map/direct/ppermute | solution.py:28
  197.4 3.8 %finish.1 = f32[40,5120]{1,0:T(8,128)} custom-call(f32[40,1280]{1,0:T(8,128)} %get-tuple-element.108.refs_0_, bf16[40,1280]{1,0:T(8,128)(2,1)} %copy-done.27, bf16[40,1280]{1,0:T(8,128)(2,1)} %copy-done.28, bf16[40,1280]{1,0:T(8,128)(2,1)} %copy-done.29, bf16[32,40,160]{2,1,0:T(8,128)(2,1)} %copy-done.3, f32[40,40]{1,0:T(8,128)} %fusion.11.refs_5_), custom_call_target="tpu_custom_call" | custom-call | tf_op jit(solution)/shard_map/finish/pallas_call | solution.py:60
  (146 shorter events, 66.1 us)
Async XLA Ops:
  7.4 23.2 %all-to-all-start = ((bf16[8,160,320]{2,1,0:T(8,128)(2,1)}), bf16[8,160,320]{2,1,0:T(8,128)(2,1)S(1)}, u32[]{:S(2)}, u32[]{:S(2)}) async-start(bf16[8,160,320]{2,1,0:T(8,128)(2,1)} %right_columns.1), calls=%async_computation | async-start | bytes 1966080 | tf_op jit(solution)/shard_map/right_gather/all_to_all | solution.py:223
  12.3 8.1 %collective-permute-start.1 = (bf16[160,640]{1,0:T(8,128)(2,1)}, bf16[160,640]{1,0:T(8,128)(2,1)S(1)}, u32[]{:S(2)}, u32[]{:S(2)}) collective-permute-start(bf16[160,640]{1,0:T(8,128)(2,1)} %get-tuple-element.67), channel_id=1, source_target_pairs={{0,8},{1,9},{2,10},{3,11},{4,12},{5,13},{6,14},{7,15},{8,0},{9,1},... | collective-permute-start | bytes 614408 | tf_op jit(solution)/shard_map/left_columns/ppermute | solution.py:28
  13.9 12.7 %collective-permute-start.2 = (bf16[160,640]{1,0:T(8,128)(2,1)}, bf16[160,640]{1,0:T(8,128)(2,1)S(1)}, u32[]{:S(2)}, u32[]{:S(2)}) collective-permute-start(bf16[160,640]{1,0:T(8,128)(2,1)} %get-tuple-element.68), channel_id=1, source_target_pairs={{0,16},{1,17},{2,18},{3,19},{4,20},{5,21},{6,22},{7,23},{8,24},{9,... | collective-permute-start | bytes 614408 | tf_op jit(solution)/shard_map/left_columns/ppermute | solution.py:28
  16.8 12.4 %collective-permute-start.3 = (bf16[160,640]{1,0:T(8,128)(2,1)}, bf16[160,640]{1,0:T(8,128)(2,1)S(1)}, u32[]{:S(2)}, u32[]{:S(2)}) collective-permute-start(bf16[160,640]{1,0:T(8,128)(2,1)} %get-tuple-element.69), channel_id=1, source_target_pairs={{0,24},{1,25},{2,26},{3,27},{4,28},{5,29},{6,30},{7,31},{8,16},{9,... | collective-permute-start | bytes 614408 | tf_op jit(solution)/shard_map/left_columns/ppermute | solution.py:28
  17.8 12.9 %collective-permute-start.4 = (bf16[80,1280]{1,0:T(8,128)(2,1)S(1)}, bf16[80,1280]{1,0:T(8,128)(2,1)S(1)}, u32[]{:S(2)}, u32[]{:S(2)}) collective-permute-start(bf16[80,1280]{1,0:T(8,128)(2,1)S(1)} %bitcast.29), channel_id=1, source_target_pairs={{0,1},{1,0},{2,3},{3,2},{4,5},{5,4},{6,7},{7,6},{8,9},{9,8},{10,11... | collective-permute-start | bytes 614408 | tf_op jit(solution)/shard_map/density_turn/ppermute | solution.py:28
  31.9 21.3 %collective-permute-start.5 = (bf16[640,640]{1,0:T(8,128)(2,1)S(1)}, bf16[640,640]{1,0:T(8,128)(2,1)}, u32[]{:S(2)}, u32[]{:S(2)}) collective-permute-start(bf16[640,640]{1,0:T(8,128)(2,1)S(1)} %pad_maximum_fusion.2), channel_id=1, source_target_pairs={{0,4},{1,5},{2,6},{3,7},{4,0},{5,1},{6,2},{7,3},{8,12},{9,13},{10,... | collective-permute-start | bytes 2457608 | tf_op jit(solution)/shard_map/left_gather/ppermute | solution.py:28
  33.5 35.9 %collective-permute-start.6 = (bf16[640,640]{1,0:T(8,128)(2,1)S(1)}, bf16[640,640]{1,0:T(8,128)(2,1)}, u32[]{:S(2)}, u32[]{:S(2)}) collective-permute-start(bf16[640,640]{1,0:T(8,128)(2,1)S(1)} %pad_maximum_fusion.2), channel_id=1, source_target_pairs={{0,1},{1,0},{2,3},{3,2},{4,5},{5,4},{6,7},{7,6},{8,9},{9,8},{10,11... | collective-permute-start | bytes 2457608 | tf_op jit(solution)/shard_map/left_gather/ppermute | solution.py:28
  34.5 36.2 %collective-permute-start.7 = (bf16[640,640]{1,0:T(8,128)(2,1)S(1)}, bf16[640,640]{1,0:T(8,128)(2,1)}, u32[]{:S(2)}, u32[]{:S(2)}) collective-permute-start(bf16[640,640]{1,0:T(8,128)(2,1)S(1)} %pad_maximum_fusion.2), channel_id=1, source_target_pairs={{0,5},{1,4},{2,7},{3,6},{4,1},{5,0},{6,3},{7,2},{8,13},{9,12},{10,... | collective-permute-start | bytes 2457608 | tf_op jit(solution)/shard_map/left_gather/ppermute | solution.py:28
  35.5 37.7 %collective-permute-start.10 = (bf16[320,1280]{1,0:T(8,128)(2,1)S(1)}, bf16[320,1280]{1,0:T(8,128)(2,1)S(1)}, u32[]{:S(2)}, u32[]{:S(2)}) collective-permute-start(bf16[320,1280]{1,0:T(8,128)(2,1)S(1)} %reshape.58), channel_id=1, source_target_pairs={{0,96},{1,97},{2,98},{3,99},{4,100},{5,101},{6,102},{7,103},{8,104... | collective-permute-start | bytes 2457608 | tf_op jit(solution)/shard_map/right_gather/ppermute | solution.py:28
  39.5 33.6 %collective-permute-start.8 = (bf16[320,1280]{1,0:T(8,128)(2,1)S(1)}, bf16[320,1280]{1,0:T(8,128)(2,1)}, u32[]{:S(2)}, u32[]{:S(2)}) collective-permute-start(bf16[320,1280]{1,0:T(8,128)(2,1)S(1)} %reshape.58), channel_id=1, source_target_pairs={{0,32},{1,33},{2,34},{3,35},{4,36},{5,37},{6,38},{7,39},{8,40},{9,... | collective-permute-start | bytes 2457608 | tf_op jit(solution)/shard_map/right_gather/ppermute | solution.py:28
  53.3 22.3 %collective-permute-start.9 = (bf16[320,1280]{1,0:T(8,128)(2,1)S(1)}, bf16[320,1280]{1,0:T(8,128)(2,1)}, u32[]{:S(2)}, u32[]{:S(2)}) collective-permute-start(bf16[320,1280]{1,0:T(8,128)(2,1)S(1)} %reshape.58), channel_id=1, source_target_pairs={{0,64},{1,65},{2,66},{3,67},{4,68},{5,69},{6,70},{7,71},{8,72},{9,... | collective-permute-start | bytes 2457608 | tf_op jit(solution)/shard_map/right_gather/ppermute | solution.py:28
  59.1 16.5 %all-to-all-start.1 = ((bf16[4,80,640]{2,1,0:T(8,128)(2,1)}), bf16[4,80,640]{2,1,0:T(8,128)(2,1)S(1)}, u32[]{:S(2)}, u32[]{:S(2)}) async-start(bf16[4,80,640]{2,1,0:T(8,128)(2,1)} %density_columns.1), calls=%async_computation.1 | async-start | bytes 819200 | tf_op jit(solution)/shard_map/density_columns/all_to_all | solution.py:242
  82.0 11.8 %collective-permute-start.15 = (bf16[320,640]{1,0:T(8,128)(2,1)S(1)}, bf16[320,640]{1,0:T(8,128)(2,1)S(1)}, u32[]{:S(2)}, u32[]{:S(2)}) collective-permute-start(bf16[320,640]{1,0:T(8,128)(2,1)S(1)} %bitcast.24), channel_id=1, source_target_pairs={{0,32},{1,33},{2,34},{3,35},{4,36},{5,37},{6,38},{7,39},{8,40},{9,... | collective-permute-start | bytes 1228808 | tf_op jit(solution)/shard_map/density_gather/ppermute | solution.py:28
  82.0 13.0 %collective-permute-start.16 = (bf16[320,640]{1,0:T(8,128)(2,1)S(1)}, bf16[320,640]{1,0:T(8,128)(2,1)S(1)}, u32[]{:S(2)}, u32[]{:S(2)}) collective-permute-start(bf16[320,640]{1,0:T(8,128)(2,1)S(1)} %bitcast.25), channel_id=1, source_target_pairs={{0,96},{1,97},{2,98},{3,99},{4,100},{5,101},{6,102},{7,103},{8,104... | collective-permute-start | bytes 1228808 | tf_op jit(solution)/shard_map/density_gather/ppermute | solution.py:28
  89.2 11.4 %collective-permute-start.13 = (f32[80,1280]{1,0:T(8,128)S(1)}, f32[80,1280]{1,0:T(8,128)S(1)}, u32[]{:S(2)}, u32[]{:S(2)}) collective-permute-start(f32[80,1280]{1,0:T(8,128)S(1)} %get-tuple-element.133), channel_id=1, source_target_pairs={{0,8},{1,9},{2,10},{3,11},{4,12},{5,13},{6,14},{7,15},{8,0},{9,1},... | collective-permute-start | bytes 1228808 | tf_op jit(solution)/shard_map/mixed_sum/ppermute | solution.py:28
  90.8 12.3 %collective-permute-start.14 = (f32[80,1280]{1,0:T(8,128)S(1)}, f32[80,1280]{1,0:T(8,128)S(1)}, u32[]{:S(2)}, u32[]{:S(2)}) collective-permute-start(f32[80,1280]{1,0:T(8,128)S(1)} %get-tuple-element.132), channel_id=1, source_target_pairs={{0,24},{1,25},{2,26},{3,27},{4,28},{5,29},{6,30},{7,31},{8,16},{9,... | collective-permute-start | bytes 1228808 | tf_op jit(solution)/shard_map/mixed_sum/ppermute | solution.py:28
  103.4 20.2 %collective-permute-start.19 = (f32[160,1280]{1,0:T(8,128)S(1)}, f32[160,1280]{1,0:T(8,128)S(1)}, u32[]{:S(2)}, u32[]{:S(2)}) collective-permute-start(f32[160,1280]{1,0:T(8,128)S(1)} %pad_maximum_fusion.4), channel_id=1, source_target_pairs={{0,24},{1,25},{2,26},{3,27},{4,28},{5,29},{6,30},{7,31},{8,16},{9,... | collective-permute-start | bytes 2457608 | tf_op jit(solution)/shard_map/mixed_sum/ppermute | solution.py:28
  106.6 19.0 %collective-permute-start.17 = (f32[160,1280]{1,0:T(8,128)}, f32[160,1280]{1,0:T(8,128)}, u32[]{:S(2)}, u32[]{:S(2)}) collective-permute-start(f32[160,1280]{1,0:T(8,128)} %pad_maximum_fusion.3), channel_id=1, source_target_pairs={{0,8},{1,9},{2,10},{3,11},{4,12},{5,13},{6,14},{7,15},{8,0},{9,1},... | collective-permute-start | bytes 2457608 | tf_op jit(solution)/shard_map/mixed_sum/ppermute | solution.py:28
  106.6 19.0 %collective-permute-start.23 = (f32[160,1280]{1,0:T(8,128)S(1)}, f32[160,1280]{1,0:T(8,128)}, u32[]{:S(2)}, u32[]{:S(2)}) collective-permute-start(f32[160,1280]{1,0:T(8,128)S(1)} %get-tuple-element.113), channel_id=1, source_target_pairs={{0,2},{1,3},{2,0},{3,1},{4,6},{5,7},{6,4},{7,5},{8,10},{9,11},{10,... | collective-permute-start | bytes 2457608 | tf_op jit(solution)/shard_map/mixed_sum/ppermute | solution.py:28
  107.9 8.5 %collective-permute-start.21 = (bf16[160,640]{1,0:T(8,128)(2,1)S(1)}, bf16[160,640]{1,0:T(8,128)(2,1)S(1)}, u32[]{:S(2)}, u32[]{:S(2)}) collective-permute-start(bf16[160,640]{1,0:T(8,128)(2,1)S(1)} %slice.75), channel_id=1, source_target_pairs={{0,96},{1,97},{2,98},{3,99},{4,100},{5,101},{6,102},{7,103},{8,104... | collective-permute-start | bytes 614408 | tf_op jit(solution)/shard_map/density_gather/ppermute | solution.py:28
  125.5 17.8 %collective-permute-start.22 = (bf16[1280,640]{1,0:T(8,128)(2,1)}, bf16[1280,640]{1,0:T(8,128)(2,1)S(1)}, u32[]{:S(2)}, u32[]{:S(2)}) collective-permute-start(bf16[1280,640]{1,0:T(8,128)(2,1)} %density_rows.1.refs_0_), channel_id=1, source_target_pairs={{0,2},{1,3},{2,0},{3,1},{4,6},{5,7},{6,4},{7,5},{8,10},{9,11},{10,... | collective-permute-start | bytes 4915208 | tf_op jit(solution)/shard_map/mixed_gather/ppermute | solution.py:28
  127.3 13.2 %collective-permute-start.24 = (bf16[160,1280]{1,0:T(8,128)(2,1)S(1)}, bf16[160,1280]{1,0:T(8,128)(2,1)S(1)}, u32[]{:S(2)}, u32[]{:S(2)}) collective-permute-start(bf16[160,1280]{1,0:T(8,128)(2,1)S(1)} %fusion.10.refs_2_), channel_id=1, source_target_pairs={{0,24},{1,25},{2,26},{3,27},{4,28},{5,29},{6,30},{7,31},{8,16},{9,... | collective-permute-start | bytes 1228808 | tf_op jit(solution)/shard_map/mixed_gather/ppermute | solution.py:28
  128.5 12.1 %collective-permute-start.25 = (bf16[160,1280]{1,0:T(8,128)(2,1)S(1)}, bf16[160,1280]{1,0:T(8,128)(2,1)S(1)}, u32[]{:S(2)}, u32[]{:S(2)}) collective-permute-start(bf16[160,1280]{1,0:T(8,128)(2,1)S(1)} %fusion.10.refs_2_), channel_id=1, source_target_pairs={{0,8},{1,9},{2,10},{3,11},{4,12},{5,13},{6,14},{7,15},{8,0},{9,1},... | collective-permute-start | bytes 1228808 | tf_op jit(solution)/shard_map/mixed_gather/ppermute | solution.py:28
  141.3 10.2 %collective-permute-start.27 = (bf16[80,1280]{1,0:T(8,128)(2,1)S(1)}, bf16[80,1280]{1,0:T(8,128)(2,1)S(1)}, u32[]{:S(2)}, u32[]{:S(2)}) collective-permute-start(bf16[80,1280]{1,0:T(8,128)(2,1)S(1)} %slice.94), channel_id=1, source_target_pairs={{0,8},{1,9},{2,10},{3,11},{4,12},{5,13},{6,14},{7,15},{8,0},{9,1},... | collective-permute-start | bytes 614408 | tf_op jit(solution)/shard_map/mixed_gather/ppermute | solution.py:28
  141.3 10.2 %collective-permute-start.28 = (bf16[80,1280]{1,0:T(8,128)(2,1)}, bf16[80,1280]{1,0:T(8,128)(2,1)S(1)}, u32[]{:S(2)}, u32[]{:S(2)}) collective-permute-start(bf16[80,1280]{1,0:T(8,128)(2,1)} %slice.95), channel_id=1, source_target_pairs={{0,24},{1,25},{2,26},{3,27},{4,28},{5,29},{6,30},{7,31},{8,16},{9,... | collective-permute-start | bytes 614408 | tf_op jit(solution)/shard_map/mixed_gather/ppermute | solution.py:28
  151.6 15.8 %collective-permute-start.31 = (bf16[2,3,40,640]{3,2,1,0:T(8,128)(2,1)}, bf16[2,3,40,640]{3,2,1,0:T(8,128)(2,1)S(1)}, u32[]{:S(2)}, u32[]{:S(2)}) collective-permute-start(bf16[2,3,40,640]{3,2,1,0:T(8,128)(2,1)} %get-tuple-element.101), channel_id=1, source_target_pairs={{0,3},{1,2},{2,5},{3,4},{4,7},{5,6},{6,1},{7,0},{8,11},{9,10},{10,... | collective-permute-start | bytes 921608 | tf_op jit(solution)/shard_map/second_product/ppermute | solution.py:42
  153.8 14.3 %collective-permute-start.29 = (bf16[2,3,40,640]{3,2,1,0:T(8,128)(2,1)}, bf16[2,3,40,640]{3,2,1,0:T(8,128)(2,1)S(1)}, u32[]{:S(2)}, u32[]{:S(2)}) collective-permute-start(bf16[2,3,40,640]{3,2,1,0:T(8,128)(2,1)} %get-tuple-element.99), channel_id=1, source_target_pairs={{0,2},{1,3},{2,4},{3,5},{4,6},{5,7},{6,0},{7,1},{8,10},{9,11},{10,... | collective-permute-start | bytes 921608 | tf_op jit(solution)/shard_map/second_product/ppermute | solution.py:42
  153.8 15.4 %collective-permute-start.30 = (bf16[2,3,40,640]{3,2,1,0:T(8,128)(2,1)}, bf16[2,3,40,640]{3,2,1,0:T(8,128)(2,1)S(1)}, u32[]{:S(2)}, u32[]{:S(2)}) collective-permute-start(bf16[2,3,40,640]{3,2,1,0:T(8,128)(2,1)} %get-tuple-element.100), channel_id=1, source_target_pairs={{0,1},{1,0},{2,7},{3,6},{4,5},{5,4},{6,3},{7,2},{8,9},{9,8},{10,15... | collective-permute-start | bytes 921608 | tf_op jit(solution)/shard_map/second_product/ppermute | solution.py:42
  160.4 8.8 %collective-permute-start.32 = (bf16[2,1,40,640]{3,2,1,0:T(8,128)(2,1)}, bf16[2,1,40,640]{3,2,1,0:T(8,128)(2,1)S(1)}, u32[]{:S(2)}, u32[]{:S(2)}) collective-permute-start(bf16[2,1,40,640]{3,2,1,0:T(8,128)(2,1)} %get-tuple-element.104), channel_id=1, source_target_pairs={{0,0},{1,1},{2,6},{3,7},{4,4},{5,5},{6,2},{7,3},{8,8},{9,9},{10,14... | collective-permute-start | bytes 307208 | tf_op jit(solution)/shard_map/second_product/ppermute | solution.py:42
  161.9 8.9 %collective-permute-start.33 = (bf16[2,1,40,640]{3,2,1,0:T(8,128)(2,1)}, bf16[2,1,40,640]{3,2,1,0:T(8,128)(2,1)S(1)}, u32[]{:S(2)}, u32[]{:S(2)}) collective-permute-start(bf16[2,1,40,640]{3,2,1,0:T(8,128)(2,1)} %get-tuple-element.105), channel_id=1, source_target_pairs={{0,2},{1,3},{2,4},{3,5},{4,6},{5,7},{6,0},{7,1},{8,10},{9,11},{10,... | collective-permute-start | bytes 307208 | tf_op jit(solution)/shard_map/second_product/ppermute | solution.py:42
  177.9 18.6 %all-to-all-start.2 = ((bf16[32,40,160]{2,1,0:T(8,128)(2,1)}), bf16[32,40,160]{2,1,0:T(8,128)(2,1)S(1)}, u32[]{:S(2)}, u32[]{:S(2)}) async-start(bf16[32,40,160]{2,1,0:T(8,128)(2,1)} %get-tuple-element.112), calls=%async_computation.2 | async-start | bytes 1310720 | tf_op jit(solution)/shard_map/transposed/all_to_all | solution.py:332
  185.7 7.6 %collective-permute-start.37 = (bf16[40,1280]{1,0:T(8,128)(2,1)}, bf16[40,1280]{1,0:T(8,128)(2,1)S(1)}, u32[]{:S(2)}, u32[]{:S(2)}) collective-permute-start(bf16[40,1280]{1,0:T(8,128)(2,1)} %get-tuple-element.110), channel_id=1, source_target_pairs={{0,16},{1,17},{2,18},{3,19},{4,20},{5,21},{6,22},{7,23},{8,24},{9,... | collective-permute-start | bytes 307208 | tf_op jit(solution)/shard_map/direct/ppermute | solution.py:28
  (41 other events, 270.2 us)

commit v16 on v14

--- a/solution.py
+++ b/solution.py
@@ -163,9 +163,9 @@
         part = jnp.concatenate(
             [slots[ny, :, nz * 320 : nz * 320 + 320] for ny in range(4)], axis=0
         )
-        part = part.T
+        part = part.astype(bf16).T
         for j in range(8):
-            turned_ref[nz * 8 + j] = part[j * 40 : j * 40 + 40].astype(bf16)
+            turned_ref[nz * 8 + j] = part[j * 40 : j * 40 + 40]
 
 
 def finish_kernel(at_ref, d0, d1, d2, d3, t_ref, kept_ref, out_ref, slots):

time: 203 us -> 203 us (level)
  no operation moved by 1% of the time
where the time goes in v16:
time: 203 us; the launch traced here: 201 us
  waiting for transfers between devices  76.8 us (38%)
  starting transfers between devices  70.1 us (35%)
  Pallas kernels  25.9 us (13%)
  other arithmetic  12.1 us (6%)
  local copies, waits for them, and re-layouts  10.5 us (5%)
  matrix products  5.35 us (3%)
    ppermute x31, waiting for transfers between devices, flip(): return lax.ppermute(value, AXES, pairs)  71 us
    ppermute x31, starting transfers between devices, flip(): return lax.ppermute(value, AXES, pairs)  38.4 us
    pallas_call x8, Pallas kernels, local_call(): pl.pallas_call(kernel, out_shape=outs, in_specs=[SMEM] + [VMEM] * len(ope...  25.9 us
    ppermute x8, starting transfers between devices, remap(): return lax.ppermute(value, AXES, pairs)  15.5 us
    unnamed x60, local copies, waits for them, and re-layouts  7.23 us
    all_to_all x1, starting transfers between devices, shards(): lax.all_to_all(turned, ('z', 'xl', 'core', 'xh'), split_axis=0, concat_ax...  6.79 us
    select_n x2, other arithmetic, shards(): mine = [jnp.where(core == 0, lefts[0, r], lefts[1, r]) for r in range(2)]  4.92 us
    all_to_all x1, starting transfers between devices, shards(): lax.all_to_all(parts, ('xl', 'core', 'xh'), split_axis=0, concat_axis=0,...  4.92 us
  transfers between devices with their start and end apart: 42, of which 23 were waited for; matrix products, arithmetic and copies ran while one was open for 7% of the time, Pallas kernels for 8%

profile of v16, /device:TPU:2, one launch (start us, length us, event | category | flops | bytes accessed | tf_op | source)
XLA Modules:
  0.0 201.1 jit_solution(11626620084483238954)
XLA Ops:
  1.9 2.7 %right_columns.1 = bf16[8,160,320]{2,1,0:T(8,128)(2,1)} custom-call(s32[5]{0:T(128)} %stack.38.at_ref, bf16[160,1280]{1,0:T(8,128)(2,1)} %first_ref.1, bf16[160,1280]{1,0:T(8,128)(2,1)} %second_ref.1), custom_call_target="tpu_custom_call" | custom-call | tf_op jit(solution)/shard_map/right_columns/right_columns/pallas_call | solution.py:58
  5.4 2.6 %left_columns.1 = (bf16[160,640]{1,0:T(8,128)(2,1)}, bf16[160,640]{1,0:T(8,128)(2,1)}, bf16[160,640]{1,0:T(8,128)(2,1)}, bf16[160,640]{1,0:T(8,128)(2,1)}) custom-call(s32[5]{0:T(128)} %stack.38.at_ref, bf16[160,1280]{1,0:T(8,128)(2,1)} %first_ref.2, bf16[160,1280]{1,0:T(8,128)(2,1)} %second_ref.2, bf16[160,1280]{1,0:T(8,128)(2,1)} %copy-done.13), custom_call_target="tpu_custom_call" | custom-call | tf_op jit(solution)/shard_map/left_columns/left_columns/pallas_call | solution.py:58
  8.0 4.9 %all-to-all-start = ((bf16[8,160,320]{2,1,0:T(8,128)(2,1)}), bf16[8,160,320]{2,1,0:T(8,128)(2,1)S(1)}, u32[]{:S(2)}, u32[]{:S(2)}) async-start(bf16[8,160,320]{2,1,0:T(8,128)(2,1)} %right_columns.1), calls=%async_computation | async-start | bytes 1966080 | tf_op jit(solution)/shard_map/right_gather/all_to_all | solution.py:222
  14.5 2.9 %collective-permute-start.2 = (bf16[160,640]{1,0:T(8,128)(2,1)}, bf16[160,640]{1,0:T(8,128)(2,1)S(1)}, u32[]{:S(2)}, u32[]{:S(2)}) collective-permute-start(bf16[160,640]{1,0:T(8,128)(2,1)} %get-tuple-element.68), channel_id=1, source_target_pairs={{0,16},{1,17},{2,18},{3,19},{4,20},{5,21},{6,22},{7,23},{8,24},{9,... | collective-permute-start | bytes 614408 | tf_op jit(solution)/shard_map/left_columns/ppermute | solution.py:28
  21.1 6.1 %collective-permute-done.2 = bf16[160,640]{1,0:T(8,128)(2,1)S(1)} collective-permute-done((bf16[160,640]{1,0:T(8,128)(2,1)}, bf16[160,640]{1,0:T(8,128)(2,1)S(1)}, u32[]{:S(2)}, u32[]{:S(2)}) %collective-permute-start.2) | collective-permute-done | bytes 204832 | tf_op jit(solution)/shard_map/left_columns/ppermute | solution.py:28
  27.2 2.6 %collective-permute-done.3 = bf16[160,640]{1,0:T(8,128)(2,1)S(1)} collective-permute-done((bf16[160,640]{1,0:T(8,128)(2,1)}, bf16[160,640]{1,0:T(8,128)(2,1)S(1)}, u32[]{:S(2)}, u32[]{:S(2)}) %collective-permute-start.3) | collective-permute-done | bytes 204832 | tf_op jit(solution)/shard_map/left_columns/ppermute | solution.py:28
  36.1 4.0 %collective-permute-start.10 = (bf16[320,1280]{1,0:T(8,128)(2,1)S(1)}, bf16[320,1280]{1,0:T(8,128)(2,1)S(1)}, u32[]{:S(2)}, u32[]{:S(2)}) collective-permute-start(bf16[320,1280]{1,0:T(8,128)(2,1)S(1)} %reshape.58), channel_id=1, source_target_pairs={{0,96},{1,97},{2,98},{3,99},{4,100},{5,101},{6,102},{7,103},{8,104... | collective-permute-start | bytes 2457608 | tf_op jit(solution)/shard_map/right_gather/ppermute | solution.py:28
  40.1 13.7 %collective-permute-done.5 = bf16[640,640]{1,0:T(8,128)(2,1)} collective-permute-done((bf16[640,640]{1,0:T(8,128)(2,1)S(1)}, bf16[640,640]{1,0:T(8,128)(2,1)}, u32[]{:S(2)}, u32[]{:S(2)}) %collective-permute-start.5) | collective-permute-done | bytes 819232 | tf_op jit(solution)/shard_map/left_gather/ppermute | solution.py:28
  53.9 3.9 %collective-permute-start.9 = (bf16[320,1280]{1,0:T(8,128)(2,1)S(1)}, bf16[320,1280]{1,0:T(8,128)(2,1)}, u32[]{:S(2)}, u32[]{:S(2)}) collective-permute-start(bf16[320,1280]{1,0:T(8,128)(2,1)S(1)} %reshape.58), channel_id=1, source_target_pairs={{0,64},{1,65},{2,66},{3,67},{4,68},{5,69},{6,70},{7,71},{8,72},{9,... | collective-permute-start | bytes 2457608 | tf_op jit(solution)/shard_map/right_gather/ppermute | solution.py:28
  59.7 4.5 %all-to-all-start.1 = ((bf16[4,80,640]{2,1,0:T(8,128)(2,1)}), bf16[4,80,640]{2,1,0:T(8,128)(2,1)S(1)}, u32[]{:S(2)}, u32[]{:S(2)}) async-start(bf16[4,80,640]{2,1,0:T(8,128)(2,1)} %density_columns.1), calls=%async_computation.1 | async-start | bytes 819200 | tf_op jit(solution)/shard_map/density_columns/all_to_all | solution.py:241
  64.1 2.5 %broadcast_select_fusion.3 = (bf16[640,640]{1,0:T(8,128)(2,1)}, bf16[640,640]{1,0:T(8,128)(2,1)}) fusion(bf16[640,640]{1,0:T(8,128)(2,1)S(1)} %pad_maximum_fusion.2, bf16[640,640]{1,0:T(8,128)(2,1)} %collective-permute-done.5, pred[]{:T(512)S(6)} %eq.8), kind=kLoop, calls=%fused_computation.28 | loop fusion | flops 819200 | bytes 3276801 | tf_op jit(solution)/shard_map/first_product/jit(_where)/select_n | solution.py:255
  66.6 3.3 %collective-permute-done.6 = bf16[640,640]{1,0:T(8,128)(2,1)} collective-permute-done((bf16[640,640]{1,0:T(8,128)(2,1)S(1)}, bf16[640,640]{1,0:T(8,128)(2,1)}, u32[]{:S(2)}, u32[]{:S(2)}) %collective-permute-start.6) | collective-permute-done | bytes 819232 | tf_op jit(solution)/shard_map/left_gather/ppermute | solution.py:28
  71.3 2.4 %broadcast_select_fusion.2 = (bf16[640,640]{1,0:T(8,128)(2,1)S(1)}, bf16[640,640]{1,0:T(8,128)(2,1)}) fusion(bf16[640,640]{1,0:T(8,128)(2,1)} %collective-permute-done.6, bf16[640,640]{1,0:T(8,128)(2,1)} %collective-permute-done.7, pred[]{:T(512)S(6)} %eq.8), kind=kLoop, calls=%fused_computation.27 | loop fusion | flops 819200 | bytes 3276801 | tf_op jit(solution)/shard_map/first_product/jit(_where)/select_n | solution.py:255
  73.8 2.4 %collective-permute-done.9 = bf16[320,1280]{1,0:T(8,128)(2,1)} collective-permute-done((bf16[320,1280]{1,0:T(8,128)(2,1)S(1)}, bf16[320,1280]{1,0:T(8,128)(2,1)}, u32[]{:S(2)}, u32[]{:S(2)}) %collective-permute-start.9) | collective-permute-done | bytes 819232 | tf_op jit(solution)/shard_map/right_gather/ppermute | solution.py:28
  79.3 2.3 %fusion.4 = f32[640,1280]{1,0:T(8,128)S(1)} fusion(bf16[640,640]{1,0:T(8,128)(2,1)S(1)} %copy-done.12, bf16[640,640]{1,0:T(8,128)(2,1)S(1)} %copy-done.11, bf16[320,1280]{1,0:T(8,128)(2,1)S(1)} %get-tuple-element.121, bf16[320,1280]{1,0:T(8,128)(2,1)S(1)} %get-tuple-element.122, bf16[320,1280]{1,0:T(8,128)(2,1)S(1)} %get-tuple-element.123, ...), kind=kOutput, calls=%fused_computation.6 | convolution fusion | flops 2113536000 | bytes 8192000 | tf_op jit(solution)/shard_map/first_product/dot_general | solution.py:50
  82.7 3.1 %collective-permute-start.16 = (bf16[320,640]{1,0:T(8,128)(2,1)S(1)}, bf16[320,640]{1,0:T(8,128)(2,1)S(1)}, u32[]{:S(2)}, u32[]{:S(2)}) collective-permute-start(bf16[320,640]{1,0:T(8,128)(2,1)S(1)} %bitcast.30), channel_id=1, source_target_pairs={{0,96},{1,97},{2,98},{3,99},{4,100},{5,101},{6,102},{7,103},{8,104... | collective-permute-start | bytes 1228808 | tf_op jit(solution)/shard_map/density_gather/ppermute | solution.py:28
  85.8 2.3 %fusion = f32[640,1280]{1,0:T(8,128)S(1)} fusion(bf16[640,640]{1,0:T(8,128)(2,1)S(1)} %get-tuple-element.126, bf16[640,640]{1,0:T(8,128)(2,1)S(1)} %copy-done.10, bf16[320,1280]{1,0:T(8,128)(2,1)S(1)} %get-tuple-element.121, bf16[320,1280]{1,0:T(8,128)(2,1)S(1)} %get-tuple-element.122, bf16[320,1280]{1,0:T(8,128)(2,1)S(1)} %get-tuple-element.123, ...), kind=kOutput, calls=%fused_computation.2 | convolution fusion | flops 2113536000 | bytes 8192000 | tf_op jit(solution)/shard_map/first_product/dot_general | solution.py:50
  95.7 5.5 %collective-permute-done.13 = f32[80,1280]{1,0:T(8,128)S(1)} collective-permute-done((f32[80,1280]{1,0:T(8,128)S(1)}, f32[80,1280]{1,0:T(8,128)S(1)}, u32[]{:S(2)}, u32[]{:S(2)}) %collective-permute-start.13) | collective-permute-done | bytes 409632 | tf_op jit(solution)/shard_map/mixed_sum/ppermute | solution.py:28
  101.2 2.5 %collective-permute-done.14 = f32[80,1280]{1,0:T(8,128)S(1)} collective-permute-done((f32[80,1280]{1,0:T(8,128)S(1)}, f32[80,1280]{1,0:T(8,128)S(1)}, u32[]{:S(2)}, u32[]{:S(2)}) %collective-permute-start.14) | collective-permute-done | bytes 409632 | tf_op jit(solution)/shard_map/mixed_sum/ppermute | solution.py:28
  109.4 5.3 %collective-permute-done.20.upper_ref = bf16[160,640]{1,0:T(8,128)(2,1)S(1)} collective-permute-done((bf16[160,640]{1,0:T(8,128)(2,1)S(1)}, bf16[160,640]{1,0:T(8,128)(2,1)S(1)}, u32[]{:S(2)}, u32[]{:S(2)}) %collective-permute-start.20) | collective-permute-done | bytes 204832 | tf_op jit(solution)/shard_map/density_gather/ppermute | solution.py:28
  117.7 2.7 %density_rows.1.mine_ref = bf16[1280,640]{1,0:T(8,128)(2,1)} custom-call(s32[5]{0:T(128)} %stack.38.at_ref, bf16[320,640]{1,0:T(8,128)(2,1)} %bitcast.31, bf16[320,640]{1,0:T(8,128)(2,1)} %copy-done.8, bf16[160,640]{1,0:T(8,128)(2,1)} %copy-done.20, bf16[160,640]{1,0:T(8,128)(2,1)} %copy-done.21, bf16[320,640]{1,0:T(8,128)(2,1)} %copy-done.9), custom_call_target="tpu_custom_call" | custom-call | tf_op jit(solution)/shard_map/density_rows/density_rows/pallas_call | solution.py:58
  120.4 3.8 %collective-permute-done.19 = f32[160,1280]{1,0:T(8,128)S(1)} collective-permute-done((f32[160,1280]{1,0:T(8,128)S(1)}, f32[160,1280]{1,0:T(8,128)S(1)}, u32[]{:S(2)}, u32[]{:S(2)}) %collective-permute-start.19) | collective-permute-done | bytes 819232 | tf_op jit(solution)/shard_map/mixed_sum/ppermute | solution.py:28
  129.1 12.0 %collective-permute-done.24.refs_2_ = bf16[160,1280]{1,0:T(8,128)(2,1)S(1)} collective-permute-done((bf16[160,1280]{1,0:T(8,128)(2,1)S(1)}, bf16[160,1280]{1,0:T(8,128)(2,1)S(1)}, u32[]{:S(2)}, u32[]{:S(2)}) %collective-permute-start.24) | collective-permute-done | bytes 409632 | tf_op jit(solution)/shard_map/mixed_gather/ppermute | solution.py:28
  144.4 5.4 %second_product.2 = (bf16[2,3,40,640]{3,2,1,0:T(8,128)(2,1)}, bf16[2,3,40,640]{3,2,1,0:T(8,128)(2,1)}, bf16[2,3,40,640]{3,2,1,0:T(8,128)(2,1)}, bf16[2,3,40,640]{3,2,1,0:T(8,128)(2,1)}) custom-call(s32[5]{0:T(128)} %stack.38.at_ref, bf16[1280,640]{1,0:T(8,128)(2,1)} %density_rows.1.mine_ref, bf16[1280,640]{1,0:T(8,128)(2,1)} %copy-done, ...), custom_call_target="tpu_custom_call" | custom-call | tf_op jit(solution)/shard_map/second_product/second_product/pallas_call | solution.py:58
  153.7 2.8 %collective-permute-start.30 = (bf16[2,3,40,640]{3,2,1,0:T(8,128)(2,1)}, bf16[2,3,40,640]{3,2,1,0:T(8,128)(2,1)S(1)}, u32[]{:S(2)}, u32[]{:S(2)}) collective-permute-start(bf16[2,3,40,640]{3,2,1,0:T(8,128)(2,1)} %get-tuple-element.100), channel_id=1, source_target_pairs={{0,1},{1,0},{2,7},{3,6},{4,5},{5,4},{6,3},{7,2},{8,9},{9,8},{10,15... | collective-permute-start | bytes 921608 | tf_op jit(solution)/shard_map/second_product/ppermute | solution.py:42
  156.5 3.7 %second_product.3 = (bf16[2,1,40,640]{3,2,1,0:T(8,128)(2,1)}, bf16[2,1,40,640]{3,2,1,0:T(8,128)(2,1)}, bf16[2,1,40,640]{3,2,1,0:T(8,128)(2,1)}, bf16[2,1,40,640]{3,2,1,0:T(8,128)(2,1)}) custom-call(s32[5]{0:T(128)} %stack.38.at_ref, bf16[1280,640]{1,0:T(8,128)(2,1)} %density_rows.1.mine_ref, bf16[1280,640]{1,0:T(8,128)(2,1)} %copy-done, ...), custom_call_target="tpu_custom_call" | custom-call | tf_op jit(solution)/shard_map/second_product/second_product/pallas_call | solution.py:58
  161.8 5.5 %collective-permute-start.33 = (bf16[2,1,40,640]{3,2,1,0:T(8,128)(2,1)}, bf16[2,1,40,640]{3,2,1,0:T(8,128)(2,1)S(1)}, u32[]{:S(2)}, u32[]{:S(2)}) collective-permute-start(bf16[2,1,40,640]{3,2,1,0:T(8,128)(2,1)} %get-tuple-element.105), channel_id=1, source_target_pairs={{0,2},{1,3},{2,4},{3,5},{4,6},{5,7},{6,0},{7,1},{8,10},{9,11},{10,... | collective-permute-start | bytes 307208 | tf_op jit(solution)/shard_map/second_product/ppermute | solution.py:42
  170.7 2.9 %collective-permute-done.34.refs_6_ = bf16[2,1,40,640]{3,2,1,0:T(8,128)(2,1)S(1)} collective-permute-done((bf16[2,1,40,640]{3,2,1,0:T(8,128)(2,1)}, bf16[2,1,40,640]{3,2,1,0:T(8,128)(2,1)S(1)}, u32[]{:S(2)}, u32[]{:S(2)}) %collective-permute-start.34) | collective-permute-done | bytes 102432 | tf_op jit(solution)/shard_map/second_product/ppermute | solution.py:42
  174.9 2.9 %spread.1 = (bf16[32,40,160]{2,1,0:T(8,128)(2,1)}, f32[40,1280]{1,0:T(8,128)}, bf16[40,1280]{1,0:T(8,128)(2,1)}, bf16[40,1280]{1,0:T(8,128)(2,1)}, bf16[40,1280]{1,0:T(8,128)(2,1)}) custom-call(s32[5]{0:T(128)} %stack.38.at_ref, bf16[2,3,40,640]{3,2,1,0:T(8,128)(2,1)} %copy-done.14, bf16[2,3,40,640]{3,2,1,0:T(8,128)(2,1)} %copy-done.16, ...), custom_call_target="tpu_custom_call" | custom-call | tf_op jit(solution)/shard_map/second_product/spread/pallas_call | solution.py:58
  177.8 6.8 %all-to-all-start.2 = ((bf16[32,40,160]{2,1,0:T(8,128)(2,1)}), bf16[32,40,160]{2,1,0:T(8,128)(2,1)S(1)}, u32[]{:S(2)}, u32[]{:S(2)}) async-start(bf16[32,40,160]{2,1,0:T(8,128)(2,1)} %get-tuple-element.112), calls=%async_computation.2 | async-start | bytes 1310720 | tf_op jit(solution)/shard_map/transposed/all_to_all | solution.py:333
  190.7 2.6 %collective-permute-done.37.d2 = bf16[40,1280]{1,0:T(8,128)(2,1)S(1)} collective-permute-done((bf16[40,1280]{1,0:T(8,128)(2,1)}, bf16[40,1280]{1,0:T(8,128)(2,1)S(1)}, u32[]{:S(2)}, u32[]{:S(2)}) %collective-permute-start.37) | collective-permute-done | bytes 102432 | tf_op jit(solution)/shard_map/direct/ppermute | solution.py:28
  197.3 3.8 %finish.1 = f32[40,5120]{1,0:T(8,128)} custom-call(s32[5]{0:T(128)} %stack.38.at_ref, f32[40,1280]{1,0:T(8,128)} %get-tuple-element.108.d0, bf16[40,1280]{1,0:T(8,128)(2,1)} %copy-done.26, bf16[40,1280]{1,0:T(8,128)(2,1)} %copy-done.27, bf16[40,1280]{1,0:T(8,128)(2,1)} %copy-done.28, bf16[32,40,160]{2,1,0:T(8,128)(2,1)} %copy-done.3, f32[40,40]{1,0:T(8,128)} %fusion.11.kept_ref), custom_call_target="tpu_custom_call" | custom-call | tf_op jit(solution)/shard_map/finish/pallas_call | solution.py:58
  (145 shorter events, 66.0 us)
Async XLA Ops:
  8.0 23.2 %all-to-all-start = ((bf16[8,160,320]{2,1,0:T(8,128)(2,1)}), bf16[8,160,320]{2,1,0:T(8,128)(2,1)S(1)}, u32[]{:S(2)}, u32[]{:S(2)}) async-start(bf16[8,160,320]{2,1,0:T(8,128)(2,1)} %right_columns.1), calls=%async_computation | async-start | bytes 1966080 | tf_op jit(solution)/shard_map/right_gather/all_to_all | solution.py:222
  13.0 8.1 %collective-permute-start.1 = (bf16[160,640]{1,0:T(8,128)(2,1)}, bf16[160,640]{1,0:T(8,128)(2,1)S(1)}, u32[]{:S(2)}, u32[]{:S(2)}) collective-permute-start(bf16[160,640]{1,0:T(8,128)(2,1)} %get-tuple-element.67), channel_id=1, source_target_pairs={{0,8},{1,9},{2,10},{3,11},{4,12},{5,13},{6,14},{7,15},{8,0},{9,1},... | collective-permute-start | bytes 614408 | tf_op jit(solution)/shard_map/left_columns/ppermute | solution.py:28
  14.5 12.7 %collective-permute-start.2 = (bf16[160,640]{1,0:T(8,128)(2,1)}, bf16[160,640]{1,0:T(8,128)(2,1)S(1)}, u32[]{:S(2)}, u32[]{:S(2)}) collective-permute-start(bf16[160,640]{1,0:T(8,128)(2,1)} %get-tuple-element.68), channel_id=1, source_target_pairs={{0,16},{1,17},{2,18},{3,19},{4,20},{5,21},{6,22},{7,23},{8,24},{9,... | collective-permute-start | bytes 614408 | tf_op jit(solution)/shard_map/left_columns/ppermute | solution.py:28
  17.4 12.4 %collective-permute-start.3 = (bf16[160,640]{1,0:T(8,128)(2,1)}, bf16[160,640]{1,0:T(8,128)(2,1)S(1)}, u32[]{:S(2)}, u32[]{:S(2)}) collective-permute-start(bf16[160,640]{1,0:T(8,128)(2,1)} %get-tuple-element.69), channel_id=1, source_target_pairs={{0,24},{1,25},{2,26},{3,27},{4,28},{5,29},{6,30},{7,31},{8,16},{9,... | collective-permute-start | bytes 614408 | tf_op jit(solution)/shard_map/left_columns/ppermute | solution.py:28
  18.4 12.9 %collective-permute-start.4 = (bf16[80,1280]{1,0:T(8,128)(2,1)S(1)}, bf16[80,1280]{1,0:T(8,128)(2,1)S(1)}, u32[]{:S(2)}, u32[]{:S(2)}) collective-permute-start(bf16[80,1280]{1,0:T(8,128)(2,1)S(1)} %bitcast.34), channel_id=1, source_target_pairs={{0,1},{1,0},{2,3},{3,2},{4,5},{5,4},{6,7},{7,6},{8,9},{9,8},{10,11... | collective-permute-start | bytes 614408 | tf_op jit(solution)/shard_map/density_turn/ppermute | solution.py:28
  32.5 21.3 %collective-permute-start.5 = (bf16[640,640]{1,0:T(8,128)(2,1)S(1)}, bf16[640,640]{1,0:T(8,128)(2,1)}, u32[]{:S(2)}, u32[]{:S(2)}) collective-permute-start(bf16[640,640]{1,0:T(8,128)(2,1)S(1)} %pad_maximum_fusion.2), channel_id=1, source_target_pairs={{0,4},{1,5},{2,6},{3,7},{4,0},{5,1},{6,2},{7,3},{8,12},{9,13},{10,... | collective-permute-start | bytes 2457608 | tf_op jit(solution)/shard_map/left_gather/ppermute | solution.py:28
  34.1 35.9 %collective-permute-start.6 = (bf16[640,640]{1,0:T(8,128)(2,1)S(1)}, bf16[640,640]{1,0:T(8,128)(2,1)}, u32[]{:S(2)}, u32[]{:S(2)}) collective-permute-start(bf16[640,640]{1,0:T(8,128)(2,1)S(1)} %pad_maximum_fusion.2), channel_id=1, source_target_pairs={{0,1},{1,0},{2,3},{3,2},{4,5},{5,4},{6,7},{7,6},{8,9},{9,8},{10,11... | collective-permute-start | bytes 2457608 | tf_op jit(solution)/shard_map/left_gather/ppermute | solution.py:28
  35.1 36.2 %collective-permute-start.7 = (bf16[640,640]{1,0:T(8,128)(2,1)S(1)}, bf16[640,640]{1,0:T(8,128)(2,1)}, u32[]{:S(2)}, u32[]{:S(2)}) collective-permute-start(bf16[640,640]{1,0:T(8,128)(2,1)S(1)} %pad_maximum_fusion.2), channel_id=1, source_target_pairs={{0,5},{1,4},{2,7},{3,6},{4,1},{5,0},{6,3},{7,2},{8,13},{9,12},{10,... | collective-permute-start | bytes 2457608 | tf_op jit(solution)/shard_map/left_gather/ppermute | solution.py:28
  36.1 37.7 %collective-permute-start.10 = (bf16[320,1280]{1,0:T(8,128)(2,1)S(1)}, bf16[320,1280]{1,0:T(8,128)(2,1)S(1)}, u32[]{:S(2)}, u32[]{:S(2)}) collective-permute-start(bf16[320,1280]{1,0:T(8,128)(2,1)S(1)} %reshape.58), channel_id=1, source_target_pairs={{0,96},{1,97},{2,98},{3,99},{4,100},{5,101},{6,102},{7,103},{8,104... | collective-permute-start | bytes 2457608 | tf_op jit(solution)/shard_map/right_gather/ppermute | solution.py:28
  40.1 33.6 %collective-permute-start.8 = (bf16[320,1280]{1,0:T(8,128)(2,1)S(1)}, bf16[320,1280]{1,0:T(8,128)(2,1)}, u32[]{:S(2)}, u32[]{:S(2)}) collective-permute-start(bf16[320,1280]{1,0:T(8,128)(2,1)S(1)} %reshape.58), channel_id=1, source_target_pairs={{0,32},{1,33},{2,34},{3,35},{4,36},{5,37},{6,38},{7,39},{8,40},{9,... | collective-permute-start | bytes 2457608 | tf_op jit(solution)/shard_map/right_gather/ppermute | solution.py:28
  53.9 22.3 %collective-permute-start.9 = (bf16[320,1280]{1,0:T(8,128)(2,1)S(1)}, bf16[320,1280]{1,0:T(8,128)(2,1)}, u32[]{:S(2)}, u32[]{:S(2)}) collective-permute-start(bf16[320,1280]{1,0:T(8,128)(2,1)S(1)} %reshape.58), channel_id=1, source_target_pairs={{0,64},{1,65},{2,66},{3,67},{4,68},{5,69},{6,70},{7,71},{8,72},{9,... | collective-permute-start | bytes 2457608 | tf_op jit(solution)/shard_map/right_gather/ppermute | solution.py:28
  59.7 16.5 %all-to-all-start.1 = ((bf16[4,80,640]{2,1,0:T(8,128)(2,1)}), bf16[4,80,640]{2,1,0:T(8,128)(2,1)S(1)}, u32[]{:S(2)}, u32[]{:S(2)}) async-start(bf16[4,80,640]{2,1,0:T(8,128)(2,1)} %density_columns.1), calls=%async_computation.1 | async-start | bytes 819200 | tf_op jit(solution)/shard_map/density_columns/all_to_all | solution.py:241
  82.7 11.8 %collective-permute-start.15 = (bf16[320,640]{1,0:T(8,128)(2,1)S(1)}, bf16[320,640]{1,0:T(8,128)(2,1)S(1)}, u32[]{:S(2)}, u32[]{:S(2)}) collective-permute-start(bf16[320,640]{1,0:T(8,128)(2,1)S(1)} %bitcast.29), channel_id=1, source_target_pairs={{0,32},{1,33},{2,34},{3,35},{4,36},{5,37},{6,38},{7,39},{8,40},{9,... | collective-permute-start | bytes 1228808 | tf_op jit(solution)/shard_map/density_gather/ppermute | solution.py:28
  82.7 13.0 %collective-permute-start.16 = (bf16[320,640]{1,0:T(8,128)(2,1)S(1)}, bf16[320,640]{1,0:T(8,128)(2,1)S(1)}, u32[]{:S(2)}, u32[]{:S(2)}) collective-permute-start(bf16[320,640]{1,0:T(8,128)(2,1)S(1)} %bitcast.30), channel_id=1, source_target_pairs={{0,96},{1,97},{2,98},{3,99},{4,100},{5,101},{6,102},{7,103},{8,104... | collective-permute-start | bytes 1228808 | tf_op jit(solution)/shard_map/density_gather/ppermute | solution.py:28
  89.8 11.4 %collective-permute-start.13 = (f32[80,1280]{1,0:T(8,128)S(1)}, f32[80,1280]{1,0:T(8,128)S(1)}, u32[]{:S(2)}, u32[]{:S(2)}) collective-permute-start(f32[80,1280]{1,0:T(8,128)S(1)} %get-tuple-element.133), channel_id=1, source_target_pairs={{0,8},{1,9},{2,10},{3,11},{4,12},{5,13},{6,14},{7,15},{8,0},{9,1},... | collective-permute-start | bytes 1228808 | tf_op jit(solution)/shard_map/mixed_sum/ppermute | solution.py:28
  91.4 12.3 %collective-permute-start.14 = (f32[80,1280]{1,0:T(8,128)S(1)}, f32[80,1280]{1,0:T(8,128)S(1)}, u32[]{:S(2)}, u32[]{:S(2)}) collective-permute-start(f32[80,1280]{1,0:T(8,128)S(1)} %get-tuple-element.132), channel_id=1, source_target_pairs={{0,24},{1,25},{2,26},{3,27},{4,28},{5,29},{6,30},{7,31},{8,16},{9,... | collective-permute-start | bytes 1228808 | tf_op jit(solution)/shard_map/mixed_sum/ppermute | solution.py:28
  104.0 20.2 %collective-permute-start.19 = (f32[160,1280]{1,0:T(8,128)S(1)}, f32[160,1280]{1,0:T(8,128)S(1)}, u32[]{:S(2)}, u32[]{:S(2)}) collective-permute-start(f32[160,1280]{1,0:T(8,128)S(1)} %pad_maximum_fusion.4), channel_id=1, source_target_pairs={{0,24},{1,25},{2,26},{3,27},{4,28},{5,29},{6,30},{7,31},{8,16},{9,... | collective-permute-start | bytes 2457608 | tf_op jit(solution)/shard_map/mixed_sum/ppermute | solution.py:28
  107.2 19.0 %collective-permute-start.17 = (f32[160,1280]{1,0:T(8,128)}, f32[160,1280]{1,0:T(8,128)}, u32[]{:S(2)}, u32[]{:S(2)}) collective-permute-start(f32[160,1280]{1,0:T(8,128)} %pad_maximum_fusion.3), channel_id=1, source_target_pairs={{0,8},{1,9},{2,10},{3,11},{4,12},{5,13},{6,14},{7,15},{8,0},{9,1},... | collective-permute-start | bytes 2457608 | tf_op jit(solution)/shard_map/mixed_sum/ppermute | solution.py:28
  107.2 19.0 %collective-permute-start.23 = (f32[160,1280]{1,0:T(8,128)S(1)}, f32[160,1280]{1,0:T(8,128)}, u32[]{:S(2)}, u32[]{:S(2)}) collective-permute-start(f32[160,1280]{1,0:T(8,128)S(1)} %get-tuple-element.113), channel_id=1, source_target_pairs={{0,2},{1,3},{2,0},{3,1},{4,6},{5,7},{6,4},{7,5},{8,10},{9,11},{10,... | collective-permute-start | bytes 2457608 | tf_op jit(solution)/shard_map/mixed_sum/ppermute | solution.py:28
  108.5 8.5 %collective-permute-start.21 = (bf16[160,640]{1,0:T(8,128)(2,1)S(1)}, bf16[160,640]{1,0:T(8,128)(2,1)S(1)}, u32[]{:S(2)}, u32[]{:S(2)}) collective-permute-start(bf16[160,640]{1,0:T(8,128)(2,1)S(1)} %slice.75), channel_id=1, source_target_pairs={{0,96},{1,97},{2,98},{3,99},{4,100},{5,101},{6,102},{7,103},{8,104... | collective-permute-start | bytes 614408 | tf_op jit(solution)/shard_map/density_gather/ppermute | solution.py:28
  126.2 17.1 %collective-permute-start.22 = (bf16[1280,640]{1,0:T(8,128)(2,1)}, bf16[1280,640]{1,0:T(8,128)(2,1)S(1)}, u32[]{:S(2)}, u32[]{:S(2)}) collective-permute-start(bf16[1280,640]{1,0:T(8,128)(2,1)} %density_rows.1.mine_ref), channel_id=1, source_target_pairs={{0,2},{1,3},{2,0},{3,1},{4,6},{5,7},{6,4},{7,5},{8,10},{9,11},{10,... | collective-permute-start | bytes 4915208 | tf_op jit(solution)/shard_map/mixed_gather/ppermute | solution.py:28
  128.0 13.2 %collective-permute-start.24 = (bf16[160,1280]{1,0:T(8,128)(2,1)S(1)}, bf16[160,1280]{1,0:T(8,128)(2,1)S(1)}, u32[]{:S(2)}, u32[]{:S(2)}) collective-permute-start(bf16[160,1280]{1,0:T(8,128)(2,1)S(1)} %fusion.10.refs_0_), channel_id=1, source_target_pairs={{0,24},{1,25},{2,26},{3,27},{4,28},{5,29},{6,30},{7,31},{8,16},{9,... | collective-permute-start | bytes 1228808 | tf_op jit(solution)/shard_map/mixed_gather/ppermute | solution.py:28
  129.1 12.1 %collective-permute-start.25 = (bf16[160,1280]{1,0:T(8,128)(2,1)S(1)}, bf16[160,1280]{1,0:T(8,128)(2,1)S(1)}, u32[]{:S(2)}, u32[]{:S(2)}) collective-permute-start(bf16[160,1280]{1,0:T(8,128)(2,1)S(1)} %fusion.10.refs_0_), channel_id=1, source_target_pairs={{0,8},{1,9},{2,10},{3,11},{4,12},{5,13},{6,14},{7,15},{8,0},{9,1},... | collective-permute-start | bytes 1228808 | tf_op jit(solution)/shard_map/mixed_gather/ppermute | solution.py:28
  141.2 10.3 %collective-permute-start.27 = (bf16[80,1280]{1,0:T(8,128)(2,1)S(1)}, bf16[80,1280]{1,0:T(8,128)(2,1)S(1)}, u32[]{:S(2)}, u32[]{:S(2)}) collective-permute-start(bf16[80,1280]{1,0:T(8,128)(2,1)S(1)} %slice.94), channel_id=1, source_target_pairs={{0,8},{1,9},{2,10},{3,11},{4,12},{5,13},{6,14},{7,15},{8,0},{9,1},... | collective-permute-start | bytes 614408 | tf_op jit(solution)/shard_map/mixed_gather/ppermute | solution.py:28
  141.3 10.2 %collective-permute-start.28 = (bf16[80,1280]{1,0:T(8,128)(2,1)S(1)}, bf16[80,1280]{1,0:T(8,128)(2,1)}, u32[]{:S(2)}, u32[]{:S(2)}) collective-permute-start(bf16[80,1280]{1,0:T(8,128)(2,1)S(1)} %slice.95), channel_id=1, source_target_pairs={{0,24},{1,25},{2,26},{3,27},{4,28},{5,29},{6,30},{7,31},{8,16},{9,... | collective-permute-start | bytes 614408 | tf_op jit(solution)/shard_map/mixed_gather/ppermute | solution.py:28
  151.5 15.8 %collective-permute-start.31 = (bf16[2,3,40,640]{3,2,1,0:T(8,128)(2,1)}, bf16[2,3,40,640]{3,2,1,0:T(8,128)(2,1)S(1)}, u32[]{:S(2)}, u32[]{:S(2)}) collective-permute-start(bf16[2,3,40,640]{3,2,1,0:T(8,128)(2,1)} %get-tuple-element.101), channel_id=1, source_target_pairs={{0,3},{1,2},{2,5},{3,4},{4,7},{5,6},{6,1},{7,0},{8,11},{9,10},{10,... | collective-permute-start | bytes 921608 | tf_op jit(solution)/shard_map/second_product/ppermute | solution.py:42
  153.7 14.2 %collective-permute-start.29 = (bf16[2,3,40,640]{3,2,1,0:T(8,128)(2,1)}, bf16[2,3,40,640]{3,2,1,0:T(8,128)(2,1)S(1)}, u32[]{:S(2)}, u32[]{:S(2)}) collective-permute-start(bf16[2,3,40,640]{3,2,1,0:T(8,128)(2,1)} %get-tuple-element.99), channel_id=1, source_target_pairs={{0,2},{1,3},{2,4},{3,5},{4,6},{5,7},{6,0},{7,1},{8,10},{9,11},{10,... | collective-permute-start | bytes 921608 | tf_op jit(solution)/shard_map/second_product/ppermute | solution.py:42
  153.7 15.4 %collective-permute-start.30 = (bf16[2,3,40,640]{3,2,1,0:T(8,128)(2,1)}, bf16[2,3,40,640]{3,2,1,0:T(8,128)(2,1)S(1)}, u32[]{:S(2)}, u32[]{:S(2)}) collective-permute-start(bf16[2,3,40,640]{3,2,1,0:T(8,128)(2,1)} %get-tuple-element.100), channel_id=1, source_target_pairs={{0,1},{1,0},{2,7},{3,6},{4,5},{5,4},{6,3},{7,2},{8,9},{9,8},{10,15... | collective-permute-start | bytes 921608 | tf_op jit(solution)/shard_map/second_product/ppermute | solution.py:42
  160.2 8.9 %collective-permute-start.32 = (bf16[2,1,40,640]{3,2,1,0:T(8,128)(2,1)}, bf16[2,1,40,640]{3,2,1,0:T(8,128)(2,1)S(1)}, u32[]{:S(2)}, u32[]{:S(2)}) collective-permute-start(bf16[2,1,40,640]{3,2,1,0:T(8,128)(2,1)} %get-tuple-element.104), channel_id=1, source_target_pairs={{0,0},{1,1},{2,6},{3,7},{4,4},{5,5},{6,2},{7,3},{8,8},{9,9},{10,14... | collective-permute-start | bytes 307208 | tf_op jit(solution)/shard_map/second_product/ppermute | solution.py:42
  161.8 9.0 %collective-permute-start.33 = (bf16[2,1,40,640]{3,2,1,0:T(8,128)(2,1)}, bf16[2,1,40,640]{3,2,1,0:T(8,128)(2,1)S(1)}, u32[]{:S(2)}, u32[]{:S(2)}) collective-permute-start(bf16[2,1,40,640]{3,2,1,0:T(8,128)(2,1)} %get-tuple-element.105), channel_id=1, source_target_pairs={{0,2},{1,3},{2,4},{3,5},{4,6},{5,7},{6,0},{7,1},{8,10},{9,11},{10,... | collective-permute-start | bytes 307208 | tf_op jit(solution)/shard_map/second_product/ppermute | solution.py:42
  177.8 18.6 %all-to-all-start.2 = ((bf16[32,40,160]{2,1,0:T(8,128)(2,1)}), bf16[32,40,160]{2,1,0:T(8,128)(2,1)S(1)}, u32[]{:S(2)}, u32[]{:S(2)}) async-start(bf16[32,40,160]{2,1,0:T(8,128)(2,1)} %get-tuple-element.112), calls=%async_computation.2 | async-start | bytes 1310720 | tf_op jit(solution)/shard_map/transposed/all_to_all | solution.py:333
  185.6 7.7 %collective-permute-start.37 = (bf16[40,1280]{1,0:T(8,128)(2,1)}, bf16[40,1280]{1,0:T(8,128)(2,1)S(1)}, u32[]{:S(2)}, u32[]{:S(2)}) collective-permute-start(bf16[40,1280]{1,0:T(8,128)(2,1)} %get-tuple-element.110), channel_id=1, source_target_pairs={{0,16},{1,17},{2,18},{3,19},{4,20},{5,21},{6,22},{7,23},{8,24},{9,... | collective-permute-start | bytes 307208 | tf_op jit(solution)/shard_map/direct/ppermute | solution.py:28
  (40 other events, 264.3 us)

commit v17 on v14

--- a/solution.py
+++ b/solution.py
@@ -317,7 +317,6 @@
         cut = list(pieces_of(3, mixed, one, three))
         cut[3], two = lax.optimization_barrier((cut[3], two))
         many = scatter(cut)
-        many[0], two = lax.optimization_barrier((many[0], two))
         last = scatter(pieces_of(1, *two))
         turned, *rows = local_call(
             spread_kernel,

time: 203 us -> 211 us (1.039)
  waiting for transfers between devices: 76.8 us -> 88.4 us
  starting transfers between devices: 70.1 us -> 65.8 us
    ppermute x8, waiting for transfers between devices: 4.57 us -> 16.2 us  [remap(): return lax.ppermute(value, AXES, pairs)]
    ppermute x8, starting transfers between devices: 15.5 us -> 11.6 us  [remap(): return lax.ppermute(value, AXES, pairs)]
    unnamed x60 -> x68, local copies, waits for them, and re-layouts: 7.23 us -> 8.37 us
  transfers between devices with their start and end apart: 42 -> 42, of which waited for: 23 -> 23; matrix products, arithmetic and copies ran while one was open for 7% -> 6% of each run, Pallas kernels for 8% -> 6%
where the time goes in v17:
time: 211 us; the launch traced here: 210 us
  waiting for transfers between devices  88.4 us (42%)
  starting transfers between devices  65.8 us (31%)
  Pallas kernels  25.8 us (12%)
  other arithmetic  12.1 us (6%)
  local copies, waits for them, and re-layouts  11.7 us (6%)
  matrix products  5.34 us (3%)
    ppermute x31, waiting for transfers between devices, flip(): return lax.ppermute(value, AXES, pairs)  71.3 us
    ppermute x31, starting transfers between devices, flip(): return lax.ppermute(value, AXES, pairs)  38.4 us
    pallas_call x8, Pallas kernels, local_call(): pl.pallas_call(kernel, out_shape=outs, in_specs=[SMEM] + [VMEM] * len(ope...  25.8 us
    ppermute x8, waiting for transfers between devices, remap(): return lax.ppermute(value, AXES, pairs)  16.2 us
    ppermute x8, starting transfers between devices, remap(): return lax.ppermute(value, AXES, pairs)  11.6 us
    unnamed x68, local copies, waits for them, and re-layouts  8.37 us
    all_to_all x1, starting transfers between devices, shards(): lax.all_to_all(turned, ('z', 'xl', 'core', 'xh'), split_axis=0, concat_ax...  6.42 us
    all_to_all x1, starting transfers between devices, shards(): lax.all_to_all(parts, ('xl', 'core', 'xh'), split_axis=0, concat_axis=0,...  4.92 us
  transfers between devices with their start and end apart: 42, of which 23 were waited for; matrix products, arithmetic and copies ran while one was open for 6% of the time, Pallas kernels for 6%

profile of v17, /device:TPU:2, one launch (start us, length us, event | category | flops | bytes accessed | tf_op | source)
XLA Modules:
  0.0 209.5 jit_solution(944310890629292699)
XLA Ops:
  1.9 2.7 %right_columns.1 = bf16[8,160,320]{2,1,0:T(8,128)(2,1)} custom-call(s32[5]{0:T(128)} %stack.38.at_ref, bf16[160,1280]{1,0:T(8,128)(2,1)} %first_ref.1, bf16[160,1280]{1,0:T(8,128)(2,1)} %second_ref.1), custom_call_target="tpu_custom_call" | custom-call | tf_op jit(solution)/shard_map/right_columns/right_columns/pallas_call | solution.py:58
  5.4 2.7 %left_columns.1 = (bf16[160,640]{1,0:T(8,128)(2,1)}, bf16[160,640]{1,0:T(8,128)(2,1)}, bf16[160,640]{1,0:T(8,128)(2,1)}, bf16[160,640]{1,0:T(8,128)(2,1)}) custom-call(s32[5]{0:T(128)} %stack.38.at_ref, bf16[160,1280]{1,0:T(8,128)(2,1)} %first_ref.2, bf16[160,1280]{1,0:T(8,128)(2,1)} %second_ref.2, bf16[160,1280]{1,0:T(8,128)(2,1)} %copy-done.13), custom_call_target="tpu_custom_call" | custom-call | tf_op jit(solution)/shard_map/left_columns/left_columns/pallas_call | solution.py:58
  8.1 4.9 %all-to-all-start = ((bf16[8,160,320]{2,1,0:T(8,128)(2,1)}), bf16[8,160,320]{2,1,0:T(8,128)(2,1)S(1)}, u32[]{:S(2)}, u32[]{:S(2)}) async-start(bf16[8,160,320]{2,1,0:T(8,128)(2,1)} %right_columns.1), calls=%async_computation | async-start | bytes 1966080 | tf_op jit(solution)/shard_map/right_gather/all_to_all | solution.py:222
  14.6 2.9 %collective-permute-start.2 = (bf16[160,640]{1,0:T(8,128)(2,1)}, bf16[160,640]{1,0:T(8,128)(2,1)S(1)}, u32[]{:S(2)}, u32[]{:S(2)}) collective-permute-start(bf16[160,640]{1,0:T(8,128)(2,1)} %get-tuple-element.65), channel_id=1, source_target_pairs={{0,16},{1,17},{2,18},{3,19},{4,20},{5,21},{6,22},{7,23},{8,24},{9,... | collective-permute-start | bytes 614408 | tf_op jit(solution)/shard_map/left_columns/ppermute | solution.py:28
  21.1 6.1 %collective-permute-done.2 = bf16[160,640]{1,0:T(8,128)(2,1)S(1)} collective-permute-done((bf16[160,640]{1,0:T(8,128)(2,1)}, bf16[160,640]{1,0:T(8,128)(2,1)S(1)}, u32[]{:S(2)}, u32[]{:S(2)}) %collective-permute-start.2) | collective-permute-done | bytes 204832 | tf_op jit(solution)/shard_map/left_columns/ppermute | solution.py:28
  27.3 2.6 %collective-permute-done.3 = bf16[160,640]{1,0:T(8,128)(2,1)S(1)} collective-permute-done((bf16[160,640]{1,0:T(8,128)(2,1)}, bf16[160,640]{1,0:T(8,128)(2,1)S(1)}, u32[]{:S(2)}, u32[]{:S(2)}) %collective-permute-start.3) | collective-permute-done | bytes 204832 | tf_op jit(solution)/shard_map/left_columns/ppermute | solution.py:28
  36.1 4.0 %collective-permute-start.10 = (bf16[320,1280]{1,0:T(8,128)(2,1)S(1)}, bf16[320,1280]{1,0:T(8,128)(2,1)S(1)}, u32[]{:S(2)}, u32[]{:S(2)}) collective-permute-start(bf16[320,1280]{1,0:T(8,128)(2,1)S(1)} %reshape.58), channel_id=1, source_target_pairs={{0,96},{1,97},{2,98},{3,99},{4,100},{5,101},{6,102},{7,103},{8,104... | collective-permute-start | bytes 2457608 | tf_op jit(solution)/shard_map/right_gather/ppermute | solution.py:28
  40.2 13.7 %collective-permute-done.5 = bf16[640,640]{1,0:T(8,128)(2,1)} collective-permute-done((bf16[640,640]{1,0:T(8,128)(2,1)S(1)}, bf16[640,640]{1,0:T(8,128)(2,1)}, u32[]{:S(2)}, u32[]{:S(2)}) %collective-permute-start.5) | collective-permute-done | bytes 819232 | tf_op jit(solution)/shard_map/left_gather/ppermute | solution.py:28
  53.9 3.9 %collective-permute-start.9 = (bf16[320,1280]{1,0:T(8,128)(2,1)S(1)}, bf16[320,1280]{1,0:T(8,128)(2,1)}, u32[]{:S(2)}, u32[]{:S(2)}) collective-permute-start(bf16[320,1280]{1,0:T(8,128)(2,1)S(1)} %reshape.58), channel_id=1, source_target_pairs={{0,64},{1,65},{2,66},{3,67},{4,68},{5,69},{6,70},{7,71},{8,72},{9,... | collective-permute-start | bytes 2457608 | tf_op jit(solution)/shard_map/right_gather/ppermute | solution.py:28
  59.7 4.5 %all-to-all-start.1 = ((bf16[4,80,640]{2,1,0:T(8,128)(2,1)}), bf16[4,80,640]{2,1,0:T(8,128)(2,1)S(1)}, u32[]{:S(2)}, u32[]{:S(2)}) async-start(bf16[4,80,640]{2,1,0:T(8,128)(2,1)} %density_columns.1), calls=%async_computation.1 | async-start | bytes 819200 | tf_op jit(solution)/shard_map/density_columns/all_to_all | solution.py:241
  64.2 2.5 %broadcast_select_fusion.3 = (bf16[640,640]{1,0:T(8,128)(2,1)}, bf16[640,640]{1,0:T(8,128)(2,1)}) fusion(bf16[640,640]{1,0:T(8,128)(2,1)S(1)} %pad_maximum_fusion.2, bf16[640,640]{1,0:T(8,128)(2,1)} %collective-permute-done.5, pred[]{:T(512)S(6)} %eq.8), kind=kLoop, calls=%fused_computation.28 | loop fusion | flops 819200 | bytes 3276801 | tf_op jit(solution)/shard_map/first_product/jit(_where)/select_n | solution.py:255
  66.6 3.3 %collective-permute-done.6 = bf16[640,640]{1,0:T(8,128)(2,1)} collective-permute-done((bf16[640,640]{1,0:T(8,128)(2,1)S(1)}, bf16[640,640]{1,0:T(8,128)(2,1)}, u32[]{:S(2)}, u32[]{:S(2)}) %collective-permute-start.6) | collective-permute-done | bytes 819232 | tf_op jit(solution)/shard_map/left_gather/ppermute | solution.py:28
  71.3 2.4 %broadcast_select_fusion.2 = (bf16[640,640]{1,0:T(8,128)(2,1)S(1)}, bf16[640,640]{1,0:T(8,128)(2,1)}) fusion(bf16[640,640]{1,0:T(8,128)(2,1)} %collective-permute-done.6, bf16[640,640]{1,0:T(8,128)(2,1)} %collective-permute-done.7, pred[]{:T(512)S(6)} %eq.8), kind=kLoop, calls=%fused_computation.27 | loop fusion | flops 819200 | bytes 3276801 | tf_op jit(solution)/shard_map/first_product/jit(_where)/select_n | solution.py:255
  73.8 2.4 %collective-permute-done.9 = bf16[320,1280]{1,0:T(8,128)(2,1)} collective-permute-done((bf16[320,1280]{1,0:T(8,128)(2,1)S(1)}, bf16[320,1280]{1,0:T(8,128)(2,1)}, u32[]{:S(2)}, u32[]{:S(2)}) %collective-permute-start.9) | collective-permute-done | bytes 819232 | tf_op jit(solution)/shard_map/right_gather/ppermute | solution.py:28
  82.7 3.1 %collective-permute-start.16 = (bf16[320,640]{1,0:T(8,128)(2,1)S(1)}, bf16[320,640]{1,0:T(8,128)(2,1)S(1)}, u32[]{:S(2)}, u32[]{:S(2)}) collective-permute-start(bf16[320,640]{1,0:T(8,128)(2,1)S(1)} %bitcast.30), channel_id=1, source_target_pairs={{0,96},{1,97},{2,98},{3,99},{4,100},{5,101},{6,102},{7,103},{8,104... | collective-permute-start | bytes 1228808 | tf_op jit(solution)/shard_map/density_gather/ppermute | solution.py:28
  95.7 5.6 %collective-permute-done.13 = f32[80,1280]{1,0:T(8,128)S(1)} collective-permute-done((f32[80,1280]{1,0:T(8,128)S(1)}, f32[80,1280]{1,0:T(8,128)S(1)}, u32[]{:S(2)}, u32[]{:S(2)}) %collective-permute-start.13) | collective-permute-done | bytes 409632 | tf_op jit(solution)/shard_map/mixed_sum/ppermute | solution.py:28
  101.3 2.5 %collective-permute-done.14 = f32[80,1280]{1,0:T(8,128)S(1)} collective-permute-done((f32[80,1280]{1,0:T(8,128)S(1)}, f32[80,1280]{1,0:T(8,128)S(1)}, u32[]{:S(2)}, u32[]{:S(2)}) %collective-permute-start.14) | collective-permute-done | bytes 409632 | tf_op jit(solution)/shard_map/mixed_sum/ppermute | solution.py:28
  109.5 5.3 %collective-permute-done.20.upper_ref = bf16[160,640]{1,0:T(8,128)(2,1)S(1)} collective-permute-done((bf16[160,640]{1,0:T(8,128)(2,1)S(1)}, bf16[160,640]{1,0:T(8,128)(2,1)S(1)}, u32[]{:S(2)}, u32[]{:S(2)}) %collective-permute-start.20) | collective-permute-done | bytes 204832 | tf_op jit(solution)/shard_map/density_gather/ppermute | solution.py:28
  117.7 2.7 %density_rows.1.mine_ref = bf16[1280,640]{1,0:T(8,128)(2,1)} custom-call(s32[5]{0:T(128)} %stack.38.at_ref, bf16[320,640]{1,0:T(8,128)(2,1)} %bitcast.31, bf16[320,640]{1,0:T(8,128)(2,1)} %copy-done.8, bf16[160,640]{1,0:T(8,128)(2,1)} %copy-done.20, bf16[160,640]{1,0:T(8,128)(2,1)} %copy-done.21, bf16[320,640]{1,0:T(8,128)(2,1)} %copy-done.9), custom_call_target="tpu_custom_call" | custom-call | tf_op jit(solution)/shard_map/density_rows/density_rows/pallas_call | solution.py:58
  120.4 3.8 %collective-permute-done.19 = f32[160,1280]{1,0:T(8,128)S(1)} collective-permute-done((f32[160,1280]{1,0:T(8,128)S(1)}, f32[160,1280]{1,0:T(8,128)S(1)}, u32[]{:S(2)}, u32[]{:S(2)}) %collective-permute-start.19) | collective-permute-done | bytes 819232 | tf_op jit(solution)/shard_map/mixed_sum/ppermute | solution.py:28
  129.1 12.0 %collective-permute-done.24.refs_2_ = bf16[160,1280]{1,0:T(8,128)(2,1)S(1)} collective-permute-done((bf16[160,1280]{1,0:T(8,128)(2,1)S(1)}, bf16[160,1280]{1,0:T(8,128)(2,1)S(1)}, u32[]{:S(2)}, u32[]{:S(2)}) %collective-permute-start.24) | collective-permute-done | bytes 409632 | tf_op jit(solution)/shard_map/mixed_gather/ppermute | solution.py:28
  144.5 5.4 %second_product.2 = (bf16[2,3,40,640]{3,2,1,0:T(8,128)(2,1)}, bf16[2,3,40,640]{3,2,1,0:T(8,128)(2,1)}, bf16[2,3,40,640]{3,2,1,0:T(8,128)(2,1)}, bf16[2,3,40,640]{3,2,1,0:T(8,128)(2,1)}) custom-call(s32[5]{0:T(128)} %stack.38.at_ref, bf16[1280,640]{1,0:T(8,128)(2,1)} %density_rows.1.mine_ref, bf16[1280,640]{1,0:T(8,128)(2,1)} %copy-done, ...), custom_call_target="tpu_custom_call" | custom-call | tf_op jit(solution)/shard_map/second_product/second_product/pallas_call | solution.py:58
  150.6 3.6 %second_product.3 = (bf16[2,1,40,640]{3,2,1,0:T(8,128)(2,1)}, bf16[2,1,40,640]{3,2,1,0:T(8,128)(2,1)}, bf16[2,1,40,640]{3,2,1,0:T(8,128)(2,1)}, bf16[2,1,40,640]{3,2,1,0:T(8,128)(2,1)}) custom-call(s32[5]{0:T(128)} %stack.38.at_ref, bf16[1280,640]{1,0:T(8,128)(2,1)} %density_rows.1.mine_ref, bf16[1280,640]{1,0:T(8,128)(2,1)} %copy-done, ...), custom_call_target="tpu_custom_call" | custom-call | tf_op jit(solution)/shard_map/second_product/second_product/pallas_call | solution.py:58
  158.8 3.0 %collective-permute-start.27 = (bf16[2,3,40,640]{3,2,1,0:T(8,128)(2,1)S(1)}, bf16[2,3,40,640]{3,2,1,0:T(8,128)(2,1)S(1)}, u32[]{:S(2)}, u32[]{:S(2)}) collective-permute-start(bf16[2,3,40,640]{3,2,1,0:T(8,128)(2,1)S(1)} %copy-done.30), channel_id=1, source_target_pairs={{0,2},{1,3},{2,4},{3,5},{4,6},{5,7},{6,0},{7,1},{8,10},{9,11},{10,... | collective-permute-start | bytes 921608 | tf_op jit(solution)/shard_map/second_product/ppermute | solution.py:42
  163.1 2.3 %collective-permute-start.34 = (bf16[2,1,40,640]{3,2,1,0:T(8,128)(2,1)}, bf16[2,1,40,640]{3,2,1,0:T(8,128)(2,1)S(1)}, u32[]{:S(2)}, u32[]{:S(2)}) collective-permute-start(bf16[2,1,40,640]{3,2,1,0:T(8,128)(2,1)} %get-tuple-element.100), channel_id=1, source_target_pairs={{0,1},{1,0},{2,7},{3,6},{4,5},{5,4},{6,3},{7,2},{8,9},{9,8},{10,15... | collective-permute-start | bytes 307208 | tf_op jit(solution)/shard_map/second_product/ppermute | solution.py:42
  165.4 12.0 %collective-permute-done.34.refs_6_ = bf16[2,1,40,640]{3,2,1,0:T(8,128)(2,1)S(1)} collective-permute-done((bf16[2,1,40,640]{3,2,1,0:T(8,128)(2,1)}, bf16[2,1,40,640]{3,2,1,0:T(8,128)(2,1)S(1)}, u32[]{:S(2)}, u32[]{:S(2)}) %collective-permute-start.34) | collective-permute-done | bytes 102432 | tf_op jit(solution)/shard_map/second_product/ppermute | solution.py:42
  177.8 4.1 %collective-permute-done.35.refs_7_ = bf16[2,1,40,640]{3,2,1,0:T(8,128)(2,1)S(1)} collective-permute-done((bf16[2,1,40,640]{3,2,1,0:T(8,128)(2,1)}, bf16[2,1,40,640]{3,2,1,0:T(8,128)(2,1)S(1)}, u32[]{:S(2)}, u32[]{:S(2)}) %collective-permute-start.35) | collective-permute-done | bytes 102432 | tf_op jit(solution)/shard_map/second_product/ppermute | solution.py:42
  183.7 2.9 %spread.1 = (bf16[32,40,160]{2,1,0:T(8,128)(2,1)}, f32[40,1280]{1,0:T(8,128)}, bf16[40,1280]{1,0:T(8,128)(2,1)}, bf16[40,1280]{1,0:T(8,128)(2,1)}, bf16[40,1280]{1,0:T(8,128)(2,1)}) custom-call(s32[5]{0:T(128)} %stack.38.at_ref, bf16[2,3,40,640]{3,2,1,0:T(8,128)(2,1)} %copy-done.15, bf16[2,3,40,640]{3,2,1,0:T(8,128)(2,1)} %copy-done.16, ...), custom_call_target="tpu_custom_call" | custom-call | tf_op jit(solution)/shard_map/second_product/spread/pallas_call | solution.py:58
  186.6 6.4 %all-to-all-start.2 = ((bf16[32,40,160]{2,1,0:T(8,128)(2,1)}), bf16[32,40,160]{2,1,0:T(8,128)(2,1)S(1)}, u32[]{:S(2)}, u32[]{:S(2)}) async-start(bf16[32,40,160]{2,1,0:T(8,128)(2,1)} %get-tuple-element.106), calls=%async_computation.2 | async-start | bytes 1310720 | tf_op jit(solution)/shard_map/transposed/all_to_all | solution.py:332
  193.3 3.3 %collective-permute-start.37 = (bf16[40,1280]{1,0:T(8,128)(2,1)}, bf16[40,1280]{1,0:T(8,128)(2,1)S(1)}, u32[]{:S(2)}, u32[]{:S(2)}) collective-permute-start(bf16[40,1280]{1,0:T(8,128)(2,1)} %get-tuple-element.104), channel_id=1, source_target_pairs={{0,16},{1,17},{2,18},{3,19},{4,20},{5,21},{6,22},{7,23},{8,24},{9,... | collective-permute-start | bytes 307208 | tf_op jit(solution)/shard_map/direct/ppermute | solution.py:28
  199.1 2.8 %collective-permute-done.37.d2 = bf16[40,1280]{1,0:T(8,128)(2,1)S(1)} collective-permute-done((bf16[40,1280]{1,0:T(8,128)(2,1)}, bf16[40,1280]{1,0:T(8,128)(2,1)S(1)}, u32[]{:S(2)}, u32[]{:S(2)}) %collective-permute-start.37) | collective-permute-done | bytes 102432 | tf_op jit(solution)/shard_map/direct/ppermute | solution.py:28
  205.7 3.8 %finish.1 = f32[40,5120]{1,0:T(8,128)} custom-call(s32[5]{0:T(128)} %stack.38.at_ref, f32[40,1280]{1,0:T(8,128)} %get-tuple-element.102.d0, bf16[40,1280]{1,0:T(8,128)(2,1)} %copy-done.26, bf16[40,1280]{1,0:T(8,128)(2,1)} %copy-done.27, bf16[40,1280]{1,0:T(8,128)(2,1)} %copy-done.28, bf16[32,40,160]{2,1,0:T(8,128)(2,1)} %copy-done.3, f32[40,40]{1,0:T(8,128)} %fusion.11.kept_ref), custom_call_target="tpu_custom_call" | custom-call | tf_op jit(solution)/shard_map/finish/pallas_call | solution.py:58
  (153 shorter events, 65.5 us)
Async XLA Ops:
  8.1 23.2 %all-to-all-start = ((bf16[8,160,320]{2,1,0:T(8,128)(2,1)}), bf16[8,160,320]{2,1,0:T(8,128)(2,1)S(1)}, u32[]{:S(2)}, u32[]{:S(2)}) async-start(bf16[8,160,320]{2,1,0:T(8,128)(2,1)} %right_columns.1), calls=%async_computation | async-start | bytes 1966080 | tf_op jit(solution)/shard_map/right_gather/all_to_all | solution.py:222
  13.0 8.1 %collective-permute-start.1 = (bf16[160,640]{1,0:T(8,128)(2,1)}, bf16[160,640]{1,0:T(8,128)(2,1)S(1)}, u32[]{:S(2)}, u32[]{:S(2)}) collective-permute-start(bf16[160,640]{1,0:T(8,128)(2,1)} %get-tuple-element.64), channel_id=1, source_target_pairs={{0,8},{1,9},{2,10},{3,11},{4,12},{5,13},{6,14},{7,15},{8,0},{9,1},... | collective-permute-start | bytes 614408 | tf_op jit(solution)/shard_map/left_columns/ppermute | solution.py:28
  14.6 12.7 %collective-permute-start.2 = (bf16[160,640]{1,0:T(8,128)(2,1)}, bf16[160,640]{1,0:T(8,128)(2,1)S(1)}, u32[]{:S(2)}, u32[]{:S(2)}) collective-permute-start(bf16[160,640]{1,0:T(8,128)(2,1)} %get-tuple-element.65), channel_id=1, source_target_pairs={{0,16},{1,17},{2,18},{3,19},{4,20},{5,21},{6,22},{7,23},{8,24},{9,... | collective-permute-start | bytes 614408 | tf_op jit(solution)/shard_map/left_columns/ppermute | solution.py:28
  17.5 12.4 %collective-permute-start.3 = (bf16[160,640]{1,0:T(8,128)(2,1)}, bf16[160,640]{1,0:T(8,128)(2,1)S(1)}, u32[]{:S(2)}, u32[]{:S(2)}) collective-permute-start(bf16[160,640]{1,0:T(8,128)(2,1)} %get-tuple-element.66), channel_id=1, source_target_pairs={{0,24},{1,25},{2,26},{3,27},{4,28},{5,29},{6,30},{7,31},{8,16},{9,... | collective-permute-start | bytes 614408 | tf_op jit(solution)/shard_map/left_columns/ppermute | solution.py:28
  18.4 12.9 %collective-permute-start.4 = (bf16[80,1280]{1,0:T(8,128)(2,1)S(1)}, bf16[80,1280]{1,0:T(8,128)(2,1)S(1)}, u32[]{:S(2)}, u32[]{:S(2)}) collective-permute-start(bf16[80,1280]{1,0:T(8,128)(2,1)S(1)} %bitcast.34), channel_id=1, source_target_pairs={{0,1},{1,0},{2,3},{3,2},{4,5},{5,4},{6,7},{7,6},{8,9},{9,8},{10,11... | collective-permute-start | bytes 614408 | tf_op jit(solution)/shard_map/density_turn/ppermute | solution.py:28
  32.5 21.3 %collective-permute-start.5 = (bf16[640,640]{1,0:T(8,128)(2,1)S(1)}, bf16[640,640]{1,0:T(8,128)(2,1)}, u32[]{:S(2)}, u32[]{:S(2)}) collective-permute-start(bf16[640,640]{1,0:T(8,128)(2,1)S(1)} %pad_maximum_fusion.2), channel_id=1, source_target_pairs={{0,4},{1,5},{2,6},{3,7},{4,0},{5,1},{6,2},{7,3},{8,12},{9,13},{10,... | collective-permute-start | bytes 2457608 | tf_op jit(solution)/shard_map/left_gather/ppermute | solution.py:28
  34.1 35.9 %collective-permute-start.6 = (bf16[640,640]{1,0:T(8,128)(2,1)S(1)}, bf16[640,640]{1,0:T(8,128)(2,1)}, u32[]{:S(2)}, u32[]{:S(2)}) collective-permute-start(bf16[640,640]{1,0:T(8,128)(2,1)S(1)} %pad_maximum_fusion.2), channel_id=1, source_target_pairs={{0,1},{1,0},{2,3},{3,2},{4,5},{5,4},{6,7},{7,6},{8,9},{9,8},{10,11... | collective-permute-start | bytes 2457608 | tf_op jit(solution)/shard_map/left_gather/ppermute | solution.py:28
  35.2 36.2 %collective-permute-start.7 = (bf16[640,640]{1,0:T(8,128)(2,1)S(1)}, bf16[640,640]{1,0:T(8,128)(2,1)}, u32[]{:S(2)}, u32[]{:S(2)}) collective-permute-start(bf16[640,640]{1,0:T(8,128)(2,1)S(1)} %pad_maximum_fusion.2), channel_id=1, source_target_pairs={{0,5},{1,4},{2,7},{3,6},{4,1},{5,0},{6,3},{7,2},{8,13},{9,12},{10,... | collective-permute-start | bytes 2457608 | tf_op jit(solution)/shard_map/left_gather/ppermute | solution.py:28
  36.1 37.7 %collective-permute-start.10 = (bf16[320,1280]{1,0:T(8,128)(2,1)S(1)}, bf16[320,1280]{1,0:T(8,128)(2,1)S(1)}, u32[]{:S(2)}, u32[]{:S(2)}) collective-permute-start(bf16[320,1280]{1,0:T(8,128)(2,1)S(1)} %reshape.58), channel_id=1, source_target_pairs={{0,96},{1,97},{2,98},{3,99},{4,100},{5,101},{6,102},{7,103},{8,104... | collective-permute-start | bytes 2457608 | tf_op jit(solution)/shard_map/right_gather/ppermute | solution.py:28
  40.2 33.6 %collective-permute-start.8 = (bf16[320,1280]{1,0:T(8,128)(2,1)S(1)}, bf16[320,1280]{1,0:T(8,128)(2,1)}, u32[]{:S(2)}, u32[]{:S(2)}) collective-permute-start(bf16[320,1280]{1,0:T(8,128)(2,1)S(1)} %reshape.58), channel_id=1, source_target_pairs={{0,32},{1,33},{2,34},{3,35},{4,36},{5,37},{6,38},{7,39},{8,40},{9,... | collective-permute-start | bytes 2457608 | tf_op jit(solution)/shard_map/right_gather/ppermute | solution.py:28
  53.9 22.3 %collective-permute-start.9 = (bf16[320,1280]{1,0:T(8,128)(2,1)S(1)}, bf16[320,1280]{1,0:T(8,128)(2,1)}, u32[]{:S(2)}, u32[]{:S(2)}) collective-permute-start(bf16[320,1280]{1,0:T(8,128)(2,1)S(1)} %reshape.58), channel_id=1, source_target_pairs={{0,64},{1,65},{2,66},{3,67},{4,68},{5,69},{6,70},{7,71},{8,72},{9,... | collective-permute-start | bytes 2457608 | tf_op jit(solution)/shard_map/right_gather/ppermute | solution.py:28
  59.7 16.5 %all-to-all-start.1 = ((bf16[4,80,640]{2,1,0:T(8,128)(2,1)}), bf16[4,80,640]{2,1,0:T(8,128)(2,1)S(1)}, u32[]{:S(2)}, u32[]{:S(2)}) async-start(bf16[4,80,640]{2,1,0:T(8,128)(2,1)} %density_columns.1), calls=%async_computation.1 | async-start | bytes 819200 | tf_op jit(solution)/shard_map/density_columns/all_to_all | solution.py:241
  82.7 11.8 %collective-permute-start.15 = (bf16[320,640]{1,0:T(8,128)(2,1)S(1)}, bf16[320,640]{1,0:T(8,128)(2,1)S(1)}, u32[]{:S(2)}, u32[]{:S(2)}) collective-permute-start(bf16[320,640]{1,0:T(8,128)(2,1)S(1)} %bitcast.29), channel_id=1, source_target_pairs={{0,32},{1,33},{2,34},{3,35},{4,36},{5,37},{6,38},{7,39},{8,40},{9,... | collective-permute-start | bytes 1228808 | tf_op jit(solution)/shard_map/density_gather/ppermute | solution.py:28
  82.7 13.0 %collective-permute-start.16 = (bf16[320,640]{1,0:T(8,128)(2,1)S(1)}, bf16[320,640]{1,0:T(8,128)(2,1)S(1)}, u32[]{:S(2)}, u32[]{:S(2)}) collective-permute-start(bf16[320,640]{1,0:T(8,128)(2,1)S(1)} %bitcast.30), channel_id=1, source_target_pairs={{0,96},{1,97},{2,98},{3,99},{4,100},{5,101},{6,102},{7,103},{8,104... | collective-permute-start | bytes 1228808 | tf_op jit(solution)/shard_map/density_gather/ppermute | solution.py:28
  89.8 11.4 %collective-permute-start.13 = (f32[80,1280]{1,0:T(8,128)S(1)}, f32[80,1280]{1,0:T(8,128)S(1)}, u32[]{:S(2)}, u32[]{:S(2)}) collective-permute-start(f32[80,1280]{1,0:T(8,128)S(1)} %get-tuple-element.127), channel_id=1, source_target_pairs={{0,8},{1,9},{2,10},{3,11},{4,12},{5,13},{6,14},{7,15},{8,0},{9,1},... | collective-permute-start | bytes 1228808 | tf_op jit(solution)/shard_map/mixed_sum/ppermute | solution.py:28
  91.5 12.3 %collective-permute-start.14 = (f32[80,1280]{1,0:T(8,128)S(1)}, f32[80,1280]{1,0:T(8,128)S(1)}, u32[]{:S(2)}, u32[]{:S(2)}) collective-permute-start(f32[80,1280]{1,0:T(8,128)S(1)} %get-tuple-element.126), channel_id=1, source_target_pairs={{0,24},{1,25},{2,26},{3,27},{4,28},{5,29},{6,30},{7,31},{8,16},{9,... | collective-permute-start | bytes 1228808 | tf_op jit(solution)/shard_map/mixed_sum/ppermute | solution.py:28
  104.0 20.2 %collective-permute-start.19 = (f32[160,1280]{1,0:T(8,128)S(1)}, f32[160,1280]{1,0:T(8,128)S(1)}, u32[]{:S(2)}, u32[]{:S(2)}) collective-permute-start(f32[160,1280]{1,0:T(8,128)S(1)} %pad_maximum_fusion.4), channel_id=1, source_target_pairs={{0,24},{1,25},{2,26},{3,27},{4,28},{5,29},{6,30},{7,31},{8,16},{9,... | collective-permute-start | bytes 2457608 | tf_op jit(solution)/shard_map/mixed_sum/ppermute | solution.py:28
  107.2 19.0 %collective-permute-start.17 = (f32[160,1280]{1,0:T(8,128)}, f32[160,1280]{1,0:T(8,128)}, u32[]{:S(2)}, u32[]{:S(2)}) collective-permute-start(f32[160,1280]{1,0:T(8,128)} %pad_maximum_fusion.3), channel_id=1, source_target_pairs={{0,8},{1,9},{2,10},{3,11},{4,12},{5,13},{6,14},{7,15},{8,0},{9,1},... | collective-permute-start | bytes 2457608 | tf_op jit(solution)/shard_map/mixed_sum/ppermute | solution.py:28
  107.2 19.0 %collective-permute-start.23 = (f32[160,1280]{1,0:T(8,128)S(1)}, f32[160,1280]{1,0:T(8,128)}, u32[]{:S(2)}, u32[]{:S(2)}) collective-permute-start(f32[160,1280]{1,0:T(8,128)S(1)} %get-tuple-element.107), channel_id=1, source_target_pairs={{0,2},{1,3},{2,0},{3,1},{4,6},{5,7},{6,4},{7,5},{8,10},{9,11},{10,... | collective-permute-start | bytes 2457608 | tf_op jit(solution)/shard_map/mixed_sum/ppermute | solution.py:28
  108.5 8.5 %collective-permute-start.21 = (bf16[160,640]{1,0:T(8,128)(2,1)S(1)}, bf16[160,640]{1,0:T(8,128)(2,1)S(1)}, u32[]{:S(2)}, u32[]{:S(2)}) collective-permute-start(bf16[160,640]{1,0:T(8,128)(2,1)S(1)} %slice.75), channel_id=1, source_target_pairs={{0,96},{1,97},{2,98},{3,99},{4,100},{5,101},{6,102},{7,103},{8,104... | collective-permute-start | bytes 614408 | tf_op jit(solution)/shard_map/density_gather/ppermute | solution.py:28
  126.2 17.1 %collective-permute-start.22 = (bf16[1280,640]{1,0:T(8,128)(2,1)}, bf16[1280,640]{1,0:T(8,128)(2,1)S(1)}, u32[]{:S(2)}, u32[]{:S(2)}) collective-permute-start(bf16[1280,640]{1,0:T(8,128)(2,1)} %density_rows.1.mine_ref), channel_id=1, source_target_pairs={{0,2},{1,3},{2,0},{3,1},{4,6},{5,7},{6,4},{7,5},{8,10},{9,11},{10,... | collective-permute-start | bytes 4915208 | tf_op jit(solution)/shard_map/mixed_gather/ppermute | solution.py:28
  128.0 13.2 %collective-permute-start.24 = (bf16[160,1280]{1,0:T(8,128)(2,1)S(1)}, bf16[160,1280]{1,0:T(8,128)(2,1)S(1)}, u32[]{:S(2)}, u32[]{:S(2)}) collective-permute-start(bf16[160,1280]{1,0:T(8,128)(2,1)S(1)} %fusion.10.refs_0_), channel_id=1, source_target_pairs={{0,24},{1,25},{2,26},{3,27},{4,28},{5,29},{6,30},{7,31},{8,16},{9,... | collective-permute-start | bytes 1228808 | tf_op jit(solution)/shard_map/mixed_gather/ppermute | solution.py:28
  129.1 12.0 %collective-permute-start.25 = (bf16[160,1280]{1,0:T(8,128)(2,1)S(1)}, bf16[160,1280]{1,0:T(8,128)(2,1)S(1)}, u32[]{:S(2)}, u32[]{:S(2)}) collective-permute-start(bf16[160,1280]{1,0:T(8,128)(2,1)S(1)} %fusion.10.refs_0_), channel_id=1, source_target_pairs={{0,8},{1,9},{2,10},{3,11},{4,12},{5,13},{6,14},{7,15},{8,0},{9,1},... | collective-permute-start | bytes 1228808 | tf_op jit(solution)/shard_map/mixed_gather/ppermute | solution.py:28
  141.2 8.6 %collective-permute-start.29 = (bf16[80,1280]{1,0:T(8,128)(2,1)S(1)}, bf16[80,1280]{1,0:T(8,128)(2,1)S(1)}, u32[]{:S(2)}, u32[]{:S(2)}) collective-permute-start(bf16[80,1280]{1,0:T(8,128)(2,1)S(1)} %slice.94), channel_id=1, source_target_pairs={{0,8},{1,9},{2,10},{3,11},{4,12},{5,13},{6,14},{7,15},{8,0},{9,1},... | collective-permute-start | bytes 614408 | tf_op jit(solution)/shard_map/mixed_gather/ppermute | solution.py:28
  141.3 8.6 %collective-permute-start.30 = (bf16[80,1280]{1,0:T(8,128)(2,1)S(1)}, bf16[80,1280]{1,0:T(8,128)(2,1)}, u32[]{:S(2)}, u32[]{:S(2)}) collective-permute-start(bf16[80,1280]{1,0:T(8,128)(2,1)S(1)} %slice.95), channel_id=1, source_target_pairs={{0,24},{1,25},{2,26},{3,27},{4,28},{5,29},{6,30},{7,31},{8,16},{9,... | collective-permute-start | bytes 614408 | tf_op jit(solution)/shard_map/mixed_gather/ppermute | solution.py:28
  157.7 24.2 %collective-permute-start.31 = (bf16[2,3,40,640]{3,2,1,0:T(8,128)(2,1)S(1)}, bf16[2,3,40,640]{3,2,1,0:T(8,128)(2,1)S(1)}, u32[]{:S(2)}, u32[]{:S(2)}) collective-permute-start(bf16[2,3,40,640]{3,2,1,0:T(8,128)(2,1)S(1)} %copy-done.32), channel_id=1, source_target_pairs={{0,3},{1,2},{2,5},{3,4},{4,7},{5,6},{6,1},{7,0},{8,11},{9,10},{10,... | collective-permute-start | bytes 921608 | tf_op jit(solution)/shard_map/second_product/ppermute | solution.py:42
  158.1 23.8 %collective-permute-start.26 = (bf16[2,3,40,640]{3,2,1,0:T(8,128)(2,1)S(1)}, bf16[2,3,40,640]{3,2,1,0:T(8,128)(2,1)S(1)}, u32[]{:S(2)}, u32[]{:S(2)}) collective-permute-start(bf16[2,3,40,640]{3,2,1,0:T(8,128)(2,1)S(1)} %copy-done.31), channel_id=1, source_target_pairs={{0,0},{1,1},{2,6},{3,7},{4,4},{5,5},{6,2},{7,3},{8,8},{9,9},{10,14... | collective-permute-start | bytes 921608 | tf_op jit(solution)/shard_map/second_product/ppermute | solution.py:42
  158.8 23.2 %collective-permute-start.27 = (bf16[2,3,40,640]{3,2,1,0:T(8,128)(2,1)S(1)}, bf16[2,3,40,640]{3,2,1,0:T(8,128)(2,1)S(1)}, u32[]{:S(2)}, u32[]{:S(2)}) collective-permute-start(bf16[2,3,40,640]{3,2,1,0:T(8,128)(2,1)S(1)} %copy-done.30), channel_id=1, source_target_pairs={{0,2},{1,3},{2,4},{3,5},{4,6},{5,7},{6,0},{7,1},{8,10},{9,11},{10,... | collective-permute-start | bytes 921608 | tf_op jit(solution)/shard_map/second_product/ppermute | solution.py:42
  161.8 20.2 %collective-permute-start.28 = (bf16[2,3,40,640]{3,2,1,0:T(8,128)(2,1)S(1)}, bf16[2,3,40,640]{3,2,1,0:T(8,128)(2,1)S(1)}, u32[]{:S(2)}, u32[]{:S(2)}) collective-permute-start(bf16[2,3,40,640]{3,2,1,0:T(8,128)(2,1)S(1)} %copy-done.29), channel_id=1, source_target_pairs={{0,1},{1,0},{2,7},{3,6},{4,5},{5,4},{6,3},{7,2},{8,9},{9,8},{10,15... | collective-permute-start | bytes 921608 | tf_op jit(solution)/shard_map/second_product/ppermute | solution.py:42
  163.1 14.3 %collective-permute-start.34 = (bf16[2,1,40,640]{3,2,1,0:T(8,128)(2,1)}, bf16[2,1,40,640]{3,2,1,0:T(8,128)(2,1)S(1)}, u32[]{:S(2)}, u32[]{:S(2)}) collective-permute-start(bf16[2,1,40,640]{3,2,1,0:T(8,128)(2,1)} %get-tuple-element.100), channel_id=1, source_target_pairs={{0,1},{1,0},{2,7},{3,6},{4,5},{5,4},{6,3},{7,2},{8,9},{9,8},{10,15... | collective-permute-start | bytes 307208 | tf_op jit(solution)/shard_map/second_product/ppermute | solution.py:42
  186.6 18.2 %all-to-all-start.2 = ((bf16[32,40,160]{2,1,0:T(8,128)(2,1)}), bf16[32,40,160]{2,1,0:T(8,128)(2,1)S(1)}, u32[]{:S(2)}, u32[]{:S(2)}) async-start(bf16[32,40,160]{2,1,0:T(8,128)(2,1)} %get-tuple-element.106), calls=%async_computation.2 | async-start | bytes 1310720 | tf_op jit(solution)/shard_map/transposed/all_to_all | solution.py:332
  193.3 8.7 %collective-permute-start.37 = (bf16[40,1280]{1,0:T(8,128)(2,1)}, bf16[40,1280]{1,0:T(8,128)(2,1)S(1)}, u32[]{:S(2)}, u32[]{:S(2)}) collective-permute-start(bf16[40,1280]{1,0:T(8,128)(2,1)} %get-tuple-element.104), channel_id=1, source_target_pairs={{0,16},{1,17},{2,18},{3,19},{4,20},{5,21},{6,22},{7,23},{8,24},{9,... | collective-permute-start | bytes 307208 | tf_op jit(solution)/shard_map/direct/ppermute | solution.py:28
  (44 other events, 313.8 us)
